TPU v7x, 32 devices: a whole 2x2x4 slice. The times are simulated.
32 devices in a mesh: grp: 4 (over x, core), ctx: 4 (over z), wt: 2 (over y).
Axes of the slice: x: 2, y: 2, z: 4, core: 2. Of those that a mesh axis runs over, the one named last changes fastest.
Arguments:
- tokens: bfloat16 [8, 2048, 1280], P(('grp', 'wt'), 'ctx'), may hold values from -6 to 6
- segments: int32 [8, 2048], P(('grp', 'wt')), may hold values from 0 to 2, as said below
- w_qkv: bfloat16 [1280, 3840], P('wt'), may hold values from -0.15625 to 0.15625
- w_proj: bfloat16 [1280, 1280], P('wt'), may hold values from -1.25 to 1.25
- w_in: bfloat16 [1280, 1280], P('wt'), may hold values from -0.15625 to 0.15625
- w_out: bfloat16 [1280, 1280], P('wt'), may hold values from -0.15625 to 0.15625
- gain_attn: float32 [1280], replicated, may hold values from 0.5 to 1.5
- gain_mlp: float32 [1280], replicated, may hold values from 0.5 to 1.5
- query_scale: float32 [80], replicated, may hold values from -0.5 to 1.5
- cotangent: bfloat16 [8, 2048, 1280], P(('grp', 'wt'), 'ctx'), may hold values from -6 to 6
Outputs:
- layer_out: bfloat16 [8, 2048, 1280], P(('grp', 'wt'), 'ctx')
- grad_tokens: bfloat16 [8, 2048, 1280], P(('grp', 'wt'), 'ctx')
- grad_w_qkv: float32 [1280, 3840], P('wt')
- grad_w_proj: float32 [1280, 1280], P('wt')
- grad_w_in: float32 [1280, 1280], P('wt')
- grad_w_out: float32 [1280, 1280], P('wt')
- grad_gain_attn: float32 [1280], replicated
- grad_gain_mlp: float32 [1280], replicated
- grad_query_scale: float32 [80], replicated
Inputs may be any that keep to these rules, and one draw needn't show every extreme that they name: `segments`: in each group the id starts at 0, never falls, and every id of 0 to 2 is used. Segment 0 ends 1024 - r tokens into the group, r below 256; each later continuation starts 512 + j tokens after the one before, j within 128 either way; the last runs to the group's end.
All inputs are finite; a program needn't handle non-finite values.
Results may differ from a plain program's by a relative error of at most 0.02.
Values may be sent and summed in bfloat16 or wider, within the bound.
No kernel may reach another device: no remote copies, remote signals or barrier semaphores. Data moves between devices by JAX's collectives and lax.ppermute only.
A program may use at most 256 MiB of HBM per device.

v0:
```python
import math

import jax
import jax.numpy as jnp
from jax import lax
from jax.sharding import PartitionSpec as P

D = 1280
H = 16
HD = 80


epsilon = 1e-06
scale_base = 1.442695041
masked_fill = -1e30


def rms_inverse(values):
    return lax.rsqrt(jnp.mean(values * values, axis=-1, keepdims=True) + epsilon)


def norm_back(values, inverse, grad_scaled):
    return inverse * grad_scaled - values * (inverse * inverse * inverse) * jnp.mean(
        grad_scaled * values, axis=-1, keepdims=True
    )


def times_trans(left, right):
    return lax.dot_general(
        left, right, (((1,), (1,)), ((), ())), preferred_element_type=jnp.float32
    )


def trans_times(left, right):
    return lax.dot_general(
        left, right, (((0,), (0,)), ((), ())), preferred_element_type=jnp.float32
    )


def visible(query_pos, query_seg, seg_row, offset, key_count):
    key_pos = offset + jnp.arange(key_count, dtype=jnp.int32)
    key_seg = lax.dynamic_slice_in_dim(seg_row, offset, key_count)
    return (key_pos[None, :] <= query_pos[:, None]) & (
        (key_seg[None, :] == 0) | (key_seg[None, :] == query_seg[:, None])
    )


def blocked(step_fn, carried, shard_rows):
    length = shard_rows.shape[0]
    width = math.gcd(length, 512)

    def advance(counter, carried_in):
        beginning = counter * width
        subrows = lax.dynamic_slice_in_dim(shard_rows, beginning, width, 0)
        return step_fn(carried_in, subrows, beginning)

    return lax.fori_loop(0, length // width, advance, carried)


def local(
    tokens, segments, w_qkv, w_proj, w_in, w_out, gain_attn, gain_mlp, query_scale, cotangent
):
    inputs = tokens[0].astype(jnp.float32)
    rows = inputs.shape[0]
    seg_row = segments[0]
    group_len = seg_row.shape[0]
    own_index = lax.axis_index("ctx")
    own_offset = own_index * rows
    query_pos = own_offset + jnp.arange(rows, dtype=jnp.int32)
    query_seg = lax.dynamic_slice_in_dim(seg_row, own_offset, rows)
    full_qkv, full_proj, full_in, full_out = (
        lax.all_gather(w_qkv, "wt", axis=0, tiled=True),
        lax.all_gather(w_proj, "wt", axis=0, tiled=True),
        lax.all_gather(w_in, "wt", axis=0, tiled=True),
        lax.all_gather(w_out, "wt", axis=0, tiled=True),
    )
    inverse_attn = rms_inverse(inputs)
    normed = (inputs * inverse_attn * gain_attn).astype(jnp.bfloat16)
    project = jnp.dot(normed, full_qkv, preferred_element_type=jnp.float32)
    dim_scale = scale_base / math.sqrt(HD) * jax.nn.softplus(query_scale)
    raw_queries = project[:, :D].reshape(rows, H, HD)
    queries = (raw_queries * dim_scale).astype(jnp.bfloat16)
    keyval = project[:, D:].astype(jnp.bfloat16)

    def forward_step(carried, subrows, offset):
        running_max, running_sum, accum = carried
        key_count = subrows.shape[0]
        keys_part = subrows[:, :D].reshape(key_count, H, HD)
        values_part = subrows[:, D:].reshape(key_count, H, HD)
        scores = jnp.einsum("qhd,khd->hqk", queries, keys_part, preferred_element_type=jnp.float32)
        allowed = visible(query_pos, query_seg, seg_row, offset, key_count)[None]
        masked = jnp.where(allowed, scores, masked_fill)
        new_max = jnp.maximum(running_max, jnp.max(masked, axis=-1))
        factor = jnp.exp(running_max - new_max)
        exponent = jnp.where(allowed, jnp.exp(masked - new_max[:, :, None]), 0.0)
        running_sum = running_sum * factor + jnp.sum(exponent, axis=-1)
        accum = accum * jnp.transpose(factor)[:, :, None] + jnp.einsum(
            "hqk,khd->qhd",
            exponent.astype(jnp.bfloat16),
            values_part,
            preferred_element_type=jnp.float32,
        )
        return (new_max, running_sum, accum)

    start_state = (
        jnp.full((H, rows), masked_fill, jnp.float32),
        jnp.zeros((H, rows), jnp.float32),
        jnp.zeros((rows, H, HD), jnp.float32),
    )
    running_max, running_sum, accum = blocked(
        forward_step, start_state, lax.all_gather(keyval, "ctx", axis=0, tiled=True)
    )
    logsum = running_max + jnp.log(running_sum)
    attn_float = accum / jnp.transpose(running_sum)[:, :, None]
    attended = attn_float.reshape(rows, D).astype(jnp.bfloat16)
    resid = inputs + jnp.dot(attended, full_proj, preferred_element_type=jnp.float32)
    inverse_mlp = rms_inverse(resid)
    normed_mlp = (resid * inverse_mlp * gain_mlp).astype(jnp.bfloat16)
    hidden = jnp.dot(normed_mlp, full_in, preferred_element_type=jnp.float32)
    active = jax.nn.silu(hidden).astype(jnp.bfloat16)
    layer_out = (resid + jnp.dot(active, full_out, preferred_element_type=jnp.float32)).astype(
        jnp.bfloat16
    )
    back_qkv, back_proj, back_in, back_out = (
        lax.all_gather(w_qkv, "wt", axis=0, tiled=True),
        lax.all_gather(w_proj, "wt", axis=0, tiled=True),
        lax.all_gather(w_in, "wt", axis=0, tiled=True),
        lax.all_gather(w_out, "wt", axis=0, tiled=True),
    )
    grad_out = cotangent[0].astype(jnp.float32)
    grad_mlp = cotangent[0]
    grad_active = times_trans(grad_mlp, back_out)
    grad_w_out = trans_times(active, grad_mlp)
    sigmoid_h = jax.nn.sigmoid(hidden)
    grad_hidden = (grad_active * sigmoid_h * (1.0 + hidden * (1.0 - sigmoid_h))).astype(
        jnp.bfloat16
    )
    grad_w_in = trans_times(normed_mlp, grad_hidden)
    grad_normed_mlp = times_trans(grad_hidden, back_in)
    grad_gain_mlp = jnp.sum(grad_normed_mlp * resid * inverse_mlp, axis=0)
    grad_resid = grad_out + norm_back(resid, inverse_mlp, grad_normed_mlp * gain_mlp)
    grad_proj = grad_resid.astype(jnp.bfloat16)
    grad_w_proj = trans_times(attended, grad_proj)
    grad_attended = times_trans(grad_proj, back_proj).astype(jnp.bfloat16).reshape(rows, H, HD)
    delta = jnp.transpose(jnp.sum(grad_attended.astype(jnp.float32) * attn_float, axis=-1))

    def backward_step(carried, subrows, offset):
        grad_queries, grad_keyval = carried
        key_count = subrows.shape[0]
        keys_part = subrows[:, :D].reshape(key_count, H, HD)
        values_part = subrows[:, D:].reshape(key_count, H, HD)
        scores = jnp.einsum("qhd,khd->hqk", queries, keys_part, preferred_element_type=jnp.float32)
        allowed = visible(query_pos, query_seg, seg_row, offset, key_count)[None]
        probs = jnp.where(
            allowed, jnp.exp(jnp.where(allowed, scores, masked_fill) - logsum[:, :, None]), 0.0
        )
        grad_probs = jnp.einsum(
            "qhd,khd->hqk", grad_attended, values_part, preferred_element_type=jnp.float32
        )
        grad_scores = (probs * (grad_probs - delta[:, :, None])).astype(jnp.bfloat16)
        grad_queries = grad_queries + jnp.einsum(
            "hqk,khd->qhd", grad_scores, keys_part, preferred_element_type=jnp.float32
        )
        grad_keys = jnp.einsum(
            "hqk,qhd->khd", grad_scores, queries, preferred_element_type=jnp.float32
        )
        grad_values = jnp.einsum(
            "hqk,qhd->khd",
            probs.astype(jnp.bfloat16),
            grad_attended,
            preferred_element_type=jnp.float32,
        )
        combined = jnp.concatenate(
            [grad_keys.reshape(key_count, D), grad_values.reshape(key_count, D)], axis=1
        )
        current = lax.dynamic_slice_in_dim(grad_keyval, offset, key_count, 0)
        grad_keyval = lax.dynamic_update_slice_in_dim(grad_keyval, current + combined, offset, 0)
        return (grad_queries, grad_keyval)

    back_state = (jnp.zeros((rows, H, HD), jnp.float32), jnp.zeros((group_len, 2 * D), jnp.float32))
    grad_queries, grad_keyval = blocked(
        backward_step, back_state, lax.all_gather(keyval, "ctx", axis=0, tiled=True)
    )
    grad_keyval_own = lax.psum_scatter(
        grad_keyval.astype(jnp.bfloat16), "ctx", scatter_dimension=0, tiled=True
    ).astype(jnp.float32)
    grad_dims = jnp.sum(grad_queries * raw_queries, axis=(0, 1))
    grad_query_scale = grad_dims * (scale_base / math.sqrt(HD)) * jax.nn.sigmoid(query_scale)
    grad_project = jnp.concatenate(
        [(grad_queries * dim_scale).reshape(rows, D), grad_keyval_own], axis=1
    ).astype(jnp.bfloat16)
    grad_w_qkv = trans_times(normed, grad_project)
    grad_normed = times_trans(grad_project, back_qkv)
    grad_gain_attn = jnp.sum(grad_normed * inputs * inverse_attn, axis=0)
    grad_tokens = (grad_resid + norm_back(inputs, inverse_attn, grad_normed * gain_attn)).astype(
        jnp.bfloat16
    )
    shard_qkv, shard_proj, shard_in, shard_out = (
        lax.psum_scatter(
            grad_w_qkv.astype(jnp.bfloat16), "wt", scatter_dimension=0, tiled=True
        ).astype(jnp.float32),
        lax.psum_scatter(
            grad_w_proj.astype(jnp.bfloat16), "wt", scatter_dimension=0, tiled=True
        ).astype(jnp.float32),
        lax.psum_scatter(
            grad_w_in.astype(jnp.bfloat16), "wt", scatter_dimension=0, tiled=True
        ).astype(jnp.float32),
        lax.psum_scatter(
            grad_w_out.astype(jnp.bfloat16), "wt", scatter_dimension=0, tiled=True
        ).astype(jnp.float32),
    )
    total_qkv, total_proj, total_in, total_out = (
        lax.psum(shard_qkv.astype(jnp.bfloat16), ("grp", "ctx")).astype(jnp.float32),
        lax.psum(shard_proj.astype(jnp.bfloat16), ("grp", "ctx")).astype(jnp.float32),
        lax.psum(shard_in.astype(jnp.bfloat16), ("grp", "ctx")).astype(jnp.float32),
        lax.psum(shard_out.astype(jnp.bfloat16), ("grp", "ctx")).astype(jnp.float32),
    )
    total_gain_attn, total_gain_mlp, total_scale = lax.psum(
        (grad_gain_attn, grad_gain_mlp, grad_query_scale), ("grp", "ctx", "wt")
    )
    return (
        layer_out[None],
        grad_tokens[None],
        total_qkv,
        total_proj,
        total_in,
        total_out,
        total_gain_attn,
        total_gain_mlp,
        total_scale,
    )


def solution(mesh):
    placed = (
        P(("grp", "wt"), "ctx", None),
        P(("grp", "wt"), None),
        P("wt", None),
        P("wt", None),
        P("wt", None),
        P("wt", None),
        P(),
        P(),
        P(),
        P(("grp", "wt"), "ctx", None),
    )
    return jax.shard_map(
        local,
        mesh=mesh,
        in_specs=placed,
        out_specs=(
            P(("grp", "wt"), "ctx", None),
            P(("grp", "wt"), "ctx", None),
            P("wt", None),
            P("wt", None),
            P("wt", None),
            P("wt", None),
            P(),
            P(),
            P(),
        ),
        check_vma=False,
    )
```

profile of v0, /device:TPU:0, one launch (start us, length us, event | category | flops | bytes accessed | tf_op | source)
XLA Modules:
  0.0 1364.7 jit_solution(8203904737533730321)
XLA Ops:
  9.4 125.2 %all-gather.6.cloned.1.call-done = bf16[1280,3840]{1,0:T(8,128)(2,1)} async-done(((bf16[640,3840]{1,0:T(8,128)(2,1)}), bf16[1280,3840]{1,0:T(8,128)(2,1)}) %all-gather.6.cloned.1.call-update) | async-done | bytes 9830416 | tf_op jit(solution)/shard_map/all_gather | solution.py:72
  156.3 175.1 %all-gather.8.cloned.1.call-done = bf16[2048,2560]{1,0:T(8,128)(2,1)} async-done(((bf16[512,2560]{1,0:T(8,128)(2,1)}), bf16[2048,2560]{1,0:T(8,128)(2,1)}) %all-gather.8.cloned.1.call-update) | async-done | bytes 10485776 | tf_op jit(solution)/shard_map/all_gather | solution.py:111
  331.5 14.6 %copy.34 = bf16[2048,2560]{0,1:T(8,128)(2,1)} copy(bf16[2048,2560]{1,0:T(8,128)(2,1)} %all-gather.8.cloned.1.call-done) | data formatting | bytes 20971520
  346.0 122.1 %while.34 = (s32[]{:T(128)}, f32[16,512]{1,0:T(8,128)S(1)}, f32[16,512]{1,0:T(8,128)S(1)}, f32[512,16,80]{0,2,1:T(8,128)}, s32[2048]{0:T(1024)S(1)}, /*index=5*/...) while((s32[]{:T(128)}, f32[16,512]{1,0:T(8,128)S(1)}, ...), condition=%wide.region_4.5_spmd.clone, body=%wide.region_1.4_spmd.clone.sunk | while | flops 1387185664 | bytes 66340068 | solution.py:57
  356.6 9.2 fusion.115
  365.8 9.7 bitcast_add_fusion.4
  386.8 10.0 fusion.115
  396.7 10.4 bitcast_add_fusion.4
  417.8 9.2 fusion.115
  427.0 10.7 bitcast_add_fusion.4
  448.4 9.2 fusion.115
  457.5 10.4 bitcast_add_fusion.4
  500.7 9.7 broadcast_in_dim.141
  510.3 188.2 %while.35 = (s32[]{:T(128)}, f32[512,16,80]{0,2,1:T(8,128)}, f32[2048,2560]{0,1:T(8,128)}, bf16[2048,2560]{0,1:T(8,128)(2,1)}, s32[2048]{0:T(1024)S(1)}, /*index...) while((s32[]{:T(128)}, f32[512,16,80]{0,2,1:T(8,128)}, ...), condition=%wide.region_9.10_spmd.clone, body=%wide.region_8.9_spmd.clone.sunk | while | flops 3402368512 | bytes 138003792 | solution.py:57
  523.1 11.4 fusion.130
  534.6 9.7 fusion.129
  568.7 11.4 fusion.130
  580.2 9.7 fusion.129
  616.1 11.4 fusion.130
  627.6 9.7 fusion.129
  663.5 11.4 fusion.130
  674.9 9.7 fusion.129
  698.6 12.3 convert_element_type.118
  736.2 151.1 %reduce-scatter.6.cloned.1.call-done = bf16[512,2560]{0,1:T(8,128)(2,1)} async-done(((bf16[2048,2560]{0,1:T(8,128)(2,1)}), bf16[512,2560]{0,1:T(8,128)(2,1)}) %reduce-scatter.6.cloned.1.call-update) | async-done | bytes 2621456 | tf_op jit(solution)/shard_map/reduce_scatter | solution.py:184
  887.3 10.8 convolution_convert_fusion
  898.4 37.6 %reduce-scatter.12.cloned.1.call-done = bf16[640,1280]{1,0:T(8,128)(2,1)} async-done(((bf16[1280,1280]{1,0:T(8,128)(2,1)}), bf16[640,1280]{1,0:T(8,128)(2,1)}) %reduce-scatter.12.cloned.1.call-update) | async-done | bytes 1638416 | tf_op jit(solution)/shard_map/reduce_scatter | solution.py:205
  936.0 47.7 %reduce-scatter.14.cloned.1.call-done = bf16[640,1280]{1,0:T(8,128)(2,1)} async-done(((bf16[1280,1280]{1,0:T(8,128)(2,1)}), bf16[640,1280]{1,0:T(8,128)(2,1)}) %reduce-scatter.14.cloned.1.call-update) | async-done | bytes 1638416 | tf_op jit(solution)/shard_map/reduce_scatter | solution.py:208
  983.7 47.6 %reduce-scatter.10.cloned.1.call-done = bf16[640,1280]{1,0:T(8,128)(2,1)} async-done(((bf16[1280,1280]{1,0:T(8,128)(2,1)}), bf16[640,1280]{1,0:T(8,128)(2,1)}) %reduce-scatter.10.cloned.1.call-update) | async-done | bytes 1638416 | tf_op jit(solution)/shard_map/reduce_scatter | solution.py:202
  1031.4 117.7 %reduce-scatter.8.cloned.1.call-done = bf16[640,3840]{1,0:T(8,128)(2,1)} async-done(((bf16[1280,3840]{1,0:T(8,128)(2,1)}), bf16[640,3840]{1,0:T(8,128)(2,1)}) %reduce-scatter.8.cloned.1.call-update) | async-done | bytes 4915216 | tf_op jit(solution)/shard_map/reduce_scatter | solution.py:199
  1156.6 12.2 fusion.40
  1168.8 41.6 %all-reduce = (f32[1280]{0:T(1024)}, f32[1280]{0:T(1024)}, f32[80]{0:T(128)}) all-reduce(f32[1280]{0:T(1024)S(1)} %get-tuple-element.469, f32[1280]{0:T(1024)S(1)} %copy-done.24, f32[80]{0:T(128)S(1)} %divide_multiply_fusion), channel_id=1, replica_groups=mesh['grp'=4,'ctx'=4,'wt'=2] {'grp','ctx','wt'}, use_global_device_ids=true, to_apply=%region_21.22 | all-reduce | flops 2640 | bytes 21120 | tf_op jit(solution)/shard_map/psum | solution.py:218
  1214.8 131.1 %all-reduce.4.cloned.1.call-done = (bf16[640,3840]{1,0:T(8,128)(2,1)}, bf16[640,1280]{1,0:T(8,128)(2,1)}, bf16[640,1280]{1,0:T(8,128)(2,1)}, bf16[640,1280]{1,0:T(8,128)(2,1)}) async-done(((bf16[640,3840]{1,0:T(8,128)(2,1)}, bf16[640,1280]{1,0:T(8,128)(2,1)}, bf16[640,1280]{1,0:T(8,128)(2,1)}, bf16[640,1280]{1,0:T(8,128)(2,1)}), (bf16[640,3840]{1,0:T(8,128)(2,1)}, bf16[640,1280]{1,0:T(8,128)(2,1)}, ...) | async-done | bytes 9830416 | tf_op jit(solution)/shard_map/psum | solution.py:213
  (222 shorter events, 251.7 us)
Async XLA Ops:
  7.2 127.5 %copy-start.19 = (f32[1280]{0:T(1024)S(1)}, f32[1280]{0:T(1024)}, u32[]{:S(2)}) copy-start(f32[1280]{0:T(1024)} %param.20) | copy-start | bytes 15364
  7.2 127.4 %all-gather.6.cloned.1.call-start = ((), (), s32[]{:S(2)}) async-start(), calls=%async_computation.5 | async-start | bytes 14745600 | tf_op jit(solution)/shard_map/all_gather | solution.py:72
  7.9 323.5 %all-gather.8.cloned.1.call-start = ((), (), s32[]{:S(2)}) async-start(), calls=%async_computation.6 | async-start | bytes 13107200 | tf_op jit(solution)/shard_map/all_gather | solution.py:111
  9.4 133.0 %copy-start.22 = (f32[512]{0:T(512)}, f32[512]{0:T(512)S(1)}, u32[]{:S(2)}) copy-start(f32[512]{0:T(512)S(1)} %get-tuple-element.537) | copy-start | bytes 6148
  147.4 324.0 %all-gather.10.cloned.1.call-start = ((), (), s32[]{:S(2)}) async-start(), calls=%async_computation.7 | async-start | bytes 4915200 | tf_op jit(solution)/shard_map/all_gather | solution.py:73
  148.1 329.1 %all-gather.12.cloned.1.call-start = ((), (), s32[]{:S(2)}) async-start(), calls=%async_computation.8 | async-start | bytes 4915200 | tf_op jit(solution)/shard_map/all_gather | solution.py:74
  148.7 334.9 %all-gather.14.cloned.1.call-start = ((), (), s32[]{:S(2)}) async-start(), calls=%async_computation.9 | async-start | bytes 4915200 | tf_op jit(solution)/shard_map/all_gather | solution.py:75
  149.3 738.0 %reduce-scatter.6.cloned.1.call-start = ((), (), s32[]{:S(2)}) async-start(), calls=%async_computation.10 | async-start | bytes 13107200 | tf_op jit(solution)/shard_map/reduce_scatter | solution.py:184
  150.0 3.9 copy-start.29
  471.4 5.9 copy-start.25
  477.2 14.2 %copy-start.27 = (f32[512]{0:T(512)}, f32[512]{0:T(512)S(1)}, u32[]{:S(2)}) copy-start(f32[512]{0:T(512)S(1)} %get-tuple-element.539) | copy-start | bytes 6148
  477.3 6.3 copy-start.16
  483.6 5.1 copy-start.6
  483.6 5.1 copy-start.31
  549.9 6.2 copy-start.12
  597.3 6.3 copy-start.12
  644.7 6.2 copy-start.12
  692.0 6.2 copy-start.12
  710.9 225.1 %reduce-scatter.12.cloned.1.call-start = ((), (), s32[]{:S(2)}) async-start(), calls=%async_computation.13 | async-start | bytes 4915200 | tf_op jit(solution)/shard_map/reduce_scatter | solution.py:205
  717.6 266.1 %reduce-scatter.14.cloned.1.call-start = ((), (), s32[]{:S(2)}) async-start(), calls=%async_computation.14 | async-start | bytes 4915200 | tf_op jit(solution)/shard_map/reduce_scatter | solution.py:208
  724.4 307.0 %reduce-scatter.10.cloned.1.call-start = ((), (), s32[]{:S(2)}) async-start(), calls=%async_computation.12 | async-start | bytes 4915200 | tf_op jit(solution)/shard_map/reduce_scatter | solution.py:202
  731.0 418.0 %reduce-scatter.8.cloned.1.call-start = ((), (), s32[]{:S(2)}) async-start(), calls=%async_computation.11 | async-start | bytes 14745600 | tf_op jit(solution)/shard_map/reduce_scatter | solution.py:199
  732.7 154.6 %copy-start.20 = (f32[1280]{0:T(1024)S(1)}, f32[1280]{0:T(1024)}, u32[]{:S(2)}) copy-start(f32[1280]{0:T(1024)} %param.20) | copy-start | bytes 15364
  732.7 154.6 %copy-start.23 = (f32[512]{0:T(512)S(1)}, f32[512]{0:T(512)}, u32[]{:S(2)}) copy-start(f32[512]{0:T(512)} %copy-done.22) | copy-start | bytes 6148
  898.2 447.7 %all-reduce.4.cloned.1.call-start = ((), (), s32[]{:S(2)}) async-start(), calls=%async_computation.15 | async-start | bytes 19660800 | tf_op jit(solution)/shard_map/psum | solution.py:213
  1149.7 6.9 copy-start.4
  1149.7 6.9 copy-start.15
  1149.7 6.9 copy-start.32
  1156.6 12.2 copy-start.24
  1156.6 53.7 %copy-start.21 = (f32[512]{0:T(512)S(1)}, f32[512]{0:T(512)}, u32[]{:S(2)}) copy-start(f32[512]{0:T(512)} %get-tuple-element.536) | copy-start | bytes 6148
  1345.9 7.5 slice-start.1
  1349.4 3.9 slice-start.2
  (27 other events, 54.0 us)
Sparse Core Ops, SparseCore 0:
  9.6 125.0 all-gather.5
  147.5 183.9 all-gather.7
  333.0 44.5 all-gather.9
  379.0 46.4 all-gather.11
  426.9 46.3 all-gather.13
  711.0 176.2 reduce-scatter.5
  890.1 45.8 reduce-scatter.11
  938.9 44.7 reduce-scatter.13
  986.5 44.7 reduce-scatter.9
  1034.2 114.7 reduce-scatter.7
  1153.0 192.8 all-reduce.3
where the time goes:
time: 1370 us; the launch traced here: 1360 us
  waiting for transfers between devices  836 us (61%)
  matrix products  296 us (22%)
  other arithmetic  108 us (8%)
  local copies, waits for them, and re-layouts  67.2 us (5%)
  blocking collectives  41.6 us (3%)
  between operations  14.4 us (1%)
    all_gather x1, waiting for transfers between devices, local(): lax.all_gather(keyval, 'ctx', axis=0, tiled=True)  175 us
    reduce_scatter x1, waiting for transfers between devices, local(): lax.psum_scatter(grad_keyval.astype(jnp.bfloat16), 'ctx', scatter_dimensi...  151 us
    psum x1, waiting for transfers between devices, local(): lax.psum(shard_qkv.astype(jnp.bfloat16), ('grp', 'ctx')).astype(jnp.float32)  131 us
    all_gather x1, waiting for transfers between devices, local(): lax.all_gather(w_qkv, 'wt', axis=0, tiled=True)  125 us
    reduce_scatter x1, waiting for transfers between devices, local(): lax.psum_scatter(grad_w_qkv.astype(jnp.bfloat16), 'wt', scatter_dimension...  118 us
    reduce_scatter x1, waiting for transfers between devices, local(): lax.psum_scatter(grad_w_out.astype(jnp.bfloat16), 'wt', scatter_dimension...  47.7 us
    reduce_scatter x1, waiting for transfers between devices, local(): lax.psum_scatter(grad_w_proj.astype(jnp.bfloat16), 'wt', scatter_dimensio...  47.6 us
    dot_general x4, matrix products, backward_step(): jnp.einsum('hqk,qhd->khd', probs.astype(jnp.bfloat16), grad_attended, pre...  45.8 us
  transfers between devices with their start and end apart: 11, of which 8 were waited for; matrix products, arithmetic and copies ran while one was open for 15% of the time, Pallas kernels for 0%

commit v1 on v0

v1 whole, which is shorter than its diff:
```python
import functools
import math

import jax
import jax.numpy as jnp
from jax import lax
from jax.experimental import pallas as pl
from jax.experimental.pallas import tpu as pltpu
from jax.sharding import Mesh
from jax.sharding import PartitionSpec as P

D = 1280
H = 16
HD = 80
LN = 128
epsilon = 1e-06
scale_base = 1.442695041
log2e = 1.4426950408889634
NEG = -1e30
f32 = jnp.float32
bf16 = jnp.bfloat16
AXES = ("gx", "gc", "ctx", "wt")


def block_flags(seg_row, bq, bk):
    n = seg_row.shape[0]
    q = seg_row.reshape(n // bq, bq)
    k = seg_row.reshape(n // bk, bk)
    qf, ql = q[:, 0][:, None], q[:, -1][:, None]
    kf, kl = k[:, 0][None], k[:, -1][None]
    qs = jnp.arange(n // bq, dtype=jnp.int32)[:, None] * bq
    ks = jnp.arange(n // bk, dtype=jnp.int32)[None] * bk
    below = ks + bk - 1 <= qs
    skip = (ks > qs + bq - 1) | ((kf > 0) & (kl < qf))
    same = (qf == ql) & (kl == ql) & ((kf == kl) | ((kf == 0) & (kl == 1)))
    full = below & ((kl == 0) | same)
    return jnp.where(skip, 0, jnp.where(full, 1, 2)).astype(jnp.int32).reshape(-1)


def put_split(base, col, lanes):
    hi = col.astype(bf16).astype(f32)
    rest = col - hi
    mid = rest.astype(bf16).astype(f32)
    out = jnp.where(lanes == HD, hi, base)
    out = jnp.where(lanes == HD + 1, mid, out)
    return jnp.where(lanes == HD + 2, rest - mid, out).astype(bf16)


def fwd_kernel(flags, q_ref, kv, segc, segr, att, of, qaug, m_s, acc_s, *, nh, bq, bk, nk):
    qi = pl.program_id(0)
    m_s[...] = jnp.full_like(m_s, NEG)
    acc_s[...] = jnp.zeros_like(acc_s)

    def step(kb, masked):
        ko = pl.multiple_of(kb * bk, bk)
        if masked:
            qpos = qi * bq + lax.broadcasted_iota(jnp.int32, (bq, bk), 0)
            kpos = ko + lax.broadcasted_iota(jnp.int32, (bq, bk), 1)
            ks = segr[:, pl.ds(ko, bk)]
            allowed = (kpos <= qpos) & ((ks == 0) | (ks == segc[...]))
        for h in range(nh):
            q = q_ref[:, h * LN : (h + 1) * LN]
            k = kv[pl.ds(ko, bk), h * LN : (h + 1) * LN]
            v = kv[pl.ds(ko, bk), (nh + h) * LN : (nh + h + 1) * LN]
            s = lax.dot_general(q, k, (((1,), (1,)), ((), ())), preferred_element_type=f32)
            if masked:
                s = jnp.where(allowed, s, NEG)
            old = m_s[h]
            new = jnp.maximum(old, jnp.max(s, axis=1, keepdims=True))
            p = jnp.exp2(s - new[:, :1]).astype(bf16)
            m_s[h] = new
            acc_s[h] = acc_s[h] * jnp.exp2(old - new) + jnp.dot(p, v, preferred_element_type=f32)

    def body(kb, carry):
        flag = flags[qi * nk + kb]

        @pl.when(flag == 1)
        def _():
            step(kb, False)

        @pl.when(flag == 2)
        def _():
            step(kb, True)

        return carry

    lax.fori_loop(0, (qi * bq + bq + bk - 1) // bk, body, 0)
    lanes = lax.broadcasted_iota(jnp.int32, (bq, LN), 1)
    outs = []
    for h in range(nh):
        acc = acc_s[h]
        total = acc[:, HD : HD + 1]
        out = acc / total
        of[:, h * LN : (h + 1) * LN] = jnp.where(lanes < HD, out, 0.0)
        outs.append(out[:, :HD])
        lse = m_s[h][:, :1] + jnp.log2(total)
        qaug[:, h * LN : (h + 1) * LN] = put_split(
            q_ref[:, h * LN : (h + 1) * LN].astype(f32), -lse, lanes
        )
    att[...] = jnp.concatenate(outs, axis=1).astype(bf16)


def attn_fwd(q, kv, seg_row, nh, bq=512, bk=512):
    n = q.shape[0]
    w = nh * LN
    spec = pltpu.PrefetchScalarGridSpec(
        num_scalar_prefetch=1,
        grid=(n // bq,),
        in_specs=[
            pl.BlockSpec((bq, w), lambda i, f: (i, 0)),
            pl.BlockSpec((n, 2 * w), lambda i, f: (0, 0)),
            pl.BlockSpec((bq, 1), lambda i, f: (i, 0)),
            pl.BlockSpec((1, n), lambda i, f: (0, 0)),
        ],
        out_specs=[
            pl.BlockSpec((bq, nh * HD), lambda i, f: (i, 0)),
            pl.BlockSpec((bq, w), lambda i, f: (i, 0)),
            pl.BlockSpec((bq, w), lambda i, f: (i, 0)),
        ],
        scratch_shapes=[pltpu.VMEM((nh, bq, LN), f32), pltpu.VMEM((nh, bq, LN), f32)],
    )
    return pl.pallas_call(
        functools.partial(fwd_kernel, nh=nh, bq=bq, bk=bk, nk=n // bk),
        out_shape=[
            jax.ShapeDtypeStruct((n, nh * HD), bf16),
            jax.ShapeDtypeStruct((n, w), f32),
            jax.ShapeDtypeStruct((n, w), bf16),
        ],
        grid_spec=spec,
        compiler_params=pltpu.CompilerParams(vmem_limit_bytes=40 << 20),
        cost_estimate=pl.CostEstimate(
            flops=20_000_000_000, transcendentals=10_000_000, bytes_accessed=16_000_000
        ),
        name="attn_fwd",
    )(block_flags(seg_row, bq, bk), q, kv, seg_row[:, None], seg_row[None])


def bwd_kernel(flags, qa, kv, do, of, segc, segr, scale, dqkv, gscale, doa_s, dq_s, dk_s, dv_s, *, nh, bq, bk, n):
    nk = n // bk
    nq = n // bq
    kb = pl.program_id(0)
    lanes = lax.broadcasted_iota(jnp.int32, (bq, LN), 1)

    @pl.when(kb == 0)
    def _():
        dq_s[...] = jnp.zeros_like(dq_s)

        def prep(i, carry):
            r = pl.multiple_of(i * bq, bq)
            d = do[pl.ds(r, bq), :].astype(f32)
            for h in range(nh):
                dh = jnp.concatenate(
                    [d[:, h * HD : (h + 1) * HD], jnp.zeros((bq, LN - HD), f32)], axis=1
                )
                delta = jnp.sum(dh * of[pl.ds(r, bq), h * LN : (h + 1) * LN], axis=1, keepdims=True)
                doa_s[pl.ds(r, bq), h * LN : (h + 1) * LN] = put_split(dh, -delta, lanes)
            return carry

        lax.fori_loop(0, nq, prep, 0)

    dk_s[...] = jnp.zeros_like(dk_s)
    dv_s[...] = jnp.zeros_like(dv_s)
    ko = kb * bk
    nt = (((1,), (1,)), ((), ()))
    tn = (((0,), (0,)), ((), ()))

    def step(qi, masked):
        qo = pl.multiple_of(qi * bq, bq)
        if masked:
            kpos = ko + lax.broadcasted_iota(jnp.int32, (bk, bq), 0)
            qpos = qo + lax.broadcasted_iota(jnp.int32, (bk, bq), 1)
            ks = segc[...]
            allowed = (kpos <= qpos) & ((ks == 0) | (ks == segr[:, pl.ds(qo, bq)]))
        for h in range(nh):
            c = slice(h * LN, (h + 1) * LN)
            q = qa[pl.ds(qo, bq), c]
            k = kv[:, c]
            v = kv[:, (nh + h) * LN : (nh + h + 1) * LN]
            d = doa_s[pl.ds(qo, bq), c]
            p = jnp.exp2(lax.dot_general(k, q, nt, preferred_element_type=f32))
            if masked:
                p = jnp.where(allowed, p, 0.0)
            ds = (p * lax.dot_general(v, d, nt, preferred_element_type=f32)).astype(bf16)
            dv_s[h] += jnp.dot(p.astype(bf16), d, preferred_element_type=f32)
            dk_s[h] += jnp.dot(ds, q, preferred_element_type=f32)
            dq_s[h, pl.ds(qo, bq), :] += lax.dot_general(ds, k, tn, preferred_element_type=f32)

    def body(qi, carry):
        flag = flags[qi * nk + kb]

        @pl.when(flag == 1)
        def _():
            step(qi, False)

        @pl.when(flag == 2)
        def _():
            step(qi, True)

        return carry

    lax.fori_loop(ko // bq, nq, body, 0)
    r = pl.multiple_of(ko, bk)
    ln2 = math.log(2.0)
    dqkv[pl.ds(r, bk), nh * HD : 3 * nh * HD] = jnp.concatenate(
        [dk_s[h][:, :HD] * ln2 for h in range(nh)] + [dv_s[h][:, :HD] for h in range(nh)], axis=1
    ).astype(bf16)

    @pl.when(kb == nk - 1)
    def _():
        gscale[...] = jnp.zeros_like(gscale)

        def fin(i, carry):
            r = pl.multiple_of(i * bq, bq)
            rows = pl.ds(r, bq)
            part = jnp.zeros((1, LN), f32)
            for h in range(nh):
                part = part + jnp.sum(
                    dq_s[h, rows, :] * qa[rows, h * LN : (h + 1) * LN].astype(f32), axis=0, keepdims=True
                )
            gscale[...] += jnp.broadcast_to(part, gscale.shape)
            grads = jnp.concatenate([dq_s[h, rows, :][:, :HD] for h in range(nh)], axis=1)
            dqkv[rows, 0 : nh * HD] = (grads * scale[...]).astype(bf16)
            return carry

        lax.fori_loop(0, nq, fin, 0)


def attn_bwd(qa, kv, do, of, seg_row, scale, nh, bq=512, bk=512):
    n = qa.shape[0]
    w = nh * LN
    spec = pltpu.PrefetchScalarGridSpec(
        num_scalar_prefetch=1,
        grid=(n // bk,),
        in_specs=[
            pl.BlockSpec((n, w), lambda i, f: (0, 0)),
            pl.BlockSpec((bk, 2 * w), lambda i, f: (i, 0)),
            pl.BlockSpec((n, nh * HD), lambda i, f: (0, 0)),
            pl.BlockSpec((n, w), lambda i, f: (0, 0)),
            pl.BlockSpec((bk, 1), lambda i, f: (i, 0)),
            pl.BlockSpec((1, n), lambda i, f: (0, 0)),
            pl.BlockSpec((1, nh * HD), lambda i, f: (0, 0)),
        ],
        out_specs=[
            pl.BlockSpec((n, 3 * nh * HD), lambda i, f: (0, 0)),
            pl.BlockSpec((8, LN), lambda i, f: (0, 0)),
        ],
        scratch_shapes=[
            pltpu.VMEM((n, w), bf16),
            pltpu.VMEM((nh, n, LN), f32),
            pltpu.VMEM((nh, bk, LN), f32),
            pltpu.VMEM((nh, bk, LN), f32),
        ],
    )
    return pl.pallas_call(
        functools.partial(bwd_kernel, nh=nh, bq=bq, bk=bk, n=n),
        out_shape=[
            jax.ShapeDtypeStruct((n, 3 * nh * HD), bf16),
            jax.ShapeDtypeStruct((8, LN), f32),
        ],
        grid_spec=spec,
        compiler_params=pltpu.CompilerParams(vmem_limit_bytes=48 << 20),
        cost_estimate=pl.CostEstimate(
            flops=40_000_000_000, transcendentals=10_000_000, bytes_accessed=20_000_000
        ),
        name="attn_bwd",
    )(block_flags(seg_row, bq, bk), qa, kv, do, of, seg_row[:, None], seg_row[None], scale)


def rms_inverse(values):
    return lax.rsqrt(jnp.mean(values * values, axis=-1, keepdims=True) + epsilon)


def norm_back(values, inverse, grad_scaled):
    return inverse * grad_scaled - values * (inverse * inverse * inverse) * jnp.mean(
        grad_scaled * values, axis=-1, keepdims=True
    )


def dot(left, right):
    return jnp.dot(left, right, preferred_element_type=f32)


def times_trans(left, right):
    return lax.dot_general(left, right, (((1,), (1,)), ((), ())), preferred_element_type=f32)


def trans_times(left, right):
    return lax.dot_general(left, right, (((0,), (0,)), ((), ())), preferred_element_type=f32)


def rows_at(array, start, count):
    return lax.dynamic_slice_in_dim(array, start, count, 0)


def put_rows(array, rows, start):
    return lax.dynamic_update_slice_in_dim(array, rows, start, 0)


def make_local(sizes):
    def pairs(target):
        found = []
        for gx in range(sizes["gx"]):
            for gc in range(sizes["gc"]):
                for z in range(sizes["ctx"]):
                    for w in range(sizes["wt"]):
                        goal = target(gx, gc, z, w)
                        if goal is not None:
                            found.append((place(gx, gc, z, w), place(*goal)))
        return found

    def place(gx, gc, z, w):
        return ((gx * sizes["gc"] + gc) * sizes["ctx"] + z) * sizes["wt"] + w

    def send(value, target):
        return lax.ppermute(value, AXES, pairs(target))

    def core_mate(gx, gc, z, w):
        return (gx, 1 - gc, z, w)

    def x_mate(gx, gc, z, w):
        return (1 - gx, gc, z, w)

    def near_mate(gx, gc, z, w):
        return (gx, gc, z ^ 1, w)

    def far_mate(gx, gc, z, w):
        return (gx, gc, z ^ 2, w)

    def cross_mate(gx, gc, z, w):
        return (gx, 1 - gc, z ^ 1, w)

    def wt_mate(gx, gc, z, w):
        return (gx, gc, z, 1 - w)

    def to_host(gx, gc, z, w):
        return (gx, z & 1, 2 * gc + (z >> 1), w)

    def to_home(gx, gc, z, w):
        return (gx, z >> 1, 2 * (z & 1) + gc, w)

    def hop1(gx, gc, z, w):
        if gc == 0:
            return (gx, 0, z - 1, w) if z > 0 else None
        return (gx, 1, z + 1, w) if z < 3 else None

    def hop2(gx, gc, z, w):
        if gc == 0:
            return (gx, 0, z - 1, w) if z in (1, 2) else None
        return (gx, 1, z + 1, w) if z in (1, 2) else None

    def hop3(gx, gc, z, w):
        if gc == 0:
            return (gx, 0, z ^ 1, w) if z < 2 else None
        return (gx, 1, z ^ 1, w) if z > 1 else None

    def lane_share(gx, gc, z, w):
        return (gx, 1 - gc, z, w) if gc == z >> 1 else None

    def gather_wt(value):
        if sizes["wt"] == 2:
            other = send(value, wt_mate)
            first = lax.axis_index("wt") == 0
            return jnp.stack([jnp.where(first, value, other), jnp.where(first, other, value)])
        return lax.all_gather(value, "wt", axis=0, tiled=False)

    def scatter_wt(value):
        if sizes["wt"] == 2:
            own = lax.axis_index("wt")
            mine = lax.dynamic_index_in_dim(value, own, 0, keepdims=False)
            other = send(lax.dynamic_index_in_dim(value, 1 - own, 0, keepdims=False), wt_mate)
            return (mine.astype(f32) + other.astype(f32)).astype(bf16)
        return lax.psum_scatter(value, "wt", scatter_dimension=0, tiled=False)

    def halve(value, bit, mate):
        half = value.shape[0] // 2
        other = send(rows_at(value, (1 - bit) * half, half), mate)
        return (rows_at(value, bit * half, half).astype(f32) + other.astype(f32)).astype(bf16)

    def double(value, bit, mate):
        other = send(value, mate)
        first = bit == 0
        return jnp.stack([jnp.where(first, value, other), jnp.where(first, other, value)])

    def sum_all(value):
        for axis in AXES:
            step = 1
            while step < sizes[axis]:

                def mate(gx, gc, z, w, axis=axis, step=step):
                    at = dict(gx=gx, gc=gc, ctx=z, wt=w)
                    at[axis] ^= step
                    return (at["gx"], at["gc"], at["ctx"], at["wt"])

                value = value + send(value, mate)
                step *= 2
        return value

    def local(
        tokens, segments, w_qkv, w_proj, w_in, w_out, gain_attn, gain_mlp, query_scale, cotangent
    ):
        gx, gc, z, wt = (lax.axis_index(axis) for axis in AXES)
        host = z // 2
        near = z % 2
        mine = 2 * near + gc
        parts = sizes["ctx"]
        nh = H // parts
        rows = tokens.shape[1]
        group_len = segments.shape[1]
        wrows = w_qkv.shape[0]
        cols = nh * HD
        lane = gc == host

        def quarter(full):
            pieces = [
                jnp.concatenate([full[:, t * D + i * cols : t * D + (i + 1) * cols] for t in range(3)], axis=1)
                for i in range(parts)
            ]
            out = pieces[0]
            for i in range(1, parts):
                out = jnp.where(mine == i, pieces[i], out)
            return out

        qkv_w = gather_wt(quarter(w_qkv)).reshape(-1, 3 * cols)
        half_rows = wrows // 2
        half_w = jnp.concatenate(
            [rows_at(w, gc * half_rows, half_rows) for w in (w_proj, w_in, w_out)], axis=1
        )
        tail_w = double(gather_wt(half_w), gc, core_mate)
        tail_w = jnp.transpose(tail_w, (1, 0, 2, 3)).reshape(-1, 3 * D)
        full_proj, full_in, full_out = tail_w[:, :D], tail_w[:, D : 2 * D], tail_w[:, 2 * D :]
        proj_perm = jnp.concatenate([rows_at(full_proj, (mine ^ j) * cols, cols) for j in range(parts)])

        own = tokens[0]
        seg_row = jnp.where(lane, segments, send(segments, core_mate))[0]
        got1 = send(own, hop1)
        got2 = send(got1, hop2)
        end = jnp.where(gc == 0, z == 0, z == 3)
        got3 = send(jnp.where(end, own, got2), hop3)
        way = 1 - 2 * host
        last = jnp.where(host == 0, jnp.where(z == 0, 3, 0), jnp.where(z == 3, 0, 3))
        places = (z, z + way, z + 2 * way, last)
        padded_w = jnp.pad(qkv_w.reshape(D, 3 * nh, HD), ((0, 0), (0, 0), (0, LN - HD))).reshape(D, -1)
        dim_scale = scale_base / math.sqrt(HD) * jax.nn.softplus(query_scale)
        lane_scale = jnp.tile(jnp.pad(dim_scale * log2e, (0, LN - HD)), nh)[None]
        ones = jnp.tile(
            ((jnp.arange(LN) >= HD) & (jnp.arange(LN) < HD + 3)).astype(f32), 2 * nh
        )[None]
        all_tokens = jnp.zeros((group_len, D), bf16)
        all_normed = jnp.zeros((group_len, D), bf16)
        queries = jnp.zeros((group_len, nh * LN), bf16)
        keyval = jnp.zeros((group_len, 2 * nh * LN), bf16)
        for shard, at in zip((own, got1, got2, got3), places):
            shard = jnp.where(lane, shard, send(shard, lane_share))
            inputs = shard.astype(f32)
            normed = (inputs * rms_inverse(inputs) * gain_attn).astype(bf16)
            project = dot(normed, padded_w)
            at = at * rows
            all_tokens = put_rows(all_tokens, shard, at)
            all_normed = put_rows(all_normed, normed, at)
            queries = put_rows(queries, (project[:, : nh * LN] * lane_scale).astype(bf16), at)
            keyval = put_rows(keyval, (project[:, nh * LN :] + ones).astype(bf16), at)

        att, att_float, q_aug = attn_fwd(queries, keyval, seg_row, nh)

        trades = (core_mate, near_mate, cross_mate)
        inputs = rows_at(all_tokens, mine * rows, rows).astype(f32)
        grad_mlp = send(cotangent[0], to_host)
        attended = jnp.concatenate(
            [rows_at(att, mine * rows, rows)]
            + [send(rows_at(att, (mine ^ (j + 1)) * rows, rows), trades[j]) for j in range(3)],
            axis=1,
        )
        resid = inputs + dot(attended, proj_perm)
        inverse_mlp = rms_inverse(resid)
        normed_mlp = (resid * inverse_mlp * gain_mlp).astype(bf16)
        hidden = dot(normed_mlp, full_in)
        active = jax.nn.silu(hidden).astype(bf16)
        layer_out = send((resid + dot(active, full_out)).astype(bf16), to_home)

        grad_out = grad_mlp.astype(f32)
        grad_active = times_trans(grad_mlp, full_out)
        sigmoid_h = jax.nn.sigmoid(hidden)
        grad_hidden = (grad_active * sigmoid_h * (1.0 + hidden * (1.0 - sigmoid_h))).astype(bf16)
        grad_normed_mlp = times_trans(grad_hidden, full_in)
        grad_gain_mlp = jnp.sum(grad_normed_mlp * resid * inverse_mlp, axis=0)
        grad_resid = grad_out + norm_back(resid, inverse_mlp, grad_normed_mlp * gain_mlp)
        grad_proj = grad_resid.astype(bf16)
        grad_attended = times_trans(grad_proj, proj_perm).astype(bf16)
        grad_heads = jnp.zeros((group_len, cols), bf16)
        for j in range(parts):
            piece = grad_attended[:, j * cols : (j + 1) * cols]
            if j:
                piece = send(piece, trades[j - 1])
            grad_heads = put_rows(grad_heads, piece, (mine ^ j) * rows)

        grad_perm = trans_times(attended, grad_proj).astype(bf16)
        grad_w_proj = jnp.zeros((D, D), bf16)
        for j in range(parts):
            grad_w_proj = put_rows(grad_w_proj, grad_perm[j * cols : (j + 1) * cols], (mine ^ j) * cols)
        grad_tail = jnp.concatenate(
            [
                grad_w_proj,
                trans_times(normed_mlp, grad_hidden).astype(bf16),
                trans_times(active, grad_mlp).astype(bf16),
            ],
            axis=1,
        )
        grad_tail = jnp.transpose(grad_tail.reshape(-1, 2, half_rows, 3 * D), (1, 0, 2, 3))
        grad_tail = halve(grad_tail.reshape(-1, half_rows, 3 * D), gc, core_mate)
        grad_tail = lax.psum(scatter_wt(grad_tail), ("gx", "ctx"))
        total_tail = double(grad_tail, gc, core_mate).reshape(wrows, 3 * D).astype(f32)

        grad_project, grad_lanes = attn_bwd(
            q_aug, keyval, grad_heads, att_float, seg_row, jnp.tile(dim_scale, nh)[None], nh
        )
        grad_query_scale = (
            grad_lanes[0, :HD]
            / (dim_scale * log2e)
            * (scale_base / math.sqrt(HD))
            * jax.nn.sigmoid(query_scale)
        )
        grad_normed = times_trans(grad_project, qkv_w).reshape(2, 2, rows, D)
        to_core = lax.dynamic_index_in_dim(grad_normed, 1 - gc, 1, keepdims=False).astype(bf16)
        keep = lax.dynamic_index_in_dim(grad_normed, gc, 1, keepdims=False) + send(
            to_core, core_mate
        ).astype(f32)
        to_near = lax.dynamic_index_in_dim(keep, 1 - near, 0, keepdims=False).astype(bf16)
        grad_normed = lax.dynamic_index_in_dim(keep, near, 0, keepdims=False) + send(
            to_near, near_mate
        ).astype(f32)
        inverse_attn = rms_inverse(inputs)
        grad_gain_attn = jnp.sum(grad_normed * inputs * inverse_attn, axis=0)
        grad_tokens = send(
            (grad_resid + norm_back(inputs, inverse_attn, grad_normed * gain_attn)).astype(bf16), to_home
        )

        grad_qkv = trans_times(all_normed, grad_project).astype(bf16).reshape(-1, wrows, 3 * cols)
        grad_qkv = scatter_wt(grad_qkv)
        grad_qkv = halve(grad_qkv, gx, x_mate)
        grad_qkv = halve(grad_qkv, host, far_mate)
        grad_qkv = double(grad_qkv, host, far_mate).reshape(-1, 3 * cols)
        grad_qkv = double(grad_qkv, gx, x_mate).reshape(wrows, 3 * cols)
        grad_qkv = double(double(grad_qkv, near, near_mate), gc, core_mate)
        total_qkv = jnp.concatenate(
            [
                grad_qkv[i % 2, i // 2, :, t * cols : (t + 1) * cols]
                for t in range(3)
                for i in range(parts)
            ],
            axis=1,
        ).astype(f32)

        small = jnp.concatenate(
            [grad_gain_attn, grad_gain_mlp, jnp.pad(grad_query_scale, (0, LN - HD))]
        ).reshape(-1, LN)
        small = sum_all(small).reshape(-1)
        return (
            layer_out[None],
            grad_tokens[None],
            total_qkv,
            total_tail[:, :D],
            total_tail[:, D : 2 * D],
            total_tail[:, 2 * D :],
            small[:D],
            small[D : 2 * D],
            small[2 * D : 2 * D + HD],
        )

    return local


def solution(mesh):
    groups, parts, wt = (mesh.shape[axis] for axis in ("grp", "ctx", "wt"))
    inner = Mesh(mesh.devices.reshape(groups // 2, 2, parts, wt), AXES)
    sizes = dict(inner.shape)
    split = P(("gx", "gc", "wt"), "ctx", None)
    weight = P("wt", None)
    return jax.shard_map(
        make_local(sizes),
        mesh=inner,
        in_specs=(
            split,
            P(("gx", "gc", "wt"), None),
            weight,
            weight,
            weight,
            weight,
            P(),
            P(),
            P(),
            split,
        ),
        out_specs=(split, split, weight, weight, weight, weight, P(), P(), P()),
        check_vma=False,
    )
```

time: 1370 us -> 805 us (0.59)
  waiting for transfers between devices: 836 us -> 251 us
  matrix products: 296 us -> 57.3 us
  local copies, waits for them, and re-layouts: 67.2 us -> 215 us
  starting transfers between devices: 1.14 us -> 96.2 us
  Pallas kernels: 0 us -> 81.4 us
  blocking collectives: 41.6 us -> 0 us
  other arithmetic: 108 us -> 78.4 us
    reduce_scatter x5 -> x0, waiting for transfers between devices: 402 us -> none  [the longest x1 151 us: local(): lax.psum_scatter(grad_keyval.astype(jnp.bfloat16), 'ctx', scatter_dimensi...]
    all_gather x5 -> x0, waiting for transfers between devices: 300 us -> none  [the longest x1 175 us: local(): lax.all_gather(keyval, 'ctx', axis=0, tiled=True)]
    dot_general x32 -> x7, matrix products: 247 us -> 22 us  [dot(): return jnp.dot(left, right, preferred_element_type=f32)]
    ppermute x0 -> x37, waiting for transfers between devices: none -> 208 us  [send(): return lax.ppermute(value, AXES, pairs(target))]
    ppermute x0 -> x37, starting transfers between devices: none -> 96.2 us  [send(): return lax.ppermute(value, AXES, pairs(target))]
    psum x1, waiting for transfers between devices: 131 us -> 43.1 us  [local(): grad_tail = lax.psum(scatter_wt(grad_tail), ('gx', 'ctx'))]
    pallas_call x0 -> x2, Pallas kernels: none -> 81.4 us  [the longest x1 44.8 us: attn_bwd(): pl.pallas_call(functools.partial(bwd_kernel, nh=nh, bq=bq, bk=bk, n=n), o...]
    dynamic_update_slice x0 -> x7, local copies, waits for them, and re-layouts: none -> 45.2 us  [put_rows(): return lax.dynamic_update_slice_in_dim(array, rows, start, 0)]
  transfers between devices with their start and end apart: 11 -> 38, of which waited for: 8 -> 19; matrix products, arithmetic and copies ran while one was open for 15% -> 38% of each run, Pallas kernels for 0% -> 10%
where the time goes in v1:
time: 805 us; the launch traced here: 795 us
  waiting for transfers between devices  251 us (31%)
  local copies, waits for them, and re-layouts  215 us (27%)
  starting transfers between devices  96.2 us (12%)
  Pallas kernels  81.4 us (10%)
  other arithmetic  78.4 us (10%)
  matrix products  57.3 us (7%)
  between operations  15.6 us (2%)
    ppermute x37, waiting for transfers between devices, send(): return lax.ppermute(value, AXES, pairs(target))  208 us
    ppermute x37, starting transfers between devices, send(): return lax.ppermute(value, AXES, pairs(target))  96.2 us
    unnamed x137, local copies, waits for them, and re-layouts  62.9 us
    dynamic_update_slice x7, local copies, waits for them, and re-layouts, put_rows(): return lax.dynamic_update_slice_in_dim(array, rows, start, 0)  45.2 us
    pallas_call x1, Pallas kernels, attn_bwd(): pl.pallas_call(functools.partial(bwd_kernel, nh=nh, bq=bq, bk=bk, n=n), o...  44.8 us
    psum x1, waiting for transfers between devices, local(): grad_tail = lax.psum(scatter_wt(grad_tail), ('gx', 'ctx'))  43.1 us
    pallas_call x1, Pallas kernels, attn_fwd(): pl.pallas_call(functools.partial(fwd_kernel, nh=nh, bq=bq, bk=bk, nk=n //...  36.6 us
    another operation x11, other arithmetic, double(): jnp.stack([jnp.where(first, value, other), jnp.where(first, other, value)])  27.7 us
  transfers between devices with their start and end apart: 38, of which 19 were waited for; matrix products, arithmetic and copies ran while one was open for 38% of the time, Pallas kernels for 10%

profile of v1, /device:TPU:0, one launch (start us, length us, event | category | flops | bytes accessed | tf_op | source)
XLA Modules:
  0.0 795.1 jit_solution(16481404796989961395)
XLA Ops:
  14.2 6.6 fusion.83
  48.9 11.4 %collective-permute-start.15 = (bf16[512,1280]{1,0:T(8,128)(2,1)}, bf16[512,1280]{1,0:T(8,128)(2,1)}, u32[]{:S(2)}, u32[]{:S(2)}) collective-permute-start(bf16[512,1280]{1,0:T(8,128)(2,1)} %bitcast.226), channel_id=1, source_target_pairs={{0,0},{1,1},{2,8},{3,9},{4,2},{5,3},{6,10},{7,11},{8,4},{9,5},{10,... | collective-permute-start | bytes 3932168 | tf_op jit(solution)/shard_map/ppermute | solution.py:315
  62.4 10.8 %collective-permute-done.8 = bf16[640,960]{0,1:T(8,128)(2,1)} collective-permute-done((bf16[640,960]{0,1:T(8,128)(2,1)}, bf16[640,960]{0,1:T(8,128)(2,1)}, u32[]{:S(2)}, u32[]{:S(2)}) %collective-permute-start.8) | collective-permute-done | bytes 1228832 | tf_op jit(solution)/shard_map/ppermute | solution.py:315
  79.3 6.6 reshape_reshape.3
  97.5 27.3 %collective-permute-done.12 = bf16[320,3840]{1,0:T(8,128)(2,1)} collective-permute-done((bf16[320,3840]{1,0:T(8,128)(2,1)}, bf16[320,3840]{1,0:T(8,128)(2,1)}, u32[]{:S(2)}, u32[]{:S(2)}) %collective-permute-start.12) | collective-permute-done | bytes 2457632 | tf_op jit(solution)/shard_map/ppermute | solution.py:315
  150.6 9.6 %collective-permute-done.5 = bf16[512,1280]{1,0:T(8,128)(2,1)S(1)} collective-permute-done((bf16[512,1280]{1,0:T(8,128)(2,1)S(1)}, bf16[512,1280]{1,0:T(8,128)(2,1)S(1)}, u32[]{:S(2)}, u32[]{:S(2)}) %collective-permute-start.5) | collective-permute-done | bytes 1310752 | tf_op jit(solution)/shard_map/ppermute | solution.py:315
  170.4 36.6 %attn_fwd.1 = (bf16[2048,320]{1,0:T(8,128)(2,1)S(1)}, f32[2048,512]{1,0:T(8,128)S(1)}, bf16[2048,512]{1,0:T(8,128)(2,1)S(1)}) custom-call(s32[16]{0:T(128)S(1)} %reshape.249.flags, bf16[2048,512]{1,0:T(8,128)(2,1)S(1)} %fusion.53.q_ref, bf16[2048,1024]{1,0:T(8,128)(2,1)} %copy-done.21, s32[2048,1]{1,0:T(8,128)S(1)} %copy.63.segc, ...), custom_call_target="tpu_custom_call" | custom-call | flops 20000000000 | bytes 16000000 | tf_op jit(solution)/shard_map/attn_fwd/pallas_call | solution.py:122
  213.6 7.2 collective-permute-done.10
  220.7 7.9 collective-permute-done.11
  232.5 8.7 %select_bitcast_fusion.1 = (bf16[1,2,320,3840]{3,2,0,1:T(8,128)(2,1)}, bf16[1,2,320,3840]{3,2,0,1:T(8,128)(2,1)}) fusion(bf16[2,320,3840]{2,1,0:T(8,128)(2,1)} %collective-permute-done.13, pred[]{:T(512)S(6)} %eq.103, bf16[1,320,3840]{2,1,0:T(8,128)(2,1)} %copy-done.7, bf16[1,320,3840]{2,1,0:T(8,128)(2,1)} %copy-done.6), kind=kLoop, calls=%fused_computation.19 | loop fusion | flops 7372800 | bytes 19660800 | tf_op jit(solution)/shard_map/stack | solution.py:382
  241.1 8.6 %pad_maximum_fusion = bf16[2,2,320,3840]{3,2,0,1:T(8,128)(2,1)} fusion(bf16[1,2,320,3840]{3,2,0,1:T(8,128)(2,1)} %get-tuple-element.48, bf16[1,2,320,3840]{3,2,0,1:T(8,128)(2,1)} %get-tuple-element.47), kind=kLoop, calls=%fused_computation | loop fusion | flops 4915200 | bytes 19660800 | tf_op jit(solution)/shard_map/stack | solution.py:382
  294.1 10.3 %dynamic_update_slice.92 = bf16[1280,1280]{0,1:T(8,128)(2,1)} dynamic-update-slice(bf16[1280,1280]{0,1:T(8,128)(2,1)} %broadcast_in_dim.60, bf16[320,1280]{0,1:T(8,128)(2,1)} %copy.78, s32[]{:T(128)S(6)} %select_n.332, s32[]{:T(128)} %constant.111.clone.1) | dynamic-update-slice | bytes 1638404 | tf_op jit(solution)/shard_map/dynamic_update_slice | solution.py:296
  304.4 11.6 %dynamic_update_slice.93 = bf16[1280,1280]{0,1:T(8,128)(2,1)} dynamic-update-slice(bf16[1280,1280]{0,1:T(8,128)(2,1)} %dynamic_update_slice.92, bf16[320,1280]{0,1:T(8,128)(2,1)} %copy.79, s32[]{:T(128)S(6)} %select_n.333, s32[]{:T(128)} %constant.111.clone.1) | dynamic-update-slice | bytes 1638404 | tf_op jit(solution)/shard_map/dynamic_update_slice | solution.py:296
  316.0 10.2 %dynamic_update_slice.94 = bf16[1280,1280]{0,1:T(8,128)(2,1)} dynamic-update-slice(bf16[1280,1280]{0,1:T(8,128)(2,1)} %dynamic_update_slice.93, bf16[320,1280]{0,1:T(8,128)(2,1)} %copy.80, s32[]{:T(128)S(6)} %select_n.334, s32[]{:T(128)} %constant.111.clone.1) | dynamic-update-slice | bytes 1638404 | tf_op jit(solution)/shard_map/dynamic_update_slice | solution.py:296
  326.2 10.9 %dynamic_update_slice.95 = bf16[1280,1280]{0,1:T(8,128)(2,1)} dynamic-update-slice(bf16[1280,1280]{0,1:T(8,128)(2,1)} %dynamic_update_slice.94, bf16[320,1280]{0,1:T(8,128)(2,1)} %copy.81, s32[]{:T(128)S(6)} %select_n.335, s32[]{:T(128)} %constant.111.clone.1) | dynamic-update-slice | bytes 1638404 | tf_op jit(solution)/shard_map/dynamic_update_slice | solution.py:296
  345.8 13.8 %copy.82 = bf16[1280,3840]{1,0:T(8,128)(2,1)} copy(bf16[1280,3840]{0,1:T(8,128)(2,1)} %pad_maximum_fusion.1) | data formatting | bytes 19660800 | tf_op jit(solution)/shard_map/concatenate | solution.py:500
  359.6 8.1 %copy.83 = bf16[2,2,320,3840]{3,2,1,0:T(8,128)(2,1)} copy(bf16[2,2,320,3840]{3,2,0,1:T(8,128)(2,1)} %bitcast.199) | data formatting | bytes 19660800 | tf_op jit(solution)/shard_map/transpose | solution.py:508
  375.4 44.8 %attn_bwd.1 = (bf16[2048,960]{1,0:T(8,128)(2,1)}, f32[8,128]{1,0:T(8,128)S(1)}) custom-call(s32[16]{0:T(128)S(1)} %reshape.249.flags, bf16[2048,512]{1,0:T(8,128)(2,1)S(1)} %copy-done.4, bf16[2048,1024]{1,0:T(8,128)(2,1)} %copy-done.21, bf16[2048,320]{1,0:T(8,128)(2,1)S(1)} %constant_dynamic-update-slice_fusion.do, f32[2048,512]{1,0:T(8,128)} %copy-done.2, ...), custom_call_target="tpu_custom_call" | custom-call | flops 40000000000 | bytes 20000000 | tf_op jit(solution)/shard_map/attn_bwd/pallas_call | solution.py:254
  420.3 9.0 %convolution_convert_fusion.3 = bf16[1280,960]{0,1:T(8,128)(2,1)} fusion(bf16[2048,1280]{1,0:T(8,128)(2,1)S(1)} %bitcast.212, bf16[2048,960]{1,0:T(8,128)(2,1)} %get-tuple-element.17), kind=kOutput, calls=%fused_computation.20 | convolution fusion | flops 5034393600 | bytes 11632640 | tf_op jit(solution)/shard_map/dot_general | solution.py:288
  435.3 7.6 constant_dynamic-slice_fusion.4
  453.3 19.4 %collective-permute-done.22 = bf16[640,960]{0,1:T(8,128)(2,1)S(1)} collective-permute-done((bf16[640,960]{0,1:T(8,128)(2,1)S(1)}, bf16[640,960]{0,1:T(8,128)(2,1)S(1)}, u32[]{:S(2)}, u32[]{:S(2)}) %collective-permute-start.22) | collective-permute-done | bytes 1228832 | tf_op jit(solution)/shard_map/ppermute | solution.py:315
  475.5 14.5 %collective-permute-done.23 = bf16[320,960]{1,0:T(8,128)(2,1)S(1)} collective-permute-done((bf16[320,960]{1,0:T(8,128)(2,1)S(1)}, bf16[320,960]{1,0:T(8,128)(2,1)S(1)}, u32[]{:S(2)}, u32[]{:S(2)}) %collective-permute-start.23) | collective-permute-done | bytes 614432 | tf_op jit(solution)/shard_map/ppermute | solution.py:315
  493.4 22.9 %collective-permute-done.24 = bf16[160,960]{0,1:T(8,128)(2,1)S(1)} collective-permute-done((bf16[160,960]{0,1:T(8,128)(2,1)S(1)}, bf16[160,960]{0,1:T(8,128)(2,1)S(1)}, u32[]{:S(2)}, u32[]{:S(2)}) %collective-permute-start.24) | collective-permute-done | bytes 307232 | tf_op jit(solution)/shard_map/ppermute | solution.py:315
  518.3 21.2 %collective-permute-done.25 = bf16[160,960]{0,1:T(8,128)(2,1)S(1)} collective-permute-done((bf16[160,960]{0,1:T(8,128)(2,1)S(1)}, bf16[160,960]{0,1:T(8,128)(2,1)S(1)}, u32[]{:S(2)}, u32[]{:S(2)}) %collective-permute-start.25) | collective-permute-done | bytes 307232 | tf_op jit(solution)/shard_map/ppermute | solution.py:315
  562.6 7.1 fusion.4
  569.7 11.2 %collective-permute-start.14 = (bf16[512,1280]{1,0:T(8,128)(2,1)}, bf16[512,1280]{1,0:T(8,128)(2,1)}, u32[]{:S(2)}, u32[]{:S(2)}) collective-permute-start(bf16[512,1280]{1,0:T(8,128)(2,1)} %fusion.4), channel_id=1, source_target_pairs={{0,0},{1,1},{2,4},{3,5},{4,8},{5,9},{6,12},{7,13},{8,2},{9,3},{10,... | collective-permute-start | bytes 3932168 | tf_op jit(solution)/shard_map/ppermute | solution.py:315
  580.9 7.8 collective-permute-done.20
  591.6 29.1 %collective-permute-done.27 = bf16[640,960]{0,1:T(8,128)(2,1)S(1)} collective-permute-done((bf16[640,960]{0,1:T(8,128)(2,1)}, bf16[640,960]{0,1:T(8,128)(2,1)S(1)}, u32[]{:S(2)}, u32[]{:S(2)}) %collective-permute-start.27) | collective-permute-done | bytes 1228832 | tf_op jit(solution)/shard_map/ppermute | solution.py:315
  643.0 34.2 %collective-permute-start.35 = (f32[21,128]{1,0:T(8,128)S(1)}, f32[21,128]{1,0:T(8,128)S(1)}, u32[]{:S(2)}, u32[]{:S(2)}) collective-permute-start(f32[21,128]{1,0:T(8,128)S(1)} %add.368), channel_id=1, source_target_pairs={{0,4},{1,5},{2,6},{3,7},{4,0},{5,1},{6,2},{7,3},{8,12},{9,13},{10,... | collective-permute-start | bytes 32264 | tf_op jit(solution)/shard_map/ppermute | solution.py:315
  677.2 19.7 %collective-permute-done.35 = f32[21,128]{1,0:T(8,128)S(1)} collective-permute-done((f32[21,128]{1,0:T(8,128)S(1)}, f32[21,128]{1,0:T(8,128)S(1)}, u32[]{:S(2)}, u32[]{:S(2)}) %collective-permute-start.35) | collective-permute-done | bytes 10784 | tf_op jit(solution)/shard_map/ppermute | solution.py:315
  708.7 43.1 %all-reduce.5.cloned.1.call-done = bf16[320,3840]{1,0:T(8,128)(2,1)} async-done(((bf16[320,3840]{1,0:T(8,128)(2,1)}), bf16[320,3840]{1,0:T(8,128)(2,1)}) %all-reduce.5.cloned.1.call-update) | async-done | bytes 2457616 | tf_op jit(solution)/shard_map/psum | solution.py:510
  767.7 8.2 %copy.84 = f32[640,3840]{1,0:T(8,128)} copy(bf16[640,3840]{0,1:T(8,128)(2,1)} %fusion.54) | data formatting | bytes 14745600
  (334 shorter events, 273.5 us)
Async XLA Ops:
  7.2 744.5 %all-reduce.5.cloned.1.call-start = ((), (), s32[]{:S(2)}) async-start(), calls=%async_computation | async-start | bytes 4915200 | tf_op jit(solution)/shard_map/psum | solution.py:510
  7.2 123.5 %collective-permute-start = (bf16[512,1280]{1,0:T(8,128)(2,1)}, bf16[512,1280]{1,0:T(8,128)(2,1)}, u32[]{:S(2)}, u32[]{:S(2)}) collective-permute-start(bf16[512,1280]{1,0:T(8,128)(2,1)} %bitcast.220), channel_id=1, source_target_pairs={{0,8},{1,9},{2,10},{3,11},{12,4},{13,5},{14,6},{15,7},{16,24},{17,... | collective-permute-start | bytes 3932168 | tf_op jit(solution)/shard_map/ppermute | solution.py:315
  10.8 83.8 %collective-permute-start.1 = (bf16[512,1280]{1,0:T(8,128)(2,1)}, bf16[512,1280]{1,0:T(8,128)(2,1)}, u32[]{:S(2)}, u32[]{:S(2)}) collective-permute-start(bf16[512,1280]{1,0:T(8,128)(2,1)} %bitcast.221), channel_id=1, source_target_pairs={{2,0},{3,1},{4,2},{5,3},{6,4},{7,5},{8,10},{9,11},{10,12},{11,13},... | collective-permute-start | bytes 3932168 | tf_op jit(solution)/shard_map/ppermute | solution.py:315
  12.1 36.8 %collective-permute-start.7 = (s32[1,2048]{1,0:T(1,128)}, s32[1,2048]{1,0:T(1,128)S(1)}, u32[]{:S(2)}, u32[]{:S(2)}) collective-permute-start(s32[1,2048]{1,0:T(1,128)} %param.11), channel_id=1, source_target_pairs={{0,8},{1,9},{2,10},{3,11},{4,12},{5,13},{6,14},{7,15},{8,0},{9,1},... | collective-permute-start | bytes 24584 | tf_op jit(solution)/shard_map/ppermute | solution.py:315
  43.0 30.2 %collective-permute-start.8 = (bf16[640,960]{0,1:T(8,128)(2,1)}, bf16[640,960]{0,1:T(8,128)(2,1)}, u32[]{:S(2)}, u32[]{:S(2)}) collective-permute-start(bf16[640,960]{0,1:T(8,128)(2,1)} %maximum_select_fusion), channel_id=1, source_target_pairs={{0,1},{1,0},{2,3},{3,2},{4,5},{5,4},{6,7},{7,6},{8,9},{9,8},{10,11... | collective-permute-start | bytes 3686408 | tf_op jit(solution)/shard_map/ppermute | solution.py:315
  47.8 77.1 %collective-permute-start.12 = (bf16[320,3840]{1,0:T(8,128)(2,1)}, bf16[320,3840]{1,0:T(8,128)(2,1)}, u32[]{:S(2)}, u32[]{:S(2)}) collective-permute-start(bf16[320,3840]{1,0:T(8,128)(2,1)} %pad_maximum_fusion.6), channel_id=1, source_target_pairs={{0,1},{1,0},{2,3},{3,2},{4,5},{5,4},{6,7},{7,6},{8,9},{9,8},{10,11... | collective-permute-start | bytes 7372808 | tf_op jit(solution)/shard_map/ppermute | solution.py:315
  48.9 209.3 %collective-permute-start.15 = (bf16[512,1280]{1,0:T(8,128)(2,1)}, bf16[512,1280]{1,0:T(8,128)(2,1)}, u32[]{:S(2)}, u32[]{:S(2)}) collective-permute-start(bf16[512,1280]{1,0:T(8,128)(2,1)} %bitcast.226), channel_id=1, source_target_pairs={{0,0},{1,1},{2,8},{3,9},{4,2},{5,3},{6,10},{7,11},{8,4},{9,5},{10,... | collective-permute-start | bytes 3932168 | tf_op jit(solution)/shard_map/ppermute | solution.py:315
  94.6 36.1 %collective-permute-start.3 = (bf16[512,1280]{1,0:T(8,128)(2,1)}, bf16[512,1280]{1,0:T(8,128)(2,1)S(1)}, u32[]{:S(2)}, u32[]{:S(2)}) collective-permute-start(bf16[512,1280]{1,0:T(8,128)(2,1)} %collective-permute-done.1), channel_id=1, source_target_pairs={{2,0},{3,1},{4,2},{5,3},{10,12},{11,13},{12,14},{13,15},{18,16},{1... | collective-permute-start | bytes 3932168 | tf_op jit(solution)/shard_map/ppermute | solution.py:315
  95.9 37.2 %collective-permute-start.2 = (bf16[512,1280]{1,0:T(8,128)(2,1)}, bf16[512,1280]{1,0:T(8,128)(2,1)S(1)}, u32[]{:S(2)}, u32[]{:S(2)}) collective-permute-start(bf16[512,1280]{1,0:T(8,128)(2,1)} %collective-permute-done.1), channel_id=1, source_target_pairs={{0,8},{1,9},{2,10},{3,11},{12,4},{13,5},{14,6},{15,7},{16,24},{17,... | collective-permute-start | bytes 3932168 | tf_op jit(solution)/shard_map/ppermute | solution.py:315
  130.8 101.7 %collective-permute-start.13 = (bf16[2,320,3840]{2,1,0:T(8,128)(2,1)}, bf16[2,320,3840]{2,1,0:T(8,128)(2,1)}, u32[]{:S(2)}, u32[]{:S(2)}) collective-permute-start(bf16[2,320,3840]{2,1,0:T(8,128)(2,1)} %pad_maximum_fusion.2), channel_id=1, source_target_pairs={{0,8},{1,9},{2,10},{3,11},{4,12},{5,13},{6,14},{7,15},{8,0},{9,1},... | collective-permute-start | bytes 14745608 | tf_op jit(solution)/shard_map/ppermute | solution.py:315
  139.7 20.4 %collective-permute-start.5 = (bf16[512,1280]{1,0:T(8,128)(2,1)S(1)}, bf16[512,1280]{1,0:T(8,128)(2,1)S(1)}, u32[]{:S(2)}, u32[]{:S(2)}) collective-permute-start(bf16[512,1280]{1,0:T(8,128)(2,1)S(1)} %get-tuple-element.91), channel_id=1, source_target_pairs={{0,2},{1,3},{2,0},{3,1},{12,14},{13,15},{14,12},{15,13},{16,18},{1... | collective-permute-start | bytes 3932168 | tf_op jit(solution)/shard_map/ppermute | solution.py:315
  160.2 4.9 collective-permute-start.6
  208.7 12.1 %collective-permute-start.10 = (bf16[512,320]{1,0:T(8,128)(2,1)S(1)}, bf16[512,320]{1,0:T(8,128)(2,1)S(1)}, u32[]{:S(2)}, u32[]{:S(2)}) collective-permute-start(bf16[512,320]{1,0:T(8,128)(2,1)S(1)} %get-tuple-element.82), channel_id=1, source_target_pairs={{0,2},{1,3},{2,0},{3,1},{4,6},{5,7},{6,4},{7,5},{8,10},{9,11},{10,... | collective-permute-start | bytes 983048 | tf_op jit(solution)/shard_map/ppermute | solution.py:315
  210.8 17.9 %collective-permute-start.11 = (bf16[512,320]{1,0:T(8,128)(2,1)S(1)}, bf16[512,320]{1,0:T(8,128)(2,1)S(1)}, u32[]{:S(2)}, u32[]{:S(2)}) collective-permute-start(bf16[512,320]{1,0:T(8,128)(2,1)S(1)} %get-tuple-element.81), channel_id=1, source_target_pairs={{0,10},{1,11},{2,8},{3,9},{4,14},{5,15},{6,12},{7,13},{8,2},{9,3},... | collective-permute-start | bytes 983048 | tf_op jit(solution)/shard_map/ppermute | solution.py:315
  279.5 93.6 %collective-permute-start.16 = (bf16[512,320]{1,0:T(8,128)(2,1)}, bf16[512,320]{1,0:T(8,128)(2,1)}, u32[]{:S(2)}, u32[]{:S(2)}) collective-permute-start(bf16[512,320]{1,0:T(8,128)(2,1)} %get-tuple-element.89), channel_id=1, source_target_pairs={{0,8},{1,9},{2,10},{3,11},{4,12},{5,13},{6,14},{7,15},{8,0},{9,1},... | collective-permute-start | bytes 983048 | tf_op jit(solution)/shard_map/ppermute | solution.py:315
  279.7 94.6 %collective-permute-start.17 = (bf16[512,320]{1,0:T(8,128)(2,1)}, bf16[512,320]{1,0:T(8,128)(2,1)}, u32[]{:S(2)}, u32[]{:S(2)}) collective-permute-start(bf16[512,320]{1,0:T(8,128)(2,1)} %get-tuple-element.88), channel_id=1, source_target_pairs={{0,2},{1,3},{2,0},{3,1},{4,6},{5,7},{6,4},{7,5},{8,10},{9,11},{10,... | collective-permute-start | bytes 983048 | tf_op jit(solution)/shard_map/ppermute | solution.py:315
  281.4 93.9 %collective-permute-start.18 = (bf16[512,320]{1,0:T(8,128)(2,1)}, bf16[512,320]{1,0:T(8,128)(2,1)S(1)}, u32[]{:S(2)}, u32[]{:S(2)}) collective-permute-start(bf16[512,320]{1,0:T(8,128)(2,1)} %get-tuple-element.87), channel_id=1, source_target_pairs={{0,10},{1,11},{2,8},{3,9},{4,14},{5,15},{6,12},{7,13},{8,2},{9,3},... | collective-permute-start | bytes 983048 | tf_op jit(solution)/shard_map/ppermute | solution.py:315
  372.8 177.0 %collective-permute-start.29 = (bf16[2,320,3840]{2,1,0:T(8,128)(2,1)}, bf16[2,320,3840]{2,1,0:T(8,128)(2,1)}, u32[]{:S(2)}, u32[]{:S(2)}) collective-permute-start(bf16[2,320,3840]{2,1,0:T(8,128)(2,1)} %constant_dynamic-slice_fusion), channel_id=1, source_target_pairs={{0,8},{1,9},{2,10},{3,11},{4,12},{5,13},{6,14},{7,15},{8,0},{9,1},... | collective-permute-start | bytes 14745608 | tf_op jit(solution)/shard_map/ppermute | solution.py:315
  443.2 29.5 %collective-permute-start.22 = (bf16[640,960]{0,1:T(8,128)(2,1)S(1)}, bf16[640,960]{0,1:T(8,128)(2,1)S(1)}, u32[]{:S(2)}, u32[]{:S(2)}) collective-permute-start(bf16[640,960]{0,1:T(8,128)(2,1)S(1)} %bitcast.222), channel_id=1, source_target_pairs={{0,1},{1,0},{2,3},{3,2},{4,5},{5,4},{6,7},{7,6},{8,9},{9,8},{10,11... | collective-permute-start | bytes 3686408 | tf_op jit(solution)/shard_map/ppermute | solution.py:315
  453.3 88.8 %collective-permute-start.19 = (bf16[2,512,1280]{2,1,0:T(8,128)(2,1)}, bf16[2,512,1280]{2,1,0:T(8,128)(2,1)}, u32[]{:S(2)}, u32[]{:S(2)}) collective-permute-start(bf16[2,512,1280]{2,1,0:T(8,128)(2,1)} %fusion.31), channel_id=1, source_target_pairs={{0,8},{1,9},{2,10},{3,11},{4,12},{5,13},{6,14},{7,15},{8,0},{9,1},... | collective-permute-start | bytes 7864328 | tf_op jit(solution)/shard_map/ppermute | solution.py:315
  473.8 16.3 %collective-permute-start.23 = (bf16[320,960]{1,0:T(8,128)(2,1)S(1)}, bf16[320,960]{1,0:T(8,128)(2,1)S(1)}, u32[]{:S(2)}, u32[]{:S(2)}) collective-permute-start(bf16[320,960]{1,0:T(8,128)(2,1)S(1)} %copy.72), channel_id=1, source_target_pairs={{0,16},{1,17},{2,18},{3,19},{4,20},{5,21},{6,22},{7,23},{8,24},{9,... | collective-permute-start | bytes 1843208 | tf_op jit(solution)/shard_map/ppermute | solution.py:315
  493.0 23.3 %collective-permute-start.24 = (bf16[160,960]{0,1:T(8,128)(2,1)S(1)}, bf16[160,960]{0,1:T(8,128)(2,1)S(1)}, u32[]{:S(2)}, u32[]{:S(2)}) collective-permute-start(bf16[160,960]{0,1:T(8,128)(2,1)S(1)} %constant_dynamic-slice_fusion.1), channel_id=1, source_target_pairs={{0,4},{1,5},{2,6},{3,7},{4,0},{5,1},{6,2},{7,3},{8,12},{9,13},{10,... | collective-permute-start | bytes 921608 | tf_op jit(solution)/shard_map/ppermute | solution.py:315
  516.6 22.9 %collective-permute-start.25 = (bf16[160,960]{0,1:T(8,128)(2,1)S(1)}, bf16[160,960]{0,1:T(8,128)(2,1)S(1)}, u32[]{:S(2)}, u32[]{:S(2)}) collective-permute-start(bf16[160,960]{0,1:T(8,128)(2,1)S(1)} %add_convert_fusion.2), channel_id=1, source_target_pairs={{0,4},{1,5},{2,6},{3,7},{4,0},{5,1},{6,2},{7,3},{8,12},{9,13},{10,... | collective-permute-start | bytes 921608 | tf_op jit(solution)/shard_map/ppermute | solution.py:315
  541.0 16.9 %collective-permute-start.26 = (bf16[320,960]{1,0:T(8,128)(2,1)}, bf16[320,960]{1,0:T(8,128)(2,1)S(1)}, u32[]{:S(2)}, u32[]{:S(2)}) collective-permute-start(bf16[320,960]{1,0:T(8,128)(2,1)} %bitcast.218), channel_id=1, source_target_pairs={{0,16},{1,17},{2,18},{3,19},{4,20},{5,21},{6,22},{7,23},{8,24},{9,... | collective-permute-start | bytes 1843208 | tf_op jit(solution)/shard_map/ppermute | solution.py:315
  549.8 38.9 %collective-permute-start.20 = (bf16[512,1280]{1,0:T(8,128)(2,1)}, bf16[512,1280]{1,0:T(8,128)(2,1)}, u32[]{:S(2)}, u32[]{:S(2)}) collective-permute-start(bf16[512,1280]{1,0:T(8,128)(2,1)} %fusion.39), channel_id=1, source_target_pairs={{0,2},{1,3},{2,0},{3,1},{4,6},{5,7},{6,4},{7,5},{8,10},{9,11},{10,... | collective-permute-start | bytes 3932168 | tf_op jit(solution)/shard_map/ppermute | solution.py:315
  555.0 68.7 %collective-permute-start.30 = (bf16[320,3840]{1,0:T(8,128)(2,1)}, bf16[320,3840]{1,0:T(8,128)(2,1)}, u32[]{:S(2)}, u32[]{:S(2)}) collective-permute-start(bf16[320,3840]{1,0:T(8,128)(2,1)} %dynamic-slice_bitcast_fusion), channel_id=1, source_target_pairs={{0,1},{1,0},{2,3},{3,2},{4,5},{5,4},{6,7},{7,6},{8,9},{9,8},{10,11... | collective-permute-start | bytes 7372808 | tf_op jit(solution)/shard_map/ppermute | solution.py:315
  561.7 59.0 %collective-permute-start.27 = (bf16[640,960]{0,1:T(8,128)(2,1)}, bf16[640,960]{0,1:T(8,128)(2,1)S(1)}, u32[]{:S(2)}, u32[]{:S(2)}) collective-permute-start(bf16[640,960]{0,1:T(8,128)(2,1)} %copy.76), channel_id=1, source_target_pairs={{0,2},{1,3},{2,0},{3,1},{4,6},{5,7},{6,4},{7,5},{8,10},{9,11},{10,... | collective-permute-start | bytes 3686408 | tf_op jit(solution)/shard_map/ppermute | solution.py:315
  569.7 128.6 %collective-permute-start.14 = (bf16[512,1280]{1,0:T(8,128)(2,1)}, bf16[512,1280]{1,0:T(8,128)(2,1)}, u32[]{:S(2)}, u32[]{:S(2)}) collective-permute-start(bf16[512,1280]{1,0:T(8,128)(2,1)} %fusion.4), channel_id=1, source_target_pairs={{0,0},{1,1},{2,4},{3,5},{4,8},{5,9},{6,12},{7,13},{8,2},{9,3},{10,... | collective-permute-start | bytes 3932168 | tf_op jit(solution)/shard_map/ppermute | solution.py:315
  623.7 79.1 %collective-permute-start.28 = (bf16[2,640,960]{1,2,0:T(8,128)(2,1)}, bf16[2,640,960]{1,2,0:T(8,128)(2,1)}, u32[]{:S(2)}, u32[]{:S(2)}) collective-permute-start(bf16[2,640,960]{1,2,0:T(8,128)(2,1)} %pad_maximum_fusion.7), channel_id=1, source_target_pairs={{0,8},{1,9},{2,10},{3,11},{4,12},{5,13},{6,14},{7,15},{8,0},{9,1},... | collective-permute-start | bytes 7372808 | tf_op jit(solution)/shard_map/ppermute | solution.py:315
  631.7 70.0 %collective-permute-start.21 = (bf16[512,1280]{1,0:T(8,128)(2,1)S(1)}, bf16[512,1280]{1,0:T(8,128)(2,1)S(1)}, u32[]{:S(2)}, u32[]{:S(2)}) collective-permute-start(bf16[512,1280]{1,0:T(8,128)(2,1)S(1)} %fusion.27), channel_id=1, source_target_pairs={{0,0},{1,1},{2,4},{3,5},{4,8},{5,9},{6,12},{7,13},{8,2},{9,3},{10,... | collective-permute-start | bytes 3932168 | tf_op jit(solution)/shard_map/ppermute | solution.py:315
  643.0 53.8 %collective-permute-start.35 = (f32[21,128]{1,0:T(8,128)S(1)}, f32[21,128]{1,0:T(8,128)S(1)}, u32[]{:S(2)}, u32[]{:S(2)}) collective-permute-start(f32[21,128]{1,0:T(8,128)S(1)} %add.368), channel_id=1, source_target_pairs={{0,4},{1,5},{2,6},{3,7},{4,0},{5,1},{6,2},{7,3},{8,12},{9,13},{10,... | collective-permute-start | bytes 32264 | tf_op jit(solution)/shard_map/ppermute | solution.py:315
  751.7 24.2 %collective-permute-start.31 = (bf16[320,3840]{1,0:T(8,128)(2,1)}, bf16[320,3840]{1,0:T(8,128)(2,1)}, u32[]{:S(2)}, u32[]{:S(2)}) collective-permute-start(bf16[320,3840]{1,0:T(8,128)(2,1)} %all-reduce.5.cloned.1.call-done), channel_id=1, source_target_pairs={{0,8},{1,9},{2,10},{3,11},{4,12},{5,13},{6,14},{7,15},{8,0},{9,1},... | collective-permute-start | bytes 7372808 | tf_op jit(solution)/shard_map/ppermute | solution.py:315
  (60 other events, 680.3 us)
Sparse Core Ops, SparseCore 0:
  627.6 124.1 all-reduce.4

commit v2 on v1

v2 whole, which is shorter than its diff:
```python
import functools
import math

import jax
import jax.numpy as jnp
from jax import lax
from jax.experimental import pallas as pl
from jax.experimental.pallas import tpu as pltpu
from jax.sharding import Mesh
from jax.sharding import PartitionSpec as P

D = 1280
H = 16
HD = 80
LN = 128
epsilon = 1e-06
scale_base = 1.442695041
log2e = 1.4426950408889634
NEG = -1e30
f32 = jnp.float32
bf16 = jnp.bfloat16
AXES = ("gx", "gc", "ctx", "wt")


def block_flags(seg_row, bq, bk):
    n = seg_row.shape[0]
    q = seg_row.reshape(n // bq, bq)
    k = seg_row.reshape(n // bk, bk)
    qf, ql = q[:, 0][:, None], q[:, -1][:, None]
    kf, kl = k[:, 0][None], k[:, -1][None]
    qs = jnp.arange(n // bq, dtype=jnp.int32)[:, None] * bq
    ks = jnp.arange(n // bk, dtype=jnp.int32)[None] * bk
    below = ks + bk - 1 <= qs
    skip = (ks > qs + bq - 1) | ((kf > 0) & (kl < qf))
    same = (qf == ql) & (kl == ql) & ((kf == kl) | ((kf == 0) & (kl == 1)))
    full = below & ((kl == 0) | same)
    return jnp.where(skip, 0, jnp.where(full, 1, 2)).astype(jnp.int32).reshape(-1)


def put_split(base, col, lanes):
    hi = col.astype(bf16).astype(f32)
    rest = col - hi
    mid = rest.astype(bf16).astype(f32)
    out = jnp.where(lanes == HD, hi, base)
    out = jnp.where(lanes == HD + 1, mid, out)
    return jnp.where(lanes == HD + 2, rest - mid, out).astype(bf16)


def fwd_kernel(flags, q_ref, kv, segc, segr, att, of, qaug, m_s, acc_s, *, nh, bq, bk, nk):
    qi = pl.program_id(0)
    count = (qi * bq + bq + bk - 1) // bk
    nt = (((1,), (1,)), ((), ()))
    acc_s[...] = jnp.zeros_like(acc_s)
    m_s[...] = jnp.zeros_like(m_s)

    def mask(ko):
        qpos = qi * bq + lax.broadcasted_iota(jnp.int32, (bq, bk), 0)
        kpos = ko + lax.broadcasted_iota(jnp.int32, (bq, bk), 1)
        ks = segr[:, pl.ds(ko, bk)]
        return (kpos <= qpos) & ((ks == 0) | (ks == segc[...]))

    def step(kb, masked):
        ko = pl.multiple_of(kb * bk, bk)
        if masked:
            allowed = mask(ko)
        for h in range(nh):
            k = kv[pl.ds(ko, bk), h * LN : (h + 1) * LN]
            v = kv[pl.ds(ko, bk), (nh + h) * LN : (nh + h + 1) * LN]
            s = lax.dot_general(q_ref[:, h * LN : (h + 1) * LN], k, nt, preferred_element_type=f32)
            p = jnp.exp2(s)
            if masked:
                p = jnp.where(allowed, p, 0.0)
            acc_s[h] += jnp.dot(p.astype(bf16), v, preferred_element_type=f32)

    def body(kb, carry):
        flag = flags[qi * nk + kb]

        @pl.when(flag == 1)
        def _():
            step(kb, False)

        @pl.when(flag == 2)
        def _():
            step(kb, True)

        return carry

    lax.fori_loop(0, count, body, 0)
    bad = jnp.zeros((bq, 1), f32)
    for h in range(nh):
        total = acc_s[h][:, HD : HD + 1]
        bad = jnp.maximum(bad, jnp.where((total > 2.0**-60) & (total < 2.0**60), 0.0, 1.0))

    @pl.when(jnp.max(bad) > 0.0)
    def _():
        def head(h, carry):
            kc = pl.ds(pl.multiple_of(h * LN, LN), LN)
            vc = pl.ds(pl.multiple_of((nh + h) * LN, LN), LN)
            m_s[h] = jnp.full((bq, LN), NEG, f32)
            acc_s[h] = jnp.zeros((bq, LN), f32)

            def inner(kb, carry):
                @pl.when(flags[qi * nk + kb] > 0)
                def _():
                    ko = pl.multiple_of(kb * bk, bk)
                    s = lax.dot_general(
                        q_ref[:, kc], kv[pl.ds(ko, bk), kc], nt, preferred_element_type=f32
                    )
                    s = jnp.where(mask(ko), s, NEG)
                    old = m_s[h]
                    new = jnp.maximum(old, jnp.max(s, axis=1, keepdims=True))
                    p = jnp.exp2(s - new[:, :1]).astype(bf16)
                    m_s[h] = new
                    acc_s[h] = acc_s[h] * jnp.exp2(old - new) + jnp.dot(
                        p, kv[pl.ds(ko, bk), vc], preferred_element_type=f32
                    )

                return carry

            lax.fori_loop(0, count, inner, 0)
            return carry

        lax.fori_loop(0, nh, head, 0)

    lanes = lax.broadcasted_iota(jnp.int32, (bq, LN), 1)
    outs = []
    for h in range(nh):
        acc = acc_s[h]
        total = acc[:, HD : HD + 1]
        out = acc * (1.0 / total)
        of[:, h * LN : (h + 1) * LN] = jnp.where(lanes < HD, out, 0.0)
        outs.append(out[:, :HD])
        lse = m_s[h][:, :1] + jnp.log2(total)
        qaug[:, h * LN : (h + 1) * LN] = put_split(
            q_ref[:, h * LN : (h + 1) * LN].astype(f32), -lse, lanes
        )
    att[...] = jnp.concatenate(outs, axis=1).astype(bf16)


def attn_fwd(q, kv, seg_row, nh, bq=512, bk=512):
    n = q.shape[0]
    w = nh * LN
    spec = pltpu.PrefetchScalarGridSpec(
        num_scalar_prefetch=1,
        grid=(n // bq,),
        in_specs=[
            pl.BlockSpec((bq, w), lambda i, f: (i, 0)),
            pl.BlockSpec((n, 2 * w), lambda i, f: (0, 0)),
            pl.BlockSpec((bq, 1), lambda i, f: (i, 0)),
            pl.BlockSpec((1, n), lambda i, f: (0, 0)),
        ],
        out_specs=[
            pl.BlockSpec((bq, nh * HD), lambda i, f: (i, 0)),
            pl.BlockSpec((bq, w), lambda i, f: (i, 0)),
            pl.BlockSpec((bq, w), lambda i, f: (i, 0)),
        ],
        scratch_shapes=[pltpu.VMEM((nh, bq, LN), f32), pltpu.VMEM((nh, bq, LN), f32)],
    )
    return pl.pallas_call(
        functools.partial(fwd_kernel, nh=nh, bq=bq, bk=bk, nk=n // bk),
        out_shape=[
            jax.ShapeDtypeStruct((n, nh * HD), bf16),
            jax.ShapeDtypeStruct((n, w), f32),
            jax.ShapeDtypeStruct((n, w), bf16),
        ],
        grid_spec=spec,
        compiler_params=pltpu.CompilerParams(vmem_limit_bytes=40 << 20),
        cost_estimate=pl.CostEstimate(
            flops=20_000_000_000, transcendentals=10_000_000, bytes_accessed=16_000_000
        ),
        name="attn_fwd",
    )(block_flags(seg_row, bq, bk), q, kv, seg_row[:, None], seg_row[None])


def bwd_kernel(
    flags, mine, qa, kk, vv, do0, do1, do2, do3, of, segc, segr, scale, dqkv, gscale, doa_s, dq_s, dk_s, dv_s, *, first, nh, bq, bk, n
):
    nk = n // bk
    nq = n // bq
    kb = pl.program_id(0)
    part = n // 4
    step_rows = 256 if part % 256 == 0 else part
    lanes = lax.broadcasted_iota(jnp.int32, (step_rows, LN), 1)

    @pl.when(kb == 0)
    def _():
        dq_s[...] = jnp.zeros_like(dq_s)
        for j, piece in enumerate((do0, do1, do2, do3)):
            start = (mine[0] ^ j) * part
            for i in range(part // step_rows):
                d = piece[i * step_rows : (i + 1) * step_rows, :].astype(f32)
                r = pl.ds(pl.multiple_of(start + i * step_rows, step_rows), step_rows)
                for h in range(nh):
                    at = (first + h) * HD
                    dh = jnp.concatenate(
                        [d[:, at : at + HD], jnp.zeros((step_rows, LN - HD), f32)], axis=1
                    )
                    c = slice(h * LN, (h + 1) * LN)
                    delta = jnp.sum(dh * of[r, c], axis=1, keepdims=True)
                    doa_s[r, c] = put_split(dh, -delta, lanes)

    dk_s[...] = jnp.zeros_like(dk_s)
    dv_s[...] = jnp.zeros_like(dv_s)
    ko = kb * bk
    nt = (((1,), (1,)), ((), ()))
    tn = (((0,), (0,)), ((), ()))

    def step(qi, masked):
        qo = pl.multiple_of(qi * bq, bq)
        if masked:
            kpos = ko + lax.broadcasted_iota(jnp.int32, (bk, bq), 0)
            qpos = qo + lax.broadcasted_iota(jnp.int32, (bk, bq), 1)
            ks = segc[...]
            allowed = (kpos <= qpos) & ((ks == 0) | (ks == segr[:, pl.ds(qo, bq)]))
        for h in range(nh):
            c = slice(h * LN, (h + 1) * LN)
            q = qa[pl.ds(qo, bq), c]
            k = kk[:, c]
            d = doa_s[pl.ds(qo, bq), c]
            p = jnp.exp2(lax.dot_general(k, q, nt, preferred_element_type=f32))
            if masked:
                p = jnp.where(allowed, p, 0.0)
            ds = (p * lax.dot_general(vv[:, c], d, nt, preferred_element_type=f32)).astype(bf16)
            dv_s[h] += jnp.dot(p.astype(bf16), d, preferred_element_type=f32)
            dk_s[h] += jnp.dot(ds, q, preferred_element_type=f32)
            dq_s[h, pl.ds(qo, bq), :] += lax.dot_general(ds, k, tn, preferred_element_type=f32)

    def body(qi, carry):
        flag = flags[qi * nk + kb]

        @pl.when(flag == 1)
        def _():
            step(qi, False)

        @pl.when(flag == 2)
        def _():
            step(qi, True)

        return carry

    lax.fori_loop(ko // bq, nq, body, 0)
    r = pl.multiple_of(ko, bk)
    ln2 = math.log(2.0)
    dqkv[pl.ds(r, bk), nh * HD : 3 * nh * HD] = jnp.concatenate(
        [dk_s[h][:, :HD] * ln2 for h in range(nh)] + [dv_s[h][:, :HD] for h in range(nh)], axis=1
    ).astype(bf16)

    @pl.when(kb == nk - 1)
    def _():
        total = jnp.zeros((1, LN), f32)
        for i in range(nq):
            rows = slice(i * bq, (i + 1) * bq)
            for h in range(nh):
                total = total + jnp.sum(
                    dq_s[h, rows, :] * qa[rows, h * LN : (h + 1) * LN].astype(f32), axis=0, keepdims=True
                )
            grads = jnp.concatenate([dq_s[h, rows, :][:, :HD] for h in range(nh)], axis=1)
            dqkv[rows, 0 : nh * HD] = (grads * scale[...]).astype(bf16)
        gscale[...] = jnp.broadcast_to(total, gscale.shape)


def attn_bwd(qa, kv, pieces, of, seg_row, mine, scale, heads, group, groups, bq=512, bk=512):
    n = qa.shape[0]
    nh = heads // groups
    w = nh * LN
    once = pl.Buffered(1)
    spec = pltpu.PrefetchScalarGridSpec(
        num_scalar_prefetch=2,
        grid=(n // bk,),
        in_specs=[
            pl.BlockSpec((n, w), lambda i, f, m: (0, group), pipeline_mode=once),
            pl.BlockSpec((bk, w), lambda i, f, m: (i, group)),
            pl.BlockSpec((bk, w), lambda i, f, m: (i, groups + group)),
        ]
        + [pl.BlockSpec((n // 4, heads * HD), lambda i, f, m: (0, 0), pipeline_mode=once)] * 4
        + [
            pl.BlockSpec((n, w), lambda i, f, m: (0, group), pipeline_mode=once),
            pl.BlockSpec((bk, 1), lambda i, f, m: (i, 0)),
            pl.BlockSpec((1, n), lambda i, f, m: (0, 0)),
            pl.BlockSpec((1, nh * HD), lambda i, f, m: (0, 0)),
        ],
        out_specs=[
            pl.BlockSpec((n, 3 * nh * HD), lambda i, f, m: (0, 0)),
            pl.BlockSpec((8, LN), lambda i, f, m: (0, 0)),
        ],
        scratch_shapes=[
            pltpu.VMEM((n, w), bf16),
            pltpu.VMEM((nh, n, LN), f32),
            pltpu.VMEM((nh, bk, LN), f32),
            pltpu.VMEM((nh, bk, LN), f32),
        ],
    )
    return pl.pallas_call(
        functools.partial(bwd_kernel, first=group * nh, nh=nh, bq=bq, bk=bk, n=n),
        out_shape=[
            jax.ShapeDtypeStruct((n, 3 * nh * HD), bf16),
            jax.ShapeDtypeStruct((8, LN), f32),
        ],
        grid_spec=spec,
        compiler_params=pltpu.CompilerParams(vmem_limit_bytes=48 << 20),
        cost_estimate=pl.CostEstimate(
            flops=15_000_000_000 * nh // 2, transcendentals=10_000_000, bytes_accessed=20_000_000
        ),
        name="attn_bwd",
    )(block_flags(seg_row, bq, bk), mine.reshape(1), qa, kv, kv, *pieces, of, seg_row[:, None], seg_row[None], scale)


def quarter_columns(place, parts, groups, nh):
    width = nh // groups * HD
    return [
        (t * D + place * nh * HD + g * width, width) for g in range(groups) for t in range(3)
    ]


def pick_kernel(mine, w_ref, out, *, parts, groups, nh):
    for i in range(parts):

        @pl.when(mine[0] == i)
        def _(i=i):
            out[...] = jnp.concatenate(
                [w_ref[:, a : a + width] for a, width in quarter_columns(i, parts, groups, nh)], axis=1
            )


def pick(w, mine, parts, groups, nh):
    rows = w.shape[0]
    step = 160 if rows % 160 == 0 else rows
    return pl.pallas_call(
        functools.partial(pick_kernel, parts=parts, groups=groups, nh=nh),
        out_shape=jax.ShapeDtypeStruct((rows, 3 * nh * HD), w.dtype),
        grid_spec=pltpu.PrefetchScalarGridSpec(
            num_scalar_prefetch=1,
            grid=(rows // step,),
            in_specs=[pl.BlockSpec((step, 3 * D), lambda i, m: (i, 0))],
            out_specs=pl.BlockSpec((step, 3 * nh * HD), lambda i, m: (i, 0)),
        ),
        name="pick",
    )(mine.reshape(1), w)


def widen_kernel(own_first, a_ref, b_ref, *outs, groups, nh):
    flats, wide = outs[:-1], outs[-1]

    def put(ref):
        value = ref[...]
        each = 3 * nh * HD // groups
        for g in range(groups):
            flats[g][...] = value[:, g * each : (g + 1) * each]
        zero = jnp.zeros((value.shape[0], LN - HD), value.dtype)
        per = nh // groups
        spread = []
        for t in range(3):
            for h in range(nh):
                at = (h // per) * each + t * per * HD + (h % per) * HD
                spread += [value[:, at : at + HD], zero]
        wide[...] = jnp.concatenate(spread, axis=1)

    half = pl.program_id(0)

    @pl.when(half == 0)
    def _():
        put(a_ref)

    @pl.when(half == 1)
    def _():
        put(b_ref)


def widen(own, other, own_at, groups, nh):
    rows, width = own.shape
    step = 160
    n = rows // step
    at = lambda i, j, m: ((i ^ m[0]) * n + j, 0)
    each = width // groups
    return pl.pallas_call(
        functools.partial(widen_kernel, groups=groups, nh=nh),
        out_shape=[jax.ShapeDtypeStruct((2 * rows, each), own.dtype)] * groups
        + [jax.ShapeDtypeStruct((2 * rows, 3 * nh * LN), own.dtype)],
        grid_spec=pltpu.PrefetchScalarGridSpec(
            num_scalar_prefetch=1,
            grid=(2, n),
            in_specs=[
                pl.BlockSpec((step, width), lambda i, j, m: (j * (1 - i), 0)),
                pl.BlockSpec((step, width), lambda i, j, m: (j * i, 0)),
            ],
            out_specs=[pl.BlockSpec((step, each), at)] * groups + [pl.BlockSpec((step, 3 * nh * LN), at)],
        ),
        name="widen",
    )(own_at.reshape(1), own, other)


def project_kernel(info, *refs, count, width, fresh):
    pairs = refs[: 2 * count]
    gain, w, scale, ones = refs[2 * count : 2 * count + 4]
    normed_ref, q_ref, kv_ref, mine_ref = refs[-4:]
    j = pl.program_id(0)

    def work(x_ref):
        value = x_ref[...]
        x = value.astype(f32)
        inverse = lax.rsqrt(jnp.mean(x * x, axis=-1, keepdims=True) + epsilon)
        normed = (x * inverse * gain[...]).astype(bf16)
        normed_ref[...] = normed
        q_ref[...] = (
            jnp.dot(normed, w[:, :width], preferred_element_type=f32) * scale[...]
        ).astype(bf16)
        kv_ref[...] = (
            jnp.dot(normed, w[:, width:], preferred_element_type=f32) + ones[...]
        ).astype(bf16)

        @pl.when(info[count + 1] == info[j])
        def _():
            mine_ref[...] = value

    if not fresh:
        mine_ref[...] = refs[2 * count + 4][...]
    for i in range(count):
        for lane in range(2):

            @pl.when((j == i) & (info[count] == lane))
            def _(i=i, lane=lane):
                work(pairs[2 * i + 1 - lane])


def project(pairs, places, lane, mine, gain, w, scale, ones, group_len, carried=None):
    count = len(pairs)
    rows, d = pairs[0][0].shape
    width = scale.shape[1]
    full = lambda i, f: (0, 0)
    at = lambda i, f: (f[i], 0)
    once = pl.Buffered(1)
    info = jnp.stack(list(places) + [lane.astype(jnp.int32), mine])
    args = [x for pair in pairs for x in pair] + [gain, w, scale, ones]
    in_specs = [pl.BlockSpec((rows, d), full, pipeline_mode=once)] * (2 * count) + [
        pl.BlockSpec((1, d), full, pipeline_mode=once),
        pl.BlockSpec(w.shape, full, pipeline_mode=once),
        pl.BlockSpec((1, width), full, pipeline_mode=once),
        pl.BlockSpec((1, 2 * width), full, pipeline_mode=once),
    ]
    aliases = {}
    if carried is not None:
        args += [carried[3], *carried[:3]]
        in_specs += [pl.BlockSpec((rows, d), full, pipeline_mode=once)] + [pl.BlockSpec(memory_space=pl.ANY)] * 3
        base = 2 * count + 6
        aliases = {base: 0, base + 1: 1, base + 2: 2}
    return pl.pallas_call(
        functools.partial(project_kernel, count=count, width=width, fresh=carried is None),
        out_shape=[
            jax.ShapeDtypeStruct((group_len, d), bf16),
            jax.ShapeDtypeStruct((group_len, width), bf16),
            jax.ShapeDtypeStruct((group_len, 2 * width), bf16),
            jax.ShapeDtypeStruct((rows, d), bf16),
        ],
        grid_spec=pltpu.PrefetchScalarGridSpec(
            num_scalar_prefetch=1,
            grid=(count,),
            in_specs=in_specs,
            out_specs=[
                pl.BlockSpec((rows, d), at),
                pl.BlockSpec((rows, width), at),
                pl.BlockSpec((rows, 2 * width), at),
                pl.BlockSpec((rows, d), full),
            ],
        ),
        input_output_aliases=aliases,
        compiler_params=pltpu.CompilerParams(vmem_limit_bytes=48 << 20),
        name="project",
    )(info, *args)


def tail_body(at, p0, p1, p2, p3, x_ref, g_ref, w_s, gain, outs):
    lo_ref, att_ref, nm_ref, gh_ref, act_ref, gp_ref, gr_ref, c0, c1, c2, c3, gg_ref = outs
    mine = at[0]
    pieces = (p0, p1, p2, p3)
    cols = p0.shape[1]
    nt = (((1,), (1,)), ((), ()))
    for i in range(4):

        @pl.when(mine == i)
        def _(i=i):
            att_ref[...] = jnp.concatenate([pieces[i ^ k][...] for k in range(4)], axis=1)

    resid = x_ref[...].astype(f32) + jnp.dot(att_ref[...], w_s[0], preferred_element_type=f32)
    inverse = lax.rsqrt(jnp.mean(resid * resid, axis=-1, keepdims=True) + epsilon)
    normed = (resid * inverse * gain[...]).astype(bf16)
    nm_ref[...] = normed
    hidden = jnp.dot(normed, w_s[1], preferred_element_type=f32)
    sig = 1.0 / (1.0 + jnp.exp(-hidden))
    active = (hidden * sig).astype(bf16)
    act_ref[...] = active
    lo_ref[...] = (resid + jnp.dot(active, w_s[2], preferred_element_type=f32)).astype(bf16)
    grad_active = lax.dot_general(g_ref[...], w_s[2], nt, preferred_element_type=f32)
    grad_hidden = (grad_active * sig * (1.0 + hidden * (1.0 - sig))).astype(bf16)
    gh_ref[...] = grad_hidden
    grad_normed = lax.dot_general(grad_hidden, w_s[1], nt, preferred_element_type=f32)
    gg_ref[...] += jnp.sum(grad_normed * resid * inverse, axis=0, keepdims=True)
    scaled = grad_normed * gain[...]
    grad_resid = (
        g_ref[...].astype(f32)
        + inverse * scaled
        - resid * (inverse * inverse * inverse) * jnp.mean(scaled * resid, axis=-1, keepdims=True)
    )
    gr_ref[...] = grad_resid
    grad_proj = grad_resid.astype(bf16)
    gp_ref[...] = grad_proj
    grad_att = lax.dot_general(grad_proj, w_s[0], nt, preferred_element_type=f32).astype(bf16)
    for i in range(4):

        @pl.when(mine == i)
        def _(i=i):
            for j, out in enumerate((c0, c1, c2, c3)):
                out[...] = grad_att[:, (i ^ j) * cols : ((i ^ j) + 1) * cols]


def tail_kernel(at, p0, p1, p2, p3, x_ref, g_ref, own, half, other, gain, *refs, rows, hrows):
    w_s = refs[-1]
    outs = refs[:-1]

    @pl.when(pl.program_id(0) == 0)
    def _():
        outs[-1][...] = jnp.zeros_like(outs[-1])
        w_s[:, pl.ds(pl.multiple_of(at[1], 16), rows), :] = own[...]
        w_s[:, pl.ds(pl.multiple_of(at[2], 16), hrows), :] = half[...]
        w_s[:, pl.ds(pl.multiple_of(at[3], 16), hrows), :] = other[...]

    tail_body(at, p0, p1, p2, p3, x_ref, g_ref, w_s, gain, outs)


def whole_tail_kernel(at, p0, p1, p2, p3, x_ref, g_ref, w, gain, *outs):
    @pl.when(pl.program_id(0) == 0)
    def _():
        outs[-1][...] = jnp.zeros_like(outs[-1])

    tail_body(at, p0, p1, p2, p3, x_ref, g_ref, w, gain, outs)


def tail(at, pieces, x, g, weights, gain, tile=256):
    rows, d = x.shape
    cols = pieces[0].shape[1]
    row = lambda i, m: (i, 0)
    once = pl.Buffered(1)
    whole = lambda *shape: pl.BlockSpec(shape, lambda i, m: (0,) * len(shape), pipeline_mode=once)
    wide = pl.BlockSpec((tile, d), row)
    slim = pl.BlockSpec((tile, cols), row)
    if len(weights) == 3:
        body = functools.partial(tail_kernel, rows=weights[0].shape[1], hrows=weights[1].shape[1])
        scratch = [pltpu.VMEM((3, d, d), bf16)]
    else:
        body = whole_tail_kernel
        scratch = []
    return pl.pallas_call(
        body,
        out_shape=[jax.ShapeDtypeStruct((rows, d), bf16)] * 6
        + [jax.ShapeDtypeStruct((rows, d), f32)]
        + [jax.ShapeDtypeStruct((rows, cols), bf16)] * 4
        + [jax.ShapeDtypeStruct((1, d), f32)],
        grid_spec=pltpu.PrefetchScalarGridSpec(
            num_scalar_prefetch=1,
            grid=(rows // tile,),
            in_specs=[slim] * 4 + [wide] * 2 + [whole(*w.shape) for w in weights] + [whole(1, d)],
            out_specs=[wide] * 7 + [slim] * 4 + [pl.BlockSpec((1, d), lambda i, m: (0, 0))],
            scratch_shapes=scratch,
        ),
        compiler_params=pltpu.CompilerParams(vmem_limit_bytes=52 << 20),
        cost_estimate=pl.CostEstimate(
            flops=10_000_000_000, transcendentals=700_000, bytes_accessed=25_000_000
        ),
        name="tail",
    )(at, *pieces, x, g, *weights, gain)


tn_dims = (((0,), (0,)), ((), ()))


def share_kernel(col, l0, l1, l2, r0, r1, r2, out):
    for i, (left, right) in enumerate(((l0, r0), (l1, r1), (l2, r2))):

        @pl.when(pl.program_id(0) == i)
        def _(left=left, right=right):
            out[...] = lax.dot_general(
                left[...], right[...], tn_dims, preferred_element_type=f32
            ).astype(bf16)


def share(lefts, rights, col):
    rows, d = lefts[0].shape
    w = d // 2
    once = pl.Buffered(1)
    return pl.pallas_call(
        share_kernel,
        out_shape=jax.ShapeDtypeStruct((d, 3 * w), bf16),
        grid_spec=pltpu.PrefetchScalarGridSpec(
            num_scalar_prefetch=1,
            grid=(3,),
            in_specs=[pl.BlockSpec((rows, d), lambda i, c: (0, 0), pipeline_mode=once)] * 3
            + [pl.BlockSpec((rows, w), lambda i, c: (0, c[0]), pipeline_mode=once)] * 3,
            out_specs=pl.BlockSpec((d, w), lambda i, c: (0, i)),
        ),
        compiler_params=pltpu.CompilerParams(vmem_limit_bytes=40 << 20),
        cost_estimate=pl.CostEstimate(
            flops=2_500_000_000, transcendentals=0, bytes_accessed=12_000_000
        ),
        name="share",
    )(col.reshape(1), *lefts, *rights)


def keep_kernel(at, l0, l1, l2, r0, r1, r2, got, a_send, a_keep, b_send, b_keep, s):
    h = a_send.shape[1]
    for i, (left, right) in enumerate(((l0, r0), (l1, r1), (l2, r2))):

        @pl.when(pl.program_id(0) == i)
        def _(left=left, right=right):
            s[...] = lax.dot_general(
                left[...], right[...], tn_dims, preferred_element_type=f32
            ) + got[...].astype(f32)

    gx, wt = at[1], at[2]
    for w in range(2):
        base = w * 4 * h
        a_send[w] = s[pl.ds(pl.multiple_of(base + (1 - gx) * h, 16), h), :].astype(bf16)
        a_keep[w] = s[pl.ds(pl.multiple_of(base + gx * h, 16), h), :].astype(bf16)
    b_send[...] = s[pl.ds(pl.multiple_of((1 - wt) * 4 * h + 2 * h, 16), 2 * h), :].astype(bf16)
    b_keep[...] = s[pl.ds(pl.multiple_of(wt * 4 * h + 2 * h, 16), 2 * h), :].astype(bf16)


def keep(lefts, rights, got, at):
    rows, d = lefts[0].shape
    w = d // 2
    h = d // 8
    once = pl.Buffered(1)
    return pl.pallas_call(
        keep_kernel,
        out_shape=[jax.ShapeDtypeStruct((2, h, 3 * w), bf16)] * 2
        + [jax.ShapeDtypeStruct((2 * h, 3 * w), bf16)] * 2,
        grid_spec=pltpu.PrefetchScalarGridSpec(
            num_scalar_prefetch=1,
            grid=(3,),
            in_specs=[pl.BlockSpec((rows, d), lambda i, c: (0, 0), pipeline_mode=once)] * 3
            + [pl.BlockSpec((rows, w), lambda i, c: (0, c[0]), pipeline_mode=once)] * 3
            + [pl.BlockSpec((d, w), lambda i, c: (0, i))],
            out_specs=[pl.BlockSpec((2, h, w), lambda i, c: (0, 0, i))] * 2
            + [pl.BlockSpec((2 * h, w), lambda i, c: (0, i))] * 2,
            scratch_shapes=[pltpu.VMEM((d, w), f32)],
        ),
        compiler_params=pltpu.CompilerParams(vmem_limit_bytes=40 << 20),
        cost_estimate=pl.CostEstimate(
            flops=2_500_000_000, transcendentals=0, bytes_accessed=16_000_000
        ),
        name="keep",
    )(at, *lefts, *rights, got)


def fold_kernel(bits, *refs, count):
    ins, outs = refs[: 4 * count], refs[4 * count :]
    for i in range(count):
        ks, gs, kk, gk = ins[4 * i : 4 * i + 4]
        outs[2 * i][...] = (ks[0].astype(f32) + gs[0].astype(f32)).astype(bf16)
        outs[2 * i + 1][...] = (kk[0].astype(f32) + gk[0].astype(f32)).astype(bf16)


def fold(items):
    in_specs, out_specs, out_shape, args = [], [], [], []
    for i, (kept, got, bit) in enumerate(items):
        shape = (1,) + kept.shape[1:]
        other = pl.BlockSpec(shape, lambda _, m, i=i: (1 - m[i], 0, 0))
        mine = pl.BlockSpec(shape, lambda _, m, i=i: (m[i], 0, 0))
        in_specs += [other, other, mine, mine]
        args += [kept, got, kept, got]
        out_specs += [pl.BlockSpec(kept.shape[1:], lambda _, m: (0, 0))] * 2
        out_shape += [jax.ShapeDtypeStruct(kept.shape[1:], bf16)] * 2
    bits = jnp.stack([bit for _, _, bit in items])
    out = pl.pallas_call(
        functools.partial(fold_kernel, count=len(items)),
        out_shape=out_shape,
        grid_spec=pltpu.PrefetchScalarGridSpec(
            num_scalar_prefetch=1, grid=(1,), in_specs=in_specs, out_specs=out_specs
        ),
        compiler_params=pltpu.CompilerParams(vmem_limit_bytes=24 << 20),
        name="fold",
    )(bits, *args)
    return [(out[2 * i], out[2 * i + 1]) for i in range(len(items))]


def place_kernel(at, c_ref, e_ref, fc_ref, fe_ref, o0, o1, o2):
    w = o0.shape[1] // 2
    mine = (pl.program_id(0) % 2) == at[0]
    for own_rows in range(2):
        for core in range(2):

            @pl.when((mine == (own_rows == 1)) & (at[1] == core))
            def _(own_rows=own_rows, core=core):
                near = c_ref if own_rows else e_ref
                mate = fc_ref if own_rows else fe_ref
                first, second = (near, mate) if core == 0 else (mate, near)
                for i, out in enumerate((o0, o1, o2)):
                    out[:, :w] = first[0, :, i * w : (i + 1) * w].astype(f32)
                    out[:, w:] = second[0, :, i * w : (i + 1) * w].astype(f32)


def place_tail(c, e, fc, fe, at):
    _, h, width = c.shape
    d = width // 3 * 2
    block = pl.BlockSpec((1, h, width), lambda i, m: (i // 2, 0, 0))
    return pl.pallas_call(
        place_kernel,
        out_shape=[jax.ShapeDtypeStruct((4 * h, d), f32)] * 3,
        grid_spec=pltpu.PrefetchScalarGridSpec(
            num_scalar_prefetch=1,
            grid=(4,),
            in_specs=[block] * 4,
            out_specs=[pl.BlockSpec((h, d), lambda i, m: (i, 0))] * 3,
        ),
        compiler_params=pltpu.CompilerParams(vmem_limit_bytes=40 << 20),
        name="place_tail",
    )(at, c, e, fc, fe)


def cross_kernel(col, x_ref, g_ref, out):
    out[...] = lax.dot_general(
        x_ref[...], g_ref[...], tn_dims, preferred_element_type=f32
    ).astype(bf16)


def cross(x, g, col):
    rows, d = x.shape
    w = d // 2
    return pl.pallas_call(
        cross_kernel,
        out_shape=jax.ShapeDtypeStruct((w, g.shape[1]), bf16),
        grid_spec=pltpu.PrefetchScalarGridSpec(
            num_scalar_prefetch=1,
            grid=(1,),
            in_specs=[
                pl.BlockSpec((rows, w), lambda i, c: (0, c[0])),
                pl.BlockSpec(g.shape, lambda i, c: (0, 0)),
            ],
            out_specs=pl.BlockSpec((w, g.shape[1]), lambda i, c: (0, 0)),
        ),
        compiler_params=pltpu.CompilerParams(vmem_limit_bytes=40 << 20),
        cost_estimate=pl.CostEstimate(
            flops=2 * rows * w * g.shape[1], transcendentals=0, bytes_accessed=6_000_000
        ),
        name="cross",
    )(col.reshape(1), x, g)


def spread_kernel(at, *refs, groups, width):
    out = refs[-1]
    gx, host, near, gc = at[0], at[1], at[2], at[3]
    block = pl.program_id(0)
    slot = ((block // 2) ^ gx) * 4 + ((block % 2) ^ host)

    def put(flip):
        cut = []
        for t in range(3):
            for n in range(2):
                for core in range(2):
                    for g in range(groups):
                        ref = refs[2 * g + (core ^ flip)]
                        part = ref[slot + 2 * (n ^ near)]
                        cut.append(part[:, t * width : (t + 1) * width])
        out[0] = jnp.concatenate(cut, axis=1).astype(f32)

    for flip in range(2):

        @pl.when(gc == flip)
        def _(flip=flip):
            put(flip)


def spread(arrays, at):
    flat = [x for pair in arrays for x in pair]
    slots, rows, cols = flat[0].shape
    full = lambda i, m: (0, 0, 0)
    groups = len(arrays)
    total = 4 * groups * cols
    return pl.pallas_call(
        functools.partial(spread_kernel, groups=groups, width=cols // 3),
        out_shape=jax.ShapeDtypeStruct((4, rows, total), f32),
        grid_spec=pltpu.PrefetchScalarGridSpec(
            num_scalar_prefetch=1,
            grid=(4,),
            in_specs=[pl.BlockSpec(x.shape, full, pipeline_mode=pl.Buffered(1)) for x in flat],
            out_specs=pl.BlockSpec((1, rows, total), lambda i, m: (i, 0, 0)),
        ),
        compiler_params=pltpu.CompilerParams(vmem_limit_bytes=40 << 20),
        name="spread",
    )(at, *flat).reshape(4 * rows, total)


def rms_inverse(values):
    return lax.rsqrt(jnp.mean(values * values, axis=-1, keepdims=True) + epsilon)


def norm_back(values, inverse, grad_scaled):
    return inverse * grad_scaled - values * (inverse * inverse * inverse) * jnp.mean(
        grad_scaled * values, axis=-1, keepdims=True
    )


def dot(left, right):
    return jnp.dot(left, right, preferred_element_type=f32)


def times_trans(left, right):
    return lax.dot_general(left, right, (((1,), (1,)), ((), ())), preferred_element_type=f32)


def trans_times(left, right):
    return lax.dot_general(left, right, (((0,), (0,)), ((), ())), preferred_element_type=f32)


def rows_at(array, start, count):
    return lax.dynamic_slice_in_dim(array, start, count, 0)


def put_rows(array, rows, start):
    return lax.dynamic_update_slice_in_dim(array, rows, start, 0)


def make_local(sizes):
    def pairs(target):
        found = []
        for gx in range(sizes["gx"]):
            for gc in range(sizes["gc"]):
                for z in range(sizes["ctx"]):
                    for w in range(sizes["wt"]):
                        goal = target(gx, gc, z, w)
                        if goal is not None:
                            found.append((place(gx, gc, z, w), place(*goal)))
        return found

    def place(gx, gc, z, w):
        return ((gx * sizes["gc"] + gc) * sizes["ctx"] + z) * sizes["wt"] + w

    def send(value, target):
        return lax.ppermute(value, AXES, pairs(target))

    def core_mate(gx, gc, z, w):
        return (gx, 1 - gc, z, w)

    def x_mate(gx, gc, z, w):
        return (1 - gx, gc, z, w)

    def near_mate(gx, gc, z, w):
        return (gx, gc, z ^ 1, w)

    def far_mate(gx, gc, z, w):
        return (gx, gc, z ^ 2, w)

    def cross_mate(gx, gc, z, w):
        return (gx, 1 - gc, z ^ 1, w)

    def wt_mate(gx, gc, z, w):
        return (gx, gc, z, 1 - w)

    def to_host(gx, gc, z, w):
        return (gx, z & 1, 2 * gc + (z >> 1), w)

    def to_home(gx, gc, z, w):
        return (gx, z >> 1, 2 * (z & 1) + gc, w)

    def hop1(gx, gc, z, w):
        if gc == 0:
            return (gx, 0, z - 1, w) if z > 0 else None
        return (gx, 1, z + 1, w) if z < 3 else None

    def hop2(gx, gc, z, w):
        if gc == 0:
            return (gx, 0, z - 1, w) if z in (1, 2) else None
        return (gx, 1, z + 1, w) if z in (1, 2) else None

    def hop3(gx, gc, z, w):
        if gc == 0:
            return (gx, 0, z ^ 1, w) if z < 2 else None
        return (gx, 1, z ^ 1, w) if z > 1 else None

    def lane_share(gx, gc, z, w):
        return (gx, 1 - gc, z, w) if gc == z >> 1 else None

    def gather_wt(value):
        if sizes["wt"] == 2:
            other = send(value, wt_mate)
            first = lax.axis_index("wt") == 0
            return jnp.stack([jnp.where(first, value, other), jnp.where(first, other, value)])
        return lax.all_gather(value, "wt", axis=0, tiled=False)

    def scatter_wt(value):
        if sizes["wt"] == 2:
            own = lax.axis_index("wt")
            mine = lax.dynamic_index_in_dim(value, own, 0, keepdims=False)
            other = send(lax.dynamic_index_in_dim(value, 1 - own, 0, keepdims=False), wt_mate)
            return (mine.astype(f32) + other.astype(f32)).astype(bf16)
        return lax.psum_scatter(value, "wt", scatter_dimension=0, tiled=False)

    def halve(value, bit, mate):
        half = value.shape[0] // 2
        other = send(rows_at(value, (1 - bit) * half, half), mate)
        return (rows_at(value, bit * half, half).astype(f32) + other.astype(f32)).astype(bf16)

    def double(value, bit, mate):
        other = send(value, mate)
        first = bit == 0
        return jnp.stack([jnp.where(first, value, other), jnp.where(first, other, value)])

    def sum_all(value):
        for axis in AXES:
            step = 1
            while step < sizes[axis]:

                def mate(gx, gc, z, w, axis=axis, step=step):
                    at = dict(gx=gx, gc=gc, ctx=z, wt=w)
                    at[axis] ^= step
                    return (at["gx"], at["gc"], at["ctx"], at["wt"])

                value = value + send(value, mate)
                step *= 2
        return value

    def local(
        tokens, segments, w_qkv, w_proj, w_in, w_out, gain_attn, gain_mlp, query_scale, cotangent
    ):
        gx, gc, z, wt = (lax.axis_index(axis) for axis in AXES)
        host = z // 2
        near = z % 2
        mine = 2 * near + gc
        parts = sizes["ctx"]
        nh = H // parts
        groups = 2
        rows = tokens.shape[1]
        group_len = segments.shape[1]
        wrows = w_qkv.shape[0]
        lane = gc == host
        pair = sizes["wt"] == 2

        def after(value, *others):
            return lax.optimization_barrier((value,) + others)[0]

        own = tokens[0]
        got1 = send(own, hop1)
        own_share = send(own, lane_share)
        seg_mate = send(segments, core_mate)
        picked = pick(w_qkv, mine, parts, groups, nh)
        got1 = after(got1, picked)
        got2 = send(got1, hop2)
        got1_share = send(got1, lane_share)
        end = jnp.where(gc == 0, z == 0, z == 3)
        if pair:
            other_w = send(picked, wt_mate)
            *flat_w, wide_w = widen(picked, other_w, wt, groups, nh)
        else:
            flat_all = lax.all_gather(picked, "wt", axis=0, tiled=True)
            each = flat_all.shape[1] // groups
            flat_w = [flat_all[:, g * each : (g + 1) * each] for g in range(groups)]
            order = jnp.transpose(flat_all.reshape(D, groups, 3, nh // groups, HD), (0, 2, 1, 3, 4))
            wide_w = jnp.pad(
                order.reshape(D, 3 * nh, HD), ((0, 0), (0, 0), (0, LN - HD))
            ).reshape(D, -1)
        got3 = send(jnp.where(end, own, got2), hop3)
        got2_share = send(got2, lane_share)
        way = 1 - 2 * host
        last = jnp.where(host == 0, jnp.where(z == 0, 3, 0), jnp.where(z == 3, 0, 3))
        places = (z, z + way, z + 2 * way, last)

        half_rows = wrows // 2
        tail_own = jnp.stack([w_proj, w_in, w_out])
        half_w = lax.dynamic_slice_in_dim(tail_own, gc * half_rows, half_rows, 1)
        if pair:
            half_w = send(after(half_w, other_w), wt_mate)
        else:
            half_w = lax.all_gather(half_w, "wt", axis=0, tiled=False)

        dim_scale = scale_base / math.sqrt(HD) * jax.nn.softplus(query_scale)
        lane_scale = jnp.tile(jnp.pad(dim_scale * log2e, (0, LN - HD)), nh)[None]
        ones = jnp.tile(
            ((jnp.arange(LN) >= HD) & (jnp.arange(LN) < HD + 3)).astype(f32), 2 * nh
        )[None]
        seg_row = jnp.where(lane, segments, seg_mate)[0]
        fixed = (lane, mine, gain_attn[None], wide_w, lane_scale, ones, group_len)
        first = project(
            ((own, own_share), (got1, got1_share), (got2, got2_share)), places[:3], *fixed
        )
        got3 = after(got3, first[0])
        got3_share = send(got3, lane_share)
        all_normed, queries, keyval, inputs = project(
            ((got3, got3_share),), places[3:], *fixed, carried=first
        )
        grad_mlp = send(after(cotangent[0], got3), to_host)

        att, att_float, q_aug = attn_fwd(queries, keyval, seg_row, nh)

        trades = (core_mate, near_mate, cross_mate)
        att_pieces = [rows_at(att, (mine ^ j) * rows, rows) for j in range(parts)]
        att_pieces = [att_pieces[0]] + [send(att_pieces[j + 1], trades[j]) for j in range(3)]
        half_mate = send(after(half_w, att), core_mate)
        if pair:
            weights = (tail_own, half_w, half_mate)
            starts = (wt * wrows, (1 - wt) * wrows + gc * half_rows, (1 - wt) * wrows + (1 - gc) * half_rows)
        else:
            one = gc == 0
            tail_w = jnp.stack(
                [jnp.where(one, half_w, half_mate), jnp.where(one, half_mate, half_w)], axis=1
            )
            weights = (jnp.transpose(tail_w, (2, 0, 1, 3, 4)).reshape(3, D, D),)
            starts = ()
        (
            layer_out,
            attended,
            normed_mlp,
            grad_hidden,
            active,
            grad_proj,
            grad_resid,
            *pieces,
            grad_gain_mlp,
        ) = tail(jnp.stack([mine, *starts]), att_pieces, inputs, grad_mlp, weights, gain_mlp[None])
        pieces = [pieces[0]] + [send(pieces[j + 1], trades[j]) for j in range(3)]

        lefts = (attended, normed_mlp, active)
        rights = (grad_proj, grad_hidden, grad_mlp)
        width = D // 2
        if pair:
            to_core = share(lefts, rights, 1 - gc)
            from_core = send(to_core, core_mate)
            layer_out = send(after(layer_out, to_core)[None], to_home)
            a_send, a_keep, b_send, b_keep = keep(
                lefts, rights, from_core, jnp.stack([gc, gx, wt])
            )
            a_got = send(a_send, x_mate)
            b_got = send(b_send, wt_mate)
            ready = a_send
        else:
            layer_out = send(layer_out[None], to_home)

            def by_column(flip):
                one = gc == flip
                return jnp.concatenate(
                    [
                        trans_times(
                            left, jnp.where(one, right[:, :width], right[:, width:])
                        ).astype(bf16)
                        for left, right in zip(lefts, rights)
                    ],
                    axis=1,
                )

            half_grad = send(by_column(1), core_mate)
            half_grad = (by_column(0).astype(f32) + half_grad.astype(f32)).astype(bf16)
            half_grad = lax.psum(scatter_wt(half_grad.reshape(-1, wrows, 3 * width)), ("gx", "ctx"))
            mate_grad = send(half_grad, core_mate)
            one = gc == 0
            totals = []
            for i in range(3):
                a = half_grad[:, i * width : (i + 1) * width]
                b = mate_grad[:, i * width : (i + 1) * width]
                totals.append(
                    jnp.concatenate([jnp.where(one, a, b), jnp.where(one, b, a)], axis=1).astype(f32)
                )
            ready = grad_proj

        scale_row = jnp.tile(dim_scale, nh // groups)[None]

        def backward(group, pieces):
            return attn_bwd(
                q_aug, keyval, pieces, att_float, seg_row, mine, scale_row, nh, group, groups
            )

        def qkv_start(grad):
            if pair:
                sent = cross(all_normed, grad, 1 - wt)
                got = send(sent, wt_mate)
                kept = cross(all_normed, grad, wt)
                return kept.reshape(2, wrows // 2, -1), got.reshape(2, wrows // 2, -1)
            kept = trans_times(all_normed, grad).astype(bf16).reshape(-1, wrows, grad.shape[1])
            kept = scatter_wt(kept).reshape(2, wrows // 2, -1)
            return kept, jnp.zeros_like(kept)

        def qkv_far(kept, got):
            (part, kept), = fold(((kept, got, gx),))
            got = send(part, x_mate)
            quarter = wrows // 4
            (part, kept), = fold(
                ((kept.reshape(2, quarter, -1), got.reshape(2, quarter, -1), host),)
            )
            return kept, send(part, far_mate)

        def qkv_gather(kept, got):
            block = (kept.astype(f32) + got.astype(f32)).astype(bf16)[None]
            for mate in (far_mate, near_mate, x_mate):
                block = jnp.concatenate([block, send(block, mate)])
            return block, send(block, core_mate)

        pieces[3] = after(pieces[3], ready)
        grad_a, lanes_a = backward(0, pieces)
        if pair:
            a_got, b_got = after(a_got, grad_a), after(b_got, grad_a)
            (a_send, a_keep), (b_send, b_keep) = fold(
                (
                    (a_keep, a_got, wt),
                    (b_keep.reshape(2, -1, 3 * width), b_got.reshape(2, -1, 3 * width), gx),
                )
            )
            a_got = send(a_send, wt_mate)
            b_got = send(b_send, x_mate)
            pieces[3] = after(pieces[3], a_send)
        start_a = qkv_start(grad_a)
        pieces[3] = after(pieces[3], start_a[0])
        grad_b, lanes_b = backward(1, pieces)
        if pair:
            a_got, b_got = after(a_got, grad_b), after(b_got, grad_b)
            block = jnp.stack(
                [
                    (k.astype(f32) + g.astype(f32)).astype(bf16)
                    for k, g in ((a_keep, a_got), (b_keep, b_got))
                ]
            )
            block = lax.psum(block, "ctx")
        start_b = qkv_start(grad_b)
        far_a = qkv_far(start_a[0], after(start_a[1], grad_b))
        far_b = qkv_far(*start_b)

        def shard_grad(shard):
            return sum(
                times_trans(rows_at(grad, shard * rows, rows), w)
                for grad, w in zip((after(grad_a, start_b[0]), after(grad_b, start_b[0])), flat_w)
            )

        to_core = jnp.stack([shard_grad(mine ^ 3), shard_grad(mine ^ 1)]).astype(bf16)
        from_core = send(to_core, core_mate).astype(f32)
        to_near = (shard_grad(mine ^ 2) + from_core[0]).astype(bf16)
        grad_normed = shard_grad(mine) + from_core[1] + send(to_near, near_mate).astype(f32)
        inputs = inputs.astype(f32)
        inverse_attn = rms_inverse(inputs)
        grad_gain_attn = jnp.sum(grad_normed * inputs * inverse_attn, axis=0)
        grad_tokens = send(
            (grad_resid + norm_back(inputs, inverse_attn, grad_normed * gain_attn)).astype(bf16)[None],
            to_home,
        )

        total_qkv = spread(
            [qkv_gather(*far_a), qkv_gather(*far_b)], jnp.stack([gx, host, near, gc])
        )
        if pair:
            from_x = send(block, x_mate)
            totals = place_tail(
                block, from_x, send(block, core_mate), send(from_x, core_mate), jnp.stack([gx, gc])
            )

        grad_query_scale = (
            (lanes_a + lanes_b)[0, :HD]
            / (dim_scale * log2e)
            * (scale_base / math.sqrt(HD))
            * jax.nn.sigmoid(query_scale)
        )
        small = jnp.concatenate(
            [grad_gain_attn, grad_gain_mlp[0], jnp.pad(grad_query_scale, (0, LN - HD))]
        ).reshape(-1, LN)
        small = sum_all(small).reshape(-1)
        return (
            layer_out,
            grad_tokens,
            total_qkv,
            *totals,
            small[:D],
            small[D : 2 * D],
            small[2 * D : 2 * D + HD],
        )

    return local


def solution(mesh):
    groups, parts, wt = (mesh.shape[axis] for axis in ("grp", "ctx", "wt"))
    inner = Mesh(mesh.devices.reshape(groups // 2, 2, parts, wt), AXES)
    sizes = dict(inner.shape)
    split = P(("gx", "gc", "wt"), "ctx", None)
    weight = P("wt", None)
    return jax.shard_map(
        make_local(sizes),
        mesh=inner,
        in_specs=(
            split,
            P(("gx", "gc", "wt"), None),
            weight,
            weight,
            weight,
            weight,
            P(),
            P(),
            P(),
            split,
        ),
        out_specs=(split, split, weight, weight, weight, weight, P(), P(), P()),
        check_vma=False,
    )
```

time: 805 us -> 586 us (0.73)
  local copies, waits for them, and re-layouts: 215 us -> 68.9 us
  Pallas kernels: 81.4 us -> 166 us
  other arithmetic: 78.4 us -> 22.8 us
  waiting for transfers between devices: 251 us -> 210 us
  matrix products: 57.3 us -> 18.1 us
  starting transfers between devices: 96.2 us -> 79.6 us
    pallas_call x1 -> x20, Pallas kernels: 44.8 us -> 141 us  [the longest x2 50.6 us: attn_bwd(): pl.pallas_call(functools.partial(bwd_kernel, first=group * nh, nh=nh, bq=...]
    dynamic_update_slice x7 -> x0, local copies, waits for them, and re-layouts: 45.2 us -> none  [put_rows(): return lax.dynamic_update_slice_in_dim(array, rows, start, 0)]
    dot_general x11 -> x0, matrix products: 40.9 us -> none  [the longest x7 22 us: dot(): return jnp.dot(left, right, preferred_element_type=f32)]
    psum x1, waiting for transfers between devices: 43.1 us -> 3.02 us  [local(): block = lax.psum(block, 'ctx')]
    another operation x15 -> x11, other arithmetic: 35 us -> 8.74 us  [the longest x3 3.62 us: local(): jnp.stack([(k.astype(f32) + g.astype(f32)).astype(bf16) for k, g in ((a_k...]
    slice x9 -> x0, local copies, waits for them, and re-layouts: 25 us -> none  [the longest x5 10.8 us: local(): grad_perm[j * cols:(j + 1) * cols]]
    concatenate x3 -> x0, local copies, waits for them, and re-layouts: 17.6 us -> none  [the longest x1 13.8 us: local(): jnp.concatenate([grad_w_proj, trans_times(normed_mlp, grad_hidden).astype...]
    ppermute x37 -> x49, starting transfers between devices: 96.2 us -> 79.5 us  [send(): return lax.ppermute(value, AXES, pairs(target))]
  transfers between devices with their start and end apart: 38 -> 50, of which waited for: 19 -> 18; matrix products, arithmetic and copies ran while one was open for 38% -> 10% of each run, Pallas kernels for 10% -> 24%
where the time goes in v2:
time: 586 us; the launch traced here: 581 us
  waiting for transfers between devices  210 us (36%)
  Pallas kernels  166 us (28%)
  starting transfers between devices  79.6 us (14%)
  local copies, waits for them, and re-layouts  68.9 us (12%)
  other arithmetic  22.8 us (4%)
  matrix products  18.1 us (3%)
  between operations  15.3 us (3%)
    ppermute x49, waiting for transfers between devices, send(): return lax.ppermute(value, AXES, pairs(target))  207 us
    ppermute x49, starting transfers between devices, send(): return lax.ppermute(value, AXES, pairs(target))  79.5 us
    pallas_call x2, Pallas kernels, attn_bwd(): pl.pallas_call(functools.partial(bwd_kernel, first=group * nh, nh=nh, bq=...  50.6 us
    unnamed x182, local copies, waits for them, and re-layouts  49 us
    pallas_call x1, Pallas kernels, attn_fwd(): pl.pallas_call(functools.partial(fwd_kernel, nh=nh, bq=bq, bk=bk, nk=n //...  25 us
    pallas_call x1, Pallas kernels, tail(): pl.pallas_call(body, out_shape=[jax.ShapeDtypeStruct((rows, d), bf16)] *...  22 us
    pallas_call x2, Pallas kernels, project(): pl.pallas_call(functools.partial(project_kernel, count=count, width=width...  20.7 us
    dot_general x8, matrix products, times_trans(): lax.dot_general(left, right, (((1,), (1,)), ((), ())), preferred_element_...  18.1 us
  transfers between devices with their start and end apart: 50, of which 18 were waited for; matrix products, arithmetic and copies ran while one was open for 10% of the time, Pallas kernels for 24%

profile of v2, /device:TPU:0, one launch (start us, length us, event | category | flops | bytes accessed | tf_op | source)
XLA Modules:
  0.0 580.5 jit_solution(7408559619803218542)
XLA Ops:
  8.5 4.6 pick.1.a_ref
  13.1 14.9 %collective-permute-done.1.refs_2_ = bf16[512,1280]{1,0:T(8,128)(2,1)} collective-permute-done((bf16[512,1280]{1,0:T(8,128)(2,1)}, bf16[512,1280]{1,0:T(8,128)(2,1)}, u32[]{:S(2)}, u32[]{:S(2)}) %collective-permute-start.1) | collective-permute-done | bytes 1310752 | tf_op jit(solution)/shard_map/ppermute | solution.py:837
  38.6 9.1 %collective-permute-done.2.refs_4_ = bf16[512,1280]{1,0:T(8,128)(2,1)S(1)} collective-permute-done((bf16[512,1280]{1,0:T(8,128)(2,1)}, bf16[512,1280]{1,0:T(8,128)(2,1)S(1)}, u32[]{:S(2)}, u32[]{:S(2)}) %collective-permute-start.2) | collective-permute-done | bytes 1310752 | tf_op jit(solution)/shard_map/ppermute | solution.py:837
  50.0 3.9 collective-permute-start.3
  65.0 7.8 %widen.1 = (bf16[1280,480]{1,0:T(8,128)(2,1)}, bf16[1280,480]{1,0:T(8,128)(2,1)}, bf16[1280,1536]{1,0:T(8,128)(2,1)}) custom-call(s32[1]{0:T(128)} %bitcast.13.own_first.col, bf16[640,960]{1,0:T(8,128)(2,1)} %pick.1.a_ref, bf16[640,960]{1,0:T(8,128)(2,1)} %copy.32.b_ref), custom_call_target="tpu_custom_call" | custom-call | tf_op jit(solution)/shard_map/widen/pallas_call | solution.py:375
  72.9 14.0 %project.2 = (bf16[2048,1280]{1,0:T(8,128)(2,1)}, bf16[2048,512]{1,0:T(8,128)(2,1)}, bf16[2048,1024]{1,0:T(8,128)(2,1)}, bf16[512,1280]{1,0:T(8,128)(2,1)S(1)}) custom-call(s32[5]{0:T(128)S(1)} %stack.122.info, bf16[512,1280]{1,0:T(8,128)(2,1)S(1)} %bitcast.104, bf16[512,1280]{1,0:T(8,128)(2,1)} %collective-permute-done.4.refs_1_, ...), custom_call_target="tpu_custom_call" | custom-call | tf_op jit(solution)/shard_map/project/pallas_call | solution.py:446
  96.5 6.8 %project.3 = (bf16[2048,1280]{1,0:T(8,128)(2,1)}, bf16[2048,512]{1,0:T(8,128)(2,1)}, bf16[2048,1024]{1,0:T(8,128)(2,1)}, bf16[512,1280]{1,0:T(8,128)(2,1)S(1)}) custom-call(s32[3]{0:T(128)S(1)} %pad_add_fusion.1.info, bf16[512,1280]{1,0:T(8,128)(2,1)S(1)} %collective-permute-done.3.refs_0_, ...), custom_call_target="tpu_custom_call", output_to_operand_aliasing={{0}: (8, {}), {1}: (9, {}), {2}: (10, {})} | custom-call | tf_op jit(solution)/shard_map/project/pallas_call | solution.py:446
  105.3 25.0 %attn_fwd.1 = (bf16[2048,320]{1,0:T(8,128)(2,1)S(1)}, f32[2048,512]{1,0:T(8,128)S(1)}, bf16[2048,512]{1,0:T(8,128)(2,1)S(1)}) custom-call(s32[16]{0:T(128)S(1)} %reshape.214.flags, bf16[2048,512]{1,0:T(8,128)(2,1)S(1)} %copy-done.32, bf16[2048,1024]{1,0:T(8,128)(2,1)} %get-tuple-element.82.kv.kk.vv, s32[2048,1]{1,0:T(8,128)S(1)} %copy-done.36, ...), custom_call_target="tpu_custom_call" | custom-call | flops 20000000000 | bytes 16000000 | tf_op jit(solution)/shard_map/attn_fwd/pallas_call | solution.py:159
  133.5 13.4 %collective-permute-done.13.half = bf16[3,320,1280]{2,1,0:T(8,128)(2,1)} collective-permute-done((bf16[3,320,1280]{2,1,0:T(8,128)(2,1)}, bf16[3,320,1280]{2,1,0:T(8,128)(2,1)}, u32[]{:S(2)}, u32[]{:S(2)}) %collective-permute-start.13) | collective-permute-done | bytes 2457632 | tf_op jit(solution)/shard_map/ppermute | solution.py:837
  150.5 5.3 collective-permute-start.9
  157.3 22.9 %collective-permute-done.10.p2 = bf16[512,320]{1,0:T(8,128)(2,1)S(1)} collective-permute-done((bf16[512,320]{1,0:T(8,128)(2,1)}, bf16[512,320]{1,0:T(8,128)(2,1)S(1)}, u32[]{:S(2)}, u32[]{:S(2)}) %collective-permute-start.10) | collective-permute-done | bytes 327712 | tf_op jit(solution)/shard_map/ppermute | solution.py:837
  181.1 22.0 %tail.1 = (bf16[512,1280]{1,0:T(8,128)(2,1)}, bf16[512,1280]{1,0:T(8,128)(2,1)}, bf16[512,1280]{1,0:T(8,128)(2,1)}, bf16[512,1280]{1,0:T(8,128)(2,1)}, bf16[512,...) custom-call(s32[4]{0:T(128)S(1)} %pad_add_fusion.at, ...), custom_call_target="tpu_custom_call" | custom-call | flops 10000000000 | bytes 25000000 | tf_op jit(solution)/shard_map/tail/pallas_call | solution.py:551
  211.7 5.2 share.1
  216.9 5.6 collective-permute-start.19
  225.5 5.7 collective-permute-done.19.got
  236.5 7.6 %keep.1 = (bf16[2,160,1920]{2,1,0:T(8,128)(2,1)}, bf16[2,160,1920]{2,1,0:T(8,128)(2,1)S(1)}, bf16[320,1920]{1,0:T(8,128)(2,1)}, bf16[320,1920]{1,0:T(8,128)(2,1)S(1)}) custom-call(s32[3]{0:T(128)S(1)} %pad_add_fusion.2.at, bf16[512,1280]{1,0:T(8,128)(2,1)S(1)} %copy-done.16, bf16[512,1280]{1,0:T(8,128)(2,1)S(1)} %copy-done.18, ...), custom_call_target="tpu_custom_call" | custom-call | flops 2500000000 | bytes 16000000 | tf_op jit(solution)/shard_map/keep/pallas_call | solution.py:631
  249.3 25.2 %attn_bwd.2 = (bf16[2048,480]{1,0:T(8,128)(2,1)S(1)}, f32[8,128]{1,0:T(8,128)S(1)}) custom-call(s32[16]{0:T(128)S(1)} %reshape.214.flags, s32[1]{0:T(128)} %bitcast.mine, bf16[2048,512]{1,0:T(8,128)(2,1)} %copy-done.54, bf16[2048,1024]{1,0:T(8,128)(2,1)} %get-tuple-element.82.kv.kk.vv, bf16[2048,1024]{1,0:T(8,128)(2,1)} %get-tuple-element.82.kv.kk.vv, ...), custom_call_target="tpu_custom_call" | custom-call | flops 15000000512 | bytes 20000000 | tf_op jit(solution)/shard_map/attn_bwd/pallas_call | solution.py:293
  289.3 25.5 %attn_bwd.3 = (bf16[2048,480]{1,0:T(8,128)(2,1)S(1)}, f32[8,128]{1,0:T(8,128)S(1)}) custom-call(s32[16]{0:T(128)S(1)} %reshape.214.flags, s32[1]{0:T(128)} %bitcast.mine, bf16[2048,512]{1,0:T(8,128)(2,1)} %copy-done.54, bf16[2048,1024]{1,0:T(8,128)(2,1)} %get-tuple-element.82.kv.kk.vv, bf16[2048,1024]{1,0:T(8,128)(2,1)} %get-tuple-element.82.kv.kk.vv, ...), custom_call_target="tpu_custom_call" | custom-call | flops 15000000512 | bytes 20000000 | tf_op jit(solution)/shard_map/attn_bwd/pallas_call | solution.py:293
  328.2 9.2 %collective-permute-done.26 = bf16[320,480]{1,0:T(8,128)(2,1)S(1)} collective-permute-done((bf16[320,480]{1,0:T(8,128)(2,1)S(1)}, bf16[320,480]{1,0:T(8,128)(2,1)S(1)}, u32[]{:S(2)}, u32[]{:S(2)}) %collective-permute-start.26) | collective-permute-done | bytes 307232 | tf_op jit(solution)/shard_map/ppermute | solution.py:837
  354.2 3.9 fusion.19
  358.1 3.7 collective-permute-done.28
  361.8 11.4 %collective-permute-start.15 = (bf16[1,512,1280]{2,1,0:T(8,128)(2,1)}, bf16[1,512,1280]{2,1,0:T(8,128)(2,1)}, u32[]{:S(2)}, u32[]{:S(2)}) collective-permute-start(bf16[1,512,1280]{2,1,0:T(8,128)(2,1)} %bitcast.22), channel_id=1, source_target_pairs={{0,0},{1,1},{2,4},{3,5},{4,8},{5,9},{6,12},{7,13},{8,2},{9,3},{10,... | collective-permute-start | bytes 3932168 | tf_op jit(solution)/shard_map/ppermute | solution.py:837
  402.6 3.4 fusion.28
  406.0 41.0 %collective-permute-done.35 = bf16[1,160,480]{2,1,0:T(8,128)(2,1)S(1)} collective-permute-done((bf16[1,160,480]{2,1,0:T(8,128)(2,1)S(1)}, bf16[1,160,480]{2,1,0:T(8,128)(2,1)S(1)}, u32[]{:S(2)}, u32[]{:S(2)}) %collective-permute-start.35) | collective-permute-done | bytes 153632 | tf_op jit(solution)/shard_map/ppermute | solution.py:837
  452.2 19.1 %collective-permute-done.36 = bf16[2,160,480]{2,1,0:T(8,128)(2,1)S(1)} collective-permute-done((bf16[2,160,480]{2,1,0:T(8,128)(2,1)S(1)}, bf16[2,160,480]{2,1,0:T(8,128)(2,1)S(1)}, u32[]{:S(2)}, u32[]{:S(2)}) %collective-permute-start.36) | collective-permute-done | bytes 307232 | tf_op jit(solution)/shard_map/ppermute | solution.py:837
  480.2 4.9 fusion.15
  485.7 5.8 %collective-permute-done.37 = bf16[4,160,480]{2,1,0:T(8,128)(2,1)} collective-permute-done((bf16[4,160,480]{2,1,0:T(8,128)(2,1)}, bf16[4,160,480]{2,1,0:T(8,128)(2,1)}, u32[]{:S(2)}, u32[]{:S(2)}) %collective-permute-start.37) | collective-permute-done | bytes 614432 | tf_op jit(solution)/shard_map/ppermute | solution.py:837
  492.9 24.8 %collective-permute-done.44 = f32[21,128]{1,0:T(8,128)S(1)} collective-permute-done((f32[21,128]{1,0:T(8,128)S(1)}, f32[21,128]{1,0:T(8,128)S(1)}, u32[]{:S(2)}, u32[]{:S(2)}) %collective-permute-start.44) | collective-permute-done | bytes 10784 | tf_op jit(solution)/shard_map/ppermute | solution.py:837
  523.5 3.5 collective-permute-start.47
  527.0 28.6 %collective-permute-done.47 = f32[21,128]{1,0:T(8,128)S(1)} collective-permute-done((f32[21,128]{1,0:T(8,128)S(1)}, f32[21,128]{1,0:T(8,128)S(1)}, u32[]{:S(2)}, u32[]{:S(2)}) %collective-permute-start.47) | collective-permute-done | bytes 10784 | tf_op jit(solution)/shard_map/ppermute | solution.py:837
  557.4 6.9 %spread.1 = f32[4,160,3840]{2,1,0:T(8,128)} custom-call(s32[4]{0:T(128)S(1)} %pad_add_fusion.4.at, bf16[8,160,480]{2,1,0:T(8,128)(2,1)} %pad_maximum_fusion.2.refs_0_, bf16[8,160,480]{2,1,0:T(8,128)(2,1)} %collective-permute-done.31.refs_1_, bf16[8,160,480]{2,1,0:T(8,128)(2,1)S(1)} %pad_maximum_fusion.3.refs_2_, ...), custom_call_target="tpu_custom_call" | custom-call | tf_op jit(solution)/shard_map/spread/pallas_call | solution.py:777
  565.4 4.6 place_tail.1
  (347 shorter events, 170.1 us)
Async XLA Ops:
  7.2 471.6 %all-reduce.4.cloned.1.call-start = ((), (), s32[]{:S(2)}) async-start(), calls=%async_computation | async-start | bytes 2457600 | tf_op jit(solution)/shard_map/psum | solution.py:1117
  29.3 43.5 %collective-permute-start.4 = (bf16[512,1280]{1,0:T(8,128)(2,1)S(1)}, bf16[512,1280]{1,0:T(8,128)(2,1)}, u32[]{:S(2)}, u32[]{:S(2)}) collective-permute-start(bf16[512,1280]{1,0:T(8,128)(2,1)S(1)} %bitcast.103), channel_id=1, source_target_pairs={{0,8},{1,9},{2,10},{3,11},{12,4},{13,5},{14,6},{15,7},{16,24},{17,... | collective-permute-start | bytes 3932168 | tf_op jit(solution)/shard_map/ppermute | solution.py:837
  34.1 28.3 %collective-permute-start.7 = (bf16[640,960]{0,1:T(8,128)(2,1)}, bf16[640,960]{0,1:T(8,128)(2,1)}, u32[]{:S(2)}, u32[]{:S(2)}) collective-permute-start(bf16[640,960]{0,1:T(8,128)(2,1)} %copy.31), channel_id=1, source_target_pairs={{0,1},{1,0},{2,3},{3,2},{4,5},{5,4},{6,7},{7,6},{8,9},{9,8},{10,11... | collective-permute-start | bytes 3686408 | tf_op jit(solution)/shard_map/ppermute | solution.py:837
  36.1 36.8 %collective-permute-start.5 = (bf16[512,1280]{1,0:T(8,128)(2,1)}, bf16[512,1280]{1,0:T(8,128)(2,1)}, u32[]{:S(2)}, u32[]{:S(2)}) collective-permute-start(bf16[512,1280]{1,0:T(8,128)(2,1)} %collective-permute-done.1.refs_2_), channel_id=1, source_target_pairs={{0,8},{1,9},{2,10},{3,11},{12,4},{13,5},{14,6},{15,7},{16,24},{17,... | collective-permute-start | bytes 3932168 | tf_op jit(solution)/shard_map/ppermute | solution.py:837
  50.0 37.9 %collective-permute-start.3 = (bf16[512,1280]{1,0:T(8,128)(2,1)}, bf16[512,1280]{1,0:T(8,128)(2,1)S(1)}, u32[]{:S(2)}, u32[]{:S(2)}) collective-permute-start(bf16[512,1280]{1,0:T(8,128)(2,1)} %broadcast_select_fusion), channel_id=1, source_target_pairs={{0,2},{1,3},{2,0},{3,1},{12,14},{13,15},{14,12},{15,13},{16,18},{1... | collective-permute-start | bytes 3932168 | tf_op jit(solution)/shard_map/ppermute | solution.py:837
  62.4 28.2 %collective-permute-start = (s32[1,2048]{1,0:T(1,128)S(1)}, s32[1,2048]{1,0:T(1,128)S(1)}, u32[]{:S(2)}, u32[]{:S(2)}) collective-permute-start(s32[1,2048]{1,0:T(1,128)S(1)} %copy-done.80), channel_id=1, source_target_pairs={{0,8},{1,9},{2,10},{3,11},{4,12},{5,13},{6,14},{7,15},{8,0},{9,1},... | collective-permute-start | bytes 24584 | tf_op jit(solution)/shard_map/ppermute | solution.py:837
  92.1 54.9 %collective-permute-start.13 = (bf16[3,320,1280]{2,1,0:T(8,128)(2,1)}, bf16[3,320,1280]{2,1,0:T(8,128)(2,1)}, u32[]{:S(2)}, u32[]{:S(2)}) collective-permute-start(bf16[3,320,1280]{2,1,0:T(8,128)(2,1)} %constant_dynamic-slice_fusion), channel_id=1, source_target_pairs={{0,1},{1,0},{2,3},{3,2},{4,5},{5,4},{6,7},{7,6},{8,9},{9,8},{10,11... | collective-permute-start | bytes 7372808 | tf_op jit(solution)/shard_map/ppermute | solution.py:837
  147.0 33.2 %collective-permute-start.14 = (bf16[3,320,1280]{2,1,0:T(8,128)(2,1)}, bf16[3,320,1280]{2,1,0:T(8,128)(2,1)}, u32[]{:S(2)}, u32[]{:S(2)}) collective-permute-start(bf16[3,320,1280]{2,1,0:T(8,128)(2,1)} %collective-permute-done.13.half), channel_id=1, source_target_pairs={{0,8},{1,9},{2,10},{3,11},{4,12},{5,13},{6,14},{7,15},{8,0},{9,1},... | collective-permute-start | bytes 7372808 | tf_op jit(solution)/shard_map/ppermute | solution.py:837
  155.7 24.5 %collective-permute-start.10 = (bf16[512,320]{1,0:T(8,128)(2,1)}, bf16[512,320]{1,0:T(8,128)(2,1)S(1)}, u32[]{:S(2)}, u32[]{:S(2)}) collective-permute-start(bf16[512,320]{1,0:T(8,128)(2,1)} %get-tuple-element.146), channel_id=1, source_target_pairs={{0,2},{1,3},{2,0},{3,1},{4,6},{5,7},{6,4},{7,5},{8,10},{9,11},{10,... | collective-permute-start | bytes 983048 | tf_op jit(solution)/shard_map/ppermute | solution.py:837
  156.3 23.9 %collective-permute-start.11 = (bf16[512,320]{1,0:T(8,128)(2,1)}, bf16[512,320]{1,0:T(8,128)(2,1)S(1)}, u32[]{:S(2)}, u32[]{:S(2)}) collective-permute-start(bf16[512,320]{1,0:T(8,128)(2,1)} %get-tuple-element.145), channel_id=1, source_target_pairs={{0,10},{1,11},{2,8},{3,9},{4,14},{5,15},{6,12},{7,13},{8,2},{9,3},... | collective-permute-start | bytes 983048 | tf_op jit(solution)/shard_map/ppermute | solution.py:837
  222.7 26.5 %collective-permute-start.16 = (bf16[512,320]{1,0:T(8,128)(2,1)}, bf16[512,320]{1,0:T(8,128)(2,1)S(1)}, u32[]{:S(2)}, u32[]{:S(2)}) collective-permute-start(bf16[512,320]{1,0:T(8,128)(2,1)} %get-tuple-element.98), channel_id=1, source_target_pairs={{0,8},{1,9},{2,10},{3,11},{4,12},{5,13},{6,14},{7,15},{8,0},{9,1},... | collective-permute-start | bytes 983048 | tf_op jit(solution)/shard_map/ppermute | solution.py:837
  222.7 26.5 %collective-permute-start.17 = (bf16[512,320]{1,0:T(8,128)(2,1)}, bf16[512,320]{1,0:T(8,128)(2,1)S(1)}, u32[]{:S(2)}, u32[]{:S(2)}) collective-permute-start(bf16[512,320]{1,0:T(8,128)(2,1)} %get-tuple-element.99), channel_id=1, source_target_pairs={{0,2},{1,3},{2,0},{3,1},{4,6},{5,7},{6,4},{7,5},{8,10},{9,11},{10,... | collective-permute-start | bytes 983048 | tf_op jit(solution)/shard_map/ppermute | solution.py:837
  225.4 22.3 %collective-permute-start.18 = (bf16[512,320]{1,0:T(8,128)(2,1)}, bf16[512,320]{1,0:T(8,128)(2,1)S(1)}, u32[]{:S(2)}, u32[]{:S(2)}) collective-permute-start(bf16[512,320]{1,0:T(8,128)(2,1)} %get-tuple-element.100), channel_id=1, source_target_pairs={{0,10},{1,11},{2,8},{3,9},{4,14},{5,15},{6,12},{7,13},{8,2},{9,3},... | collective-permute-start | bytes 983048 | tf_op jit(solution)/shard_map/ppermute | solution.py:837
  246.2 37.6 %collective-permute-start.20 = (bf16[2,160,1920]{2,1,0:T(8,128)(2,1)}, bf16[2,160,1920]{2,1,0:T(8,128)(2,1)S(1)}, u32[]{:S(2)}, u32[]{:S(2)}) collective-permute-start(bf16[2,160,1920]{2,1,0:T(8,128)(2,1)} %get-tuple-element.101), channel_id=1, source_target_pairs={{0,16},{1,17},{2,18},{3,19},{4,20},{5,21},{6,22},{7,23},{8,24},{9,... | collective-permute-start | bytes 3686408 | tf_op jit(solution)/shard_map/ppermute | solution.py:837
  247.7 36.1 %collective-permute-start.21 = (bf16[320,1920]{1,0:T(8,128)(2,1)}, bf16[320,1920]{1,0:T(8,128)(2,1)}, u32[]{:S(2)}, u32[]{:S(2)}) collective-permute-start(bf16[320,1920]{1,0:T(8,128)(2,1)} %get-tuple-element.109), channel_id=1, source_target_pairs={{0,1},{1,0},{2,3},{3,2},{4,5},{5,4},{6,7},{7,6},{8,9},{9,8},{10,11... | collective-permute-start | bytes 3686408 | tf_op jit(solution)/shard_map/ppermute | solution.py:837
  279.2 43.4 %collective-permute-start.25 = (bf16[640,480]{0,1:T(8,128)(2,1)}, bf16[640,480]{0,1:T(8,128)(2,1)}, u32[]{:S(2)}, u32[]{:S(2)}) collective-permute-start(bf16[640,480]{0,1:T(8,128)(2,1)} %copy.36), channel_id=1, source_target_pairs={{0,1},{1,0},{2,3},{3,2},{4,5},{5,4},{6,7},{7,6},{8,9},{9,8},{10,11... | collective-permute-start | bytes 1843208 | tf_op jit(solution)/shard_map/ppermute | solution.py:837
  322.6 64.9 %collective-permute-start.22 = (bf16[2,512,1280]{2,1,0:T(8,128)(2,1)}, bf16[2,512,1280]{2,1,0:T(8,128)(2,1)}, u32[]{:S(2)}, u32[]{:S(2)}) collective-permute-start(bf16[2,512,1280]{2,1,0:T(8,128)(2,1)} %pad_maximum_fusion.1), channel_id=1, source_target_pairs={{0,8},{1,9},{2,10},{3,11},{4,12},{5,13},{6,14},{7,15},{8,0},{9,1},... | collective-permute-start | bytes 7864328 | tf_op jit(solution)/shard_map/ppermute | solution.py:837
  340.2 40.7 %collective-permute-start.39 = (bf16[160,1920]{1,0:T(8,128)(2,1)}, bf16[160,1920]{1,0:T(8,128)(2,1)}, u32[]{:S(2)}, u32[]{:S(2)}) collective-permute-start(bf16[160,1920]{1,0:T(8,128)(2,1)} %copy-done.45), channel_id=1, source_target_pairs={{0,1},{1,0},{2,3},{3,2},{4,5},{5,4},{6,7},{7,6},{8,9},{9,8},{10,11... | collective-permute-start | bytes 1843208 | tf_op jit(solution)/shard_map/ppermute | solution.py:837
  350.5 23.5 %collective-permute-start.32 = (bf16[640,480]{0,1:T(8,128)(2,1)}, bf16[640,480]{0,1:T(8,128)(2,1)S(1)}, u32[]{:S(2)}, u32[]{:S(2)}) collective-permute-start(bf16[640,480]{0,1:T(8,128)(2,1)} %copy.38), channel_id=1, source_target_pairs={{0,1},{1,0},{2,3},{3,2},{4,5},{5,4},{6,7},{7,6},{8,9},{9,8},{10,11... | collective-permute-start | bytes 1843208 | tf_op jit(solution)/shard_map/ppermute | solution.py:837
  351.0 28.4 %collective-permute-start.40 = (bf16[160,1920]{1,0:T(8,128)(2,1)}, bf16[160,1920]{1,0:T(8,128)(2,1)}, u32[]{:S(2)}, u32[]{:S(2)}) collective-permute-start(bf16[160,1920]{1,0:T(8,128)(2,1)} %copy-done.46), channel_id=1, source_target_pairs={{0,16},{1,17},{2,18},{3,19},{4,20},{5,21},{6,22},{7,23},{8,24},{9,... | collective-permute-start | bytes 1843208 | tf_op jit(solution)/shard_map/ppermute | solution.py:837
  361.8 161.7 %collective-permute-start.15 = (bf16[1,512,1280]{2,1,0:T(8,128)(2,1)}, bf16[1,512,1280]{2,1,0:T(8,128)(2,1)}, u32[]{:S(2)}, u32[]{:S(2)}) collective-permute-start(bf16[1,512,1280]{2,1,0:T(8,128)(2,1)} %bitcast.22), channel_id=1, source_target_pairs={{0,0},{1,1},{2,4},{3,5},{4,8},{5,9},{6,12},{7,13},{8,2},{9,3},{10,... | collective-permute-start | bytes 3932168 | tf_op jit(solution)/shard_map/ppermute | solution.py:837
  393.0 87.2 %collective-permute-start.23 = (bf16[512,1280]{1,0:T(8,128)(2,1)}, bf16[512,1280]{1,0:T(8,128)(2,1)}, u32[]{:S(2)}, u32[]{:S(2)}) collective-permute-start(bf16[512,1280]{1,0:T(8,128)(2,1)} %fusion.3), channel_id=1, source_target_pairs={{0,2},{1,3},{2,0},{3,1},{4,6},{5,7},{6,4},{7,5},{8,10},{9,11},{10,... | collective-permute-start | bytes 3932168 | tf_op jit(solution)/shard_map/ppermute | solution.py:837
  397.4 52.6 %collective-permute-start.30 = (bf16[4,160,480]{2,1,0:T(8,128)(2,1)S(1)}, bf16[4,160,480]{2,1,0:T(8,128)(2,1)S(1)}, u32[]{:S(2)}, u32[]{:S(2)}) collective-permute-start(bf16[4,160,480]{2,1,0:T(8,128)(2,1)S(1)} %pad_maximum_fusion.5), channel_id=1, source_target_pairs={{0,16},{1,17},{2,18},{3,19},{4,20},{5,21},{6,22},{7,23},{8,24},{9,... | collective-permute-start | bytes 1843208 | tf_op jit(solution)/shard_map/ppermute | solution.py:837
  401.3 45.7 %collective-permute-start.35 = (bf16[1,160,480]{2,1,0:T(8,128)(2,1)S(1)}, bf16[1,160,480]{2,1,0:T(8,128)(2,1)S(1)}, u32[]{:S(2)}, u32[]{:S(2)}) collective-permute-start(bf16[1,160,480]{2,1,0:T(8,128)(2,1)S(1)} %fusion.32), channel_id=1, source_target_pairs={{0,4},{1,5},{2,6},{3,7},{4,0},{5,1},{6,2},{7,3},{8,12},{9,13},{10,... | collective-permute-start | bytes 460808 | tf_op jit(solution)/shard_map/ppermute | solution.py:837
  447.0 24.4 %collective-permute-start.36 = (bf16[2,160,480]{2,1,0:T(8,128)(2,1)S(1)}, bf16[2,160,480]{2,1,0:T(8,128)(2,1)S(1)}, u32[]{:S(2)}, u32[]{:S(2)}) collective-permute-start(bf16[2,160,480]{2,1,0:T(8,128)(2,1)S(1)} %pad_maximum_fusion.8), channel_id=1, source_target_pairs={{0,2},{1,3},{2,0},{3,1},{4,6},{5,7},{6,4},{7,5},{8,10},{9,11},{10,... | collective-permute-start | bytes 921608 | tf_op jit(solution)/shard_map/ppermute | solution.py:837
  452.2 103.5 %collective-permute-start.31 = (bf16[8,160,480]{2,1,0:T(8,128)(2,1)}, bf16[8,160,480]{2,1,0:T(8,128)(2,1)}, u32[]{:S(2)}, u32[]{:S(2)}) collective-permute-start(bf16[8,160,480]{2,1,0:T(8,128)(2,1)} %pad_maximum_fusion.2.refs_0_), channel_id=1, source_target_pairs={{0,8},{1,9},{2,10},{3,11},{4,12},{5,13},{6,14},{7,15},{8,0},{9,1},... | collective-permute-start | bytes 3686408 | tf_op jit(solution)/shard_map/ppermute | solution.py:837
  478.7 48.3 %collective-permute-start.41 = (bf16[2,160,1920]{2,1,0:T(8,128)(2,1)}, bf16[2,160,1920]{2,1,0:T(8,128)(2,1)S(1)}, u32[]{:S(2)}, u32[]{:S(2)}) collective-permute-start(bf16[2,160,1920]{2,1,0:T(8,128)(2,1)} %all-reduce.4.cloned.1.call-done.c_ref), channel_id=1, source_target_pairs={{0,16},{1,17},{2,18},{3,19},{4,20},{5,21},{6,22},{7,23},{8,24},{9,... | collective-permute-start | bytes 3686408 | tf_op jit(solution)/shard_map/ppermute | solution.py:837
  485.1 32.6 %collective-permute-start.44 = (f32[21,128]{1,0:T(8,128)S(1)}, f32[21,128]{1,0:T(8,128)S(1)}, u32[]{:S(2)}, u32[]{:S(2)}) collective-permute-start(f32[21,128]{1,0:T(8,128)S(1)} %fusion.33), channel_id=1, source_target_pairs={{0,16},{1,17},{2,18},{3,19},{4,20},{5,21},{6,22},{7,23},{8,24},{9,... | collective-permute-start | bytes 32264 | tf_op jit(solution)/shard_map/ppermute | solution.py:837
  492.8 64.6 %collective-permute-start.38 = (bf16[8,160,480]{2,1,0:T(8,128)(2,1)S(1)}, bf16[8,160,480]{2,1,0:T(8,128)(2,1)S(1)}, u32[]{:S(2)}, u32[]{:S(2)}) collective-permute-start(bf16[8,160,480]{2,1,0:T(8,128)(2,1)S(1)} %pad_maximum_fusion.3.refs_2_), channel_id=1, source_target_pairs={{0,8},{1,9},{2,10},{3,11},{4,12},{5,13},{6,14},{7,15},{8,0},{9,1},... | collective-permute-start | bytes 3686408 | tf_op jit(solution)/shard_map/ppermute | solution.py:837
  522.7 47.3 %collective-permute-start.24 = (bf16[1,512,1280]{2,1,0:T(8,128)(2,1)S(1)}, bf16[1,512,1280]{2,1,0:T(8,128)(2,1)S(1)}, u32[]{:S(2)}, u32[]{:S(2)}) collective-permute-start(bf16[1,512,1280]{2,1,0:T(8,128)(2,1)S(1)} %fusion.16), channel_id=1, source_target_pairs={{0,0},{1,1},{2,4},{3,5},{4,8},{5,9},{6,12},{7,13},{8,2},{9,3},{10,... | collective-permute-start | bytes 3932168 | tf_op jit(solution)/shard_map/ppermute | solution.py:837
  523.5 32.2 %collective-permute-start.47 = (f32[21,128]{1,0:T(8,128)S(1)}, f32[21,128]{1,0:T(8,128)S(1)}, u32[]{:S(2)}, u32[]{:S(2)}) collective-permute-start(f32[21,128]{1,0:T(8,128)S(1)} %add.180), channel_id=1, source_target_pairs={{0,4},{1,5},{2,6},{3,7},{4,0},{5,1},{6,2},{7,3},{8,12},{9,13},{10,... | collective-permute-start | bytes 32264 | tf_op jit(solution)/shard_map/ppermute | solution.py:837
  527.0 38.4 %collective-permute-start.42 = (bf16[2,160,1920]{2,1,0:T(8,128)(2,1)S(1)}, bf16[2,160,1920]{2,1,0:T(8,128)(2,1)S(1)}, u32[]{:S(2)}, u32[]{:S(2)}) collective-permute-start(bf16[2,160,1920]{2,1,0:T(8,128)(2,1)S(1)} %copy-done.35), channel_id=1, source_target_pairs={{0,8},{1,9},{2,10},{3,11},{4,12},{5,13},{6,14},{7,15},{8,0},{9,1},... | collective-permute-start | bytes 3686408 | tf_op jit(solution)/shard_map/ppermute | solution.py:837
  (107 other events, 1053.9 us)
Sparse Core Ops, SparseCore 0:
  396.3 82.4 all-reduce.3

commit v3 on v2

--- a/solution.py
+++ b/solution.py
@@ -17,9 +17,10 @@
 scale_base = 1.442695041
 log2e = 1.4426950408889634
 NEG = -1e30
+CHEAP = pl.CostEstimate(flops=1000, transcendentals=0, bytes_accessed=1000)
 f32 = jnp.float32
 bf16 = jnp.bfloat16
-AXES = ("gx", "gc", "ctx", "wt")
+AXES = ("gx", "gc", "far", "near", "wt")
 
 
 def block_flags(seg_row, bq, bk):
@@ -165,9 +166,7 @@
         ],
         grid_spec=spec,
         compiler_params=pltpu.CompilerParams(vmem_limit_bytes=40 << 20),
-        cost_estimate=pl.CostEstimate(
-            flops=20_000_000_000, transcendentals=10_000_000, bytes_accessed=16_000_000
-        ),
+        cost_estimate=CHEAP,
         name="attn_fwd",
     )(block_flags(seg_row, bq, bk), q, kv, seg_row[:, None], seg_row[None])
 
@@ -241,8 +240,12 @@
     lax.fori_loop(ko // bq, nq, body, 0)
     r = pl.multiple_of(ko, bk)
     ln2 = math.log(2.0)
-    dqkv[pl.ds(r, bk), nh * HD : 3 * nh * HD] = jnp.concatenate(
-        [dk_s[h][:, :HD] * ln2 for h in range(nh)] + [dv_s[h][:, :HD] for h in range(nh)], axis=1
+    gap = dqkv.shape[1] - 3 * nh * HD
+    dqkv[pl.ds(r, bk), nh * HD :] = jnp.concatenate(
+        [dk_s[h][:, :HD] * ln2 for h in range(nh)]
+        + [dv_s[h][:, :HD] for h in range(nh)]
+        + [jnp.zeros((bk, gap), f32)],
+        axis=1,
     ).astype(bf16)
 
     @pl.when(kb == nk - 1)
@@ -280,7 +283,7 @@
             pl.BlockSpec((1, nh * HD), lambda i, f, m: (0, 0)),
         ],
         out_specs=[
-            pl.BlockSpec((n, 3 * nh * HD), lambda i, f, m: (0, 0)),
+            pl.BlockSpec((n, lanes_up(3 * nh * HD)), lambda i, f, m: (0, 0)),
             pl.BlockSpec((8, LN), lambda i, f, m: (0, 0)),
         ],
         scratch_shapes=[
@@ -293,14 +296,12 @@
     return pl.pallas_call(
         functools.partial(bwd_kernel, first=group * nh, nh=nh, bq=bq, bk=bk, n=n),
         out_shape=[
-            jax.ShapeDtypeStruct((n, 3 * nh * HD), bf16),
+            jax.ShapeDtypeStruct((n, lanes_up(3 * nh * HD)), bf16),
             jax.ShapeDtypeStruct((8, LN), f32),
         ],
         grid_spec=spec,
         compiler_params=pltpu.CompilerParams(vmem_limit_bytes=48 << 20),
-        cost_estimate=pl.CostEstimate(
-            flops=15_000_000_000 * nh // 2, transcendentals=10_000_000, bytes_accessed=20_000_000
-        ),
+        cost_estimate=CHEAP,
         name="attn_bwd",
     )(block_flags(seg_row, bq, bk), mine.reshape(1), qa, kv, kv, *pieces, of, seg_row[:, None], seg_row[None], scale)
 
@@ -317,9 +318,14 @@
 
         @pl.when(mine[0] == i)
         def _(i=i):
-            out[...] = jnp.concatenate(
-                [w_ref[:, a : a + width] for a, width in quarter_columns(i, parts, groups, nh)], axis=1
-            )
+            cut = [w_ref[:, a : a + width] for a, width in quarter_columns(i, parts, groups, nh)]
+            used = sum(x.shape[1] for x in cut)
+            pad = jnp.zeros((cut[0].shape[0], out.shape[1] - used), out.dtype)
+            out[...] = jnp.concatenate(cut + [pad], axis=1)
+
+
+def lanes_up(n):
+    return -(-n // LN) * LN
 
 
 def pick(w, mine, parts, groups, nh):
@@ -327,13 +333,14 @@
     step = 160 if rows % 160 == 0 else rows
     return pl.pallas_call(
         functools.partial(pick_kernel, parts=parts, groups=groups, nh=nh),
-        out_shape=jax.ShapeDtypeStruct((rows, 3 * nh * HD), w.dtype),
+        out_shape=jax.ShapeDtypeStruct((rows, lanes_up(3 * nh * HD)), w.dtype),
         grid_spec=pltpu.PrefetchScalarGridSpec(
             num_scalar_prefetch=1,
             grid=(rows // step,),
             in_specs=[pl.BlockSpec((step, 3 * D), lambda i, m: (i, 0))],
-            out_specs=pl.BlockSpec((step, 3 * nh * HD), lambda i, m: (i, 0)),
+            out_specs=pl.BlockSpec((step, lanes_up(3 * nh * HD)), lambda i, m: (i, 0)),
         ),
+        cost_estimate=CHEAP,
         name="pick",
     )(mine.reshape(1), w)
 
@@ -344,8 +351,9 @@
     def put(ref):
         value = ref[...]
         each = 3 * nh * HD // groups
+        gap = jnp.zeros((value.shape[0], lanes_up(each) - each), value.dtype)
         for g in range(groups):
-            flats[g][...] = value[:, g * each : (g + 1) * each]
+            flats[g][...] = jnp.concatenate([value[:, g * each : (g + 1) * each], gap], axis=1)
         zero = jnp.zeros((value.shape[0], LN - HD), value.dtype)
         per = nh // groups
         spread = []
@@ -371,7 +379,7 @@
     step = 160
     n = rows // step
     at = lambda i, j, m: ((i ^ m[0]) * n + j, 0)
-    each = width // groups
+    each = lanes_up(3 * nh * HD // groups)
     return pl.pallas_call(
         functools.partial(widen_kernel, groups=groups, nh=nh),
         out_shape=[jax.ShapeDtypeStruct((2 * rows, each), own.dtype)] * groups
@@ -385,6 +393,7 @@
             ],
             out_specs=[pl.BlockSpec((step, each), at)] * groups + [pl.BlockSpec((step, 3 * nh * LN), at)],
         ),
+        cost_estimate=CHEAP,
         name="widen",
     )(own_at.reshape(1), own, other)
 
@@ -464,6 +473,7 @@
         ),
         input_output_aliases=aliases,
         compiler_params=pltpu.CompilerParams(vmem_limit_bytes=48 << 20),
+        cost_estimate=CHEAP,
         name="project",
     )(info, *args)
 
@@ -562,9 +572,7 @@
             scratch_shapes=scratch,
         ),
         compiler_params=pltpu.CompilerParams(vmem_limit_bytes=52 << 20),
-        cost_estimate=pl.CostEstimate(
-            flops=10_000_000_000, transcendentals=700_000, bytes_accessed=25_000_000
-        ),
+        cost_estimate=CHEAP,
         name="tail",
     )(at, *pieces, x, g, *weights, gain)
 
@@ -597,151 +605,151 @@
             out_specs=pl.BlockSpec((d, w), lambda i, c: (0, i)),
         ),
         compiler_params=pltpu.CompilerParams(vmem_limit_bytes=40 << 20),
-        cost_estimate=pl.CostEstimate(
-            flops=2_500_000_000, transcendentals=0, bytes_accessed=12_000_000
-        ),
+        cost_estimate=CHEAP,
         name="share",
     )(col.reshape(1), *lefts, *rights)
 
 
-def keep_kernel(at, l0, l1, l2, r0, r1, r2, got, a_send, a_keep, b_send, b_keep, s):
-    h = a_send.shape[1]
+def keep_kernel(col, l0, l1, l2, r0, r1, r2, got, out):
     for i, (left, right) in enumerate(((l0, r0), (l1, r1), (l2, r2))):
 
         @pl.when(pl.program_id(0) == i)
         def _(left=left, right=right):
-            s[...] = lax.dot_general(
-                left[...], right[...], tn_dims, preferred_element_type=f32
-            ) + got[...].astype(f32)
-
-    gx, wt = at[1], at[2]
-    for w in range(2):
-        base = w * 4 * h
-        a_send[w] = s[pl.ds(pl.multiple_of(base + (1 - gx) * h, 16), h), :].astype(bf16)
-        a_keep[w] = s[pl.ds(pl.multiple_of(base + gx * h, 16), h), :].astype(bf16)
-    b_send[...] = s[pl.ds(pl.multiple_of((1 - wt) * 4 * h + 2 * h, 16), 2 * h), :].astype(bf16)
-    b_keep[...] = s[pl.ds(pl.multiple_of(wt * 4 * h + 2 * h, 16), 2 * h), :].astype(bf16)
-
-
-def keep(lefts, rights, got, at):
+            out[...] = (
+                lax.dot_general(left[...], right[...], tn_dims, preferred_element_type=f32)
+                + got[...].astype(f32)
+            ).astype(bf16)
+
+
+def keep(lefts, rights, got, col):
     rows, d = lefts[0].shape
     w = d // 2
-    h = d // 8
     once = pl.Buffered(1)
+    block = pl.BlockSpec((d, w), lambda i, c: (0, i))
     return pl.pallas_call(
         keep_kernel,
-        out_shape=[jax.ShapeDtypeStruct((2, h, 3 * w), bf16)] * 2
-        + [jax.ShapeDtypeStruct((2 * h, 3 * w), bf16)] * 2,
+        out_shape=jax.ShapeDtypeStruct((d, 3 * w), bf16),
         grid_spec=pltpu.PrefetchScalarGridSpec(
             num_scalar_prefetch=1,
             grid=(3,),
             in_specs=[pl.BlockSpec((rows, d), lambda i, c: (0, 0), pipeline_mode=once)] * 3
             + [pl.BlockSpec((rows, w), lambda i, c: (0, c[0]), pipeline_mode=once)] * 3
-            + [pl.BlockSpec((d, w), lambda i, c: (0, i))],
-            out_specs=[pl.BlockSpec((2, h, w), lambda i, c: (0, 0, i))] * 2
-            + [pl.BlockSpec((2 * h, w), lambda i, c: (0, i))] * 2,
-            scratch_shapes=[pltpu.VMEM((d, w), f32)],
+            + [block],
+            out_specs=block,
         ),
         compiler_params=pltpu.CompilerParams(vmem_limit_bytes=40 << 20),
-        cost_estimate=pl.CostEstimate(
-            flops=2_500_000_000, transcendentals=0, bytes_accessed=16_000_000
-        ),
+        cost_estimate=CHEAP,
         name="keep",
-    )(at, *lefts, *rights, got)
-
-
-def fold_kernel(bits, *refs, count):
-    ins, outs = refs[: 4 * count], refs[4 * count :]
-    for i in range(count):
-        ks, gs, kk, gk = ins[4 * i : 4 * i + 4]
-        outs[2 * i][...] = (ks[0].astype(f32) + gs[0].astype(f32)).astype(bf16)
-        outs[2 * i + 1][...] = (kk[0].astype(f32) + gk[0].astype(f32)).astype(bf16)
-
-
-def fold(items):
-    in_specs, out_specs, out_shape, args = [], [], [], []
-    for i, (kept, got, bit) in enumerate(items):
-        shape = (1,) + kept.shape[1:]
-        other = pl.BlockSpec(shape, lambda _, m, i=i: (1 - m[i], 0, 0))
-        mine = pl.BlockSpec(shape, lambda _, m, i=i: (m[i], 0, 0))
-        in_specs += [other, other, mine, mine]
-        args += [kept, got, kept, got]
-        out_specs += [pl.BlockSpec(kept.shape[1:], lambda _, m: (0, 0))] * 2
-        out_shape += [jax.ShapeDtypeStruct(kept.shape[1:], bf16)] * 2
-    bits = jnp.stack([bit for _, _, bit in items])
-    out = pl.pallas_call(
-        functools.partial(fold_kernel, count=len(items)),
-        out_shape=out_shape,
-        grid_spec=pltpu.PrefetchScalarGridSpec(
-            num_scalar_prefetch=1, grid=(1,), in_specs=in_specs, out_specs=out_specs
-        ),
-        compiler_params=pltpu.CompilerParams(vmem_limit_bytes=24 << 20),
-        name="fold",
-    )(bits, *args)
-    return [(out[2 * i], out[2 * i + 1]) for i in range(len(items))]
-
-
-def place_kernel(at, c_ref, e_ref, fc_ref, fe_ref, o0, o1, o2):
-    w = o0.shape[1] // 2
-    mine = (pl.program_id(0) % 2) == at[0]
-    for own_rows in range(2):
-        for core in range(2):
-
-            @pl.when((mine == (own_rows == 1)) & (at[1] == core))
-            def _(own_rows=own_rows, core=core):
-                near = c_ref if own_rows else e_ref
-                mate = fc_ref if own_rows else fe_ref
-                first, second = (near, mate) if core == 0 else (mate, near)
-                for i, out in enumerate((o0, o1, o2)):
-                    out[:, :w] = first[0, :, i * w : (i + 1) * w].astype(f32)
-                    out[:, w:] = second[0, :, i * w : (i + 1) * w].astype(f32)
-
-
-def place_tail(c, e, fc, fe, at):
-    _, h, width = c.shape
-    d = width // 3 * 2
-    block = pl.BlockSpec((1, h, width), lambda i, m: (i // 2, 0, 0))
+    )(col.reshape(1), *lefts, *rights, got)
+
+
+def total_kernel(bit, *refs):
+    ins, outs = refs[:-2], refs[-2:]
+    for half, out in zip((1 - bit[0], bit[0]), outs):
+        acc = jnp.zeros(out.shape, f32)
+        for ref in ins:
+            for i in range(ref.shape[0]):
+                acc = acc + ref[i, half].astype(f32)
+        out[...] = acc.astype(bf16)
+
+
+def total(arrays, bit):
+    _, _, r, c = arrays[0].shape
+    w = c
+    for cut in (640, 512):
+        if c % cut == 0:
+            w = cut
+            break
     return pl.pallas_call(
-        place_kernel,
-        out_shape=[jax.ShapeDtypeStruct((4 * h, d), f32)] * 3,
+        total_kernel,
+        out_shape=[jax.ShapeDtypeStruct((r, c), bf16)] * 2,
         grid_spec=pltpu.PrefetchScalarGridSpec(
             num_scalar_prefetch=1,
-            grid=(4,),
-            in_specs=[block] * 4,
-            out_specs=[pl.BlockSpec((h, d), lambda i, m: (i, 0))] * 3,
+            grid=(c // w,),
+            in_specs=[pl.BlockSpec((x.shape[0], 2, r, w), lambda i, m: (0, 0, 0, i)) for x in arrays],
+            out_specs=[pl.BlockSpec((r, w), lambda i, m: (0, i))] * 2,
         ),
         compiler_params=pltpu.CompilerParams(vmem_limit_bytes=40 << 20),
+        cost_estimate=CHEAP,
+        name="total",
+    )(bit.reshape(1), *arrays)
+
+
+def place_kernel(at, own_ref, mate_ref, o0, o1, o2):
+    block = pl.program_id(0)
+    slot = ((block // 4) ^ at[0]) * 4 + (((block // 2) % 2) ^ at[1]) * 2 + ((block % 2) ^ at[2])
+    w = o0.shape[2] // 2
+
+    def put(refs):
+        for side, ref in enumerate(refs):
+            part = ref[slot].astype(f32)
+            for i, out in enumerate((o0, o1, o2)):
+                out[0, :, side * w : (side + 1) * w] = part[:, i * w : (i + 1) * w]
+
+    @pl.when(at[3] == 0)
+    def _():
+        put((own_ref, mate_ref))
+
+    @pl.when(at[3] == 1)
+    def _():
+        put((mate_ref, own_ref))
+
+
+def place_tail(own, mate, at):
+    n, h, width = own.shape
+    d = width // 3 * 2
+    whole = pl.BlockSpec(own.shape, lambda i, m: (0, 0, 0), pipeline_mode=pl.Buffered(1))
+    outs = pl.pallas_call(
+        place_kernel,
+        out_shape=[jax.ShapeDtypeStruct((n, h, d), f32)] * 3,
+        grid_spec=pltpu.PrefetchScalarGridSpec(
+            num_scalar_prefetch=1,
+            grid=(n,),
+            in_specs=[whole] * 2,
+            out_specs=[pl.BlockSpec((1, h, d), lambda i, m: (i, 0, 0))] * 3,
+        ),
+        compiler_params=pltpu.CompilerParams(vmem_limit_bytes=40 << 20),
+        cost_estimate=CHEAP,
         name="place_tail",
-    )(at, c, e, fc, fe)
-
-
-def cross_kernel(col, x_ref, g_ref, out):
-    out[...] = lax.dot_general(
-        x_ref[...], g_ref[...], tn_dims, preferred_element_type=f32
-    ).astype(bf16)
-
-
-def cross(x, g, col):
+    )(at, own, mate)
+    return [out.reshape(n * h, d) for out in outs]
+
+
+def cross_kernel(at, x_ref, g_ref, *refs):
+    s = refs[-1]
+    s[...] = lax.dot_general(x_ref[...], g_ref[...], tn_dims, preferred_element_type=f32).astype(bf16)
+    step = pl.program_id(0)
+    half = s.shape[0] // 2
+    for w in range(2):
+
+        @pl.when(step == w)
+        def _(w=w):
+            for x in range(2):
+                rows = pl.ds(pl.multiple_of((at[1] ^ x) * half, 16), half)
+                refs[2 * w + x][...] = s[rows, :]
+
+
+def cross(x, g, at):
     rows, d = x.shape
     w = d // 2
+    block = pl.BlockSpec((w // 2, g.shape[1]), lambda i, m: (0, 0))
     return pl.pallas_call(
         cross_kernel,
-        out_shape=jax.ShapeDtypeStruct((w, g.shape[1]), bf16),
+        out_shape=[jax.ShapeDtypeStruct((w // 2, g.shape[1]), bf16)] * 4,
         grid_spec=pltpu.PrefetchScalarGridSpec(
             num_scalar_prefetch=1,
-            grid=(1,),
+            grid=(2,),
             in_specs=[
-                pl.BlockSpec((rows, w), lambda i, c: (0, c[0])),
-                pl.BlockSpec(g.shape, lambda i, c: (0, 0)),
+                pl.BlockSpec((rows, w), lambda i, m: (0, m[0] ^ i)),
+                pl.BlockSpec(g.shape, lambda i, m: (0, 0)),
             ],
-            out_specs=pl.BlockSpec((w, g.shape[1]), lambda i, c: (0, 0)),
+            out_specs=[block] * 4,
+            scratch_shapes=[pltpu.VMEM((w, g.shape[1]), bf16)],
         ),
         compiler_params=pltpu.CompilerParams(vmem_limit_bytes=40 << 20),
-        cost_estimate=pl.CostEstimate(
-            flops=2 * rows * w * g.shape[1], transcendentals=0, bytes_accessed=6_000_000
-        ),
+        cost_estimate=CHEAP,
         name="cross",
-    )(col.reshape(1), x, g)
+    )(at, x, g)
 
 
 def spread_kernel(at, *refs, groups, width):
@@ -768,14 +776,14 @@
             put(flip)
 
 
-def spread(arrays, at):
+def spread(arrays, at, used):
     flat = [x for pair in arrays for x in pair]
     slots, rows, cols = flat[0].shape
     full = lambda i, m: (0, 0, 0)
     groups = len(arrays)
-    total = 4 * groups * cols
+    total = 4 * groups * used
     return pl.pallas_call(
-        functools.partial(spread_kernel, groups=groups, width=cols // 3),
+        functools.partial(spread_kernel, groups=groups, width=used // 3),
         out_shape=jax.ShapeDtypeStruct((4, rows, total), f32),
         grid_spec=pltpu.PrefetchScalarGridSpec(
             num_scalar_prefetch=1,
@@ -784,6 +792,7 @@
             out_specs=pl.BlockSpec((1, rows, total), lambda i, m: (i, 0, 0)),
         ),
         compiler_params=pltpu.CompilerParams(vmem_limit_bytes=40 << 20),
+        cost_estimate=CHEAP,
         name="spread",
     )(at, *flat).reshape(4 * rows, total)
 
@@ -823,7 +832,7 @@
         found = []
         for gx in range(sizes["gx"]):
             for gc in range(sizes["gc"]):
-                for z in range(sizes["ctx"]):
+                for z in range(4):
                     for w in range(sizes["wt"]):
                         goal = target(gx, gc, z, w)
                         if goal is not None:
@@ -831,7 +840,7 @@
         return found
 
     def place(gx, gc, z, w):
-        return ((gx * sizes["gc"] + gc) * sizes["ctx"] + z) * sizes["wt"] + w
+        return ((gx * sizes["gc"] + gc) * 4 + z) * sizes["wt"] + w
 
     def send(value, target):
         return lax.ppermute(value, AXES, pairs(target))
@@ -853,6 +862,9 @@
 
     def wt_mate(gx, gc, z, w):
         return (gx, gc, z, 1 - w)
+
+    def wt_x_mate(gx, gc, z, w):
+        return (1 - gx, gc, z, 1 - w)
 
     def to_host(gx, gc, z, w):
         return (gx, z & 1, 2 * gc + (z >> 1), w)
@@ -878,40 +890,15 @@
     def lane_share(gx, gc, z, w):
         return (gx, 1 - gc, z, w) if gc == z >> 1 else None
 
-    def gather_wt(value):
-        if sizes["wt"] == 2:
-            other = send(value, wt_mate)
-            first = lax.axis_index("wt") == 0
-            return jnp.stack([jnp.where(first, value, other), jnp.where(first, other, value)])
-        return lax.all_gather(value, "wt", axis=0, tiled=False)
-
-    def scatter_wt(value):
-        if sizes["wt"] == 2:
-            own = lax.axis_index("wt")
-            mine = lax.dynamic_index_in_dim(value, own, 0, keepdims=False)
-            other = send(lax.dynamic_index_in_dim(value, 1 - own, 0, keepdims=False), wt_mate)
-            return (mine.astype(f32) + other.astype(f32)).astype(bf16)
-        return lax.psum_scatter(value, "wt", scatter_dimension=0, tiled=False)
-
-    def halve(value, bit, mate):
-        half = value.shape[0] // 2
-        other = send(rows_at(value, (1 - bit) * half, half), mate)
-        return (rows_at(value, bit * half, half).astype(f32) + other.astype(f32)).astype(bf16)
-
-    def double(value, bit, mate):
-        other = send(value, mate)
-        first = bit == 0
-        return jnp.stack([jnp.where(first, value, other), jnp.where(first, other, value)])
-
     def sum_all(value):
         for axis in AXES:
             step = 1
             while step < sizes[axis]:
 
                 def mate(gx, gc, z, w, axis=axis, step=step):
-                    at = dict(gx=gx, gc=gc, ctx=z, wt=w)
+                    at = dict(gx=gx, gc=gc, far=z >> 1, near=z & 1, wt=w)
                     at[axis] ^= step
-                    return (at["gx"], at["gc"], at["ctx"], at["wt"])
+                    return (at["gx"], at["gc"], 2 * at["far"] + at["near"], at["wt"])
 
                 value = value + send(value, mate)
                 step *= 2
@@ -920,11 +907,10 @@
     def local(
         tokens, segments, w_qkv, w_proj, w_in, w_out, gain_attn, gain_mlp, query_scale, cotangent
     ):
-        gx, gc, z, wt = (lax.axis_index(axis) for axis in AXES)
-        host = z // 2
-        near = z % 2
+        gx, gc, host, near, wt = (lax.axis_index(axis) for axis in AXES)
+        z = 2 * host + near
         mine = 2 * near + gc
-        parts = sizes["ctx"]
+        parts = 4
         nh = H // parts
         groups = 2
         rows = tokens.shape[1]
@@ -949,9 +935,12 @@
             other_w = send(picked, wt_mate)
             *flat_w, wide_w = widen(picked, other_w, wt, groups, nh)
         else:
-            flat_all = lax.all_gather(picked, "wt", axis=0, tiled=True)
+            flat_all = lax.all_gather(picked, "wt", axis=0, tiled=True)[:, : 3 * nh * HD]
             each = flat_all.shape[1] // groups
-            flat_w = [flat_all[:, g * each : (g + 1) * each] for g in range(groups)]
+            flat_w = [
+                jnp.pad(flat_all[:, g * each : (g + 1) * each], ((0, 0), (0, lanes_up(each) - each)))
+                for g in range(groups)
+            ]
             order = jnp.transpose(flat_all.reshape(D, groups, 3, nh // groups, HD), (0, 2, 1, 3, 4))
             wide_w = jnp.pad(
                 order.reshape(D, 3 * nh, HD), ((0, 0), (0, 0), (0, LN - HD))
@@ -992,7 +981,7 @@
         trades = (core_mate, near_mate, cross_mate)
         att_pieces = [rows_at(att, (mine ^ j) * rows, rows) for j in range(parts)]
         att_pieces = [att_pieces[0]] + [send(att_pieces[j + 1], trades[j]) for j in range(3)]
-        half_mate = send(after(half_w, att), core_mate)
+        half_mate = send(after(half_w, att_pieces[1]), core_mate)
         if pair:
             weights = (tail_own, half_w, half_mate)
             starts = (wt * wrows, (1 - wt) * wrows + gc * half_rows, (1 - wt) * wrows + (1 - gc) * half_rows)
@@ -1018,45 +1007,10 @@
 
         lefts = (attended, normed_mlp, active)
         rights = (grad_proj, grad_hidden, grad_mlp)
-        width = D // 2
-        if pair:
-            to_core = share(lefts, rights, 1 - gc)
-            from_core = send(to_core, core_mate)
-            layer_out = send(after(layer_out, to_core)[None], to_home)
-            a_send, a_keep, b_send, b_keep = keep(
-                lefts, rights, from_core, jnp.stack([gc, gx, wt])
-            )
-            a_got = send(a_send, x_mate)
-            b_got = send(b_send, wt_mate)
-            ready = a_send
-        else:
-            layer_out = send(layer_out[None], to_home)
-
-            def by_column(flip):
-                one = gc == flip
-                return jnp.concatenate(
-                    [
-                        trans_times(
-                            left, jnp.where(one, right[:, :width], right[:, width:])
-                        ).astype(bf16)
-                        for left, right in zip(lefts, rights)
-                    ],
-                    axis=1,
-                )
-
-            half_grad = send(by_column(1), core_mate)
-            half_grad = (by_column(0).astype(f32) + half_grad.astype(f32)).astype(bf16)
-            half_grad = lax.psum(scatter_wt(half_grad.reshape(-1, wrows, 3 * width)), ("gx", "ctx"))
-            mate_grad = send(half_grad, core_mate)
-            one = gc == 0
-            totals = []
-            for i in range(3):
-                a = half_grad[:, i * width : (i + 1) * width]
-                b = mate_grad[:, i * width : (i + 1) * width]
-                totals.append(
-                    jnp.concatenate([jnp.where(one, a, b), jnp.where(one, b, a)], axis=1).astype(f32)
-                )
-            ready = grad_proj
+        from_core = send(share(lefts, rights, 1 - gc), core_mate)
+        layer_out = send(after(layer_out, pieces[2])[None], to_home)
+        summed = keep(lefts, rights, after(from_core, *pieces[1:]), gc)
+        kept = lax.all_to_all(summed, ("wt", "gx", "near"), 0, 0, tiled=True)
 
         scale_row = jnp.tile(dim_scale, nh // groups)[None]
 
@@ -1065,64 +1019,45 @@
                 q_aug, keyval, pieces, att_float, seg_row, mine, scale_row, nh, group, groups
             )
 
-        def qkv_start(grad):
-            if pair:
-                sent = cross(all_normed, grad, 1 - wt)
-                got = send(sent, wt_mate)
-                kept = cross(all_normed, grad, wt)
-                return kept.reshape(2, wrows // 2, -1), got.reshape(2, wrows // 2, -1)
-            kept = trans_times(all_normed, grad).astype(bf16).reshape(-1, wrows, grad.shape[1])
-            kept = scatter_wt(kept).reshape(2, wrows // 2, -1)
-            return kept, jnp.zeros_like(kept)
-
-        def qkv_far(kept, got):
-            (part, kept), = fold(((kept, got, gx),))
-            got = send(part, x_mate)
-            quarter = wrows // 4
-            (part, kept), = fold(
-                ((kept.reshape(2, quarter, -1), got.reshape(2, quarter, -1), host),)
-            )
-            return kept, send(part, far_mate)
-
-        def qkv_gather(kept, got):
-            block = (kept.astype(f32) + got.astype(f32)).astype(bf16)[None]
+        def gather(block):
             for mate in (far_mate, near_mate, x_mate):
                 block = jnp.concatenate([block, send(block, mate)])
             return block, send(block, core_mate)
 
-        pieces[3] = after(pieces[3], ready)
+        def far_sum(pair):
+            part, kept = pair
+            return (kept.astype(f32) + send(part, far_mate).astype(f32)).astype(bf16)[None]
+
+        def by_rows(grad):
+            if pair:
+                own, *rest = cross(all_normed, grad, jnp.stack([wt, gx]))
+                got = [send(part, mate) for part, mate in zip(rest, (x_mate, wt_mate, wt_x_mate))]
+                return [part.reshape(1, 2, part.shape[0] // 2, -1) for part in (own, *got)]
+            part = trans_times(all_normed, grad).astype(bf16)
+            sources = sizes["wt"] * 2
+            got = lax.all_to_all(part, ("wt", "gx"), 0, 0, tiled=True)
+            return [got.reshape(sources, 2, D // sources // 2, -1)]
+
+        pieces[3] = after(pieces[3], summed)
         grad_a, lanes_a = backward(0, pieces)
-        if pair:
-            a_got, b_got = after(a_got, grad_a), after(b_got, grad_a)
-            (a_send, a_keep), (b_send, b_keep) = fold(
-                (
-                    (a_keep, a_got, wt),
-                    (b_keep.reshape(2, -1, 3 * width), b_got.reshape(2, -1, 3 * width), gx),
-                )
-            )
-            a_got = send(a_send, wt_mate)
-            b_got = send(b_send, x_mate)
-            pieces[3] = after(pieces[3], a_send)
-        start_a = qkv_start(grad_a)
-        pieces[3] = after(pieces[3], start_a[0])
+        rows_a = by_rows(grad_a)
+        pieces[3] = after(pieces[3], rows_a[0], layer_out)
         grad_b, lanes_b = backward(1, pieces)
-        if pair:
-            a_got, b_got = after(a_got, grad_b), after(b_got, grad_b)
-            block = jnp.stack(
-                [
-                    (k.astype(f32) + g.astype(f32)).astype(bf16)
-                    for k, g in ((a_keep, a_got), (b_keep, b_got))
-                ]
-            )
-            block = lax.psum(block, "ctx")
-        start_b = qkv_start(grad_b)
-        far_a = qkv_far(start_a[0], after(start_a[1], grad_b))
-        far_b = qkv_far(*start_b)
+        rows_a[0] = after(rows_a[0], grad_b)
+        half_a = total(rows_a, host)
+        grad_b = after(grad_b, half_a[0])
+        rows_b = by_rows(grad_b)
+        block_a = far_sum(half_a)
+        block_b = far_sum(total(rows_b, host))
+        sources = sizes["wt"] * 4
+        block = far_sum(
+            total([after(kept, rows_b[0]).reshape(sources, 2, D // sources // 2, -1)], host)
+        )
 
         def shard_grad(shard):
             return sum(
                 times_trans(rows_at(grad, shard * rows, rows), w)
-                for grad, w in zip((after(grad_a, start_b[0]), after(grad_b, start_b[0])), flat_w)
+                for grad, w in zip((after(grad_a, rows_b[0]), after(grad_b, rows_b[0])), flat_w)
             )
 
         to_core = jnp.stack([shard_grad(mine ^ 3), shard_grad(mine ^ 1)]).astype(bf16)
@@ -1138,13 +1073,9 @@
         )
 
         total_qkv = spread(
-            [qkv_gather(*far_a), qkv_gather(*far_b)], jnp.stack([gx, host, near, gc])
+            [gather(block_a), gather(block_b)], jnp.stack([gx, host, near, gc]), 3 * nh // groups * HD
         )
-        if pair:
-            from_x = send(block, x_mate)
-            totals = place_tail(
-                block, from_x, send(block, core_mate), send(from_x, core_mate), jnp.stack([gx, gc])
-            )
+        totals = place_tail(*gather(block), jnp.stack([gx, near, host, gc]))
 
         grad_query_scale = (
             (lanes_a + lanes_b)[0, :HD]
@@ -1171,9 +1102,9 @@
 
 def solution(mesh):
     groups, parts, wt = (mesh.shape[axis] for axis in ("grp", "ctx", "wt"))
-    inner = Mesh(mesh.devices.reshape(groups // 2, 2, parts, wt), AXES)
+    inner = Mesh(mesh.devices.reshape(groups // 2, 2, parts // 2, 2, wt), AXES)
     sizes = dict(inner.shape)
-    split = P(("gx", "gc", "wt"), "ctx", None)
+    split = P(("gx", "gc", "wt"), ("far", "near"), None)
     weight = P("wt", None)
     return jax.shard_map(
         make_local(sizes),

time: 586 us -> 549 us (0.937)
  starting transfers between devices: 79.6 us -> 123 us
  local copies, waits for them, and re-layouts: 68.9 us -> 36.2 us
  waiting for transfers between devices: 210 us -> 191 us
  between operations: 15.3 us -> 1.78 us
  matrix products: 18.1 us -> 8.97 us
  other arithmetic: 22.8 us -> 15.2 us
    ppermute x49, starting transfers between devices: 79.5 us -> 119 us  [send(): return lax.ppermute(value, AXES, pairs(target))]
    unnamed x182 -> x108, local copies, waits for them, and re-layouts: 49 us -> 30.2 us
    ppermute x49, waiting for transfers between devices: 207 us -> 191 us  [send(): return lax.ppermute(value, AXES, pairs(target))]
    dot_general x8, matrix products: 18.1 us -> 8.97 us  [times_trans(): lax.dot_general(left, right, (((1,), (1,)), ((), ())), preferred_element_...]
    ppermute x3 -> x0, local copies, waits for them, and re-layouts: 6.91 us -> none  [send(): return lax.ppermute(value, AXES, pairs(target))]
    pallas_call x3 -> x0, local copies, waits for them, and re-layouts: 6.79 us -> none  [the longest x2 4.39 us: cross(): pl.pallas_call(cross_kernel, out_shape=jax.ShapeDtypeStruct((w, g.shape[1...]
    pallas_call x12 -> x8, Pallas kernels: 30 us -> 33.1 us  [the longest x2 8.5 us: cross(): pl.pallas_call(cross_kernel, out_shape=[jax.ShapeDtypeStruct((w // 2, g.s...]
  transfers between devices with their start and end apart: 50 -> 50, of which waited for: 18 -> 22; matrix products, arithmetic and copies ran while one was open for 10% -> 6% of each run, Pallas kernels for 24% -> 24%
where the time goes in v3:
time: 549 us; the launch traced here: 544 us
  waiting for transfers between devices  191 us (35%)
  Pallas kernels  167 us (30%)
  starting transfers between devices  123 us (22%)
  local copies, waits for them, and re-layouts  36.2 us (7%)
  other arithmetic  15.2 us (3%)
  matrix products  8.97 us (2%)
    ppermute x49, waiting for transfers between devices, send(): return lax.ppermute(value, AXES, pairs(target))  191 us
    ppermute x49, starting transfers between devices, send(): return lax.ppermute(value, AXES, pairs(target))  119 us
    pallas_call x2, Pallas kernels, attn_bwd(): pl.pallas_call(functools.partial(bwd_kernel, first=group * nh, nh=nh, bq=...  49.5 us
    unnamed x108, local copies, waits for them, and re-layouts  30.2 us
    pallas_call x1, Pallas kernels, attn_fwd(): pl.pallas_call(functools.partial(fwd_kernel, nh=nh, bq=bq, bk=bk, nk=n //...  24.9 us
    pallas_call x1, Pallas kernels, tail(): pl.pallas_call(body, out_shape=[jax.ShapeDtypeStruct((rows, d), bf16)] *...  21.7 us
    pallas_call x2, Pallas kernels, project(): pl.pallas_call(functools.partial(project_kernel, count=count, width=width...  21.2 us
  transfers between devices with their start and end apart: 50, of which 22 were waited for; matrix products, arithmetic and copies ran while one was open for 6% of the time, Pallas kernels for 24%

profile of v3, /device:TPU:0, one launch (start us, length us, event | category | flops | bytes accessed | tf_op | source)
XLA Modules:
  0.0 543.7 jit_solution(12518062882167925768)
XLA Ops:
  2.0 4.6 pick.1.a_ref
  6.5 14.9 %collective-permute-done.1.refs_2_ = bf16[512,1280]{1,0:T(8,128)(2,1)} collective-permute-done((bf16[512,1280]{1,0:T(8,128)(2,1)}, bf16[512,1280]{1,0:T(8,128)(2,1)}, u32[]{:S(2)}, u32[]{:S(2)}) %collective-permute-start.1) | collective-permute-done | bytes 1310752 | tf_op jit(solution)/shard_map/ppermute | solution.py:846
  29.5 11.7 %collective-permute-done.2.refs_4_ = bf16[512,1280]{1,0:T(8,128)(2,1)} collective-permute-done((bf16[512,1280]{1,0:T(8,128)(2,1)}, bf16[512,1280]{1,0:T(8,128)(2,1)}, u32[]{:S(2)}, u32[]{:S(2)}) %collective-permute-start.2) | collective-permute-done | bytes 1310752 | tf_op jit(solution)/shard_map/ppermute | solution.py:846
  42.5 5.2 collective-permute-start.3
  58.8 7.8 %widen.1 = (bf16[1280,512]{1,0:T(8,128)(2,1)}, bf16[1280,512]{1,0:T(8,128)(2,1)}, bf16[1280,1536]{1,0:T(8,128)(2,1)}) custom-call(s32[1]{0:T(128)} %bitcast.13.own_first, bf16[640,1024]{1,0:T(8,128)(2,1)} %pick.1.a_ref, bf16[640,1024]{1,0:T(8,128)(2,1)} %collective-permute-done.7.b_ref), custom_call_target="tpu_custom_call" | custom-call | flops 1000 | bytes 1000 | tf_op jit(solution)/shard_map/widen/pallas_call | solution.py:383
  66.7 13.9 %project.2 = (bf16[2048,1280]{1,0:T(8,128)(2,1)}, bf16[2048,512]{1,0:T(8,128)(2,1)}, bf16[2048,1024]{1,0:T(8,128)(2,1)}, bf16[512,1280]{1,0:T(8,128)(2,1)S(1)}) custom-call(s32[5]{0:T(128)S(1)} %stack.104.info, bf16[512,1280]{1,0:T(8,128)(2,1)S(1)} %bitcast.96, bf16[512,1280]{1,0:T(8,128)(2,1)} %collective-permute-done.4.refs_1_, ...), custom_call_target="tpu_custom_call" | custom-call | flops 1000 | bytes 1000 | tf_op jit(solution)/shard_map/project/pallas_call | solution.py:455
  88.8 7.2 %project.3 = (bf16[2048,1280]{1,0:T(8,128)(2,1)}, bf16[2048,512]{1,0:T(8,128)(2,1)}, bf16[2048,1024]{1,0:T(8,128)(2,1)}, bf16[512,1280]{1,0:T(8,128)(2,1)S(1)}) custom-call(s32[3]{0:T(128)S(1)} %pad_add_fusion.1.info, bf16[512,1280]{1,0:T(8,128)(2,1)S(1)} %collective-permute-done.3.refs_0_, ...), custom_call_target="tpu_custom_call", output_to_operand_aliasing={{0}: (8, {}), {1}: (9, {}), {2}: (10, {})} | custom-call | flops 1000 | bytes 1000 | tf_op jit(solution)/shard_map/project/pallas_call | solution.py:455
  98.1 24.9 %attn_fwd.1 = (bf16[2048,320]{1,0:T(8,128)(2,1)S(1)}, f32[2048,512]{1,0:T(8,128)S(1)}, bf16[2048,512]{1,0:T(8,128)(2,1)S(1)}) custom-call(s32[16]{0:T(128)S(1)} %reshape.227.flags, bf16[2048,512]{1,0:T(8,128)(2,1)S(1)} %copy-done.9, bf16[2048,1024]{1,0:T(8,128)(2,1)} %get-tuple-element.78.kv.kk.vv, s32[2048,1]{1,0:T(8,128)S(1)} %copy.26.segc, ...), custom_call_target="tpu_custom_call" | custom-call | flops 1000 | bytes 1000 | tf_op jit(solution)/shard_map/attn_fwd/pallas_call | solution.py:160
  134.0 26.3 %collective-permute-done.10.p2 = bf16[512,320]{1,0:T(8,128)(2,1)S(1)} collective-permute-done((bf16[512,320]{1,0:T(8,128)(2,1)}, bf16[512,320]{1,0:T(8,128)(2,1)S(1)}, u32[]{:S(2)}, u32[]{:S(2)}) %collective-permute-start.10) | collective-permute-done | bytes 327712 | tf_op jit(solution)/shard_map/ppermute | solution.py:846
  161.1 21.7 %tail.1 = (bf16[512,1280]{1,0:T(8,128)(2,1)}, bf16[512,1280]{1,0:T(8,128)(2,1)}, bf16[512,1280]{1,0:T(8,128)(2,1)}, bf16[512,1280]{1,0:T(8,128)(2,1)}, bf16[512,...) custom-call(s32[4]{0:T(128)S(1)} %pad_add_fusion.at, ...), custom_call_target="tpu_custom_call" | custom-call | flops 1000 | bytes 1000 | tf_op jit(solution)/shard_map/tail/pallas_call | solution.py:561
  200.8 9.8 %collective-permute-done.15.do2 = bf16[512,320]{1,0:T(8,128)(2,1)S(1)} collective-permute-done((bf16[512,320]{1,0:T(8,128)(2,1)S(1)}, bf16[512,320]{1,0:T(8,128)(2,1)S(1)}, u32[]{:S(2)}, u32[]{:S(2)}) %collective-permute-start.15) | collective-permute-done | bytes 327712 | tf_op jit(solution)/shard_map/ppermute | solution.py:846
  210.6 6.7 %collective-permute-done.18.do3 = bf16[512,320]{1,0:T(8,128)(2,1)S(1)} collective-permute-done((bf16[512,320]{1,0:T(8,128)(2,1)S(1)}, bf16[512,320]{1,0:T(8,128)(2,1)S(1)}, u32[]{:S(2)}, u32[]{:S(2)}) %collective-permute-start.18) | collective-permute-done | bytes 327712 | tf_op jit(solution)/shard_map/ppermute | solution.py:846
  219.5 5.8 %keep.1 = bf16[1280,1920]{1,0:T(8,128)(2,1)S(1)} custom-call(s32[1]{0:T(128)} %bitcast.22.col, bf16[512,1280]{1,0:T(8,128)(2,1)S(1)} %copy-done.11, bf16[512,1280]{1,0:T(8,128)(2,1)S(1)} %copy-done.12, bf16[512,1280]{1,0:T(8,128)(2,1)S(1)} %copy-done.14, bf16[512,1280]{1,0:T(8,128)(2,1)S(1)} %copy-done.15, bf16[512,1280]{1,0:T(8,128)(2,1)S(1)} %copy-done.13, ...), custom_call_target="tpu_custom_call" | custom-call | flops 1000 | bytes 1000 | tf_op jit(solution)/shard_map/keep/pallas_call | solution.py:629
  227.6 4.8 all-to-all-start
  232.4 11.3 %collective-permute-start.16 = (bf16[1,512,1280]{2,1,0:T(8,128)(2,1)}, bf16[1,512,1280]{2,1,0:T(8,128)(2,1)}, u32[]{:S(2)}, u32[]{:S(2)}) collective-permute-start(bf16[1,512,1280]{2,1,0:T(8,128)(2,1)} %bitcast.21), channel_id=1, source_target_pairs={{0,0},{1,1},{2,4},{3,5},{4,8},{5,9},{6,12},{7,13},{8,2},{9,3},{10,... | collective-permute-start | bytes 3932168 | tf_op jit(solution)/shard_map/ppermute | solution.py:846
  247.2 24.3 %attn_bwd.2 = (bf16[2048,512]{1,0:T(8,128)(2,1)S(1)}, f32[8,128]{1,0:T(8,128)S(1)}) custom-call(s32[16]{0:T(128)S(1)} %reshape.227.flags, s32[1]{0:T(128)} %bitcast.mine, bf16[2048,512]{1,0:T(8,128)(2,1)} %copy-done.10, bf16[2048,1024]{1,0:T(8,128)(2,1)} %get-tuple-element.78.kv.kk.vv, bf16[2048,1024]{1,0:T(8,128)(2,1)} %get-tuple-element.78.kv.kk.vv, ...), custom_call_target="tpu_custom_call" | custom-call | flops 1000 | bytes 1000 | tf_op jit(solution)/shard_map/attn_bwd/pallas_call | solution.py:296
  279.4 25.2 %attn_bwd.3 = (bf16[2048,512]{1,0:T(8,128)(2,1)S(1)}, f32[8,128]{1,0:T(8,128)S(1)}) custom-call(s32[16]{0:T(128)S(1)} %reshape.227.flags, s32[1]{0:T(128)} %bitcast.mine, bf16[2048,512]{1,0:T(8,128)(2,1)} %copy-done.10, bf16[2048,1024]{1,0:T(8,128)(2,1)} %get-tuple-element.78.kv.kk.vv, bf16[2048,1024]{1,0:T(8,128)(2,1)} %get-tuple-element.78.kv.kk.vv, ...), custom_call_target="tpu_custom_call" | custom-call | flops 1000 | bytes 1000 | tf_op jit(solution)/shard_map/attn_bwd/pallas_call | solution.py:296
  308.7 4.4 collective-permute-done.22
  323.3 13.9 %collective-permute-start.23 = (bf16[2,512,1280]{2,1,0:T(8,128)(2,1)}, bf16[2,512,1280]{2,1,0:T(8,128)(2,1)}, u32[]{:S(2)}, u32[]{:S(2)}) collective-permute-start(bf16[2,512,1280]{2,1,0:T(8,128)(2,1)} %pad_maximum_fusion.1), channel_id=1, source_target_pairs={{0,8},{1,9},{2,10},{3,11},{4,12},{5,13},{6,14},{7,15},{8,0},{9,1},... | collective-permute-start | bytes 7864328 | tf_op jit(solution)/shard_map/ppermute | solution.py:846
  341.0 9.4 %collective-permute-start.39 = (bf16[80,1920]{1,0:T(8,128)(2,1)S(1)}, bf16[80,1920]{1,0:T(8,128)(2,1)S(1)}, u32[]{:S(2)}, u32[]{:S(2)}) collective-permute-start(bf16[80,1920]{1,0:T(8,128)(2,1)S(1)} %get-tuple-element.124), channel_id=1, source_target_pairs={{0,4},{1,5},{2,6},{3,7},{4,0},{5,1},{6,2},{7,3},{8,12},{9,13},{10,... | collective-permute-start | bytes 921608 | tf_op jit(solution)/shard_map/ppermute | solution.py:846
  350.5 5.9 %collective-permute-start.31 = (bf16[320,512]{1,0:T(8,128)(2,1)S(1)}, bf16[320,512]{1,0:T(8,128)(2,1)S(1)}, u32[]{:S(2)}, u32[]{:S(2)}) collective-permute-start(bf16[320,512]{1,0:T(8,128)(2,1)S(1)} %copy-done.32), channel_id=1, source_target_pairs={{0,16},{1,17},{2,18},{3,19},{4,20},{5,21},{6,22},{7,23},{8,24},{9,... | collective-permute-start | bytes 983048 | tf_op jit(solution)/shard_map/ppermute | solution.py:846
  357.7 10.1 %collective-permute-done.39 = bf16[80,1920]{1,0:T(8,128)(2,1)S(1)} collective-permute-done((bf16[80,1920]{1,0:T(8,128)(2,1)S(1)}, bf16[80,1920]{1,0:T(8,128)(2,1)S(1)}, u32[]{:S(2)}, u32[]{:S(2)}) %collective-permute-start.39) | collective-permute-done | bytes 307232 | tf_op jit(solution)/shard_map/ppermute | solution.py:846
  367.7 7.6 %collective-permute-start.33 = (bf16[320,512]{1,0:T(8,128)(2,1)S(1)}, bf16[320,512]{1,0:T(8,128)(2,1)S(1)}, u32[]{:S(2)}, u32[]{:S(2)}) collective-permute-start(bf16[320,512]{1,0:T(8,128)(2,1)S(1)} %get-tuple-element.119), channel_id=1, source_target_pairs={{0,17},{1,16},{2,19},{3,18},{4,21},{5,20},{6,23},{7,22},{8,25},{9,... | collective-permute-start | bytes 983048 | tf_op jit(solution)/shard_map/ppermute | solution.py:846
  381.6 15.0 %collective-permute-done.40 = bf16[1,80,1920]{2,1,0:T(8,128)(2,1)S(1)} collective-permute-done((bf16[1,80,1920]{2,1,0:T(8,128)(2,1)S(1)}, bf16[1,80,1920]{2,1,0:T(8,128)(2,1)S(1)}, u32[]{:S(2)}, u32[]{:S(2)}) %collective-permute-start.40) | collective-permute-done | bytes 307232 | tf_op jit(solution)/shard_map/ppermute | solution.py:846
  396.8 6.9 %collective-permute-done.34 = bf16[160,512]{1,0:T(8,128)(2,1)S(1)} collective-permute-done((bf16[160,512]{1,0:T(8,128)(2,1)S(1)}, bf16[160,512]{1,0:T(8,128)(2,1)S(1)}, u32[]{:S(2)}, u32[]{:S(2)}) %collective-permute-start.34) | collective-permute-done | bytes 163872 | tf_op jit(solution)/shard_map/ppermute | solution.py:846
  407.1 7.4 %collective-permute-done.35 = bf16[1,160,512]{2,1,0:T(8,128)(2,1)S(1)} collective-permute-done((bf16[1,160,512]{2,1,0:T(8,128)(2,1)S(1)}, bf16[1,160,512]{2,1,0:T(8,128)(2,1)S(1)}, u32[]{:S(2)}, u32[]{:S(2)}) %collective-permute-start.35) | collective-permute-done | bytes 163872 | tf_op jit(solution)/shard_map/ppermute | solution.py:846
  438.4 27.0 %collective-permute-done.29 = bf16[4,160,512]{2,1,0:T(8,128)(2,1)S(1)} collective-permute-done((bf16[4,160,512]{2,1,0:T(8,128)(2,1)S(1)}, bf16[4,160,512]{2,1,0:T(8,128)(2,1)S(1)}, u32[]{:S(2)}, u32[]{:S(2)}) %collective-permute-start.29) | collective-permute-done | bytes 655392 | tf_op jit(solution)/shard_map/ppermute | solution.py:846
  466.6 12.1 %collective-permute-done.37 = bf16[4,160,512]{2,1,0:T(8,128)(2,1)S(1)} collective-permute-done((bf16[4,160,512]{2,1,0:T(8,128)(2,1)S(1)}, bf16[4,160,512]{2,1,0:T(8,128)(2,1)S(1)}, u32[]{:S(2)}, u32[]{:S(2)}) %collective-permute-start.37) | collective-permute-done | bytes 655392 | tf_op jit(solution)/shard_map/ppermute | solution.py:846
  485.4 11.3 %collective-permute-start.25 = (bf16[1,512,1280]{2,1,0:T(8,128)(2,1)}, bf16[1,512,1280]{2,1,0:T(8,128)(2,1)}, u32[]{:S(2)}, u32[]{:S(2)}) collective-permute-start(bf16[1,512,1280]{2,1,0:T(8,128)(2,1)} %fusion.16), channel_id=1, source_target_pairs={{0,0},{1,1},{2,4},{3,5},{4,8},{5,9},{6,12},{7,13},{8,2},{9,3},{10,... | collective-permute-start | bytes 3932168 | tf_op jit(solution)/shard_map/ppermute | solution.py:846
  501.9 15.8 %collective-permute-done.46 = f32[21,128]{1,0:T(8,128)S(1)} collective-permute-done((f32[21,128]{1,0:T(8,128)S(1)}, f32[21,128]{1,0:T(8,128)S(1)}, u32[]{:S(2)}, u32[]{:S(2)}) %collective-permute-start.46) | collective-permute-done | bytes 10784 | tf_op jit(solution)/shard_map/ppermute | solution.py:846
  522.7 7.7 %spread.1 = f32[4,160,3840]{2,1,0:T(8,128)} custom-call(s32[4]{0:T(128)S(1)} %add_add_fusion.at, bf16[8,160,512]{2,1,0:T(8,128)(2,1)} %pad_maximum_fusion.3.refs_0_, bf16[8,160,512]{2,1,0:T(8,128)(2,1)} %collective-permute-done.30.refs_1_, bf16[8,160,512]{2,1,0:T(8,128)(2,1)} %pad_maximum_fusion.4.refs_2_, bf16[8,160,512]{2,1,0:T(8,128)(2,1)} %collective-permute-done.38.refs_3_), custom_call_target="tpu_custom_call" | custom-call | flops 1000 | bytes 1000 | tf_op jit(solution)/shard_map/spread/pallas_call | solution.py:785
  531.5 7.1 %place_tail.1 = (f32[8,80,1280]{2,1,0:T(8,128)}, f32[8,80,1280]{2,1,0:T(8,128)}, f32[8,80,1280]{2,1,0:T(8,128)}) custom-call(s32[4]{0:T(128)S(1)} %add_add_fusion.1.at, bf16[8,80,1920]{2,1,0:T(8,128)(2,1)S(1)} %pad_maximum_fusion.2.own_ref, bf16[8,80,1920]{2,1,0:T(8,128)(2,1)} %collective-permute-done.43.mate_ref), custom_call_target="tpu_custom_call" | custom-call | flops 1000 | bytes 1000 | tf_op jit(solution)/shard_map/place_tail/pallas_call | solution.py:702
  (261 shorter events, 154.1 us)
Async XLA Ops:
  22.8 33.2 %collective-permute-start.7 = (bf16[640,1024]{1,0:T(8,128)(2,1)}, bf16[640,1024]{1,0:T(8,128)(2,1)}, u32[]{:S(2)}, u32[]{:S(2)}) collective-permute-start(bf16[640,1024]{1,0:T(8,128)(2,1)} %pick.1.a_ref), channel_id=1, source_target_pairs={{0,1},{1,0},{2,3},{3,2},{4,5},{5,4},{6,7},{7,6},{8,9},{9,8},{10,11... | collective-permute-start | bytes 3932168 | tf_op jit(solution)/shard_map/ppermute | solution.py:846
  24.8 41.8 %collective-permute-start.4 = (bf16[512,1280]{1,0:T(8,128)(2,1)S(1)}, bf16[512,1280]{1,0:T(8,128)(2,1)}, u32[]{:S(2)}, u32[]{:S(2)}) collective-permute-start(bf16[512,1280]{1,0:T(8,128)(2,1)S(1)} %bitcast.95), channel_id=1, source_target_pairs={{0,8},{1,9},{2,10},{3,11},{12,4},{13,5},{14,6},{15,7},{16,24},{17,... | collective-permute-start | bytes 3932168 | tf_op jit(solution)/shard_map/ppermute | solution.py:846
  27.2 39.5 %collective-permute-start.5 = (bf16[512,1280]{1,0:T(8,128)(2,1)}, bf16[512,1280]{1,0:T(8,128)(2,1)}, u32[]{:S(2)}, u32[]{:S(2)}) collective-permute-start(bf16[512,1280]{1,0:T(8,128)(2,1)} %collective-permute-done.1.refs_2_), channel_id=1, source_target_pairs={{0,8},{1,9},{2,10},{3,11},{12,4},{13,5},{14,6},{15,7},{16,24},{17,... | collective-permute-start | bytes 3932168 | tf_op jit(solution)/shard_map/ppermute | solution.py:846
  42.5 39.2 %collective-permute-start.3 = (bf16[512,1280]{1,0:T(8,128)(2,1)}, bf16[512,1280]{1,0:T(8,128)(2,1)S(1)}, u32[]{:S(2)}, u32[]{:S(2)}) collective-permute-start(bf16[512,1280]{1,0:T(8,128)(2,1)} %broadcast_select_fusion), channel_id=1, source_target_pairs={{0,2},{1,3},{2,0},{3,1},{12,14},{13,15},{14,12},{15,13},{16,18},{1... | collective-permute-start | bytes 3932168 | tf_op jit(solution)/shard_map/ppermute | solution.py:846
  56.0 70.2 %collective-permute-start.13 = (bf16[3,320,1280]{2,1,0:T(8,128)(2,1)}, bf16[3,320,1280]{2,1,0:T(8,128)(2,1)}, u32[]{:S(2)}, u32[]{:S(2)}) collective-permute-start(bf16[3,320,1280]{2,1,0:T(8,128)(2,1)} %constant_dynamic-slice_fusion), channel_id=1, source_target_pairs={{0,1},{1,0},{2,3},{3,2},{4,5},{5,4},{6,7},{7,6},{8,9},{9,8},{10,11... | collective-permute-start | bytes 7372808 | tf_op jit(solution)/shard_map/ppermute | solution.py:846
  127.9 32.5 %collective-permute-start.14 = (bf16[3,320,1280]{2,1,0:T(8,128)(2,1)}, bf16[3,320,1280]{2,1,0:T(8,128)(2,1)}, u32[]{:S(2)}, u32[]{:S(2)}) collective-permute-start(bf16[3,320,1280]{2,1,0:T(8,128)(2,1)} %collective-permute-done.13.half), channel_id=1, source_target_pairs={{0,8},{1,9},{2,10},{3,11},{4,12},{5,13},{6,14},{7,15},{8,0},{9,1},... | collective-permute-start | bytes 7372808 | tf_op jit(solution)/shard_map/ppermute | solution.py:846
  130.4 30.0 %collective-permute-start.10 = (bf16[512,320]{1,0:T(8,128)(2,1)}, bf16[512,320]{1,0:T(8,128)(2,1)S(1)}, u32[]{:S(2)}, u32[]{:S(2)}) collective-permute-start(bf16[512,320]{1,0:T(8,128)(2,1)} %get-tuple-element.138), channel_id=1, source_target_pairs={{0,2},{1,3},{2,0},{3,1},{4,6},{5,7},{6,4},{7,5},{8,10},{9,11},{10,... | collective-permute-start | bytes 983048 | tf_op jit(solution)/shard_map/ppermute | solution.py:846
  132.4 27.9 %collective-permute-start.11 = (bf16[512,320]{1,0:T(8,128)(2,1)}, bf16[512,320]{1,0:T(8,128)(2,1)}, u32[]{:S(2)}, u32[]{:S(2)}) collective-permute-start(bf16[512,320]{1,0:T(8,128)(2,1)} %get-tuple-element.137), channel_id=1, source_target_pairs={{0,10},{1,11},{2,8},{3,9},{4,14},{5,15},{6,12},{7,13},{8,2},{9,3},... | collective-permute-start | bytes 983048 | tf_op jit(solution)/shard_map/ppermute | solution.py:846
  195.1 22.2 %collective-permute-start.19 = (bf16[1280,1920]{1,0:T(8,128)(2,1)S(1)}, bf16[1280,1920]{1,0:T(8,128)(2,1)S(1)}, u32[]{:S(2)}, u32[]{:S(2)}) collective-permute-start(bf16[1280,1920]{1,0:T(8,128)(2,1)S(1)} %share.1), channel_id=1, source_target_pairs={{0,8},{1,9},{2,10},{3,11},{4,12},{5,13},{6,14},{7,15},{8,0},{9,1},... | collective-permute-start | bytes 14745608 | tf_op jit(solution)/shard_map/ppermute | solution.py:846
  227.6 109.6 %all-to-all-start = ((bf16[8,160,1920]{2,1,0:T(8,128)(2,1)}), bf16[8,160,1920]{2,1,0:T(8,128)(2,1)}, u32[]{:S(2)}, u32[]{:S(2)}) async-start(bf16[8,160,1920]{2,1,0:T(8,128)(2,1)} %bitcast.93), calls=%async_computation | async-start | bytes 9830400 | tf_op jit(solution)/shard_map/all_to_all | solution.py:1013
  232.4 47.1 %collective-permute-start.16 = (bf16[1,512,1280]{2,1,0:T(8,128)(2,1)}, bf16[1,512,1280]{2,1,0:T(8,128)(2,1)}, u32[]{:S(2)}, u32[]{:S(2)}) collective-permute-start(bf16[1,512,1280]{2,1,0:T(8,128)(2,1)} %bitcast.21), channel_id=1, source_target_pairs={{0,0},{1,1},{2,4},{3,5},{4,8},{5,9},{6,12},{7,13},{8,2},{9,3},{10,... | collective-permute-start | bytes 3932168 | tf_op jit(solution)/shard_map/ppermute | solution.py:846
  275.9 32.9 %collective-permute-start.20 = (bf16[320,512]{1,0:T(8,128)(2,1)S(1)}, bf16[320,512]{1,0:T(8,128)(2,1)S(1)}, u32[]{:S(2)}, u32[]{:S(2)}) collective-permute-start(bf16[320,512]{1,0:T(8,128)(2,1)S(1)} %get-tuple-element.106), channel_id=1, source_target_pairs={{0,16},{1,17},{2,18},{3,19},{4,20},{5,21},{6,22},{7,23},{8,24},{9,... | collective-permute-start | bytes 983048 | tf_op jit(solution)/shard_map/ppermute | solution.py:846
  277.8 30.9 %collective-permute-start.21 = (bf16[320,512]{1,0:T(8,128)(2,1)S(1)}, bf16[320,512]{1,0:T(8,128)(2,1)S(1)}, u32[]{:S(2)}, u32[]{:S(2)}) collective-permute-start(bf16[320,512]{1,0:T(8,128)(2,1)S(1)} %get-tuple-element.107), channel_id=1, source_target_pairs={{0,1},{1,0},{2,3},{3,2},{4,5},{5,4},{6,7},{7,6},{8,9},{9,8},{10,11... | collective-permute-start | bytes 983048 | tf_op jit(solution)/shard_map/ppermute | solution.py:846
  279.3 33.9 %collective-permute-start.22 = (bf16[320,512]{1,0:T(8,128)(2,1)S(1)}, bf16[320,512]{1,0:T(8,128)(2,1)S(1)}, u32[]{:S(2)}, u32[]{:S(2)}) collective-permute-start(bf16[320,512]{1,0:T(8,128)(2,1)S(1)} %get-tuple-element.108), channel_id=1, source_target_pairs={{0,17},{1,16},{2,19},{3,18},{4,21},{5,20},{6,23},{7,22},{8,25},{9,... | collective-permute-start | bytes 983048 | tf_op jit(solution)/shard_map/ppermute | solution.py:846
  323.3 94.0 %collective-permute-start.23 = (bf16[2,512,1280]{2,1,0:T(8,128)(2,1)}, bf16[2,512,1280]{2,1,0:T(8,128)(2,1)}, u32[]{:S(2)}, u32[]{:S(2)}) collective-permute-start(bf16[2,512,1280]{2,1,0:T(8,128)(2,1)} %pad_maximum_fusion.1), channel_id=1, source_target_pairs={{0,8},{1,9},{2,10},{3,11},{4,12},{5,13},{6,14},{7,15},{8,0},{9,1},... | collective-permute-start | bytes 7864328 | tf_op jit(solution)/shard_map/ppermute | solution.py:846
  341.0 26.7 %collective-permute-start.39 = (bf16[80,1920]{1,0:T(8,128)(2,1)S(1)}, bf16[80,1920]{1,0:T(8,128)(2,1)S(1)}, u32[]{:S(2)}, u32[]{:S(2)}) collective-permute-start(bf16[80,1920]{1,0:T(8,128)(2,1)S(1)} %get-tuple-element.124), channel_id=1, source_target_pairs={{0,4},{1,5},{2,6},{3,7},{4,0},{5,1},{6,2},{7,3},{8,12},{9,13},{10,... | collective-permute-start | bytes 921608 | tf_op jit(solution)/shard_map/ppermute | solution.py:846
  350.5 24.9 %collective-permute-start.26 = (bf16[160,512]{1,0:T(8,128)(2,1)S(1)}, bf16[160,512]{1,0:T(8,128)(2,1)S(1)}, u32[]{:S(2)}, u32[]{:S(2)}) collective-permute-start(bf16[160,512]{1,0:T(8,128)(2,1)S(1)} %get-tuple-element.109), channel_id=1, source_target_pairs={{0,4},{1,5},{2,6},{3,7},{4,0},{5,1},{6,2},{7,3},{8,12},{9,13},{10,... | collective-permute-start | bytes 491528 | tf_op jit(solution)/shard_map/ppermute | solution.py:846
  350.5 25.3 %collective-permute-start.31 = (bf16[320,512]{1,0:T(8,128)(2,1)S(1)}, bf16[320,512]{1,0:T(8,128)(2,1)S(1)}, u32[]{:S(2)}, u32[]{:S(2)}) collective-permute-start(bf16[320,512]{1,0:T(8,128)(2,1)S(1)} %copy-done.32), channel_id=1, source_target_pairs={{0,16},{1,17},{2,18},{3,19},{4,20},{5,21},{6,22},{7,23},{8,24},{9,... | collective-permute-start | bytes 983048 | tf_op jit(solution)/shard_map/ppermute | solution.py:846
  356.4 22.5 %collective-permute-start.32 = (bf16[320,512]{1,0:T(8,128)(2,1)S(1)}, bf16[320,512]{1,0:T(8,128)(2,1)S(1)}, u32[]{:S(2)}, u32[]{:S(2)}) collective-permute-start(bf16[320,512]{1,0:T(8,128)(2,1)S(1)} %get-tuple-element.118), channel_id=1, source_target_pairs={{0,1},{1,0},{2,3},{3,2},{4,5},{5,4},{6,7},{7,6},{8,9},{9,8},{10,11... | collective-permute-start | bytes 983048 | tf_op jit(solution)/shard_map/ppermute | solution.py:846
  375.4 21.3 %collective-permute-start.40 = (bf16[1,80,1920]{2,1,0:T(8,128)(2,1)S(1)}, bf16[1,80,1920]{2,1,0:T(8,128)(2,1)S(1)}, u32[]{:S(2)}, u32[]{:S(2)}) collective-permute-start(bf16[1,80,1920]{2,1,0:T(8,128)(2,1)S(1)} %fusion.29), channel_id=1, source_target_pairs={{0,4},{1,5},{2,6},{3,7},{4,0},{5,1},{6,2},{7,3},{8,12},{9,13},{10,... | collective-permute-start | bytes 921608 | tf_op jit(solution)/shard_map/ppermute | solution.py:846
  375.9 28.8 %collective-permute-start.27 = (bf16[1,160,512]{2,1,0:T(8,128)(2,1)S(1)}, bf16[1,160,512]{2,1,0:T(8,128)(2,1)S(1)}, u32[]{:S(2)}, u32[]{:S(2)}) collective-permute-start(bf16[1,160,512]{2,1,0:T(8,128)(2,1)S(1)} %fusion.30), channel_id=1, source_target_pairs={{0,4},{1,5},{2,6},{3,7},{4,0},{5,1},{6,2},{7,3},{8,12},{9,13},{10,... | collective-permute-start | bytes 491528 | tf_op jit(solution)/shard_map/ppermute | solution.py:846
  381.6 22.1 %collective-permute-start.34 = (bf16[160,512]{1,0:T(8,128)(2,1)S(1)}, bf16[160,512]{1,0:T(8,128)(2,1)S(1)}, u32[]{:S(2)}, u32[]{:S(2)}) collective-permute-start(bf16[160,512]{1,0:T(8,128)(2,1)S(1)} %get-tuple-element.121), channel_id=1, source_target_pairs={{0,4},{1,5},{2,6},{3,7},{4,0},{5,1},{6,2},{7,3},{8,12},{9,13},{10,... | collective-permute-start | bytes 491528 | tf_op jit(solution)/shard_map/ppermute | solution.py:846
  396.7 23.6 %collective-permute-start.41 = (bf16[2,80,1920]{2,1,0:T(8,128)(2,1)S(1)}, bf16[2,80,1920]{2,1,0:T(8,128)(2,1)S(1)}, u32[]{:S(2)}, u32[]{:S(2)}) collective-permute-start(bf16[2,80,1920]{2,1,0:T(8,128)(2,1)S(1)} %pad_maximum_fusion.8), channel_id=1, source_target_pairs={{0,2},{1,3},{2,0},{3,1},{4,6},{5,7},{6,4},{7,5},{8,10},{9,11},{10,... | collective-permute-start | bytes 1843208 | tf_op jit(solution)/shard_map/ppermute | solution.py:846
  404.8 22.6 %collective-permute-start.28 = (bf16[2,160,512]{2,1,0:T(8,128)(2,1)S(1)}, bf16[2,160,512]{2,1,0:T(8,128)(2,1)S(1)}, u32[]{:S(2)}, u32[]{:S(2)}) collective-permute-start(bf16[2,160,512]{2,1,0:T(8,128)(2,1)S(1)} %pad_maximum_fusion.9), channel_id=1, source_target_pairs={{0,2},{1,3},{2,0},{3,1},{4,6},{5,7},{6,4},{7,5},{8,10},{9,11},{10,... | collective-permute-start | bytes 983048 | tf_op jit(solution)/shard_map/ppermute | solution.py:846
  420.5 59.4 %collective-permute-start.42 = (bf16[4,80,1920]{2,1,0:T(8,128)(2,1)S(1)}, bf16[4,80,1920]{2,1,0:T(8,128)(2,1)S(1)}, u32[]{:S(2)}, u32[]{:S(2)}) collective-permute-start(bf16[4,80,1920]{2,1,0:T(8,128)(2,1)S(1)} %pad_maximum_fusion.5), channel_id=1, source_target_pairs={{0,16},{1,17},{2,18},{3,19},{4,20},{5,21},{6,22},{7,23},{8,24},{9,... | collective-permute-start | bytes 3686408 | tf_op jit(solution)/shard_map/ppermute | solution.py:846
  424.5 56.3 %collective-permute-start.24 = (bf16[512,1280]{1,0:T(8,128)(2,1)S(1)}, bf16[512,1280]{1,0:T(8,128)(2,1)S(1)}, u32[]{:S(2)}, u32[]{:S(2)}) collective-permute-start(bf16[512,1280]{1,0:T(8,128)(2,1)S(1)} %fusion.3), channel_id=1, source_target_pairs={{0,2},{1,3},{2,0},{3,1},{4,6},{5,7},{6,4},{7,5},{8,10},{9,11},{10,... | collective-permute-start | bytes 3932168 | tf_op jit(solution)/shard_map/ppermute | solution.py:846
  427.5 37.9 %collective-permute-start.29 = (bf16[4,160,512]{2,1,0:T(8,128)(2,1)S(1)}, bf16[4,160,512]{2,1,0:T(8,128)(2,1)S(1)}, u32[]{:S(2)}, u32[]{:S(2)}) collective-permute-start(bf16[4,160,512]{2,1,0:T(8,128)(2,1)S(1)} %pad_maximum_fusion.6), channel_id=1, source_target_pairs={{0,16},{1,17},{2,18},{3,19},{4,20},{5,21},{6,22},{7,23},{8,24},{9,... | collective-permute-start | bytes 1966088 | tf_op jit(solution)/shard_map/ppermute | solution.py:846
  434.5 44.2 %collective-permute-start.37 = (bf16[4,160,512]{2,1,0:T(8,128)(2,1)S(1)}, bf16[4,160,512]{2,1,0:T(8,128)(2,1)S(1)}, u32[]{:S(2)}, u32[]{:S(2)}) collective-permute-start(bf16[4,160,512]{2,1,0:T(8,128)(2,1)S(1)} %pad_maximum_fusion.7), channel_id=1, source_target_pairs={{0,16},{1,17},{2,18},{3,19},{4,20},{5,21},{6,22},{7,23},{8,24},{9,... | collective-permute-start | bytes 1966088 | tf_op jit(solution)/shard_map/ppermute | solution.py:846
  466.6 56.1 %collective-permute-start.30 = (bf16[8,160,512]{2,1,0:T(8,128)(2,1)}, bf16[8,160,512]{2,1,0:T(8,128)(2,1)}, u32[]{:S(2)}, u32[]{:S(2)}) collective-permute-start(bf16[8,160,512]{2,1,0:T(8,128)(2,1)} %pad_maximum_fusion.3.refs_0_), channel_id=1, source_target_pairs={{0,8},{1,9},{2,10},{3,11},{4,12},{5,13},{6,14},{7,15},{8,0},{9,1},... | collective-permute-start | bytes 3932168 | tf_op jit(solution)/shard_map/ppermute | solution.py:846
  479.9 42.8 %collective-permute-start.38 = (bf16[8,160,512]{2,1,0:T(8,128)(2,1)}, bf16[8,160,512]{2,1,0:T(8,128)(2,1)}, u32[]{:S(2)}, u32[]{:S(2)}) collective-permute-start(bf16[8,160,512]{2,1,0:T(8,128)(2,1)} %pad_maximum_fusion.4.refs_2_), channel_id=1, source_target_pairs={{0,8},{1,9},{2,10},{3,11},{4,12},{5,13},{6,14},{7,15},{8,0},{9,1},... | collective-permute-start | bytes 3932168 | tf_op jit(solution)/shard_map/ppermute | solution.py:846
  480.2 51.3 %collective-permute-start.43 = (bf16[8,80,1920]{2,1,0:T(8,128)(2,1)S(1)}, bf16[8,80,1920]{2,1,0:T(8,128)(2,1)}, u32[]{:S(2)}, u32[]{:S(2)}) collective-permute-start(bf16[8,80,1920]{2,1,0:T(8,128)(2,1)S(1)} %pad_maximum_fusion.2.own_ref), channel_id=1, source_target_pairs={{0,8},{1,9},{2,10},{3,11},{4,12},{5,13},{6,14},{7,15},{8,0},{9,1},... | collective-permute-start | bytes 7372808 | tf_op jit(solution)/shard_map/ppermute | solution.py:846
  485.4 46.1 %collective-permute-start.25 = (bf16[1,512,1280]{2,1,0:T(8,128)(2,1)}, bf16[1,512,1280]{2,1,0:T(8,128)(2,1)}, u32[]{:S(2)}, u32[]{:S(2)}) collective-permute-start(bf16[1,512,1280]{2,1,0:T(8,128)(2,1)} %fusion.16), channel_id=1, source_target_pairs={{0,0},{1,1},{2,4},{3,5},{4,8},{5,9},{6,12},{7,13},{8,2},{9,3},{10,... | collective-permute-start | bytes 3932168 | tf_op jit(solution)/shard_map/ppermute | solution.py:846
  (70 other events, 857.6 us)

commit v4 on v3

--- a/solution.py
+++ b/solution.py
@@ -17,7 +17,11 @@
 scale_base = 1.442695041
 log2e = 1.4426950408889634
 NEG = -1e30
-CHEAP = pl.CostEstimate(flops=1000, transcendentals=0, bytes_accessed=1000)
+def cost(us):
+    return pl.CostEstimate(flops=int(us * 1_000_000_000), transcendentals=0, bytes_accessed=1000)
+
+
+CHEAP = cost(0.001)
 f32 = jnp.float32
 bf16 = jnp.bfloat16
 AXES = ("gx", "gc", "far", "near", "wt")
@@ -166,7 +170,7 @@
         ],
         grid_spec=spec,
         compiler_params=pltpu.CompilerParams(vmem_limit_bytes=40 << 20),
-        cost_estimate=CHEAP,
+        cost_estimate=cost(0.01),
         name="attn_fwd",
     )(block_flags(seg_row, bq, bk), q, kv, seg_row[:, None], seg_row[None])
 
@@ -301,7 +305,7 @@
         ],
         grid_spec=spec,
         compiler_params=pltpu.CompilerParams(vmem_limit_bytes=48 << 20),
-        cost_estimate=CHEAP,
+        cost_estimate=cost(0.01),
         name="attn_bwd",
     )(block_flags(seg_row, bq, bk), mine.reshape(1), qa, kv, kv, *pieces, of, seg_row[:, None], seg_row[None], scale)
 
@@ -340,7 +344,7 @@
             in_specs=[pl.BlockSpec((step, 3 * D), lambda i, m: (i, 0))],
             out_specs=pl.BlockSpec((step, lanes_up(3 * nh * HD)), lambda i, m: (i, 0)),
         ),
-        cost_estimate=CHEAP,
+        cost_estimate=cost(5),
         name="pick",
     )(mine.reshape(1), w)
 
@@ -393,7 +397,7 @@
             ],
             out_specs=[pl.BlockSpec((step, each), at)] * groups + [pl.BlockSpec((step, 3 * nh * LN), at)],
         ),
-        cost_estimate=CHEAP,
+        cost_estimate=cost(16),
         name="widen",
     )(own_at.reshape(1), own, other)
 
@@ -473,7 +477,7 @@
         ),
         input_output_aliases=aliases,
         compiler_params=pltpu.CompilerParams(vmem_limit_bytes=48 << 20),
-        cost_estimate=CHEAP,
+        cost_estimate=cost(10),
         name="project",
     )(info, *args)
 
@@ -572,7 +576,7 @@
             scratch_shapes=scratch,
         ),
         compiler_params=pltpu.CompilerParams(vmem_limit_bytes=52 << 20),
-        cost_estimate=CHEAP,
+        cost_estimate=cost(0.01),
         name="tail",
     )(at, *pieces, x, g, *weights, gain)
 
@@ -605,7 +609,7 @@
             out_specs=pl.BlockSpec((d, w), lambda i, c: (0, i)),
         ),
         compiler_params=pltpu.CompilerParams(vmem_limit_bytes=40 << 20),
-        cost_estimate=CHEAP,
+        cost_estimate=cost(.01),
         name="share",
     )(col.reshape(1), *lefts, *rights)
 
@@ -638,46 +642,44 @@
             out_specs=block,
         ),
         compiler_params=pltpu.CompilerParams(vmem_limit_bytes=40 << 20),
-        cost_estimate=CHEAP,
+        cost_estimate=cost(.01),
         name="keep",
     )(col.reshape(1), *lefts, *rights, got)
 
 
-def total_kernel(bit, *refs):
-    ins, outs = refs[:-2], refs[-2:]
-    for half, out in zip((1 - bit[0], bit[0]), outs):
-        acc = jnp.zeros(out.shape, f32)
-        for ref in ins:
-            for i in range(ref.shape[0]):
-                acc = acc + ref[i, half].astype(f32)
-        out[...] = acc.astype(bf16)
-
-
-def total(arrays, bit):
-    _, _, r, c = arrays[0].shape
+def total_kernel(*refs):
+    acc = jnp.zeros(refs[-1].shape, f32)
+    for ref in refs[:-1]:
+        for i in range(ref.shape[0]):
+            acc = acc + ref[i].astype(f32)
+    refs[-1][...] = acc.astype(bf16)
+
+
+def total(arrays):
+    _, r, c = arrays[0].shape
     w = c
-    for cut in (640, 512):
+    for cut in (640, 256):
         if c % cut == 0:
             w = cut
             break
     return pl.pallas_call(
         total_kernel,
-        out_shape=[jax.ShapeDtypeStruct((r, c), bf16)] * 2,
+        out_shape=jax.ShapeDtypeStruct((r, c), bf16),
         grid_spec=pltpu.PrefetchScalarGridSpec(
-            num_scalar_prefetch=1,
+            num_scalar_prefetch=0,
             grid=(c // w,),
-            in_specs=[pl.BlockSpec((x.shape[0], 2, r, w), lambda i, m: (0, 0, 0, i)) for x in arrays],
-            out_specs=[pl.BlockSpec((r, w), lambda i, m: (0, i))] * 2,
+            in_specs=[pl.BlockSpec((x.shape[0], r, w), lambda i: (0, 0, i)) for x in arrays],
+            out_specs=pl.BlockSpec((r, w), lambda i: (0, i)),
         ),
         compiler_params=pltpu.CompilerParams(vmem_limit_bytes=40 << 20),
-        cost_estimate=CHEAP,
+        cost_estimate=cost(10),
         name="total",
-    )(bit.reshape(1), *arrays)
+    )(*arrays)
 
 
 def place_kernel(at, own_ref, mate_ref, o0, o1, o2):
     block = pl.program_id(0)
-    slot = ((block // 4) ^ at[0]) * 4 + (((block // 2) % 2) ^ at[1]) * 2 + ((block % 2) ^ at[2])
+    slot = ((block // 2) ^ at[0]) * 2 + ((block % 2) ^ at[1])
     w = o0.shape[2] // 2
 
     def put(refs):
@@ -686,11 +688,11 @@
             for i, out in enumerate((o0, o1, o2)):
                 out[0, :, side * w : (side + 1) * w] = part[:, i * w : (i + 1) * w]
 
-    @pl.when(at[3] == 0)
+    @pl.when(at[2] == 0)
     def _():
         put((own_ref, mate_ref))
 
-    @pl.when(at[3] == 1)
+    @pl.when(at[2] == 1)
     def _():
         put((mate_ref, own_ref))
 
@@ -709,7 +711,7 @@
             out_specs=[pl.BlockSpec((1, h, d), lambda i, m: (i, 0, 0))] * 3,
         ),
         compiler_params=pltpu.CompilerParams(vmem_limit_bytes=40 << 20),
-        cost_estimate=CHEAP,
+        cost_estimate=cost(.1),
         name="place_tail",
     )(at, own, mate)
     return [out.reshape(n * h, d) for out in outs]
@@ -747,16 +749,16 @@
             scratch_shapes=[pltpu.VMEM((w, g.shape[1]), bf16)],
         ),
         compiler_params=pltpu.CompilerParams(vmem_limit_bytes=40 << 20),
-        cost_estimate=CHEAP,
+        cost_estimate=cost(0.1),
         name="cross",
     )(at, x, g)
 
 
 def spread_kernel(at, *refs, groups, width):
     out = refs[-1]
-    gx, host, near, gc = at[0], at[1], at[2], at[3]
-    block = pl.program_id(0)
-    slot = ((block // 2) ^ gx) * 4 + ((block % 2) ^ host)
+    step = out.shape[1]
+    slot = (pl.program_id(0) ^ at[0]) * 2
+    rows = pl.ds(pl.multiple_of(pl.program_id(1) * step, step), step)
 
     def put(flip):
         cut = []
@@ -764,37 +766,38 @@
             for n in range(2):
                 for core in range(2):
                     for g in range(groups):
-                        ref = refs[2 * g + (core ^ flip)]
-                        part = ref[slot + 2 * (n ^ near)]
+                        part = refs[2 * g + (core ^ flip)][slot + (n ^ at[1]), rows, :]
                         cut.append(part[:, t * width : (t + 1) * width])
         out[0] = jnp.concatenate(cut, axis=1).astype(f32)
 
     for flip in range(2):
 
-        @pl.when(gc == flip)
+        @pl.when(at[2] == flip)
         def _(flip=flip):
             put(flip)
 
 
 def spread(arrays, at, used):
     flat = [x for pair in arrays for x in pair]
-    slots, rows, cols = flat[0].shape
-    full = lambda i, m: (0, 0, 0)
+    _, rows, _ = flat[0].shape
     groups = len(arrays)
-    total = 4 * groups * used
+    width = 4 * groups * used
+    cuts = 2 if rows % 32 == 0 else 1
     return pl.pallas_call(
         functools.partial(spread_kernel, groups=groups, width=used // 3),
-        out_shape=jax.ShapeDtypeStruct((4, rows, total), f32),
+        out_shape=jax.ShapeDtypeStruct((2, rows, width), f32),
         grid_spec=pltpu.PrefetchScalarGridSpec(
             num_scalar_prefetch=1,
-            grid=(4,),
-            in_specs=[pl.BlockSpec(x.shape, full, pipeline_mode=pl.Buffered(1)) for x in flat],
-            out_specs=pl.BlockSpec((1, rows, total), lambda i, m: (i, 0, 0)),
+            grid=(2, cuts),
+            in_specs=[
+                pl.BlockSpec(x.shape, lambda i, j, m: (0, 0, 0), pipeline_mode=pl.Buffered(1)) for x in flat
+            ],
+            out_specs=pl.BlockSpec((1, rows // cuts, width), lambda i, j, m: (i, j, 0)),
         ),
         compiler_params=pltpu.CompilerParams(vmem_limit_bytes=40 << 20),
-        cost_estimate=CHEAP,
+        cost_estimate=cost(0.1),
         name="spread",
-    )(at, *flat).reshape(4 * rows, total)
+    )(at, *flat).reshape(2 * rows, width)
 
 
 def rms_inverse(values):
@@ -835,7 +838,7 @@
                 for z in range(4):
                     for w in range(sizes["wt"]):
                         goal = target(gx, gc, z, w)
-                        if goal is not None:
+                        if goal is not None and goal != (gx, gc, z, w):
                             found.append((place(gx, gc, z, w), place(*goal)))
         return found
 
@@ -844,6 +847,9 @@
 
     def send(value, target):
         return lax.ppermute(value, AXES, pairs(target))
+
+    def move(value, target, still):
+        return jnp.where(still, value, send(value, target))
 
     def core_mate(gx, gc, z, w):
         return (gx, 1 - gc, z, w)
@@ -922,12 +928,11 @@
         def after(value, *others):
             return lax.optimization_barrier((value,) + others)[0]
 
-        own = tokens[0]
+        picked = pick(w_qkv, mine, parts, groups, nh)
+        own = after(tokens[0], picked)
         got1 = send(own, hop1)
         own_share = send(own, lane_share)
         seg_mate = send(segments, core_mate)
-        picked = pick(w_qkv, mine, parts, groups, nh)
-        got1 = after(got1, picked)
         got2 = send(got1, hop2)
         got1_share = send(got1, lane_share)
         end = jnp.where(gc == 0, z == 0, z == 3)
@@ -966,17 +971,18 @@
         )[None]
         seg_row = jnp.where(lane, segments, seg_mate)[0]
         fixed = (lane, mine, gain_attn[None], wide_w, lane_scale, ones, group_len)
-        first = project(
-            ((own, own_share), (got1, got1_share), (got2, got2_share)), places[:3], *fixed
+        carried = project(((own, own_share), (got1, got1_share)), places[:2], *fixed)
+        got2_share = after(got2_share, carried[0])
+        got3_share = send(after(got3, carried[0]), lane_share)
+        carried = project(((got2, got2_share),), places[2:3], *fixed, carried=carried)
+        all_normed, queries, keyval, inputs = project(
+            ((got3, after(got3_share, carried[0])),), places[3:], *fixed, carried=carried
         )
-        got3 = after(got3, first[0])
-        got3_share = send(got3, lane_share)
-        all_normed, queries, keyval, inputs = project(
-            ((got3, got3_share),), places[3:], *fixed, carried=first
-        )
-        grad_mlp = send(after(cotangent[0], got3), to_host)
+        still = lane & end
+        grad_mlp = move(after(cotangent[0], got3), to_host, still)
 
         att, att_float, q_aug = attn_fwd(queries, keyval, seg_row, nh)
+        att = after(att, grad_mlp)
 
         trades = (core_mate, near_mate, cross_mate)
         att_pieces = [rows_at(att, (mine ^ j) * rows, rows) for j in range(parts)]
@@ -1005,10 +1011,10 @@
         ) = tail(jnp.stack([mine, *starts]), att_pieces, inputs, grad_mlp, weights, gain_mlp[None])
         pieces = [pieces[0]] + [send(pieces[j + 1], trades[j]) for j in range(3)]
 
-        lefts = (attended, normed_mlp, active)
+        lefts = (after(attended, pieces[1]), normed_mlp, active)
         rights = (grad_proj, grad_hidden, grad_mlp)
         from_core = send(share(lefts, rights, 1 - gc), core_mate)
-        layer_out = send(after(layer_out, pieces[2])[None], to_home)
+        home_out = send(after(layer_out, pieces[2]), to_home)
         summed = keep(lefts, rights, after(from_core, *pieces[1:]), gc)
         kept = lax.all_to_all(summed, ("wt", "gx", "near"), 0, 0, tiled=True)
 
@@ -1020,62 +1026,66 @@
             )
 
         def gather(block):
-            for mate in (far_mate, near_mate, x_mate):
+            for mate in (near_mate, x_mate):
                 block = jnp.concatenate([block, send(block, mate)])
             return block, send(block, core_mate)
 
-        def far_sum(pair):
-            part, kept = pair
-            return (kept.astype(f32) + send(part, far_mate).astype(f32)).astype(bf16)[None]
+        def far_sum(part):
+            return (part.astype(f32) + send(part, far_mate).astype(f32)).astype(bf16)[None]
 
         def by_rows(grad):
             if pair:
                 own, *rest = cross(all_normed, grad, jnp.stack([wt, gx]))
                 got = [send(part, mate) for part, mate in zip(rest, (x_mate, wt_mate, wt_x_mate))]
-                return [part.reshape(1, 2, part.shape[0] // 2, -1) for part in (own, *got)]
+                return [part[None] for part in (own, *got)]
             part = trans_times(all_normed, grad).astype(bf16)
             sources = sizes["wt"] * 2
             got = lax.all_to_all(part, ("wt", "gx"), 0, 0, tiled=True)
-            return [got.reshape(sources, 2, D // sources // 2, -1)]
+            return [got.reshape(sources, D // sources, -1)]
 
         pieces[3] = after(pieces[3], summed)
         grad_a, lanes_a = backward(0, pieces)
         rows_a = by_rows(grad_a)
-        pieces[3] = after(pieces[3], rows_a[0], layer_out)
+        pieces[3] = after(pieces[3], rows_a[0])
         grad_b, lanes_b = backward(1, pieces)
         rows_a[0] = after(rows_a[0], grad_b)
-        half_a = total(rows_a, host)
-        grad_b = after(grad_b, half_a[0])
+        sum_a = total(rows_a)
+        grad_b = after(grad_b, sum_a)
         rows_b = by_rows(grad_b)
-        block_a = far_sum(half_a)
-        block_b = far_sum(total(rows_b, host))
+        layer_out = jnp.where(still, after(layer_out, rows_b[0]), home_out)
+        block_a = far_sum(sum_a)
         sources = sizes["wt"] * 4
-        block = far_sum(
-            total([after(kept, rows_b[0]).reshape(sources, 2, D // sources // 2, -1)], host)
-        )
-
-        def shard_grad(shard):
+        tail_sum = total([after(kept, rows_b[0], layer_out).reshape(sources, D // sources, -1)])
+        block = far_sum(tail_sum)
+        rows_b[0] = after(rows_b[0], block_a)
+        sum_b = total(rows_b)
+        block_b = far_sum(sum_b)
+
+        def shard_grad(shard, *others):
             return sum(
-                times_trans(rows_at(grad, shard * rows, rows), w)
-                for grad, w in zip((after(grad_a, rows_b[0]), after(grad_b, rows_b[0])), flat_w)
+                times_trans(rows_at(after(grad, *others), shard * rows, rows), w)
+                for grad, w in zip((grad_a, grad_b), flat_w)
             )
 
-        to_core = jnp.stack([shard_grad(mine ^ 3), shard_grad(mine ^ 1)]).astype(bf16)
+        to_core = jnp.stack(
+            [shard_grad(mine ^ 3, tail_sum), shard_grad(mine ^ 1, tail_sum)]
+        ).astype(bf16)
         from_core = send(to_core, core_mate).astype(f32)
-        to_near = (shard_grad(mine ^ 2) + from_core[0]).astype(bf16)
-        grad_normed = shard_grad(mine) + from_core[1] + send(to_near, near_mate).astype(f32)
+        to_near = (shard_grad(mine ^ 2, sum_b) + from_core[0]).astype(bf16)
+        grad_normed = shard_grad(mine, sum_b) + from_core[1] + send(to_near, near_mate).astype(f32)
         inputs = inputs.astype(f32)
         inverse_attn = rms_inverse(inputs)
         grad_gain_attn = jnp.sum(grad_normed * inputs * inverse_attn, axis=0)
-        grad_tokens = send(
-            (grad_resid + norm_back(inputs, inverse_attn, grad_normed * gain_attn)).astype(bf16)[None],
+        grad_tokens = move(
+            (grad_resid + norm_back(inputs, inverse_attn, grad_normed * gain_attn)).astype(bf16),
             to_home,
+            still,
         )
 
         total_qkv = spread(
-            [gather(block_a), gather(block_b)], jnp.stack([gx, host, near, gc]), 3 * nh // groups * HD
+            [gather(block_a), gather(block_b)], jnp.stack([gx, near, gc]), 3 * nh // groups * HD
         )
-        totals = place_tail(*gather(block), jnp.stack([gx, near, host, gc]))
+        totals = place_tail(*gather(block), jnp.stack([gx, near, gc]))
 
         grad_query_scale = (
             (lanes_a + lanes_b)[0, :HD]
@@ -1088,8 +1098,8 @@
         ).reshape(-1, LN)
         small = sum_all(small).reshape(-1)
         return (
-            layer_out,
-            grad_tokens,
+            layer_out[None],
+            grad_tokens[None],
             total_qkv,
             *totals,
             small[:D],

time: 549 us -> 504 us (0.918)
  starting transfers between devices: 123 us -> 62.5 us
  waiting for transfers between devices: 191 us -> 201 us
  local copies, waits for them, and re-layouts: 36.2 us -> 26.9 us
  Pallas kernels: 167 us -> 174 us
    ppermute x49 -> x46, starting transfers between devices: 119 us -> 57.9 us  [send(): return lax.ppermute(value, AXES, pairs(target))]
    ppermute x49 -> x46, waiting for transfers between devices: 191 us -> 201 us  [send(): return lax.ppermute(value, AXES, pairs(target))]
    unnamed x108 -> x102, local copies, waits for them, and re-layouts: 30.2 us -> 22.9 us
    pallas_call x2 -> x3, Pallas kernels: 21.2 us -> 25.6 us  [project(): pl.pallas_call(functools.partial(project_kernel, count=count, width=width...]
  transfers between devices with their start and end apart: 50 -> 47, of which waited for: 22 -> 22; matrix products, arithmetic and copies ran while one was open for 6% -> 6% of each run, Pallas kernels for 24% -> 28%
where the time goes in v4:
time: 504 us; the launch traced here: 494 us
  waiting for transfers between devices  201 us (40%)
  Pallas kernels  174 us (35%)
  starting transfers between devices  62.5 us (12%)
  local copies, waits for them, and re-layouts  26.9 us (5%)
  other arithmetic  18.6 us (4%)
  matrix products  9.08 us (2%)
    ppermute x46, waiting for transfers between devices, send(): return lax.ppermute(value, AXES, pairs(target))  201 us
    ppermute x46, starting transfers between devices, send(): return lax.ppermute(value, AXES, pairs(target))  57.9 us
    pallas_call x2, Pallas kernels, attn_bwd(): pl.pallas_call(functools.partial(bwd_kernel, first=group * nh, nh=nh, bq=...  49.6 us
    pallas_call x3, Pallas kernels, project(): pl.pallas_call(functools.partial(project_kernel, count=count, width=width...  25.6 us
    pallas_call x1, Pallas kernels, attn_fwd(): pl.pallas_call(functools.partial(fwd_kernel, nh=nh, bq=bq, bk=bk, nk=n //...  24.9 us
    unnamed x102, local copies, waits for them, and re-layouts  22.9 us
    pallas_call x1, Pallas kernels, tail(): pl.pallas_call(body, out_shape=[jax.ShapeDtypeStruct((rows, d), bf16)] *...  22.2 us
  transfers between devices with their start and end apart: 47, of which 22 were waited for; matrix products, arithmetic and copies ran while one was open for 6% of the time, Pallas kernels for 28%

profile of v4, /device:TPU:0, one launch (start us, length us, event | category | flops | bytes accessed | tf_op | source)
XLA Modules:
  0.0 494.0 jit_solution(10537492571355814453)
XLA Ops:
  0.7 4.6 pick.1.a_ref
  9.6 5.4 %collective-permute-start.4 = (bf16[512,1280]{1,0:T(8,128)(2,1)S(1)}, bf16[512,1280]{1,0:T(8,128)(2,1)}, u32[]{:S(2)}, u32[]{:S(2)}) collective-permute-start(bf16[512,1280]{1,0:T(8,128)(2,1)S(1)} %bitcast.93), channel_id=1, source_target_pairs={{0,8},{1,9},{2,10},{3,11},{12,4},{13,5},{14,6},{15,7},{16,24},{17,... | collective-permute-start | bytes 3932168 | tf_op jit(solution)/shard_map/ppermute | solution.py:849
  17.4 8.5 %collective-permute-done.1.refs_2_ = bf16[512,1280]{1,0:T(8,128)(2,1)} collective-permute-done((bf16[512,1280]{1,0:T(8,128)(2,1)S(1)}, bf16[512,1280]{1,0:T(8,128)(2,1)}, u32[]{:S(2)}, u32[]{:S(2)}) %collective-permute-start.1) | collective-permute-done | bytes 1310752 | tf_op jit(solution)/shard_map/ppermute | solution.py:849
  32.8 12.8 %collective-permute-done.2.refs_0_ = bf16[512,1280]{1,0:T(8,128)(2,1)S(1)} collective-permute-done((bf16[512,1280]{1,0:T(8,128)(2,1)}, bf16[512,1280]{1,0:T(8,128)(2,1)S(1)}, u32[]{:S(2)}, u32[]{:S(2)}) %collective-permute-start.2) | collective-permute-done | bytes 1310752 | tf_op jit(solution)/shard_map/ppermute | solution.py:849
  46.8 3.9 collective-permute-start.3
  50.8 7.6 %widen.1 = (bf16[1280,512]{1,0:T(8,128)(2,1)}, bf16[1280,512]{1,0:T(8,128)(2,1)}, bf16[1280,1536]{1,0:T(8,128)(2,1)}) custom-call(s32[1]{0:T(128)} %bitcast.12.own_first, bf16[640,1024]{1,0:T(8,128)(2,1)} %pick.1.a_ref, bf16[640,1024]{1,0:T(8,128)(2,1)} %collective-permute-done.6.b_ref), custom_call_target="tpu_custom_call" | custom-call | flops 16000000000 | bytes 1000 | tf_op jit(solution)/shard_map/widen/pallas_call | solution.py:387
  60.8 10.6 %project.3 = (bf16[2048,1280]{1,0:T(8,128)(2,1)}, bf16[2048,512]{1,0:T(8,128)(2,1)}, bf16[2048,1024]{1,0:T(8,128)(2,1)}, bf16[512,1280]{1,0:T(8,128)(2,1)S(1)}) custom-call(s32[4]{0:T(128)S(1)} %pad_add_fusion.1.info, bf16[512,1280]{1,0:T(8,128)(2,1)S(1)} %bitcast.95, bf16[512,1280]{1,0:T(8,128)(2,1)} %collective-permute-done.4.refs_1_, ...), custom_call_target="tpu_custom_call" | custom-call | flops 10000000000 | bytes 1000 | tf_op jit(solution)/shard_map/project/pallas_call | solution.py:459
  79.0 7.4 %project.4 = (bf16[2048,1280]{1,0:T(8,128)(2,1)}, bf16[2048,512]{1,0:T(8,128)(2,1)}, bf16[2048,1024]{1,0:T(8,128)(2,1)}, bf16[512,1280]{1,0:T(8,128)(2,1)S(1)}) custom-call(s32[3]{0:T(128)S(1)} %add_add_fusion.1.info, bf16[512,1280]{1,0:T(8,128)(2,1)S(1)} %collective-permute-done.2.refs_0_, ...), custom_call_target="tpu_custom_call", output_to_operand_aliasing={{0}: (8, {}), {1}: (9, {}), {2}: (10, {})} | custom-call | flops 10000000000 | bytes 1000 | tf_op jit(solution)/shard_map/project/pallas_call | solution.py:459
  86.4 7.6 %project.5 = (bf16[2048,1280]{1,0:T(8,128)(2,1)}, bf16[2048,512]{1,0:T(8,128)(2,1)}, bf16[2048,1024]{1,0:T(8,128)(2,1)}, bf16[512,1280]{1,0:T(8,128)(2,1)S(1)}) custom-call(s32[3]{0:T(128)S(1)} %add_add_fusion.info, bf16[512,1280]{1,0:T(8,128)(2,1)} %collective-permute-done.3.refs_0_, ...), custom_call_target="tpu_custom_call", output_to_operand_aliasing={{0}: (8, {}), {1}: (9, {}), {2}: (10, {})} | custom-call | flops 10000000000 | bytes 1000 | tf_op jit(solution)/shard_map/project/pallas_call | solution.py:459
  96.1 24.9 %attn_fwd.1 = (bf16[2048,320]{1,0:T(8,128)(2,1)S(1)}, f32[2048,512]{1,0:T(8,128)S(1)}, bf16[2048,512]{1,0:T(8,128)(2,1)S(1)}) custom-call(s32[16]{0:T(128)S(1)} %reshape.189.flags, bf16[2048,512]{1,0:T(8,128)(2,1)S(1)} %copy-done.14, bf16[2048,1024]{1,0:T(8,128)(2,1)} %get-tuple-element.90.kv.kk.vv, s32[2048,1]{1,0:T(8,128)S(1)} %copy.29.segc, ...), custom_call_target="tpu_custom_call" | custom-call | flops 10000000 | bytes 1000 | tf_op jit(solution)/shard_map/attn_fwd/pallas_call | solution.py:164
  128.0 10.1 %collective-permute-done.11.p2 = bf16[512,320]{1,0:T(8,128)(2,1)S(1)} collective-permute-done((bf16[512,320]{1,0:T(8,128)(2,1)S(1)}, bf16[512,320]{1,0:T(8,128)(2,1)S(1)}, u32[]{:S(2)}, u32[]{:S(2)}) %collective-permute-start.11) | collective-permute-done | bytes 327712 | tf_op jit(solution)/shard_map/ppermute | solution.py:849
  138.1 7.3 %collective-permute-done.12.p3 = bf16[512,320]{1,0:T(8,128)(2,1)S(1)} collective-permute-done((bf16[512,320]{1,0:T(8,128)(2,1)S(1)}, bf16[512,320]{1,0:T(8,128)(2,1)S(1)}, u32[]{:S(2)}, u32[]{:S(2)}) %collective-permute-start.12) | collective-permute-done | bytes 327712 | tf_op jit(solution)/shard_map/ppermute | solution.py:849
  146.2 22.2 %tail.1 = (bf16[512,1280]{1,0:T(8,128)(2,1)}, bf16[512,1280]{1,0:T(8,128)(2,1)}, bf16[512,1280]{1,0:T(8,128)(2,1)}, bf16[512,1280]{1,0:T(8,128)(2,1)}, bf16[512,...) custom-call(s32[4]{0:T(128)S(1)} %pad_add_fusion.at, ...), custom_call_target="tpu_custom_call" | custom-call | flops 10000000 | bytes 1000 | tf_op jit(solution)/shard_map/tail/pallas_call | solution.py:565
  176.9 4.4 share.1
  183.4 10.3 %collective-permute-done.16.do2 = bf16[512,320]{1,0:T(8,128)(2,1)S(1)} collective-permute-done((bf16[512,320]{1,0:T(8,128)(2,1)S(1)}, bf16[512,320]{1,0:T(8,128)(2,1)S(1)}, u32[]{:S(2)}, u32[]{:S(2)}) %collective-permute-start.16) | collective-permute-done | bytes 327712 | tf_op jit(solution)/shard_map/ppermute | solution.py:849
  194.5 6.1 %collective-permute-done.17.do3 = bf16[512,320]{1,0:T(8,128)(2,1)S(1)} collective-permute-done((bf16[512,320]{1,0:T(8,128)(2,1)S(1)}, bf16[512,320]{1,0:T(8,128)(2,1)S(1)}, u32[]{:S(2)}, u32[]{:S(2)}) %collective-permute-start.17) | collective-permute-done | bytes 327712 | tf_op jit(solution)/shard_map/ppermute | solution.py:849
  202.8 5.9 %keep.1 = bf16[1280,1920]{1,0:T(8,128)(2,1)S(1)} custom-call(s32[1]{0:T(128)} %bitcast.22.col, bf16[512,1280]{1,0:T(8,128)(2,1)S(1)} %copy-done.9, bf16[512,1280]{1,0:T(8,128)(2,1)S(1)} %copy-done.10, bf16[512,1280]{1,0:T(8,128)(2,1)S(1)} %copy-done.12, bf16[512,1280]{1,0:T(8,128)(2,1)S(1)} %copy-done.13, bf16[512,1280]{1,0:T(8,128)(2,1)S(1)} %copy-done.11, ...), custom_call_target="tpu_custom_call" | custom-call | flops 10000000 | bytes 1000 | tf_op jit(solution)/shard_map/keep/pallas_call | solution.py:633
  211.0 4.6 all-to-all-start
  221.5 24.4 %attn_bwd.2 = (bf16[2048,512]{1,0:T(8,128)(2,1)S(1)}, f32[8,128]{1,0:T(8,128)S(1)}) custom-call(s32[16]{0:T(128)S(1)} %reshape.189.flags, s32[1]{0:T(128)} %bitcast.mine, bf16[2048,512]{1,0:T(8,128)(2,1)} %copy-done.8, bf16[2048,1024]{1,0:T(8,128)(2,1)} %get-tuple-element.90.kv.kk.vv, bf16[2048,1024]{1,0:T(8,128)(2,1)} %get-tuple-element.90.kv.kk.vv, ...), custom_call_target="tpu_custom_call" | custom-call | flops 10000000 | bytes 1000 | tf_op jit(solution)/shard_map/attn_bwd/pallas_call | solution.py:300
  245.9 4.3 cross.2
  253.8 25.2 %attn_bwd.3 = (bf16[2048,512]{1,0:T(8,128)(2,1)S(1)}, f32[8,128]{1,0:T(8,128)S(1)}) custom-call(s32[16]{0:T(128)S(1)} %reshape.189.flags, s32[1]{0:T(128)} %bitcast.mine, bf16[2048,512]{1,0:T(8,128)(2,1)} %copy-done.8, bf16[2048,1024]{1,0:T(8,128)(2,1)} %get-tuple-element.90.kv.kk.vv, bf16[2048,1024]{1,0:T(8,128)(2,1)} %get-tuple-element.90.kv.kk.vv, ...), custom_call_target="tpu_custom_call" | custom-call | flops 10000000 | bytes 1000 | tf_op jit(solution)/shard_map/attn_bwd/pallas_call | solution.py:300
  279.0 6.4 %collective-permute-done.19 = bf16[320,512]{1,0:T(8,128)(2,1)S(1)} collective-permute-done((bf16[320,512]{1,0:T(8,128)(2,1)S(1)}, bf16[320,512]{1,0:T(8,128)(2,1)S(1)}, u32[]{:S(2)}, u32[]{:S(2)}) %collective-permute-start.19) | collective-permute-done | bytes 327712 | tf_op jit(solution)/shard_map/ppermute | solution.py:849
  285.4 9.5 %collective-permute-done.21 = bf16[320,512]{1,0:T(8,128)(2,1)S(1)} collective-permute-done((bf16[320,512]{1,0:T(8,128)(2,1)S(1)}, bf16[320,512]{1,0:T(8,128)(2,1)S(1)}, u32[]{:S(2)}, u32[]{:S(2)}) %collective-permute-start.21) | collective-permute-done | bytes 327712 | tf_op jit(solution)/shard_map/ppermute | solution.py:849
  296.4 5.1 %cross.3 = (bf16[320,512]{1,0:T(8,128)(2,1)S(1)}, bf16[320,512]{1,0:T(8,128)(2,1)}, bf16[320,512]{1,0:T(8,128)(2,1)}, bf16[320,512]{1,0:T(8,128)(2,1)S(1)}) custom-call(s32[2]{0:T(128)S(1)} %copy-done.28, bf16[2048,1280]{1,0:T(8,128)(2,1)S(1)} %bitcast.90, bf16[2048,512]{1,0:T(8,128)(2,1)S(1)} %get-tuple-element.136.g_ref), custom_call_target="tpu_custom_call" | custom-call | flops 100000000 | bytes 1000 | tf_op jit(solution)/shard_map/cross/pallas_call | solution.py:738
  323.3 32.0 %collective-permute-done.37 = bf16[160,1920]{1,0:T(8,128)(2,1)S(1)} collective-permute-done((bf16[160,1920]{1,0:T(8,128)(2,1)S(1)}, bf16[160,1920]{1,0:T(8,128)(2,1)S(1)}, u32[]{:S(2)}, u32[]{:S(2)}) %collective-permute-start.37) | collective-permute-done | bytes 614432 | tf_op jit(solution)/shard_map/ppermute | solution.py:849
  362.1 13.0 %collective-permute-done.38 = bf16[1,160,1920]{2,1,0:T(8,128)(2,1)S(1)} collective-permute-done((bf16[1,160,1920]{2,1,0:T(8,128)(2,1)S(1)}, bf16[1,160,1920]{2,1,0:T(8,128)(2,1)S(1)}, u32[]{:S(2)}, u32[]{:S(2)}) %collective-permute-start.38) | collective-permute-done | bytes 614432 | tf_op jit(solution)/shard_map/ppermute | solution.py:849
  384.3 4.9 collective-permute-done.34
  392.2 27.0 %collective-permute-done.31 = bf16[2,320,512]{2,1,0:T(8,128)(2,1)S(1)} collective-permute-done((bf16[2,320,512]{2,1,0:T(8,128)(2,1)S(1)}, bf16[2,320,512]{2,1,0:T(8,128)(2,1)S(1)}, u32[]{:S(2)}, u32[]{:S(2)}) %collective-permute-start.31) | collective-permute-done | bytes 655392 | tf_op jit(solution)/shard_map/ppermute | solution.py:849
  420.4 12.1 %collective-permute-done.35 = bf16[2,320,512]{2,1,0:T(8,128)(2,1)S(1)} collective-permute-done((bf16[2,320,512]{2,1,0:T(8,128)(2,1)S(1)}, bf16[2,320,512]{2,1,0:T(8,128)(2,1)S(1)}, u32[]{:S(2)}, u32[]{:S(2)}) %collective-permute-start.35) | collective-permute-done | bytes 655392 | tf_op jit(solution)/shard_map/ppermute | solution.py:849
  449.0 22.6 %collective-permute-done.43 = f32[21,128]{1,0:T(8,128)S(1)} collective-permute-done((f32[21,128]{1,0:T(8,128)S(1)}, f32[21,128]{1,0:T(8,128)S(1)}, u32[]{:S(2)}, u32[]{:S(2)}) %collective-permute-start.43) | collective-permute-done | bytes 10784 | tf_op jit(solution)/shard_map/ppermute | solution.py:849
  476.0 7.7 %spread.1 = f32[2,320,3840]{2,1,0:T(8,128)} custom-call(s32[3]{0:T(128)S(1)} %pad_add_fusion.3.at, bf16[4,320,512]{2,1,0:T(8,128)(2,1)} %pad_maximum_fusion.3.refs_0_, bf16[4,320,512]{2,1,0:T(8,128)(2,1)} %collective-permute-done.32.refs_1_, bf16[4,320,512]{2,1,0:T(8,128)(2,1)} %pad_maximum_fusion.4.refs_2_, bf16[4,320,512]{2,1,0:T(8,128)(2,1)} %collective-permute-done.36.refs_3_), custom_call_target="tpu_custom_call" | custom-call | flops 100000000 | bytes 1000 | tf_op jit(solution)/shard_map/spread/pallas_call | solution.py:786
  484.8 6.2 %place_tail.1 = (f32[4,160,1280]{2,1,0:T(8,128)}, f32[4,160,1280]{2,1,0:T(8,128)}, f32[4,160,1280]{2,1,0:T(8,128)}) custom-call(s32[3]{0:T(128)S(1)} %pad_add_fusion.3.at, bf16[4,160,1920]{2,1,0:T(8,128)(2,1)S(1)} %pad_maximum_fusion.2.own_ref, bf16[4,160,1920]{2,1,0:T(8,128)(2,1)} %collective-permute-done.40.mate_ref), custom_call_target="tpu_custom_call" | custom-call | flops 100000000 | bytes 1000 | tf_op jit(solution)/shard_map/place_tail/pallas_call | solution.py:704
  (250 shorter events, 127.6 us)
Async XLA Ops:
  5.3 20.6 %collective-permute-start.1 = (bf16[512,1280]{1,0:T(8,128)(2,1)S(1)}, bf16[512,1280]{1,0:T(8,128)(2,1)}, u32[]{:S(2)}, u32[]{:S(2)}) collective-permute-start(bf16[512,1280]{1,0:T(8,128)(2,1)S(1)} %bitcast.92), channel_id=1, source_target_pairs={{2,0},{3,1},{4,2},{5,3},{6,4},{7,5},{8,10},{9,11},{10,12},{11,13},... | collective-permute-start | bytes 3932168 | tf_op jit(solution)/shard_map/ppermute | solution.py:849
  6.6 44.1 %collective-permute-start.6 = (bf16[640,1024]{1,0:T(8,128)(2,1)}, bf16[640,1024]{1,0:T(8,128)(2,1)}, u32[]{:S(2)}, u32[]{:S(2)}) collective-permute-start(bf16[640,1024]{1,0:T(8,128)(2,1)} %pick.1.a_ref), channel_id=1, source_target_pairs={{0,1},{1,0},{2,3},{3,2},{4,5},{5,4},{6,7},{7,6},{8,9},{9,8},{10,11... | collective-permute-start | bytes 3932168 | tf_op jit(solution)/shard_map/ppermute | solution.py:849
  9.6 51.1 %collective-permute-start.4 = (bf16[512,1280]{1,0:T(8,128)(2,1)S(1)}, bf16[512,1280]{1,0:T(8,128)(2,1)}, u32[]{:S(2)}, u32[]{:S(2)}) collective-permute-start(bf16[512,1280]{1,0:T(8,128)(2,1)S(1)} %bitcast.93), channel_id=1, source_target_pairs={{0,8},{1,9},{2,10},{3,11},{12,4},{13,5},{14,6},{15,7},{16,24},{17,... | collective-permute-start | bytes 3932168 | tf_op jit(solution)/shard_map/ppermute | solution.py:849
  25.9 19.7 %collective-permute-start.2 = (bf16[512,1280]{1,0:T(8,128)(2,1)}, bf16[512,1280]{1,0:T(8,128)(2,1)S(1)}, u32[]{:S(2)}, u32[]{:S(2)}) collective-permute-start(bf16[512,1280]{1,0:T(8,128)(2,1)} %collective-permute-done.1.refs_2_), channel_id=1, source_target_pairs={{2,0},{3,1},{4,2},{5,3},{10,12},{11,13},{12,14},{13,15},{18,16},{1... | collective-permute-start | bytes 3932168 | tf_op jit(solution)/shard_map/ppermute | solution.py:849
  30.4 30.3 %collective-permute-start.5 = (bf16[512,1280]{1,0:T(8,128)(2,1)}, bf16[512,1280]{1,0:T(8,128)(2,1)}, u32[]{:S(2)}, u32[]{:S(2)}) collective-permute-start(bf16[512,1280]{1,0:T(8,128)(2,1)} %collective-permute-done.1.refs_2_), channel_id=1, source_target_pairs={{0,8},{1,9},{2,10},{3,11},{12,4},{13,5},{14,6},{15,7},{16,24},{17,... | collective-permute-start | bytes 3932168 | tf_op jit(solution)/shard_map/ppermute | solution.py:849
  46.8 25.6 %collective-permute-start.3 = (bf16[512,1280]{1,0:T(8,128)(2,1)}, bf16[512,1280]{1,0:T(8,128)(2,1)}, u32[]{:S(2)}, u32[]{:S(2)}) collective-permute-start(bf16[512,1280]{1,0:T(8,128)(2,1)} %broadcast_select_fusion), channel_id=1, source_target_pairs={{0,2},{1,3},{2,0},{3,1},{12,14},{13,15},{14,12},{15,13},{16,18},{1... | collective-permute-start | bytes 3932168 | tf_op jit(solution)/shard_map/ppermute | solution.py:849
  58.4 18.6 %collective-permute-start.8 = (bf16[512,1280]{1,0:T(8,128)(2,1)S(1)}, bf16[512,1280]{1,0:T(8,128)(2,1)}, u32[]{:S(2)}, u32[]{:S(2)}) collective-permute-start(bf16[512,1280]{1,0:T(8,128)(2,1)S(1)} %collective-permute-done.2.refs_0_), channel_id=1, source_target_pairs={{0,8},{1,9},{2,10},{3,11},{12,4},{13,5},{14,6},{15,7},{16,24},{17,... | collective-permute-start | bytes 3932168 | tf_op jit(solution)/shard_map/ppermute | solution.py:849
  75.4 48.8 %collective-permute-start.13 = (bf16[3,320,1280]{2,1,0:T(8,128)(2,1)}, bf16[3,320,1280]{2,1,0:T(8,128)(2,1)}, u32[]{:S(2)}, u32[]{:S(2)}) collective-permute-start(bf16[3,320,1280]{2,1,0:T(8,128)(2,1)} %constant_dynamic-slice_fusion), channel_id=1, source_target_pairs={{0,1},{1,0},{2,3},{3,2},{4,5},{5,4},{6,7},{7,6},{8,9},{9,8},{10,11... | collective-permute-start | bytes 7372808 | tf_op jit(solution)/shard_map/ppermute | solution.py:849
  77.0 44.1 %collective-permute-start.9 = (bf16[512,1280]{1,0:T(8,128)(2,1)}, bf16[512,1280]{1,0:T(8,128)(2,1)S(1)}, u32[]{:S(2)}, u32[]{:S(2)}) collective-permute-start(bf16[512,1280]{1,0:T(8,128)(2,1)} %bitcast.113), channel_id=1, source_target_pairs={{2,8},{3,9},{4,2},{5,3},{6,10},{7,11},{8,4},{9,5},{10,12},{11,13},... | collective-permute-start | bytes 3932168 | tf_op jit(solution)/shard_map/ppermute | solution.py:849
  126.0 19.4 %collective-permute-start.14 = (bf16[3,320,1280]{2,1,0:T(8,128)(2,1)}, bf16[3,320,1280]{2,1,0:T(8,128)(2,1)}, u32[]{:S(2)}, u32[]{:S(2)}) collective-permute-start(bf16[3,320,1280]{2,1,0:T(8,128)(2,1)} %collective-permute-done.13.half), channel_id=1, source_target_pairs={{0,8},{1,9},{2,10},{3,11},{4,12},{5,13},{6,14},{7,15},{8,0},{9,1},... | collective-permute-start | bytes 7372808 | tf_op jit(solution)/shard_map/ppermute | solution.py:849
  181.3 19.2 %collective-permute-start.18 = (bf16[1280,1920]{1,0:T(8,128)(2,1)S(1)}, bf16[1280,1920]{1,0:T(8,128)(2,1)S(1)}, u32[]{:S(2)}, u32[]{:S(2)}) collective-permute-start(bf16[1280,1920]{1,0:T(8,128)(2,1)S(1)} %share.1), channel_id=1, source_target_pairs={{0,8},{1,9},{2,10},{3,11},{4,12},{5,13},{6,14},{7,15},{8,0},{9,1},... | collective-permute-start | bytes 14745608 | tf_op jit(solution)/shard_map/ppermute | solution.py:849
  211.0 97.3 %all-to-all-start = ((bf16[8,160,1920]{2,1,0:T(8,128)(2,1)}), bf16[8,160,1920]{2,1,0:T(8,128)(2,1)}, u32[]{:S(2)}, u32[]{:S(2)}) async-start(bf16[8,160,1920]{2,1,0:T(8,128)(2,1)} %bitcast.91), calls=%async_computation | async-start | bytes 9830400 | tf_op jit(solution)/shard_map/all_to_all | solution.py:1019
  215.6 90.1 %collective-permute-start.22 = (bf16[512,1280]{1,0:T(8,128)(2,1)}, bf16[512,1280]{1,0:T(8,128)(2,1)}, u32[]{:S(2)}, u32[]{:S(2)}) collective-permute-start(bf16[512,1280]{1,0:T(8,128)(2,1)} %get-tuple-element.124), channel_id=1, source_target_pairs={{2,4},{3,5},{4,8},{5,9},{6,12},{7,13},{8,2},{9,3},{10,6},{11,7},{1... | collective-permute-start | bytes 3932168 | tf_op jit(solution)/shard_map/ppermute | solution.py:849
  250.2 35.2 %collective-permute-start.19 = (bf16[320,512]{1,0:T(8,128)(2,1)S(1)}, bf16[320,512]{1,0:T(8,128)(2,1)S(1)}, u32[]{:S(2)}, u32[]{:S(2)}) collective-permute-start(bf16[320,512]{1,0:T(8,128)(2,1)S(1)} %get-tuple-element.118), channel_id=1, source_target_pairs={{0,16},{1,17},{2,18},{3,19},{4,20},{5,21},{6,22},{7,23},{8,24},{9,... | collective-permute-start | bytes 983048 | tf_op jit(solution)/shard_map/ppermute | solution.py:849
  251.8 33.6 %collective-permute-start.20 = (bf16[320,512]{1,0:T(8,128)(2,1)S(1)}, bf16[320,512]{1,0:T(8,128)(2,1)S(1)}, u32[]{:S(2)}, u32[]{:S(2)}) collective-permute-start(bf16[320,512]{1,0:T(8,128)(2,1)S(1)} %get-tuple-element.119), channel_id=1, source_target_pairs={{0,1},{1,0},{2,3},{3,2},{4,5},{5,4},{6,7},{7,6},{8,9},{9,8},{10,11... | collective-permute-start | bytes 983048 | tf_op jit(solution)/shard_map/ppermute | solution.py:849
  253.6 41.2 %collective-permute-start.21 = (bf16[320,512]{1,0:T(8,128)(2,1)S(1)}, bf16[320,512]{1,0:T(8,128)(2,1)S(1)}, u32[]{:S(2)}, u32[]{:S(2)}) collective-permute-start(bf16[320,512]{1,0:T(8,128)(2,1)S(1)} %get-tuple-element.120), channel_id=1, source_target_pairs={{0,17},{1,16},{2,19},{3,18},{4,21},{5,20},{6,23},{7,22},{8,25},{9,... | collective-permute-start | bytes 983048 | tf_op jit(solution)/shard_map/ppermute | solution.py:849
  295.2 21.2 %collective-permute-start.23 = (bf16[320,512]{1,0:T(8,128)(2,1)S(1)}, bf16[320,512]{1,0:T(8,128)(2,1)}, u32[]{:S(2)}, u32[]{:S(2)}) collective-permute-start(bf16[320,512]{1,0:T(8,128)(2,1)S(1)} %total.3), channel_id=1, source_target_pairs={{0,4},{1,5},{2,6},{3,7},{4,0},{5,1},{6,2},{7,3},{8,12},{9,13},{10,... | collective-permute-start | bytes 983048 | tf_op jit(solution)/shard_map/ppermute | solution.py:849
  316.3 61.1 %collective-permute-start.27 = (bf16[2,512,1280]{2,1,0:T(8,128)(2,1)S(1)}, bf16[2,512,1280]{2,1,0:T(8,128)(2,1)S(1)}, u32[]{:S(2)}, u32[]{:S(2)}) collective-permute-start(bf16[2,512,1280]{2,1,0:T(8,128)(2,1)S(1)} %pad_maximum_fusion.1), channel_id=1, source_target_pairs={{0,8},{1,9},{2,10},{3,11},{4,12},{5,13},{6,14},{7,15},{8,0},{9,1},... | collective-permute-start | bytes 7864328 | tf_op jit(solution)/shard_map/ppermute | solution.py:849
  317.4 37.8 %collective-permute-start.37 = (bf16[160,1920]{1,0:T(8,128)(2,1)S(1)}, bf16[160,1920]{1,0:T(8,128)(2,1)S(1)}, u32[]{:S(2)}, u32[]{:S(2)}) collective-permute-start(bf16[160,1920]{1,0:T(8,128)(2,1)S(1)} %total.5), channel_id=1, source_target_pairs={{0,4},{1,5},{2,6},{3,7},{4,0},{5,1},{6,2},{7,3},{8,12},{9,13},{10,... | collective-permute-start | bytes 1843208 | tf_op jit(solution)/shard_map/ppermute | solution.py:849
  322.3 39.7 %collective-permute-start.33 = (bf16[320,512]{1,0:T(8,128)(2,1)S(1)}, bf16[320,512]{1,0:T(8,128)(2,1)S(1)}, u32[]{:S(2)}, u32[]{:S(2)}) collective-permute-start(bf16[320,512]{1,0:T(8,128)(2,1)S(1)} %total.4), channel_id=1, source_target_pairs={{0,4},{1,5},{2,6},{3,7},{4,0},{5,1},{6,2},{7,3},{8,12},{9,13},{10,... | collective-permute-start | bytes 983048 | tf_op jit(solution)/shard_map/ppermute | solution.py:849
  355.4 19.7 %collective-permute-start.38 = (bf16[1,160,1920]{2,1,0:T(8,128)(2,1)S(1)}, bf16[1,160,1920]{2,1,0:T(8,128)(2,1)S(1)}, u32[]{:S(2)}, u32[]{:S(2)}) collective-permute-start(bf16[1,160,1920]{2,1,0:T(8,128)(2,1)S(1)} %fusion.16), channel_id=1, source_target_pairs={{0,2},{1,3},{2,0},{3,1},{4,6},{5,7},{6,4},{7,5},{8,10},{9,11},{10,... | collective-permute-start | bytes 1843208 | tf_op jit(solution)/shard_map/ppermute | solution.py:849
  355.8 26.3 %collective-permute-start.30 = (bf16[1,320,512]{2,1,0:T(8,128)(2,1)S(1)}, bf16[1,320,512]{2,1,0:T(8,128)(2,1)S(1)}, u32[]{:S(2)}, u32[]{:S(2)}) collective-permute-start(bf16[1,320,512]{2,1,0:T(8,128)(2,1)S(1)} %fusion.29), channel_id=1, source_target_pairs={{0,2},{1,3},{2,0},{3,1},{4,6},{5,7},{6,4},{7,5},{8,10},{9,11},{10,... | collective-permute-start | bytes 983048 | tf_op jit(solution)/shard_map/ppermute | solution.py:849
  362.1 27.1 %collective-permute-start.34 = (bf16[1,320,512]{2,1,0:T(8,128)(2,1)S(1)}, bf16[1,320,512]{2,1,0:T(8,128)(2,1)S(1)}, u32[]{:S(2)}, u32[]{:S(2)}) collective-permute-start(bf16[1,320,512]{2,1,0:T(8,128)(2,1)S(1)} %fusion.30), channel_id=1, source_target_pairs={{0,2},{1,3},{2,0},{3,1},{4,6},{5,7},{6,4},{7,5},{8,10},{9,11},{10,... | collective-permute-start | bytes 983048 | tf_op jit(solution)/shard_map/ppermute | solution.py:849
  375.3 58.5 %collective-permute-start.39 = (bf16[2,160,1920]{2,1,0:T(8,128)(2,1)S(1)}, bf16[2,160,1920]{2,1,0:T(8,128)(2,1)S(1)}, u32[]{:S(2)}, u32[]{:S(2)}) collective-permute-start(bf16[2,160,1920]{2,1,0:T(8,128)(2,1)S(1)} %pad_maximum_fusion.5), channel_id=1, source_target_pairs={{0,16},{1,17},{2,18},{3,19},{4,20},{5,21},{6,22},{7,23},{8,24},{9,... | collective-permute-start | bytes 3686408 | tf_op jit(solution)/shard_map/ppermute | solution.py:849
  378.7 55.9 %collective-permute-start.28 = (bf16[512,1280]{1,0:T(8,128)(2,1)S(1)}, bf16[512,1280]{1,0:T(8,128)(2,1)S(1)}, u32[]{:S(2)}, u32[]{:S(2)}) collective-permute-start(bf16[512,1280]{1,0:T(8,128)(2,1)S(1)} %fusion.3), channel_id=1, source_target_pairs={{0,2},{1,3},{2,0},{3,1},{4,6},{5,7},{6,4},{7,5},{8,10},{9,11},{10,... | collective-permute-start | bytes 3932168 | tf_op jit(solution)/shard_map/ppermute | solution.py:849
  382.2 37.0 %collective-permute-start.31 = (bf16[2,320,512]{2,1,0:T(8,128)(2,1)S(1)}, bf16[2,320,512]{2,1,0:T(8,128)(2,1)S(1)}, u32[]{:S(2)}, u32[]{:S(2)}) collective-permute-start(bf16[2,320,512]{2,1,0:T(8,128)(2,1)S(1)} %pad_maximum_fusion.6), channel_id=1, source_target_pairs={{0,16},{1,17},{2,18},{3,19},{4,20},{5,21},{6,22},{7,23},{8,24},{9,... | collective-permute-start | bytes 1966088 | tf_op jit(solution)/shard_map/ppermute | solution.py:849
  389.2 43.3 %collective-permute-start.35 = (bf16[2,320,512]{2,1,0:T(8,128)(2,1)S(1)}, bf16[2,320,512]{2,1,0:T(8,128)(2,1)S(1)}, u32[]{:S(2)}, u32[]{:S(2)}) collective-permute-start(bf16[2,320,512]{2,1,0:T(8,128)(2,1)S(1)} %pad_maximum_fusion.7), channel_id=1, source_target_pairs={{0,16},{1,17},{2,18},{3,19},{4,20},{5,21},{6,22},{7,23},{8,24},{9,... | collective-permute-start | bytes 1966088 | tf_op jit(solution)/shard_map/ppermute | solution.py:849
  420.4 55.6 %collective-permute-start.32 = (bf16[4,320,512]{2,1,0:T(8,128)(2,1)}, bf16[4,320,512]{2,1,0:T(8,128)(2,1)}, u32[]{:S(2)}, u32[]{:S(2)}) collective-permute-start(bf16[4,320,512]{2,1,0:T(8,128)(2,1)} %pad_maximum_fusion.3.refs_0_), channel_id=1, source_target_pairs={{0,8},{1,9},{2,10},{3,11},{4,12},{5,13},{6,14},{7,15},{8,0},{9,1},... | collective-permute-start | bytes 3932168 | tf_op jit(solution)/shard_map/ppermute | solution.py:849
  433.8 42.3 %collective-permute-start.36 = (bf16[4,320,512]{2,1,0:T(8,128)(2,1)}, bf16[4,320,512]{2,1,0:T(8,128)(2,1)}, u32[]{:S(2)}, u32[]{:S(2)}) collective-permute-start(bf16[4,320,512]{2,1,0:T(8,128)(2,1)} %pad_maximum_fusion.4.refs_2_), channel_id=1, source_target_pairs={{0,8},{1,9},{2,10},{3,11},{4,12},{5,13},{6,14},{7,15},{8,0},{9,1},... | collective-permute-start | bytes 3932168 | tf_op jit(solution)/shard_map/ppermute | solution.py:849
  434.1 50.8 %collective-permute-start.40 = (bf16[4,160,1920]{2,1,0:T(8,128)(2,1)S(1)}, bf16[4,160,1920]{2,1,0:T(8,128)(2,1)}, u32[]{:S(2)}, u32[]{:S(2)}) collective-permute-start(bf16[4,160,1920]{2,1,0:T(8,128)(2,1)S(1)} %pad_maximum_fusion.2.own_ref), channel_id=1, source_target_pairs={{0,8},{1,9},{2,10},{3,11},{4,12},{5,13},{6,14},{7,15},{8,0},{9,1},... | collective-permute-start | bytes 7372808 | tf_op jit(solution)/shard_map/ppermute | solution.py:849
  439.3 51.7 %collective-permute-start.29 = (bf16[512,1280]{1,0:T(8,128)(2,1)}, bf16[512,1280]{1,0:T(8,128)(2,1)}, u32[]{:S(2)}, u32[]{:S(2)}) collective-permute-start(bf16[512,1280]{1,0:T(8,128)(2,1)} %fusion.12), channel_id=1, source_target_pairs={{2,4},{3,5},{4,8},{5,9},{6,12},{7,13},{8,2},{9,3},{10,6},{11,7},{1... | collective-permute-start | bytes 3932168 | tf_op jit(solution)/shard_map/ppermute | solution.py:849
  446.2 25.4 %collective-permute-start.43 = (f32[21,128]{1,0:T(8,128)S(1)}, f32[21,128]{1,0:T(8,128)S(1)}, u32[]{:S(2)}, u32[]{:S(2)}) collective-permute-start(f32[21,128]{1,0:T(8,128)S(1)} %fusion.51), channel_id=1, source_target_pairs={{0,4},{1,5},{2,6},{3,7},{4,0},{5,1},{6,2},{7,3},{8,12},{9,13},{10,... | collective-permute-start | bytes 32264 | tf_op jit(solution)/shard_map/ppermute | solution.py:849
  (65 other events, 687.2 us)

commit v5 on v4

--- a/solution.py
+++ b/solution.py
@@ -25,6 +25,10 @@
 f32 = jnp.float32
 bf16 = jnp.bfloat16
 AXES = ("gx", "gc", "far", "near", "wt")
+
+
+def hbm(x):
+    return pltpu.with_memory_space_constraint(x, pltpu.HBM)
 
 
 def block_flags(seg_row, bq, bk):
@@ -164,43 +168,27 @@
     return pl.pallas_call(
         functools.partial(fwd_kernel, nh=nh, bq=bq, bk=bk, nk=n // bk),
         out_shape=[
-            jax.ShapeDtypeStruct((n, nh * HD), bf16),
-            jax.ShapeDtypeStruct((n, w), f32),
-            jax.ShapeDtypeStruct((n, w), bf16),
+            pltpu.HBM((n, nh * HD), bf16),
+            pltpu.HBM((n, w), f32),
+            pltpu.HBM((n, w), bf16),
         ],
         grid_spec=spec,
         compiler_params=pltpu.CompilerParams(vmem_limit_bytes=40 << 20),
         cost_estimate=cost(0.01),
         name="attn_fwd",
-    )(block_flags(seg_row, bq, bk), q, kv, seg_row[:, None], seg_row[None])
+    )(block_flags(seg_row, bq, bk), hbm(q), hbm(kv), seg_row[:, None], seg_row[None])
 
 
 def bwd_kernel(
-    flags, mine, qa, kk, vv, do0, do1, do2, do3, of, segc, segr, scale, dqkv, gscale, doa_s, dq_s, dk_s, dv_s, *, first, nh, bq, bk, n
+    flags, qa, kk, vv, doa_s, segc, segr, scale, dqkv, gscale, dq_s, dk_s, dv_s, *, nh, bq, bk, n
 ):
     nk = n // bk
     nq = n // bq
     kb = pl.program_id(0)
-    part = n // 4
-    step_rows = 256 if part % 256 == 0 else part
-    lanes = lax.broadcasted_iota(jnp.int32, (step_rows, LN), 1)
 
     @pl.when(kb == 0)
     def _():
         dq_s[...] = jnp.zeros_like(dq_s)
-        for j, piece in enumerate((do0, do1, do2, do3)):
-            start = (mine[0] ^ j) * part
-            for i in range(part // step_rows):
-                d = piece[i * step_rows : (i + 1) * step_rows, :].astype(f32)
-                r = pl.ds(pl.multiple_of(start + i * step_rows, step_rows), step_rows)
-                for h in range(nh):
-                    at = (first + h) * HD
-                    dh = jnp.concatenate(
-                        [d[:, at : at + HD], jnp.zeros((step_rows, LN - HD), f32)], axis=1
-                    )
-                    c = slice(h * LN, (h + 1) * LN)
-                    delta = jnp.sum(dh * of[r, c], axis=1, keepdims=True)
-                    doa_s[r, c] = put_split(dh, -delta, lanes)
 
     dk_s[...] = jnp.zeros_like(dk_s)
     dv_s[...] = jnp.zeros_like(dv_s)
@@ -266,48 +254,87 @@
         gscale[...] = jnp.broadcast_to(total, gscale.shape)
 
 
-def attn_bwd(qa, kv, pieces, of, seg_row, mine, scale, heads, group, groups, bq=512, bk=512):
+def prep_kernel(mine, do0, do1, do2, do3, of, out, *, nh):
+    tile = of.shape[0]
+    lanes = lax.broadcasted_iota(jnp.int32, (tile, LN), 1)
+    for j, piece in enumerate((do0, do1, do2, do3)):
+
+        @pl.when(pl.program_id(0) == j)
+        def _(piece=piece):
+            d = piece[...].astype(f32)
+            for h in range(nh):
+                dh = jnp.concatenate(
+                    [d[:, h * HD : (h + 1) * HD], jnp.zeros((tile, LN - HD), f32)], axis=1
+                )
+                c = slice(h * LN, (h + 1) * LN)
+                delta = jnp.sum(dh * of[:, c], axis=1, keepdims=True)
+                out[:, c] = put_split(dh, -delta, lanes)
+
+
+def prep(pieces, of, mine, nh, tile=256):
+    n, w = of.shape
+    per = n // 4 // tile
+    at = lambda j, i, m: ((m[0] ^ j) * per + i, 0)
+    return pl.pallas_call(
+        functools.partial(prep_kernel, nh=nh),
+        out_shape=pltpu.HBM((n, w), bf16),
+        grid_spec=pltpu.PrefetchScalarGridSpec(
+            num_scalar_prefetch=1,
+            grid=(4, per),
+            in_specs=[
+                pl.BlockSpec(
+                    (tile, nh * HD),
+                    lambda j, i, m, k=k: (jnp.where(j == k, i, jnp.where(j > k, per - 1, 0)), 0),
+                )
+                for k in range(4)
+            ]
+            + [pl.BlockSpec((tile, w), at)],
+            out_specs=pl.BlockSpec((tile, w), at),
+        ),
+        compiler_params=pltpu.CompilerParams(vmem_limit_bytes=24 << 20),
+        cost_estimate=cost(1000),
+        name="prep",
+    )(mine.reshape(1), *pieces, hbm(of))
+
+
+def attn_bwd(qa, kv, doa, seg_row, scale, heads, group, groups, bq=512, bk=512):
     n = qa.shape[0]
     nh = heads // groups
     w = nh * LN
     once = pl.Buffered(1)
     spec = pltpu.PrefetchScalarGridSpec(
-        num_scalar_prefetch=2,
+        num_scalar_prefetch=1,
         grid=(n // bk,),
         in_specs=[
-            pl.BlockSpec((n, w), lambda i, f, m: (0, group), pipeline_mode=once),
-            pl.BlockSpec((bk, w), lambda i, f, m: (i, group)),
-            pl.BlockSpec((bk, w), lambda i, f, m: (i, groups + group)),
-        ]
-        + [pl.BlockSpec((n // 4, heads * HD), lambda i, f, m: (0, 0), pipeline_mode=once)] * 4
-        + [
-            pl.BlockSpec((n, w), lambda i, f, m: (0, group), pipeline_mode=once),
-            pl.BlockSpec((bk, 1), lambda i, f, m: (i, 0)),
-            pl.BlockSpec((1, n), lambda i, f, m: (0, 0)),
-            pl.BlockSpec((1, nh * HD), lambda i, f, m: (0, 0)),
+            pl.BlockSpec((n, w), lambda i, f: (0, group), pipeline_mode=once),
+            pl.BlockSpec((bk, w), lambda i, f: (i, group)),
+            pl.BlockSpec((bk, w), lambda i, f: (i, groups + group)),
+            pl.BlockSpec((n, w), lambda i, f: (0, group), pipeline_mode=once),
+            pl.BlockSpec((bk, 1), lambda i, f: (i, 0)),
+            pl.BlockSpec((1, n), lambda i, f: (0, 0)),
+            pl.BlockSpec((1, nh * HD), lambda i, f: (0, 0)),
         ],
         out_specs=[
-            pl.BlockSpec((n, lanes_up(3 * nh * HD)), lambda i, f, m: (0, 0)),
-            pl.BlockSpec((8, LN), lambda i, f, m: (0, 0)),
+            pl.BlockSpec((n, lanes_up(3 * nh * HD)), lambda i, f: (0, 0)),
+            pl.BlockSpec((8, LN), lambda i, f: (0, 0)),
         ],
         scratch_shapes=[
-            pltpu.VMEM((n, w), bf16),
             pltpu.VMEM((nh, n, LN), f32),
             pltpu.VMEM((nh, bk, LN), f32),
             pltpu.VMEM((nh, bk, LN), f32),
         ],
     )
     return pl.pallas_call(
-        functools.partial(bwd_kernel, first=group * nh, nh=nh, bq=bq, bk=bk, n=n),
+        functools.partial(bwd_kernel, nh=nh, bq=bq, bk=bk, n=n),
         out_shape=[
-            jax.ShapeDtypeStruct((n, lanes_up(3 * nh * HD)), bf16),
-            jax.ShapeDtypeStruct((8, LN), f32),
+            pltpu.HBM((n, lanes_up(3 * nh * HD)), bf16),
+            pltpu.HBM((8, LN), f32),
         ],
         grid_spec=spec,
         compiler_params=pltpu.CompilerParams(vmem_limit_bytes=48 << 20),
         cost_estimate=cost(0.01),
         name="attn_bwd",
-    )(block_flags(seg_row, bq, bk), mine.reshape(1), qa, kv, kv, *pieces, of, seg_row[:, None], seg_row[None], scale)
+    )(block_flags(seg_row, bq, bk), hbm(qa), hbm(kv), hbm(kv), hbm(doa), seg_row[:, None], seg_row[None], scale)
 
 
 def quarter_columns(place, parts, groups, nh):
@@ -337,7 +364,7 @@
     step = 160 if rows % 160 == 0 else rows
     return pl.pallas_call(
         functools.partial(pick_kernel, parts=parts, groups=groups, nh=nh),
-        out_shape=jax.ShapeDtypeStruct((rows, lanes_up(3 * nh * HD)), w.dtype),
+        out_shape=pltpu.HBM((rows, lanes_up(3 * nh * HD)), w.dtype),
         grid_spec=pltpu.PrefetchScalarGridSpec(
             num_scalar_prefetch=1,
             grid=(rows // step,),
@@ -346,26 +373,42 @@
         ),
         cost_estimate=cost(5),
         name="pick",
-    )(mine.reshape(1), w)
-
-
-def widen_kernel(own_first, a_ref, b_ref, *outs, groups, nh):
-    flats, wide = outs[:-1], outs[-1]
-
+    )(mine.reshape(1), hbm(w))
+
+
+def stretch_kernel(x_ref, out, *, groups, nh):
+    value = x_ref[...]
+    each = 3 * nh * HD // groups
+    zero = jnp.zeros((value.shape[0], LN - HD), value.dtype)
+    per = nh // groups
+    wide = []
+    for t in range(3):
+        for h in range(nh):
+            at = (h // per) * each + t * per * HD + (h % per) * HD
+            wide += [value[:, at : at + HD], zero]
+    out[...] = jnp.concatenate(wide, axis=1)
+
+
+def stretch(x, groups, nh, us):
+    rows, width = x.shape
+    step = 160
+    return pl.pallas_call(
+        functools.partial(stretch_kernel, groups=groups, nh=nh),
+        out_shape=pltpu.HBM((rows, 3 * nh * LN), x.dtype),
+        grid=(rows // step,),
+        in_specs=[pl.BlockSpec((step, width), lambda i: (i, 0))],
+        out_specs=pl.BlockSpec((step, 3 * nh * LN), lambda i: (i, 0)),
+        cost_estimate=cost(us),
+        name="stretch",
+    )(hbm(x))
+
+
+def order_kernel(own_first, a_ref, b_ref, *outs, each):
     def put(ref):
         value = ref[...]
-        each = 3 * nh * HD // groups
-        gap = jnp.zeros((value.shape[0], lanes_up(each) - each), value.dtype)
-        for g in range(groups):
-            flats[g][...] = jnp.concatenate([value[:, g * each : (g + 1) * each], gap], axis=1)
-        zero = jnp.zeros((value.shape[0], LN - HD), value.dtype)
-        per = nh // groups
-        spread = []
-        for t in range(3):
-            for h in range(nh):
-                at = (h // per) * each + t * per * HD + (h % per) * HD
-                spread += [value[:, at : at + HD], zero]
-        wide[...] = jnp.concatenate(spread, axis=1)
+        for g, out in enumerate(outs):
+            gap = jnp.zeros((value.shape[0], out.shape[1] - each), value.dtype)
+            out[...] = jnp.concatenate([value[:, g * each : (g + 1) * each], gap], axis=1)
 
     half = pl.program_id(0)
 
@@ -378,16 +421,15 @@
         put(b_ref)
 
 
-def widen(own, other, own_at, groups, nh):
+def order(own, other, own_at, groups, nh):
     rows, width = own.shape
-    step = 160
+    step = 320
     n = rows // step
     at = lambda i, j, m: ((i ^ m[0]) * n + j, 0)
-    each = lanes_up(3 * nh * HD // groups)
+    each = 3 * nh * HD // groups
     return pl.pallas_call(
-        functools.partial(widen_kernel, groups=groups, nh=nh),
-        out_shape=[jax.ShapeDtypeStruct((2 * rows, each), own.dtype)] * groups
-        + [jax.ShapeDtypeStruct((2 * rows, 3 * nh * LN), own.dtype)],
+        functools.partial(order_kernel, each=each),
+        out_shape=[pltpu.HBM((2 * rows, lanes_up(each)), own.dtype)] * groups,
         grid_spec=pltpu.PrefetchScalarGridSpec(
             num_scalar_prefetch=1,
             grid=(2, n),
@@ -395,18 +437,30 @@
                 pl.BlockSpec((step, width), lambda i, j, m: (j * (1 - i), 0)),
                 pl.BlockSpec((step, width), lambda i, j, m: (j * i, 0)),
             ],
-            out_specs=[pl.BlockSpec((step, each), at)] * groups + [pl.BlockSpec((step, 3 * nh * LN), at)],
+            out_specs=[pl.BlockSpec((step, lanes_up(each)), at)] * groups,
         ),
-        cost_estimate=cost(16),
-        name="widen",
-    )(own_at.reshape(1), own, other)
-
-
-def project_kernel(info, *refs, count, width, fresh):
+        cost_estimate=cost(3),
+        name="order",
+    )(own_at.reshape(1), hbm(own), hbm(other))
+
+
+def project_kernel(info, *refs, count, halves, width, fresh):
     pairs = refs[: 2 * count]
-    gain, w, scale, ones = refs[2 * count : 2 * count + 4]
-    normed_ref, q_ref, kv_ref, mine_ref = refs[-4:]
-    j = pl.program_id(0)
+    gain = refs[2 * count]
+    weights = refs[2 * count + 1 : 2 * count + 1 + halves]
+    scale, ones = refs[2 * count + 1 + halves : 2 * count + 3 + halves]
+    normed_ref, q_ref, kv_ref, mine_ref, w = refs[-5:]
+    j, tile = pl.program_id(0), pl.program_id(1)
+    step = normed_ref.shape[0]
+
+    @pl.when((j == 0) & (tile == 0))
+    def _():
+        for i, ref in enumerate(weights):
+            h = ref.shape[0]
+            start = (info[count + 2] ^ i) * h if halves == 2 else 0
+            w[pl.ds(pl.multiple_of(start, 16), h), :] = ref[...]
+        if not fresh:
+            mine_ref[...] = refs[2 * count + 3 + halves][...]
 
     def work(x_ref):
         value = x_ref[...]
@@ -423,10 +477,8 @@
 
         @pl.when(info[count + 1] == info[j])
         def _():
-            mine_ref[...] = value
-
-    if not fresh:
-        mine_ref[...] = refs[2 * count + 4][...]
+            mine_ref[pl.ds(pl.multiple_of(tile * step, step), step), :] = value
+
     for i in range(count):
         for lane in range(2):
 
@@ -435,45 +487,59 @@
                 work(pairs[2 * i + 1 - lane])
 
 
-def project(pairs, places, lane, mine, gain, w, scale, ones, group_len, carried=None):
+def project(pairs, places, lane, mine, wt, gain, weights, scale, ones, group_len, carried=None):
     count = len(pairs)
     rows, d = pairs[0][0].shape
     width = scale.shape[1]
-    full = lambda i, f: (0, 0)
-    at = lambda i, f: (f[i], 0)
+    step = 128
+    tiles = rows // step
+    full = lambda j, t, f: (0, 0)
+    at = lambda j, t, f: (f[j] * tiles + t, 0)
     once = pl.Buffered(1)
-    info = jnp.stack(list(places) + [lane.astype(jnp.int32), mine])
-    args = [x for pair in pairs for x in pair] + [gain, w, scale, ones]
-    in_specs = [pl.BlockSpec((rows, d), full, pipeline_mode=once)] * (2 * count) + [
-        pl.BlockSpec((1, d), full, pipeline_mode=once),
-        pl.BlockSpec(w.shape, full, pipeline_mode=once),
+    info = jnp.stack(list(places) + [lane.astype(jnp.int32), mine, wt])
+    args = [x for pair in pairs for x in pair] + [gain, *map(hbm, weights), scale, ones]
+    in_specs = [
+        pl.BlockSpec(
+            (step, d),
+            lambda j, t, f, i=i: (jnp.where(j == i, t, jnp.where(j > i, tiles - 1, 0)), 0),
+        )
+        for i in range(count)
+        for _ in range(2)
+    ]
+    in_specs += [pl.BlockSpec((1, d), full, pipeline_mode=once)]
+    in_specs += [pl.BlockSpec(w.shape, full, pipeline_mode=once) for w in weights]
+    in_specs += [
         pl.BlockSpec((1, width), full, pipeline_mode=once),
         pl.BlockSpec((1, 2 * width), full, pipeline_mode=once),
     ]
     aliases = {}
     if carried is not None:
-        args += [carried[3], *carried[:3]]
-        in_specs += [pl.BlockSpec((rows, d), full, pipeline_mode=once)] + [pl.BlockSpec(memory_space=pl.ANY)] * 3
-        base = 2 * count + 6
+        base = len(args) + 2
+        args += [hbm(x) for x in (carried[3], *carried[:3])]
+        in_specs += [pl.BlockSpec((rows, d), full, pipeline_mode=once)]
+        in_specs += [pl.BlockSpec(memory_space=pl.ANY)] * 3
         aliases = {base: 0, base + 1: 1, base + 2: 2}
     return pl.pallas_call(
-        functools.partial(project_kernel, count=count, width=width, fresh=carried is None),
+        functools.partial(
+            project_kernel, count=count, halves=len(weights), width=width, fresh=carried is None
+        ),
         out_shape=[
-            jax.ShapeDtypeStruct((group_len, d), bf16),
-            jax.ShapeDtypeStruct((group_len, width), bf16),
-            jax.ShapeDtypeStruct((group_len, 2 * width), bf16),
-            jax.ShapeDtypeStruct((rows, d), bf16),
+            pltpu.HBM((group_len, d), bf16),
+            pltpu.HBM((group_len, width), bf16),
+            pltpu.HBM((group_len, 2 * width), bf16),
+            pltpu.HBM((rows, d), bf16),
         ],
         grid_spec=pltpu.PrefetchScalarGridSpec(
             num_scalar_prefetch=1,
-            grid=(count,),
+            grid=(count, tiles),
             in_specs=in_specs,
             out_specs=[
-                pl.BlockSpec((rows, d), at),
-                pl.BlockSpec((rows, width), at),
-                pl.BlockSpec((rows, 2 * width), at),
+                pl.BlockSpec((step, d), at),
+                pl.BlockSpec((step, width), at),
+                pl.BlockSpec((step, 2 * width), at),
                 pl.BlockSpec((rows, d), full),
             ],
+            scratch_shapes=[pltpu.VMEM((d, 3 * width), bf16)],
         ),
         input_output_aliases=aliases,
         compiler_params=pltpu.CompilerParams(vmem_limit_bytes=48 << 20),
@@ -564,10 +630,10 @@
         scratch = []
     return pl.pallas_call(
         body,
-        out_shape=[jax.ShapeDtypeStruct((rows, d), bf16)] * 6
-        + [jax.ShapeDtypeStruct((rows, d), f32)]
-        + [jax.ShapeDtypeStruct((rows, cols), bf16)] * 4
-        + [jax.ShapeDtypeStruct((1, d), f32)],
+        out_shape=[pltpu.HBM((rows, d), bf16)] * 6
+        + [pltpu.HBM((rows, d), f32)]
+        + [pltpu.HBM((rows, cols), bf16)] * 4
+        + [pltpu.HBM((1, d), f32)],
         grid_spec=pltpu.PrefetchScalarGridSpec(
             num_scalar_prefetch=1,
             grid=(rows // tile,),
@@ -578,7 +644,7 @@
         compiler_params=pltpu.CompilerParams(vmem_limit_bytes=52 << 20),
         cost_estimate=cost(0.01),
         name="tail",
-    )(at, *pieces, x, g, *weights, gain)
+    )(at, *pieces, hbm(x), g, *map(hbm, weights), gain)
 
 
 tn_dims = (((0,), (0,)), ((), ()))
@@ -600,7 +666,7 @@
     once = pl.Buffered(1)
     return pl.pallas_call(
         share_kernel,
-        out_shape=jax.ShapeDtypeStruct((d, 3 * w), bf16),
+        out_shape=pltpu.HBM((d, 3 * w), bf16),
         grid_spec=pltpu.PrefetchScalarGridSpec(
             num_scalar_prefetch=1,
             grid=(3,),
@@ -611,7 +677,7 @@
         compiler_params=pltpu.CompilerParams(vmem_limit_bytes=40 << 20),
         cost_estimate=cost(.01),
         name="share",
-    )(col.reshape(1), *lefts, *rights)
+    )(col.reshape(1), *map(hbm, lefts), *map(hbm, rights))
 
 
 def keep_kernel(col, l0, l1, l2, r0, r1, r2, got, out):
@@ -632,7 +698,7 @@
     block = pl.BlockSpec((d, w), lambda i, c: (0, i))
     return pl.pallas_call(
         keep_kernel,
-        out_shape=jax.ShapeDtypeStruct((d, 3 * w), bf16),
+        out_shape=pltpu.HBM((d, 3 * w), bf16),
         grid_spec=pltpu.PrefetchScalarGridSpec(
             num_scalar_prefetch=1,
             grid=(3,),
@@ -644,7 +710,7 @@
         compiler_params=pltpu.CompilerParams(vmem_limit_bytes=40 << 20),
         cost_estimate=cost(.01),
         name="keep",
-    )(col.reshape(1), *lefts, *rights, got)
+    )(col.reshape(1), *map(hbm, lefts), *map(hbm, rights), hbm(got))
 
 
 def total_kernel(*refs):
@@ -664,7 +730,7 @@
             break
     return pl.pallas_call(
         total_kernel,
-        out_shape=jax.ShapeDtypeStruct((r, c), bf16),
+        out_shape=pltpu.HBM((r, c), bf16),
         grid_spec=pltpu.PrefetchScalarGridSpec(
             num_scalar_prefetch=0,
             grid=(c // w,),
@@ -703,7 +769,7 @@
     whole = pl.BlockSpec(own.shape, lambda i, m: (0, 0, 0), pipeline_mode=pl.Buffered(1))
     outs = pl.pallas_call(
         place_kernel,
-        out_shape=[jax.ShapeDtypeStruct((n, h, d), f32)] * 3,
+        out_shape=[pltpu.HBM((n, h, d), f32)] * 3,
         grid_spec=pltpu.PrefetchScalarGridSpec(
             num_scalar_prefetch=1,
             grid=(n,),
@@ -713,7 +779,7 @@
         compiler_params=pltpu.CompilerParams(vmem_limit_bytes=40 << 20),
         cost_estimate=cost(.1),
         name="place_tail",
-    )(at, own, mate)
+    )(at, hbm(own), hbm(mate))
     return [out.reshape(n * h, d) for out in outs]
 
 
@@ -737,7 +803,7 @@
     block = pl.BlockSpec((w // 2, g.shape[1]), lambda i, m: (0, 0))
     return pl.pallas_call(
         cross_kernel,
-        out_shape=[jax.ShapeDtypeStruct((w // 2, g.shape[1]), bf16)] * 4,
+        out_shape=[pltpu.HBM((w // 2, g.shape[1]), bf16)] * 4,
         grid_spec=pltpu.PrefetchScalarGridSpec(
             num_scalar_prefetch=1,
             grid=(2,),
@@ -751,7 +817,7 @@
         compiler_params=pltpu.CompilerParams(vmem_limit_bytes=40 << 20),
         cost_estimate=cost(0.1),
         name="cross",
-    )(at, x, g)
+    )(at, hbm(x), hbm(g))
 
 
 def spread_kernel(at, *refs, groups, width):
@@ -785,7 +851,7 @@
     cuts = 2 if rows % 32 == 0 else 1
     return pl.pallas_call(
         functools.partial(spread_kernel, groups=groups, width=used // 3),
-        out_shape=jax.ShapeDtypeStruct((2, rows, width), f32),
+        out_shape=pltpu.HBM((2, rows, width), f32),
         grid_spec=pltpu.PrefetchScalarGridSpec(
             num_scalar_prefetch=1,
             grid=(2, cuts),
@@ -797,7 +863,7 @@
         compiler_params=pltpu.CompilerParams(vmem_limit_bytes=40 << 20),
         cost_estimate=cost(0.1),
         name="spread",
-    )(at, *flat).reshape(2 * rows, width)
+    )(at, *map(hbm, flat)).reshape(2 * rows, width)
 
 
 def rms_inverse(values):
@@ -937,8 +1003,10 @@
         got1_share = send(got1, lane_share)
         end = jnp.where(gc == 0, z == 0, z == 3)
         if pair:
+            wide_own = stretch(picked, groups, nh, 2)
+            got1 = after(got1, wide_own)
             other_w = send(picked, wt_mate)
-            *flat_w, wide_w = widen(picked, other_w, wt, groups, nh)
+            wide_w = (wide_own, stretch(other_w, groups, nh, 10))
         else:
             flat_all = lax.all_gather(picked, "wt", axis=0, tiled=True)[:, : 3 * nh * HD]
             each = flat_all.shape[1] // groups
@@ -946,10 +1014,12 @@
                 jnp.pad(flat_all[:, g * each : (g + 1) * each], ((0, 0), (0, lanes_up(each) - each)))
                 for g in range(groups)
             ]
-            order = jnp.transpose(flat_all.reshape(D, groups, 3, nh // groups, HD), (0, 2, 1, 3, 4))
-            wide_w = jnp.pad(
-                order.reshape(D, 3 * nh, HD), ((0, 0), (0, 0), (0, LN - HD))
-            ).reshape(D, -1)
+            by_head = jnp.transpose(flat_all.reshape(D, groups, 3, nh // groups, HD), (0, 2, 1, 3, 4))
+            wide_w = (
+                jnp.pad(
+                    by_head.reshape(D, 3 * nh, HD), ((0, 0), (0, 0), (0, LN - HD))
+                ).reshape(D, -1),
+            )
         got3 = send(jnp.where(end, own, got2), hop3)
         got2_share = send(got2, lane_share)
         way = 1 - 2 * host
@@ -970,7 +1040,7 @@
             ((jnp.arange(LN) >= HD) & (jnp.arange(LN) < HD + 3)).astype(f32), 2 * nh
         )[None]
         seg_row = jnp.where(lane, segments, seg_mate)[0]
-        fixed = (lane, mine, gain_attn[None], wide_w, lane_scale, ones, group_len)
+        fixed = (lane, mine, wt, gain_attn[None], wide_w, lane_scale, ones, group_len)
         carried = project(((own, own_share), (got1, got1_share)), places[:2], *fixed)
         got2_share = after(got2_share, carried[0])
         got3_share = send(after(got3, carried[0]), lane_share)
@@ -983,6 +1053,8 @@
 
         att, att_float, q_aug = attn_fwd(queries, keyval, seg_row, nh)
         att = after(att, grad_mlp)
+        if pair:
+            flat_w = order(after(picked, att), other_w, wt, groups, nh)
 
         trades = (core_mate, near_mate, cross_mate)
         att_pieces = [rows_at(att, (mine ^ j) * rows, rows) for j in range(parts)]
@@ -1008,21 +1080,24 @@
             grad_resid,
             *pieces,
             grad_gain_mlp,
-        ) = tail(jnp.stack([mine, *starts]), att_pieces, inputs, grad_mlp, weights, gain_mlp[None])
+        ) = tail(
+            jnp.stack([mine, *starts]), att_pieces, after(inputs, flat_w[0]), grad_mlp, weights, gain_mlp[None]
+        )
         pieces = [pieces[0]] + [send(pieces[j + 1], trades[j]) for j in range(3)]
 
         lefts = (after(attended, pieces[1]), normed_mlp, active)
         rights = (grad_proj, grad_hidden, grad_mlp)
         from_core = send(share(lefts, rights, 1 - gc), core_mate)
-        home_out = send(after(layer_out, pieces[2]), to_home)
-        summed = keep(lefts, rights, after(from_core, *pieces[1:]), gc)
+        home_out = send(after(layer_out, *pieces[1:]), to_home)
+        prepared = prep(pieces, att_float, mine, nh)
+        summed = keep(lefts, rights, after(from_core, prepared), gc)
         kept = lax.all_to_all(summed, ("wt", "gx", "near"), 0, 0, tiled=True)
 
         scale_row = jnp.tile(dim_scale, nh // groups)[None]
 
-        def backward(group, pieces):
+        def backward(group, *others):
             return attn_bwd(
-                q_aug, keyval, pieces, att_float, seg_row, mine, scale_row, nh, group, groups
+                q_aug, keyval, after(prepared, summed, *others), seg_row, scale_row, nh, group, groups
             )
 
         def gather(block):
@@ -1043,23 +1118,13 @@
             got = lax.all_to_all(part, ("wt", "gx"), 0, 0, tiled=True)
             return [got.reshape(sources, D // sources, -1)]
 
-        pieces[3] = after(pieces[3], summed)
-        grad_a, lanes_a = backward(0, pieces)
-        rows_a = by_rows(grad_a)
-        pieces[3] = after(pieces[3], rows_a[0])
-        grad_b, lanes_b = backward(1, pieces)
+        grad_a, lanes_a = backward(0)
+        layer_out = jnp.where(still, after(layer_out, grad_a), home_out)
+        rows_a = by_rows(after(grad_a, layer_out))
+        grad_b, lanes_b = backward(1, rows_a[0])
         rows_a[0] = after(rows_a[0], grad_b)
         sum_a = total(rows_a)
-        grad_b = after(grad_b, sum_a)
-        rows_b = by_rows(grad_b)
-        layer_out = jnp.where(still, after(layer_out, rows_b[0]), home_out)
         block_a = far_sum(sum_a)
-        sources = sizes["wt"] * 4
-        tail_sum = total([after(kept, rows_b[0], layer_out).reshape(sources, D // sources, -1)])
-        block = far_sum(tail_sum)
-        rows_b[0] = after(rows_b[0], block_a)
-        sum_b = total(rows_b)
-        block_b = far_sum(sum_b)
 
         def shard_grad(shard, *others):
             return sum(
@@ -1067,12 +1132,21 @@
                 for grad, w in zip((grad_a, grad_b), flat_w)
             )
 
-        to_core = jnp.stack(
-            [shard_grad(mine ^ 3, tail_sum), shard_grad(mine ^ 1, tail_sum)]
-        ).astype(bf16)
+        to_core = jnp.stack([shard_grad(mine ^ 3, sum_a), shard_grad(mine ^ 1, sum_a)]).astype(bf16)
         from_core = send(to_core, core_mate).astype(f32)
-        to_near = (shard_grad(mine ^ 2, sum_b) + from_core[0]).astype(bf16)
-        grad_normed = shard_grad(mine, sum_b) + from_core[1] + send(to_near, near_mate).astype(f32)
+        rows_b = by_rows(after(grad_b, to_core))
+        to_near = (shard_grad(mine ^ 2, rows_b[0]) + from_core[0]).astype(bf16)
+        grad_normed = shard_grad(mine, rows_b[0]) + from_core[1]
+        from_near = send(to_near, near_mate).astype(f32)
+        sources = sizes["wt"] * 4
+        tail_sum = total(
+            [after(kept, rows_b[0], to_near).reshape(sources, D // sources, -1)]
+        )
+        block = far_sum(tail_sum)
+        rows_b[0] = after(rows_b[0], block_a)
+        sum_b = total(rows_b)
+        block_b = far_sum(sum_b)
+        grad_normed = grad_normed + from_near
         inputs = inputs.astype(f32)
         inverse_attn = rms_inverse(inputs)
         grad_gain_attn = jnp.sum(grad_normed * inputs * inverse_attn, axis=0)

time: 504 us -> 530 us (1.052)
  starting transfers between devices: 62.5 us -> 103 us
  Pallas kernels: 174 us -> 204 us
  waiting for transfers between devices: 201 us -> 171 us
  local copies, waits for them, and re-layouts: 26.9 us -> 11.2 us
    ppermute x46, starting transfers between devices: 57.9 us -> 98.5 us  [send(): return lax.ppermute(value, AXES, pairs(target))]
    ppermute x46, waiting for transfers between devices: 201 us -> 171 us  [send(): return lax.ppermute(value, AXES, pairs(target))]
    pallas_call x15 -> x18, Pallas kernels: 136 us -> 165 us  [the longest x2 47.9 us: attn_bwd(): pl.pallas_call(functools.partial(bwd_kernel, nh=nh, bq=bq, bk=bk, n=n), o...]
    unnamed x102 -> x76, local copies, waits for them, and re-layouts: 22.9 us -> 5.4 us
  transfers between devices with their start and end apart: 47 -> 47, of which waited for: 22 -> 19; matrix products, arithmetic and copies ran while one was open for 6% -> 7% of each run, Pallas kernels for 28% -> 31%
where the time goes in v5:
time: 530 us; the launch traced here: 523 us
  Pallas kernels  204 us (38%)
  waiting for transfers between devices  171 us (32%)
  starting transfers between devices  103 us (19%)
  other arithmetic  19.6 us (4%)
  matrix products  12.3 us (2%)
  local copies, waits for them, and re-layouts  11.2 us (2%)
    ppermute x46, waiting for transfers between devices, send(): return lax.ppermute(value, AXES, pairs(target))  171 us
    ppermute x46, starting transfers between devices, send(): return lax.ppermute(value, AXES, pairs(target))  98.5 us
    pallas_call x2, Pallas kernels, attn_bwd(): pl.pallas_call(functools.partial(bwd_kernel, nh=nh, bq=bq, bk=bk, n=n), o...  47.9 us
    pallas_call x3, Pallas kernels, project(): pl.pallas_call(functools.partial(project_kernel, count=count, halves=len(...  30 us
    pallas_call x1, Pallas kernels, attn_fwd(): pl.pallas_call(functools.partial(fwd_kernel, nh=nh, bq=bq, bk=bk, nk=n //...  26.3 us
    pallas_call x1, Pallas kernels, tail(): pl.pallas_call(body, out_shape=[pltpu.HBM((rows, d), bf16)] * 6 + [pltpu....  21.9 us
    pallas_call x2, Pallas kernels, cross(): pl.pallas_call(cross_kernel, out_shape=[pltpu.HBM((w // 2, g.shape[1]), b...  14.4 us
    dot_general x8, matrix products, times_trans(): lax.dot_general(left, right, (((1,), (1,)), ((), ())), preferred_element_...  12.3 us
  transfers between devices with their start and end apart: 47, of which 19 were waited for; matrix products, arithmetic and copies ran while one was open for 7% of the time, Pallas kernels for 31%

profile of v5, /device:TPU:0, one launch (start us, length us, event | category | flops | bytes accessed | tf_op | source)
XLA Modules:
  0.0 522.9 jit_solution(9027915851783609247)
XLA Ops:
  9.6 5.4 %collective-permute-start.4 = (bf16[512,1280]{1,0:T(8,128)(2,1)S(1)}, bf16[512,1280]{1,0:T(8,128)(2,1)}, u32[]{:S(2)}, u32[]{:S(2)}) collective-permute-start(bf16[512,1280]{1,0:T(8,128)(2,1)S(1)} %bitcast.90), channel_id=1, source_target_pairs={{0,8},{1,9},{2,10},{3,11},{12,4},{13,5},{14,6},{15,7},{16,24},{17,... | collective-permute-start | bytes 3932168 | tf_op jit(solution)/shard_map/ppermute | solution.py:915
  15.7 4.7 pad_maximum_fusion.own
  20.4 5.4 %collective-permute-done.1.refs_2_ = bf16[512,1280]{1,0:T(8,128)(2,1)} collective-permute-done((bf16[512,1280]{1,0:T(8,128)(2,1)S(1)}, bf16[512,1280]{1,0:T(8,128)(2,1)}, u32[]{:S(2)}, u32[]{:S(2)}) %collective-permute-start.1) | collective-permute-done | bytes 1310752 | tf_op jit(solution)/shard_map/ppermute | solution.py:915
  38.6 7.0 %collective-permute-done.2.refs_0_ = bf16[512,1280]{1,0:T(8,128)(2,1)S(1)} collective-permute-done((bf16[512,1280]{1,0:T(8,128)(2,1)}, bf16[512,1280]{1,0:T(8,128)(2,1)S(1)}, u32[]{:S(2)}, u32[]{:S(2)}) %collective-permute-start.2) | collective-permute-done | bytes 1310752 | tf_op jit(solution)/shard_map/ppermute | solution.py:915
  57.2 12.7 %project.3 = (bf16[2048,1280]{1,0:T(8,128)(2,1)}, bf16[2048,512]{1,0:T(8,128)(2,1)}, bf16[2048,1024]{1,0:T(8,128)(2,1)}, bf16[512,1280]{1,0:T(8,128)(2,1)}) custom-call(s32[5]{0:T(128)S(1)} %stack.110.info, bf16[512,1280]{1,0:T(8,128)(2,1)S(1)} %bitcast.92, bf16[512,1280]{1,0:T(8,128)(2,1)} %collective-permute-done.4.refs_1_, ...), custom_call_target="tpu_custom_call" | custom-call | flops 10000000000 | bytes 1000 | tf_op jit(solution)/shard_map/project/pallas_call | solution.py:522
  75.4 8.5 %project.4 = (bf16[2048,1280]{1,0:T(8,128)(2,1)}, bf16[2048,512]{1,0:T(8,128)(2,1)}, bf16[2048,1024]{1,0:T(8,128)(2,1)}, bf16[512,1280]{1,0:T(8,128)(2,1)}) custom-call(s32[4]{0:T(128)S(1)} %add_add_fusion.1.info, bf16[512,1280]{1,0:T(8,128)(2,1)S(1)} %collective-permute-done.2.refs_0_, ...), custom_call_target="tpu_custom_call", output_to_operand_aliasing={{0}: (9, {}), {1}: (10, {}), {2}: (11, {})} | custom-call | flops 10000000000 | bytes 1000 | tf_op jit(solution)/shard_map/project/pallas_call | solution.py:522
  83.9 8.8 %project.5 = (bf16[2048,1280]{1,0:T(8,128)(2,1)}, bf16[2048,512]{1,0:T(8,128)(2,1)}, bf16[2048,1024]{1,0:T(8,128)(2,1)}, bf16[512,1280]{1,0:T(8,128)(2,1)}) custom-call(s32[4]{0:T(128)S(1)} %add_add_fusion.info, bf16[512,1280]{1,0:T(8,128)(2,1)} %collective-permute-done.3.refs_0_, ...), custom_call_target="tpu_custom_call", output_to_operand_aliasing={{0}: (9, {}), {1}: (10, {}), {2}: (11, {})} | custom-call | flops 10000000000 | bytes 1000 | tf_op jit(solution)/shard_map/project/pallas_call | solution.py:522
  92.7 26.3 %attn_fwd.1 = (bf16[2048,320]{1,0:T(8,128)(2,1)}, f32[2048,512]{1,0:T(8,128)}, bf16[2048,512]{1,0:T(8,128)(2,1)}) custom-call(s32[16]{0:T(128)S(1)} %reshape.185.flags, bf16[2048,512]{1,0:T(8,128)(2,1)} %get-tuple-element.92.q_ref, bf16[2048,1024]{1,0:T(8,128)(2,1)} %get-tuple-element.93.kv.kk.vv, s32[2048,1]{1,0:T(8,128)S(1)} %copy.29.segc, ...), custom_call_target="tpu_custom_call" | custom-call | flops 10000000 | bytes 1000 | tf_op jit(solution)/shard_map/attn_fwd/pallas_call | solution.py:168
  129.3 5.6 %collective-permute-done.11.p2 = bf16[512,320]{1,0:T(8,128)(2,1)S(1)} collective-permute-done((bf16[512,320]{1,0:T(8,128)(2,1)S(1)}, bf16[512,320]{1,0:T(8,128)(2,1)S(1)}, u32[]{:S(2)}, u32[]{:S(2)}) %collective-permute-start.11) | collective-permute-done | bytes 327712 | tf_op jit(solution)/shard_map/ppermute | solution.py:915
  134.9 7.3 %collective-permute-done.12.p3 = bf16[512,320]{1,0:T(8,128)(2,1)S(1)} collective-permute-done((bf16[512,320]{1,0:T(8,128)(2,1)S(1)}, bf16[512,320]{1,0:T(8,128)(2,1)S(1)}, u32[]{:S(2)}, u32[]{:S(2)}) %collective-permute-start.12) | collective-permute-done | bytes 327712 | tf_op jit(solution)/shard_map/ppermute | solution.py:915
  142.3 21.9 %tail.1 = (bf16[512,1280]{1,0:T(8,128)(2,1)}, bf16[512,1280]{1,0:T(8,128)(2,1)}, bf16[512,1280]{1,0:T(8,128)(2,1)}, bf16[512,1280]{1,0:T(8,128)(2,1)}, bf16[512,...) custom-call(s32[4]{0:T(128)S(1)} %pad_add_fusion.at, ...), custom_call_target="tpu_custom_call" | custom-call | flops 10000000 | bytes 1000 | tf_op jit(solution)/shard_map/tail/pallas_call | solution.py:631
  166.3 7.8 %share.1 = bf16[1280,1920]{1,0:T(8,128)(2,1)} custom-call(s32[1]{0:T(128)} %bitcast.22.col, bf16[512,1280]{1,0:T(8,128)(2,1)} %get-tuple-element.111.l0, bf16[512,1280]{1,0:T(8,128)(2,1)} %get-tuple-element.112.l1, bf16[512,1280]{1,0:T(8,128)(2,1)} %get-tuple-element.113.l2, bf16[512,1280]{1,0:T(8,128)(2,1)} %get-tuple-element.114.r0, ...), custom_call_target="tpu_custom_call" | custom-call | flops 10000000 | bytes 1000 | tf_op jit(solution)/shard_map/share/pallas_call | solution.py:667
  176.8 6.9 %collective-permute-done.17.do3 = bf16[512,320]{1,0:T(8,128)(2,1)S(1)} collective-permute-done((bf16[512,320]{1,0:T(8,128)(2,1)}, bf16[512,320]{1,0:T(8,128)(2,1)S(1)}, u32[]{:S(2)}, u32[]{:S(2)}) %collective-permute-start.17) | collective-permute-done | bytes 327712 | tf_op jit(solution)/shard_map/ppermute | solution.py:915
  183.7 8.1 %prep.1.doa_s = bf16[2048,512]{1,0:T(8,128)(2,1)} custom-call(s32[1]{0:T(128)} %bitcast.mine, bf16[512,320]{1,0:T(8,128)(2,1)S(1)} %copy-done.3, bf16[512,320]{1,0:T(8,128)(2,1)S(1)} %collective-permute-done.15.do1, bf16[512,320]{1,0:T(8,128)(2,1)S(1)} %collective-permute-done.16.do2, bf16[512,320]{1,0:T(8,128)(2,1)S(1)} %collective-permute-done.17.do3, ...), custom_call_target="tpu_custom_call" | custom-call | flops 999999995904 | bytes 1000 | tf_op jit(solution)/shard_map/prep/pallas_call | solution.py:278
  191.8 8.9 %keep.1 = bf16[1280,1920]{1,0:T(8,128)(2,1)} custom-call(s32[1]{0:T(128)} %bitcast.21.col, bf16[512,1280]{1,0:T(8,128)(2,1)} %get-tuple-element.111.l0, bf16[512,1280]{1,0:T(8,128)(2,1)} %get-tuple-element.112.l1, bf16[512,1280]{1,0:T(8,128)(2,1)} %get-tuple-element.113.l2, bf16[512,1280]{1,0:T(8,128)(2,1)} %get-tuple-element.114.r0, ...), custom_call_target="tpu_custom_call" | custom-call | flops 10000000 | bytes 1000 | tf_op jit(solution)/shard_map/keep/pallas_call | solution.py:699
  200.7 4.8 all-to-all-start
  207.4 24.0 %attn_bwd.2 = (bf16[2048,512]{1,0:T(8,128)(2,1)}, f32[8,128]{1,0:T(8,128)}) custom-call(s32[16]{0:T(128)S(1)} %copy-done.2, bf16[2048,512]{1,0:T(8,128)(2,1)} %get-tuple-element.104.qa, bf16[2048,1024]{1,0:T(8,128)(2,1)} %get-tuple-element.93.kv.kk.vv, bf16[2048,1024]{1,0:T(8,128)(2,1)} %get-tuple-element.93.kv.kk.vv, bf16[2048,512]{1,0:T(8,128)(2,1)} %prep.1.doa_s, ...), custom_call_target="tpu_custom_call" | custom-call | flops 10000000 | bytes 1000 | tf_op jit(solution)/shard_map/attn_bwd/pallas_call | solution.py:327
  232.6 7.2 %cross.2 = (bf16[320,512]{1,0:T(8,128)(2,1)}, bf16[320,512]{1,0:T(8,128)(2,1)}, bf16[320,512]{1,0:T(8,128)(2,1)}, bf16[320,512]{1,0:T(8,128)(2,1)}) custom-call(s32[2]{0:T(128)S(1)} %pad_add_fusion.1.at, bf16[2048,1280]{1,0:T(8,128)(2,1)} %get-tuple-element.122.x_ref, bf16[2048,512]{1,0:T(8,128)(2,1)} %get-tuple-element.136.g_ref), custom_call_target="tpu_custom_call" | custom-call | flops 100000000 | bytes 1000 | tf_op jit(solution)/shard_map/cross/pallas_call | solution.py:804
  243.3 23.9 %attn_bwd.3 = (bf16[2048,512]{1,0:T(8,128)(2,1)}, f32[8,128]{1,0:T(8,128)}) custom-call(s32[16]{0:T(128)S(1)} %copy-done.2, bf16[2048,512]{1,0:T(8,128)(2,1)} %get-tuple-element.104.qa, bf16[2048,1024]{1,0:T(8,128)(2,1)} %get-tuple-element.93.kv.kk.vv, bf16[2048,1024]{1,0:T(8,128)(2,1)} %get-tuple-element.93.kv.kk.vv, bf16[2048,512]{1,0:T(8,128)(2,1)} %prep.1.doa_s, ...), custom_call_target="tpu_custom_call" | custom-call | flops 10000000 | bytes 1000 | tf_op jit(solution)/shard_map/attn_bwd/pallas_call | solution.py:327
  267.2 12.0 %collective-permute-done.22 = bf16[320,512]{1,0:T(8,128)(2,1)S(1)} collective-permute-done((bf16[320,512]{1,0:T(8,128)(2,1)}, bf16[320,512]{1,0:T(8,128)(2,1)S(1)}, u32[]{:S(2)}, u32[]{:S(2)}) %collective-permute-start.22) | collective-permute-done | bytes 327712 | tf_op jit(solution)/shard_map/ppermute | solution.py:915
  286.2 42.5 %collective-permute-start.23 = (bf16[2,512,1280]{2,1,0:T(8,128)(2,1)S(1)}, bf16[2,512,1280]{2,1,0:T(8,128)(2,1)S(1)}, u32[]{:S(2)}, u32[]{:S(2)}) collective-permute-start(bf16[2,512,1280]{2,1,0:T(8,128)(2,1)S(1)} %pad_maximum_fusion.1), channel_id=1, source_target_pairs={{0,8},{1,9},{2,10},{3,11},{4,12},{5,13},{6,14},{7,15},{8,0},{9,1},... | collective-permute-start | bytes 7864328 | tf_op jit(solution)/shard_map/ppermute | solution.py:915
  330.1 7.2 %cross.3 = (bf16[320,512]{1,0:T(8,128)(2,1)}, bf16[320,512]{1,0:T(8,128)(2,1)}, bf16[320,512]{1,0:T(8,128)(2,1)}, bf16[320,512]{1,0:T(8,128)(2,1)}) custom-call(s32[2]{0:T(128)S(1)} %pad_add_fusion.1.at, bf16[2048,1280]{1,0:T(8,128)(2,1)} %get-tuple-element.122.x_ref, bf16[2048,512]{1,0:T(8,128)(2,1)} %get-tuple-element.137.g_ref), custom_call_target="tpu_custom_call" | custom-call | flops 100000000 | bytes 1000 | tf_op jit(solution)/shard_map/cross/pallas_call | solution.py:804
  342.7 5.0 collective-permute-done.26
  360.8 34.1 %collective-permute-done.37 = bf16[160,1920]{1,0:T(8,128)(2,1)S(1)} collective-permute-done((bf16[160,1920]{1,0:T(8,128)(2,1)}, bf16[160,1920]{1,0:T(8,128)(2,1)S(1)}, u32[]{:S(2)}, u32[]{:S(2)}) %collective-permute-start.37) | collective-permute-done | bytes 614432 | tf_op jit(solution)/shard_map/ppermute | solution.py:915
  395.0 6.1 %collective-permute-done.33 = bf16[320,512]{1,0:T(8,128)(2,1)S(1)} collective-permute-done((bf16[320,512]{1,0:T(8,128)(2,1)}, bf16[320,512]{1,0:T(8,128)(2,1)S(1)}, u32[]{:S(2)}, u32[]{:S(2)}) %collective-permute-start.33) | collective-permute-done | bytes 327712 | tf_op jit(solution)/shard_map/ppermute | solution.py:915
  406.2 15.1 %collective-permute-done.34 = bf16[1,320,512]{2,1,0:T(8,128)(2,1)S(1)} collective-permute-done((bf16[1,320,512]{2,1,0:T(8,128)(2,1)S(1)}, bf16[1,320,512]{2,1,0:T(8,128)(2,1)S(1)}, u32[]{:S(2)}, u32[]{:S(2)}) %collective-permute-start.34) | collective-permute-done | bytes 327712 | tf_op jit(solution)/shard_map/ppermute | solution.py:915
  427.0 12.0 %collective-permute-done.35 = bf16[2,320,512]{2,1,0:T(8,128)(2,1)S(1)} collective-permute-done((bf16[2,320,512]{2,1,0:T(8,128)(2,1)S(1)}, bf16[2,320,512]{2,1,0:T(8,128)(2,1)S(1)}, u32[]{:S(2)}, u32[]{:S(2)}) %collective-permute-start.35) | collective-permute-done | bytes 655392 | tf_op jit(solution)/shard_map/ppermute | solution.py:915
  440.2 9.1 %collective-permute-done.24 = bf16[512,1280]{1,0:T(8,128)(2,1)S(1)} collective-permute-done((bf16[512,1280]{1,0:T(8,128)(2,1)S(1)}, bf16[512,1280]{1,0:T(8,128)(2,1)S(1)}, u32[]{:S(2)}, u32[]{:S(2)}) %collective-permute-start.24) | collective-permute-done | bytes 1310752 | tf_op jit(solution)/shard_map/ppermute | solution.py:915
  452.0 12.3 %collective-permute-done.39 = bf16[2,160,1920]{2,1,0:T(8,128)(2,1)S(1)} collective-permute-done((bf16[2,160,1920]{2,1,0:T(8,128)(2,1)S(1)}, bf16[2,160,1920]{2,1,0:T(8,128)(2,1)S(1)}, u32[]{:S(2)}, u32[]{:S(2)}) %collective-permute-start.39) | collective-permute-done | bytes 1228832 | tf_op jit(solution)/shard_map/ppermute | solution.py:915
  476.7 22.6 %collective-permute-done.43 = f32[21,128]{1,0:T(8,128)S(1)} collective-permute-done((f32[21,128]{1,0:T(8,128)S(1)}, f32[21,128]{1,0:T(8,128)S(1)}, u32[]{:S(2)}, u32[]{:S(2)}) %collective-permute-start.43) | collective-permute-done | bytes 10784 | tf_op jit(solution)/shard_map/ppermute | solution.py:915
  504.4 7.7 %spread.1 = f32[2,320,3840]{2,1,0:T(8,128)} custom-call(s32[3]{0:T(128)S(1)} %pad_add_fusion.2.at, bf16[4,320,512]{2,1,0:T(8,128)(2,1)} %pad_maximum_fusion.3.refs_0_, bf16[4,320,512]{2,1,0:T(8,128)(2,1)} %collective-permute-done.29.refs_1_, bf16[4,320,512]{2,1,0:T(8,128)(2,1)} %pad_maximum_fusion.4.refs_2_, bf16[4,320,512]{2,1,0:T(8,128)(2,1)} %collective-permute-done.36.refs_3_), custom_call_target="tpu_custom_call" | custom-call | flops 100000000 | bytes 1000 | tf_op jit(solution)/shard_map/spread/pallas_call | solution.py:852
  515.7 7.0 %place_tail.1 = (f32[4,160,1280]{2,1,0:T(8,128)}, f32[4,160,1280]{2,1,0:T(8,128)}, f32[4,160,1280]{2,1,0:T(8,128)}) custom-call(s32[3]{0:T(128)S(1)} %pad_add_fusion.2.at, bf16[4,160,1920]{2,1,0:T(8,128)(2,1)} %copy-done.12, bf16[4,160,1920]{2,1,0:T(8,128)(2,1)} %collective-permute-done.40.mate_ref), custom_call_target="tpu_custom_call" | custom-call | flops 100000000 | bytes 1000 | tf_op jit(solution)/shard_map/place_tail/pallas_call | solution.py:770
  (227 shorter events, 123.6 us)
Async XLA Ops:
  5.3 20.6 %collective-permute-start.1 = (bf16[512,1280]{1,0:T(8,128)(2,1)S(1)}, bf16[512,1280]{1,0:T(8,128)(2,1)}, u32[]{:S(2)}, u32[]{:S(2)}) collective-permute-start(bf16[512,1280]{1,0:T(8,128)(2,1)S(1)} %bitcast.89), channel_id=1, source_target_pairs={{2,0},{3,1},{4,2},{5,3},{6,4},{7,5},{8,10},{9,11},{10,12},{11,13},... | collective-permute-start | bytes 3932168 | tf_op jit(solution)/shard_map/ppermute | solution.py:915
  6.6 44.1 %collective-permute-start.6 = (bf16[640,1024]{1,0:T(8,128)(2,1)}, bf16[640,1024]{1,0:T(8,128)(2,1)}, u32[]{:S(2)}, u32[]{:S(2)}) collective-permute-start(bf16[640,1024]{1,0:T(8,128)(2,1)} %pick.1.x_ref.a_ref), channel_id=1, source_target_pairs={{0,1},{1,0},{2,3},{3,2},{4,5},{5,4},{6,7},{7,6},{8,9},{9,8},{10,11... | collective-permute-start | bytes 3932168 | tf_op jit(solution)/shard_map/ppermute | solution.py:915
  9.6 47.5 %collective-permute-start.4 = (bf16[512,1280]{1,0:T(8,128)(2,1)S(1)}, bf16[512,1280]{1,0:T(8,128)(2,1)}, u32[]{:S(2)}, u32[]{:S(2)}) collective-permute-start(bf16[512,1280]{1,0:T(8,128)(2,1)S(1)} %bitcast.90), channel_id=1, source_target_pairs={{0,8},{1,9},{2,10},{3,11},{12,4},{13,5},{14,6},{15,7},{16,24},{17,... | collective-permute-start | bytes 3932168 | tf_op jit(solution)/shard_map/ppermute | solution.py:915
  15.1 19.7 %collective-permute-start = (s32[1,2048]{1,0:T(1,128)S(1)}, s32[1,2048]{1,0:T(1,128)S(1)}, u32[]{:S(2)}, u32[]{:S(2)}) collective-permute-start(s32[1,2048]{1,0:T(1,128)S(1)} %copy-done.26), channel_id=1, source_target_pairs={{0,8},{1,9},{2,10},{3,11},{4,12},{5,13},{6,14},{7,15},{8,0},{9,1},... | collective-permute-start | bytes 24584 | tf_op jit(solution)/shard_map/ppermute | solution.py:915
  25.9 19.7 %collective-permute-start.2 = (bf16[512,1280]{1,0:T(8,128)(2,1)}, bf16[512,1280]{1,0:T(8,128)(2,1)S(1)}, u32[]{:S(2)}, u32[]{:S(2)}) collective-permute-start(bf16[512,1280]{1,0:T(8,128)(2,1)} %collective-permute-done.1.refs_2_), channel_id=1, source_target_pairs={{2,0},{3,1},{4,2},{5,3},{10,12},{11,13},{12,14},{13,15},{18,16},{1... | collective-permute-start | bytes 3932168 | tf_op jit(solution)/shard_map/ppermute | solution.py:915
  36.2 21.0 %collective-permute-start.5 = (bf16[512,1280]{1,0:T(8,128)(2,1)}, bf16[512,1280]{1,0:T(8,128)(2,1)}, u32[]{:S(2)}, u32[]{:S(2)}) collective-permute-start(bf16[512,1280]{1,0:T(8,128)(2,1)} %collective-permute-done.1.refs_2_), channel_id=1, source_target_pairs={{0,8},{1,9},{2,10},{3,11},{12,4},{13,5},{14,6},{15,7},{16,24},{17,... | collective-permute-start | bytes 3932168 | tf_op jit(solution)/shard_map/ppermute | solution.py:915
  46.8 23.1 %collective-permute-start.3 = (bf16[512,1280]{1,0:T(8,128)(2,1)}, bf16[512,1280]{1,0:T(8,128)(2,1)}, u32[]{:S(2)}, u32[]{:S(2)}) collective-permute-start(bf16[512,1280]{1,0:T(8,128)(2,1)} %broadcast_select_fusion), channel_id=1, source_target_pairs={{0,2},{1,3},{2,0},{3,1},{12,14},{13,15},{14,12},{15,13},{16,18},{1... | collective-permute-start | bytes 3932168 | tf_op jit(solution)/shard_map/ppermute | solution.py:915
  54.8 19.6 %collective-permute-start.8 = (bf16[512,1280]{1,0:T(8,128)(2,1)S(1)}, bf16[512,1280]{1,0:T(8,128)(2,1)}, u32[]{:S(2)}, u32[]{:S(2)}) collective-permute-start(bf16[512,1280]{1,0:T(8,128)(2,1)S(1)} %collective-permute-done.2.refs_0_), channel_id=1, source_target_pairs={{0,8},{1,9},{2,10},{3,11},{12,4},{13,5},{14,6},{15,7},{16,24},{17,... | collective-permute-start | bytes 3932168 | tf_op jit(solution)/shard_map/ppermute | solution.py:915
  72.9 48.3 %collective-permute-start.13 = (bf16[3,320,1280]{2,1,0:T(8,128)(2,1)}, bf16[3,320,1280]{2,1,0:T(8,128)(2,1)}, u32[]{:S(2)}, u32[]{:S(2)}) collective-permute-start(bf16[3,320,1280]{2,1,0:T(8,128)(2,1)} %constant_dynamic-slice_fusion), channel_id=1, source_target_pairs={{0,1},{1,0},{2,3},{3,2},{4,5},{5,4},{6,7},{7,6},{8,9},{9,8},{10,11... | collective-permute-start | bytes 7372808 | tf_op jit(solution)/shard_map/ppermute | solution.py:915
  74.5 44.6 %collective-permute-start.9 = (bf16[512,1280]{1,0:T(8,128)(2,1)}, bf16[512,1280]{1,0:T(8,128)(2,1)S(1)}, u32[]{:S(2)}, u32[]{:S(2)}) collective-permute-start(bf16[512,1280]{1,0:T(8,128)(2,1)} %bitcast.115), channel_id=1, source_target_pairs={{2,8},{3,9},{4,2},{5,3},{6,10},{7,11},{8,4},{9,5},{10,12},{11,13},... | collective-permute-start | bytes 3932168 | tf_op jit(solution)/shard_map/ppermute | solution.py:915
  122.9 19.4 %collective-permute-start.14 = (bf16[3,320,1280]{2,1,0:T(8,128)(2,1)}, bf16[3,320,1280]{2,1,0:T(8,128)(2,1)}, u32[]{:S(2)}, u32[]{:S(2)}) collective-permute-start(bf16[3,320,1280]{2,1,0:T(8,128)(2,1)} %collective-permute-done.13.half), channel_id=1, source_target_pairs={{0,8},{1,9},{2,10},{3,11},{4,12},{5,13},{6,14},{7,15},{8,0},{9,1},... | collective-permute-start | bytes 7372808 | tf_op jit(solution)/shard_map/ppermute | solution.py:915
  200.7 151.8 %all-to-all-start = ((bf16[8,160,1920]{2,1,0:T(8,128)(2,1)}), bf16[8,160,1920]{2,1,0:T(8,128)(2,1)}, u32[]{:S(2)}, u32[]{:S(2)}) async-start(bf16[8,160,1920]{2,1,0:T(8,128)(2,1)} %bitcast.110), calls=%async_computation | async-start | bytes 9830400 | tf_op jit(solution)/shard_map/all_to_all | solution.py:1094
  205.5 25.9 %collective-permute-start.19 = (bf16[512,1280]{1,0:T(8,128)(2,1)S(1)}, bf16[512,1280]{1,0:T(8,128)(2,1)}, u32[]{:S(2)}, u32[]{:S(2)}) collective-permute-start(bf16[512,1280]{1,0:T(8,128)(2,1)S(1)} %copy-done.19), channel_id=1, source_target_pairs={{2,4},{3,5},{4,8},{5,9},{6,12},{7,13},{8,2},{9,3},{10,6},{11,7},{1... | collective-permute-start | bytes 3932168 | tf_op jit(solution)/shard_map/ppermute | solution.py:915
  239.8 27.4 %collective-permute-start.20 = (bf16[320,512]{1,0:T(8,128)(2,1)}, bf16[320,512]{1,0:T(8,128)(2,1)S(1)}, u32[]{:S(2)}, u32[]{:S(2)}) collective-permute-start(bf16[320,512]{1,0:T(8,128)(2,1)} %get-tuple-element.128), channel_id=1, source_target_pairs={{0,16},{1,17},{2,18},{3,19},{4,20},{5,21},{6,22},{7,23},{8,24},{9,... | collective-permute-start | bytes 983048 | tf_op jit(solution)/shard_map/ppermute | solution.py:915
  241.6 25.5 %collective-permute-start.21 = (bf16[320,512]{1,0:T(8,128)(2,1)}, bf16[320,512]{1,0:T(8,128)(2,1)S(1)}, u32[]{:S(2)}, u32[]{:S(2)}) collective-permute-start(bf16[320,512]{1,0:T(8,128)(2,1)} %get-tuple-element.129), channel_id=1, source_target_pairs={{0,1},{1,0},{2,3},{3,2},{4,5},{5,4},{6,7},{7,6},{8,9},{9,8},{10,11... | collective-permute-start | bytes 983048 | tf_op jit(solution)/shard_map/ppermute | solution.py:915
  243.1 36.0 %collective-permute-start.22 = (bf16[320,512]{1,0:T(8,128)(2,1)}, bf16[320,512]{1,0:T(8,128)(2,1)S(1)}, u32[]{:S(2)}, u32[]{:S(2)}) collective-permute-start(bf16[320,512]{1,0:T(8,128)(2,1)} %get-tuple-element.130), channel_id=1, source_target_pairs={{0,17},{1,16},{2,19},{3,18},{4,21},{5,20},{6,23},{7,22},{8,25},{9,... | collective-permute-start | bytes 983048 | tf_op jit(solution)/shard_map/ppermute | solution.py:915
  286.2 61.6 %collective-permute-start.23 = (bf16[2,512,1280]{2,1,0:T(8,128)(2,1)S(1)}, bf16[2,512,1280]{2,1,0:T(8,128)(2,1)S(1)}, u32[]{:S(2)}, u32[]{:S(2)}) collective-permute-start(bf16[2,512,1280]{2,1,0:T(8,128)(2,1)S(1)} %pad_maximum_fusion.1), channel_id=1, source_target_pairs={{0,8},{1,9},{2,10},{3,11},{4,12},{5,13},{6,14},{7,15},{8,0},{9,1},... | collective-permute-start | bytes 7864328 | tf_op jit(solution)/shard_map/ppermute | solution.py:915
  337.3 21.9 %collective-permute-start.30 = (bf16[320,512]{1,0:T(8,128)(2,1)}, bf16[320,512]{1,0:T(8,128)(2,1)S(1)}, u32[]{:S(2)}, u32[]{:S(2)}) collective-permute-start(bf16[320,512]{1,0:T(8,128)(2,1)} %get-tuple-element.139), channel_id=1, source_target_pairs={{0,16},{1,17},{2,18},{3,19},{4,20},{5,21},{6,22},{7,23},{8,24},{9,... | collective-permute-start | bytes 983048 | tf_op jit(solution)/shard_map/ppermute | solution.py:915
  338.1 21.1 %collective-permute-start.31 = (bf16[320,512]{1,0:T(8,128)(2,1)}, bf16[320,512]{1,0:T(8,128)(2,1)S(1)}, u32[]{:S(2)}, u32[]{:S(2)}) collective-permute-start(bf16[320,512]{1,0:T(8,128)(2,1)} %get-tuple-element.140), channel_id=1, source_target_pairs={{0,1},{1,0},{2,3},{3,2},{4,5},{5,4},{6,7},{7,6},{8,9},{9,8},{10,11... | collective-permute-start | bytes 983048 | tf_op jit(solution)/shard_map/ppermute | solution.py:915
  339.4 19.8 %collective-permute-start.32 = (bf16[320,512]{1,0:T(8,128)(2,1)}, bf16[320,512]{1,0:T(8,128)(2,1)S(1)}, u32[]{:S(2)}, u32[]{:S(2)}) collective-permute-start(bf16[320,512]{1,0:T(8,128)(2,1)} %get-tuple-element.141), channel_id=1, source_target_pairs={{0,17},{1,16},{2,19},{3,18},{4,21},{5,20},{6,23},{7,22},{8,25},{9,... | collective-permute-start | bytes 983048 | tf_op jit(solution)/shard_map/ppermute | solution.py:915
  347.7 56.6 %collective-permute-start.27 = (bf16[1,320,512]{2,1,0:T(8,128)(2,1)S(1)}, bf16[1,320,512]{2,1,0:T(8,128)(2,1)S(1)}, u32[]{:S(2)}, u32[]{:S(2)}) collective-permute-start(bf16[1,320,512]{2,1,0:T(8,128)(2,1)S(1)} %fusion.29), channel_id=1, source_target_pairs={{0,2},{1,3},{2,0},{3,1},{4,6},{5,7},{6,4},{7,5},{8,10},{9,11},{10,... | collective-permute-start | bytes 983048 | tf_op jit(solution)/shard_map/ppermute | solution.py:915
  356.8 38.0 %collective-permute-start.37 = (bf16[160,1920]{1,0:T(8,128)(2,1)}, bf16[160,1920]{1,0:T(8,128)(2,1)S(1)}, u32[]{:S(2)}, u32[]{:S(2)}) collective-permute-start(bf16[160,1920]{1,0:T(8,128)(2,1)} %total.5), channel_id=1, source_target_pairs={{0,4},{1,5},{2,6},{3,7},{4,0},{5,1},{6,2},{7,3},{8,12},{9,13},{10,... | collective-permute-start | bytes 1843208 | tf_op jit(solution)/shard_map/ppermute | solution.py:915
  360.2 40.9 %collective-permute-start.33 = (bf16[320,512]{1,0:T(8,128)(2,1)}, bf16[320,512]{1,0:T(8,128)(2,1)S(1)}, u32[]{:S(2)}, u32[]{:S(2)}) collective-permute-start(bf16[320,512]{1,0:T(8,128)(2,1)} %total.4), channel_id=1, source_target_pairs={{0,4},{1,5},{2,6},{3,7},{4,0},{5,1},{6,2},{7,3},{8,12},{9,13},{10,... | collective-permute-start | bytes 983048 | tf_op jit(solution)/shard_map/ppermute | solution.py:915
  395.0 28.2 %collective-permute-start.38 = (bf16[1,160,1920]{2,1,0:T(8,128)(2,1)S(1)}, bf16[1,160,1920]{2,1,0:T(8,128)(2,1)S(1)}, u32[]{:S(2)}, u32[]{:S(2)}) collective-permute-start(bf16[1,160,1920]{2,1,0:T(8,128)(2,1)S(1)} %fusion.16), channel_id=1, source_target_pairs={{0,2},{1,3},{2,0},{3,1},{4,6},{5,7},{6,4},{7,5},{8,10},{9,11},{10,... | collective-permute-start | bytes 1843208 | tf_op jit(solution)/shard_map/ppermute | solution.py:915
  402.3 47.0 %collective-permute-start.24 = (bf16[512,1280]{1,0:T(8,128)(2,1)S(1)}, bf16[512,1280]{1,0:T(8,128)(2,1)S(1)}, u32[]{:S(2)}, u32[]{:S(2)}) collective-permute-start(bf16[512,1280]{1,0:T(8,128)(2,1)S(1)} %copy-done.20), channel_id=1, source_target_pairs={{0,2},{1,3},{2,0},{3,1},{4,6},{5,7},{6,4},{7,5},{8,10},{9,11},{10,... | collective-permute-start | bytes 3932168 | tf_op jit(solution)/shard_map/ppermute | solution.py:915
  404.3 21.5 %collective-permute-start.28 = (bf16[2,320,512]{2,1,0:T(8,128)(2,1)S(1)}, bf16[2,320,512]{2,1,0:T(8,128)(2,1)S(1)}, u32[]{:S(2)}, u32[]{:S(2)}) collective-permute-start(bf16[2,320,512]{2,1,0:T(8,128)(2,1)S(1)} %pad_maximum_fusion.6), channel_id=1, source_target_pairs={{0,16},{1,17},{2,18},{3,19},{4,20},{5,21},{6,22},{7,23},{8,24},{9,... | collective-permute-start | bytes 1966088 | tf_op jit(solution)/shard_map/ppermute | solution.py:915
  423.3 41.0 %collective-permute-start.39 = (bf16[2,160,1920]{2,1,0:T(8,128)(2,1)S(1)}, bf16[2,160,1920]{2,1,0:T(8,128)(2,1)S(1)}, u32[]{:S(2)}, u32[]{:S(2)}) collective-permute-start(bf16[2,160,1920]{2,1,0:T(8,128)(2,1)S(1)} %pad_maximum_fusion.5), channel_id=1, source_target_pairs={{0,16},{1,17},{2,18},{3,19},{4,20},{5,21},{6,22},{7,23},{8,24},{9,... | collective-permute-start | bytes 3686408 | tf_op jit(solution)/shard_map/ppermute | solution.py:915
  427.0 77.3 %collective-permute-start.29 = (bf16[4,320,512]{2,1,0:T(8,128)(2,1)}, bf16[4,320,512]{2,1,0:T(8,128)(2,1)}, u32[]{:S(2)}, u32[]{:S(2)}) collective-permute-start(bf16[4,320,512]{2,1,0:T(8,128)(2,1)} %pad_maximum_fusion.3.refs_0_), channel_id=1, source_target_pairs={{0,8},{1,9},{2,10},{3,11},{4,12},{5,13},{6,14},{7,15},{8,0},{9,1},... | collective-permute-start | bytes 3932168 | tf_op jit(solution)/shard_map/ppermute | solution.py:915
  440.2 64.2 %collective-permute-start.36 = (bf16[4,320,512]{2,1,0:T(8,128)(2,1)}, bf16[4,320,512]{2,1,0:T(8,128)(2,1)}, u32[]{:S(2)}, u32[]{:S(2)}) collective-permute-start(bf16[4,320,512]{2,1,0:T(8,128)(2,1)} %pad_maximum_fusion.4.refs_2_), channel_id=1, source_target_pairs={{0,8},{1,9},{2,10},{3,11},{4,12},{5,13},{6,14},{7,15},{8,0},{9,1},... | collective-permute-start | bytes 3932168 | tf_op jit(solution)/shard_map/ppermute | solution.py:915
  464.6 51.1 %collective-permute-start.40 = (bf16[4,160,1920]{2,1,0:T(8,128)(2,1)S(1)}, bf16[4,160,1920]{2,1,0:T(8,128)(2,1)}, u32[]{:S(2)}, u32[]{:S(2)}) collective-permute-start(bf16[4,160,1920]{2,1,0:T(8,128)(2,1)S(1)} %pad_maximum_fusion.2.own_ref), channel_id=1, source_target_pairs={{0,8},{1,9},{2,10},{3,11},{4,12},{5,13},{6,14},{7,15},{8,0},{9,1},... | collective-permute-start | bytes 7372808 | tf_op jit(solution)/shard_map/ppermute | solution.py:915
  466.6 46.6 %collective-permute-start.25 = (bf16[512,1280]{1,0:T(8,128)(2,1)}, bf16[512,1280]{1,0:T(8,128)(2,1)}, u32[]{:S(2)}, u32[]{:S(2)}) collective-permute-start(bf16[512,1280]{1,0:T(8,128)(2,1)} %fusion.12), channel_id=1, source_target_pairs={{2,4},{3,5},{4,8},{5,9},{6,12},{7,13},{8,2},{9,3},{10,6},{11,7},{1... | collective-permute-start | bytes 3932168 | tf_op jit(solution)/shard_map/ppermute | solution.py:915
  473.4 25.9 %collective-permute-start.43 = (f32[21,128]{1,0:T(8,128)S(1)}, f32[21,128]{1,0:T(8,128)S(1)}, u32[]{:S(2)}, u32[]{:S(2)}) collective-permute-start(f32[21,128]{1,0:T(8,128)S(1)} %fusion.51), channel_id=1, source_target_pairs={{0,4},{1,5},{2,6},{3,7},{4,0},{5,1},{6,2},{7,3},{8,12},{9,13},{10,... | collective-permute-start | bytes 32264 | tf_op jit(solution)/shard_map/ppermute | solution.py:915
  (52 other events, 683.3 us)

commit v6 on v5

--- a/solution.py
+++ b/solution.py
@@ -137,7 +137,7 @@
         acc = acc_s[h]
         total = acc[:, HD : HD + 1]
         out = acc * (1.0 / total)
-        of[:, h * LN : (h + 1) * LN] = jnp.where(lanes < HD, out, 0.0)
+        of[:, h * LN : (h + 1) * LN] = jnp.where(lanes < HD, out, 0.0).astype(bf16)
         outs.append(out[:, :HD])
         lse = m_s[h][:, :1] + jnp.log2(total)
         qaug[:, h * LN : (h + 1) * LN] = put_split(
@@ -169,7 +169,7 @@
         functools.partial(fwd_kernel, nh=nh, bq=bq, bk=bk, nk=n // bk),
         out_shape=[
             pltpu.HBM((n, nh * HD), bf16),
-            pltpu.HBM((n, w), f32),
+            pltpu.HBM((n, w), bf16),
             pltpu.HBM((n, w), bf16),
         ],
         grid_spec=spec,
@@ -267,7 +267,7 @@
                     [d[:, h * HD : (h + 1) * HD], jnp.zeros((tile, LN - HD), f32)], axis=1
                 )
                 c = slice(h * LN, (h + 1) * LN)
-                delta = jnp.sum(dh * of[:, c], axis=1, keepdims=True)
+                delta = jnp.sum(dh * of[:, c].astype(f32), axis=1, keepdims=True)
                 out[:, c] = put_split(dh, -delta, lanes)
 
 
@@ -332,7 +332,7 @@
         ],
         grid_spec=spec,
         compiler_params=pltpu.CompilerParams(vmem_limit_bytes=48 << 20),
-        cost_estimate=cost(0.01),
+        cost_estimate=cost(300 if group == 0 else 0.001),
         name="attn_bwd",
     )(block_flags(seg_row, bq, bk), hbm(qa), hbm(kv), hbm(kv), hbm(doa), seg_row[:, None], seg_row[None], scale)
 
@@ -491,7 +491,7 @@
     count = len(pairs)
     rows, d = pairs[0][0].shape
     width = scale.shape[1]
-    step = 128
+    step = 256
     tiles = rows // step
     full = lambda j, t, f: (0, 0)
     at = lambda j, t, f: (f[j] * tiles + t, 0)
@@ -675,7 +675,7 @@
             out_specs=pl.BlockSpec((d, w), lambda i, c: (0, i)),
         ),
         compiler_params=pltpu.CompilerParams(vmem_limit_bytes=40 << 20),
-        cost_estimate=cost(.01),
+        cost_estimate=cost(0.01),
         name="share",
     )(col.reshape(1), *map(hbm, lefts), *map(hbm, rights))
 
@@ -708,79 +708,107 @@
             out_specs=block,
         ),
         compiler_params=pltpu.CompilerParams(vmem_limit_bytes=40 << 20),
-        cost_estimate=cost(.01),
+        cost_estimate=cost(0.01),
         name="keep",
     )(col.reshape(1), *map(hbm, lefts), *map(hbm, rights), hbm(got))
 
 
-def total_kernel(*refs):
-    acc = jnp.zeros(refs[-1].shape, f32)
-    for ref in refs[:-1]:
-        for i in range(ref.shape[0]):
-            acc = acc + ref[i].astype(f32)
-    refs[-1][...] = acc.astype(bf16)
-
-
-def total(arrays):
-    _, r, c = arrays[0].shape
-    w = c
-    for cut in (640, 256):
-        if c % cut == 0:
-            w = cut
-            break
-    return pl.pallas_call(
-        total_kernel,
-        out_shape=pltpu.HBM((r, c), bf16),
-        grid_spec=pltpu.PrefetchScalarGridSpec(
-            num_scalar_prefetch=0,
-            grid=(c // w,),
-            in_specs=[pl.BlockSpec((x.shape[0], r, w), lambda i: (0, 0, i)) for x in arrays],
-            out_specs=pl.BlockSpec((r, w), lambda i: (0, i)),
-        ),
+def total_kernel(*refs, counts):
+    out = refs[-1]
+    start, column = 0, 0
+    for count in counts:
+        group = refs[start : start + count]
+        start += count
+        acc = jnp.zeros(group[0].shape[1:], f32)
+        for ref in group:
+            for i in range(ref.shape[0]):
+                acc = acc + ref[i].astype(f32)
+        out[:, column : column + acc.shape[1]] = acc.astype(bf16)
+        column += acc.shape[1]
+
+
+def total(groups):
+    flat = [x for group in groups for x in group]
+    rows = flat[0].shape[1]
+    cuts = 2 if rows % 32 == 0 else 1
+    width = sum(group[0].shape[2] for group in groups)
+    return pl.pallas_call(
+        functools.partial(total_kernel, counts=[len(group) for group in groups]),
+        out_shape=pltpu.HBM((rows, width), bf16),
+        grid=(cuts,),
+        in_specs=[
+            pl.BlockSpec((x.shape[0], rows // cuts, x.shape[2]), lambda i: (0, i, 0)) for x in flat
+        ],
+        out_specs=pl.BlockSpec((rows // cuts, width), lambda i: (i, 0)),
         compiler_params=pltpu.CompilerParams(vmem_limit_bytes=40 << 20),
-        cost_estimate=cost(10),
+        cost_estimate=cost(0.001),
         name="total",
-    )(*arrays)
-
-
-def place_kernel(at, own_ref, mate_ref, o0, o1, o2):
+    )(*flat)
+
+
+def add_kernel(a_ref, b_ref, out):
+    out[...] = (a_ref[...].astype(f32) + b_ref[...].astype(f32)).astype(bf16)
+
+
+def add(a, b):
+    return pl.pallas_call(
+        add_kernel, out_shape=pltpu.HBM(a.shape, bf16), cost_estimate=CHEAP, name="add"
+    )(a, b)
+
+
+def pair_kernel(a_ref, b_ref, out):
+    out[0] = a_ref[...]
+    out[1] = b_ref[...]
+
+
+def pair_up(a, b):
+    return pl.pallas_call(
+        pair_kernel, out_shape=pltpu.HBM((2,) + a.shape, bf16), cost_estimate=CHEAP, name="pair_up"
+    )(a, b)
+
+
+def by_bits(first, second, put):
+    for i in range(2):
+        for j in range(2):
+
+            @pl.when((first == i) & (second == j))
+            def _(i=i, j=j):
+                put(i, j)
+
+
+def place_kernel(at, own, own_x, mate, mate_x, o0, o1, o2):
     block = pl.program_id(0)
-    slot = ((block // 2) ^ at[0]) * 2 + ((block % 2) ^ at[1])
+    slot = (block % 2) ^ at[1]
     w = o0.shape[2] // 2
 
-    def put(refs):
-        for side, ref in enumerate(refs):
-            part = ref[slot].astype(f32)
+    def put(other_x, core):
+        refs = (own_x, mate_x) if other_x else (own, mate)
+        for side in range(2):
+            part = refs[side ^ core][slot].astype(f32)
             for i, out in enumerate((o0, o1, o2)):
                 out[0, :, side * w : (side + 1) * w] = part[:, i * w : (i + 1) * w]
 
-    @pl.when(at[2] == 0)
-    def _():
-        put((own_ref, mate_ref))
-
-    @pl.when(at[2] == 1)
-    def _():
-        put((mate_ref, own_ref))
-
-
-def place_tail(own, mate, at):
-    n, h, width = own.shape
+    by_bits((block // 2) ^ at[0], at[2], put)
+
+
+def place_tail(arrays, at):
+    _, h, width = arrays[0].shape
     d = width // 3 * 2
-    whole = pl.BlockSpec(own.shape, lambda i, m: (0, 0, 0), pipeline_mode=pl.Buffered(1))
+    whole = pl.BlockSpec((2, h, width), lambda i, m: (0, 0, 0), pipeline_mode=pl.Buffered(1))
     outs = pl.pallas_call(
         place_kernel,
-        out_shape=[pltpu.HBM((n, h, d), f32)] * 3,
+        out_shape=[pltpu.HBM((4, h, d), f32)] * 3,
         grid_spec=pltpu.PrefetchScalarGridSpec(
             num_scalar_prefetch=1,
-            grid=(n,),
-            in_specs=[whole] * 2,
+            grid=(4,),
+            in_specs=[whole] * 4,
             out_specs=[pl.BlockSpec((1, h, d), lambda i, m: (i, 0, 0))] * 3,
         ),
         compiler_params=pltpu.CompilerParams(vmem_limit_bytes=40 << 20),
-        cost_estimate=cost(.1),
+        cost_estimate=cost(0.001),
         name="place_tail",
-    )(at, hbm(own), hbm(mate))
-    return [out.reshape(n * h, d) for out in outs]
+    )(at, *arrays)
+    return [out.reshape(4 * h, d) for out in outs]
 
 
 def cross_kernel(at, x_ref, g_ref, *refs):
@@ -815,55 +843,144 @@
             scratch_shapes=[pltpu.VMEM((w, g.shape[1]), bf16)],
         ),
         compiler_params=pltpu.CompilerParams(vmem_limit_bytes=40 << 20),
-        cost_estimate=cost(0.1),
+        cost_estimate=cost(0.001),
         name="cross",
-    )(at, hbm(x), hbm(g))
+    )(at, x, g)
 
 
 def spread_kernel(at, *refs, groups, width):
     out = refs[-1]
     step = out.shape[1]
-    slot = (pl.program_id(0) ^ at[0]) * 2
     rows = pl.ds(pl.multiple_of(pl.program_id(1) * step, step), step)
 
-    def put(flip):
+    def put(other_x, core):
         cut = []
         for t in range(3):
             for n in range(2):
-                for core in range(2):
+                for c in range(2):
                     for g in range(groups):
-                        part = refs[2 * g + (core ^ flip)][slot + (n ^ at[1]), rows, :]
+                        part = refs[4 * g + other_x + 2 * (c ^ core)][n ^ at[1], rows, :]
                         cut.append(part[:, t * width : (t + 1) * width])
         out[0] = jnp.concatenate(cut, axis=1).astype(f32)
 
-    for flip in range(2):
-
-        @pl.when(at[2] == flip)
-        def _(flip=flip):
-            put(flip)
+    by_bits(pl.program_id(0) ^ at[0], at[2], put)
 
 
 def spread(arrays, at, used):
-    flat = [x for pair in arrays for x in pair]
-    _, rows, _ = flat[0].shape
+    flat = [x for group in arrays for x in group]
     groups = len(arrays)
+    _, rows, cols = flat[0].shape
     width = 4 * groups * used
     cuts = 2 if rows % 32 == 0 else 1
+    whole = pl.BlockSpec((2, rows, cols), lambda i, j, m: (0, 0, 0), pipeline_mode=pl.Buffered(1))
     return pl.pallas_call(
         functools.partial(spread_kernel, groups=groups, width=used // 3),
         out_shape=pltpu.HBM((2, rows, width), f32),
         grid_spec=pltpu.PrefetchScalarGridSpec(
             num_scalar_prefetch=1,
             grid=(2, cuts),
-            in_specs=[
-                pl.BlockSpec(x.shape, lambda i, j, m: (0, 0, 0), pipeline_mode=pl.Buffered(1)) for x in flat
-            ],
+            in_specs=[whole] * len(flat),
             out_specs=pl.BlockSpec((1, rows // cuts, width), lambda i, j, m: (i, j, 0)),
         ),
         compiler_params=pltpu.CompilerParams(vmem_limit_bytes=40 << 20),
-        cost_estimate=cost(0.1),
+        cost_estimate=CHEAP,
         name="spread",
-    )(at, *map(hbm, flat)).reshape(2 * rows, width)
+    )(at, *flat).reshape(2 * rows, width)
+
+
+nt_dims = (((1,), (1,)), ((), ()))
+
+
+def back_kernel(shards, *refs, groups, extra):
+    grads, weights = refs[:groups], refs[groups : 2 * groups]
+    out = refs[-1]
+    acc = sum(
+        lax.dot_general(g[...], w[...], nt_dims, preferred_element_type=f32)
+        for g, w in zip(grads, weights)
+    )
+    if extra:
+        acc = acc + refs[2 * groups][0].astype(f32)
+    out[0] = acc.astype(bf16)
+
+
+def back(grads, weights, shards, rows, got=None):
+    groups = len(grads)
+    d, c = weights[0].shape
+    n = shards.shape[0]
+    in_specs = [pl.BlockSpec((rows, c), lambda i, f: (f[i], 0))] * groups
+    in_specs += [pl.BlockSpec((d, c), lambda i, f: (0, 0), pipeline_mode=pl.Buffered(1))] * groups
+    args = [*grads, *weights]
+    if got is not None:
+        in_specs.append(pl.BlockSpec((1, rows, d), lambda i, f: (0, 0, 0)))
+        args.append(got)
+    return pl.pallas_call(
+        functools.partial(back_kernel, groups=groups, extra=got is not None),
+        out_shape=pltpu.HBM((n, rows, d), bf16),
+        grid_spec=pltpu.PrefetchScalarGridSpec(
+            num_scalar_prefetch=1,
+            grid=(n,),
+            in_specs=in_specs,
+            out_specs=pl.BlockSpec((1, rows, d), lambda i, f: (i, 0, 0)),
+        ),
+        compiler_params=pltpu.CompilerParams(vmem_limit_bytes=40 << 20),
+        cost_estimate=CHEAP,
+        name="back",
+    )(shards, *args)
+
+
+def finish_kernel(shard, *refs, groups):
+    grads, weights = refs[:groups], refs[groups : 2 * groups]
+    core, near, x_ref, resid, gain, out, gain_out = refs[2 * groups :]
+    grad = sum(
+        lax.dot_general(g[...], w[...], nt_dims, preferred_element_type=f32)
+        for g, w in zip(grads, weights)
+    )
+    grad = grad + core[0].astype(f32) + near[0].astype(f32)
+    x = x_ref[...].astype(f32)
+    inverse = lax.rsqrt(jnp.mean(x * x, axis=-1, keepdims=True) + epsilon)
+    part = jnp.sum(grad * x * inverse, axis=0, keepdims=True)
+
+    @pl.when(pl.program_id(0) == 0)
+    def _():
+        gain_out[...] = jnp.zeros_like(gain_out)
+
+    gain_out[...] += part
+    scaled = grad * gain[...]
+    out[...] = (
+        resid[...]
+        + inverse * scaled
+        - x * (inverse * inverse * inverse) * jnp.mean(scaled * x, axis=-1, keepdims=True)
+    ).astype(bf16)
+
+
+def finish(grads, weights, shard, core, near, x, resid, gain, tile=256):
+    groups = len(grads)
+    rows, d = x.shape
+    c = weights[0].shape[1]
+    tiles = rows // tile
+    row = lambda i, f: (i, 0)
+    once = pl.Buffered(1)
+    return pl.pallas_call(
+        functools.partial(finish_kernel, groups=groups),
+        out_shape=[pltpu.HBM((rows, d), bf16), jax.ShapeDtypeStruct((1, d), f32)],
+        grid_spec=pltpu.PrefetchScalarGridSpec(
+            num_scalar_prefetch=1,
+            grid=(tiles,),
+            in_specs=[pl.BlockSpec((tile, c), lambda i, f: (f[0] * tiles + i, 0))] * groups
+            + [pl.BlockSpec((d, c), lambda i, f: (0, 0), pipeline_mode=once)] * groups
+            + [
+                pl.BlockSpec((1, tile, d), lambda i, f: (1, i, 0)),
+                pl.BlockSpec((1, tile, d), lambda i, f: (0, i, 0)),
+                pl.BlockSpec((tile, d), row),
+                pl.BlockSpec((tile, d), row),
+                pl.BlockSpec((1, d), lambda i, f: (0, 0)),
+            ],
+            out_specs=[pl.BlockSpec((tile, d), row), pl.BlockSpec((1, d), lambda i, f: (0, 0))],
+        ),
+        compiler_params=pltpu.CompilerParams(vmem_limit_bytes=40 << 20),
+        cost_estimate=CHEAP,
+        name="finish",
+    )(shard.reshape(1), *grads, *weights, core, near, x, resid, gain)
 
 
 def rms_inverse(values):
@@ -1087,7 +1204,9 @@
 
         lefts = (after(attended, pieces[1]), normed_mlp, active)
         rights = (grad_proj, grad_hidden, grad_mlp)
-        from_core = send(share(lefts, rights, 1 - gc), core_mate)
+        shared = share(lefts, rights, 1 - gc)
+        from_core = send(shared, core_mate)
+        pieces[2:] = [after(piece, shared) for piece in pieces[2:]]
         home_out = send(after(layer_out, *pieces[1:]), to_home)
         prepared = prep(pieces, att_float, mine, nh)
         summed = keep(lefts, rights, after(from_core, prepared), gc)
@@ -1099,14 +1218,6 @@
             return attn_bwd(
                 q_aug, keyval, after(prepared, summed, *others), seg_row, scale_row, nh, group, groups
             )
-
-        def gather(block):
-            for mate in (near_mate, x_mate):
-                block = jnp.concatenate([block, send(block, mate)])
-            return block, send(block, core_mate)
-
-        def far_sum(part):
-            return (part.astype(f32) + send(part, far_mate).astype(f32)).astype(bf16)[None]
 
         def by_rows(grad):
             if pair:
@@ -1122,44 +1233,64 @@
         layer_out = jnp.where(still, after(layer_out, grad_a), home_out)
         rows_a = by_rows(after(grad_a, layer_out))
         grad_b, lanes_b = backward(1, rows_a[0])
-        rows_a[0] = after(rows_a[0], grad_b)
-        sum_a = total(rows_a)
-        block_a = far_sum(sum_a)
-
-        def shard_grad(shard, *others):
-            return sum(
-                times_trans(rows_at(after(grad, *others), shard * rows, rows), w)
-                for grad, w in zip((grad_a, grad_b), flat_w)
-            )
-
-        to_core = jnp.stack([shard_grad(mine ^ 3, sum_a), shard_grad(mine ^ 1, sum_a)]).astype(bf16)
-        from_core = send(to_core, core_mate).astype(f32)
-        rows_b = by_rows(after(grad_b, to_core))
-        to_near = (shard_grad(mine ^ 2, rows_b[0]) + from_core[0]).astype(bf16)
-        grad_normed = shard_grad(mine, rows_b[0]) + from_core[1]
-        from_near = send(to_near, near_mate).astype(f32)
+        last_step = [grad_b]
+
+        def turn(value):
+            return after(value, *last_step)
+
+        def done(value):
+            last_step[0] = value
+            return value
+
+        grads = (grad_a, grad_b)
+        rows_a[0] = turn(rows_a[0])
+        a1 = done(total([rows_a]))
+        a1_far = send(a1, far_mate)
+        to_core = done(back((grad_a, turn(grad_b)), flat_w, jnp.stack([mine ^ 3, mine ^ 1]), rows))
+        from_core = send(to_core, core_mate)
         sources = sizes["wt"] * 4
-        tail_sum = total(
-            [after(kept, rows_b[0], to_near).reshape(sources, D // sources, -1)]
+        t1 = done(total([[turn(kept).reshape(sources, D // sources, -1)]]))
+        t1_far = send(t1, far_mate)
+        to_near = done(back(grads, flat_w, (mine ^ 2).reshape(1), rows, turn(from_core)))
+        from_near = send(to_near, near_mate)
+        rows_b = by_rows(turn(grad_b))
+        done(rows_b[0])
+        a2 = done(add(turn(a1), a1_far))
+        a2_near = send(a2, near_mate)
+        rows_b[0] = turn(rows_b[0])
+        b1 = done(total([rows_b]))
+        b1_far = send(b1, far_mate)
+        t2 = done(add(turn(t1), t1_far))
+        t2_near = send(t2, near_mate)
+        a4 = done(pair_up(turn(a2), a2_near))
+        a4_x = send(a4, x_mate)
+        a4_core = send(a4, core_mate)
+        grad_tokens, grad_gain_attn = finish(
+            grads, flat_w, mine, from_core, turn(from_near), inputs, grad_resid, gain_attn[None]
         )
-        block = far_sum(tail_sum)
-        rows_b[0] = after(rows_b[0], block_a)
-        sum_b = total(rows_b)
-        block_b = far_sum(sum_b)
-        grad_normed = grad_normed + from_near
-        inputs = inputs.astype(f32)
-        inverse_attn = rms_inverse(inputs)
-        grad_gain_attn = jnp.sum(grad_normed * inputs * inverse_attn, axis=0)
-        grad_tokens = move(
-            (grad_resid + norm_back(inputs, inverse_attn, grad_normed * gain_attn)).astype(bf16),
-            to_home,
-            still,
+        done(grad_tokens)
+        home_grad = send(grad_tokens, to_home)
+        t4 = done(pair_up(turn(t2), t2_near))
+        t4_x = send(t4, x_mate)
+        t4_core = send(t4, core_mate)
+        b2 = done(add(turn(b1), b1_far))
+        b2_near = send(b2, near_mate)
+        a4_x = done(turn(a4_x))
+        a4_cross = send(a4_x, core_mate)
+        b4 = done(pair_up(turn(b2), b2_near))
+        b4_x = send(b4, x_mate)
+        b4_core = send(b4, core_mate)
+        grad_tokens = done(jnp.where(still, turn(grad_tokens), home_grad))
+        t4_x = done(turn(t4_x))
+        t4_cross = send(t4_x, core_mate)
+        b4_x = done(turn(b4_x))
+        b4_cross = send(b4_x, core_mate)
+        at = jnp.stack([gx, near, gc])
+        totals = place_tail((turn(t4), t4_x, t4_core, t4_cross), at)
+        done(totals[0])
+        total_qkv = spread(
+            [(turn(a4), a4_x, a4_core, a4_cross), (b4, b4_x, b4_core, b4_cross)], at, 3 * nh // groups * HD
         )
-
-        total_qkv = spread(
-            [gather(block_a), gather(block_b)], jnp.stack([gx, near, gc]), 3 * nh // groups * HD
-        )
-        totals = place_tail(*gather(block), jnp.stack([gx, near, gc]))
 
         grad_query_scale = (
             (lanes_a + lanes_b)[0, :HD]
@@ -1168,7 +1299,7 @@
             * jax.nn.sigmoid(query_scale)
         )
         small = jnp.concatenate(
-            [grad_gain_attn, grad_gain_mlp[0], jnp.pad(grad_query_scale, (0, LN - HD))]
+            [grad_gain_attn[0], grad_gain_mlp[0], jnp.pad(grad_query_scale, (0, LN - HD))]
         ).reshape(-1, LN)
         small = sum_all(small).reshape(-1)
         return (

time: 530 us -> 485 us (0.915)
  starting transfers between devices: 103 us -> 72.3 us
  waiting for transfers between devices: 171 us -> 152 us
  Pallas kernels: 204 us -> 219 us
  matrix products: 12.3 us -> 0 us
  local copies, waits for them, and re-layouts: 11.2 us -> 18.9 us
  other arithmetic: 19.6 us -> 13.6 us
    ppermute x46 -> x49, starting transfers between devices: 98.5 us -> 64.3 us  [send(): return lax.ppermute(value, AXES, pairs(target))]
    pallas_call x4 -> x13, Pallas kernels: 13.3 us -> 37.7 us  [the longest x2 8.84 us: back(): pl.pallas_call(functools.partial(back_kernel, groups=groups, extra=got is...]
    ppermute x46 -> x49, waiting for transfers between devices: 171 us -> 152 us  [send(): return lax.ppermute(value, AXES, pairs(target))]
    dot_general x8 -> x0, matrix products: 12.3 us -> none  [times_trans(): lax.dot_general(left, right, (((1,), (1,)), ((), ())), preferred_element_...]
    unnamed x76 -> x86, local copies, waits for them, and re-layouts: 5.4 us -> 13.1 us
  transfers between devices with their start and end apart: 47 -> 50, of which waited for: 19 -> 21; matrix products, arithmetic and copies ran while one was open for 7% -> 4% of each run, Pallas kernels for 31% -> 37%
where the time goes in v6:
time: 485 us; the launch traced here: 478 us
  Pallas kernels  219 us (45%)
  waiting for transfers between devices  152 us (31%)
  starting transfers between devices  72.3 us (15%)
  local copies, waits for them, and re-layouts  18.9 us (4%)
  other arithmetic  13.6 us (3%)
    ppermute x49, waiting for transfers between devices, send(): return lax.ppermute(value, AXES, pairs(target))  152 us
    ppermute x49, starting transfers between devices, send(): return lax.ppermute(value, AXES, pairs(target))  64.3 us
    pallas_call x2, Pallas kernels, attn_bwd(): pl.pallas_call(functools.partial(bwd_kernel, nh=nh, bq=bq, bk=bk, n=n), o...  47.8 us
    pallas_call x3, Pallas kernels, project(): pl.pallas_call(functools.partial(project_kernel, count=count, halves=len(...  27.3 us
    pallas_call x1, Pallas kernels, attn_fwd(): pl.pallas_call(functools.partial(fwd_kernel, nh=nh, bq=bq, bk=bk, nk=n //...  26 us
    pallas_call x1, Pallas kernels, tail(): pl.pallas_call(body, out_shape=[pltpu.HBM((rows, d), bf16)] * 6 + [pltpu....  21.9 us
    unnamed x86, local copies, waits for them, and re-layouts  13.1 us
    pallas_call x2, Pallas kernels, cross(): pl.pallas_call(cross_kernel, out_shape=[pltpu.HBM((w // 2, g.shape[1]), b...  10.6 us
  transfers between devices with their start and end apart: 50, of which 21 were waited for; matrix products, arithmetic and copies ran while one was open for 4% of the time, Pallas kernels for 37%

profile of v6, /device:TPU:0, one launch (start us, length us, event | category | flops | bytes accessed | tf_op | source)
XLA Modules:
  0.0 477.5 jit_solution(15372727810896227429)
XLA Ops:
  0.7 4.6 pick.1.x_ref.a_ref
  9.6 5.4 %collective-permute-start.4 = (bf16[512,1280]{1,0:T(8,128)(2,1)S(1)}, bf16[512,1280]{1,0:T(8,128)(2,1)}, u32[]{:S(2)}, u32[]{:S(2)}) collective-permute-start(bf16[512,1280]{1,0:T(8,128)(2,1)S(1)} %bitcast.68), channel_id=1, source_target_pairs={{0,8},{1,9},{2,10},{3,11},{12,4},{13,5},{14,6},{15,7},{16,24},{17,... | collective-permute-start | bytes 3932168 | tf_op jit(solution)/shard_map/ppermute | solution.py:1032
  15.7 4.7 pad_maximum_fusion.own
  20.4 5.5 %collective-permute-done.1.refs_2_ = bf16[512,1280]{1,0:T(8,128)(2,1)} collective-permute-done((bf16[512,1280]{1,0:T(8,128)(2,1)S(1)}, bf16[512,1280]{1,0:T(8,128)(2,1)}, u32[]{:S(2)}, u32[]{:S(2)}) %collective-permute-start.1) | collective-permute-done | bytes 1310752 | tf_op jit(solution)/shard_map/ppermute | solution.py:1032
  38.6 7.0 %collective-permute-done.2.refs_0_ = bf16[512,1280]{1,0:T(8,128)(2,1)S(1)} collective-permute-done((bf16[512,1280]{1,0:T(8,128)(2,1)}, bf16[512,1280]{1,0:T(8,128)(2,1)S(1)}, u32[]{:S(2)}, u32[]{:S(2)}) %collective-permute-start.2) | collective-permute-done | bytes 1310752 | tf_op jit(solution)/shard_map/ppermute | solution.py:1032
  57.1 11.2 %project.3 = (bf16[2048,1280]{1,0:T(8,128)(2,1)}, bf16[2048,512]{1,0:T(8,128)(2,1)}, bf16[2048,1024]{1,0:T(8,128)(2,1)}, bf16[512,1280]{1,0:T(8,128)(2,1)}) custom-call(s32[5]{0:T(128)S(1)} %stack.103.info, bf16[512,1280]{1,0:T(8,128)(2,1)S(1)} %bitcast.70, bf16[512,1280]{1,0:T(8,128)(2,1)} %collective-permute-done.4.refs_1_, ...), custom_call_target="tpu_custom_call" | custom-call | flops 10000000000 | bytes 1000 | tf_op jit(solution)/shard_map/project/pallas_call | solution.py:522
  73.8 7.9 %project.4 = (bf16[2048,1280]{1,0:T(8,128)(2,1)}, bf16[2048,512]{1,0:T(8,128)(2,1)}, bf16[2048,1024]{1,0:T(8,128)(2,1)}, bf16[512,1280]{1,0:T(8,128)(2,1)}) custom-call(s32[4]{0:T(128)S(1)} %add_add_fusion.1.info, bf16[512,1280]{1,0:T(8,128)(2,1)S(1)} %collective-permute-done.2.refs_0_, ...), custom_call_target="tpu_custom_call", output_to_operand_aliasing={{0}: (9, {}), {1}: (10, {}), {2}: (11, {})} | custom-call | flops 10000000000 | bytes 1000 | tf_op jit(solution)/shard_map/project/pallas_call | solution.py:522
  81.8 8.2 %project.5 = (bf16[2048,1280]{1,0:T(8,128)(2,1)}, bf16[2048,512]{1,0:T(8,128)(2,1)}, bf16[2048,1024]{1,0:T(8,128)(2,1)}, bf16[512,1280]{1,0:T(8,128)(2,1)}) custom-call(s32[4]{0:T(128)S(1)} %add_add_fusion.info, bf16[512,1280]{1,0:T(8,128)(2,1)} %collective-permute-done.3.refs_0_, ...), custom_call_target="tpu_custom_call", output_to_operand_aliasing={{0}: (9, {}), {1}: (10, {}), {2}: (11, {})} | custom-call | flops 10000000000 | bytes 1000 | tf_op jit(solution)/shard_map/project/pallas_call | solution.py:522
  90.0 26.0 %attn_fwd.1 = (bf16[2048,320]{1,0:T(8,128)(2,1)}, bf16[2048,512]{1,0:T(8,128)(2,1)}, bf16[2048,512]{1,0:T(8,128)(2,1)}) custom-call(s32[16]{0:T(128)S(1)} %reshape.171.flags, bf16[2048,512]{1,0:T(8,128)(2,1)} %get-tuple-element.107.q_ref, bf16[2048,1024]{1,0:T(8,128)(2,1)} %get-tuple-element.108.kv.kk.vv, s32[2048,1]{1,0:T(8,128)S(1)} %copy.29.segc, ...), custom_call_target="tpu_custom_call" | custom-call | flops 10000000 | bytes 1000 | tf_op jit(solution)/shard_map/attn_fwd/pallas_call | solution.py:168
  126.6 5.3 %collective-permute-done.11.p2 = bf16[512,320]{1,0:T(8,128)(2,1)S(1)} collective-permute-done((bf16[512,320]{1,0:T(8,128)(2,1)S(1)}, bf16[512,320]{1,0:T(8,128)(2,1)S(1)}, u32[]{:S(2)}, u32[]{:S(2)}) %collective-permute-start.11) | collective-permute-done | bytes 327712 | tf_op jit(solution)/shard_map/ppermute | solution.py:1032
  131.9 8.0 %collective-permute-done.12.p3 = bf16[512,320]{1,0:T(8,128)(2,1)S(1)} collective-permute-done((bf16[512,320]{1,0:T(8,128)(2,1)S(1)}, bf16[512,320]{1,0:T(8,128)(2,1)S(1)}, u32[]{:S(2)}, u32[]{:S(2)}) %collective-permute-start.12) | collective-permute-done | bytes 327712 | tf_op jit(solution)/shard_map/ppermute | solution.py:1032
  139.9 21.9 %tail.1 = (bf16[512,1280]{1,0:T(8,128)(2,1)}, bf16[512,1280]{1,0:T(8,128)(2,1)}, bf16[512,1280]{1,0:T(8,128)(2,1)}, bf16[512,1280]{1,0:T(8,128)(2,1)}, bf16[512,...) custom-call(s32[4]{0:T(128)S(1)} %pad_add_fusion.at, ...), custom_call_target="tpu_custom_call" | custom-call | flops 10000000 | bytes 1000 | tf_op jit(solution)/shard_map/tail/pallas_call | solution.py:631
  164.2 7.8 %share.1 = bf16[1280,1920]{1,0:T(8,128)(2,1)} custom-call(s32[1]{0:T(128)} %bitcast.21.col, bf16[512,1280]{1,0:T(8,128)(2,1)} %get-tuple-element.124.l0, bf16[512,1280]{1,0:T(8,128)(2,1)} %get-tuple-element.125.l1, bf16[512,1280]{1,0:T(8,128)(2,1)} %get-tuple-element.126.l2, bf16[512,1280]{1,0:T(8,128)(2,1)} %get-tuple-element.127.r0, ...), custom_call_target="tpu_custom_call" | custom-call | flops 10000000 | bytes 1000 | tf_op jit(solution)/shard_map/share/pallas_call | solution.py:667
  173.4 8.7 %collective-permute-done.16.do2 = bf16[512,320]{1,0:T(8,128)(2,1)S(1)} collective-permute-done((bf16[512,320]{1,0:T(8,128)(2,1)}, bf16[512,320]{1,0:T(8,128)(2,1)S(1)}, u32[]{:S(2)}, u32[]{:S(2)}) %collective-permute-start.16) | collective-permute-done | bytes 327712 | tf_op jit(solution)/shard_map/ppermute | solution.py:1032
  183.8 7.5 %prep.1.doa_s = bf16[2048,512]{1,0:T(8,128)(2,1)} custom-call(s32[1]{0:T(128)} %bitcast.mine.shard, bf16[512,320]{1,0:T(8,128)(2,1)S(1)} %copy-done.21, bf16[512,320]{1,0:T(8,128)(2,1)S(1)} %collective-permute-done.15.do1, bf16[512,320]{1,0:T(8,128)(2,1)S(1)} %collective-permute-done.16.do2, bf16[512,320]{1,0:T(8,128)(2,1)S(1)} %collective-permute-done.17.do3, ...), custom_call_target="tpu_custom_call" | custom-call | flops 999999995904 | bytes 1000 | tf_op jit(solution)/shard_map/prep/pallas_call | solution.py:278
  191.3 9.0 %keep.1 = bf16[1280,1920]{1,0:T(8,128)(2,1)} custom-call(s32[1]{0:T(128)} %bitcast.22.col, bf16[512,1280]{1,0:T(8,128)(2,1)} %get-tuple-element.124.l0, bf16[512,1280]{1,0:T(8,128)(2,1)} %get-tuple-element.125.l1, bf16[512,1280]{1,0:T(8,128)(2,1)} %get-tuple-element.126.l2, bf16[512,1280]{1,0:T(8,128)(2,1)} %get-tuple-element.127.r0, ...), custom_call_target="tpu_custom_call" | custom-call | flops 10000000 | bytes 1000 | tf_op jit(solution)/shard_map/keep/pallas_call | solution.py:699
  200.3 8.0 %all-to-all-start = ((bf16[8,160,1920]{2,1,0:T(8,128)(2,1)}), bf16[8,160,1920]{2,1,0:T(8,128)(2,1)}, u32[]{:S(2)}, u32[]{:S(2)}) async-start(bf16[8,160,1920]{2,1,0:T(8,128)(2,1)} %bitcast.83), calls=%async_computation | async-start | bytes 9830400 | tf_op jit(solution)/shard_map/all_to_all | solution.py:1213
  208.4 23.9 %attn_bwd.2 = (bf16[2048,512]{1,0:T(8,128)(2,1)}, f32[8,128]{1,0:T(8,128)}) custom-call(s32[16]{0:T(128)S(1)} %copy-done.20, bf16[2048,512]{1,0:T(8,128)(2,1)} %get-tuple-element.119.qa, bf16[2048,1024]{1,0:T(8,128)(2,1)} %get-tuple-element.108.kv.kk.vv, bf16[2048,1024]{1,0:T(8,128)(2,1)} %get-tuple-element.108.kv.kk.vv, bf16[2048,512]{1,0:T(8,128)(2,1)} %prep.1.doa_s, ...), custom_call_target="tpu_custom_call" | custom-call | flops 299999985664 | bytes 1000 | tf_op jit(solution)/shard_map/attn_bwd/pallas_call | solution.py:327
  237.4 5.3 %cross.2 = (bf16[320,512]{1,0:T(8,128)(2,1)}, bf16[320,512]{1,0:T(8,128)(2,1)}, bf16[320,512]{1,0:T(8,128)(2,1)}, bf16[320,512]{1,0:T(8,128)(2,1)}) custom-call(s32[2]{0:T(128)S(1)} %pad_add_fusion.1.at, bf16[2048,1280]{1,0:T(8,128)(2,1)S(1)} %copy-done.4, bf16[2048,512]{1,0:T(8,128)(2,1)S(1)} %copy-done), custom_call_target="tpu_custom_call" | custom-call | flops 1000000 | bytes 1000 | tf_op jit(solution)/shard_map/cross/pallas_call | solution.py:832
  246.3 23.9 %attn_bwd.3 = (bf16[2048,512]{1,0:T(8,128)(2,1)}, f32[8,128]{1,0:T(8,128)}) custom-call(s32[16]{0:T(128)S(1)} %copy-done.20, bf16[2048,512]{1,0:T(8,128)(2,1)} %get-tuple-element.119.qa, bf16[2048,1024]{1,0:T(8,128)(2,1)} %get-tuple-element.108.kv.kk.vv, bf16[2048,1024]{1,0:T(8,128)(2,1)} %get-tuple-element.108.kv.kk.vv, bf16[2048,512]{1,0:T(8,128)(2,1)} %prep.1.doa_s, ...), custom_call_target="tpu_custom_call" | custom-call | flops 1000000 | bytes 1000 | tf_op jit(solution)/shard_map/attn_bwd/pallas_call | solution.py:327
  270.2 9.4 %collective-permute-done.20 = bf16[320,512]{1,0:T(8,128)(2,1)S(1)} collective-permute-done((bf16[320,512]{1,0:T(8,128)(2,1)}, bf16[320,512]{1,0:T(8,128)(2,1)S(1)}, u32[]{:S(2)}, u32[]{:S(2)}) %collective-permute-start.20) | collective-permute-done | bytes 327712 | tf_op jit(solution)/shard_map/ppermute | solution.py:1032
  279.6 5.4 %collective-permute-done.22 = bf16[320,512]{1,0:T(8,128)(2,1)S(1)} collective-permute-done((bf16[320,512]{1,0:T(8,128)(2,1)}, bf16[320,512]{1,0:T(8,128)(2,1)S(1)}, u32[]{:S(2)}, u32[]{:S(2)}) %collective-permute-start.22) | collective-permute-done | bytes 327712 | tf_op jit(solution)/shard_map/ppermute | solution.py:1032
  287.4 4.7 back.2
  304.3 5.3 %cross.3 = (bf16[320,512]{1,0:T(8,128)(2,1)}, bf16[320,512]{1,0:T(8,128)(2,1)}, bf16[320,512]{1,0:T(8,128)(2,1)}, bf16[320,512]{1,0:T(8,128)(2,1)}) custom-call(s32[2]{0:T(128)S(1)} %pad_add_fusion.1.at, bf16[2048,1280]{1,0:T(8,128)(2,1)S(1)} %bitcast.66, bf16[2048,512]{1,0:T(8,128)(2,1)S(1)} %copy-done.2), custom_call_target="tpu_custom_call" | custom-call | flops 1000000 | bytes 1000 | tf_op jit(solution)/shard_map/cross/pallas_call | solution.py:832
  316.3 24.3 %collective-permute-done.25.b_ref = bf16[320,512]{1,0:T(8,128)(2,1)S(1)} collective-permute-done((bf16[320,512]{1,0:T(8,128)(2,1)S(1)}, bf16[320,512]{1,0:T(8,128)(2,1)S(1)}, u32[]{:S(2)}, u32[]{:S(2)}) %collective-permute-start.25) | collective-permute-done | bytes 327712 | tf_op jit(solution)/shard_map/ppermute | solution.py:1032
  346.5 4.8 %collective-permute-done.28 = bf16[320,512]{1,0:T(8,128)(2,1)} collective-permute-done((bf16[320,512]{1,0:T(8,128)(2,1)}, bf16[320,512]{1,0:T(8,128)(2,1)}, u32[]{:S(2)}, u32[]{:S(2)}) %collective-permute-start.28) | collective-permute-done | bytes 327712 | tf_op jit(solution)/shard_map/ppermute | solution.py:1032
  367.0 5.4 %finish.1 = (bf16[512,1280]{1,0:T(8,128)(2,1)}, f32[1,1280]{1,0:T(1,128)S(1)}) custom-call(s32[1]{0:T(128)} %bitcast.mine.shard, bf16[2048,512]{1,0:T(8,128)(2,1)S(1)} %copy-done, bf16[2048,512]{1,0:T(8,128)(2,1)S(1)} %copy-done.3, bf16[1280,512]{1,0:T(8,128)(2,1)S(1)} %copy-done.5, bf16[1280,512]{1,0:T(8,128)(2,1)S(1)} %copy-done.8, ...), custom_call_target="tpu_custom_call" | custom-call | flops 1000000 | bytes 1000 | tf_op jit(solution)/shard_map/finish/pallas_call | solution.py:963
  380.2 18.4 %collective-permute-done.31.b_ref = bf16[160,1920]{1,0:T(8,128)(2,1)S(1)} collective-permute-done((bf16[160,1920]{1,0:T(8,128)(2,1)S(1)}, bf16[160,1920]{1,0:T(8,128)(2,1)S(1)}, u32[]{:S(2)}, u32[]{:S(2)}) %collective-permute-start.31) | collective-permute-done | bytes 614432 | tf_op jit(solution)/shard_map/ppermute | solution.py:1032
  405.3 14.5 %collective-permute-done.32.b_ref = bf16[320,512]{1,0:T(8,128)(2,1)S(1)} collective-permute-done((bf16[320,512]{1,0:T(8,128)(2,1)}, bf16[320,512]{1,0:T(8,128)(2,1)S(1)}, u32[]{:S(2)}, u32[]{:S(2)}) %collective-permute-start.32) | collective-permute-done | bytes 327712 | tf_op jit(solution)/shard_map/ppermute | solution.py:1032
  422.6 9.3 %collective-permute-done.34.b_ref = bf16[320,512]{1,0:T(8,128)(2,1)} collective-permute-done((bf16[320,512]{1,0:T(8,128)(2,1)}, bf16[320,512]{1,0:T(8,128)(2,1)}, u32[]{:S(2)}, u32[]{:S(2)}) %collective-permute-start.34) | collective-permute-done | bytes 327712 | tf_op jit(solution)/shard_map/ppermute | solution.py:1032
  440.1 11.3 %collective-permute-done.44 = f32[21,128]{1,0:T(8,128)S(1)} collective-permute-done((f32[21,128]{1,0:T(8,128)S(1)}, f32[21,128]{1,0:T(8,128)S(1)}, u32[]{:S(2)}, u32[]{:S(2)}) %collective-permute-start.44) | collective-permute-done | bytes 10784 | tf_op jit(solution)/shard_map/ppermute | solution.py:1032
  471.0 6.3 %spread.1 = f32[2,320,3840]{2,1,0:T(8,128)} custom-call(s32[3]{0:T(128)S(1)} %pad_add_fusion.3.at, bf16[2,320,512]{2,1,0:T(8,128)(2,1)} %pair_up.3.refs_0_, bf16[2,320,512]{2,1,0:T(8,128)(2,1)S(1)} %collective-permute-done.33.refs_1_, bf16[2,320,512]{2,1,0:T(8,128)(2,1)S(1)} %collective-permute-done.40.refs_2_, ...), custom_call_target="tpu_custom_call" | custom-call | flops 1000000 | bytes 1000 | tf_op jit(solution)/shard_map/spread/pallas_call | solution.py:876
  (231 shorter events, 147.3 us)
Async XLA Ops:
  5.3 20.6 %collective-permute-start.1 = (bf16[512,1280]{1,0:T(8,128)(2,1)S(1)}, bf16[512,1280]{1,0:T(8,128)(2,1)}, u32[]{:S(2)}, u32[]{:S(2)}) collective-permute-start(bf16[512,1280]{1,0:T(8,128)(2,1)S(1)} %bitcast.67), channel_id=1, source_target_pairs={{2,0},{3,1},{4,2},{5,3},{6,4},{7,5},{8,10},{9,11},{10,12},{11,13},... | collective-permute-start | bytes 3932168 | tf_op jit(solution)/shard_map/ppermute | solution.py:1032
  6.6 44.1 %collective-permute-start.6 = (bf16[640,1024]{1,0:T(8,128)(2,1)}, bf16[640,1024]{1,0:T(8,128)(2,1)}, u32[]{:S(2)}, u32[]{:S(2)}) collective-permute-start(bf16[640,1024]{1,0:T(8,128)(2,1)} %pick.1.x_ref.a_ref), channel_id=1, source_target_pairs={{0,1},{1,0},{2,3},{3,2},{4,5},{5,4},{6,7},{7,6},{8,9},{9,8},{10,11... | collective-permute-start | bytes 3932168 | tf_op jit(solution)/shard_map/ppermute | solution.py:1032
  9.6 47.5 %collective-permute-start.4 = (bf16[512,1280]{1,0:T(8,128)(2,1)S(1)}, bf16[512,1280]{1,0:T(8,128)(2,1)}, u32[]{:S(2)}, u32[]{:S(2)}) collective-permute-start(bf16[512,1280]{1,0:T(8,128)(2,1)S(1)} %bitcast.68), channel_id=1, source_target_pairs={{0,8},{1,9},{2,10},{3,11},{12,4},{13,5},{14,6},{15,7},{16,24},{17,... | collective-permute-start | bytes 3932168 | tf_op jit(solution)/shard_map/ppermute | solution.py:1032
  15.0 19.7 %collective-permute-start = (s32[1,2048]{1,0:T(1,128)S(1)}, s32[1,2048]{1,0:T(1,128)S(1)}, u32[]{:S(2)}, u32[]{:S(2)}) collective-permute-start(s32[1,2048]{1,0:T(1,128)S(1)} %copy-done.32), channel_id=1, source_target_pairs={{0,8},{1,9},{2,10},{3,11},{4,12},{5,13},{6,14},{7,15},{8,0},{9,1},... | collective-permute-start | bytes 24584 | tf_op jit(solution)/shard_map/ppermute | solution.py:1032
  25.9 19.7 %collective-permute-start.2 = (bf16[512,1280]{1,0:T(8,128)(2,1)}, bf16[512,1280]{1,0:T(8,128)(2,1)S(1)}, u32[]{:S(2)}, u32[]{:S(2)}) collective-permute-start(bf16[512,1280]{1,0:T(8,128)(2,1)} %collective-permute-done.1.refs_2_), channel_id=1, source_target_pairs={{2,0},{3,1},{4,2},{5,3},{10,12},{11,13},{12,14},{13,15},{18,16},{1... | collective-permute-start | bytes 3932168 | tf_op jit(solution)/shard_map/ppermute | solution.py:1032
  36.3 20.9 %collective-permute-start.5 = (bf16[512,1280]{1,0:T(8,128)(2,1)}, bf16[512,1280]{1,0:T(8,128)(2,1)}, u32[]{:S(2)}, u32[]{:S(2)}) collective-permute-start(bf16[512,1280]{1,0:T(8,128)(2,1)} %collective-permute-done.1.refs_2_), channel_id=1, source_target_pairs={{0,8},{1,9},{2,10},{3,11},{12,4},{13,5},{14,6},{15,7},{16,24},{17,... | collective-permute-start | bytes 3932168 | tf_op jit(solution)/shard_map/ppermute | solution.py:1032
  46.8 21.6 %collective-permute-start.3 = (bf16[512,1280]{1,0:T(8,128)(2,1)}, bf16[512,1280]{1,0:T(8,128)(2,1)}, u32[]{:S(2)}, u32[]{:S(2)}) collective-permute-start(bf16[512,1280]{1,0:T(8,128)(2,1)} %broadcast_select_fusion), channel_id=1, source_target_pairs={{0,2},{1,3},{2,0},{3,1},{12,14},{13,15},{14,12},{15,13},{16,18},{1... | collective-permute-start | bytes 3932168 | tf_op jit(solution)/shard_map/ppermute | solution.py:1032
  54.8 18.1 %collective-permute-start.8 = (bf16[512,1280]{1,0:T(8,128)(2,1)S(1)}, bf16[512,1280]{1,0:T(8,128)(2,1)}, u32[]{:S(2)}, u32[]{:S(2)}) collective-permute-start(bf16[512,1280]{1,0:T(8,128)(2,1)S(1)} %collective-permute-done.2.refs_0_), channel_id=1, source_target_pairs={{0,8},{1,9},{2,10},{3,11},{12,4},{13,5},{14,6},{15,7},{16,24},{17,... | collective-permute-start | bytes 3932168 | tf_op jit(solution)/shard_map/ppermute | solution.py:1032
  71.3 46.8 %collective-permute-start.13 = (bf16[3,320,1280]{2,1,0:T(8,128)(2,1)}, bf16[3,320,1280]{2,1,0:T(8,128)(2,1)}, u32[]{:S(2)}, u32[]{:S(2)}) collective-permute-start(bf16[3,320,1280]{2,1,0:T(8,128)(2,1)} %constant_dynamic-slice_fusion), channel_id=1, source_target_pairs={{0,1},{1,0},{2,3},{3,2},{4,5},{5,4},{6,7},{7,6},{8,9},{9,8},{10,11... | collective-permute-start | bytes 7372808 | tf_op jit(solution)/shard_map/ppermute | solution.py:1032
  72.9 43.0 %collective-permute-start.9 = (bf16[512,1280]{1,0:T(8,128)(2,1)}, bf16[512,1280]{1,0:T(8,128)(2,1)S(1)}, u32[]{:S(2)}, u32[]{:S(2)}) collective-permute-start(bf16[512,1280]{1,0:T(8,128)(2,1)} %bitcast.88), channel_id=1, source_target_pairs={{2,8},{3,9},{4,2},{5,3},{6,10},{7,11},{8,4},{9,5},{10,12},{11,13},... | collective-permute-start | bytes 3932168 | tf_op jit(solution)/shard_map/ppermute | solution.py:1032
  119.8 20.1 %collective-permute-start.14 = (bf16[3,320,1280]{2,1,0:T(8,128)(2,1)}, bf16[3,320,1280]{2,1,0:T(8,128)(2,1)}, u32[]{:S(2)}, u32[]{:S(2)}) collective-permute-start(bf16[3,320,1280]{2,1,0:T(8,128)(2,1)} %collective-permute-done.13.half), channel_id=1, source_target_pairs={{0,8},{1,9},{2,10},{3,11},{4,12},{5,13},{6,14},{7,15},{8,0},{9,1},... | collective-permute-start | bytes 7372808 | tf_op jit(solution)/shard_map/ppermute | solution.py:1032
  121.9 18.0 %collective-permute-start.12 = (bf16[512,320]{1,0:T(8,128)(2,1)S(1)}, bf16[512,320]{1,0:T(8,128)(2,1)S(1)}, u32[]{:S(2)}, u32[]{:S(2)}) collective-permute-start(bf16[512,320]{1,0:T(8,128)(2,1)S(1)} %get-tuple-element.183), channel_id=1, source_target_pairs={{0,10},{1,11},{2,8},{3,9},{4,14},{5,15},{6,12},{7,13},{8,2},{9,3},... | collective-permute-start | bytes 983048 | tf_op jit(solution)/shard_map/ppermute | solution.py:1032
  163.6 18.5 %collective-permute-start.16 = (bf16[512,320]{1,0:T(8,128)(2,1)}, bf16[512,320]{1,0:T(8,128)(2,1)S(1)}, u32[]{:S(2)}, u32[]{:S(2)}) collective-permute-start(bf16[512,320]{1,0:T(8,128)(2,1)} %get-tuple-element.122), channel_id=1, source_target_pairs={{0,2},{1,3},{2,0},{3,1},{4,6},{5,7},{6,4},{7,5},{8,10},{9,11},{10,... | collective-permute-start | bytes 983048 | tf_op jit(solution)/shard_map/ppermute | solution.py:1032
  172.0 19.3 %collective-permute-start.18 = (bf16[1280,1920]{1,0:T(8,128)(2,1)}, bf16[1280,1920]{1,0:T(8,128)(2,1)}, u32[]{:S(2)}, u32[]{:S(2)}) collective-permute-start(bf16[1280,1920]{1,0:T(8,128)(2,1)} %share.1), channel_id=1, source_target_pairs={{0,8},{1,9},{2,10},{3,11},{4,12},{5,13},{6,14},{7,15},{8,0},{9,1},... | collective-permute-start | bytes 14745608 | tf_op jit(solution)/shard_map/ppermute | solution.py:1032
  182.1 50.2 %collective-permute-start.19 = (bf16[512,1280]{1,0:T(8,128)(2,1)}, bf16[512,1280]{1,0:T(8,128)(2,1)}, u32[]{:S(2)}, u32[]{:S(2)}) collective-permute-start(bf16[512,1280]{1,0:T(8,128)(2,1)} %get-tuple-element.137), channel_id=1, source_target_pairs={{2,4},{3,5},{4,8},{5,9},{6,12},{7,13},{8,2},{9,3},{10,6},{11,7},{1... | collective-permute-start | bytes 3932168 | tf_op jit(solution)/shard_map/ppermute | solution.py:1032
  200.3 91.8 %all-to-all-start = ((bf16[8,160,1920]{2,1,0:T(8,128)(2,1)}), bf16[8,160,1920]{2,1,0:T(8,128)(2,1)}, u32[]{:S(2)}, u32[]{:S(2)}) async-start(bf16[8,160,1920]{2,1,0:T(8,128)(2,1)} %bitcast.83), calls=%async_computation | async-start | bytes 9830400 | tf_op jit(solution)/shard_map/all_to_all | solution.py:1213
  242.7 36.8 %collective-permute-start.20 = (bf16[320,512]{1,0:T(8,128)(2,1)}, bf16[320,512]{1,0:T(8,128)(2,1)S(1)}, u32[]{:S(2)}, u32[]{:S(2)}) collective-permute-start(bf16[320,512]{1,0:T(8,128)(2,1)} %get-tuple-element.145), channel_id=1, source_target_pairs={{0,16},{1,17},{2,18},{3,19},{4,20},{5,21},{6,22},{7,23},{8,24},{9,... | collective-permute-start | bytes 983048 | tf_op jit(solution)/shard_map/ppermute | solution.py:1032
  244.8 34.8 %collective-permute-start.21 = (bf16[320,512]{1,0:T(8,128)(2,1)}, bf16[320,512]{1,0:T(8,128)(2,1)S(1)}, u32[]{:S(2)}, u32[]{:S(2)}) collective-permute-start(bf16[320,512]{1,0:T(8,128)(2,1)} %get-tuple-element.146), channel_id=1, source_target_pairs={{0,1},{1,0},{2,3},{3,2},{4,5},{5,4},{6,7},{7,6},{8,9},{9,8},{10,11... | collective-permute-start | bytes 983048 | tf_op jit(solution)/shard_map/ppermute | solution.py:1032
  245.8 39.1 %collective-permute-start.22 = (bf16[320,512]{1,0:T(8,128)(2,1)}, bf16[320,512]{1,0:T(8,128)(2,1)S(1)}, u32[]{:S(2)}, u32[]{:S(2)}) collective-permute-start(bf16[320,512]{1,0:T(8,128)(2,1)} %get-tuple-element.147), channel_id=1, source_target_pairs={{0,17},{1,16},{2,19},{3,18},{4,21},{5,20},{6,23},{7,22},{8,25},{9,... | collective-permute-start | bytes 983048 | tf_op jit(solution)/shard_map/ppermute | solution.py:1032
  301.5 61.3 %collective-permute-start.24 = (bf16[1,512,1280]{2,1,0:T(8,128)(2,1)}, bf16[1,512,1280]{2,1,0:T(8,128)(2,1)}, u32[]{:S(2)}, u32[]{:S(2)}) collective-permute-start(bf16[1,512,1280]{2,1,0:T(8,128)(2,1)} %back.3), channel_id=1, source_target_pairs={{0,2},{1,3},{2,0},{3,1},{4,6},{5,7},{6,4},{7,5},{8,10},{9,11},{10,... | collective-permute-start | bytes 3932168 | tf_op jit(solution)/shard_map/ppermute | solution.py:1032
  304.2 36.4 %collective-permute-start.25 = (bf16[320,512]{1,0:T(8,128)(2,1)S(1)}, bf16[320,512]{1,0:T(8,128)(2,1)S(1)}, u32[]{:S(2)}, u32[]{:S(2)}) collective-permute-start(bf16[320,512]{1,0:T(8,128)(2,1)S(1)} %copy-done.26), channel_id=1, source_target_pairs={{0,4},{1,5},{2,6},{3,7},{4,0},{5,1},{6,2},{7,3},{8,12},{9,13},{10,... | collective-permute-start | bytes 983048 | tf_op jit(solution)/shard_map/ppermute | solution.py:1032
  309.5 36.9 %collective-permute-start.26 = (bf16[320,512]{1,0:T(8,128)(2,1)}, bf16[320,512]{1,0:T(8,128)(2,1)}, u32[]{:S(2)}, u32[]{:S(2)}) collective-permute-start(bf16[320,512]{1,0:T(8,128)(2,1)} %get-tuple-element.155), channel_id=1, source_target_pairs={{0,16},{1,17},{2,18},{3,19},{4,20},{5,21},{6,22},{7,23},{8,24},{9,... | collective-permute-start | bytes 983048 | tf_op jit(solution)/shard_map/ppermute | solution.py:1032
  313.1 41.2 %collective-permute-start.29 = (bf16[160,1920]{1,0:T(8,128)(2,1)}, bf16[160,1920]{1,0:T(8,128)(2,1)}, u32[]{:S(2)}, u32[]{:S(2)}) collective-permute-start(bf16[160,1920]{1,0:T(8,128)(2,1)} %total.4.a_ref), channel_id=1, source_target_pairs={{0,4},{1,5},{2,6},{3,7},{4,0},{5,1},{6,2},{7,3},{8,12},{9,13},{10,... | collective-permute-start | bytes 1843208 | tf_op jit(solution)/shard_map/ppermute | solution.py:1032
  316.0 30.5 %collective-permute-start.27 = (bf16[320,512]{1,0:T(8,128)(2,1)}, bf16[320,512]{1,0:T(8,128)(2,1)}, u32[]{:S(2)}, u32[]{:S(2)}) collective-permute-start(bf16[320,512]{1,0:T(8,128)(2,1)} %get-tuple-element.156), channel_id=1, source_target_pairs={{0,1},{1,0},{2,3},{3,2},{4,5},{5,4},{6,7},{7,6},{8,9},{9,8},{10,11... | collective-permute-start | bytes 983048 | tf_op jit(solution)/shard_map/ppermute | solution.py:1032
  372.5 64.9 %collective-permute-start.35 = (bf16[512,1280]{1,0:T(8,128)(2,1)}, bf16[512,1280]{1,0:T(8,128)(2,1)}, u32[]{:S(2)}, u32[]{:S(2)}) collective-permute-start(bf16[512,1280]{1,0:T(8,128)(2,1)} %get-tuple-element.167), channel_id=1, source_target_pairs={{2,4},{3,5},{4,8},{5,9},{6,12},{7,13},{8,2},{9,3},{10,6},{11,7},{1... | collective-permute-start | bytes 3932168 | tf_op jit(solution)/shard_map/ppermute | solution.py:1032
  374.2 24.4 %collective-permute-start.31 = (bf16[160,1920]{1,0:T(8,128)(2,1)S(1)}, bf16[160,1920]{1,0:T(8,128)(2,1)S(1)}, u32[]{:S(2)}, u32[]{:S(2)}) collective-permute-start(bf16[160,1920]{1,0:T(8,128)(2,1)S(1)} %copy-done.22), channel_id=1, source_target_pairs={{0,2},{1,3},{2,0},{3,1},{4,6},{5,7},{6,4},{7,5},{8,10},{9,11},{10,... | collective-permute-start | bytes 1843208 | tf_op jit(solution)/shard_map/ppermute | solution.py:1032
  376.2 46.4 %collective-permute-start.33 = (bf16[2,320,512]{2,1,0:T(8,128)(2,1)}, bf16[2,320,512]{2,1,0:T(8,128)(2,1)S(1)}, u32[]{:S(2)}, u32[]{:S(2)}) collective-permute-start(bf16[2,320,512]{2,1,0:T(8,128)(2,1)} %pair_up.3.refs_0_), channel_id=1, source_target_pairs={{0,16},{1,17},{2,18},{3,19},{4,20},{5,21},{6,22},{7,23},{8,24},{9,... | collective-permute-start | bytes 1966088 | tf_op jit(solution)/shard_map/ppermute | solution.py:1032
  379.7 40.1 %collective-permute-start.32 = (bf16[320,512]{1,0:T(8,128)(2,1)}, bf16[320,512]{1,0:T(8,128)(2,1)S(1)}, u32[]{:S(2)}, u32[]{:S(2)}) collective-permute-start(bf16[320,512]{1,0:T(8,128)(2,1)} %total.5.a_ref), channel_id=1, source_target_pairs={{0,4},{1,5},{2,6},{3,7},{4,0},{5,1},{6,2},{7,3},{8,12},{9,13},{10,... | collective-permute-start | bytes 983048 | tf_op jit(solution)/shard_map/ppermute | solution.py:1032
  401.8 38.0 %collective-permute-start.37 = (bf16[2,160,1920]{2,1,0:T(8,128)(2,1)}, bf16[2,160,1920]{2,1,0:T(8,128)(2,1)S(1)}, u32[]{:S(2)}, u32[]{:S(2)}) collective-permute-start(bf16[2,160,1920]{2,1,0:T(8,128)(2,1)} %pair_up.4.own), channel_id=1, source_target_pairs={{0,16},{1,17},{2,18},{3,19},{4,20},{5,21},{6,22},{7,23},{8,24},{9,... | collective-permute-start | bytes 3686408 | tf_op jit(solution)/shard_map/ppermute | solution.py:1032
  422.4 42.3 %collective-permute-start.38 = (bf16[2,160,1920]{2,1,0:T(8,128)(2,1)}, bf16[2,160,1920]{2,1,0:T(8,128)(2,1)S(1)}, u32[]{:S(2)}, u32[]{:S(2)}) collective-permute-start(bf16[2,160,1920]{2,1,0:T(8,128)(2,1)} %pair_up.4.own), channel_id=1, source_target_pairs={{0,8},{1,9},{2,10},{3,11},{4,12},{5,13},{6,14},{7,15},{8,0},{9,1},... | collective-permute-start | bytes 3686408 | tf_op jit(solution)/shard_map/ppermute | solution.py:1032
  433.8 27.6 %collective-permute-start.36 = (bf16[2,320,512]{2,1,0:T(8,128)(2,1)}, bf16[2,320,512]{2,1,0:T(8,128)(2,1)S(1)}, u32[]{:S(2)}, u32[]{:S(2)}) collective-permute-start(bf16[2,320,512]{2,1,0:T(8,128)(2,1)} %pair_up.5.refs_4_), channel_id=1, source_target_pairs={{0,16},{1,17},{2,18},{3,19},{4,20},{5,21},{6,22},{7,23},{8,24},{9,... | collective-permute-start | bytes 1966088 | tf_op jit(solution)/shard_map/ppermute | solution.py:1032
  439.8 26.6 %collective-permute-start.39 = (bf16[2,160,1920]{2,1,0:T(8,128)(2,1)S(1)}, bf16[2,160,1920]{2,1,0:T(8,128)(2,1)S(1)}, u32[]{:S(2)}, u32[]{:S(2)}) collective-permute-start(bf16[2,160,1920]{2,1,0:T(8,128)(2,1)S(1)} %collective-permute-done.37.own_x), channel_id=1, source_target_pairs={{0,8},{1,9},{2,10},{3,11},{4,12},{5,13},{6,14},{7,15},{8,0},{9,1},... | collective-permute-start | bytes 3686408 | tf_op jit(solution)/shard_map/ppermute | solution.py:1032
  (60 other events, 929.2 us)

commit v7 on v6

--- a/solution.py
+++ b/solution.py
@@ -180,15 +180,31 @@
 
 
 def bwd_kernel(
-    flags, qa, kk, vv, doa_s, segc, segr, scale, dqkv, gscale, dq_s, dk_s, dv_s, *, nh, bq, bk, n
+    flags, mine, qa, kk, vv, do0, do1, do2, do3, of, segc, segr, scale, dqkv, gscale, doa_s, dq_s, dk_s, dv_s, *, first, nh, bq, bk, n
 ):
     nk = n // bk
     nq = n // bq
     kb = pl.program_id(0)
+    part = n // 4
+    step_rows = 256 if part % 256 == 0 else part
+    lanes = lax.broadcasted_iota(jnp.int32, (step_rows, LN), 1)
 
     @pl.when(kb == 0)
     def _():
         dq_s[...] = jnp.zeros_like(dq_s)
+        for j, piece in enumerate((do0, do1, do2, do3)):
+            start = (mine[0] ^ j) * part
+            for i in range(part // step_rows):
+                d = piece[i * step_rows : (i + 1) * step_rows, :].astype(f32)
+                r = pl.ds(pl.multiple_of(start + i * step_rows, step_rows), step_rows)
+                for h in range(nh):
+                    at = (first + h) * HD
+                    dh = jnp.concatenate(
+                        [d[:, at : at + HD], jnp.zeros((step_rows, LN - HD), f32)], axis=1
+                    )
+                    c = slice(h * LN, (h + 1) * LN)
+                    delta = jnp.sum(dh * of[r, c].astype(f32), axis=1, keepdims=True)
+                    doa_s[r, c] = put_split(dh, -delta, lanes)
 
     dk_s[...] = jnp.zeros_like(dk_s)
     dv_s[...] = jnp.zeros_like(dv_s)
@@ -254,78 +270,37 @@
         gscale[...] = jnp.broadcast_to(total, gscale.shape)
 
 
-def prep_kernel(mine, do0, do1, do2, do3, of, out, *, nh):
-    tile = of.shape[0]
-    lanes = lax.broadcasted_iota(jnp.int32, (tile, LN), 1)
-    for j, piece in enumerate((do0, do1, do2, do3)):
-
-        @pl.when(pl.program_id(0) == j)
-        def _(piece=piece):
-            d = piece[...].astype(f32)
-            for h in range(nh):
-                dh = jnp.concatenate(
-                    [d[:, h * HD : (h + 1) * HD], jnp.zeros((tile, LN - HD), f32)], axis=1
-                )
-                c = slice(h * LN, (h + 1) * LN)
-                delta = jnp.sum(dh * of[:, c].astype(f32), axis=1, keepdims=True)
-                out[:, c] = put_split(dh, -delta, lanes)
-
-
-def prep(pieces, of, mine, nh, tile=256):
-    n, w = of.shape
-    per = n // 4 // tile
-    at = lambda j, i, m: ((m[0] ^ j) * per + i, 0)
-    return pl.pallas_call(
-        functools.partial(prep_kernel, nh=nh),
-        out_shape=pltpu.HBM((n, w), bf16),
-        grid_spec=pltpu.PrefetchScalarGridSpec(
-            num_scalar_prefetch=1,
-            grid=(4, per),
-            in_specs=[
-                pl.BlockSpec(
-                    (tile, nh * HD),
-                    lambda j, i, m, k=k: (jnp.where(j == k, i, jnp.where(j > k, per - 1, 0)), 0),
-                )
-                for k in range(4)
-            ]
-            + [pl.BlockSpec((tile, w), at)],
-            out_specs=pl.BlockSpec((tile, w), at),
-        ),
-        compiler_params=pltpu.CompilerParams(vmem_limit_bytes=24 << 20),
-        cost_estimate=cost(1000),
-        name="prep",
-    )(mine.reshape(1), *pieces, hbm(of))
-
-
-def attn_bwd(qa, kv, doa, seg_row, scale, heads, group, groups, bq=512, bk=512):
+def attn_bwd(qa, kv, pieces, of, mine, seg_row, scale, heads, group, groups, bq=512, bk=512):
     n = qa.shape[0]
     nh = heads // groups
     w = nh * LN
     once = pl.Buffered(1)
     spec = pltpu.PrefetchScalarGridSpec(
-        num_scalar_prefetch=1,
+        num_scalar_prefetch=2,
         grid=(n // bk,),
         in_specs=[
-            pl.BlockSpec((n, w), lambda i, f: (0, group), pipeline_mode=once),
-            pl.BlockSpec((bk, w), lambda i, f: (i, group)),
-            pl.BlockSpec((bk, w), lambda i, f: (i, groups + group)),
-            pl.BlockSpec((n, w), lambda i, f: (0, group), pipeline_mode=once),
-            pl.BlockSpec((bk, 1), lambda i, f: (i, 0)),
-            pl.BlockSpec((1, n), lambda i, f: (0, 0)),
-            pl.BlockSpec((1, nh * HD), lambda i, f: (0, 0)),
+            pl.BlockSpec((n, w), lambda i, f, m: (0, group), pipeline_mode=once),
+            pl.BlockSpec((bk, w), lambda i, f, m: (i, group)),
+            pl.BlockSpec((bk, w), lambda i, f, m: (i, groups + group)),
+            *[pl.BlockSpec((n // 4, heads * HD), lambda i, f, m: (0, 0), pipeline_mode=once)] * 4,
+            pl.BlockSpec((n, w), lambda i, f, m: (0, group), pipeline_mode=once),
+            pl.BlockSpec((bk, 1), lambda i, f, m: (i, 0)),
+            pl.BlockSpec((1, n), lambda i, f, m: (0, 0)),
+            pl.BlockSpec((1, nh * HD), lambda i, f, m: (0, 0)),
         ],
         out_specs=[
-            pl.BlockSpec((n, lanes_up(3 * nh * HD)), lambda i, f: (0, 0)),
-            pl.BlockSpec((8, LN), lambda i, f: (0, 0)),
+            pl.BlockSpec((n, lanes_up(3 * nh * HD)), lambda i, f, m: (0, 0)),
+            pl.BlockSpec((8, LN), lambda i, f, m: (0, 0)),
         ],
         scratch_shapes=[
+            pltpu.VMEM((n, w), bf16),
             pltpu.VMEM((nh, n, LN), f32),
             pltpu.VMEM((nh, bk, LN), f32),
             pltpu.VMEM((nh, bk, LN), f32),
         ],
     )
     return pl.pallas_call(
-        functools.partial(bwd_kernel, nh=nh, bq=bq, bk=bk, n=n),
+        functools.partial(bwd_kernel, first=group * nh, nh=nh, bq=bq, bk=bk, n=n),
         out_shape=[
             pltpu.HBM((n, lanes_up(3 * nh * HD)), bf16),
             pltpu.HBM((8, LN), f32),
@@ -334,7 +309,7 @@
         compiler_params=pltpu.CompilerParams(vmem_limit_bytes=48 << 20),
         cost_estimate=cost(300 if group == 0 else 0.001),
         name="attn_bwd",
-    )(block_flags(seg_row, bq, bk), hbm(qa), hbm(kv), hbm(kv), hbm(doa), seg_row[:, None], seg_row[None], scale)
+    )(block_flags(seg_row, bq, bk), mine.reshape(1), hbm(qa), hbm(kv), hbm(kv), *pieces, hbm(of), seg_row[:, None], seg_row[None], scale)
 
 
 def quarter_columns(place, parts, groups, nh):
@@ -549,7 +524,10 @@
 
 
 def tail_body(at, p0, p1, p2, p3, x_ref, g_ref, w_s, gain, outs):
-    lo_ref, att_ref, nm_ref, gh_ref, act_ref, gp_ref, gr_ref, c0, c1, c2, c3, gg_ref = outs
+    lo_ref, left_ref, right_ref, gr_ref, c0, c1, c2, c3, gg_ref = outs
+    att_ref, nm_ref, act_ref = (left_ref.at[i] for i in range(3))
+    gp_ref, gh_ref = (right_ref.at[i] for i in range(2))
+    right_ref[2] = g_ref[...]
     mine = at[0]
     pieces = (p0, p1, p2, p3)
     cols = p0.shape[1]
@@ -630,7 +608,8 @@
         scratch = []
     return pl.pallas_call(
         body,
-        out_shape=[pltpu.HBM((rows, d), bf16)] * 6
+        out_shape=[pltpu.HBM((rows, d), bf16)]
+        + [pltpu.HBM((3, rows, d), bf16)] * 2
         + [pltpu.HBM((rows, d), f32)]
         + [pltpu.HBM((rows, cols), bf16)] * 4
         + [pltpu.HBM((1, d), f32)],
@@ -638,7 +617,11 @@
             num_scalar_prefetch=1,
             grid=(rows // tile,),
             in_specs=[slim] * 4 + [wide] * 2 + [whole(*w.shape) for w in weights] + [whole(1, d)],
-            out_specs=[wide] * 7 + [slim] * 4 + [pl.BlockSpec((1, d), lambda i, m: (0, 0))],
+            out_specs=[wide]
+            + [pl.BlockSpec((3, tile, d), lambda i, m: (0, i, 0))] * 2
+            + [wide]
+            + [slim] * 4
+            + [pl.BlockSpec((1, d), lambda i, m: (0, 0))],
             scratch_shapes=scratch,
         ),
         compiler_params=pltpu.CompilerParams(vmem_limit_bytes=52 << 20),
@@ -650,67 +633,44 @@
 tn_dims = (((0,), (0,)), ((), ()))
 
 
-def share_kernel(col, l0, l1, l2, r0, r1, r2, out):
-    for i, (left, right) in enumerate(((l0, r0), (l1, r1), (l2, r2))):
-
-        @pl.when(pl.program_id(0) == i)
-        def _(left=left, right=right):
-            out[...] = lax.dot_general(
-                left[...], right[...], tn_dims, preferred_element_type=f32
-            ).astype(bf16)
-
-
-def share(lefts, rights, col):
-    rows, d = lefts[0].shape
+def share_kernel(col, left, right, *refs):
+    value = lax.dot_general(left[0], right[0], tn_dims, preferred_element_type=f32)
+    if len(refs) == 2:
+        value = value + refs[0][...].astype(f32)
+    refs[-1][...] = value.astype(bf16)
+
+
+def share(left, right, col, got=None):
+    n, rows, d = left.shape
     w = d // 2
-    once = pl.Buffered(1)
+    block = pl.BlockSpec((d, w), lambda i, c: (0, i))
     return pl.pallas_call(
         share_kernel,
-        out_shape=pltpu.HBM((d, 3 * w), bf16),
+        out_shape=pltpu.HBM((d, n * w), bf16),
         grid_spec=pltpu.PrefetchScalarGridSpec(
             num_scalar_prefetch=1,
-            grid=(3,),
-            in_specs=[pl.BlockSpec((rows, d), lambda i, c: (0, 0), pipeline_mode=once)] * 3
-            + [pl.BlockSpec((rows, w), lambda i, c: (0, c[0]), pipeline_mode=once)] * 3,
-            out_specs=pl.BlockSpec((d, w), lambda i, c: (0, i)),
-        ),
-        compiler_params=pltpu.CompilerParams(vmem_limit_bytes=40 << 20),
-        cost_estimate=cost(0.01),
-        name="share",
-    )(col.reshape(1), *map(hbm, lefts), *map(hbm, rights))
-
-
-def keep_kernel(col, l0, l1, l2, r0, r1, r2, got, out):
-    for i, (left, right) in enumerate(((l0, r0), (l1, r1), (l2, r2))):
-
-        @pl.when(pl.program_id(0) == i)
-        def _(left=left, right=right):
-            out[...] = (
-                lax.dot_general(left[...], right[...], tn_dims, preferred_element_type=f32)
-                + got[...].astype(f32)
-            ).astype(bf16)
-
-
-def keep(lefts, rights, got, col):
-    rows, d = lefts[0].shape
-    w = d // 2
-    once = pl.Buffered(1)
-    block = pl.BlockSpec((d, w), lambda i, c: (0, i))
-    return pl.pallas_call(
-        keep_kernel,
-        out_shape=pltpu.HBM((d, 3 * w), bf16),
-        grid_spec=pltpu.PrefetchScalarGridSpec(
-            num_scalar_prefetch=1,
-            grid=(3,),
-            in_specs=[pl.BlockSpec((rows, d), lambda i, c: (0, 0), pipeline_mode=once)] * 3
-            + [pl.BlockSpec((rows, w), lambda i, c: (0, c[0]), pipeline_mode=once)] * 3
-            + [block],
+            grid=(n,),
+            in_specs=[
+                pl.BlockSpec((1, rows, d), lambda i, c: (i, 0, 0)),
+                pl.BlockSpec((1, rows, w), lambda i, c: (i, 0, c[0])),
+            ]
+            + [block] * (got is not None),
             out_specs=block,
         ),
         compiler_params=pltpu.CompilerParams(vmem_limit_bytes=40 << 20),
-        cost_estimate=cost(0.01),
-        name="keep",
-    )(col.reshape(1), *map(hbm, lefts), *map(hbm, rights), hbm(got))
+        cost_estimate=CHEAP,
+        name="share",
+    )(col.reshape(1), hbm(left), hbm(right), *(() if got is None else (hbm(got),)))
+
+
+def tick_kernel(x_ref, out):
+    out[...] = x_ref[...]
+
+
+def tick(x):
+    return pl.pallas_call(
+        tick_kernel, out_shape=jax.ShapeDtypeStruct(x.shape, x.dtype), cost_estimate=cost(200.0), name="tick"
+    )(x)
 
 
 def total_kernel(*refs, counts):
@@ -750,9 +710,9 @@
     out[...] = (a_ref[...].astype(f32) + b_ref[...].astype(f32)).astype(bf16)
 
 
-def add(a, b):
-    return pl.pallas_call(
-        add_kernel, out_shape=pltpu.HBM(a.shape, bf16), cost_estimate=CHEAP, name="add"
+def add(a, b, us):
+    return pl.pallas_call(
+        add_kernel, out_shape=pltpu.HBM(a.shape, bf16), cost_estimate=cost(us), name="add"
     )(a, b)
 
 
@@ -909,7 +869,7 @@
     n = shards.shape[0]
     in_specs = [pl.BlockSpec((rows, c), lambda i, f: (f[i], 0))] * groups
     in_specs += [pl.BlockSpec((d, c), lambda i, f: (0, 0), pipeline_mode=pl.Buffered(1))] * groups
-    args = [*grads, *weights]
+    args = [*map(hbm, grads), *map(hbm, weights)]
     if got is not None:
         in_specs.append(pl.BlockSpec((1, rows, d), lambda i, f: (0, 0, 0)))
         args.append(got)
@@ -980,7 +940,7 @@
         compiler_params=pltpu.CompilerParams(vmem_limit_bytes=40 << 20),
         cost_estimate=CHEAP,
         name="finish",
-    )(shard.reshape(1), *grads, *weights, core, near, x, resid, gain)
+    )(shard.reshape(1), *map(hbm, grads), *map(hbm, weights), core, near, hbm(x), hbm(resid), gain)
 
 
 def rms_inverse(values):
@@ -1031,9 +991,6 @@
     def send(value, target):
         return lax.ppermute(value, AXES, pairs(target))
 
-    def move(value, target, still):
-        return jnp.where(still, value, send(value, target))
-
     def core_mate(gx, gc, z, w):
         return (gx, 1 - gc, z, w)
 
@@ -1056,10 +1013,10 @@
         return (1 - gx, gc, z, 1 - w)
 
     def to_host(gx, gc, z, w):
-        return (gx, z & 1, 2 * gc + (z >> 1), w)
+        return (gx, 1 - (z & 1), 2 * gc + (z >> 1), w)
 
     def to_home(gx, gc, z, w):
-        return (gx, z >> 1, 2 * (z & 1) + gc, w)
+        return (gx, z >> 1, 2 * (z & 1) + 1 - gc, w)
 
     def hop1(gx, gc, z, w):
         if gc == 0:
@@ -1098,10 +1055,10 @@
     ):
         gx, gc, host, near, wt = (lax.axis_index(axis) for axis in AXES)
         z = 2 * host + near
-        mine = 2 * near + gc
+        mine = 2 * near + 1 - gc
         parts = 4
         nh = H // parts
-        groups = 2
+        groups = 1
         rows = tokens.shape[1]
         group_len = segments.shape[1]
         wrows = w_qkv.shape[0]
@@ -1159,23 +1116,20 @@
         seg_row = jnp.where(lane, segments, seg_mate)[0]
         fixed = (lane, mine, wt, gain_attn[None], wide_w, lane_scale, ones, group_len)
         carried = project(((own, own_share), (got1, got1_share)), places[:2], *fixed)
-        got2_share = after(got2_share, carried[0])
         got3_share = send(after(got3, carried[0]), lane_share)
-        carried = project(((got2, got2_share),), places[2:3], *fixed, carried=carried)
         all_normed, queries, keyval, inputs = project(
-            ((got3, after(got3_share, carried[0])),), places[3:], *fixed, carried=carried
+            ((got2, got2_share), (got3, got3_share)), places[2:], *fixed, carried=carried
         )
-        still = lane & end
-        grad_mlp = move(after(cotangent[0], got3), to_host, still)
+        grad_mlp = send(after(cotangent[0], got3_share), to_host)
 
         att, att_float, q_aug = attn_fwd(queries, keyval, seg_row, nh)
         att = after(att, grad_mlp)
-        if pair:
-            flat_w = order(after(picked, att), other_w, wt, groups, nh)
 
         trades = (core_mate, near_mate, cross_mate)
         att_pieces = [rows_at(att, (mine ^ j) * rows, rows) for j in range(parts)]
         att_pieces = [att_pieces[0]] + [send(att_pieces[j + 1], trades[j]) for j in range(3)]
+        if pair:
+            flat_w = order(after(picked, att_pieces[1]), other_w, wt, groups, nh)
         half_mate = send(after(half_w, att_pieces[1]), core_mate)
         if pair:
             weights = (tail_own, half_w, half_mate)
@@ -1189,11 +1143,8 @@
             starts = ()
         (
             layer_out,
-            attended,
-            normed_mlp,
-            grad_hidden,
-            active,
-            grad_proj,
+            left,
+            right,
             grad_resid,
             *pieces,
             grad_gain_mlp,
@@ -1202,21 +1153,29 @@
         )
         pieces = [pieces[0]] + [send(pieces[j + 1], trades[j]) for j in range(3)]
 
-        lefts = (after(attended, pieces[1]), normed_mlp, active)
-        rights = (grad_proj, grad_hidden, grad_mlp)
-        shared = share(lefts, rights, 1 - gc)
+        shared = share(after(left, pieces[1]), right, 1 - gc)
         from_core = send(shared, core_mate)
         pieces[2:] = [after(piece, shared) for piece in pieces[2:]]
         home_out = send(after(layer_out, *pieces[1:]), to_home)
-        prepared = prep(pieces, att_float, mine, nh)
-        summed = keep(lefts, rights, after(from_core, prepared), gc)
+        late_gain = tick(after(gain_attn.reshape(-1, LN), *pieces[1:]))
+        summed = share(left, right, gc, after(from_core, late_gain))
         kept = lax.all_to_all(summed, ("wt", "gx", "near"), 0, 0, tiled=True)
 
         scale_row = jnp.tile(dim_scale, nh // groups)[None]
 
         def backward(group, *others):
+            first, *rest = pieces
             return attn_bwd(
-                q_aug, keyval, after(prepared, summed, *others), seg_row, scale_row, nh, group, groups
+                q_aug,
+                keyval,
+                (after(first, summed, *others), *rest),
+                att_float,
+                mine,
+                seg_row,
+                scale_row,
+                nh,
+                group,
+                groups,
             )
 
         def by_rows(grad):
@@ -1229,11 +1188,10 @@
             got = lax.all_to_all(part, ("wt", "gx"), 0, 0, tiled=True)
             return [got.reshape(sources, D // sources, -1)]
 
-        grad_a, lanes_a = backward(0)
-        layer_out = jnp.where(still, after(layer_out, grad_a), home_out)
-        rows_a = by_rows(after(grad_a, layer_out))
-        grad_b, lanes_b = backward(1, rows_a[0])
-        last_step = [grad_b]
+        grad_project, grad_lanes = backward(0)
+        layer_out = after(home_out, grad_project)
+
+        last_step = [layer_out]
 
         def turn(value):
             return after(value, *last_step)
@@ -1242,58 +1200,56 @@
             last_step[0] = value
             return value
 
-        grads = (grad_a, grad_b)
-        rows_a[0] = turn(rows_a[0])
-        a1 = done(total([rows_a]))
-        a1_far = send(a1, far_mate)
-        to_core = done(back((grad_a, turn(grad_b)), flat_w, jnp.stack([mine ^ 3, mine ^ 1]), rows))
-        from_core = send(to_core, core_mate)
         sources = sizes["wt"] * 4
         t1 = done(total([[turn(kept).reshape(sources, D // sources, -1)]]))
         t1_far = send(t1, far_mate)
-        to_near = done(back(grads, flat_w, (mine ^ 2).reshape(1), rows, turn(from_core)))
+        to_core = done(back((turn(grad_project),), flat_w, jnp.stack([mine ^ 3, mine ^ 1]), rows))
+        from_core = send(to_core, core_mate)
+        by_place = by_rows(turn(grad_project))
+        done(by_place[0])
+        to_near = done(back((grad_project,), flat_w, (mine ^ 2).reshape(1), rows, turn(from_core)))
         from_near = send(to_near, near_mate)
-        rows_b = by_rows(turn(grad_b))
-        done(rows_b[0])
-        a2 = done(add(turn(a1), a1_far))
-        a2_near = send(a2, near_mate)
-        rows_b[0] = turn(rows_b[0])
-        b1 = done(total([rows_b]))
-        b1_far = send(b1, far_mate)
-        t2 = done(add(turn(t1), t1_far))
+        by_place[0] = turn(by_place[0])
+        q1 = done(total([by_place]))
+        q1_far = send(q1, far_mate)
+        t2 = done(add(turn(t1), t1_far, 200))
         t2_near = send(t2, near_mate)
-        a4 = done(pair_up(turn(a2), a2_near))
-        a4_x = send(a4, x_mate)
-        a4_core = send(a4, core_mate)
         grad_tokens, grad_gain_attn = finish(
-            grads, flat_w, mine, from_core, turn(from_near), inputs, grad_resid, gain_attn[None]
+            (grad_project,),
+            flat_w,
+            mine,
+            from_core,
+            turn(from_near),
+            inputs,
+            grad_resid,
+            late_gain.reshape(1, -1),
         )
         done(grad_tokens)
         home_grad = send(grad_tokens, to_home)
         t4 = done(pair_up(turn(t2), t2_near))
         t4_x = send(t4, x_mate)
         t4_core = send(t4, core_mate)
-        b2 = done(add(turn(b1), b1_far))
-        b2_near = send(b2, near_mate)
-        a4_x = done(turn(a4_x))
-        a4_cross = send(a4_x, core_mate)
-        b4 = done(pair_up(turn(b2), b2_near))
-        b4_x = send(b4, x_mate)
-        b4_core = send(b4, core_mate)
-        grad_tokens = done(jnp.where(still, turn(grad_tokens), home_grad))
+        q2 = done(add(turn(q1), q1_far, 0.001))
+        q2_near = send(q2, near_mate)
+        q4 = done(pair_up(turn(q2), q2_near))
+        q4_x = send(q4, x_mate)
+        q4_core = send(q4, core_mate)
         t4_x = done(turn(t4_x))
         t4_cross = send(t4_x, core_mate)
-        b4_x = done(turn(b4_x))
-        b4_cross = send(b4_x, core_mate)
         at = jnp.stack([gx, near, gc])
         totals = place_tail((turn(t4), t4_x, t4_core, t4_cross), at)
         done(totals[0])
+        grad_tokens = done(turn(home_grad))
+        q4_x = done(turn(q4_x))
+        q4_cross = send(q4_x, core_mate)
         total_qkv = spread(
-            [(turn(a4), a4_x, a4_core, a4_cross), (b4, b4_x, b4_core, b4_cross)], at, 3 * nh // groups * HD
+            [(turn(q4), q4_x, q4_core, q4_cross)],
+            jnp.stack([gx, near, 1 - gc]),
+            3 * nh // groups * HD,
         )
 
         grad_query_scale = (
-            (lanes_a + lanes_b)[0, :HD]
+            grad_lanes[0, :HD]
             / (dim_scale * log2e)
             * (scale_base / math.sqrt(HD))
             * jax.nn.sigmoid(query_scale)

time: 485 us -> 497 us (1.025)
  waiting for transfers between devices: 152 us -> 194 us
  Pallas kernels: 219 us -> 203 us
  other arithmetic: 13.6 us -> 6.45 us
  starting transfers between devices: 72.3 us -> 67.2 us
    ppermute x49 -> x41, waiting for transfers between devices: 152 us -> 175 us  [send(): return lax.ppermute(value, AXES, pairs(target))]
    all_to_all x1, waiting for transfers between devices: 0.01 us -> 19.5 us  [local(): kept = lax.all_to_all(summed, ('wt', 'gx', 'near'), 0, 0, tiled=True)]
    pallas_call x6 -> x5, Pallas kernels: 94 us -> 83.9 us  [the longest x1 44.2 us: attn_bwd(): pl.pallas_call(functools.partial(bwd_kernel, first=group * nh, nh=nh, bq=...]
    select_n x3 -> x0, other arithmetic: 6.37 us -> none  [the longest x1 2.67 us: local(): layer_out = jnp.where(still, after(layer_out, grad_a), home_out)]
    pallas_call x3 -> x2, Pallas kernels: 27.3 us -> 23 us  [project(): pl.pallas_call(functools.partial(project_kernel, count=count, halves=len(...]
    unnamed x86 -> x71, local copies, waits for them, and re-layouts: 13.1 us -> 10.7 us
    ppermute x49 -> x41, starting transfers between devices: 64.3 us -> 62 us  [send(): return lax.ppermute(value, AXES, pairs(target))]
    pallas_call x2 -> x1, Pallas kernels: 10.6 us -> 8.57 us  [cross(): pl.pallas_call(cross_kernel, out_shape=[pltpu.HBM((w // 2, g.shape[1]), b...]
  transfers between devices with their start and end apart: 50 -> 42, of which waited for: 21 -> 23; matrix products, arithmetic and copies ran while one was open for 4% -> 3% of each run, Pallas kernels for 37% -> 32%
where the time goes in v7:
time: 497 us; the launch traced here: 490 us
  Pallas kernels  203 us (41%)
  waiting for transfers between devices  194 us (39%)
  starting transfers between devices  67.2 us (14%)
  local copies, waits for them, and re-layouts  18 us (4%)
  other arithmetic  6.45 us (1%)
    ppermute x41, waiting for transfers between devices, send(): return lax.ppermute(value, AXES, pairs(target))  175 us
    ppermute x41, starting transfers between devices, send(): return lax.ppermute(value, AXES, pairs(target))  62 us
    pallas_call x1, Pallas kernels, attn_bwd(): pl.pallas_call(functools.partial(bwd_kernel, first=group * nh, nh=nh, bq=...  44.2 us
    pallas_call x1, Pallas kernels, attn_fwd(): pl.pallas_call(functools.partial(fwd_kernel, nh=nh, bq=bq, bk=bk, nk=n //...  25.7 us
    pallas_call x2, Pallas kernels, project(): pl.pallas_call(functools.partial(project_kernel, count=count, halves=len(...  23 us
    pallas_call x1, Pallas kernels, tail(): pl.pallas_call(body, out_shape=[pltpu.HBM((rows, d), bf16)] + [pltpu.HBM(...  22 us
    all_to_all x1, waiting for transfers between devices, local(): kept = lax.all_to_all(summed, ('wt', 'gx', 'near'), 0, 0, tiled=True)  19.5 us
    pallas_call x2, Pallas kernels, share(): pl.pallas_call(share_kernel, out_shape=pltpu.HBM((d, n * w), bf16), grid_...  16.3 us
  transfers between devices with their start and end apart: 42, of which 23 were waited for; matrix products, arithmetic and copies ran while one was open for 3% of the time, Pallas kernels for 32%

profile of v7, /device:TPU:0, one launch (start us, length us, event | category | flops | bytes accessed | tf_op | source)
XLA Modules:
  0.0 489.9 jit_solution(6209276281075147465)
XLA Ops:
  0.7 4.5 pick.1.x_ref.a_ref
  6.5 19.3 %collective-permute-done.1.refs_2_ = bf16[512,1280]{1,0:T(8,128)(2,1)} collective-permute-done((bf16[512,1280]{1,0:T(8,128)(2,1)S(1)}, bf16[512,1280]{1,0:T(8,128)(2,1)}, u32[]{:S(2)}, u32[]{:S(2)}) %collective-permute-start.1) | collective-permute-done | bytes 1310752 | tf_op jit(solution)/shard_map/ppermute | solution.py:992
  39.7 5.8 %collective-permute-done.2.refs_0_ = bf16[512,1280]{1,0:T(8,128)(2,1)S(1)} collective-permute-done((bf16[512,1280]{1,0:T(8,128)(2,1)}, bf16[512,1280]{1,0:T(8,128)(2,1)S(1)}, u32[]{:S(2)}, u32[]{:S(2)}) %collective-permute-start.2) | collective-permute-done | bytes 1310752 | tf_op jit(solution)/shard_map/ppermute | solution.py:992
  50.6 5.3 %collective-permute-done.7.x_ref.b_ref = bf16[640,1024]{1,0:T(8,128)(2,1)} collective-permute-done((bf16[640,1024]{1,0:T(8,128)(2,1)}, bf16[640,1024]{1,0:T(8,128)(2,1)}, u32[]{:S(2)}, u32[]{:S(2)}) %collective-permute-start.7) | collective-permute-done | bytes 1310752 | tf_op jit(solution)/shard_map/ppermute | solution.py:992
  60.1 11.4 %project.2 = (bf16[2048,1280]{1,0:T(8,128)(2,1)}, bf16[2048,512]{1,0:T(8,128)(2,1)}, bf16[2048,1024]{1,0:T(8,128)(2,1)}, bf16[512,1280]{1,0:T(8,128)(2,1)}) custom-call(s32[5]{0:T(128)S(1)} %stack.101.info, bf16[512,1280]{1,0:T(8,128)(2,1)S(1)} %bitcast.70, bf16[512,1280]{1,0:T(8,128)(2,1)} %collective-permute-done.5.refs_1_, ...), custom_call_target="tpu_custom_call" | custom-call | flops 10000000000 | bytes 1000 | tf_op jit(solution)/shard_map/project/pallas_call | solution.py:497
  86.5 11.6 %project.3 = (bf16[2048,1280]{1,0:T(8,128)(2,1)}, bf16[2048,512]{1,0:T(8,128)(2,1)}, bf16[2048,1024]{1,0:T(8,128)(2,1)}, bf16[512,1280]{1,0:T(8,128)(2,1)}) custom-call(s32[5]{0:T(128)S(1)} %stack.98.info, bf16[512,1280]{1,0:T(8,128)(2,1)S(1)} %collective-permute-done.2.refs_0_, ...), custom_call_target="tpu_custom_call", output_to_operand_aliasing={{0}: (11, {}), {1}: (12, {}), {2}: (13, {})} | custom-call | flops 10000000000 | bytes 1000 | tf_op jit(solution)/shard_map/project/pallas_call | solution.py:497
  98.1 25.7 %attn_fwd.1 = (bf16[2048,320]{1,0:T(8,128)(2,1)}, bf16[2048,512]{1,0:T(8,128)(2,1)}, bf16[2048,512]{1,0:T(8,128)(2,1)}) custom-call(s32[16]{0:T(128)S(1)} %reshape.178.flags, bf16[2048,512]{1,0:T(8,128)(2,1)} %get-tuple-element.79.q_ref, bf16[2048,1024]{1,0:T(8,128)(2,1)} %get-tuple-element.80.kv.kk.vv, s32[2048,1]{1,0:T(8,128)S(1)} %copy.26.segc, ...), custom_call_target="tpu_custom_call" | custom-call | flops 10000000 | bytes 1000 | tf_op jit(solution)/shard_map/attn_fwd/pallas_call | solution.py:168
  125.4 6.4 %collective-permute-start.10 = (bf16[512,320]{1,0:T(8,128)(2,1)S(1)}, bf16[512,320]{1,0:T(8,128)(2,1)S(1)}, u32[]{:S(2)}, u32[]{:S(2)}) collective-permute-start(bf16[512,320]{1,0:T(8,128)(2,1)S(1)} %get-tuple-element.141), channel_id=1, source_target_pairs={{0,8},{1,9},{2,10},{3,11},{4,12},{5,13},{6,14},{7,15},{8,0},{9,1},... | collective-permute-start | bytes 983048 | tf_op jit(solution)/shard_map/ppermute | solution.py:992
  133.5 7.1 %collective-permute-start.11 = (bf16[512,320]{1,0:T(8,128)(2,1)S(1)}, bf16[512,320]{1,0:T(8,128)(2,1)S(1)}, u32[]{:S(2)}, u32[]{:S(2)}) collective-permute-start(bf16[512,320]{1,0:T(8,128)(2,1)S(1)} %get-tuple-element.140), channel_id=1, source_target_pairs={{0,2},{1,3},{2,0},{3,1},{4,6},{5,7},{6,4},{7,5},{8,10},{9,11},{10,... | collective-permute-start | bytes 983048 | tf_op jit(solution)/shard_map/ppermute | solution.py:992
  145.1 5.5 %collective-permute-done.11.p2 = bf16[512,320]{1,0:T(8,128)(2,1)S(1)} collective-permute-done((bf16[512,320]{1,0:T(8,128)(2,1)S(1)}, bf16[512,320]{1,0:T(8,128)(2,1)S(1)}, u32[]{:S(2)}, u32[]{:S(2)}) %collective-permute-start.11) | collective-permute-done | bytes 327712 | tf_op jit(solution)/shard_map/ppermute | solution.py:992
  150.6 8.1 %collective-permute-done.12.p3 = bf16[512,320]{1,0:T(8,128)(2,1)S(1)} collective-permute-done((bf16[512,320]{1,0:T(8,128)(2,1)S(1)}, bf16[512,320]{1,0:T(8,128)(2,1)S(1)}, u32[]{:S(2)}, u32[]{:S(2)}) %collective-permute-start.12) | collective-permute-done | bytes 327712 | tf_op jit(solution)/shard_map/ppermute | solution.py:992
  158.6 22.0 %tail.1 = (bf16[512,1280]{1,0:T(8,128)(2,1)}, bf16[3,512,1280]{2,1,0:T(8,128)(2,1)}, bf16[3,512,1280]{2,1,0:T(8,128)(2,1)}, f32[512,1280]{1,0:T(8,128)}, bf16[51...) custom-call(s32[4]{0:T(128)S(1)} %pad_add_fusion.at, ...), custom_call_target="tpu_custom_call" | custom-call | flops 10000000 | bytes 1000 | tf_op jit(solution)/shard_map/tail/pallas_call | solution.py:609
  183.0 7.4 %share.2 = bf16[1280,1920]{1,0:T(8,128)(2,1)} custom-call(s32[1]{0:T(128)} %bitcast.21.col, bf16[3,512,1280]{2,1,0:T(8,128)(2,1)} %get-tuple-element.93.left, bf16[3,512,1280]{2,1,0:T(8,128)(2,1)} %get-tuple-element.94.right), custom_call_target="tpu_custom_call" | custom-call | flops 1000000 | bytes 1000 | tf_op jit(solution)/shard_map/share/pallas_call | solution.py:647
  192.1 8.8 %collective-permute-done.16.do2 = bf16[512,320]{1,0:T(8,128)(2,1)S(1)} collective-permute-done((bf16[512,320]{1,0:T(8,128)(2,1)}, bf16[512,320]{1,0:T(8,128)(2,1)S(1)}, u32[]{:S(2)}, u32[]{:S(2)}) %collective-permute-start.16) | collective-permute-done | bytes 327712 | tf_op jit(solution)/shard_map/ppermute | solution.py:992
  203.8 8.9 %share.3 = bf16[1280,1920]{1,0:T(8,128)(2,1)} custom-call(s32[1]{0:T(128)} %bitcast.22.col, bf16[3,512,1280]{2,1,0:T(8,128)(2,1)} %get-tuple-element.93.left, bf16[3,512,1280]{2,1,0:T(8,128)(2,1)} %get-tuple-element.94.right, bf16[1280,1920]{1,0:T(8,128)(2,1)} %collective-permute-done.19.refs_0_), custom_call_target="tpu_custom_call" | custom-call | flops 1000000 | bytes 1000 | tf_op jit(solution)/shard_map/share/pallas_call | solution.py:647
  212.8 5.2 %all-to-all-start = ((bf16[8,160,1920]{2,1,0:T(8,128)(2,1)}), bf16[8,160,1920]{2,1,0:T(8,128)(2,1)}, u32[]{:S(2)}, u32[]{:S(2)}) async-start(bf16[8,160,1920]{2,1,0:T(8,128)(2,1)} %bitcast.81), calls=%async_computation | async-start | bytes 9830400 | tf_op jit(solution)/shard_map/all_to_all | solution.py:1162
  218.0 44.2 %attn_bwd.1 = (bf16[2048,1024]{1,0:T(8,128)(2,1)}, f32[8,128]{1,0:T(8,128)}) custom-call(s32[16]{0:T(128)S(1)} %copy-done.9, s32[1]{0:T(128)} %bitcast.mine.shard, bf16[2048,512]{1,0:T(8,128)(2,1)} %get-tuple-element.99.qa, bf16[2048,1024]{1,0:T(8,128)(2,1)} %get-tuple-element.80.kv.kk.vv, bf16[2048,1024]{1,0:T(8,128)(2,1)} %get-tuple-element.80.kv.kk.vv, ...), custom_call_target="tpu_custom_call" | custom-call | flops 299999985664 | bytes 1000 | tf_op jit(solution)/shard_map/attn_bwd/pallas_call | solution.py:302
  262.2 19.5 %all-to-all-done = bf16[8,160,1920]{2,1,0:T(8,128)(2,1)} async-done(((bf16[8,160,1920]{2,1,0:T(8,128)(2,1)}), bf16[8,160,1920]{2,1,0:T(8,128)(2,1)}, u32[]{:S(2)}, u32[]{:S(2)}) %all-to-all-start) | async-done | bytes 4915232 | tf_op jit(solution)/shard_map/all_to_all | solution.py:1162
  285.2 7.1 %back.2 = bf16[2,512,1280]{2,1,0:T(8,128)(2,1)} custom-call(s32[2]{0:T(128)S(1)} %pad_add_fusion.1.shards, bf16[2048,1024]{1,0:T(8,128)(2,1)} %get-tuple-element.110.refs_0_.g_ref, bf16[1280,1024]{1,0:T(8,128)(2,1)} %order.1.refs_1_), custom_call_target="tpu_custom_call" | custom-call | flops 1000000 | bytes 1000 | tf_op jit(solution)/shard_map/back/pallas_call | solution.py:876
  297.1 8.6 %cross.1 = (bf16[320,1024]{1,0:T(8,128)(2,1)}, bf16[320,1024]{1,0:T(8,128)(2,1)}, bf16[320,1024]{1,0:T(8,128)(2,1)}, bf16[320,1024]{1,0:T(8,128)(2,1)}) custom-call(s32[2]{0:T(128)S(1)} %pad_add_fusion.2.at, bf16[2048,1280]{1,0:T(8,128)(2,1)S(1)} %copy-done.2, bf16[2048,1024]{1,0:T(8,128)(2,1)S(1)} %copy-done), custom_call_target="tpu_custom_call" | custom-call | flops 1000000 | bytes 1000 | tf_op jit(solution)/shard_map/cross/pallas_call | solution.py:792
  305.6 6.4 %collective-permute-start.22 = (bf16[320,1024]{1,0:T(8,128)(2,1)}, bf16[320,1024]{1,0:T(8,128)(2,1)S(1)}, u32[]{:S(2)}, u32[]{:S(2)}) collective-permute-start(bf16[320,1024]{1,0:T(8,128)(2,1)} %get-tuple-element.114), channel_id=1, source_target_pairs={{0,16},{1,17},{2,18},{3,19},{4,20},{5,21},{6,22},{7,23},{8,24},{9,... | collective-permute-start | bytes 1966088 | tf_op jit(solution)/shard_map/ppermute | solution.py:992
  315.7 4.7 back.3
  322.9 5.0 %collective-permute-done.22 = bf16[320,1024]{1,0:T(8,128)(2,1)S(1)} collective-permute-done((bf16[320,1024]{1,0:T(8,128)(2,1)}, bf16[320,1024]{1,0:T(8,128)(2,1)S(1)}, u32[]{:S(2)}, u32[]{:S(2)}) %collective-permute-start.22) | collective-permute-done | bytes 655392 | tf_op jit(solution)/shard_map/ppermute | solution.py:992
  327.8 15.3 %collective-permute-done.23 = bf16[320,1024]{1,0:T(8,128)(2,1)S(1)} collective-permute-done((bf16[320,1024]{1,0:T(8,128)(2,1)}, bf16[320,1024]{1,0:T(8,128)(2,1)S(1)}, u32[]{:S(2)}, u32[]{:S(2)}) %collective-permute-start.23) | collective-permute-done | bytes 655392 | tf_op jit(solution)/shard_map/ppermute | solution.py:992
  350.2 28.6 %collective-permute-done.21.refs_3_ = bf16[1,512,1280]{2,1,0:T(8,128)(2,1)} collective-permute-done((bf16[1,512,1280]{2,1,0:T(8,128)(2,1)}, bf16[1,512,1280]{2,1,0:T(8,128)(2,1)}, u32[]{:S(2)}, u32[]{:S(2)}) %collective-permute-start.21) | collective-permute-done | bytes 1310752 | tf_op jit(solution)/shard_map/ppermute | solution.py:992
  378.9 6.8 %finish.1 = (bf16[512,1280]{1,0:T(8,128)(2,1)}, f32[1,1280]{1,0:T(1,128)S(1)}) custom-call(s32[1]{0:T(128)} %bitcast.mine.shard, bf16[2048,1024]{1,0:T(8,128)(2,1)} %get-tuple-element.110.refs_0_.g_ref, bf16[1280,1024]{1,0:T(8,128)(2,1)} %order.1.refs_1_, bf16[2,512,1280]{2,1,0:T(8,128)(2,1)S(1)} %collective-permute-done.20.refs_2_, ...), custom_call_target="tpu_custom_call" | custom-call | flops 1000000 | bytes 1000 | tf_op jit(solution)/shard_map/finish/pallas_call | solution.py:923
  385.6 5.1 %collective-permute-done.27.b_ref = bf16[160,1920]{1,0:T(8,128)(2,1)} collective-permute-done((bf16[160,1920]{1,0:T(8,128)(2,1)}, bf16[160,1920]{1,0:T(8,128)(2,1)}, u32[]{:S(2)}, u32[]{:S(2)}) %collective-permute-start.27) | collective-permute-done | bytes 614432 | tf_op jit(solution)/shard_map/ppermute | solution.py:992
  398.8 27.7 %collective-permute-done.30.b_ref = bf16[320,1024]{1,0:T(8,128)(2,1)S(1)} collective-permute-done((bf16[320,1024]{1,0:T(8,128)(2,1)}, bf16[320,1024]{1,0:T(8,128)(2,1)S(1)}, u32[]{:S(2)}, u32[]{:S(2)}) %collective-permute-start.30) | collective-permute-done | bytes 655392 | tf_op jit(solution)/shard_map/ppermute | solution.py:992
  436.3 5.8 %place_tail.1 = (f32[4,160,1280]{2,1,0:T(8,128)}, f32[4,160,1280]{2,1,0:T(8,128)}, f32[4,160,1280]{2,1,0:T(8,128)}) custom-call(s32[3]{0:T(128)S(1)} %pad_add_fusion.3.at, bf16[2,160,1920]{2,1,0:T(8,128)(2,1)S(1)} %copy-done.3, bf16[2,160,1920]{2,1,0:T(8,128)(2,1)} %collective-permute-done.28.own_x, bf16[2,160,1920]{2,1,0:T(8,128)(2,1)S(1)} %collective-permute-done.31.mate, ...), custom_call_target="tpu_custom_call" | custom-call | flops 1000000 | bytes 1000 | tf_op jit(solution)/shard_map/place_tail/pallas_call | solution.py:758
  442.1 16.9 %collective-permute-done.33.refs_1_ = bf16[2,320,1024]{2,1,0:T(8,128)(2,1)} collective-permute-done((bf16[2,320,1024]{2,1,0:T(8,128)(2,1)}, bf16[2,320,1024]{2,1,0:T(8,128)(2,1)}, u32[]{:S(2)}, u32[]{:S(2)}) %collective-permute-start.33) | collective-permute-done | bytes 1310752 | tf_op jit(solution)/shard_map/ppermute | solution.py:992
  464.9 4.6 collective-permute-done.38
  478.1 6.5 %spread.1 = f32[2,320,3840]{2,1,0:T(8,128)} custom-call(s32[3]{0:T(128)S(1)} %pad_add_fusion.5.at, bf16[2,320,1024]{2,1,0:T(8,128)(2,1)S(1)} %copy-done.1, bf16[2,320,1024]{2,1,0:T(8,128)(2,1)} %collective-permute-done.33.refs_1_, bf16[2,320,1024]{2,1,0:T(8,128)(2,1)} %collective-permute-done.34.refs_2_, ...), custom_call_target="tpu_custom_call" | custom-call | flops 1000000 | bytes 1000 | tf_op jit(solution)/shard_map/spread/pallas_call | solution.py:836
  (189 shorter events, 112.6 us)
Async XLA Ops:
  5.2 20.6 %collective-permute-start.1 = (bf16[512,1280]{1,0:T(8,128)(2,1)S(1)}, bf16[512,1280]{1,0:T(8,128)(2,1)}, u32[]{:S(2)}, u32[]{:S(2)}) collective-permute-start(bf16[512,1280]{1,0:T(8,128)(2,1)S(1)} %bitcast.67), channel_id=1, source_target_pairs={{2,0},{3,1},{4,2},{5,3},{6,4},{7,5},{8,10},{9,11},{10,12},{11,13},... | collective-permute-start | bytes 3932168 | tf_op jit(solution)/shard_map/ppermute | solution.py:992
  25.8 19.7 %collective-permute-start.2 = (bf16[512,1280]{1,0:T(8,128)(2,1)}, bf16[512,1280]{1,0:T(8,128)(2,1)S(1)}, u32[]{:S(2)}, u32[]{:S(2)}) collective-permute-start(bf16[512,1280]{1,0:T(8,128)(2,1)} %collective-permute-done.1.refs_2_), channel_id=1, source_target_pairs={{2,0},{3,1},{4,2},{5,3},{10,12},{11,13},{12,14},{13,15},{18,16},{1... | collective-permute-start | bytes 3932168 | tf_op jit(solution)/shard_map/ppermute | solution.py:992
  27.1 28.9 %collective-permute-start.7 = (bf16[640,1024]{1,0:T(8,128)(2,1)}, bf16[640,1024]{1,0:T(8,128)(2,1)}, u32[]{:S(2)}, u32[]{:S(2)}) collective-permute-start(bf16[640,1024]{1,0:T(8,128)(2,1)} %pick.1.x_ref.a_ref), channel_id=1, source_target_pairs={{0,1},{1,0},{2,3},{3,2},{4,5},{5,4},{6,7},{7,6},{8,9},{9,8},{10,11... | collective-permute-start | bytes 3932168 | tf_op jit(solution)/shard_map/ppermute | solution.py:992
  29.1 30.9 %collective-permute-start.5 = (bf16[512,1280]{1,0:T(8,128)(2,1)S(1)}, bf16[512,1280]{1,0:T(8,128)(2,1)}, u32[]{:S(2)}, u32[]{:S(2)}) collective-permute-start(bf16[512,1280]{1,0:T(8,128)(2,1)S(1)} %bitcast.68), channel_id=1, source_target_pairs={{0,8},{1,9},{2,10},{3,11},{12,4},{13,5},{14,6},{15,7},{16,24},{17,... | collective-permute-start | bytes 3932168 | tf_op jit(solution)/shard_map/ppermute | solution.py:992
  31.5 52.4 %collective-permute-start = (s32[1,2048]{1,0:T(1,128)S(1)}, s32[1,2048]{1,0:T(1,128)S(1)}, u32[]{:S(2)}, u32[]{:S(2)}) collective-permute-start(s32[1,2048]{1,0:T(1,128)S(1)} %copy-done.26), channel_id=1, source_target_pairs={{0,8},{1,9},{2,10},{3,11},{4,12},{5,13},{6,14},{7,15},{8,0},{9,1},... | collective-permute-start | bytes 24584 | tf_op jit(solution)/shard_map/ppermute | solution.py:992
  36.2 23.8 %collective-permute-start.6 = (bf16[512,1280]{1,0:T(8,128)(2,1)}, bf16[512,1280]{1,0:T(8,128)(2,1)}, u32[]{:S(2)}, u32[]{:S(2)}) collective-permute-start(bf16[512,1280]{1,0:T(8,128)(2,1)} %collective-permute-done.1.refs_2_), channel_id=1, source_target_pairs={{0,8},{1,9},{2,10},{3,11},{12,4},{13,5},{14,6},{15,7},{16,24},{17,... | collective-permute-start | bytes 3932168 | tf_op jit(solution)/shard_map/ppermute | solution.py:992
  46.7 24.8 %collective-permute-start.4 = (bf16[512,1280]{1,0:T(8,128)(2,1)}, bf16[512,1280]{1,0:T(8,128)(2,1)}, u32[]{:S(2)}, u32[]{:S(2)}) collective-permute-start(bf16[512,1280]{1,0:T(8,128)(2,1)} %broadcast_select_fusion), channel_id=1, source_target_pairs={{0,2},{1,3},{2,0},{3,1},{12,14},{13,15},{14,12},{15,13},{16,18},{1... | collective-permute-start | bytes 3932168 | tf_op jit(solution)/shard_map/ppermute | solution.py:992
  71.5 13.9 %collective-permute-start.8 = (bf16[512,1280]{1,0:T(8,128)(2,1)}, bf16[512,1280]{1,0:T(8,128)(2,1)}, u32[]{:S(2)}, u32[]{:S(2)}) collective-permute-start(bf16[512,1280]{1,0:T(8,128)(2,1)} %collective-permute-done.4.refs_2_), channel_id=1, source_target_pairs={{0,8},{1,9},{2,10},{3,11},{12,4},{13,5},{14,6},{15,7},{16,24},{17,... | collective-permute-start | bytes 3932168 | tf_op jit(solution)/shard_map/ppermute | solution.py:992
  82.4 50.4 %collective-permute-start.13 = (bf16[3,320,1280]{2,1,0:T(8,128)(2,1)}, bf16[3,320,1280]{2,1,0:T(8,128)(2,1)}, u32[]{:S(2)}, u32[]{:S(2)}) collective-permute-start(bf16[3,320,1280]{2,1,0:T(8,128)(2,1)} %constant_dynamic-slice_fusion), channel_id=1, source_target_pairs={{0,1},{1,0},{2,3},{3,2},{4,5},{5,4},{6,7},{7,6},{8,9},{9,8},{10,11... | collective-permute-start | bytes 7372808 | tf_op jit(solution)/shard_map/ppermute | solution.py:992
  85.4 38.4 %collective-permute-start.9 = (bf16[512,1280]{1,0:T(8,128)(2,1)}, bf16[512,1280]{1,0:T(8,128)(2,1)}, u32[]{:S(2)}, u32[]{:S(2)}) collective-permute-start(bf16[512,1280]{1,0:T(8,128)(2,1)} %bitcast.94), channel_id=1, source_target_pairs={{0,8},{1,9},{2,0},{3,1},{4,10},{5,11},{6,2},{7,3},{8,12},{9,13},{1... | collective-permute-start | bytes 3932168 | tf_op jit(solution)/shard_map/ppermute | solution.py:992
  133.1 25.5 %collective-permute-start.14 = (bf16[3,320,1280]{2,1,0:T(8,128)(2,1)}, bf16[3,320,1280]{2,1,0:T(8,128)(2,1)}, u32[]{:S(2)}, u32[]{:S(2)}) collective-permute-start(bf16[3,320,1280]{2,1,0:T(8,128)(2,1)} %collective-permute-done.13.half), channel_id=1, source_target_pairs={{0,8},{1,9},{2,10},{3,11},{4,12},{5,13},{6,14},{7,15},{8,0},{9,1},... | collective-permute-start | bytes 7372808 | tf_op jit(solution)/shard_map/ppermute | solution.py:992
  133.5 17.1 %collective-permute-start.11 = (bf16[512,320]{1,0:T(8,128)(2,1)S(1)}, bf16[512,320]{1,0:T(8,128)(2,1)S(1)}, u32[]{:S(2)}, u32[]{:S(2)}) collective-permute-start(bf16[512,320]{1,0:T(8,128)(2,1)S(1)} %get-tuple-element.140), channel_id=1, source_target_pairs={{0,2},{1,3},{2,0},{3,1},{4,6},{5,7},{6,4},{7,5},{8,10},{9,11},{10,... | collective-permute-start | bytes 983048 | tf_op jit(solution)/shard_map/ppermute | solution.py:992
  140.6 18.0 %collective-permute-start.12 = (bf16[512,320]{1,0:T(8,128)(2,1)S(1)}, bf16[512,320]{1,0:T(8,128)(2,1)S(1)}, u32[]{:S(2)}, u32[]{:S(2)}) collective-permute-start(bf16[512,320]{1,0:T(8,128)(2,1)S(1)} %get-tuple-element.139), channel_id=1, source_target_pairs={{0,10},{1,11},{2,8},{3,9},{4,14},{5,15},{6,12},{7,13},{8,2},{9,3},... | collective-permute-start | bytes 983048 | tf_op jit(solution)/shard_map/ppermute | solution.py:992
  180.8 11.3 %collective-permute-start.17 = (bf16[512,320]{1,0:T(8,128)(2,1)}, bf16[512,320]{1,0:T(8,128)(2,1)S(1)}, u32[]{:S(2)}, u32[]{:S(2)}) collective-permute-start(bf16[512,320]{1,0:T(8,128)(2,1)} %get-tuple-element.96), channel_id=1, source_target_pairs={{0,10},{1,11},{2,8},{3,9},{4,14},{5,15},{6,12},{7,13},{8,2},{9,3},... | collective-permute-start | bytes 983048 | tf_op jit(solution)/shard_map/ppermute | solution.py:992
  182.3 18.5 %collective-permute-start.16 = (bf16[512,320]{1,0:T(8,128)(2,1)}, bf16[512,320]{1,0:T(8,128)(2,1)S(1)}, u32[]{:S(2)}, u32[]{:S(2)}) collective-permute-start(bf16[512,320]{1,0:T(8,128)(2,1)} %get-tuple-element.91), channel_id=1, source_target_pairs={{0,2},{1,3},{2,0},{3,1},{4,6},{5,7},{6,4},{7,5},{8,10},{9,11},{10,... | collective-permute-start | bytes 983048 | tf_op jit(solution)/shard_map/ppermute | solution.py:992
  190.4 13.4 %collective-permute-start.19 = (bf16[1280,1920]{1,0:T(8,128)(2,1)}, bf16[1280,1920]{1,0:T(8,128)(2,1)}, u32[]{:S(2)}, u32[]{:S(2)}) collective-permute-start(bf16[1280,1920]{1,0:T(8,128)(2,1)} %share.2), channel_id=1, source_target_pairs={{0,8},{1,9},{2,10},{3,11},{4,12},{5,13},{6,14},{7,15},{8,0},{9,1},... | collective-permute-start | bytes 14745608 | tf_op jit(solution)/shard_map/ppermute | solution.py:992
  202.2 60.1 %collective-permute-start.18 = (bf16[512,1280]{1,0:T(8,128)(2,1)}, bf16[512,1280]{1,0:T(8,128)(2,1)}, u32[]{:S(2)}, u32[]{:S(2)}) collective-permute-start(bf16[512,1280]{1,0:T(8,128)(2,1)} %get-tuple-element.98), channel_id=1, source_target_pairs={{0,2},{1,3},{2,6},{3,7},{4,10},{5,11},{6,14},{7,15},{8,0},{9,1},{1... | collective-permute-start | bytes 3932168 | tf_op jit(solution)/shard_map/ppermute | solution.py:992
  212.8 69.0 %all-to-all-start = ((bf16[8,160,1920]{2,1,0:T(8,128)(2,1)}), bf16[8,160,1920]{2,1,0:T(8,128)(2,1)}, u32[]{:S(2)}, u32[]{:S(2)}) async-start(bf16[8,160,1920]{2,1,0:T(8,128)(2,1)} %bitcast.81), calls=%async_computation | async-start | bytes 9830400 | tf_op jit(solution)/shard_map/all_to_all | solution.py:1162
  292.3 23.3 %collective-permute-start.20 = (bf16[2,512,1280]{2,1,0:T(8,128)(2,1)}, bf16[2,512,1280]{2,1,0:T(8,128)(2,1)S(1)}, u32[]{:S(2)}, u32[]{:S(2)}) collective-permute-start(bf16[2,512,1280]{2,1,0:T(8,128)(2,1)} %back.2), channel_id=1, source_target_pairs={{0,8},{1,9},{2,10},{3,11},{4,12},{5,13},{6,14},{7,15},{8,0},{9,1},... | collective-permute-start | bytes 7864328 | tf_op jit(solution)/shard_map/ppermute | solution.py:992
  305.6 22.2 %collective-permute-start.22 = (bf16[320,1024]{1,0:T(8,128)(2,1)}, bf16[320,1024]{1,0:T(8,128)(2,1)S(1)}, u32[]{:S(2)}, u32[]{:S(2)}) collective-permute-start(bf16[320,1024]{1,0:T(8,128)(2,1)} %get-tuple-element.114), channel_id=1, source_target_pairs={{0,16},{1,17},{2,18},{3,19},{4,20},{5,21},{6,22},{7,23},{8,24},{9,... | collective-permute-start | bytes 1966088 | tf_op jit(solution)/shard_map/ppermute | solution.py:992
  312.1 31.1 %collective-permute-start.23 = (bf16[320,1024]{1,0:T(8,128)(2,1)}, bf16[320,1024]{1,0:T(8,128)(2,1)S(1)}, u32[]{:S(2)}, u32[]{:S(2)}) collective-permute-start(bf16[320,1024]{1,0:T(8,128)(2,1)} %get-tuple-element.115), channel_id=1, source_target_pairs={{0,1},{1,0},{2,3},{3,2},{4,5},{5,4},{6,7},{7,6},{8,9},{9,8},{10,11... | collective-permute-start | bytes 1966088 | tf_op jit(solution)/shard_map/ppermute | solution.py:992
  313.5 29.7 %collective-permute-start.24 = (bf16[320,1024]{1,0:T(8,128)(2,1)}, bf16[320,1024]{1,0:T(8,128)(2,1)S(1)}, u32[]{:S(2)}, u32[]{:S(2)}) collective-permute-start(bf16[320,1024]{1,0:T(8,128)(2,1)} %get-tuple-element.116), channel_id=1, source_target_pairs={{0,17},{1,16},{2,19},{3,18},{4,21},{5,20},{6,23},{7,22},{8,25},{9,... | collective-permute-start | bytes 1966088 | tf_op jit(solution)/shard_map/ppermute | solution.py:992
  313.5 30.7 %collective-permute-start.25 = (bf16[160,1920]{1,0:T(8,128)(2,1)S(1)}, bf16[160,1920]{1,0:T(8,128)(2,1)}, u32[]{:S(2)}, u32[]{:S(2)}) collective-permute-start(bf16[160,1920]{1,0:T(8,128)(2,1)S(1)} %copy-done.22), channel_id=1, source_target_pairs={{0,4},{1,5},{2,6},{3,7},{4,0},{5,1},{6,2},{7,3},{8,12},{9,13},{10,... | collective-permute-start | bytes 1843208 | tf_op jit(solution)/shard_map/ppermute | solution.py:992
  320.4 58.5 %collective-permute-start.21 = (bf16[1,512,1280]{2,1,0:T(8,128)(2,1)}, bf16[1,512,1280]{2,1,0:T(8,128)(2,1)}, u32[]{:S(2)}, u32[]{:S(2)}) collective-permute-start(bf16[1,512,1280]{2,1,0:T(8,128)(2,1)} %back.3), channel_id=1, source_target_pairs={{0,2},{1,3},{2,0},{3,1},{4,6},{5,7},{6,4},{7,5},{8,10},{9,11},{10,... | collective-permute-start | bytes 3932168 | tf_op jit(solution)/shard_map/ppermute | solution.py:992
  346.6 44.1 %collective-permute-start.27 = (bf16[160,1920]{1,0:T(8,128)(2,1)}, bf16[160,1920]{1,0:T(8,128)(2,1)}, u32[]{:S(2)}, u32[]{:S(2)}) collective-permute-start(bf16[160,1920]{1,0:T(8,128)(2,1)} %add.137.a_ref), channel_id=1, source_target_pairs={{0,2},{1,3},{2,0},{3,1},{4,6},{5,7},{6,4},{7,5},{8,10},{9,11},{10,... | collective-permute-start | bytes 1843208 | tf_op jit(solution)/shard_map/ppermute | solution.py:992
  346.6 47.9 %collective-permute-start.29 = (bf16[320,1024]{1,0:T(8,128)(2,1)S(1)}, bf16[320,1024]{1,0:T(8,128)(2,1)}, u32[]{:S(2)}, u32[]{:S(2)}) collective-permute-start(bf16[320,1024]{1,0:T(8,128)(2,1)S(1)} %copy-done.17), channel_id=1, source_target_pairs={{0,4},{1,5},{2,6},{3,7},{4,0},{5,1},{6,2},{7,3},{8,12},{9,13},{10,... | collective-permute-start | bytes 1966088 | tf_op jit(solution)/shard_map/ppermute | solution.py:992
  393.1 37.0 %collective-permute-start.28 = (bf16[2,160,1920]{2,1,0:T(8,128)(2,1)}, bf16[2,160,1920]{2,1,0:T(8,128)(2,1)}, u32[]{:S(2)}, u32[]{:S(2)}) collective-permute-start(bf16[2,160,1920]{2,1,0:T(8,128)(2,1)} %pair_up.2.own), channel_id=1, source_target_pairs={{0,16},{1,17},{2,18},{3,19},{4,20},{5,21},{6,22},{7,23},{8,24},{9,... | collective-permute-start | bytes 3686408 | tf_op jit(solution)/shard_map/ppermute | solution.py:992
  396.7 29.7 %collective-permute-start.30 = (bf16[320,1024]{1,0:T(8,128)(2,1)}, bf16[320,1024]{1,0:T(8,128)(2,1)S(1)}, u32[]{:S(2)}, u32[]{:S(2)}) collective-permute-start(bf16[320,1024]{1,0:T(8,128)(2,1)} %add.138.a_ref), channel_id=1, source_target_pairs={{0,2},{1,3},{2,0},{3,1},{4,6},{5,7},{6,4},{7,5},{8,10},{9,11},{10,... | collective-permute-start | bytes 1966088 | tf_op jit(solution)/shard_map/ppermute | solution.py:992
  396.7 45.4 %collective-permute-start.26 = (bf16[512,1280]{1,0:T(8,128)(2,1)}, bf16[512,1280]{1,0:T(8,128)(2,1)}, u32[]{:S(2)}, u32[]{:S(2)}) collective-permute-start(bf16[512,1280]{1,0:T(8,128)(2,1)} %get-tuple-element.120), channel_id=1, source_target_pairs={{0,2},{1,3},{2,6},{3,7},{4,10},{5,11},{6,14},{7,15},{8,0},{9,1},{1... | collective-permute-start | bytes 3932168 | tf_op jit(solution)/shard_map/ppermute | solution.py:992
  429.7 29.3 %collective-permute-start.33 = (bf16[2,320,1024]{2,1,0:T(8,128)(2,1)}, bf16[2,320,1024]{2,1,0:T(8,128)(2,1)}, u32[]{:S(2)}, u32[]{:S(2)}) collective-permute-start(bf16[2,320,1024]{2,1,0:T(8,128)(2,1)} %pair_up.3.refs_0_), channel_id=1, source_target_pairs={{0,16},{1,17},{2,18},{3,19},{4,20},{5,21},{6,22},{7,23},{8,24},{9,... | collective-permute-start | bytes 3932168 | tf_op jit(solution)/shard_map/ppermute | solution.py:992
  430.6 47.4 %collective-permute-start.34 = (bf16[2,320,1024]{2,1,0:T(8,128)(2,1)}, bf16[2,320,1024]{2,1,0:T(8,128)(2,1)}, u32[]{:S(2)}, u32[]{:S(2)}) collective-permute-start(bf16[2,320,1024]{2,1,0:T(8,128)(2,1)} %pair_up.3.refs_0_), channel_id=1, source_target_pairs={{0,8},{1,9},{2,10},{3,11},{4,12},{5,13},{6,14},{7,15},{8,0},{9,1},... | collective-permute-start | bytes 3932168 | tf_op jit(solution)/shard_map/ppermute | solution.py:992
  459.0 19.0 %collective-permute-start.35 = (bf16[2,320,1024]{2,1,0:T(8,128)(2,1)}, bf16[2,320,1024]{2,1,0:T(8,128)(2,1)S(1)}, u32[]{:S(2)}, u32[]{:S(2)}) collective-permute-start(bf16[2,320,1024]{2,1,0:T(8,128)(2,1)} %collective-permute-done.33.refs_1_), channel_id=1, source_target_pairs={{0,8},{1,9},{2,10},{3,11},{4,12},{5,13},{6,14},{7,15},{8,0},{9,1},... | collective-permute-start | bytes 3932168 | tf_op jit(solution)/shard_map/ppermute | solution.py:992
  (43 other events, 530.1 us)

commit v8 on v7

--- a/solution.py
+++ b/solution.py
@@ -518,7 +518,7 @@
         ),
         input_output_aliases=aliases,
         compiler_params=pltpu.CompilerParams(vmem_limit_bytes=48 << 20),
-        cost_estimate=cost(10),
+        cost_estimate=cost(15),
         name="project",
     )(info, *args)
 
@@ -663,6 +663,12 @@
     )(col.reshape(1), hbm(left), hbm(right), *(() if got is None else (hbm(got),)))
 
 
+def copy(x):
+    return pl.pallas_call(
+        tick_kernel, out_shape=pltpu.HBM(x.shape, x.dtype), cost_estimate=CHEAP, name="copy"
+    )(x)
+
+
 def tick_kernel(x_ref, out):
     out[...] = x_ref[...]
 
@@ -710,9 +716,9 @@
     out[...] = (a_ref[...].astype(f32) + b_ref[...].astype(f32)).astype(bf16)
 
 
-def add(a, b, us):
-    return pl.pallas_call(
-        add_kernel, out_shape=pltpu.HBM(a.shape, bf16), cost_estimate=cost(us), name="add"
+def add(a, b):
+    return pl.pallas_call(
+        add_kernel, out_shape=pltpu.HBM(a.shape, bf16), cost_estimate=CHEAP, name="add"
     )(a, b)
 
 
@@ -1201,19 +1207,18 @@
             return value
 
         sources = sizes["wt"] * 4
-        t1 = done(total([[turn(kept).reshape(sources, D // sources, -1)]]))
-        t1_far = send(t1, far_mate)
         to_core = done(back((turn(grad_project),), flat_w, jnp.stack([mine ^ 3, mine ^ 1]), rows))
         from_core = send(to_core, core_mate)
         by_place = by_rows(turn(grad_project))
         done(by_place[0])
         to_near = done(back((grad_project,), flat_w, (mine ^ 2).reshape(1), rows, turn(from_core)))
         from_near = send(to_near, near_mate)
+        t1 = done(total([[turn(kept).reshape(sources, D // sources, -1)]]))
+        t1_far = send(t1, far_mate)
+        layer_out = done(copy(turn(layer_out)))
         by_place[0] = turn(by_place[0])
         q1 = done(total([by_place]))
         q1_far = send(q1, far_mate)
-        t2 = done(add(turn(t1), t1_far, 200))
-        t2_near = send(t2, near_mate)
         grad_tokens, grad_gain_attn = finish(
             (grad_project,),
             flat_w,
@@ -1226,11 +1231,14 @@
         )
         done(grad_tokens)
         home_grad = send(grad_tokens, to_home)
+        t2 = done(add(turn(t1), t1_far))
+        t2_near = send(t2, near_mate)
+        q2 = done(add(turn(q1), q1_far))
+        q2_near = send(q2, near_mate)
         t4 = done(pair_up(turn(t2), t2_near))
         t4_x = send(t4, x_mate)
         t4_core = send(t4, core_mate)
-        q2 = done(add(turn(q1), q1_far, 0.001))
-        q2_near = send(q2, near_mate)
+        grad_tokens = done(turn(home_grad))
         q4 = done(pair_up(turn(q2), q2_near))
         q4_x = send(q4, x_mate)
         q4_core = send(q4, core_mate)
@@ -1239,7 +1247,6 @@
         at = jnp.stack([gx, near, gc])
         totals = place_tail((turn(t4), t4_x, t4_core, t4_cross), at)
         done(totals[0])
-        grad_tokens = done(turn(home_grad))
         q4_x = done(turn(q4_x))
         q4_cross = send(q4_x, core_mate)
         total_qkv = spread(

time: 497 us -> 456 us (0.918)
  waiting for transfers between devices: 194 us -> 164 us
  starting transfers between devices: 67.2 us -> 52.8 us
    all_to_all x1, waiting for transfers between devices: 19.5 us -> 0.01 us  [local(): kept = lax.all_to_all(summed, ('wt', 'gx', 'near'), 0, 0, tiled=True)]
    ppermute x41, starting transfers between devices: 62 us -> 47.5 us  [send(): return lax.ppermute(value, AXES, pairs(target))]
    ppermute x41, waiting for transfers between devices: 175 us -> 164 us  [send(): return lax.ppermute(value, AXES, pairs(target))]
    unnamed x71 -> x70, local copies, waits for them, and re-layouts: 10.7 us -> 9.93 us
  transfers between devices with their start and end apart: 42 -> 42, of which waited for: 23 -> 23; matrix products, arithmetic and copies ran while one was open for 3% -> 3% of each run, Pallas kernels for 32% -> 39%
where the time goes in v8:
time: 456 us; the launch traced here: 449 us
  Pallas kernels  207 us (45%)
  waiting for transfers between devices  164 us (36%)
  starting transfers between devices  52.8 us (12%)
  local copies, waits for them, and re-layouts  16 us (4%)
  other arithmetic  7.28 us (2%)
    ppermute x41, waiting for transfers between devices, send(): return lax.ppermute(value, AXES, pairs(target))  164 us
    ppermute x41, starting transfers between devices, send(): return lax.ppermute(value, AXES, pairs(target))  47.5 us
    pallas_call x1, Pallas kernels, attn_bwd(): pl.pallas_call(functools.partial(bwd_kernel, first=group * nh, nh=nh, bq=...  44.6 us
    pallas_call x1, Pallas kernels, attn_fwd(): pl.pallas_call(functools.partial(fwd_kernel, nh=nh, bq=bq, bk=bk, nk=n //...  25.9 us
    pallas_call x2, Pallas kernels, project(): pl.pallas_call(functools.partial(project_kernel, count=count, halves=len(...  23 us
    pallas_call x1, Pallas kernels, tail(): pl.pallas_call(body, out_shape=[pltpu.HBM((rows, d), bf16)] + [pltpu.HBM(...  22 us
    pallas_call x2, Pallas kernels, share(): pl.pallas_call(share_kernel, out_shape=pltpu.HBM((d, n * w), bf16), grid_...  16.4 us
    pallas_call x2, Pallas kernels, back(): pl.pallas_call(functools.partial(back_kernel, groups=groups, extra=got is...  11.8 us
  transfers between devices with their start and end apart: 42, of which 23 were waited for; matrix products, arithmetic and copies ran while one was open for 3% of the time, Pallas kernels for 39%

profile of v8, /device:TPU:0, one launch (start us, length us, event | category | flops | bytes accessed | tf_op | source)
XLA Modules:
  0.0 449.0 jit_solution(7959916671113592180)
XLA Ops:
  0.7 4.5 %pick.1.x_ref.a_ref = bf16[640,1024]{1,0:T(8,128)(2,1)} custom-call(s32[1]{0:T(128)} %bitcast.mine.shard, bf16[640,3840]{1,0:T(8,128)(2,1)} %w_ref.1), custom_call_target="tpu_custom_call" | custom-call | flops 5000000000 | bytes 1000 | tf_op jit(solution)/shard_map/pick/pallas_call | solution.py:340
  9.5 5.4 %collective-permute-start.5 = (bf16[512,1280]{1,0:T(8,128)(2,1)S(1)}, bf16[512,1280]{1,0:T(8,128)(2,1)}, u32[]{:S(2)}, u32[]{:S(2)}) collective-permute-start(bf16[512,1280]{1,0:T(8,128)(2,1)S(1)} %bitcast.68), channel_id=1, source_target_pairs={{0,8},{1,9},{2,10},{3,11},{12,4},{13,5},{14,6},{15,7},{16,24},{17,... | collective-permute-start | bytes 3932168 | tf_op jit(solution)/shard_map/ppermute | solution.py:998
  19.1 6.7 %collective-permute-done.1.refs_2_ = bf16[512,1280]{1,0:T(8,128)(2,1)} collective-permute-done((bf16[512,1280]{1,0:T(8,128)(2,1)S(1)}, bf16[512,1280]{1,0:T(8,128)(2,1)}, u32[]{:S(2)}, u32[]{:S(2)}) %collective-permute-start.1) | collective-permute-done | bytes 1310752 | tf_op jit(solution)/shard_map/ppermute | solution.py:998
  27.1 5.2 %pad_maximum_fusion.own = bf16[3,640,1280]{2,1,0:T(8,128)(2,1)} fusion(bf16[1,640,1280]{2,1,0:T(8,128)(2,1)} %bitcast.82, bf16[1,640,1280]{2,1,0:T(8,128)(2,1)} %bitcast.83, bf16[1,640,1280]{2,1,0:T(8,128)(2,1)} %bitcast.84), kind=kLoop, calls=%fused_computation | loop fusion | flops 4915200 | bytes 9830400 | tf_op jit(solution)/shard_map/stack | solution.py:1110
  52.0 11.4 %project.2 = (bf16[2048,1280]{1,0:T(8,128)(2,1)}, bf16[2048,512]{1,0:T(8,128)(2,1)}, bf16[2048,1024]{1,0:T(8,128)(2,1)}, bf16[512,1280]{1,0:T(8,128)(2,1)}) custom-call(s32[5]{0:T(128)S(1)} %stack.101.info, bf16[512,1280]{1,0:T(8,128)(2,1)S(1)} %bitcast.70, bf16[512,1280]{1,0:T(8,128)(2,1)} %collective-permute-done.5.refs_1_, ...), custom_call_target="tpu_custom_call" | custom-call | flops 15000000512 | bytes 1000 | tf_op jit(solution)/shard_map/project/pallas_call | solution.py:497
  73.9 11.6 %project.3 = (bf16[2048,1280]{1,0:T(8,128)(2,1)}, bf16[2048,512]{1,0:T(8,128)(2,1)}, bf16[2048,1024]{1,0:T(8,128)(2,1)}, bf16[512,1280]{1,0:T(8,128)(2,1)}) custom-call(s32[5]{0:T(128)S(1)} %stack.98.info, bf16[512,1280]{1,0:T(8,128)(2,1)S(1)} %collective-permute-done.2.refs_0_, ...), custom_call_target="tpu_custom_call", output_to_operand_aliasing={{0}: (11, {}), {1}: (12, {}), {2}: (13, {})} | custom-call | flops 15000000512 | bytes 1000 | tf_op jit(solution)/shard_map/project/pallas_call | solution.py:497
  85.5 25.9 %attn_fwd.1 = (bf16[2048,320]{1,0:T(8,128)(2,1)}, bf16[2048,512]{1,0:T(8,128)(2,1)}, bf16[2048,512]{1,0:T(8,128)(2,1)}) custom-call(s32[16]{0:T(128)S(1)} %reshape.178.flags, bf16[2048,512]{1,0:T(8,128)(2,1)} %get-tuple-element.80.q_ref, bf16[2048,1024]{1,0:T(8,128)(2,1)} %get-tuple-element.81.kv.kk.vv, s32[2048,1]{1,0:T(8,128)S(1)} %copy.27.segc, ...), custom_call_target="tpu_custom_call" | custom-call | flops 10000000 | bytes 1000 | tf_op jit(solution)/shard_map/attn_fwd/pallas_call | solution.py:168
  113.5 5.1 %collective-permute-done.13.half = bf16[3,320,1280]{2,1,0:T(8,128)(2,1)} collective-permute-done((bf16[3,320,1280]{2,1,0:T(8,128)(2,1)}, bf16[3,320,1280]{2,1,0:T(8,128)(2,1)}, u32[]{:S(2)}, u32[]{:S(2)}) %collective-permute-start.13) | collective-permute-done | bytes 2457632 | tf_op jit(solution)/shard_map/ppermute | solution.py:998
  121.2 4.2 order.1.refs_1_
  125.5 5.6 %collective-permute-done.11.p2 = bf16[512,320]{1,0:T(8,128)(2,1)S(1)} collective-permute-done((bf16[512,320]{1,0:T(8,128)(2,1)S(1)}, bf16[512,320]{1,0:T(8,128)(2,1)S(1)}, u32[]{:S(2)}, u32[]{:S(2)}) %collective-permute-start.11) | collective-permute-done | bytes 327712 | tf_op jit(solution)/shard_map/ppermute | solution.py:998
  131.1 7.9 %collective-permute-done.12.p3 = bf16[512,320]{1,0:T(8,128)(2,1)S(1)} collective-permute-done((bf16[512,320]{1,0:T(8,128)(2,1)S(1)}, bf16[512,320]{1,0:T(8,128)(2,1)S(1)}, u32[]{:S(2)}, u32[]{:S(2)}) %collective-permute-start.12) | collective-permute-done | bytes 327712 | tf_op jit(solution)/shard_map/ppermute | solution.py:998
  138.9 22.0 %tail.1 = (bf16[512,1280]{1,0:T(8,128)(2,1)}, bf16[3,512,1280]{2,1,0:T(8,128)(2,1)}, bf16[3,512,1280]{2,1,0:T(8,128)(2,1)}, f32[512,1280]{1,0:T(8,128)}, bf16[51...) custom-call(s32[4]{0:T(128)S(1)} %pad_add_fusion.at, ...), custom_call_target="tpu_custom_call" | custom-call | flops 10000000 | bytes 1000 | tf_op jit(solution)/shard_map/tail/pallas_call | solution.py:609
  163.4 7.4 %share.2 = bf16[1280,1920]{1,0:T(8,128)(2,1)} custom-call(s32[1]{0:T(128)} %bitcast.21.col, bf16[3,512,1280]{2,1,0:T(8,128)(2,1)} %get-tuple-element.94.left, bf16[3,512,1280]{2,1,0:T(8,128)(2,1)} %get-tuple-element.95.right), custom_call_target="tpu_custom_call" | custom-call | flops 1000000 | bytes 1000 | tf_op jit(solution)/shard_map/share/pallas_call | solution.py:647
  172.5 8.8 %collective-permute-done.16.do2 = bf16[512,320]{1,0:T(8,128)(2,1)S(1)} collective-permute-done((bf16[512,320]{1,0:T(8,128)(2,1)}, bf16[512,320]{1,0:T(8,128)(2,1)S(1)}, u32[]{:S(2)}, u32[]{:S(2)}) %collective-permute-start.16) | collective-permute-done | bytes 327712 | tf_op jit(solution)/shard_map/ppermute | solution.py:998
  184.3 8.9 %share.3 = bf16[1280,1920]{1,0:T(8,128)(2,1)} custom-call(s32[1]{0:T(128)} %bitcast.22.col, bf16[3,512,1280]{2,1,0:T(8,128)(2,1)} %get-tuple-element.94.left, bf16[3,512,1280]{2,1,0:T(8,128)(2,1)} %get-tuple-element.95.right, bf16[1280,1920]{1,0:T(8,128)(2,1)} %collective-permute-done.19.refs_0_), custom_call_target="tpu_custom_call" | custom-call | flops 1000000 | bytes 1000 | tf_op jit(solution)/shard_map/share/pallas_call | solution.py:647
  193.2 5.3 %all-to-all-start = ((bf16[8,160,1920]{2,1,0:T(8,128)(2,1)}), bf16[8,160,1920]{2,1,0:T(8,128)(2,1)}, u32[]{:S(2)}, u32[]{:S(2)}) async-start(bf16[8,160,1920]{2,1,0:T(8,128)(2,1)} %bitcast.80), calls=%async_computation | async-start | bytes 9830400 | tf_op jit(solution)/shard_map/all_to_all | solution.py:1168
  198.6 44.6 %attn_bwd.1 = (bf16[2048,1024]{1,0:T(8,128)(2,1)}, f32[8,128]{1,0:T(8,128)}) custom-call(s32[16]{0:T(128)S(1)} %copy-done.9, s32[1]{0:T(128)} %bitcast.mine.shard, bf16[2048,512]{1,0:T(8,128)(2,1)} %get-tuple-element.100.qa, bf16[2048,1024]{1,0:T(8,128)(2,1)} %get-tuple-element.81.kv.kk.vv, bf16[2048,1024]{1,0:T(8,128)(2,1)} %get-tuple-element.81.kv.kk.vv, ...), custom_call_target="tpu_custom_call" | custom-call | flops 299999985664 | bytes 1000 | tf_op jit(solution)/shard_map/attn_bwd/pallas_call | solution.py:302
  243.3 7.1 %back.2 = bf16[2,512,1280]{2,1,0:T(8,128)(2,1)} custom-call(s32[2]{0:T(128)S(1)} %pad_add_fusion.1.shards, bf16[2048,1024]{1,0:T(8,128)(2,1)} %get-tuple-element.110.refs_0_.g_ref, bf16[1280,1024]{1,0:T(8,128)(2,1)} %order.1.refs_1_), custom_call_target="tpu_custom_call" | custom-call | flops 1000000 | bytes 1000 | tf_op jit(solution)/shard_map/back/pallas_call | solution.py:882
  255.3 8.5 %cross.1 = (bf16[320,1024]{1,0:T(8,128)(2,1)}, bf16[320,1024]{1,0:T(8,128)(2,1)}, bf16[320,1024]{1,0:T(8,128)(2,1)}, bf16[320,1024]{1,0:T(8,128)(2,1)}) custom-call(s32[2]{0:T(128)S(1)} %pad_add_fusion.2.at, bf16[2048,1280]{1,0:T(8,128)(2,1)S(1)} %copy-done.2, bf16[2048,1024]{1,0:T(8,128)(2,1)S(1)} %copy-done), custom_call_target="tpu_custom_call" | custom-call | flops 1000000 | bytes 1000 | tf_op jit(solution)/shard_map/cross/pallas_call | solution.py:798
  263.8 4.7 %back.3 = bf16[1,512,1280]{2,1,0:T(8,128)(2,1)} custom-call(s32[1]{0:T(128)} %bitcast.26.shards, bf16[2048,1024]{1,0:T(8,128)(2,1)} %get-tuple-element.110.refs_0_.g_ref, bf16[1280,1024]{1,0:T(8,128)(2,1)} %order.1.refs_1_, bf16[2,512,1280]{2,1,0:T(8,128)(2,1)S(1)} %collective-permute-done.20.refs_2_), custom_call_target="tpu_custom_call" | custom-call | flops 1000000 | bytes 1000 | tf_op jit(solution)/shard_map/back/pallas_call | solution.py:882
  280.9 7.3 %collective-permute-done.22 = bf16[320,1024]{1,0:T(8,128)(2,1)} collective-permute-done((bf16[320,1024]{1,0:T(8,128)(2,1)}, bf16[320,1024]{1,0:T(8,128)(2,1)}, u32[]{:S(2)}, u32[]{:S(2)}) %collective-permute-start.22) | collective-permute-done | bytes 655392 | tf_op jit(solution)/shard_map/ppermute | solution.py:998
  288.2 14.5 %collective-permute-done.23 = bf16[320,1024]{1,0:T(8,128)(2,1)} collective-permute-done((bf16[320,1024]{1,0:T(8,128)(2,1)}, bf16[320,1024]{1,0:T(8,128)(2,1)}, u32[]{:S(2)}, u32[]{:S(2)}) %collective-permute-start.23) | collective-permute-done | bytes 655392 | tf_op jit(solution)/shard_map/ppermute | solution.py:998
  306.3 7.1 %collective-permute-done.21.refs_3_ = bf16[1,512,1280]{2,1,0:T(8,128)(2,1)} collective-permute-done((bf16[1,512,1280]{2,1,0:T(8,128)(2,1)}, bf16[1,512,1280]{2,1,0:T(8,128)(2,1)}, u32[]{:S(2)}, u32[]{:S(2)}) %collective-permute-start.21) | collective-permute-done | bytes 1310752 | tf_op jit(solution)/shard_map/ppermute | solution.py:998
  313.4 6.8 %finish.1 = (bf16[512,1280]{1,0:T(8,128)(2,1)}, f32[1,1280]{1,0:T(1,128)S(1)}) custom-call(s32[1]{0:T(128)} %bitcast.mine.shard, bf16[2048,1024]{1,0:T(8,128)(2,1)} %get-tuple-element.110.refs_0_.g_ref, bf16[1280,1024]{1,0:T(8,128)(2,1)} %order.1.refs_1_, bf16[2,512,1280]{2,1,0:T(8,128)(2,1)S(1)} %collective-permute-done.20.refs_2_, ...), custom_call_target="tpu_custom_call" | custom-call | flops 1000000 | bytes 1000 | tf_op jit(solution)/shard_map/finish/pallas_call | solution.py:929
  324.4 17.6 %collective-permute-done.27.b_ref = bf16[320,1024]{1,0:T(8,128)(2,1)S(1)} collective-permute-done((bf16[320,1024]{1,0:T(8,128)(2,1)}, bf16[320,1024]{1,0:T(8,128)(2,1)S(1)}, u32[]{:S(2)}, u32[]{:S(2)}) %collective-permute-start.27) | collective-permute-done | bytes 655392 | tf_op jit(solution)/shard_map/ppermute | solution.py:998
  345.1 17.2 %collective-permute-done.28.b_ref = bf16[160,1920]{1,0:T(8,128)(2,1)S(1)} collective-permute-done((bf16[160,1920]{1,0:T(8,128)(2,1)}, bf16[160,1920]{1,0:T(8,128)(2,1)S(1)}, u32[]{:S(2)}, u32[]{:S(2)}) %collective-permute-start.28) | collective-permute-done | bytes 614432 | tf_op jit(solution)/shard_map/ppermute | solution.py:998
  367.2 15.3 %collective-permute-done.29.b_ref = bf16[320,1024]{1,0:T(8,128)(2,1)S(1)} collective-permute-done((bf16[320,1024]{1,0:T(8,128)(2,1)S(1)}, bf16[320,1024]{1,0:T(8,128)(2,1)S(1)}, u32[]{:S(2)}, u32[]{:S(2)}) %collective-permute-start.29) | collective-permute-done | bytes 655392 | tf_op jit(solution)/shard_map/ppermute | solution.py:998
  386.9 8.9 %collective-permute-done.31.own_x = bf16[2,160,1920]{2,1,0:T(8,128)(2,1)} collective-permute-done((bf16[2,160,1920]{2,1,0:T(8,128)(2,1)}, bf16[2,160,1920]{2,1,0:T(8,128)(2,1)}, u32[]{:S(2)}, u32[]{:S(2)}) %collective-permute-start.31) | collective-permute-done | bytes 1228832 | tf_op jit(solution)/shard_map/ppermute | solution.py:998
  399.1 5.8 %place_tail.1 = (f32[4,160,1280]{2,1,0:T(8,128)}, f32[4,160,1280]{2,1,0:T(8,128)}, f32[4,160,1280]{2,1,0:T(8,128)}) custom-call(s32[3]{0:T(128)S(1)} %pad_add_fusion.5.at, bf16[2,160,1920]{2,1,0:T(8,128)(2,1)S(1)} %copy-done.3, bf16[2,160,1920]{2,1,0:T(8,128)(2,1)} %collective-permute-done.31.own_x, bf16[2,160,1920]{2,1,0:T(8,128)(2,1)S(1)} %collective-permute-done.32.mate, ...), custom_call_target="tpu_custom_call" | custom-call | flops 1000000 | bytes 1000 | tf_op jit(solution)/shard_map/place_tail/pallas_call | solution.py:764
  404.9 15.7 %collective-permute-done.30.refs_1_ = bf16[2,320,1024]{2,1,0:T(8,128)(2,1)} collective-permute-done((bf16[2,320,1024]{2,1,0:T(8,128)(2,1)}, bf16[2,320,1024]{2,1,0:T(8,128)(2,1)}, u32[]{:S(2)}, u32[]{:S(2)}) %collective-permute-start.30) | collective-permute-done | bytes 1310752 | tf_op jit(solution)/shard_map/ppermute | solution.py:998
  426.5 4.6 %collective-permute-done.38 = f32[21,128]{1,0:T(8,128)S(1)} collective-permute-done((f32[21,128]{1,0:T(8,128)S(1)}, f32[21,128]{1,0:T(8,128)S(1)}, u32[]{:S(2)}, u32[]{:S(2)}) %collective-permute-start.38) | collective-permute-done | bytes 10784 | tf_op jit(solution)/shard_map/ppermute | solution.py:998
  439.6 6.5 %spread.1 = f32[2,320,3840]{2,1,0:T(8,128)} custom-call(s32[3]{0:T(128)S(1)} %pad_add_fusion.3.at, bf16[2,320,1024]{2,1,0:T(8,128)(2,1)S(1)} %copy-done.1, bf16[2,320,1024]{2,1,0:T(8,128)(2,1)} %collective-permute-done.30.refs_1_, bf16[2,320,1024]{2,1,0:T(8,128)(2,1)} %collective-permute-done.34.refs_2_, ...), custom_call_target="tpu_custom_call" | custom-call | flops 1000000 | bytes 1000 | tf_op jit(solution)/shard_map/spread/pallas_call | solution.py:842
  (190 shorter events, 109.1 us)
Async XLA Ops:
  5.2 20.6 %collective-permute-start.1 = (bf16[512,1280]{1,0:T(8,128)(2,1)S(1)}, bf16[512,1280]{1,0:T(8,128)(2,1)}, u32[]{:S(2)}, u32[]{:S(2)}) collective-permute-start(bf16[512,1280]{1,0:T(8,128)(2,1)S(1)} %bitcast.67), channel_id=1, source_target_pairs={{2,0},{3,1},{4,2},{5,3},{6,4},{7,5},{8,10},{9,11},{10,12},{11,13},... | collective-permute-start | bytes 3932168 | tf_op jit(solution)/shard_map/ppermute | solution.py:998
  6.5 30.7 %collective-permute-start.7 = (bf16[640,1024]{1,0:T(8,128)(2,1)}, bf16[640,1024]{1,0:T(8,128)(2,1)}, u32[]{:S(2)}, u32[]{:S(2)}) collective-permute-start(bf16[640,1024]{1,0:T(8,128)(2,1)} %pick.1.x_ref.a_ref), channel_id=1, source_target_pairs={{0,1},{1,0},{2,3},{3,2},{4,5},{5,4},{6,7},{7,6},{8,9},{9,8},{10,11... | collective-permute-start | bytes 3932168 | tf_op jit(solution)/shard_map/ppermute | solution.py:998
  9.5 42.4 %collective-permute-start.5 = (bf16[512,1280]{1,0:T(8,128)(2,1)S(1)}, bf16[512,1280]{1,0:T(8,128)(2,1)}, u32[]{:S(2)}, u32[]{:S(2)}) collective-permute-start(bf16[512,1280]{1,0:T(8,128)(2,1)S(1)} %bitcast.68), channel_id=1, source_target_pairs={{0,8},{1,9},{2,10},{3,11},{12,4},{13,5},{14,6},{15,7},{16,24},{17,... | collective-permute-start | bytes 3932168 | tf_op jit(solution)/shard_map/ppermute | solution.py:998
  14.9 54.4 %collective-permute-start = (s32[1,2048]{1,0:T(1,128)S(1)}, s32[1,2048]{1,0:T(1,128)S(1)}, u32[]{:S(2)}, u32[]{:S(2)}) collective-permute-start(s32[1,2048]{1,0:T(1,128)S(1)} %copy-done.25), channel_id=1, source_target_pairs={{0,8},{1,9},{2,10},{3,11},{4,12},{5,13},{6,14},{7,15},{8,0},{9,1},... | collective-permute-start | bytes 24584 | tf_op jit(solution)/shard_map/ppermute | solution.py:998
  25.8 19.7 %collective-permute-start.2 = (bf16[512,1280]{1,0:T(8,128)(2,1)}, bf16[512,1280]{1,0:T(8,128)(2,1)S(1)}, u32[]{:S(2)}, u32[]{:S(2)}) collective-permute-start(bf16[512,1280]{1,0:T(8,128)(2,1)} %collective-permute-done.1.refs_2_), channel_id=1, source_target_pairs={{2,0},{3,1},{4,2},{5,3},{10,12},{11,13},{12,14},{13,15},{18,16},{1... | collective-permute-start | bytes 3932168 | tf_op jit(solution)/shard_map/ppermute | solution.py:998
  32.3 19.7 %collective-permute-start.6 = (bf16[512,1280]{1,0:T(8,128)(2,1)}, bf16[512,1280]{1,0:T(8,128)(2,1)}, u32[]{:S(2)}, u32[]{:S(2)}) collective-permute-start(bf16[512,1280]{1,0:T(8,128)(2,1)} %collective-permute-done.1.refs_2_), channel_id=1, source_target_pairs={{0,8},{1,9},{2,10},{3,11},{12,4},{13,5},{14,6},{15,7},{16,24},{17,... | collective-permute-start | bytes 3932168 | tf_op jit(solution)/shard_map/ppermute | solution.py:998
  45.6 19.6 %collective-permute-start.4 = (bf16[512,1280]{1,0:T(8,128)(2,1)S(1)}, bf16[512,1280]{1,0:T(8,128)(2,1)}, u32[]{:S(2)}, u32[]{:S(2)}) collective-permute-start(bf16[512,1280]{1,0:T(8,128)(2,1)S(1)} %broadcast_select_fusion), channel_id=1, source_target_pairs={{0,2},{1,3},{2,0},{3,1},{12,14},{13,15},{14,12},{15,13},{16,18},{1... | collective-permute-start | bytes 3932168 | tf_op jit(solution)/shard_map/ppermute | solution.py:998
  49.6 24.3 %collective-permute-start.3 = (bf16[512,1280]{1,0:T(8,128)(2,1)S(1)}, bf16[512,1280]{1,0:T(8,128)(2,1)}, u32[]{:S(2)}, u32[]{:S(2)}) collective-permute-start(bf16[512,1280]{1,0:T(8,128)(2,1)S(1)} %collective-permute-done.2.refs_0_), channel_id=1, source_target_pairs={{0,8},{1,9},{2,10},{3,11},{12,4},{13,5},{14,6},{15,7},{16,24},{17,... | collective-permute-start | bytes 3932168 | tf_op jit(solution)/shard_map/ppermute | solution.py:998
  70.8 47.8 %collective-permute-start.13 = (bf16[3,320,1280]{2,1,0:T(8,128)(2,1)}, bf16[3,320,1280]{2,1,0:T(8,128)(2,1)}, u32[]{:S(2)}, u32[]{:S(2)}) collective-permute-start(bf16[3,320,1280]{2,1,0:T(8,128)(2,1)} %constant_dynamic-slice_fusion), channel_id=1, source_target_pairs={{0,1},{1,0},{2,3},{3,2},{4,5},{5,4},{6,7},{7,6},{8,9},{9,8},{10,11... | collective-permute-start | bytes 7372808 | tf_op jit(solution)/shard_map/ppermute | solution.py:998
  73.3 38.1 %collective-permute-start.9 = (bf16[512,1280]{1,0:T(8,128)(2,1)}, bf16[512,1280]{1,0:T(8,128)(2,1)S(1)}, u32[]{:S(2)}, u32[]{:S(2)}) collective-permute-start(bf16[512,1280]{1,0:T(8,128)(2,1)} %bitcast.94), channel_id=1, source_target_pairs={{0,8},{1,9},{2,0},{3,1},{4,10},{5,11},{6,2},{7,3},{8,12},{9,13},{1... | collective-permute-start | bytes 3932168 | tf_op jit(solution)/shard_map/ppermute | solution.py:998
  118.6 20.3 %collective-permute-start.14 = (bf16[3,320,1280]{2,1,0:T(8,128)(2,1)}, bf16[3,320,1280]{2,1,0:T(8,128)(2,1)}, u32[]{:S(2)}, u32[]{:S(2)}) collective-permute-start(bf16[3,320,1280]{2,1,0:T(8,128)(2,1)} %collective-permute-done.13.half), channel_id=1, source_target_pairs={{0,8},{1,9},{2,10},{3,11},{4,12},{5,13},{6,14},{7,15},{8,0},{9,1},... | collective-permute-start | bytes 7372808 | tf_op jit(solution)/shard_map/ppermute | solution.py:998
  118.7 12.4 %collective-permute-start.11 = (bf16[512,320]{1,0:T(8,128)(2,1)S(1)}, bf16[512,320]{1,0:T(8,128)(2,1)S(1)}, u32[]{:S(2)}, u32[]{:S(2)}) collective-permute-start(bf16[512,320]{1,0:T(8,128)(2,1)S(1)} %get-tuple-element.142), channel_id=1, source_target_pairs={{0,2},{1,3},{2,0},{3,1},{4,6},{5,7},{6,4},{7,5},{8,10},{9,11},{10,... | collective-permute-start | bytes 983048 | tf_op jit(solution)/shard_map/ppermute | solution.py:998
  121.1 17.9 %collective-permute-start.12 = (bf16[512,320]{1,0:T(8,128)(2,1)S(1)}, bf16[512,320]{1,0:T(8,128)(2,1)S(1)}, u32[]{:S(2)}, u32[]{:S(2)}) collective-permute-start(bf16[512,320]{1,0:T(8,128)(2,1)S(1)} %get-tuple-element.141), channel_id=1, source_target_pairs={{0,10},{1,11},{2,8},{3,9},{4,14},{5,15},{6,12},{7,13},{8,2},{9,3},... | collective-permute-start | bytes 983048 | tf_op jit(solution)/shard_map/ppermute | solution.py:998
  161.2 11.3 %collective-permute-start.17 = (bf16[512,320]{1,0:T(8,128)(2,1)}, bf16[512,320]{1,0:T(8,128)(2,1)S(1)}, u32[]{:S(2)}, u32[]{:S(2)}) collective-permute-start(bf16[512,320]{1,0:T(8,128)(2,1)} %get-tuple-element.97), channel_id=1, source_target_pairs={{0,10},{1,11},{2,8},{3,9},{4,14},{5,15},{6,12},{7,13},{8,2},{9,3},... | collective-permute-start | bytes 983048 | tf_op jit(solution)/shard_map/ppermute | solution.py:998
  162.7 18.5 %collective-permute-start.16 = (bf16[512,320]{1,0:T(8,128)(2,1)}, bf16[512,320]{1,0:T(8,128)(2,1)S(1)}, u32[]{:S(2)}, u32[]{:S(2)}) collective-permute-start(bf16[512,320]{1,0:T(8,128)(2,1)} %get-tuple-element.92), channel_id=1, source_target_pairs={{0,2},{1,3},{2,0},{3,1},{4,6},{5,7},{6,4},{7,5},{8,10},{9,11},{10,... | collective-permute-start | bytes 983048 | tf_op jit(solution)/shard_map/ppermute | solution.py:998
  170.8 13.5 %collective-permute-start.19 = (bf16[1280,1920]{1,0:T(8,128)(2,1)}, bf16[1280,1920]{1,0:T(8,128)(2,1)}, u32[]{:S(2)}, u32[]{:S(2)}) collective-permute-start(bf16[1280,1920]{1,0:T(8,128)(2,1)} %share.2), channel_id=1, source_target_pairs={{0,8},{1,9},{2,10},{3,11},{4,12},{5,13},{6,14},{7,15},{8,0},{9,1},... | collective-permute-start | bytes 14745608 | tf_op jit(solution)/shard_map/ppermute | solution.py:998
  182.6 60.7 %collective-permute-start.18 = (bf16[512,1280]{1,0:T(8,128)(2,1)}, bf16[512,1280]{1,0:T(8,128)(2,1)}, u32[]{:S(2)}, u32[]{:S(2)}) collective-permute-start(bf16[512,1280]{1,0:T(8,128)(2,1)} %get-tuple-element.99), channel_id=1, source_target_pairs={{0,2},{1,3},{2,6},{3,7},{4,10},{5,11},{6,14},{7,15},{8,0},{9,1},{1... | collective-permute-start | bytes 3932168 | tf_op jit(solution)/shard_map/ppermute | solution.py:998
  193.2 80.6 %all-to-all-start = ((bf16[8,160,1920]{2,1,0:T(8,128)(2,1)}), bf16[8,160,1920]{2,1,0:T(8,128)(2,1)}, u32[]{:S(2)}, u32[]{:S(2)}) async-start(bf16[8,160,1920]{2,1,0:T(8,128)(2,1)} %bitcast.80), calls=%async_computation | async-start | bytes 9830400 | tf_op jit(solution)/shard_map/all_to_all | solution.py:1168
  250.4 13.4 %collective-permute-start.20 = (bf16[2,512,1280]{2,1,0:T(8,128)(2,1)}, bf16[2,512,1280]{2,1,0:T(8,128)(2,1)S(1)}, u32[]{:S(2)}, u32[]{:S(2)}) collective-permute-start(bf16[2,512,1280]{2,1,0:T(8,128)(2,1)} %back.2), channel_id=1, source_target_pairs={{0,8},{1,9},{2,10},{3,11},{4,12},{5,13},{6,14},{7,15},{8,0},{9,1},... | collective-permute-start | bytes 7864328 | tf_op jit(solution)/shard_map/ppermute | solution.py:998
  268.5 44.9 %collective-permute-start.21 = (bf16[1,512,1280]{2,1,0:T(8,128)(2,1)}, bf16[1,512,1280]{2,1,0:T(8,128)(2,1)}, u32[]{:S(2)}, u32[]{:S(2)}) collective-permute-start(bf16[1,512,1280]{2,1,0:T(8,128)(2,1)} %back.3), channel_id=1, source_target_pairs={{0,2},{1,3},{2,0},{3,1},{4,6},{5,7},{6,4},{7,5},{8,10},{9,11},{10,... | collective-permute-start | bytes 3932168 | tf_op jit(solution)/shard_map/ppermute | solution.py:998
  270.4 17.9 %collective-permute-start.22 = (bf16[320,1024]{1,0:T(8,128)(2,1)}, bf16[320,1024]{1,0:T(8,128)(2,1)}, u32[]{:S(2)}, u32[]{:S(2)}) collective-permute-start(bf16[320,1024]{1,0:T(8,128)(2,1)} %get-tuple-element.116), channel_id=1, source_target_pairs={{0,16},{1,17},{2,18},{3,19},{4,20},{5,21},{6,22},{7,23},{8,24},{9,... | collective-permute-start | bytes 1966088 | tf_op jit(solution)/shard_map/ppermute | solution.py:998
  271.8 30.9 %collective-permute-start.23 = (bf16[320,1024]{1,0:T(8,128)(2,1)}, bf16[320,1024]{1,0:T(8,128)(2,1)}, u32[]{:S(2)}, u32[]{:S(2)}) collective-permute-start(bf16[320,1024]{1,0:T(8,128)(2,1)} %get-tuple-element.117), channel_id=1, source_target_pairs={{0,1},{1,0},{2,3},{3,2},{4,5},{5,4},{6,7},{7,6},{8,9},{9,8},{10,11... | collective-permute-start | bytes 1966088 | tf_op jit(solution)/shard_map/ppermute | solution.py:998
  273.3 29.5 %collective-permute-start.24 = (bf16[320,1024]{1,0:T(8,128)(2,1)}, bf16[320,1024]{1,0:T(8,128)(2,1)}, u32[]{:S(2)}, u32[]{:S(2)}) collective-permute-start(bf16[320,1024]{1,0:T(8,128)(2,1)} %get-tuple-element.118), channel_id=1, source_target_pairs={{0,17},{1,16},{2,19},{3,18},{4,21},{5,20},{6,23},{7,22},{8,25},{9,... | collective-permute-start | bytes 1966088 | tf_op jit(solution)/shard_map/ppermute | solution.py:998
  277.3 42.8 %collective-permute-start.26 = (bf16[160,1920]{1,0:T(8,128)(2,1)}, bf16[160,1920]{1,0:T(8,128)(2,1)}, u32[]{:S(2)}, u32[]{:S(2)}) collective-permute-start(bf16[160,1920]{1,0:T(8,128)(2,1)} %total.2.a_ref), channel_id=1, source_target_pairs={{0,4},{1,5},{2,6},{3,7},{4,0},{5,1},{6,2},{7,3},{8,12},{9,13},{10,... | collective-permute-start | bytes 1843208 | tf_op jit(solution)/shard_map/ppermute | solution.py:998
  305.2 36.9 %collective-permute-start.27 = (bf16[320,1024]{1,0:T(8,128)(2,1)}, bf16[320,1024]{1,0:T(8,128)(2,1)S(1)}, u32[]{:S(2)}, u32[]{:S(2)}) collective-permute-start(bf16[320,1024]{1,0:T(8,128)(2,1)} %total.3.a_ref), channel_id=1, source_target_pairs={{0,4},{1,5},{2,6},{3,7},{4,0},{5,1},{6,2},{7,3},{8,12},{9,13},{10,... | collective-permute-start | bytes 1966088 | tf_op jit(solution)/shard_map/ppermute | solution.py:998
  322.4 40.0 %collective-permute-start.28 = (bf16[160,1920]{1,0:T(8,128)(2,1)}, bf16[160,1920]{1,0:T(8,128)(2,1)S(1)}, u32[]{:S(2)}, u32[]{:S(2)}) collective-permute-start(bf16[160,1920]{1,0:T(8,128)(2,1)} %add.137.a_ref), channel_id=1, source_target_pairs={{0,2},{1,3},{2,0},{3,1},{4,6},{5,7},{6,4},{7,5},{8,10},{9,11},{10,... | collective-permute-start | bytes 1843208 | tf_op jit(solution)/shard_map/ppermute | solution.py:998
  322.4 44.8 %collective-permute-start.25 = (bf16[512,1280]{1,0:T(8,128)(2,1)}, bf16[512,1280]{1,0:T(8,128)(2,1)}, u32[]{:S(2)}, u32[]{:S(2)}) collective-permute-start(bf16[512,1280]{1,0:T(8,128)(2,1)} %get-tuple-element.121), channel_id=1, source_target_pairs={{0,2},{1,3},{2,6},{3,7},{4,10},{5,11},{6,14},{7,15},{8,0},{9,1},{1... | collective-permute-start | bytes 3932168 | tf_op jit(solution)/shard_map/ppermute | solution.py:998
  365.6 30.3 %collective-permute-start.31 = (bf16[2,160,1920]{2,1,0:T(8,128)(2,1)}, bf16[2,160,1920]{2,1,0:T(8,128)(2,1)}, u32[]{:S(2)}, u32[]{:S(2)}) collective-permute-start(bf16[2,160,1920]{2,1,0:T(8,128)(2,1)} %pair_up.2.own), channel_id=1, source_target_pairs={{0,16},{1,17},{2,18},{3,19},{4,20},{5,21},{6,22},{7,23},{8,24},{9,... | collective-permute-start | bytes 3686408 | tf_op jit(solution)/shard_map/ppermute | solution.py:998
  367.2 15.3 %collective-permute-start.29 = (bf16[320,1024]{1,0:T(8,128)(2,1)S(1)}, bf16[320,1024]{1,0:T(8,128)(2,1)S(1)}, u32[]{:S(2)}, u32[]{:S(2)}) collective-permute-start(bf16[320,1024]{1,0:T(8,128)(2,1)S(1)} %copy-done.17), channel_id=1, source_target_pairs={{0,2},{1,3},{2,0},{3,1},{4,6},{5,7},{6,4},{7,5},{8,10},{9,11},{10,... | collective-permute-start | bytes 1966088 | tf_op jit(solution)/shard_map/ppermute | solution.py:998
  385.8 34.8 %collective-permute-start.30 = (bf16[2,320,1024]{2,1,0:T(8,128)(2,1)}, bf16[2,320,1024]{2,1,0:T(8,128)(2,1)}, u32[]{:S(2)}, u32[]{:S(2)}) collective-permute-start(bf16[2,320,1024]{2,1,0:T(8,128)(2,1)} %pair_up.3.refs_0_), channel_id=1, source_target_pairs={{0,16},{1,17},{2,18},{3,19},{4,20},{5,21},{6,22},{7,23},{8,24},{9,... | collective-permute-start | bytes 3932168 | tf_op jit(solution)/shard_map/ppermute | solution.py:998
  395.9 43.6 %collective-permute-start.34 = (bf16[2,320,1024]{2,1,0:T(8,128)(2,1)}, bf16[2,320,1024]{2,1,0:T(8,128)(2,1)}, u32[]{:S(2)}, u32[]{:S(2)}) collective-permute-start(bf16[2,320,1024]{2,1,0:T(8,128)(2,1)} %pair_up.3.refs_0_), channel_id=1, source_target_pairs={{0,8},{1,9},{2,10},{3,11},{4,12},{5,13},{6,14},{7,15},{8,0},{9,1},... | collective-permute-start | bytes 3932168 | tf_op jit(solution)/shard_map/ppermute | solution.py:998
  420.6 19.0 %collective-permute-start.35 = (bf16[2,320,1024]{2,1,0:T(8,128)(2,1)}, bf16[2,320,1024]{2,1,0:T(8,128)(2,1)S(1)}, u32[]{:S(2)}, u32[]{:S(2)}) collective-permute-start(bf16[2,320,1024]{2,1,0:T(8,128)(2,1)} %collective-permute-done.30.refs_1_), channel_id=1, source_target_pairs={{0,8},{1,9},{2,10},{3,11},{4,12},{5,13},{6,14},{7,15},{8,0},{9,1},... | collective-permute-start | bytes 3932168 | tf_op jit(solution)/shard_map/ppermute | solution.py:998
  (43 other events, 421.2 us)

commit v9 on v8

--- a/solution.py
+++ b/solution.py
@@ -378,45 +378,54 @@
     )(hbm(x))
 
 
-def order_kernel(own_first, a_ref, b_ref, *outs, each):
-    def put(ref):
-        value = ref[...]
-        for g, out in enumerate(outs):
-            gap = jnp.zeros((value.shape[0], out.shape[1] - each), value.dtype)
-            out[...] = jnp.concatenate([value[:, g * each : (g + 1) * each], gap], axis=1)
-
+def order_kernel(own_first, a_ref, b_ref, out):
     half = pl.program_id(0)
 
     @pl.when(half == 0)
     def _():
-        put(a_ref)
+        out[...] = a_ref[...].T
 
     @pl.when(half == 1)
     def _():
-        put(b_ref)
-
-
-def order(own, other, own_at, groups, nh):
+        out[...] = b_ref[...].T
+
+
+def order(own, other, own_at):
     rows, width = own.shape
-    step = 320
-    n = rows // step
-    at = lambda i, j, m: ((i ^ m[0]) * n + j, 0)
-    each = 3 * nh * HD // groups
-    return pl.pallas_call(
-        functools.partial(order_kernel, each=each),
-        out_shape=[pltpu.HBM((2 * rows, lanes_up(each)), own.dtype)] * groups,
+    step = 256
+    return pl.pallas_call(
+        order_kernel,
+        out_shape=pltpu.HBM((width, 2 * rows), own.dtype),
         grid_spec=pltpu.PrefetchScalarGridSpec(
             num_scalar_prefetch=1,
-            grid=(2, n),
+            grid=(2, width // step),
             in_specs=[
-                pl.BlockSpec((step, width), lambda i, j, m: (j * (1 - i), 0)),
-                pl.BlockSpec((step, width), lambda i, j, m: (j * i, 0)),
+                pl.BlockSpec((rows, step), lambda i, j, m: (0, j * (1 - i))),
+                pl.BlockSpec((rows, step), lambda i, j, m: (0, j * i)),
             ],
-            out_specs=[pl.BlockSpec((step, lanes_up(each)), at)] * groups,
+            out_specs=pl.BlockSpec((step, rows), lambda i, j, m: (j, i ^ m[0])),
         ),
-        cost_estimate=cost(3),
+        cost_estimate=cost(200.0),
         name="order",
     )(own_at.reshape(1), hbm(own), hbm(other))
+
+
+def transpose_kernel(x_ref, out):
+    out[...] = x_ref[...].T
+
+
+def transpose(x):
+    rows, cols = x.shape
+    step = 256
+    return pl.pallas_call(
+        transpose_kernel,
+        out_shape=pltpu.HBM((cols, rows), x.dtype),
+        grid=(rows // step,),
+        in_specs=[pl.BlockSpec((step, cols), lambda i: (i, 0))],
+        out_specs=pl.BlockSpec((cols, step), lambda i: (0, i)),
+        cost_estimate=CHEAP,
+        name="transpose",
+    )(hbm(x))
 
 
 def project_kernel(info, *refs, count, halves, width, fresh):
@@ -727,9 +736,9 @@
     out[1] = b_ref[...]
 
 
-def pair_up(a, b):
-    return pl.pallas_call(
-        pair_kernel, out_shape=pltpu.HBM((2,) + a.shape, bf16), cost_estimate=CHEAP, name="pair_up"
+def pair_up(a, b, us=0.001):
+    return pl.pallas_call(
+        pair_kernel, out_shape=pltpu.HBM((2,) + a.shape, bf16), cost_estimate=cost(us), name="pair_up"
     )(a, b)
 
 
@@ -778,109 +787,115 @@
 
 
 def cross_kernel(at, x_ref, g_ref, *refs):
-    s = refs[-1]
-    s[...] = lax.dot_general(x_ref[...], g_ref[...], tn_dims, preferred_element_type=f32).astype(bf16)
-    step = pl.program_id(0)
-    half = s.shape[0] // 2
-    for w in range(2):
-
-        @pl.when(step == w)
-        def _(w=w):
+    acc = refs[-1]
+    w, k = pl.program_id(0), pl.program_id(1)
+    value = jnp.dot(x_ref[...], g_ref[...], preferred_element_type=f32)
+
+    @pl.when(k == 0)
+    def _():
+        acc[...] = value
+
+    @pl.when(k > 0)
+    def _():
+        acc[...] += value
+
+    half = acc.shape[0] // 2
+    for i in range(2):
+
+        @pl.when((w == i) & (k == pl.num_programs(1) - 1))
+        def _(i=i):
             for x in range(2):
                 rows = pl.ds(pl.multiple_of((at[1] ^ x) * half, 16), half)
-                refs[2 * w + x][...] = s[rows, :]
+                refs[2 * i + x][...] = acc[rows, :].astype(bf16)
 
 
 def cross(x, g, at):
-    rows, d = x.shape
+    d, rows = x.shape
     w = d // 2
-    block = pl.BlockSpec((w // 2, g.shape[1]), lambda i, m: (0, 0))
+    step = 512
+    block = pl.BlockSpec((w // 2, g.shape[1]), lambda i, k, m: (0, 0))
     return pl.pallas_call(
         cross_kernel,
         out_shape=[pltpu.HBM((w // 2, g.shape[1]), bf16)] * 4,
         grid_spec=pltpu.PrefetchScalarGridSpec(
             num_scalar_prefetch=1,
-            grid=(2,),
+            grid=(2, rows // step),
             in_specs=[
-                pl.BlockSpec((rows, w), lambda i, m: (0, m[0] ^ i)),
-                pl.BlockSpec(g.shape, lambda i, m: (0, 0)),
+                pl.BlockSpec((w, step), lambda i, k, m: (m[0] ^ i, k)),
+                pl.BlockSpec((step, g.shape[1]), lambda i, k, m: (k, 0)),
             ],
             out_specs=[block] * 4,
-            scratch_shapes=[pltpu.VMEM((w, g.shape[1]), bf16)],
+            scratch_shapes=[pltpu.VMEM((w, g.shape[1]), f32)],
         ),
         compiler_params=pltpu.CompilerParams(vmem_limit_bytes=40 << 20),
-        cost_estimate=cost(0.001),
+        cost_estimate=CHEAP,
         name="cross",
-    )(at, x, g)
-
-
-def spread_kernel(at, *refs, groups, width):
+    )(at, hbm(x), hbm(g))
+
+
+def spread_kernel(at, own, mate, *refs, width, other_x):
     out = refs[-1]
     step = out.shape[1]
-    rows = pl.ds(pl.multiple_of(pl.program_id(1) * step, step), step)
-
-    def put(other_x, core):
+    rows = pl.ds(pl.multiple_of(pl.program_id(0) * step, step), step)
+
+    def put(core):
         cut = []
         for t in range(3):
             for n in range(2):
                 for c in range(2):
-                    for g in range(groups):
-                        part = refs[4 * g + other_x + 2 * (c ^ core)][n ^ at[1], rows, :]
-                        cut.append(part[:, t * width : (t + 1) * width])
+                    part = (own, mate)[c ^ core][n ^ at[1], rows, :]
+                    cut.append(part[:, t * width : (t + 1) * width])
         out[0] = jnp.concatenate(cut, axis=1).astype(f32)
 
-    by_bits(pl.program_id(0) ^ at[0], at[2], put)
-
-
-def spread(arrays, at, used):
-    flat = [x for group in arrays for x in group]
-    groups = len(arrays)
-    _, rows, cols = flat[0].shape
-    width = 4 * groups * used
+    for core in range(2):
+
+        @pl.when(at[2] == core)
+        def _(core=core):
+            put(core)
+
+
+def spread(own, mate, at, used, other_x, carried=None):
+    _, rows, cols = own.shape
+    width = 4 * used
     cuts = 2 if rows % 32 == 0 else 1
-    whole = pl.BlockSpec((2, rows, cols), lambda i, j, m: (0, 0, 0), pipeline_mode=pl.Buffered(1))
-    return pl.pallas_call(
-        functools.partial(spread_kernel, groups=groups, width=used // 3),
+    whole = pl.BlockSpec((2, rows, cols), lambda j, m: (0, 0, 0), pipeline_mode=pl.Buffered(1))
+    more = () if carried is None else (carried,)
+    return pl.pallas_call(
+        functools.partial(spread_kernel, width=used // 3, other_x=other_x),
         out_shape=pltpu.HBM((2, rows, width), f32),
         grid_spec=pltpu.PrefetchScalarGridSpec(
             num_scalar_prefetch=1,
-            grid=(2, cuts),
-            in_specs=[whole] * len(flat),
-            out_specs=pl.BlockSpec((1, rows // cuts, width), lambda i, j, m: (i, j, 0)),
+            grid=(cuts,),
+            in_specs=[whole] * 2 + [pl.BlockSpec(memory_space=pl.ANY)] * len(more),
+            out_specs=pl.BlockSpec((1, rows // cuts, width), lambda j, m: (m[0] ^ other_x, j, 0)),
         ),
+        input_output_aliases={3: 0} if more else {},
         compiler_params=pltpu.CompilerParams(vmem_limit_bytes=40 << 20),
         cost_estimate=CHEAP,
         name="spread",
-    )(at, *flat).reshape(2 * rows, width)
-
-
-nt_dims = (((1,), (1,)), ((), ()))
-
-
-def back_kernel(shards, *refs, groups, extra):
-    grads, weights = refs[:groups], refs[groups : 2 * groups]
-    out = refs[-1]
-    acc = sum(
-        lax.dot_general(g[...], w[...], nt_dims, preferred_element_type=f32)
-        for g, w in zip(grads, weights)
-    )
-    if extra:
-        acc = acc + refs[2 * groups][0].astype(f32)
-    out[0] = acc.astype(bf16)
-
-
-def back(grads, weights, shards, rows, got=None):
-    groups = len(grads)
-    d, c = weights[0].shape
+    )(at, own, mate, *more)
+
+
+def back_kernel(shards, g_ref, w_ref, *refs):
+    acc = jnp.dot(g_ref[...], w_ref[...], preferred_element_type=f32)
+    if len(refs) == 2:
+        acc = acc + refs[0][0].astype(f32)
+    refs[-1][0] = acc.astype(bf16)
+
+
+def back(grad, w, shards, rows, got=None):
+    c, d = w.shape
     n = shards.shape[0]
-    in_specs = [pl.BlockSpec((rows, c), lambda i, f: (f[i], 0))] * groups
-    in_specs += [pl.BlockSpec((d, c), lambda i, f: (0, 0), pipeline_mode=pl.Buffered(1))] * groups
-    args = [*map(hbm, grads), *map(hbm, weights)]
+    in_specs = [
+        pl.BlockSpec((rows, c), lambda i, f: (f[i], 0)),
+        pl.BlockSpec((c, d), lambda i, f: (0, 0), pipeline_mode=pl.Buffered(1)),
+    ]
+    args = [hbm(grad), hbm(w)]
     if got is not None:
         in_specs.append(pl.BlockSpec((1, rows, d), lambda i, f: (0, 0, 0)))
         args.append(got)
     return pl.pallas_call(
-        functools.partial(back_kernel, groups=groups, extra=got is not None),
+        back_kernel,
         out_shape=pltpu.HBM((n, rows, d), bf16),
         grid_spec=pltpu.PrefetchScalarGridSpec(
             num_scalar_prefetch=1,
@@ -894,13 +909,8 @@
     )(shards, *args)
 
 
-def finish_kernel(shard, *refs, groups):
-    grads, weights = refs[:groups], refs[groups : 2 * groups]
-    core, near, x_ref, resid, gain, out, gain_out = refs[2 * groups :]
-    grad = sum(
-        lax.dot_general(g[...], w[...], nt_dims, preferred_element_type=f32)
-        for g, w in zip(grads, weights)
-    )
+def finish_kernel(shard, g_ref, w_ref, core, near, x_ref, resid, gain, out, gain_out):
+    grad = jnp.dot(g_ref[...], w_ref[...], preferred_element_type=f32)
     grad = grad + core[0].astype(f32) + near[0].astype(f32)
     x = x_ref[...].astype(f32)
     inverse = lax.rsqrt(jnp.mean(x * x, axis=-1, keepdims=True) + epsilon)
@@ -919,22 +929,21 @@
     ).astype(bf16)
 
 
-def finish(grads, weights, shard, core, near, x, resid, gain, tile=256):
-    groups = len(grads)
+def finish(grad, w, shard, core, near, x, resid, gain, tile=256):
     rows, d = x.shape
-    c = weights[0].shape[1]
+    c = w.shape[0]
     tiles = rows // tile
     row = lambda i, f: (i, 0)
     once = pl.Buffered(1)
     return pl.pallas_call(
-        functools.partial(finish_kernel, groups=groups),
+        finish_kernel,
         out_shape=[pltpu.HBM((rows, d), bf16), jax.ShapeDtypeStruct((1, d), f32)],
         grid_spec=pltpu.PrefetchScalarGridSpec(
             num_scalar_prefetch=1,
             grid=(tiles,),
-            in_specs=[pl.BlockSpec((tile, c), lambda i, f: (f[0] * tiles + i, 0))] * groups
-            + [pl.BlockSpec((d, c), lambda i, f: (0, 0), pipeline_mode=once)] * groups
-            + [
+            in_specs=[
+                pl.BlockSpec((tile, c), lambda i, f: (f[0] * tiles + i, 0)),
+                pl.BlockSpec((c, d), lambda i, f: (0, 0), pipeline_mode=once),
                 pl.BlockSpec((1, tile, d), lambda i, f: (1, i, 0)),
                 pl.BlockSpec((1, tile, d), lambda i, f: (0, i, 0)),
                 pl.BlockSpec((tile, d), row),
@@ -946,7 +955,7 @@
         compiler_params=pltpu.CompilerParams(vmem_limit_bytes=40 << 20),
         cost_estimate=CHEAP,
         name="finish",
-    )(shard.reshape(1), *map(hbm, grads), *map(hbm, weights), core, near, hbm(x), hbm(resid), gain)
+    )(shard.reshape(1), hbm(grad), hbm(w), core, near, hbm(x), hbm(resid), gain)
 
 
 def rms_inverse(values):
@@ -1075,7 +1084,7 @@
             return lax.optimization_barrier((value,) + others)[0]
 
         picked = pick(w_qkv, mine, parts, groups, nh)
-        own = after(tokens[0], picked)
+        own = tokens[0]
         got1 = send(own, hop1)
         own_share = send(own, lane_share)
         seg_mate = send(segments, core_mate)
@@ -1088,13 +1097,10 @@
             other_w = send(picked, wt_mate)
             wide_w = (wide_own, stretch(other_w, groups, nh, 10))
         else:
-            flat_all = lax.all_gather(picked, "wt", axis=0, tiled=True)[:, : 3 * nh * HD]
-            each = flat_all.shape[1] // groups
-            flat_w = [
-                jnp.pad(flat_all[:, g * each : (g + 1) * each], ((0, 0), (0, lanes_up(each) - each)))
-                for g in range(groups)
-            ]
-            by_head = jnp.transpose(flat_all.reshape(D, groups, 3, nh // groups, HD), (0, 2, 1, 3, 4))
+            flat_all = lax.all_gather(picked, "wt", axis=0, tiled=True)
+            by_head = jnp.transpose(
+                flat_all[:, : 3 * nh * HD].reshape(D, groups, 3, nh // groups, HD), (0, 2, 1, 3, 4)
+            )
             wide_w = (
                 jnp.pad(
                     by_head.reshape(D, 3 * nh, HD), ((0, 0), (0, 0), (0, LN - HD))
@@ -1129,14 +1135,17 @@
         grad_mlp = send(after(cotangent[0], got3_share), to_host)
 
         att, att_float, q_aug = attn_fwd(queries, keyval, seg_row, nh)
-        att = after(att, grad_mlp)
+        att, half_w, _ = lax.optimization_barrier((att, half_w, grad_mlp))
 
         trades = (core_mate, near_mate, cross_mate)
         att_pieces = [rows_at(att, (mine ^ j) * rows, rows) for j in range(parts)]
         att_pieces = [att_pieces[0]] + [send(att_pieces[j + 1], trades[j]) for j in range(3)]
+        half_mate = send(half_w, core_mate)
         if pair:
-            flat_w = order(after(picked, att_pieces[1]), other_w, wt, groups, nh)
-        half_mate = send(after(half_w, att_pieces[1]), core_mate)
+            w_trans = order(after(picked, att), other_w, wt)
+        else:
+            w_trans = flat_all.T
+        normed_trans = transpose(after(all_normed, w_trans))
         if pair:
             weights = (tail_own, half_w, half_mate)
             starts = (wt * wrows, (1 - wt) * wrows + gc * half_rows, (1 - wt) * wrows + (1 - gc) * half_rows)
@@ -1155,7 +1164,7 @@
             *pieces,
             grad_gain_mlp,
         ) = tail(
-            jnp.stack([mine, *starts]), att_pieces, after(inputs, flat_w[0]), grad_mlp, weights, gain_mlp[None]
+            jnp.stack([mine, *starts]), att_pieces, after(inputs, normed_trans), grad_mlp, weights, gain_mlp[None]
         )
         pieces = [pieces[0]] + [send(pieces[j + 1], trades[j]) for j in range(3)]
 
@@ -1186,10 +1195,10 @@
 
         def by_rows(grad):
             if pair:
-                own, *rest = cross(all_normed, grad, jnp.stack([wt, gx]))
+                own, *rest = cross(normed_trans, grad, jnp.stack([wt, gx]))
                 got = [send(part, mate) for part, mate in zip(rest, (x_mate, wt_mate, wt_x_mate))]
                 return [part[None] for part in (own, *got)]
-            part = trans_times(all_normed, grad).astype(bf16)
+            part = dot(normed_trans, grad).astype(bf16)
             sources = sizes["wt"] * 2
             got = lax.all_to_all(part, ("wt", "gx"), 0, 0, tiled=True)
             return [got.reshape(sources, D // sources, -1)]
@@ -1207,11 +1216,11 @@
             return value
 
         sources = sizes["wt"] * 4
-        to_core = done(back((turn(grad_project),), flat_w, jnp.stack([mine ^ 3, mine ^ 1]), rows))
+        to_core = done(back(turn(grad_project), w_trans, jnp.stack([mine ^ 3, mine ^ 1]), rows))
         from_core = send(to_core, core_mate)
         by_place = by_rows(turn(grad_project))
         done(by_place[0])
-        to_near = done(back((grad_project,), flat_w, (mine ^ 2).reshape(1), rows, turn(from_core)))
+        to_near = done(back(grad_project, w_trans, (mine ^ 2).reshape(1), rows, turn(from_core)))
         from_near = send(to_near, near_mate)
         t1 = done(total([[turn(kept).reshape(sources, D // sources, -1)]]))
         t1_far = send(t1, far_mate)
@@ -1220,8 +1229,8 @@
         q1 = done(total([by_place]))
         q1_far = send(q1, far_mate)
         grad_tokens, grad_gain_attn = finish(
-            (grad_project,),
-            flat_w,
+            grad_project,
+            w_trans,
             mine,
             from_core,
             turn(from_near),
@@ -1233,6 +1242,15 @@
         home_grad = send(grad_tokens, to_home)
         t2 = done(add(turn(t1), t1_far))
         t2_near = send(t2, near_mate)
+        grad_query_scale = (
+            grad_lanes[0, :HD]
+            / (dim_scale * log2e)
+            * (scale_base / math.sqrt(HD))
+            * jax.nn.sigmoid(query_scale)
+        )
+        small = jnp.concatenate(
+            [grad_gain_attn[0], grad_gain_mlp[0], jnp.pad(grad_query_scale, (0, LN - HD))]
+        ).reshape(-1, LN)
         q2 = done(add(turn(q1), q1_far))
         q2_near = send(q2, near_mate)
         t4 = done(pair_up(turn(t2), t2_near))
@@ -1244,27 +1262,15 @@
         q4_core = send(q4, core_mate)
         t4_x = done(turn(t4_x))
         t4_cross = send(t4_x, core_mate)
-        at = jnp.stack([gx, near, gc])
-        totals = place_tail((turn(t4), t4_x, t4_core, t4_cross), at)
+        used = 3 * nh * HD
+        spread_at = jnp.stack([gx, near, 1 - gc])
+        totals = place_tail((turn(t4), t4_x, t4_core, t4_cross), jnp.stack([gx, near, gc]))
         done(totals[0])
+        total_qkv = done(spread(turn(q4), q4_core, spread_at, used, 0))
+        small = done(sum_all(turn(small))).reshape(-1)
         q4_x = done(turn(q4_x))
         q4_cross = send(q4_x, core_mate)
-        total_qkv = spread(
-            [(turn(q4), q4_x, q4_core, q4_cross)],
-            jnp.stack([gx, near, 1 - gc]),
-            3 * nh // groups * HD,
-        )
-
-        grad_query_scale = (
-            grad_lanes[0, :HD]
-            / (dim_scale * log2e)
-            * (scale_base / math.sqrt(HD))
-            * jax.nn.sigmoid(query_scale)
-        )
-        small = jnp.concatenate(
-            [grad_gain_attn[0], grad_gain_mlp[0], jnp.pad(grad_query_scale, (0, LN - HD))]
-        ).reshape(-1, LN)
-        small = sum_all(small).reshape(-1)
+        total_qkv = spread(turn(q4_x), q4_cross, spread_at, used, 1, total_qkv).reshape(wrows, 3 * D)
         return (
             layer_out[None],
             grad_tokens[None],

time: 456 us -> 456 us (level)
  Pallas kernels: 207 us -> 224 us
  waiting for transfers between devices: 164 us -> 151 us
    ppermute x41, waiting for transfers between devices: 164 us -> 151 us  [send(): return lax.ppermute(value, AXES, pairs(target))]
    pallas_call x5 -> x7, Pallas kernels: 29.3 us -> 40 us  [the longest x2 11.7 us: back(): pl.pallas_call(back_kernel, out_shape=pltpu.HBM((n, rows, d), bf16), grid...]
    ppermute x41, starting transfers between devices: 47.5 us -> 41.2 us  [send(): return lax.ppermute(value, AXES, pairs(target))]
    pallas_call x1, Pallas kernels: 8.52 us -> 13.7 us  [cross(): pl.pallas_call(cross_kernel, out_shape=[pltpu.HBM((w // 2, g.shape[1]), b...]
    unnamed x70 -> x68, local copies, waits for them, and re-layouts: 9.93 us -> 6.31 us
  transfers between devices with their start and end apart: 42 -> 42, of which waited for: 23 -> 20; matrix products, arithmetic and copies ran while one was open for 3% -> 3% of each run, Pallas kernels for 39% -> 44%
where the time goes in v9:
time: 456 us; the launch traced here: 449 us
  Pallas kernels  224 us (49%)
  waiting for transfers between devices  151 us (33%)
  starting transfers between devices  51.1 us (11%)
  local copies, waits for them, and re-layouts  14.4 us (3%)
  other arithmetic  6.85 us (2%)
    ppermute x41, waiting for transfers between devices, send(): return lax.ppermute(value, AXES, pairs(target))  151 us
    pallas_call x1, Pallas kernels, attn_bwd(): pl.pallas_call(functools.partial(bwd_kernel, first=group * nh, nh=nh, bq=...  44.7 us
    ppermute x41, starting transfers between devices, send(): return lax.ppermute(value, AXES, pairs(target))  41.2 us
    pallas_call x1, Pallas kernels, attn_fwd(): pl.pallas_call(functools.partial(fwd_kernel, nh=nh, bq=bq, bk=bk, nk=n //...  26 us
    pallas_call x2, Pallas kernels, project(): pl.pallas_call(functools.partial(project_kernel, count=count, halves=len(...  22.8 us
    pallas_call x1, Pallas kernels, tail(): pl.pallas_call(body, out_shape=[pltpu.HBM((rows, d), bf16)] + [pltpu.HBM(...  22.4 us
    pallas_call x2, Pallas kernels, share(): pl.pallas_call(share_kernel, out_shape=pltpu.HBM((d, n * w), bf16), grid_...  16.2 us
    pallas_call x1, Pallas kernels, cross(): pl.pallas_call(cross_kernel, out_shape=[pltpu.HBM((w // 2, g.shape[1]), b...  13.7 us
  transfers between devices with their start and end apart: 42, of which 20 were waited for; matrix products, arithmetic and copies ran while one was open for 3% of the time, Pallas kernels for 44%

profile of v9, /device:TPU:0, one launch (start us, length us, event | category | flops | bytes accessed | tf_op | source)
XLA Modules:
  0.0 448.6 jit_solution(3932411142231947816)
XLA Ops:
  1.9 7.2 %collective-permute-start.5 = (bf16[512,1280]{1,0:T(8,128)(2,1)}, bf16[512,1280]{1,0:T(8,128)(2,1)}, u32[]{:S(2)}, u32[]{:S(2)}) collective-permute-start(bf16[512,1280]{1,0:T(8,128)(2,1)} %bitcast.65), channel_id=1, source_target_pairs={{0,8},{1,9},{2,10},{3,11},{12,4},{13,5},{14,6},{15,7},{16,24},{17,... | collective-permute-start | bytes 3932168 | tf_op jit(solution)/shard_map/ppermute | solution.py:1007
  9.2 4.4 pick.1.x_ref.a_ref
  15.7 4.2 stretch.2.refs_5_
  19.9 4.2 pad_maximum_fusion.own
  32.0 10.9 %collective-permute-done.7.x_ref.b_ref = bf16[640,1024]{1,0:T(8,128)(2,1)} collective-permute-done((bf16[640,1024]{1,0:T(8,128)(2,1)}, bf16[640,1024]{1,0:T(8,128)(2,1)}, u32[]{:S(2)}, u32[]{:S(2)}) %collective-permute-start.7) | collective-permute-done | bytes 1310752 | tf_op jit(solution)/shard_map/ppermute | solution.py:1007
  51.9 11.2 %project.2 = (bf16[2048,1280]{1,0:T(8,128)(2,1)}, bf16[2048,512]{1,0:T(8,128)(2,1)}, bf16[2048,1024]{1,0:T(8,128)(2,1)}, bf16[512,1280]{1,0:T(8,128)(2,1)}) custom-call(s32[5]{0:T(128)S(1)} %stack.101.info, bf16[512,1280]{1,0:T(8,128)(2,1)S(1)} %bitcast.66, bf16[512,1280]{1,0:T(8,128)(2,1)} %collective-permute-done.5.refs_1_, ...), custom_call_target="tpu_custom_call" | custom-call | flops 15000000512 | bytes 1000 | tf_op jit(solution)/shard_map/project/pallas_call | solution.py:506
  73.4 11.6 %project.3 = (bf16[2048,1280]{1,0:T(8,128)(2,1)}, bf16[2048,512]{1,0:T(8,128)(2,1)}, bf16[2048,1024]{1,0:T(8,128)(2,1)}, bf16[512,1280]{1,0:T(8,128)(2,1)}) custom-call(s32[5]{0:T(128)S(1)} %stack.98.info, bf16[512,1280]{1,0:T(8,128)(2,1)S(1)} %collective-permute-done.2.refs_0_, ...), custom_call_target="tpu_custom_call", output_to_operand_aliasing={{0}: (11, {}), {1}: (12, {}), {2}: (13, {})} | custom-call | flops 15000000512 | bytes 1000 | tf_op jit(solution)/shard_map/project/pallas_call | solution.py:506
  85.0 26.0 %attn_fwd.1 = (bf16[2048,320]{1,0:T(8,128)(2,1)}, bf16[2048,512]{1,0:T(8,128)(2,1)}, bf16[2048,512]{1,0:T(8,128)(2,1)}) custom-call(s32[16]{0:T(128)S(1)} %reshape.178.flags, bf16[2048,512]{1,0:T(8,128)(2,1)} %get-tuple-element.81.q_ref, bf16[2048,1024]{1,0:T(8,128)(2,1)} %get-tuple-element.82.kv.kk.vv, s32[2048,1]{1,0:T(8,128)S(1)} %copy.28.segc, ...), custom_call_target="tpu_custom_call" | custom-call | flops 10000000 | bytes 1000 | tf_op jit(solution)/shard_map/attn_fwd/pallas_call | solution.py:168
  111.0 4.8 %collective-permute-done.9.half = bf16[3,320,1280]{2,1,0:T(8,128)(2,1)} collective-permute-done((bf16[3,320,1280]{2,1,0:T(8,128)(2,1)}, bf16[3,320,1280]{2,1,0:T(8,128)(2,1)}, u32[]{:S(2)}, u32[]{:S(2)}) %collective-permute-start.9) | collective-permute-done | bytes 2457632 | tf_op jit(solution)/shard_map/ppermute | solution.py:1007
  121.1 6.4 %order.1.w_ref = bf16[1024,1280]{1,0:T(8,128)(2,1)} custom-call(s32[1]{0:T(128)} %bitcast.10.own_first, bf16[640,1024]{1,0:T(8,128)(2,1)} %pick.1.x_ref.a_ref, bf16[640,1024]{1,0:T(8,128)(2,1)} %collective-permute-done.7.x_ref.b_ref), custom_call_target="tpu_custom_call" | custom-call | flops 199999995904 | bytes 1000 | tf_op jit(solution)/shard_map/order/pallas_call | solution.py:396
  127.5 7.8 %transpose.15.x_ref = bf16[1280,2048]{1,0:T(8,128)(2,1)} custom-call(bf16[2048,1280]{1,0:T(8,128)(2,1)} %get-tuple-element.90.x_ref), custom_call_target="tpu_custom_call" | custom-call | flops 1000000 | bytes 1000 | tf_op jit(solution)/shard_map/transpose/pallas_call | solution.py:420
  138.6 22.4 %tail.1 = (bf16[512,1280]{1,0:T(8,128)(2,1)}, bf16[3,512,1280]{2,1,0:T(8,128)(2,1)}, bf16[3,512,1280]{2,1,0:T(8,128)(2,1)}, f32[512,1280]{1,0:T(8,128)}, bf16[51...) custom-call(s32[4]{0:T(128)S(1)} %pad_add_fusion.at, ...), custom_call_target="tpu_custom_call" | custom-call | flops 10000000 | bytes 1000 | tf_op jit(solution)/shard_map/tail/pallas_call | solution.py:618
  163.7 7.3 %share.2 = bf16[1280,1920]{1,0:T(8,128)(2,1)} custom-call(s32[1]{0:T(128)} %bitcast.21.col, bf16[3,512,1280]{2,1,0:T(8,128)(2,1)} %get-tuple-element.97.left, bf16[3,512,1280]{2,1,0:T(8,128)(2,1)} %get-tuple-element.98.right), custom_call_target="tpu_custom_call" | custom-call | flops 1000000 | bytes 1000 | tf_op jit(solution)/shard_map/share/pallas_call | solution.py:656
  173.2 8.7 %collective-permute-done.16.do2 = bf16[512,320]{1,0:T(8,128)(2,1)S(1)} collective-permute-done((bf16[512,320]{1,0:T(8,128)(2,1)}, bf16[512,320]{1,0:T(8,128)(2,1)S(1)}, u32[]{:S(2)}, u32[]{:S(2)}) %collective-permute-start.16) | collective-permute-done | bytes 327712 | tf_op jit(solution)/shard_map/ppermute | solution.py:1007
  183.7 8.9 %share.3 = bf16[1280,1920]{1,0:T(8,128)(2,1)} custom-call(s32[1]{0:T(128)} %bitcast.22.col, bf16[3,512,1280]{2,1,0:T(8,128)(2,1)} %get-tuple-element.97.left, bf16[3,512,1280]{2,1,0:T(8,128)(2,1)} %get-tuple-element.98.right, bf16[1280,1920]{1,0:T(8,128)(2,1)} %collective-permute-done.19.refs_0_), custom_call_target="tpu_custom_call" | custom-call | flops 1000000 | bytes 1000 | tf_op jit(solution)/shard_map/share/pallas_call | solution.py:656
  192.6 9.8 %all-to-all-start = ((bf16[8,160,1920]{2,1,0:T(8,128)(2,1)}), bf16[8,160,1920]{2,1,0:T(8,128)(2,1)}, u32[]{:S(2)}, u32[]{:S(2)}) async-start(bf16[8,160,1920]{2,1,0:T(8,128)(2,1)} %bitcast.75), calls=%async_computation | async-start | bytes 9830400 | tf_op jit(solution)/shard_map/all_to_all | solution.py:1177
  202.5 44.7 %attn_bwd.1 = (bf16[2048,1024]{1,0:T(8,128)(2,1)}, f32[8,128]{1,0:T(8,128)}) custom-call(s32[16]{0:T(128)S(1)} %copy-done.7, s32[1]{0:T(128)} %bitcast.mine.shard, bf16[2048,512]{1,0:T(8,128)(2,1)} %get-tuple-element.103.qa, bf16[2048,1024]{1,0:T(8,128)(2,1)} %get-tuple-element.82.kv.kk.vv, bf16[2048,1024]{1,0:T(8,128)(2,1)} %get-tuple-element.82.kv.kk.vv, ...), custom_call_target="tpu_custom_call" | custom-call | flops 299999985664 | bytes 1000 | tf_op jit(solution)/shard_map/attn_bwd/pallas_call | solution.py:302
  247.2 7.0 %back.2 = bf16[2,512,1280]{2,1,0:T(8,128)(2,1)} custom-call(s32[2]{0:T(128)S(1)} %pad_add_fusion.1.shards, bf16[2048,1024]{1,0:T(8,128)(2,1)} %get-tuple-element.112.g_ref, bf16[1024,1280]{1,0:T(8,128)(2,1)} %order.1.w_ref), custom_call_target="tpu_custom_call" | custom-call | flops 1000000 | bytes 1000 | tf_op jit(solution)/shard_map/back/pallas_call | solution.py:897
  254.3 13.7 %cross.1 = (bf16[320,1024]{1,0:T(8,128)(2,1)}, bf16[320,1024]{1,0:T(8,128)(2,1)}, bf16[320,1024]{1,0:T(8,128)(2,1)}, bf16[320,1024]{1,0:T(8,128)(2,1)}) custom-call(s32[2]{0:T(128)S(1)} %pad_add_fusion.2.at, bf16[1280,2048]{1,0:T(8,128)(2,1)} %transpose.15.x_ref, bf16[2048,1024]{1,0:T(8,128)(2,1)} %get-tuple-element.112.g_ref), custom_call_target="tpu_custom_call" | custom-call | flops 1000000 | bytes 1000 | tf_op jit(solution)/shard_map/cross/pallas_call | solution.py:817
  268.0 4.7 %back.3 = bf16[1,512,1280]{2,1,0:T(8,128)(2,1)} custom-call(s32[1]{0:T(128)} %bitcast.26.shards, bf16[2048,1024]{1,0:T(8,128)(2,1)} %get-tuple-element.112.g_ref, bf16[1024,1280]{1,0:T(8,128)(2,1)} %order.1.w_ref, bf16[2,512,1280]{2,1,0:T(8,128)(2,1)S(1)} %collective-permute-done.20.refs_0_.core), custom_call_target="tpu_custom_call" | custom-call | flops 1000000 | bytes 1000 | tf_op jit(solution)/shard_map/back/pallas_call | solution.py:897
  284.1 8.4 %collective-permute-done.22 = bf16[320,1024]{1,0:T(8,128)(2,1)} collective-permute-done((bf16[320,1024]{1,0:T(8,128)(2,1)}, bf16[320,1024]{1,0:T(8,128)(2,1)}, u32[]{:S(2)}, u32[]{:S(2)}) %collective-permute-start.22) | collective-permute-done | bytes 655392 | tf_op jit(solution)/shard_map/ppermute | solution.py:1007
  292.5 14.5 %collective-permute-done.23 = bf16[320,1024]{1,0:T(8,128)(2,1)} collective-permute-done((bf16[320,1024]{1,0:T(8,128)(2,1)}, bf16[320,1024]{1,0:T(8,128)(2,1)}, u32[]{:S(2)}, u32[]{:S(2)}) %collective-permute-start.23) | collective-permute-done | bytes 655392 | tf_op jit(solution)/shard_map/ppermute | solution.py:1007
  309.5 8.2 %collective-permute-done.21.near = bf16[1,512,1280]{2,1,0:T(8,128)(2,1)} collective-permute-done((bf16[1,512,1280]{2,1,0:T(8,128)(2,1)}, bf16[1,512,1280]{2,1,0:T(8,128)(2,1)}, u32[]{:S(2)}, u32[]{:S(2)}) %collective-permute-start.21) | collective-permute-done | bytes 1310752 | tf_op jit(solution)/shard_map/ppermute | solution.py:1007
  317.7 6.6 %finish.1 = (bf16[512,1280]{1,0:T(8,128)(2,1)}, f32[1,1280]{1,0:T(1,128)S(1)}) custom-call(s32[1]{0:T(128)} %bitcast.mine.shard, bf16[2048,1024]{1,0:T(8,128)(2,1)} %get-tuple-element.112.g_ref, bf16[1024,1280]{1,0:T(8,128)(2,1)} %order.1.w_ref, bf16[2,512,1280]{2,1,0:T(8,128)(2,1)S(1)} %collective-permute-done.20.refs_0_.core, ...), custom_call_target="tpu_custom_call" | custom-call | flops 1000000 | bytes 1000 | tf_op jit(solution)/shard_map/finish/pallas_call | solution.py:938
  328.5 16.7 %collective-permute-done.27.b_ref = bf16[320,1024]{1,0:T(8,128)(2,1)S(1)} collective-permute-done((bf16[320,1024]{1,0:T(8,128)(2,1)}, bf16[320,1024]{1,0:T(8,128)(2,1)S(1)}, u32[]{:S(2)}, u32[]{:S(2)}) %collective-permute-start.27) | collective-permute-done | bytes 655392 | tf_op jit(solution)/shard_map/ppermute | solution.py:1007
  348.3 19.3 %collective-permute-done.28.b_ref = bf16[160,1920]{1,0:T(8,128)(2,1)S(1)} collective-permute-done((bf16[160,1920]{1,0:T(8,128)(2,1)}, bf16[160,1920]{1,0:T(8,128)(2,1)S(1)}, u32[]{:S(2)}, u32[]{:S(2)}) %collective-permute-start.28) | collective-permute-done | bytes 614432 | tf_op jit(solution)/shard_map/ppermute | solution.py:1007
  372.2 14.4 %collective-permute-done.29.b_ref = bf16[320,1024]{1,0:T(8,128)(2,1)S(1)} collective-permute-done((bf16[320,1024]{1,0:T(8,128)(2,1)S(1)}, bf16[320,1024]{1,0:T(8,128)(2,1)S(1)}, u32[]{:S(2)}, u32[]{:S(2)}) %collective-permute-start.29) | collective-permute-done | bytes 655392 | tf_op jit(solution)/shard_map/ppermute | solution.py:1007
  391.6 9.6 %collective-permute-done.31.own_x = bf16[2,160,1920]{2,1,0:T(8,128)(2,1)} collective-permute-done((bf16[2,160,1920]{2,1,0:T(8,128)(2,1)}, bf16[2,160,1920]{2,1,0:T(8,128)(2,1)}, u32[]{:S(2)}, u32[]{:S(2)}) %collective-permute-start.31) | collective-permute-done | bytes 1228832 | tf_op jit(solution)/shard_map/ppermute | solution.py:1007
  404.4 6.6 %place_tail.1 = (f32[4,160,1280]{2,1,0:T(8,128)}, f32[4,160,1280]{2,1,0:T(8,128)}, f32[4,160,1280]{2,1,0:T(8,128)}) custom-call(s32[3]{0:T(128)S(1)} %pad_add_fusion.5.at, bf16[2,160,1920]{2,1,0:T(8,128)(2,1)S(1)} %copy-done.1, bf16[2,160,1920]{2,1,0:T(8,128)(2,1)} %collective-permute-done.31.own_x, bf16[2,160,1920]{2,1,0:T(8,128)(2,1)} %collective-permute-done.32.mate, ...), custom_call_target="tpu_custom_call" | custom-call | flops 1000000 | bytes 1000 | tf_op jit(solution)/shard_map/place_tail/pallas_call | solution.py:773
  411.0 4.4 spread.2.refs_0_
  416.7 9.7 %collective-permute-done.35 = f32[21,128]{1,0:T(8,128)S(1)} collective-permute-done((f32[21,128]{1,0:T(8,128)S(1)}, f32[21,128]{1,0:T(8,128)S(1)}, u32[]{:S(2)}, u32[]{:S(2)}) %collective-permute-start.35) | collective-permute-done | bytes 10784 | tf_op jit(solution)/shard_map/ppermute | solution.py:1007
  427.6 4.6 %collective-permute-done.37 = f32[21,128]{1,0:T(8,128)S(1)} collective-permute-done((f32[21,128]{1,0:T(8,128)S(1)}, f32[21,128]{1,0:T(8,128)S(1)}, u32[]{:S(2)}, u32[]{:S(2)}) %collective-permute-start.37) | collective-permute-done | bytes 10784 | tf_op jit(solution)/shard_map/ppermute | solution.py:1007
  (189 shorter events, 98.2 us)
Async XLA Ops:
  0.6 23.5 %collective-permute-start.1 = (bf16[512,1280]{1,0:T(8,128)(2,1)}, bf16[512,1280]{1,0:T(8,128)(2,1)}, u32[]{:S(2)}, u32[]{:S(2)}) collective-permute-start(bf16[512,1280]{1,0:T(8,128)(2,1)} %bitcast.64), channel_id=1, source_target_pairs={{2,0},{3,1},{4,2},{5,3},{6,4},{7,5},{8,10},{9,11},{10,12},{11,13},... | collective-permute-start | bytes 3932168 | tf_op jit(solution)/shard_map/ppermute | solution.py:1007
  1.9 49.9 %collective-permute-start.5 = (bf16[512,1280]{1,0:T(8,128)(2,1)}, bf16[512,1280]{1,0:T(8,128)(2,1)}, u32[]{:S(2)}, u32[]{:S(2)}) collective-permute-start(bf16[512,1280]{1,0:T(8,128)(2,1)} %bitcast.65), channel_id=1, source_target_pairs={{0,8},{1,9},{2,10},{3,11},{12,4},{13,5},{14,6},{15,7},{16,24},{17,... | collective-permute-start | bytes 3932168 | tf_op jit(solution)/shard_map/ppermute | solution.py:1007
  13.6 29.3 %collective-permute-start.7 = (bf16[640,1024]{1,0:T(8,128)(2,1)}, bf16[640,1024]{1,0:T(8,128)(2,1)}, u32[]{:S(2)}, u32[]{:S(2)}) collective-permute-start(bf16[640,1024]{1,0:T(8,128)(2,1)} %pick.1.x_ref.a_ref), channel_id=1, source_target_pairs={{0,1},{1,0},{2,3},{3,2},{4,5},{5,4},{6,7},{7,6},{8,9},{9,8},{10,11... | collective-permute-start | bytes 3932168 | tf_op jit(solution)/shard_map/ppermute | solution.py:1007
  15.1 55.6 %collective-permute-start = (s32[1,2048]{1,0:T(1,128)S(1)}, s32[1,2048]{1,0:T(1,128)S(1)}, u32[]{:S(2)}, u32[]{:S(2)}) collective-permute-start(s32[1,2048]{1,0:T(1,128)S(1)} %copy-done.25), channel_id=1, source_target_pairs={{0,8},{1,9},{2,10},{3,11},{4,12},{5,13},{6,14},{7,15},{8,0},{9,1},... | collective-permute-start | bytes 24584 | tf_op jit(solution)/shard_map/ppermute | solution.py:1007
  24.1 22.8 %collective-permute-start.2 = (bf16[512,1280]{1,0:T(8,128)(2,1)}, bf16[512,1280]{1,0:T(8,128)(2,1)S(1)}, u32[]{:S(2)}, u32[]{:S(2)}) collective-permute-start(bf16[512,1280]{1,0:T(8,128)(2,1)} %collective-permute-done.1.refs_2_), channel_id=1, source_target_pairs={{2,0},{3,1},{4,2},{5,3},{10,12},{11,13},{12,14},{13,15},{18,16},{1... | collective-permute-start | bytes 3932168 | tf_op jit(solution)/shard_map/ppermute | solution.py:1007
  28.9 22.9 %collective-permute-start.6 = (bf16[512,1280]{1,0:T(8,128)(2,1)}, bf16[512,1280]{1,0:T(8,128)(2,1)}, u32[]{:S(2)}, u32[]{:S(2)}) collective-permute-start(bf16[512,1280]{1,0:T(8,128)(2,1)} %collective-permute-done.1.refs_2_), channel_id=1, source_target_pairs={{0,8},{1,9},{2,10},{3,11},{12,4},{13,5},{14,6},{15,7},{16,24},{17,... | collective-permute-start | bytes 3932168 | tf_op jit(solution)/shard_map/ppermute | solution.py:1007
  47.1 19.6 %collective-permute-start.4 = (bf16[512,1280]{1,0:T(8,128)(2,1)S(1)}, bf16[512,1280]{1,0:T(8,128)(2,1)}, u32[]{:S(2)}, u32[]{:S(2)}) collective-permute-start(bf16[512,1280]{1,0:T(8,128)(2,1)S(1)} %broadcast_select_fusion), channel_id=1, source_target_pairs={{0,2},{1,3},{2,0},{3,1},{12,14},{13,15},{14,12},{15,13},{16,18},{1... | collective-permute-start | bytes 3932168 | tf_op jit(solution)/shard_map/ppermute | solution.py:1007
  49.5 23.9 %collective-permute-start.3 = (bf16[512,1280]{1,0:T(8,128)(2,1)S(1)}, bf16[512,1280]{1,0:T(8,128)(2,1)}, u32[]{:S(2)}, u32[]{:S(2)}) collective-permute-start(bf16[512,1280]{1,0:T(8,128)(2,1)S(1)} %collective-permute-done.2.refs_0_), channel_id=1, source_target_pairs={{0,8},{1,9},{2,10},{3,11},{12,4},{13,5},{14,6},{15,7},{16,24},{17,... | collective-permute-start | bytes 3932168 | tf_op jit(solution)/shard_map/ppermute | solution.py:1007
  69.2 46.6 %collective-permute-start.9 = (bf16[3,320,1280]{2,1,0:T(8,128)(2,1)}, bf16[3,320,1280]{2,1,0:T(8,128)(2,1)}, u32[]{:S(2)}, u32[]{:S(2)}) collective-permute-start(bf16[3,320,1280]{2,1,0:T(8,128)(2,1)} %constant_dynamic-slice_fusion.4), channel_id=1, source_target_pairs={{0,1},{1,0},{2,3},{3,2},{4,5},{5,4},{6,7},{7,6},{8,9},{9,8},{10,11... | collective-permute-start | bytes 7372808 | tf_op jit(solution)/shard_map/ppermute | solution.py:1007
  72.8 43.0 %collective-permute-start.10 = (bf16[512,1280]{1,0:T(8,128)(2,1)}, bf16[512,1280]{1,0:T(8,128)(2,1)S(1)}, u32[]{:S(2)}, u32[]{:S(2)}) collective-permute-start(bf16[512,1280]{1,0:T(8,128)(2,1)} %bitcast.88), channel_id=1, source_target_pairs={{0,8},{1,9},{2,0},{3,1},{4,10},{5,11},{6,2},{7,3},{8,12},{9,13},{1... | collective-permute-start | bytes 3932168 | tf_op jit(solution)/shard_map/ppermute | solution.py:1007
  116.9 21.7 %collective-permute-start.14 = (bf16[3,320,1280]{2,1,0:T(8,128)(2,1)}, bf16[3,320,1280]{2,1,0:T(8,128)(2,1)}, u32[]{:S(2)}, u32[]{:S(2)}) collective-permute-start(bf16[3,320,1280]{2,1,0:T(8,128)(2,1)} %collective-permute-done.9.half), channel_id=1, source_target_pairs={{0,8},{1,9},{2,10},{3,11},{4,12},{5,13},{6,14},{7,15},{8,0},{9,1},... | collective-permute-start | bytes 7372808 | tf_op jit(solution)/shard_map/ppermute | solution.py:1007
  119.3 16.1 %collective-permute-start.11 = (bf16[512,320]{1,0:T(8,128)(2,1)}, bf16[512,320]{1,0:T(8,128)(2,1)}, u32[]{:S(2)}, u32[]{:S(2)}) collective-permute-start(bf16[512,320]{1,0:T(8,128)(2,1)} %get-tuple-element.147), channel_id=1, source_target_pairs={{0,8},{1,9},{2,10},{3,11},{4,12},{5,13},{6,14},{7,15},{8,0},{9,1},... | collective-permute-start | bytes 983048 | tf_op jit(solution)/shard_map/ppermute | solution.py:1007
  119.8 15.6 %collective-permute-start.12 = (bf16[512,320]{1,0:T(8,128)(2,1)}, bf16[512,320]{1,0:T(8,128)(2,1)}, u32[]{:S(2)}, u32[]{:S(2)}) collective-permute-start(bf16[512,320]{1,0:T(8,128)(2,1)} %get-tuple-element.146), channel_id=1, source_target_pairs={{0,2},{1,3},{2,0},{3,1},{4,6},{5,7},{6,4},{7,5},{8,10},{9,11},{10,... | collective-permute-start | bytes 983048 | tf_op jit(solution)/shard_map/ppermute | solution.py:1007
  120.2 18.3 %collective-permute-start.13 = (bf16[512,320]{1,0:T(8,128)(2,1)}, bf16[512,320]{1,0:T(8,128)(2,1)}, u32[]{:S(2)}, u32[]{:S(2)}) collective-permute-start(bf16[512,320]{1,0:T(8,128)(2,1)} %get-tuple-element.145), channel_id=1, source_target_pairs={{0,10},{1,11},{2,8},{3,9},{4,14},{5,15},{6,12},{7,13},{8,2},{9,3},... | collective-permute-start | bytes 983048 | tf_op jit(solution)/shard_map/ppermute | solution.py:1007
  161.9 11.4 %collective-permute-start.17 = (bf16[512,320]{1,0:T(8,128)(2,1)}, bf16[512,320]{1,0:T(8,128)(2,1)S(1)}, u32[]{:S(2)}, u32[]{:S(2)}) collective-permute-start(bf16[512,320]{1,0:T(8,128)(2,1)} %get-tuple-element.100), channel_id=1, source_target_pairs={{0,10},{1,11},{2,8},{3,9},{4,14},{5,15},{6,12},{7,13},{8,2},{9,3},... | collective-permute-start | bytes 983048 | tf_op jit(solution)/shard_map/ppermute | solution.py:1007
  162.0 19.9 %collective-permute-start.16 = (bf16[512,320]{1,0:T(8,128)(2,1)}, bf16[512,320]{1,0:T(8,128)(2,1)S(1)}, u32[]{:S(2)}, u32[]{:S(2)}) collective-permute-start(bf16[512,320]{1,0:T(8,128)(2,1)} %get-tuple-element.95), channel_id=1, source_target_pairs={{0,2},{1,3},{2,0},{3,1},{4,6},{5,7},{6,4},{7,5},{8,10},{9,11},{10,... | collective-permute-start | bytes 983048 | tf_op jit(solution)/shard_map/ppermute | solution.py:1007
  171.1 12.6 %collective-permute-start.19 = (bf16[1280,1920]{1,0:T(8,128)(2,1)}, bf16[1280,1920]{1,0:T(8,128)(2,1)}, u32[]{:S(2)}, u32[]{:S(2)}) collective-permute-start(bf16[1280,1920]{1,0:T(8,128)(2,1)} %share.2), channel_id=1, source_target_pairs={{0,8},{1,9},{2,10},{3,11},{4,12},{5,13},{6,14},{7,15},{8,0},{9,1},... | collective-permute-start | bytes 14745608 | tf_op jit(solution)/shard_map/ppermute | solution.py:1007
  183.2 64.0 %collective-permute-start.18 = (bf16[512,1280]{1,0:T(8,128)(2,1)}, bf16[512,1280]{1,0:T(8,128)(2,1)}, u32[]{:S(2)}, u32[]{:S(2)}) collective-permute-start(bf16[512,1280]{1,0:T(8,128)(2,1)} %get-tuple-element.102), channel_id=1, source_target_pairs={{0,2},{1,3},{2,6},{3,7},{4,10},{5,11},{6,14},{7,15},{8,0},{9,1},{1... | collective-permute-start | bytes 3932168 | tf_op jit(solution)/shard_map/ppermute | solution.py:1007
  192.6 85.5 %all-to-all-start = ((bf16[8,160,1920]{2,1,0:T(8,128)(2,1)}), bf16[8,160,1920]{2,1,0:T(8,128)(2,1)}, u32[]{:S(2)}, u32[]{:S(2)}) async-start(bf16[8,160,1920]{2,1,0:T(8,128)(2,1)} %bitcast.75), calls=%async_computation | async-start | bytes 9830400 | tf_op jit(solution)/shard_map/all_to_all | solution.py:1177
  254.2 13.8 %collective-permute-start.20 = (bf16[2,512,1280]{2,1,0:T(8,128)(2,1)}, bf16[2,512,1280]{2,1,0:T(8,128)(2,1)S(1)}, u32[]{:S(2)}, u32[]{:S(2)}) collective-permute-start(bf16[2,512,1280]{2,1,0:T(8,128)(2,1)} %back.2), channel_id=1, source_target_pairs={{0,8},{1,9},{2,10},{3,11},{4,12},{5,13},{6,14},{7,15},{8,0},{9,1},... | collective-permute-start | bytes 7864328 | tf_op jit(solution)/shard_map/ppermute | solution.py:1007
  272.6 45.0 %collective-permute-start.21 = (bf16[1,512,1280]{2,1,0:T(8,128)(2,1)}, bf16[1,512,1280]{2,1,0:T(8,128)(2,1)}, u32[]{:S(2)}, u32[]{:S(2)}) collective-permute-start(bf16[1,512,1280]{2,1,0:T(8,128)(2,1)} %back.3), channel_id=1, source_target_pairs={{0,2},{1,3},{2,0},{3,1},{4,6},{5,7},{6,4},{7,5},{8,10},{9,11},{10,... | collective-permute-start | bytes 3932168 | tf_op jit(solution)/shard_map/ppermute | solution.py:1007
  274.6 17.9 %collective-permute-start.22 = (bf16[320,1024]{1,0:T(8,128)(2,1)}, bf16[320,1024]{1,0:T(8,128)(2,1)}, u32[]{:S(2)}, u32[]{:S(2)}) collective-permute-start(bf16[320,1024]{1,0:T(8,128)(2,1)} %get-tuple-element.118), channel_id=1, source_target_pairs={{0,16},{1,17},{2,18},{3,19},{4,20},{5,21},{6,22},{7,23},{8,24},{9,... | collective-permute-start | bytes 1966088 | tf_op jit(solution)/shard_map/ppermute | solution.py:1007
  276.1 30.9 %collective-permute-start.23 = (bf16[320,1024]{1,0:T(8,128)(2,1)}, bf16[320,1024]{1,0:T(8,128)(2,1)}, u32[]{:S(2)}, u32[]{:S(2)}) collective-permute-start(bf16[320,1024]{1,0:T(8,128)(2,1)} %get-tuple-element.119), channel_id=1, source_target_pairs={{0,1},{1,0},{2,3},{3,2},{4,5},{5,4},{6,7},{7,6},{8,9},{9,8},{10,11... | collective-permute-start | bytes 1966088 | tf_op jit(solution)/shard_map/ppermute | solution.py:1007
  277.6 29.5 %collective-permute-start.24 = (bf16[320,1024]{1,0:T(8,128)(2,1)}, bf16[320,1024]{1,0:T(8,128)(2,1)}, u32[]{:S(2)}, u32[]{:S(2)}) collective-permute-start(bf16[320,1024]{1,0:T(8,128)(2,1)} %get-tuple-element.120), channel_id=1, source_target_pairs={{0,17},{1,16},{2,19},{3,18},{4,21},{5,20},{6,23},{7,22},{8,25},{9,... | collective-permute-start | bytes 1966088 | tf_op jit(solution)/shard_map/ppermute | solution.py:1007
  281.6 42.6 %collective-permute-start.26 = (bf16[160,1920]{1,0:T(8,128)(2,1)}, bf16[160,1920]{1,0:T(8,128)(2,1)}, u32[]{:S(2)}, u32[]{:S(2)}) collective-permute-start(bf16[160,1920]{1,0:T(8,128)(2,1)} %total.2.a_ref), channel_id=1, source_target_pairs={{0,4},{1,5},{2,6},{3,7},{4,0},{5,1},{6,2},{7,3},{8,12},{9,13},{10,... | collective-permute-start | bytes 1843208 | tf_op jit(solution)/shard_map/ppermute | solution.py:1007
  309.4 35.8 %collective-permute-start.27 = (bf16[320,1024]{1,0:T(8,128)(2,1)}, bf16[320,1024]{1,0:T(8,128)(2,1)S(1)}, u32[]{:S(2)}, u32[]{:S(2)}) collective-permute-start(bf16[320,1024]{1,0:T(8,128)(2,1)} %total.3.a_ref), channel_id=1, source_target_pairs={{0,4},{1,5},{2,6},{3,7},{4,0},{5,1},{6,2},{7,3},{8,12},{9,13},{10,... | collective-permute-start | bytes 1966088 | tf_op jit(solution)/shard_map/ppermute | solution.py:1007
  326.4 41.2 %collective-permute-start.28 = (bf16[160,1920]{1,0:T(8,128)(2,1)}, bf16[160,1920]{1,0:T(8,128)(2,1)S(1)}, u32[]{:S(2)}, u32[]{:S(2)}) collective-permute-start(bf16[160,1920]{1,0:T(8,128)(2,1)} %add.133.a_ref), channel_id=1, source_target_pairs={{0,2},{1,3},{2,0},{3,1},{4,6},{5,7},{6,4},{7,5},{8,10},{9,11},{10,... | collective-permute-start | bytes 1843208 | tf_op jit(solution)/shard_map/ppermute | solution.py:1007
  326.4 45.8 %collective-permute-start.25 = (bf16[512,1280]{1,0:T(8,128)(2,1)}, bf16[512,1280]{1,0:T(8,128)(2,1)}, u32[]{:S(2)}, u32[]{:S(2)}) collective-permute-start(bf16[512,1280]{1,0:T(8,128)(2,1)} %get-tuple-element.123), channel_id=1, source_target_pairs={{0,2},{1,3},{2,6},{3,7},{4,10},{5,11},{6,14},{7,15},{8,0},{9,1},{1... | collective-permute-start | bytes 3932168 | tf_op jit(solution)/shard_map/ppermute | solution.py:1007
  370.8 30.3 %collective-permute-start.31 = (bf16[2,160,1920]{2,1,0:T(8,128)(2,1)}, bf16[2,160,1920]{2,1,0:T(8,128)(2,1)}, u32[]{:S(2)}, u32[]{:S(2)}) collective-permute-start(bf16[2,160,1920]{2,1,0:T(8,128)(2,1)} %pair_up.2.own), channel_id=1, source_target_pairs={{0,16},{1,17},{2,18},{3,19},{4,20},{5,21},{6,22},{7,23},{8,24},{9,... | collective-permute-start | bytes 3686408 | tf_op jit(solution)/shard_map/ppermute | solution.py:1007
  372.2 14.4 %collective-permute-start.29 = (bf16[320,1024]{1,0:T(8,128)(2,1)S(1)}, bf16[320,1024]{1,0:T(8,128)(2,1)S(1)}, u32[]{:S(2)}, u32[]{:S(2)}) collective-permute-start(bf16[320,1024]{1,0:T(8,128)(2,1)S(1)} %copy-done.15), channel_id=1, source_target_pairs={{0,2},{1,3},{2,0},{3,1},{4,6},{5,7},{6,4},{7,5},{8,10},{9,11},{10,... | collective-permute-start | bytes 1966088 | tf_op jit(solution)/shard_map/ppermute | solution.py:1007
  389.9 21.1 %collective-permute-start.34 = (bf16[2,320,1024]{2,1,0:T(8,128)(2,1)}, bf16[2,320,1024]{2,1,0:T(8,128)(2,1)}, u32[]{:S(2)}, u32[]{:S(2)}) collective-permute-start(bf16[2,320,1024]{2,1,0:T(8,128)(2,1)} %pair_up.3.own), channel_id=1, source_target_pairs={{0,8},{1,9},{2,10},{3,11},{4,12},{5,13},{6,14},{7,15},{8,0},{9,1},... | collective-permute-start | bytes 3932168 | tf_op jit(solution)/shard_map/ppermute | solution.py:1007
  389.9 49.7 %collective-permute-start.30 = (bf16[2,320,1024]{2,1,0:T(8,128)(2,1)}, bf16[2,320,1024]{2,1,0:T(8,128)(2,1)S(1)}, u32[]{:S(2)}, u32[]{:S(2)}) collective-permute-start(bf16[2,320,1024]{2,1,0:T(8,128)(2,1)} %pair_up.3.own), channel_id=1, source_target_pairs={{0,16},{1,17},{2,18},{3,19},{4,20},{5,21},{6,22},{7,23},{8,24},{9,... | collective-permute-start | bytes 3932168 | tf_op jit(solution)/shard_map/ppermute | solution.py:1007
  (42 other events, 420.2 us)

commit v10 on v9

--- a/solution.py
+++ b/solution.py
@@ -43,7 +43,10 @@
     skip = (ks > qs + bq - 1) | ((kf > 0) & (kl < qf))
     same = (qf == ql) & (kl == ql) & ((kf == kl) | ((kf == 0) & (kl == 1)))
     full = below & ((kl == 0) | same)
-    return jnp.where(skip, 0, jnp.where(full, 1, 2)).astype(jnp.int32).reshape(-1)
+    flags = jnp.where(skip, 0, jnp.where(full, 1, 2))
+    if bq == bk:
+        flags = jnp.where(qs == ks, 3, flags)
+    return flags.astype(jnp.int32).reshape(-1)
 
 
 def put_split(base, col, lanes):
@@ -62,24 +65,25 @@
     acc_s[...] = jnp.zeros_like(acc_s)
     m_s[...] = jnp.zeros_like(m_s)
 
-    def mask(ko):
-        qpos = qi * bq + lax.broadcasted_iota(jnp.int32, (bq, bk), 0)
-        kpos = ko + lax.broadcasted_iota(jnp.int32, (bq, bk), 1)
-        ks = segr[:, pl.ds(ko, bk)]
-        return (kpos <= qpos) & ((ks == 0) | (ks == segc[...]))
-
-    def step(kb, masked):
+    def mask(ko, q0=0, qn=bq, kn=bk):
+        qpos = qi * bq + q0 + lax.broadcasted_iota(jnp.int32, (qn, kn), 0)
+        kpos = ko + lax.broadcasted_iota(jnp.int32, (qn, kn), 1)
+        ks = segr[:, pl.ds(ko, kn)]
+        return (kpos <= qpos) & ((ks == 0) | (ks == segc[q0 : q0 + qn, :]))
+
+    def step(kb, masked, q0=0, qn=bq, kn=bk):
         ko = pl.multiple_of(kb * bk, bk)
         if masked:
-            allowed = mask(ko)
+            allowed = mask(ko, q0, qn, kn)
+        rows = slice(q0, q0 + qn)
         for h in range(nh):
-            k = kv[pl.ds(ko, bk), h * LN : (h + 1) * LN]
-            v = kv[pl.ds(ko, bk), (nh + h) * LN : (nh + h + 1) * LN]
-            s = lax.dot_general(q_ref[:, h * LN : (h + 1) * LN], k, nt, preferred_element_type=f32)
-            p = jnp.exp2(s)
+            k = kv[pl.ds(ko, kn), h * LN : (h + 1) * LN]
+            v = kv[pl.ds(ko, kn), (nh + h) * LN : (nh + h + 1) * LN]
+            q = q_ref[rows, h * LN : (h + 1) * LN]
+            p = jnp.exp2(lax.dot_general(q, k, nt, preferred_element_type=f32))
             if masked:
                 p = jnp.where(allowed, p, 0.0)
-            acc_s[h] += jnp.dot(p.astype(bf16), v, preferred_element_type=f32)
+            acc_s[h, rows, :] += jnp.dot(p.astype(bf16), v, preferred_element_type=f32)
 
     def body(kb, carry):
         flag = flags[qi * nk + kb]
@@ -91,6 +95,13 @@
         @pl.when(flag == 2)
         def _():
             step(kb, True)
+
+        if bq == bk:
+
+            @pl.when(flag == 3)
+            def _():
+                step(kb, True, 0, bq // 2, bk // 2)
+                step(kb, True, bq // 2, bq // 2, bk)
 
         return carry
 
@@ -212,25 +223,26 @@
     nt = (((1,), (1,)), ((), ()))
     tn = (((0,), (0,)), ((), ()))
 
-    def step(qi, masked):
-        qo = pl.multiple_of(qi * bq, bq)
+    def step(qi, masked, q0=0, qn=bq, kn=bk):
+        qo = pl.multiple_of(qi * bq + q0, qn)
+        rows = slice(0, kn)
         if masked:
-            kpos = ko + lax.broadcasted_iota(jnp.int32, (bk, bq), 0)
-            qpos = qo + lax.broadcasted_iota(jnp.int32, (bk, bq), 1)
-            ks = segc[...]
-            allowed = (kpos <= qpos) & ((ks == 0) | (ks == segr[:, pl.ds(qo, bq)]))
+            kpos = ko + lax.broadcasted_iota(jnp.int32, (kn, qn), 0)
+            qpos = qo + lax.broadcasted_iota(jnp.int32, (kn, qn), 1)
+            ks = segc[rows, :]
+            allowed = (kpos <= qpos) & ((ks == 0) | (ks == segr[:, pl.ds(qo, qn)]))
         for h in range(nh):
             c = slice(h * LN, (h + 1) * LN)
-            q = qa[pl.ds(qo, bq), c]
-            k = kk[:, c]
-            d = doa_s[pl.ds(qo, bq), c]
+            q = qa[pl.ds(qo, qn), c]
+            k = kk[rows, c]
+            d = doa_s[pl.ds(qo, qn), c]
             p = jnp.exp2(lax.dot_general(k, q, nt, preferred_element_type=f32))
             if masked:
                 p = jnp.where(allowed, p, 0.0)
-            ds = (p * lax.dot_general(vv[:, c], d, nt, preferred_element_type=f32)).astype(bf16)
-            dv_s[h] += jnp.dot(p.astype(bf16), d, preferred_element_type=f32)
-            dk_s[h] += jnp.dot(ds, q, preferred_element_type=f32)
-            dq_s[h, pl.ds(qo, bq), :] += lax.dot_general(ds, k, tn, preferred_element_type=f32)
+            ds = (p * lax.dot_general(vv[rows, c], d, nt, preferred_element_type=f32)).astype(bf16)
+            dv_s[h, rows, :] += jnp.dot(p.astype(bf16), d, preferred_element_type=f32)
+            dk_s[h, rows, :] += jnp.dot(ds, q, preferred_element_type=f32)
+            dq_s[h, pl.ds(qo, qn), :] += lax.dot_general(ds, k, tn, preferred_element_type=f32)
 
     def body(qi, carry):
         flag = flags[qi * nk + kb]
@@ -242,6 +254,13 @@
         @pl.when(flag == 2)
         def _():
             step(qi, True)
+
+        if bq == bk:
+
+            @pl.when(flag == 3)
+            def _():
+                step(qi, True, 0, bq // 2, bk // 2)
+                step(qi, True, bq // 2, bq // 2, bk)
 
         return carry
 
@@ -532,7 +551,7 @@
     )(info, *args)
 
 
-def tail_body(at, p0, p1, p2, p3, x_ref, g_ref, w_s, gain, outs):
+def tail_body(at, p0, p1, p2, p3, x_ref, g_ref, w_s, gain, outs, need):
     lo_ref, left_ref, right_ref, gr_ref, c0, c1, c2, c3, gg_ref = outs
     att_ref, nm_ref, act_ref = (left_ref.at[i] for i in range(3))
     gp_ref, gh_ref = (right_ref.at[i] for i in range(2))
@@ -547,14 +566,17 @@
         def _(i=i):
             att_ref[...] = jnp.concatenate([pieces[i ^ k][...] for k in range(4)], axis=1)
 
+    need(0)
     resid = x_ref[...].astype(f32) + jnp.dot(att_ref[...], w_s[0], preferred_element_type=f32)
     inverse = lax.rsqrt(jnp.mean(resid * resid, axis=-1, keepdims=True) + epsilon)
     normed = (resid * inverse * gain[...]).astype(bf16)
     nm_ref[...] = normed
+    need(1)
     hidden = jnp.dot(normed, w_s[1], preferred_element_type=f32)
     sig = 1.0 / (1.0 + jnp.exp(-hidden))
     active = (hidden * sig).astype(bf16)
     act_ref[...] = active
+    need(2)
     lo_ref[...] = (resid + jnp.dot(active, w_s[2], preferred_element_type=f32)).astype(bf16)
     grad_active = lax.dot_general(g_ref[...], w_s[2], nt, preferred_element_type=f32)
     grad_hidden = (grad_active * sig * (1.0 + hidden * (1.0 - sig))).astype(bf16)
@@ -579,18 +601,33 @@
                 out[...] = grad_att[:, (i ^ j) * cols : ((i ^ j) + 1) * cols]
 
 
-def tail_kernel(at, p0, p1, p2, p3, x_ref, g_ref, own, half, other, gain, *refs, rows, hrows):
-    w_s = refs[-1]
-    outs = refs[:-1]
+def tail_kernel(at, p0, p1, p2, p3, x_ref, g_ref, own0, own1, own2, half, other, gain, *refs, rows, hrows):
+    w_s, sems = refs[-2:]
+    outs = refs[:-2]
+
+    def copies(i):
+        parts = (((own0, own1, own2)[i], at[1], rows), (half.at[i], at[2], hrows), (other.at[i], at[3], hrows))
+        return [
+            pltpu.make_async_copy(
+                part, w_s.at[i, pl.ds(pl.multiple_of(start, 16), n), :], sems.at[3 * i + k]
+            )
+            for k, (part, start, n) in enumerate(parts)
+        ]
 
     @pl.when(pl.program_id(0) == 0)
     def _():
         outs[-1][...] = jnp.zeros_like(outs[-1])
-        w_s[:, pl.ds(pl.multiple_of(at[1], 16), rows), :] = own[...]
-        w_s[:, pl.ds(pl.multiple_of(at[2], 16), hrows), :] = half[...]
-        w_s[:, pl.ds(pl.multiple_of(at[3], 16), hrows), :] = other[...]
-
-    tail_body(at, p0, p1, p2, p3, x_ref, g_ref, w_s, gain, outs)
+        for i in range(3):
+            for c in copies(i):
+                c.start()
+
+    def need(i):
+        @pl.when(pl.program_id(0) == 0)
+        def _():
+            for c in copies(i):
+                c.wait()
+
+    tail_body(at, p0, p1, p2, p3, x_ref, g_ref, w_s, gain, outs, need)
 
 
 def whole_tail_kernel(at, p0, p1, p2, p3, x_ref, g_ref, w, gain, *outs):
@@ -598,7 +635,7 @@
     def _():
         outs[-1][...] = jnp.zeros_like(outs[-1])
 
-    tail_body(at, p0, p1, p2, p3, x_ref, g_ref, w, gain, outs)
+    tail_body(at, p0, p1, p2, p3, x_ref, g_ref, w, gain, outs, lambda i: None)
 
 
 def tail(at, pieces, x, g, weights, gain, tile=256):
@@ -609,12 +646,14 @@
     whole = lambda *shape: pl.BlockSpec(shape, lambda i, m: (0,) * len(shape), pipeline_mode=once)
     wide = pl.BlockSpec((tile, d), row)
     slim = pl.BlockSpec((tile, cols), row)
-    if len(weights) == 3:
-        body = functools.partial(tail_kernel, rows=weights[0].shape[1], hrows=weights[1].shape[1])
-        scratch = [pltpu.VMEM((3, d, d), bf16)]
+    if len(weights) == 5:
+        body = functools.partial(tail_kernel, rows=weights[0].shape[0], hrows=weights[3].shape[1])
+        scratch = [pltpu.VMEM((3, d, d), bf16), pltpu.SemaphoreType.DMA((9,))]
+        weight_specs = [pl.BlockSpec(memory_space=pl.ANY)] * 5
     else:
         body = whole_tail_kernel
         scratch = []
+        weight_specs = [whole(*w.shape) for w in weights]
     return pl.pallas_call(
         body,
         out_shape=[pltpu.HBM((rows, d), bf16)]
@@ -625,7 +664,7 @@
         grid_spec=pltpu.PrefetchScalarGridSpec(
             num_scalar_prefetch=1,
             grid=(rows // tile,),
-            in_specs=[slim] * 4 + [wide] * 2 + [whole(*w.shape) for w in weights] + [whole(1, d)],
+            in_specs=[slim] * 4 + [wide] * 2 + weight_specs + [whole(1, d)],
             out_specs=[wide]
             + [pl.BlockSpec((3, tile, d), lambda i, m: (0, i, 0))] * 2
             + [wide]
@@ -787,45 +826,38 @@
 
 
 def cross_kernel(at, x_ref, g_ref, *refs):
-    acc = refs[-1]
-    w, k = pl.program_id(0), pl.program_id(1)
-    value = jnp.dot(x_ref[...], g_ref[...], preferred_element_type=f32)
-
-    @pl.when(k == 0)
-    def _():
-        acc[...] = value
-
-    @pl.when(k > 0)
-    def _():
-        acc[...] += value
-
-    half = acc.shape[0] // 2
-    for i in range(2):
-
-        @pl.when((w == i) & (k == pl.num_programs(1) - 1))
-        def _(i=i):
+    s = refs[-1]
+    s[...] = jnp.dot(x_ref[...], g_ref[...], preferred_element_type=f32)
+    half = s.shape[0] // 2
+    for w in range(2):
+
+        @pl.when(pl.program_id(0) == w)
+        def _(w=w):
             for x in range(2):
                 rows = pl.ds(pl.multiple_of((at[1] ^ x) * half, 16), half)
-                refs[2 * i + x][...] = acc[rows, :].astype(bf16)
+                refs[2 * w + x][...] = s[rows, :].astype(bf16)
 
 
 def cross(x, g, at):
     d, rows = x.shape
     w = d // 2
-    step = 512
-    block = pl.BlockSpec((w // 2, g.shape[1]), lambda i, k, m: (0, 0))
+    cols = g.shape[1]
+    step = 512 if cols % 512 == 0 else cols
+    n = cols // step
+    first = pl.BlockSpec((w // 2, step), lambda i, j, m: (0, jnp.where(i == 0, j, n - 1)))
+    second = pl.BlockSpec((w // 2, step), lambda i, j, m: (0, jnp.where(i == 1, j, 0)))
     return pl.pallas_call(
         cross_kernel,
-        out_shape=[pltpu.HBM((w // 2, g.shape[1]), bf16)] * 4,
+        out_shape=[pltpu.HBM((w // 2, cols), bf16)] * 4,
         grid_spec=pltpu.PrefetchScalarGridSpec(
             num_scalar_prefetch=1,
-            grid=(2, rows // step),
+            grid=(2, n),
             in_specs=[
-                pl.BlockSpec((w, step), lambda i, k, m: (m[0] ^ i, k)),
-                pl.BlockSpec((step, g.shape[1]), lambda i, k, m: (k, 0)),
+                pl.BlockSpec((w, rows), lambda i, j, m: (m[0] ^ i, 0)),
+                pl.BlockSpec((rows, step), lambda i, j, m: (0, j)),
             ],
-            out_specs=[block] * 4,
-            scratch_shapes=[pltpu.VMEM((w, g.shape[1]), f32)],
+            out_specs=[first, first, second, second],
+            scratch_shapes=[pltpu.VMEM((w, step), f32)],
         ),
         compiler_params=pltpu.CompilerParams(vmem_limit_bytes=40 << 20),
         cost_estimate=CHEAP,
@@ -886,22 +918,21 @@
 def back(grad, w, shards, rows, got=None):
     c, d = w.shape
     n = shards.shape[0]
+    step = 640 if d % 640 == 0 else d
+    out = pl.BlockSpec((1, rows, step), lambda j, i, f: (i, 0, j))
     in_specs = [
-        pl.BlockSpec((rows, c), lambda i, f: (f[i], 0)),
-        pl.BlockSpec((c, d), lambda i, f: (0, 0), pipeline_mode=pl.Buffered(1)),
+        pl.BlockSpec((rows, c), lambda j, i, f: (f[i], 0)),
+        pl.BlockSpec((c, step), lambda j, i, f: (0, j)),
     ]
     args = [hbm(grad), hbm(w)]
     if got is not None:
-        in_specs.append(pl.BlockSpec((1, rows, d), lambda i, f: (0, 0, 0)))
+        in_specs.append(pl.BlockSpec((1, rows, step), lambda j, i, f: (0, 0, j)))
         args.append(got)
     return pl.pallas_call(
         back_kernel,
         out_shape=pltpu.HBM((n, rows, d), bf16),
         grid_spec=pltpu.PrefetchScalarGridSpec(
-            num_scalar_prefetch=1,
-            grid=(n,),
-            in_specs=in_specs,
-            out_specs=pl.BlockSpec((1, rows, d), lambda i, f: (i, 0, 0)),
+            num_scalar_prefetch=1, grid=(d // step, n), in_specs=in_specs, out_specs=out
         ),
         compiler_params=pltpu.CompilerParams(vmem_limit_bytes=40 << 20),
         cost_estimate=CHEAP,
@@ -1113,8 +1144,7 @@
         places = (z, z + way, z + 2 * way, last)
 
         half_rows = wrows // 2
-        tail_own = jnp.stack([w_proj, w_in, w_out])
-        half_w = lax.dynamic_slice_in_dim(tail_own, gc * half_rows, half_rows, 1)
+        half_w = jnp.stack([rows_at(w, gc * half_rows, half_rows) for w in (w_proj, w_in, w_out)])
         if pair:
             half_w = send(after(half_w, other_w), wt_mate)
         else:
@@ -1147,7 +1177,7 @@
             w_trans = flat_all.T
         normed_trans = transpose(after(all_normed, w_trans))
         if pair:
-            weights = (tail_own, half_w, half_mate)
+            weights = (w_proj, w_in, w_out, half_w, half_mate)
             starts = (wt * wrows, (1 - wt) * wrows + gc * half_rows, (1 - wt) * wrows + (1 - gc) * half_rows)
         else:
             one = gc == 0
@@ -1256,7 +1286,7 @@
         t4 = done(pair_up(turn(t2), t2_near))
         t4_x = send(t4, x_mate)
         t4_core = send(t4, core_mate)
-        grad_tokens = done(turn(home_grad))
+        grad_tokens = done(copy(turn(home_grad)))
         q4 = done(pair_up(turn(q2), q2_near))
         q4_x = send(q4, x_mate)
         q4_core = send(q4, core_mate)
@@ -1264,12 +1294,14 @@
         t4_cross = send(t4_x, core_mate)
         used = 3 * nh * HD
         spread_at = jnp.stack([gx, near, 1 - gc])
+        t4_core = done(after(turn(t4_core), t4_cross))
+        q4_core = done(turn(q4_core))
+        small = done(sum_all(turn(small))).reshape(-1)
+        q4_x = done(turn(q4_x))
+        q4_cross = send(q4_x, core_mate)
         totals = place_tail((turn(t4), t4_x, t4_core, t4_cross), jnp.stack([gx, near, gc]))
         done(totals[0])
         total_qkv = done(spread(turn(q4), q4_core, spread_at, used, 0))
-        small = done(sum_all(turn(small))).reshape(-1)
-        q4_x = done(turn(q4_x))
-        q4_cross = send(q4_x, core_mate)
         total_qkv = spread(turn(q4_x), q4_cross, spread_at, used, 1, total_qkv).reshape(wrows, 3 * D)
         return (
             layer_out[None],

time: 456 us -> 459 us (level)
  waiting for transfers between devices: 151 us -> 159 us
    ppermute x41, waiting for transfers between devices: 151 us -> 159 us  [send(): return lax.ppermute(value, AXES, pairs(target))]
  transfers between devices with their start and end apart: 42 -> 42, of which waited for: 20 -> 19; matrix products, arithmetic and copies ran while one was open for 3% -> 2% of each run, Pallas kernels for 44% -> 44%
where the time goes in v10:
time: 459 us; the launch traced here: 452 us
  Pallas kernels  224 us (49%)
  waiting for transfers between devices  159 us (35%)
  starting transfers between devices  48.6 us (11%)
  local copies, waits for them, and re-layouts  12.7 us (3%)
  other arithmetic  5.95 us (1%)
    ppermute x41, waiting for transfers between devices, send(): return lax.ppermute(value, AXES, pairs(target))  159 us
    pallas_call x1, Pallas kernels, attn_bwd(): pl.pallas_call(functools.partial(bwd_kernel, first=group * nh, nh=nh, bq=...  43.6 us
    ppermute x41, starting transfers between devices, send(): return lax.ppermute(value, AXES, pairs(target))  42.2 us
    pallas_call x1, Pallas kernels, attn_fwd(): pl.pallas_call(functools.partial(fwd_kernel, nh=nh, bq=bq, bk=bk, nk=n //...  26.4 us
    pallas_call x2, Pallas kernels, project(): pl.pallas_call(functools.partial(project_kernel, count=count, halves=len(...  23.2 us
    pallas_call x1, Pallas kernels, tail(): pl.pallas_call(body, out_shape=[pltpu.HBM((rows, d), bf16)] + [pltpu.HBM(...  21.3 us
    pallas_call x2, Pallas kernels, share(): pl.pallas_call(share_kernel, out_shape=pltpu.HBM((d, n * w), bf16), grid_...  16.2 us
    pallas_call x2, Pallas kernels, back(): pl.pallas_call(back_kernel, out_shape=pltpu.HBM((n, rows, d), bf16), grid...  12.4 us
  transfers between devices with their start and end apart: 42, of which 19 were waited for; matrix products, arithmetic and copies ran while one was open for 2% of the time, Pallas kernels for 44%

profile of v10, /device:TPU:0, one launch (start us, length us, event | category | flops | bytes accessed | tf_op | source)
XLA Modules:
  0.0 451.5 jit_solution(10496185264777852833)
XLA Ops:
  1.9 7.3 %collective-permute-start.5 = (bf16[512,1280]{1,0:T(8,128)(2,1)}, bf16[512,1280]{1,0:T(8,128)(2,1)}, u32[]{:S(2)}, u32[]{:S(2)}) collective-permute-start(bf16[512,1280]{1,0:T(8,128)(2,1)} %bitcast.68), channel_id=1, source_target_pairs={{0,8},{1,9},{2,10},{3,11},{12,4},{13,5},{14,6},{15,7},{16,24},{17,... | collective-permute-start | bytes 3932168 | tf_op jit(solution)/shard_map/ppermute | solution.py:1038
  9.2 4.4 pick.1.x_ref.a_ref
  15.7 4.2 stretch.2.refs_5_
  30.4 14.6 %collective-permute-done.7.x_ref.b_ref = bf16[640,1024]{1,0:T(8,128)(2,1)} collective-permute-done((bf16[640,1024]{1,0:T(8,128)(2,1)}, bf16[640,1024]{1,0:T(8,128)(2,1)}, u32[]{:S(2)}, u32[]{:S(2)}) %collective-permute-start.7) | collective-permute-done | bytes 1310752 | tf_op jit(solution)/shard_map/ppermute | solution.py:1038
  45.1 4.1 stretch.3.refs_6_
  54.1 11.2 %project.2 = (bf16[2048,1280]{1,0:T(8,128)(2,1)}, bf16[2048,512]{1,0:T(8,128)(2,1)}, bf16[2048,1024]{1,0:T(8,128)(2,1)}, bf16[512,1280]{1,0:T(8,128)(2,1)}) custom-call(s32[5]{0:T(128)S(1)} %stack.101.info, bf16[512,1280]{1,0:T(8,128)(2,1)S(1)} %bitcast.69, bf16[512,1280]{1,0:T(8,128)(2,1)} %collective-permute-done.5.refs_1_, ...), custom_call_target="tpu_custom_call" | custom-call | flops 15000000512 | bytes 1000 | tf_op jit(solution)/shard_map/project/pallas_call | solution.py:525
  75.2 12.0 %project.3 = (bf16[2048,1280]{1,0:T(8,128)(2,1)}, bf16[2048,512]{1,0:T(8,128)(2,1)}, bf16[2048,1024]{1,0:T(8,128)(2,1)}, bf16[512,1280]{1,0:T(8,128)(2,1)}) custom-call(s32[5]{0:T(128)S(1)} %stack.98.info, bf16[512,1280]{1,0:T(8,128)(2,1)S(1)} %collective-permute-done.2.refs_0_, ...), custom_call_target="tpu_custom_call", output_to_operand_aliasing={{0}: (11, {}), {1}: (12, {}), {2}: (13, {})} | custom-call | flops 15000000512 | bytes 1000 | tf_op jit(solution)/shard_map/project/pallas_call | solution.py:525
  87.2 26.4 %attn_fwd.1 = (bf16[2048,320]{1,0:T(8,128)(2,1)}, bf16[2048,512]{1,0:T(8,128)(2,1)}, bf16[2048,512]{1,0:T(8,128)(2,1)}) custom-call(s32[16]{0:T(128)S(1)} %reshape.183.flags, bf16[2048,512]{1,0:T(8,128)(2,1)} %get-tuple-element.84.q_ref, bf16[2048,1024]{1,0:T(8,128)(2,1)} %get-tuple-element.85.kv.kk.vv, s32[2048,1]{1,0:T(8,128)S(1)} %copy.29.segc, ...), custom_call_target="tpu_custom_call" | custom-call | flops 10000000 | bytes 1000 | tf_op jit(solution)/shard_map/attn_fwd/pallas_call | solution.py:179
  113.6 6.8 %collective-permute-done.9.half = bf16[3,320,1280]{2,1,0:T(8,128)(2,1)} collective-permute-done((bf16[3,320,1280]{2,1,0:T(8,128)(2,1)}, bf16[3,320,1280]{2,1,0:T(8,128)(2,1)}, u32[]{:S(2)}, u32[]{:S(2)}) %collective-permute-start.9) | collective-permute-done | bytes 2457632 | tf_op jit(solution)/shard_map/ppermute | solution.py:1038
  126.0 6.6 %order.1.w_ref = bf16[1024,1280]{1,0:T(8,128)(2,1)} custom-call(s32[1]{0:T(128)} %bitcast.10.own_first, bf16[640,1024]{1,0:T(8,128)(2,1)} %pick.1.x_ref.a_ref, bf16[640,1024]{1,0:T(8,128)(2,1)} %collective-permute-done.7.x_ref.b_ref), custom_call_target="tpu_custom_call" | custom-call | flops 199999995904 | bytes 1000 | tf_op jit(solution)/shard_map/order/pallas_call | solution.py:415
  132.6 7.9 %transpose.15.x_ref = bf16[1280,2048]{1,0:T(8,128)(2,1)} custom-call(bf16[2048,1280]{1,0:T(8,128)(2,1)} %get-tuple-element.93.x_ref), custom_call_target="tpu_custom_call" | custom-call | flops 1000000 | bytes 1000 | tf_op jit(solution)/shard_map/transpose/pallas_call | solution.py:439
  143.8 21.3 %tail.1 = (bf16[512,1280]{1,0:T(8,128)(2,1)}, bf16[3,512,1280]{2,1,0:T(8,128)(2,1)}, bf16[3,512,1280]{2,1,0:T(8,128)(2,1)}, f32[512,1280]{1,0:T(8,128)}, bf16[51...) custom-call(s32[4]{0:T(128)S(1)} %pad_add_fusion.at, ...), custom_call_target="tpu_custom_call" | custom-call | flops 10000000 | bytes 1000 | tf_op jit(solution)/shard_map/tail/pallas_call | solution.py:657
  167.2 7.3 %share.2 = bf16[1280,1920]{1,0:T(8,128)(2,1)} custom-call(s32[1]{0:T(128)} %bitcast.21.col, bf16[3,512,1280]{2,1,0:T(8,128)(2,1)} %get-tuple-element.100.left, bf16[3,512,1280]{2,1,0:T(8,128)(2,1)} %get-tuple-element.101.right), custom_call_target="tpu_custom_call" | custom-call | flops 1000000 | bytes 1000 | tf_op jit(solution)/shard_map/share/pallas_call | solution.py:695
  177.5 7.2 %collective-permute-done.17.do3 = bf16[512,320]{1,0:T(8,128)(2,1)S(1)} collective-permute-done((bf16[512,320]{1,0:T(8,128)(2,1)}, bf16[512,320]{1,0:T(8,128)(2,1)S(1)}, u32[]{:S(2)}, u32[]{:S(2)}) %collective-permute-start.17) | collective-permute-done | bytes 327712 | tf_op jit(solution)/shard_map/ppermute | solution.py:1038
  186.5 8.9 %share.3 = bf16[1280,1920]{1,0:T(8,128)(2,1)} custom-call(s32[1]{0:T(128)} %bitcast.22.col, bf16[3,512,1280]{2,1,0:T(8,128)(2,1)} %get-tuple-element.100.left, bf16[3,512,1280]{2,1,0:T(8,128)(2,1)} %get-tuple-element.101.right, bf16[1280,1920]{1,0:T(8,128)(2,1)} %collective-permute-done.19.refs_0_), custom_call_target="tpu_custom_call" | custom-call | flops 1000000 | bytes 1000 | tf_op jit(solution)/shard_map/share/pallas_call | solution.py:695
  195.4 6.4 %all-to-all-start = ((bf16[8,160,1920]{2,1,0:T(8,128)(2,1)}), bf16[8,160,1920]{2,1,0:T(8,128)(2,1)}, u32[]{:S(2)}, u32[]{:S(2)}) async-start(bf16[8,160,1920]{2,1,0:T(8,128)(2,1)} %bitcast.78), calls=%async_computation | async-start | bytes 9830400 | tf_op jit(solution)/shard_map/all_to_all | solution.py:1207
  201.9 43.6 %attn_bwd.1 = (bf16[2048,1024]{1,0:T(8,128)(2,1)}, f32[8,128]{1,0:T(8,128)}) custom-call(s32[16]{0:T(128)S(1)} %copy-done.7, s32[1]{0:T(128)} %bitcast.mine.shard, bf16[2048,512]{1,0:T(8,128)(2,1)} %get-tuple-element.106.qa, bf16[2048,1024]{1,0:T(8,128)(2,1)} %get-tuple-element.85.kv.kk.vv, bf16[2048,1024]{1,0:T(8,128)(2,1)} %get-tuple-element.85.kv.kk.vv, ...), custom_call_target="tpu_custom_call" | custom-call | flops 299999985664 | bytes 1000 | tf_op jit(solution)/shard_map/attn_bwd/pallas_call | solution.py:321
  245.5 7.9 %back.2 = bf16[2,512,1280]{2,1,0:T(8,128)(2,1)} custom-call(s32[2]{0:T(128)S(1)} %pad_add_fusion.1.shards, bf16[2048,1024]{1,0:T(8,128)(2,1)} %get-tuple-element.115.g_ref, bf16[1024,1280]{1,0:T(8,128)(2,1)} %order.1.w_ref), custom_call_target="tpu_custom_call" | custom-call | flops 1000000 | bytes 1000 | tf_op jit(solution)/shard_map/back/pallas_call | solution.py:931
  253.5 11.6 %cross.1 = (bf16[320,1024]{1,0:T(8,128)(2,1)}, bf16[320,1024]{1,0:T(8,128)(2,1)}, bf16[320,1024]{1,0:T(8,128)(2,1)}, bf16[320,1024]{1,0:T(8,128)(2,1)}) custom-call(s32[2]{0:T(128)S(1)} %pad_add_fusion.2.at, bf16[1280,2048]{1,0:T(8,128)(2,1)} %transpose.15.x_ref, bf16[2048,1024]{1,0:T(8,128)(2,1)} %get-tuple-element.115.g_ref), custom_call_target="tpu_custom_call" | custom-call | flops 1000000 | bytes 1000 | tf_op jit(solution)/shard_map/cross/pallas_call | solution.py:849
  265.0 4.5 back.3
  281.6 7.8 %collective-permute-done.22 = bf16[320,1024]{1,0:T(8,128)(2,1)} collective-permute-done((bf16[320,1024]{1,0:T(8,128)(2,1)}, bf16[320,1024]{1,0:T(8,128)(2,1)}, u32[]{:S(2)}, u32[]{:S(2)}) %collective-permute-start.22) | collective-permute-done | bytes 655392 | tf_op jit(solution)/shard_map/ppermute | solution.py:1038
  289.4 14.5 %collective-permute-done.23 = bf16[320,1024]{1,0:T(8,128)(2,1)} collective-permute-done((bf16[320,1024]{1,0:T(8,128)(2,1)}, bf16[320,1024]{1,0:T(8,128)(2,1)}, u32[]{:S(2)}, u32[]{:S(2)}) %collective-permute-start.23) | collective-permute-done | bytes 655392 | tf_op jit(solution)/shard_map/ppermute | solution.py:1038
  307.0 7.5 %collective-permute-done.21.near = bf16[1,512,1280]{2,1,0:T(8,128)(2,1)} collective-permute-done((bf16[1,512,1280]{2,1,0:T(8,128)(2,1)}, bf16[1,512,1280]{2,1,0:T(8,128)(2,1)}, u32[]{:S(2)}, u32[]{:S(2)}) %collective-permute-start.21) | collective-permute-done | bytes 1310752 | tf_op jit(solution)/shard_map/ppermute | solution.py:1038
  314.5 6.6 %finish.1 = (bf16[512,1280]{1,0:T(8,128)(2,1)}, f32[1,1280]{1,0:T(1,128)S(1)}) custom-call(s32[1]{0:T(128)} %bitcast.mine.shard, bf16[2048,1024]{1,0:T(8,128)(2,1)} %get-tuple-element.115.g_ref, bf16[1024,1280]{1,0:T(8,128)(2,1)} %order.1.w_ref, bf16[2,512,1280]{2,1,0:T(8,128)(2,1)S(1)} %collective-permute-done.20.refs_0_.core, ...), custom_call_target="tpu_custom_call" | custom-call | flops 1000000 | bytes 1000 | tf_op jit(solution)/shard_map/finish/pallas_call | solution.py:969
  325.3 17.4 %collective-permute-done.27.b_ref = bf16[320,1024]{1,0:T(8,128)(2,1)S(1)} collective-permute-done((bf16[320,1024]{1,0:T(8,128)(2,1)}, bf16[320,1024]{1,0:T(8,128)(2,1)S(1)}, u32[]{:S(2)}, u32[]{:S(2)}) %collective-permute-start.27) | collective-permute-done | bytes 655392 | tf_op jit(solution)/shard_map/ppermute | solution.py:1038
  345.9 18.0 %collective-permute-done.28.b_ref = bf16[160,1920]{1,0:T(8,128)(2,1)S(1)} collective-permute-done((bf16[160,1920]{1,0:T(8,128)(2,1)}, bf16[160,1920]{1,0:T(8,128)(2,1)S(1)}, u32[]{:S(2)}, u32[]{:S(2)}) %collective-permute-start.28) | collective-permute-done | bytes 614432 | tf_op jit(solution)/shard_map/ppermute | solution.py:1038
  371.9 11.5 %collective-permute-done.29.b_ref = bf16[320,1024]{1,0:T(8,128)(2,1)S(1)} collective-permute-done((bf16[320,1024]{1,0:T(8,128)(2,1)S(1)}, bf16[320,1024]{1,0:T(8,128)(2,1)S(1)}, u32[]{:S(2)}, u32[]{:S(2)}) %collective-permute-start.29) | collective-permute-done | bytes 655392 | tf_op jit(solution)/shard_map/ppermute | solution.py:1038
  388.4 8.9 %collective-permute-done.33.own_x = bf16[2,160,1920]{2,1,0:T(8,128)(2,1)} collective-permute-done((bf16[2,160,1920]{2,1,0:T(8,128)(2,1)}, bf16[2,160,1920]{2,1,0:T(8,128)(2,1)}, u32[]{:S(2)}, u32[]{:S(2)}) %collective-permute-start.33) | collective-permute-done | bytes 1228832 | tf_op jit(solution)/shard_map/ppermute | solution.py:1038
  401.9 20.6 %collective-permute-done.35 = f32[21,128]{1,0:T(8,128)S(1)} collective-permute-done((f32[21,128]{1,0:T(8,128)S(1)}, f32[21,128]{1,0:T(8,128)S(1)}, u32[]{:S(2)}, u32[]{:S(2)}) %collective-permute-start.35) | collective-permute-done | bytes 10784 | tf_op jit(solution)/shard_map/ppermute | solution.py:1038
  423.7 4.6 %collective-permute-done.37 = f32[21,128]{1,0:T(8,128)S(1)} collective-permute-done((f32[21,128]{1,0:T(8,128)S(1)}, f32[21,128]{1,0:T(8,128)S(1)}, u32[]{:S(2)}, u32[]{:S(2)}) %collective-permute-start.37) | collective-permute-done | bytes 10784 | tf_op jit(solution)/shard_map/ppermute | solution.py:1038
  435.9 6.6 %place_tail.1 = (f32[4,160,1280]{2,1,0:T(8,128)}, f32[4,160,1280]{2,1,0:T(8,128)}, f32[4,160,1280]{2,1,0:T(8,128)}) custom-call(s32[3]{0:T(128)S(1)} %pad_add_fusion.5.at, bf16[2,160,1920]{2,1,0:T(8,128)(2,1)S(1)} %copy-done.1, bf16[2,160,1920]{2,1,0:T(8,128)(2,1)} %collective-permute-done.33.own_x, bf16[2,160,1920]{2,1,0:T(8,128)(2,1)} %collective-permute-done.32.mate, ...), custom_call_target="tpu_custom_call" | custom-call | flops 1000000 | bytes 1000 | tf_op jit(solution)/shard_map/place_tail/pallas_call | solution.py:812
  442.4 4.4 spread.2.refs_0_
  (194 shorter events, 97.5 us)
Async XLA Ops:
  0.6 22.2 %collective-permute-start.1 = (bf16[512,1280]{1,0:T(8,128)(2,1)}, bf16[512,1280]{1,0:T(8,128)(2,1)}, u32[]{:S(2)}, u32[]{:S(2)}) collective-permute-start(bf16[512,1280]{1,0:T(8,128)(2,1)} %bitcast.67), channel_id=1, source_target_pairs={{2,0},{3,1},{4,2},{5,3},{6,4},{7,5},{8,10},{9,11},{10,12},{11,13},... | collective-permute-start | bytes 3932168 | tf_op jit(solution)/shard_map/ppermute | solution.py:1038
  1.9 52.1 %collective-permute-start.5 = (bf16[512,1280]{1,0:T(8,128)(2,1)}, bf16[512,1280]{1,0:T(8,128)(2,1)}, u32[]{:S(2)}, u32[]{:S(2)}) collective-permute-start(bf16[512,1280]{1,0:T(8,128)(2,1)} %bitcast.68), channel_id=1, source_target_pairs={{0,8},{1,9},{2,10},{3,11},{12,4},{13,5},{14,6},{15,7},{16,24},{17,... | collective-permute-start | bytes 3932168 | tf_op jit(solution)/shard_map/ppermute | solution.py:1038
  9.2 63.8 %collective-permute-start = (s32[1,2048]{1,0:T(1,128)}, s32[1,2048]{1,0:T(1,128)S(1)}, u32[]{:S(2)}, u32[]{:S(2)}) collective-permute-start(s32[1,2048]{1,0:T(1,128)} %param.11), channel_id=1, source_target_pairs={{0,8},{1,9},{2,10},{3,11},{4,12},{5,13},{6,14},{7,15},{8,0},{9,1},... | collective-permute-start | bytes 24584 | tf_op jit(solution)/shard_map/ppermute | solution.py:1038
  13.6 31.5 %collective-permute-start.7 = (bf16[640,1024]{1,0:T(8,128)(2,1)}, bf16[640,1024]{1,0:T(8,128)(2,1)}, u32[]{:S(2)}, u32[]{:S(2)}) collective-permute-start(bf16[640,1024]{1,0:T(8,128)(2,1)} %pick.1.x_ref.a_ref), channel_id=1, source_target_pairs={{0,1},{1,0},{2,3},{3,2},{4,5},{5,4},{6,7},{7,6},{8,9},{9,8},{10,11... | collective-permute-start | bytes 3932168 | tf_op jit(solution)/shard_map/ppermute | solution.py:1038
  22.8 26.3 %collective-permute-start.2 = (bf16[512,1280]{1,0:T(8,128)(2,1)}, bf16[512,1280]{1,0:T(8,128)(2,1)S(1)}, u32[]{:S(2)}, u32[]{:S(2)}) collective-permute-start(bf16[512,1280]{1,0:T(8,128)(2,1)} %collective-permute-done.1.refs_2_), channel_id=1, source_target_pairs={{2,0},{3,1},{4,2},{5,3},{10,12},{11,13},{12,14},{13,15},{18,16},{1... | collective-permute-start | bytes 3932168 | tf_op jit(solution)/shard_map/ppermute | solution.py:1038
  27.7 26.4 %collective-permute-start.6 = (bf16[512,1280]{1,0:T(8,128)(2,1)}, bf16[512,1280]{1,0:T(8,128)(2,1)}, u32[]{:S(2)}, u32[]{:S(2)}) collective-permute-start(bf16[512,1280]{1,0:T(8,128)(2,1)} %collective-permute-done.1.refs_2_), channel_id=1, source_target_pairs={{0,8},{1,9},{2,10},{3,11},{12,4},{13,5},{14,6},{15,7},{16,24},{17,... | collective-permute-start | bytes 3932168 | tf_op jit(solution)/shard_map/ppermute | solution.py:1038
  49.3 19.6 %collective-permute-start.4 = (bf16[512,1280]{1,0:T(8,128)(2,1)S(1)}, bf16[512,1280]{1,0:T(8,128)(2,1)}, u32[]{:S(2)}, u32[]{:S(2)}) collective-permute-start(bf16[512,1280]{1,0:T(8,128)(2,1)S(1)} %broadcast_select_fusion), channel_id=1, source_target_pairs={{0,2},{1,3},{2,0},{3,1},{12,14},{13,15},{14,12},{15,13},{16,18},{1... | collective-permute-start | bytes 3932168 | tf_op jit(solution)/shard_map/ppermute | solution.py:1038
  51.7 23.5 %collective-permute-start.3 = (bf16[512,1280]{1,0:T(8,128)(2,1)S(1)}, bf16[512,1280]{1,0:T(8,128)(2,1)}, u32[]{:S(2)}, u32[]{:S(2)}) collective-permute-start(bf16[512,1280]{1,0:T(8,128)(2,1)S(1)} %collective-permute-done.2.refs_0_), channel_id=1, source_target_pairs={{0,8},{1,9},{2,10},{3,11},{12,4},{13,5},{14,6},{15,7},{16,24},{17,... | collective-permute-start | bytes 3932168 | tf_op jit(solution)/shard_map/ppermute | solution.py:1038
  71.5 48.9 %collective-permute-start.9 = (bf16[3,320,1280]{2,1,0:T(8,128)(2,1)}, bf16[3,320,1280]{2,1,0:T(8,128)(2,1)}, u32[]{:S(2)}, u32[]{:S(2)}) collective-permute-start(bf16[3,320,1280]{2,1,0:T(8,128)(2,1)} %pad_maximum_fusion), channel_id=1, source_target_pairs={{0,1},{1,0},{2,3},{3,2},{4,5},{5,4},{6,7},{7,6},{8,9},{9,8},{10,11... | collective-permute-start | bytes 7372808 | tf_op jit(solution)/shard_map/ppermute | solution.py:1038
  75.1 45.3 %collective-permute-start.10 = (bf16[512,1280]{1,0:T(8,128)(2,1)}, bf16[512,1280]{1,0:T(8,128)(2,1)S(1)}, u32[]{:S(2)}, u32[]{:S(2)}) collective-permute-start(bf16[512,1280]{1,0:T(8,128)(2,1)} %bitcast.89), channel_id=1, source_target_pairs={{0,8},{1,9},{2,0},{3,1},{4,10},{5,11},{6,2},{7,3},{8,12},{9,13},{1... | collective-permute-start | bytes 3932168 | tf_op jit(solution)/shard_map/ppermute | solution.py:1038
  123.9 16.6 %collective-permute-start.11 = (bf16[512,320]{1,0:T(8,128)(2,1)}, bf16[512,320]{1,0:T(8,128)(2,1)}, u32[]{:S(2)}, u32[]{:S(2)}) collective-permute-start(bf16[512,320]{1,0:T(8,128)(2,1)} %get-tuple-element.153), channel_id=1, source_target_pairs={{0,8},{1,9},{2,10},{3,11},{4,12},{5,13},{6,14},{7,15},{8,0},{9,1},... | collective-permute-start | bytes 983048 | tf_op jit(solution)/shard_map/ppermute | solution.py:1038
  123.9 16.6 %collective-permute-start.12 = (bf16[512,320]{1,0:T(8,128)(2,1)}, bf16[512,320]{1,0:T(8,128)(2,1)}, u32[]{:S(2)}, u32[]{:S(2)}) collective-permute-start(bf16[512,320]{1,0:T(8,128)(2,1)} %get-tuple-element.152), channel_id=1, source_target_pairs={{0,2},{1,3},{2,0},{3,1},{4,6},{5,7},{6,4},{7,5},{8,10},{9,11},{10,... | collective-permute-start | bytes 983048 | tf_op jit(solution)/shard_map/ppermute | solution.py:1038
  124.3 19.4 %collective-permute-start.13 = (bf16[512,320]{1,0:T(8,128)(2,1)}, bf16[512,320]{1,0:T(8,128)(2,1)}, u32[]{:S(2)}, u32[]{:S(2)}) collective-permute-start(bf16[512,320]{1,0:T(8,128)(2,1)} %get-tuple-element.151), channel_id=1, source_target_pairs={{0,10},{1,11},{2,8},{3,9},{4,14},{5,15},{6,12},{7,13},{8,2},{9,3},... | collective-permute-start | bytes 983048 | tf_op jit(solution)/shard_map/ppermute | solution.py:1038
  125.7 18.0 %collective-permute-start.14 = (bf16[3,320,1280]{2,1,0:T(8,128)(2,1)}, bf16[3,320,1280]{2,1,0:T(8,128)(2,1)}, u32[]{:S(2)}, u32[]{:S(2)}) collective-permute-start(bf16[3,320,1280]{2,1,0:T(8,128)(2,1)} %collective-permute-done.9.half), channel_id=1, source_target_pairs={{0,8},{1,9},{2,10},{3,11},{4,12},{5,13},{6,14},{7,15},{8,0},{9,1},... | collective-permute-start | bytes 7372808 | tf_op jit(solution)/shard_map/ppermute | solution.py:1038
  165.4 12.1 %collective-permute-start.16 = (bf16[512,320]{1,0:T(8,128)(2,1)}, bf16[512,320]{1,0:T(8,128)(2,1)S(1)}, u32[]{:S(2)}, u32[]{:S(2)}) collective-permute-start(bf16[512,320]{1,0:T(8,128)(2,1)} %get-tuple-element.98), channel_id=1, source_target_pairs={{0,2},{1,3},{2,0},{3,1},{4,6},{5,7},{6,4},{7,5},{8,10},{9,11},{10,... | collective-permute-start | bytes 983048 | tf_op jit(solution)/shard_map/ppermute | solution.py:1038
  165.8 18.9 %collective-permute-start.17 = (bf16[512,320]{1,0:T(8,128)(2,1)}, bf16[512,320]{1,0:T(8,128)(2,1)S(1)}, u32[]{:S(2)}, u32[]{:S(2)}) collective-permute-start(bf16[512,320]{1,0:T(8,128)(2,1)} %get-tuple-element.103), channel_id=1, source_target_pairs={{0,10},{1,11},{2,8},{3,9},{4,14},{5,15},{6,12},{7,13},{8,2},{9,3},... | collective-permute-start | bytes 983048 | tf_op jit(solution)/shard_map/ppermute | solution.py:1038
  184.7 60.8 %collective-permute-start.18 = (bf16[512,1280]{1,0:T(8,128)(2,1)}, bf16[512,1280]{1,0:T(8,128)(2,1)}, u32[]{:S(2)}, u32[]{:S(2)}) collective-permute-start(bf16[512,1280]{1,0:T(8,128)(2,1)} %get-tuple-element.105), channel_id=1, source_target_pairs={{0,2},{1,3},{2,6},{3,7},{4,10},{5,11},{6,14},{7,15},{8,0},{9,1},{1... | collective-permute-start | bytes 3932168 | tf_op jit(solution)/shard_map/ppermute | solution.py:1038
  195.4 79.6 %all-to-all-start = ((bf16[8,160,1920]{2,1,0:T(8,128)(2,1)}), bf16[8,160,1920]{2,1,0:T(8,128)(2,1)}, u32[]{:S(2)}, u32[]{:S(2)}) async-start(bf16[8,160,1920]{2,1,0:T(8,128)(2,1)} %bitcast.78), calls=%async_computation | async-start | bytes 9830400 | tf_op jit(solution)/shard_map/all_to_all | solution.py:1207
  269.5 45.0 %collective-permute-start.21 = (bf16[1,512,1280]{2,1,0:T(8,128)(2,1)}, bf16[1,512,1280]{2,1,0:T(8,128)(2,1)}, u32[]{:S(2)}, u32[]{:S(2)}) collective-permute-start(bf16[1,512,1280]{2,1,0:T(8,128)(2,1)} %back.3), channel_id=1, source_target_pairs={{0,2},{1,3},{2,0},{3,1},{4,6},{5,7},{6,4},{7,5},{8,10},{9,11},{10,... | collective-permute-start | bytes 3932168 | tf_op jit(solution)/shard_map/ppermute | solution.py:1038
  271.5 17.9 %collective-permute-start.22 = (bf16[320,1024]{1,0:T(8,128)(2,1)}, bf16[320,1024]{1,0:T(8,128)(2,1)}, u32[]{:S(2)}, u32[]{:S(2)}) collective-permute-start(bf16[320,1024]{1,0:T(8,128)(2,1)} %get-tuple-element.121), channel_id=1, source_target_pairs={{0,16},{1,17},{2,18},{3,19},{4,20},{5,21},{6,22},{7,23},{8,24},{9,... | collective-permute-start | bytes 1966088 | tf_op jit(solution)/shard_map/ppermute | solution.py:1038
  273.0 30.9 %collective-permute-start.23 = (bf16[320,1024]{1,0:T(8,128)(2,1)}, bf16[320,1024]{1,0:T(8,128)(2,1)}, u32[]{:S(2)}, u32[]{:S(2)}) collective-permute-start(bf16[320,1024]{1,0:T(8,128)(2,1)} %get-tuple-element.122), channel_id=1, source_target_pairs={{0,1},{1,0},{2,3},{3,2},{4,5},{5,4},{6,7},{7,6},{8,9},{9,8},{10,11... | collective-permute-start | bytes 1966088 | tf_op jit(solution)/shard_map/ppermute | solution.py:1038
  274.4 29.5 %collective-permute-start.24 = (bf16[320,1024]{1,0:T(8,128)(2,1)}, bf16[320,1024]{1,0:T(8,128)(2,1)}, u32[]{:S(2)}, u32[]{:S(2)}) collective-permute-start(bf16[320,1024]{1,0:T(8,128)(2,1)} %get-tuple-element.123), channel_id=1, source_target_pairs={{0,17},{1,16},{2,19},{3,18},{4,21},{5,20},{6,23},{7,22},{8,25},{9,... | collective-permute-start | bytes 1966088 | tf_op jit(solution)/shard_map/ppermute | solution.py:1038
  278.5 42.6 %collective-permute-start.26 = (bf16[160,1920]{1,0:T(8,128)(2,1)}, bf16[160,1920]{1,0:T(8,128)(2,1)}, u32[]{:S(2)}, u32[]{:S(2)}) collective-permute-start(bf16[160,1920]{1,0:T(8,128)(2,1)} %total.2.a_ref), channel_id=1, source_target_pairs={{0,4},{1,5},{2,6},{3,7},{4,0},{5,1},{6,2},{7,3},{8,12},{9,13},{10,... | collective-permute-start | bytes 1843208 | tf_op jit(solution)/shard_map/ppermute | solution.py:1038
  306.3 36.4 %collective-permute-start.27 = (bf16[320,1024]{1,0:T(8,128)(2,1)}, bf16[320,1024]{1,0:T(8,128)(2,1)S(1)}, u32[]{:S(2)}, u32[]{:S(2)}) collective-permute-start(bf16[320,1024]{1,0:T(8,128)(2,1)} %total.3.a_ref), channel_id=1, source_target_pairs={{0,4},{1,5},{2,6},{3,7},{4,0},{5,1},{6,2},{7,3},{8,12},{9,13},{10,... | collective-permute-start | bytes 1966088 | tf_op jit(solution)/shard_map/ppermute | solution.py:1038
  323.3 40.5 %collective-permute-start.28 = (bf16[160,1920]{1,0:T(8,128)(2,1)}, bf16[160,1920]{1,0:T(8,128)(2,1)S(1)}, u32[]{:S(2)}, u32[]{:S(2)}) collective-permute-start(bf16[160,1920]{1,0:T(8,128)(2,1)} %add.135.a_ref), channel_id=1, source_target_pairs={{0,2},{1,3},{2,0},{3,1},{4,6},{5,7},{6,4},{7,5},{8,10},{9,11},{10,... | collective-permute-start | bytes 1843208 | tf_op jit(solution)/shard_map/ppermute | solution.py:1038
  323.3 45.1 %collective-permute-start.25 = (bf16[512,1280]{1,0:T(8,128)(2,1)}, bf16[512,1280]{1,0:T(8,128)(2,1)S(1)}, u32[]{:S(2)}, u32[]{:S(2)}) collective-permute-start(bf16[512,1280]{1,0:T(8,128)(2,1)} %get-tuple-element.126), channel_id=1, source_target_pairs={{0,2},{1,3},{2,6},{3,7},{4,10},{5,11},{6,14},{7,15},{8,0},{9,1},{1... | collective-permute-start | bytes 3932168 | tf_op jit(solution)/shard_map/ppermute | solution.py:1038
  367.0 30.3 %collective-permute-start.33 = (bf16[2,160,1920]{2,1,0:T(8,128)(2,1)}, bf16[2,160,1920]{2,1,0:T(8,128)(2,1)}, u32[]{:S(2)}, u32[]{:S(2)}) collective-permute-start(bf16[2,160,1920]{2,1,0:T(8,128)(2,1)} %pair_up.2.own), channel_id=1, source_target_pairs={{0,16},{1,17},{2,18},{3,19},{4,20},{5,21},{6,22},{7,23},{8,24},{9,... | collective-permute-start | bytes 3686408 | tf_op jit(solution)/shard_map/ppermute | solution.py:1038
  368.4 15.1 %collective-permute-start.29 = (bf16[320,1024]{1,0:T(8,128)(2,1)S(1)}, bf16[320,1024]{1,0:T(8,128)(2,1)S(1)}, u32[]{:S(2)}, u32[]{:S(2)}) collective-permute-start(bf16[320,1024]{1,0:T(8,128)(2,1)S(1)} %copy-done.18), channel_id=1, source_target_pairs={{0,2},{1,3},{2,0},{3,1},{4,6},{5,7},{6,4},{7,5},{8,10},{9,11},{10,... | collective-permute-start | bytes 1966088 | tf_op jit(solution)/shard_map/ppermute | solution.py:1038
  386.7 13.8 %collective-permute-start.31 = (bf16[2,320,1024]{2,1,0:T(8,128)(2,1)}, bf16[2,320,1024]{2,1,0:T(8,128)(2,1)}, u32[]{:S(2)}, u32[]{:S(2)}) collective-permute-start(bf16[2,320,1024]{2,1,0:T(8,128)(2,1)} %pair_up.3.own), channel_id=1, source_target_pairs={{0,8},{1,9},{2,10},{3,11},{4,12},{5,13},{6,14},{7,15},{8,0},{9,1},... | collective-permute-start | bytes 3932168 | tf_op jit(solution)/shard_map/ppermute | solution.py:1038
  386.7 49.0 %collective-permute-start.30 = (bf16[2,320,1024]{2,1,0:T(8,128)(2,1)}, bf16[2,320,1024]{2,1,0:T(8,128)(2,1)S(1)}, u32[]{:S(2)}, u32[]{:S(2)}) collective-permute-start(bf16[2,320,1024]{2,1,0:T(8,128)(2,1)} %pair_up.3.own), channel_id=1, source_target_pairs={{0,16},{1,17},{2,18},{3,19},{4,20},{5,21},{6,22},{7,23},{8,24},{9,... | collective-permute-start | bytes 3932168 | tf_op jit(solution)/shard_map/ppermute | solution.py:1038
  400.6 22.0 %collective-permute-start.35 = (f32[21,128]{1,0:T(8,128)S(1)}, f32[21,128]{1,0:T(8,128)S(1)}, u32[]{:S(2)}, u32[]{:S(2)}) collective-permute-start(f32[21,128]{1,0:T(8,128)S(1)} %fusion), channel_id=1, source_target_pairs={{0,16},{1,17},{2,18},{3,19},{4,20},{5,21},{6,22},{7,23},{8,24},{9,... | collective-permute-start | bytes 32264 | tf_op jit(solution)/shard_map/ppermute | solution.py:1038
  435.7 12.3 %collective-permute-start.40 = (bf16[2,320,1024]{2,1,0:T(8,128)(2,1)S(1)}, bf16[2,320,1024]{2,1,0:T(8,128)(2,1)S(1)}, u32[]{:S(2)}, u32[]{:S(2)}) collective-permute-start(bf16[2,320,1024]{2,1,0:T(8,128)(2,1)S(1)} %collective-permute-done.30.own), channel_id=1, source_target_pairs={{0,8},{1,9},{2,10},{3,11},{4,12},{5,13},{6,14},{7,15},{8,0},{9,1},... | collective-permute-start | bytes 3932168 | tf_op jit(solution)/shard_map/ppermute | solution.py:1038
  (44 other events, 400.6 us)

commit v11 on v10

--- a/solution.py
+++ b/solution.py
@@ -92,16 +92,9 @@
         def _():
             step(kb, False)
 
-        @pl.when(flag == 2)
+        @pl.when(flag >= 2)
         def _():
             step(kb, True)
-
-        if bq == bk:
-
-            @pl.when(flag == 3)
-            def _():
-                step(kb, True, 0, bq // 2, bk // 2)
-                step(kb, True, bq // 2, bq // 2, bk)
 
         return carry
 
@@ -918,7 +911,7 @@
 def back(grad, w, shards, rows, got=None):
     c, d = w.shape
     n = shards.shape[0]
-    step = 640 if d % 640 == 0 else d
+    step = d
     out = pl.BlockSpec((1, rows, step), lambda j, i, f: (i, 0, j))
     in_specs = [
         pl.BlockSpec((rows, c), lambda j, i, f: (f[i], 0)),
@@ -1083,7 +1076,7 @@
         return (gx, 1 - gc, z, w) if gc == z >> 1 else None
 
     def sum_all(value):
-        for axis in AXES:
+        for axis in ("gc", "wt", "near", "far", "gx"):
             step = 1
             while step < sizes[axis]:
 
@@ -1269,7 +1262,6 @@
             late_gain.reshape(1, -1),
         )
         done(grad_tokens)
-        home_grad = send(grad_tokens, to_home)
         t2 = done(add(turn(t1), t1_far))
         t2_near = send(t2, near_mate)
         grad_query_scale = (
@@ -1286,7 +1278,7 @@
         t4 = done(pair_up(turn(t2), t2_near))
         t4_x = send(t4, x_mate)
         t4_core = send(t4, core_mate)
-        grad_tokens = done(copy(turn(home_grad)))
+        home_grad = send(turn(grad_tokens), to_home)
         q4 = done(pair_up(turn(q2), q2_near))
         q4_x = send(q4, x_mate)
         q4_core = send(q4, core_mate)
@@ -1294,13 +1286,13 @@
         t4_cross = send(t4_x, core_mate)
         used = 3 * nh * HD
         spread_at = jnp.stack([gx, near, 1 - gc])
-        t4_core = done(after(turn(t4_core), t4_cross))
+        totals = place_tail((turn(t4), t4_x, t4_core, t4_cross), jnp.stack([gx, near, gc]))
+        done(totals[0])
         q4_core = done(turn(q4_core))
         small = done(sum_all(turn(small))).reshape(-1)
+        grad_tokens = done(copy(turn(home_grad)))
         q4_x = done(turn(q4_x))
         q4_cross = send(q4_x, core_mate)
-        totals = place_tail((turn(t4), t4_x, t4_core, t4_cross), jnp.stack([gx, near, gc]))
-        done(totals[0])
         total_qkv = done(spread(turn(q4), q4_core, spread_at, used, 0))
         total_qkv = spread(turn(q4_x), q4_cross, spread_at, used, 1, total_qkv).reshape(wrows, 3 * D)
         return (

time: 459 us -> 432 us (0.941)
  waiting for transfers between devices: 159 us -> 136 us
    ppermute x41, waiting for transfers between devices: 159 us -> 136 us  [send(): return lax.ppermute(value, AXES, pairs(target))]
  transfers between devices with their start and end apart: 42 -> 42, of which waited for: 19 -> 19; matrix products, arithmetic and copies ran while one was open for 2% -> 3% of each run, Pallas kernels for 44% -> 46%
where the time goes in v11:
time: 432 us; the launch traced here: 424 us
  Pallas kernels  222 us (51%)
  waiting for transfers between devices  136 us (31%)
  starting transfers between devices  47.8 us (11%)
  local copies, waits for them, and re-layouts  11.7 us (3%)
  other arithmetic  5.94 us (1%)
    ppermute x41, waiting for transfers between devices, send(): return lax.ppermute(value, AXES, pairs(target))  136 us
    pallas_call x1, Pallas kernels, attn_bwd(): pl.pallas_call(functools.partial(bwd_kernel, first=group * nh, nh=nh, bq=...  43.5 us
    ppermute x41, starting transfers between devices, send(): return lax.ppermute(value, AXES, pairs(target))  41.4 us
    pallas_call x1, Pallas kernels, attn_fwd(): pl.pallas_call(functools.partial(fwd_kernel, nh=nh, bq=bq, bk=bk, nk=n //...  26 us
    pallas_call x2, Pallas kernels, project(): pl.pallas_call(functools.partial(project_kernel, count=count, halves=len(...  22.8 us
    pallas_call x1, Pallas kernels, tail(): pl.pallas_call(body, out_shape=[pltpu.HBM((rows, d), bf16)] + [pltpu.HBM(...  21.5 us
    pallas_call x2, Pallas kernels, share(): pl.pallas_call(share_kernel, out_shape=pltpu.HBM((d, n * w), bf16), grid_...  16.2 us
    pallas_call x1, Pallas kernels, cross(): pl.pallas_call(cross_kernel, out_shape=[pltpu.HBM((w // 2, cols), bf16)]...  11.6 us
  transfers between devices with their start and end apart: 42, of which 19 were waited for; matrix products, arithmetic and copies ran while one was open for 3% of the time, Pallas kernels for 46%

profile of v11, /device:TPU:0, one launch (start us, length us, event | category | flops | bytes accessed | tf_op | source)
XLA Modules:
  0.0 424.4 jit_solution(2248423721804617349)
XLA Ops:
  1.9 7.2 %collective-permute-start.5 = (bf16[512,1280]{1,0:T(8,128)(2,1)}, bf16[512,1280]{1,0:T(8,128)(2,1)}, u32[]{:S(2)}, u32[]{:S(2)}) collective-permute-start(bf16[512,1280]{1,0:T(8,128)(2,1)} %bitcast.68), channel_id=1, source_target_pairs={{0,8},{1,9},{2,10},{3,11},{12,4},{13,5},{14,6},{15,7},{16,24},{17,... | collective-permute-start | bytes 3932168 | tf_op jit(solution)/shard_map/ppermute | solution.py:1031
  9.2 4.4 %pick.1.x_ref.a_ref = bf16[640,1024]{1,0:T(8,128)(2,1)} custom-call(s32[1]{0:T(128)} %bitcast.mine.shard, bf16[640,3840]{1,0:T(8,128)(2,1)} %w_ref.1), custom_call_target="tpu_custom_call" | custom-call | flops 5000000000 | bytes 1000 | tf_op jit(solution)/shard_map/pick/pallas_call | solution.py:352
  15.7 4.2 stretch.2.refs_5_
  30.4 14.7 %collective-permute-done.7.x_ref.b_ref = bf16[640,1024]{1,0:T(8,128)(2,1)} collective-permute-done((bf16[640,1024]{1,0:T(8,128)(2,1)}, bf16[640,1024]{1,0:T(8,128)(2,1)}, u32[]{:S(2)}, u32[]{:S(2)}) %collective-permute-start.7) | collective-permute-done | bytes 1310752 | tf_op jit(solution)/shard_map/ppermute | solution.py:1031
  45.1 4.0 stretch.3.refs_6_
  54.1 11.2 %project.2 = (bf16[2048,1280]{1,0:T(8,128)(2,1)}, bf16[2048,512]{1,0:T(8,128)(2,1)}, bf16[2048,1024]{1,0:T(8,128)(2,1)}, bf16[512,1280]{1,0:T(8,128)(2,1)}) custom-call(s32[5]{0:T(128)S(1)} %stack.101.info, bf16[512,1280]{1,0:T(8,128)(2,1)S(1)} %bitcast.69, bf16[512,1280]{1,0:T(8,128)(2,1)} %collective-permute-done.5.refs_1_, ...), custom_call_target="tpu_custom_call" | custom-call | flops 15000000512 | bytes 1000 | tf_op jit(solution)/shard_map/project/pallas_call | solution.py:518
  75.6 11.6 %project.3 = (bf16[2048,1280]{1,0:T(8,128)(2,1)}, bf16[2048,512]{1,0:T(8,128)(2,1)}, bf16[2048,1024]{1,0:T(8,128)(2,1)}, bf16[512,1280]{1,0:T(8,128)(2,1)}) custom-call(s32[5]{0:T(128)S(1)} %stack.98.info, bf16[512,1280]{1,0:T(8,128)(2,1)S(1)} %collective-permute-done.2.refs_0_, ...), custom_call_target="tpu_custom_call", output_to_operand_aliasing={{0}: (11, {}), {1}: (12, {}), {2}: (13, {})} | custom-call | flops 15000000512 | bytes 1000 | tf_op jit(solution)/shard_map/project/pallas_call | solution.py:518
  87.2 26.0 %attn_fwd.1 = (bf16[2048,320]{1,0:T(8,128)(2,1)}, bf16[2048,512]{1,0:T(8,128)(2,1)}, bf16[2048,512]{1,0:T(8,128)(2,1)}) custom-call(s32[16]{0:T(128)S(1)} %reshape.183.flags, bf16[2048,512]{1,0:T(8,128)(2,1)} %get-tuple-element.83.q_ref, bf16[2048,1024]{1,0:T(8,128)(2,1)} %get-tuple-element.84.kv.kk.vv, s32[2048,1]{1,0:T(8,128)S(1)} %copy.29.segc, ...), custom_call_target="tpu_custom_call" | custom-call | flops 10000000 | bytes 1000 | tf_op jit(solution)/shard_map/attn_fwd/pallas_call | solution.py:172
  113.2 7.2 %collective-permute-done.9.half = bf16[3,320,1280]{2,1,0:T(8,128)(2,1)} collective-permute-done((bf16[3,320,1280]{2,1,0:T(8,128)(2,1)}, bf16[3,320,1280]{2,1,0:T(8,128)(2,1)}, u32[]{:S(2)}, u32[]{:S(2)}) %collective-permute-start.9) | collective-permute-done | bytes 2457632 | tf_op jit(solution)/shard_map/ppermute | solution.py:1031
  126.0 6.4 %order.1.w_ref = bf16[1024,1280]{1,0:T(8,128)(2,1)} custom-call(s32[1]{0:T(128)} %bitcast.10.own_first, bf16[640,1024]{1,0:T(8,128)(2,1)} %pick.1.x_ref.a_ref, bf16[640,1024]{1,0:T(8,128)(2,1)} %collective-permute-done.7.x_ref.b_ref), custom_call_target="tpu_custom_call" | custom-call | flops 199999995904 | bytes 1000 | tf_op jit(solution)/shard_map/order/pallas_call | solution.py:408
  132.4 7.8 %transpose.15.x_ref = bf16[1280,2048]{1,0:T(8,128)(2,1)} custom-call(bf16[2048,1280]{1,0:T(8,128)(2,1)} %get-tuple-element.92.x_ref), custom_call_target="tpu_custom_call" | custom-call | flops 1000000 | bytes 1000 | tf_op jit(solution)/shard_map/transpose/pallas_call | solution.py:432
  143.7 21.5 %tail.1 = (bf16[512,1280]{1,0:T(8,128)(2,1)}, bf16[3,512,1280]{2,1,0:T(8,128)(2,1)}, bf16[3,512,1280]{2,1,0:T(8,128)(2,1)}, f32[512,1280]{1,0:T(8,128)}, bf16[51...) custom-call(s32[4]{0:T(128)S(1)} %pad_add_fusion.at, ...), custom_call_target="tpu_custom_call" | custom-call | flops 10000000 | bytes 1000 | tf_op jit(solution)/shard_map/tail/pallas_call | solution.py:650
  167.3 7.3 %share.2 = bf16[1280,1920]{1,0:T(8,128)(2,1)} custom-call(s32[1]{0:T(128)} %bitcast.21.col, bf16[3,512,1280]{2,1,0:T(8,128)(2,1)} %get-tuple-element.99.left, bf16[3,512,1280]{2,1,0:T(8,128)(2,1)} %get-tuple-element.100.right), custom_call_target="tpu_custom_call" | custom-call | flops 1000000 | bytes 1000 | tf_op jit(solution)/shard_map/share/pallas_call | solution.py:688
  177.7 7.2 %collective-permute-done.17.do3 = bf16[512,320]{1,0:T(8,128)(2,1)S(1)} collective-permute-done((bf16[512,320]{1,0:T(8,128)(2,1)}, bf16[512,320]{1,0:T(8,128)(2,1)S(1)}, u32[]{:S(2)}, u32[]{:S(2)}) %collective-permute-start.17) | collective-permute-done | bytes 327712 | tf_op jit(solution)/shard_map/ppermute | solution.py:1031
  186.6 8.9 %share.3 = bf16[1280,1920]{1,0:T(8,128)(2,1)} custom-call(s32[1]{0:T(128)} %bitcast.22.col, bf16[3,512,1280]{2,1,0:T(8,128)(2,1)} %get-tuple-element.99.left, bf16[3,512,1280]{2,1,0:T(8,128)(2,1)} %get-tuple-element.100.right, bf16[1280,1920]{1,0:T(8,128)(2,1)} %collective-permute-done.19.refs_0_), custom_call_target="tpu_custom_call" | custom-call | flops 1000000 | bytes 1000 | tf_op jit(solution)/shard_map/share/pallas_call | solution.py:688
  195.5 6.4 %all-to-all-start = ((bf16[8,160,1920]{2,1,0:T(8,128)(2,1)}), bf16[8,160,1920]{2,1,0:T(8,128)(2,1)}, u32[]{:S(2)}, u32[]{:S(2)}) async-start(bf16[8,160,1920]{2,1,0:T(8,128)(2,1)} %bitcast.78), calls=%async_computation | async-start | bytes 9830400 | tf_op jit(solution)/shard_map/all_to_all | solution.py:1200
  202.0 43.5 %attn_bwd.1 = (bf16[2048,1024]{1,0:T(8,128)(2,1)}, f32[8,128]{1,0:T(8,128)}) custom-call(s32[16]{0:T(128)S(1)} %copy-done.7, s32[1]{0:T(128)} %bitcast.mine.shard, bf16[2048,512]{1,0:T(8,128)(2,1)} %get-tuple-element.105.qa, bf16[2048,1024]{1,0:T(8,128)(2,1)} %get-tuple-element.84.kv.kk.vv, bf16[2048,1024]{1,0:T(8,128)(2,1)} %get-tuple-element.84.kv.kk.vv, ...), custom_call_target="tpu_custom_call" | custom-call | flops 299999985664 | bytes 1000 | tf_op jit(solution)/shard_map/attn_bwd/pallas_call | solution.py:314
  245.6 6.8 %back.2 = bf16[2,512,1280]{2,1,0:T(8,128)(2,1)} custom-call(s32[2]{0:T(128)S(1)} %pad_add_fusion.1.shards, bf16[2048,1024]{1,0:T(8,128)(2,1)} %get-tuple-element.114.g_ref, bf16[1024,1280]{1,0:T(8,128)(2,1)} %order.1.w_ref), custom_call_target="tpu_custom_call" | custom-call | flops 1000000 | bytes 1000 | tf_op jit(solution)/shard_map/back/pallas_call | solution.py:924
  252.4 11.6 %cross.1 = (bf16[320,1024]{1,0:T(8,128)(2,1)}, bf16[320,1024]{1,0:T(8,128)(2,1)}, bf16[320,1024]{1,0:T(8,128)(2,1)}, bf16[320,1024]{1,0:T(8,128)(2,1)}) custom-call(s32[2]{0:T(128)S(1)} %pad_add_fusion.2.at, bf16[1280,2048]{1,0:T(8,128)(2,1)} %transpose.15.x_ref, bf16[2048,1024]{1,0:T(8,128)(2,1)} %get-tuple-element.114.g_ref), custom_call_target="tpu_custom_call" | custom-call | flops 1000000 | bytes 1000 | tf_op jit(solution)/shard_map/cross/pallas_call | solution.py:842
  264.0 4.7 %back.3 = bf16[1,512,1280]{2,1,0:T(8,128)(2,1)} custom-call(s32[1]{0:T(128)} %bitcast.26.shards, bf16[2048,1024]{1,0:T(8,128)(2,1)} %get-tuple-element.114.g_ref, bf16[1024,1280]{1,0:T(8,128)(2,1)} %order.1.w_ref, bf16[2,512,1280]{2,1,0:T(8,128)(2,1)S(1)} %collective-permute-done.20.refs_0_.core), custom_call_target="tpu_custom_call" | custom-call | flops 1000000 | bytes 1000 | tf_op jit(solution)/shard_map/back/pallas_call | solution.py:924
  280.8 7.8 %collective-permute-done.22 = bf16[320,1024]{1,0:T(8,128)(2,1)} collective-permute-done((bf16[320,1024]{1,0:T(8,128)(2,1)}, bf16[320,1024]{1,0:T(8,128)(2,1)}, u32[]{:S(2)}, u32[]{:S(2)}) %collective-permute-start.22) | collective-permute-done | bytes 655392 | tf_op jit(solution)/shard_map/ppermute | solution.py:1031
  288.6 14.5 %collective-permute-done.23 = bf16[320,1024]{1,0:T(8,128)(2,1)} collective-permute-done((bf16[320,1024]{1,0:T(8,128)(2,1)}, bf16[320,1024]{1,0:T(8,128)(2,1)}, u32[]{:S(2)}, u32[]{:S(2)}) %collective-permute-start.23) | collective-permute-done | bytes 655392 | tf_op jit(solution)/shard_map/ppermute | solution.py:1031
  306.2 7.5 %collective-permute-done.21.near = bf16[1,512,1280]{2,1,0:T(8,128)(2,1)} collective-permute-done((bf16[1,512,1280]{2,1,0:T(8,128)(2,1)}, bf16[1,512,1280]{2,1,0:T(8,128)(2,1)}, u32[]{:S(2)}, u32[]{:S(2)}) %collective-permute-start.21) | collective-permute-done | bytes 1310752 | tf_op jit(solution)/shard_map/ppermute | solution.py:1031
  313.7 6.6 %finish.1 = (bf16[512,1280]{1,0:T(8,128)(2,1)}, f32[1,1280]{1,0:T(1,128)S(1)}) custom-call(s32[1]{0:T(128)} %bitcast.mine.shard, bf16[2048,1024]{1,0:T(8,128)(2,1)} %get-tuple-element.114.g_ref, bf16[1024,1280]{1,0:T(8,128)(2,1)} %order.1.w_ref, bf16[2,512,1280]{2,1,0:T(8,128)(2,1)S(1)} %collective-permute-done.20.refs_0_.core, ...), custom_call_target="tpu_custom_call" | custom-call | flops 1000000 | bytes 1000 | tf_op jit(solution)/shard_map/finish/pallas_call | solution.py:962
  322.5 19.3 %collective-permute-done.26.b_ref = bf16[320,1024]{1,0:T(8,128)(2,1)S(1)} collective-permute-done((bf16[320,1024]{1,0:T(8,128)(2,1)}, bf16[320,1024]{1,0:T(8,128)(2,1)S(1)}, u32[]{:S(2)}, u32[]{:S(2)}) %collective-permute-start.26) | collective-permute-done | bytes 655392 | tf_op jit(solution)/shard_map/ppermute | solution.py:1031
  344.9 7.4 %collective-permute-done.27.b_ref = bf16[160,1920]{1,0:T(8,128)(2,1)S(1)} collective-permute-done((bf16[160,1920]{1,0:T(8,128)(2,1)}, bf16[160,1920]{1,0:T(8,128)(2,1)S(1)}, u32[]{:S(2)}, u32[]{:S(2)}) %collective-permute-start.27) | collective-permute-done | bytes 614432 | tf_op jit(solution)/shard_map/ppermute | solution.py:1031
  357.2 15.2 %collective-permute-done.29.b_ref = bf16[320,1024]{1,0:T(8,128)(2,1)S(1)} collective-permute-done((bf16[320,1024]{1,0:T(8,128)(2,1)S(1)}, bf16[320,1024]{1,0:T(8,128)(2,1)S(1)}, u32[]{:S(2)}, u32[]{:S(2)}) %collective-permute-start.29) | collective-permute-done | bytes 655392 | tf_op jit(solution)/shard_map/ppermute | solution.py:1031
  376.6 9.3 %collective-permute-done.31.own_x = bf16[2,160,1920]{2,1,0:T(8,128)(2,1)} collective-permute-done((bf16[2,160,1920]{2,1,0:T(8,128)(2,1)}, bf16[2,160,1920]{2,1,0:T(8,128)(2,1)}, u32[]{:S(2)}, u32[]{:S(2)}) %collective-permute-start.31) | collective-permute-done | bytes 1228832 | tf_op jit(solution)/shard_map/ppermute | solution.py:1031
  389.2 6.6 %place_tail.1 = (f32[4,160,1280]{2,1,0:T(8,128)}, f32[4,160,1280]{2,1,0:T(8,128)}, f32[4,160,1280]{2,1,0:T(8,128)}) custom-call(s32[3]{0:T(128)S(1)} %pad_add_fusion.3.at, bf16[2,160,1920]{2,1,0:T(8,128)(2,1)S(1)} %copy-done.1, bf16[2,160,1920]{2,1,0:T(8,128)(2,1)} %collective-permute-done.31.own_x, bf16[2,160,1920]{2,1,0:T(8,128)(2,1)} %collective-permute-done.32.mate, ...), custom_call_target="tpu_custom_call" | custom-call | flops 1000000 | bytes 1000 | tf_op jit(solution)/shard_map/place_tail/pallas_call | solution.py:805
  400.7 3.8 collective-permute-done.36
  404.6 4.5 %collective-permute-done.37 = f32[21,128]{1,0:T(8,128)S(1)} collective-permute-done((f32[21,128]{1,0:T(8,128)S(1)}, f32[21,128]{1,0:T(8,128)S(1)}, u32[]{:S(2)}, u32[]{:S(2)}) %collective-permute-start.37) | collective-permute-done | bytes 10784 | tf_op jit(solution)/shard_map/ppermute | solution.py:1031
  415.3 4.4 %spread.2.refs_0_ = f32[2,320,3840]{2,1,0:T(8,128)} custom-call(s32[3]{0:T(128)S(1)} %pad_add_fusion.5.at, bf16[2,320,1024]{2,1,0:T(8,128)(2,1)S(1)} %copy-done, bf16[2,320,1024]{2,1,0:T(8,128)(2,1)} %collective-permute-done.30.mate), custom_call_target="tpu_custom_call" | custom-call | flops 1000000 | bytes 1000 | tf_op jit(solution)/shard_map/spread/pallas_call | solution.py:888
  (192 shorter events, 93.5 us)
Async XLA Ops:
  0.6 22.2 %collective-permute-start.1 = (bf16[512,1280]{1,0:T(8,128)(2,1)}, bf16[512,1280]{1,0:T(8,128)(2,1)}, u32[]{:S(2)}, u32[]{:S(2)}) collective-permute-start(bf16[512,1280]{1,0:T(8,128)(2,1)} %bitcast.67), channel_id=1, source_target_pairs={{2,0},{3,1},{4,2},{5,3},{6,4},{7,5},{8,10},{9,11},{10,12},{11,13},... | collective-permute-start | bytes 3932168 | tf_op jit(solution)/shard_map/ppermute | solution.py:1031
  1.9 52.1 %collective-permute-start.5 = (bf16[512,1280]{1,0:T(8,128)(2,1)}, bf16[512,1280]{1,0:T(8,128)(2,1)}, u32[]{:S(2)}, u32[]{:S(2)}) collective-permute-start(bf16[512,1280]{1,0:T(8,128)(2,1)} %bitcast.68), channel_id=1, source_target_pairs={{0,8},{1,9},{2,10},{3,11},{12,4},{13,5},{14,6},{15,7},{16,24},{17,... | collective-permute-start | bytes 3932168 | tf_op jit(solution)/shard_map/ppermute | solution.py:1031
  9.2 63.8 %collective-permute-start = (s32[1,2048]{1,0:T(1,128)}, s32[1,2048]{1,0:T(1,128)S(1)}, u32[]{:S(2)}, u32[]{:S(2)}) collective-permute-start(s32[1,2048]{1,0:T(1,128)} %param.11), channel_id=1, source_target_pairs={{0,8},{1,9},{2,10},{3,11},{4,12},{5,13},{6,14},{7,15},{8,0},{9,1},... | collective-permute-start | bytes 24584 | tf_op jit(solution)/shard_map/ppermute | solution.py:1031
  13.6 31.5 %collective-permute-start.7 = (bf16[640,1024]{1,0:T(8,128)(2,1)}, bf16[640,1024]{1,0:T(8,128)(2,1)}, u32[]{:S(2)}, u32[]{:S(2)}) collective-permute-start(bf16[640,1024]{1,0:T(8,128)(2,1)} %pick.1.x_ref.a_ref), channel_id=1, source_target_pairs={{0,1},{1,0},{2,3},{3,2},{4,5},{5,4},{6,7},{7,6},{8,9},{9,8},{10,11... | collective-permute-start | bytes 3932168 | tf_op jit(solution)/shard_map/ppermute | solution.py:1031
  22.8 26.3 %collective-permute-start.2 = (bf16[512,1280]{1,0:T(8,128)(2,1)}, bf16[512,1280]{1,0:T(8,128)(2,1)S(1)}, u32[]{:S(2)}, u32[]{:S(2)}) collective-permute-start(bf16[512,1280]{1,0:T(8,128)(2,1)} %collective-permute-done.1.refs_2_), channel_id=1, source_target_pairs={{2,0},{3,1},{4,2},{5,3},{10,12},{11,13},{12,14},{13,15},{18,16},{1... | collective-permute-start | bytes 3932168 | tf_op jit(solution)/shard_map/ppermute | solution.py:1031
  27.6 26.4 %collective-permute-start.6 = (bf16[512,1280]{1,0:T(8,128)(2,1)}, bf16[512,1280]{1,0:T(8,128)(2,1)}, u32[]{:S(2)}, u32[]{:S(2)}) collective-permute-start(bf16[512,1280]{1,0:T(8,128)(2,1)} %collective-permute-done.1.refs_2_), channel_id=1, source_target_pairs={{0,8},{1,9},{2,10},{3,11},{12,4},{13,5},{14,6},{15,7},{16,24},{17,... | collective-permute-start | bytes 3932168 | tf_op jit(solution)/shard_map/ppermute | solution.py:1031
  49.3 19.6 %collective-permute-start.4 = (bf16[512,1280]{1,0:T(8,128)(2,1)S(1)}, bf16[512,1280]{1,0:T(8,128)(2,1)}, u32[]{:S(2)}, u32[]{:S(2)}) collective-permute-start(bf16[512,1280]{1,0:T(8,128)(2,1)S(1)} %broadcast_select_fusion), channel_id=1, source_target_pairs={{0,2},{1,3},{2,0},{3,1},{12,14},{13,15},{14,12},{15,13},{16,18},{1... | collective-permute-start | bytes 3932168 | tf_op jit(solution)/shard_map/ppermute | solution.py:1031
  51.7 23.9 %collective-permute-start.3 = (bf16[512,1280]{1,0:T(8,128)(2,1)S(1)}, bf16[512,1280]{1,0:T(8,128)(2,1)}, u32[]{:S(2)}, u32[]{:S(2)}) collective-permute-start(bf16[512,1280]{1,0:T(8,128)(2,1)S(1)} %collective-permute-done.2.refs_0_), channel_id=1, source_target_pairs={{0,8},{1,9},{2,10},{3,11},{12,4},{13,5},{14,6},{15,7},{16,24},{17,... | collective-permute-start | bytes 3932168 | tf_op jit(solution)/shard_map/ppermute | solution.py:1031
  71.4 48.9 %collective-permute-start.9 = (bf16[3,320,1280]{2,1,0:T(8,128)(2,1)}, bf16[3,320,1280]{2,1,0:T(8,128)(2,1)}, u32[]{:S(2)}, u32[]{:S(2)}) collective-permute-start(bf16[3,320,1280]{2,1,0:T(8,128)(2,1)} %pad_maximum_fusion), channel_id=1, source_target_pairs={{0,1},{1,0},{2,3},{3,2},{4,5},{5,4},{6,7},{7,6},{8,9},{9,8},{10,11... | collective-permute-start | bytes 7372808 | tf_op jit(solution)/shard_map/ppermute | solution.py:1031
  75.0 45.3 %collective-permute-start.10 = (bf16[512,1280]{1,0:T(8,128)(2,1)}, bf16[512,1280]{1,0:T(8,128)(2,1)S(1)}, u32[]{:S(2)}, u32[]{:S(2)}) collective-permute-start(bf16[512,1280]{1,0:T(8,128)(2,1)} %bitcast.89), channel_id=1, source_target_pairs={{0,8},{1,9},{2,0},{3,1},{4,10},{5,11},{6,2},{7,3},{8,12},{9,13},{1... | collective-permute-start | bytes 3932168 | tf_op jit(solution)/shard_map/ppermute | solution.py:1031
  123.8 16.4 %collective-permute-start.11 = (bf16[512,320]{1,0:T(8,128)(2,1)}, bf16[512,320]{1,0:T(8,128)(2,1)}, u32[]{:S(2)}, u32[]{:S(2)}) collective-permute-start(bf16[512,320]{1,0:T(8,128)(2,1)} %get-tuple-element.151), channel_id=1, source_target_pairs={{0,8},{1,9},{2,10},{3,11},{4,12},{5,13},{6,14},{7,15},{8,0},{9,1},... | collective-permute-start | bytes 983048 | tf_op jit(solution)/shard_map/ppermute | solution.py:1031
  123.8 16.4 %collective-permute-start.12 = (bf16[512,320]{1,0:T(8,128)(2,1)}, bf16[512,320]{1,0:T(8,128)(2,1)}, u32[]{:S(2)}, u32[]{:S(2)}) collective-permute-start(bf16[512,320]{1,0:T(8,128)(2,1)} %get-tuple-element.150), channel_id=1, source_target_pairs={{0,2},{1,3},{2,0},{3,1},{4,6},{5,7},{6,4},{7,5},{8,10},{9,11},{10,... | collective-permute-start | bytes 983048 | tf_op jit(solution)/shard_map/ppermute | solution.py:1031
  124.3 19.4 %collective-permute-start.13 = (bf16[512,320]{1,0:T(8,128)(2,1)}, bf16[512,320]{1,0:T(8,128)(2,1)}, u32[]{:S(2)}, u32[]{:S(2)}) collective-permute-start(bf16[512,320]{1,0:T(8,128)(2,1)} %get-tuple-element.149), channel_id=1, source_target_pairs={{0,10},{1,11},{2,8},{3,9},{4,14},{5,15},{6,12},{7,13},{8,2},{9,3},... | collective-permute-start | bytes 983048 | tf_op jit(solution)/shard_map/ppermute | solution.py:1031
  125.7 18.0 %collective-permute-start.14 = (bf16[3,320,1280]{2,1,0:T(8,128)(2,1)}, bf16[3,320,1280]{2,1,0:T(8,128)(2,1)}, u32[]{:S(2)}, u32[]{:S(2)}) collective-permute-start(bf16[3,320,1280]{2,1,0:T(8,128)(2,1)} %collective-permute-done.9.half), channel_id=1, source_target_pairs={{0,8},{1,9},{2,10},{3,11},{4,12},{5,13},{6,14},{7,15},{8,0},{9,1},... | collective-permute-start | bytes 7372808 | tf_op jit(solution)/shard_map/ppermute | solution.py:1031
  165.5 12.1 %collective-permute-start.16 = (bf16[512,320]{1,0:T(8,128)(2,1)}, bf16[512,320]{1,0:T(8,128)(2,1)S(1)}, u32[]{:S(2)}, u32[]{:S(2)}) collective-permute-start(bf16[512,320]{1,0:T(8,128)(2,1)} %get-tuple-element.97), channel_id=1, source_target_pairs={{0,2},{1,3},{2,0},{3,1},{4,6},{5,7},{6,4},{7,5},{8,10},{9,11},{10,... | collective-permute-start | bytes 983048 | tf_op jit(solution)/shard_map/ppermute | solution.py:1031
  166.0 18.9 %collective-permute-start.17 = (bf16[512,320]{1,0:T(8,128)(2,1)}, bf16[512,320]{1,0:T(8,128)(2,1)S(1)}, u32[]{:S(2)}, u32[]{:S(2)}) collective-permute-start(bf16[512,320]{1,0:T(8,128)(2,1)} %get-tuple-element.102), channel_id=1, source_target_pairs={{0,10},{1,11},{2,8},{3,9},{4,14},{5,15},{6,12},{7,13},{8,2},{9,3},... | collective-permute-start | bytes 983048 | tf_op jit(solution)/shard_map/ppermute | solution.py:1031
  174.7 11.9 %collective-permute-start.19 = (bf16[1280,1920]{1,0:T(8,128)(2,1)}, bf16[1280,1920]{1,0:T(8,128)(2,1)}, u32[]{:S(2)}, u32[]{:S(2)}) collective-permute-start(bf16[1280,1920]{1,0:T(8,128)(2,1)} %share.2), channel_id=1, source_target_pairs={{0,8},{1,9},{2,10},{3,11},{4,12},{5,13},{6,14},{7,15},{8,0},{9,1},... | collective-permute-start | bytes 14745608 | tf_op jit(solution)/shard_map/ppermute | solution.py:1031
  184.8 60.8 %collective-permute-start.18 = (bf16[512,1280]{1,0:T(8,128)(2,1)}, bf16[512,1280]{1,0:T(8,128)(2,1)}, u32[]{:S(2)}, u32[]{:S(2)}) collective-permute-start(bf16[512,1280]{1,0:T(8,128)(2,1)} %get-tuple-element.104), channel_id=1, source_target_pairs={{0,2},{1,3},{2,6},{3,7},{4,10},{5,11},{6,14},{7,15},{8,0},{9,1},{1... | collective-permute-start | bytes 3932168 | tf_op jit(solution)/shard_map/ppermute | solution.py:1031
  195.5 78.6 %all-to-all-start = ((bf16[8,160,1920]{2,1,0:T(8,128)(2,1)}), bf16[8,160,1920]{2,1,0:T(8,128)(2,1)}, u32[]{:S(2)}, u32[]{:S(2)}) async-start(bf16[8,160,1920]{2,1,0:T(8,128)(2,1)} %bitcast.78), calls=%async_computation | async-start | bytes 9830400 | tf_op jit(solution)/shard_map/all_to_all | solution.py:1200
  252.4 11.6 %collective-permute-start.20 = (bf16[2,512,1280]{2,1,0:T(8,128)(2,1)}, bf16[2,512,1280]{2,1,0:T(8,128)(2,1)S(1)}, u32[]{:S(2)}, u32[]{:S(2)}) collective-permute-start(bf16[2,512,1280]{2,1,0:T(8,128)(2,1)} %back.2), channel_id=1, source_target_pairs={{0,8},{1,9},{2,10},{3,11},{4,12},{5,13},{6,14},{7,15},{8,0},{9,1},... | collective-permute-start | bytes 7864328 | tf_op jit(solution)/shard_map/ppermute | solution.py:1031
  268.6 45.0 %collective-permute-start.21 = (bf16[1,512,1280]{2,1,0:T(8,128)(2,1)}, bf16[1,512,1280]{2,1,0:T(8,128)(2,1)}, u32[]{:S(2)}, u32[]{:S(2)}) collective-permute-start(bf16[1,512,1280]{2,1,0:T(8,128)(2,1)} %back.3), channel_id=1, source_target_pairs={{0,2},{1,3},{2,0},{3,1},{4,6},{5,7},{6,4},{7,5},{8,10},{9,11},{10,... | collective-permute-start | bytes 3932168 | tf_op jit(solution)/shard_map/ppermute | solution.py:1031
  270.7 17.9 %collective-permute-start.22 = (bf16[320,1024]{1,0:T(8,128)(2,1)}, bf16[320,1024]{1,0:T(8,128)(2,1)}, u32[]{:S(2)}, u32[]{:S(2)}) collective-permute-start(bf16[320,1024]{1,0:T(8,128)(2,1)} %get-tuple-element.120), channel_id=1, source_target_pairs={{0,16},{1,17},{2,18},{3,19},{4,20},{5,21},{6,22},{7,23},{8,24},{9,... | collective-permute-start | bytes 1966088 | tf_op jit(solution)/shard_map/ppermute | solution.py:1031
  272.1 30.9 %collective-permute-start.23 = (bf16[320,1024]{1,0:T(8,128)(2,1)}, bf16[320,1024]{1,0:T(8,128)(2,1)}, u32[]{:S(2)}, u32[]{:S(2)}) collective-permute-start(bf16[320,1024]{1,0:T(8,128)(2,1)} %get-tuple-element.121), channel_id=1, source_target_pairs={{0,1},{1,0},{2,3},{3,2},{4,5},{5,4},{6,7},{7,6},{8,9},{9,8},{10,11... | collective-permute-start | bytes 1966088 | tf_op jit(solution)/shard_map/ppermute | solution.py:1031
  273.6 29.5 %collective-permute-start.24 = (bf16[320,1024]{1,0:T(8,128)(2,1)}, bf16[320,1024]{1,0:T(8,128)(2,1)}, u32[]{:S(2)}, u32[]{:S(2)}) collective-permute-start(bf16[320,1024]{1,0:T(8,128)(2,1)} %get-tuple-element.122), channel_id=1, source_target_pairs={{0,17},{1,16},{2,19},{3,18},{4,21},{5,20},{6,23},{7,22},{8,25},{9,... | collective-permute-start | bytes 1966088 | tf_op jit(solution)/shard_map/ppermute | solution.py:1031
  277.6 42.6 %collective-permute-start.25 = (bf16[160,1920]{1,0:T(8,128)(2,1)}, bf16[160,1920]{1,0:T(8,128)(2,1)}, u32[]{:S(2)}, u32[]{:S(2)}) collective-permute-start(bf16[160,1920]{1,0:T(8,128)(2,1)} %total.2.a_ref), channel_id=1, source_target_pairs={{0,4},{1,5},{2,6},{3,7},{4,0},{5,1},{6,2},{7,3},{8,12},{9,13},{10,... | collective-permute-start | bytes 1843208 | tf_op jit(solution)/shard_map/ppermute | solution.py:1031
  305.5 36.4 %collective-permute-start.26 = (bf16[320,1024]{1,0:T(8,128)(2,1)}, bf16[320,1024]{1,0:T(8,128)(2,1)S(1)}, u32[]{:S(2)}, u32[]{:S(2)}) collective-permute-start(bf16[320,1024]{1,0:T(8,128)(2,1)} %total.3.a_ref), channel_id=1, source_target_pairs={{0,4},{1,5},{2,6},{3,7},{4,0},{5,1},{6,2},{7,3},{8,12},{9,13},{10,... | collective-permute-start | bytes 1966088 | tf_op jit(solution)/shard_map/ppermute | solution.py:1031
  322.5 29.8 %collective-permute-start.27 = (bf16[160,1920]{1,0:T(8,128)(2,1)}, bf16[160,1920]{1,0:T(8,128)(2,1)S(1)}, u32[]{:S(2)}, u32[]{:S(2)}) collective-permute-start(bf16[160,1920]{1,0:T(8,128)(2,1)} %add.135.a_ref), channel_id=1, source_target_pairs={{0,2},{1,3},{2,0},{3,1},{4,6},{5,7},{6,4},{7,5},{8,10},{9,11},{10,... | collective-permute-start | bytes 1843208 | tf_op jit(solution)/shard_map/ppermute | solution.py:1031
  355.6 30.3 %collective-permute-start.31 = (bf16[2,160,1920]{2,1,0:T(8,128)(2,1)}, bf16[2,160,1920]{2,1,0:T(8,128)(2,1)}, u32[]{:S(2)}, u32[]{:S(2)}) collective-permute-start(bf16[2,160,1920]{2,1,0:T(8,128)(2,1)} %pair_up.2.own), channel_id=1, source_target_pairs={{0,16},{1,17},{2,18},{3,19},{4,20},{5,21},{6,22},{7,23},{8,24},{9,... | collective-permute-start | bytes 3686408 | tf_op jit(solution)/shard_map/ppermute | solution.py:1031
  357.2 15.2 %collective-permute-start.29 = (bf16[320,1024]{1,0:T(8,128)(2,1)S(1)}, bf16[320,1024]{1,0:T(8,128)(2,1)S(1)}, u32[]{:S(2)}, u32[]{:S(2)}) collective-permute-start(bf16[320,1024]{1,0:T(8,128)(2,1)S(1)} %copy-done.18), channel_id=1, source_target_pairs={{0,2},{1,3},{2,0},{3,1},{4,6},{5,7},{6,4},{7,5},{8,10},{9,11},{10,... | collective-permute-start | bytes 1966088 | tf_op jit(solution)/shard_map/ppermute | solution.py:1031
  375.6 20.1 %collective-permute-start.30 = (bf16[2,320,1024]{2,1,0:T(8,128)(2,1)}, bf16[2,320,1024]{2,1,0:T(8,128)(2,1)}, u32[]{:S(2)}, u32[]{:S(2)}) collective-permute-start(bf16[2,320,1024]{2,1,0:T(8,128)(2,1)} %pair_up.3.own), channel_id=1, source_target_pairs={{0,8},{1,9},{2,10},{3,11},{4,12},{5,13},{6,14},{7,15},{8,0},{9,1},... | collective-permute-start | bytes 3932168 | tf_op jit(solution)/shard_map/ppermute | solution.py:1031
  375.6 37.2 %collective-permute-start.28 = (bf16[512,1280]{1,0:T(8,128)(2,1)}, bf16[512,1280]{1,0:T(8,128)(2,1)}, u32[]{:S(2)}, u32[]{:S(2)}) collective-permute-start(bf16[512,1280]{1,0:T(8,128)(2,1)} %get-tuple-element.129), channel_id=1, source_target_pairs={{0,2},{1,3},{2,6},{3,7},{4,10},{5,11},{6,14},{7,15},{8,0},{9,1},{1... | collective-permute-start | bytes 3932168 | tf_op jit(solution)/shard_map/ppermute | solution.py:1031
  375.9 39.3 %collective-permute-start.39 = (bf16[2,320,1024]{2,1,0:T(8,128)(2,1)}, bf16[2,320,1024]{2,1,0:T(8,128)(2,1)S(1)}, u32[]{:S(2)}, u32[]{:S(2)}) collective-permute-start(bf16[2,320,1024]{2,1,0:T(8,128)(2,1)} %pair_up.3.own), channel_id=1, source_target_pairs={{0,16},{1,17},{2,18},{3,19},{4,20},{5,21},{6,22},{7,23},{8,24},{9,... | collective-permute-start | bytes 3932168 | tf_op jit(solution)/shard_map/ppermute | solution.py:1031
  (43 other events, 408.5 us)

commit v12 on v11

--- a/solution.py
+++ b/solution.py
@@ -1251,6 +1251,8 @@
         by_place[0] = turn(by_place[0])
         q1 = done(total([by_place]))
         q1_far = send(q1, far_mate)
+        t2 = done(add(turn(t1), t1_far))
+        t2_near = send(t2, near_mate)
         grad_tokens, grad_gain_attn = finish(
             grad_project,
             w_trans,
@@ -1262,8 +1264,6 @@
             late_gain.reshape(1, -1),
         )
         done(grad_tokens)
-        t2 = done(add(turn(t1), t1_far))
-        t2_near = send(t2, near_mate)
         grad_query_scale = (
             grad_lanes[0, :HD]
             / (dim_scale * log2e)

time: 432 us -> 425 us (0.984)
  waiting for transfers between devices: 136 us -> 127 us
    ppermute x41, waiting for transfers between devices: 136 us -> 127 us  [send(): return lax.ppermute(value, AXES, pairs(target))]
  transfers between devices with their start and end apart: 42 -> 42, of which waited for: 19 -> 18; matrix products, arithmetic and copies ran while one was open for 3% -> 3% of each run, Pallas kernels for 46% -> 47%
where the time goes in v12:
time: 425 us; the launch traced here: 418 us
  Pallas kernels  222 us (52%)
  waiting for transfers between devices  127 us (30%)
  starting transfers between devices  50.3 us (12%)
  local copies, waits for them, and re-layouts  10.8 us (3%)
  other arithmetic  5.96 us (1%)
    ppermute x41, waiting for transfers between devices, send(): return lax.ppermute(value, AXES, pairs(target))  127 us
    ppermute x41, starting transfers between devices, send(): return lax.ppermute(value, AXES, pairs(target))  43.8 us
    pallas_call x1, Pallas kernels, attn_bwd(): pl.pallas_call(functools.partial(bwd_kernel, first=group * nh, nh=nh, bq=...  43.6 us
    pallas_call x1, Pallas kernels, attn_fwd(): pl.pallas_call(functools.partial(fwd_kernel, nh=nh, bq=bq, bk=bk, nk=n //...  26 us
    pallas_call x2, Pallas kernels, project(): pl.pallas_call(functools.partial(project_kernel, count=count, halves=len(...  22.8 us
    pallas_call x1, Pallas kernels, tail(): pl.pallas_call(body, out_shape=[pltpu.HBM((rows, d), bf16)] + [pltpu.HBM(...  21.5 us
    pallas_call x2, Pallas kernels, share(): pl.pallas_call(share_kernel, out_shape=pltpu.HBM((d, n * w), bf16), grid_...  16.2 us
    pallas_call x1, Pallas kernels, cross(): pl.pallas_call(cross_kernel, out_shape=[pltpu.HBM((w // 2, cols), bf16)]...  11.6 us
  transfers between devices with their start and end apart: 42, of which 18 were waited for; matrix products, arithmetic and copies ran while one was open for 3% of the time, Pallas kernels for 47%

profile of v12, /device:TPU:0, one launch (start us, length us, event | category | flops | bytes accessed | tf_op | source)
XLA Modules:
  0.0 418.0 jit_solution(13094786137587505369)
XLA Ops:
  1.9 7.3 %collective-permute-start.5 = (bf16[512,1280]{1,0:T(8,128)(2,1)}, bf16[512,1280]{1,0:T(8,128)(2,1)}, u32[]{:S(2)}, u32[]{:S(2)}) collective-permute-start(bf16[512,1280]{1,0:T(8,128)(2,1)} %bitcast.68), channel_id=1, source_target_pairs={{0,8},{1,9},{2,10},{3,11},{12,4},{13,5},{14,6},{15,7},{16,24},{17,... | collective-permute-start | bytes 3932168 | tf_op jit(solution)/shard_map/ppermute | solution.py:1031
  9.2 4.4 %pick.1.x_ref.a_ref = bf16[640,1024]{1,0:T(8,128)(2,1)} custom-call(s32[1]{0:T(128)} %bitcast.mine.shard, bf16[640,3840]{1,0:T(8,128)(2,1)} %w_ref.1), custom_call_target="tpu_custom_call" | custom-call | flops 5000000000 | bytes 1000 | tf_op jit(solution)/shard_map/pick/pallas_call | solution.py:352
  15.7 4.2 stretch.2.refs_5_
  30.4 14.7 %collective-permute-done.7.x_ref.b_ref = bf16[640,1024]{1,0:T(8,128)(2,1)} collective-permute-done((bf16[640,1024]{1,0:T(8,128)(2,1)}, bf16[640,1024]{1,0:T(8,128)(2,1)}, u32[]{:S(2)}, u32[]{:S(2)}) %collective-permute-start.7) | collective-permute-done | bytes 1310752 | tf_op jit(solution)/shard_map/ppermute | solution.py:1031
  45.1 4.0 stretch.3.refs_6_
  54.1 11.2 %project.2 = (bf16[2048,1280]{1,0:T(8,128)(2,1)}, bf16[2048,512]{1,0:T(8,128)(2,1)}, bf16[2048,1024]{1,0:T(8,128)(2,1)}, bf16[512,1280]{1,0:T(8,128)(2,1)}) custom-call(s32[5]{0:T(128)S(1)} %stack.101.info, bf16[512,1280]{1,0:T(8,128)(2,1)S(1)} %bitcast.69, bf16[512,1280]{1,0:T(8,128)(2,1)} %collective-permute-done.5.refs_1_, ...), custom_call_target="tpu_custom_call" | custom-call | flops 15000000512 | bytes 1000 | tf_op jit(solution)/shard_map/project/pallas_call | solution.py:518
  65.3 3.6 collective-permute-done.4.refs_2_
  75.6 11.6 %project.3 = (bf16[2048,1280]{1,0:T(8,128)(2,1)}, bf16[2048,512]{1,0:T(8,128)(2,1)}, bf16[2048,1024]{1,0:T(8,128)(2,1)}, bf16[512,1280]{1,0:T(8,128)(2,1)}) custom-call(s32[5]{0:T(128)S(1)} %stack.98.info, bf16[512,1280]{1,0:T(8,128)(2,1)S(1)} %collective-permute-done.2.refs_0_, ...), custom_call_target="tpu_custom_call", output_to_operand_aliasing={{0}: (11, {}), {1}: (12, {}), {2}: (13, {})} | custom-call | flops 15000000512 | bytes 1000 | tf_op jit(solution)/shard_map/project/pallas_call | solution.py:518
  87.2 26.0 %attn_fwd.1 = (bf16[2048,320]{1,0:T(8,128)(2,1)}, bf16[2048,512]{1,0:T(8,128)(2,1)}, bf16[2048,512]{1,0:T(8,128)(2,1)}) custom-call(s32[16]{0:T(128)S(1)} %reshape.183.flags, bf16[2048,512]{1,0:T(8,128)(2,1)} %get-tuple-element.83.q_ref, bf16[2048,1024]{1,0:T(8,128)(2,1)} %get-tuple-element.84.kv.kk.vv, s32[2048,1]{1,0:T(8,128)S(1)} %copy.29.segc, ...), custom_call_target="tpu_custom_call" | custom-call | flops 10000000 | bytes 1000 | tf_op jit(solution)/shard_map/attn_fwd/pallas_call | solution.py:172
  113.2 7.2 %collective-permute-done.9.half = bf16[3,320,1280]{2,1,0:T(8,128)(2,1)} collective-permute-done((bf16[3,320,1280]{2,1,0:T(8,128)(2,1)}, bf16[3,320,1280]{2,1,0:T(8,128)(2,1)}, u32[]{:S(2)}, u32[]{:S(2)}) %collective-permute-start.9) | collective-permute-done | bytes 2457632 | tf_op jit(solution)/shard_map/ppermute | solution.py:1031
  126.0 6.4 %order.1.w_ref = bf16[1024,1280]{1,0:T(8,128)(2,1)} custom-call(s32[1]{0:T(128)} %bitcast.10.own_first, bf16[640,1024]{1,0:T(8,128)(2,1)} %pick.1.x_ref.a_ref, bf16[640,1024]{1,0:T(8,128)(2,1)} %collective-permute-done.7.x_ref.b_ref), custom_call_target="tpu_custom_call" | custom-call | flops 199999995904 | bytes 1000 | tf_op jit(solution)/shard_map/order/pallas_call | solution.py:408
  132.4 7.9 %transpose.15.x_ref = bf16[1280,2048]{1,0:T(8,128)(2,1)} custom-call(bf16[2048,1280]{1,0:T(8,128)(2,1)} %get-tuple-element.92.x_ref), custom_call_target="tpu_custom_call" | custom-call | flops 1000000 | bytes 1000 | tf_op jit(solution)/shard_map/transpose/pallas_call | solution.py:432
  143.7 21.5 %tail.1 = (bf16[512,1280]{1,0:T(8,128)(2,1)}, bf16[3,512,1280]{2,1,0:T(8,128)(2,1)}, bf16[3,512,1280]{2,1,0:T(8,128)(2,1)}, f32[512,1280]{1,0:T(8,128)}, bf16[51...) custom-call(s32[4]{0:T(128)S(1)} %pad_add_fusion.at, ...), custom_call_target="tpu_custom_call" | custom-call | flops 10000000 | bytes 1000 | tf_op jit(solution)/shard_map/tail/pallas_call | solution.py:650
  167.4 7.3 %share.2 = bf16[1280,1920]{1,0:T(8,128)(2,1)} custom-call(s32[1]{0:T(128)} %bitcast.21.col, bf16[3,512,1280]{2,1,0:T(8,128)(2,1)} %get-tuple-element.99.left, bf16[3,512,1280]{2,1,0:T(8,128)(2,1)} %get-tuple-element.100.right), custom_call_target="tpu_custom_call" | custom-call | flops 1000000 | bytes 1000 | tf_op jit(solution)/shard_map/share/pallas_call | solution.py:688
  177.7 7.1 %collective-permute-done.17.do3 = bf16[512,320]{1,0:T(8,128)(2,1)S(1)} collective-permute-done((bf16[512,320]{1,0:T(8,128)(2,1)}, bf16[512,320]{1,0:T(8,128)(2,1)S(1)}, u32[]{:S(2)}, u32[]{:S(2)}) %collective-permute-start.17) | collective-permute-done | bytes 327712 | tf_op jit(solution)/shard_map/ppermute | solution.py:1031
  186.6 8.9 %share.3 = bf16[1280,1920]{1,0:T(8,128)(2,1)} custom-call(s32[1]{0:T(128)} %bitcast.22.col, bf16[3,512,1280]{2,1,0:T(8,128)(2,1)} %get-tuple-element.99.left, bf16[3,512,1280]{2,1,0:T(8,128)(2,1)} %get-tuple-element.100.right, bf16[1280,1920]{1,0:T(8,128)(2,1)} %collective-permute-done.19.refs_0_), custom_call_target="tpu_custom_call" | custom-call | flops 1000000 | bytes 1000 | tf_op jit(solution)/shard_map/share/pallas_call | solution.py:688
  195.5 6.4 %all-to-all-start = ((bf16[8,160,1920]{2,1,0:T(8,128)(2,1)}), bf16[8,160,1920]{2,1,0:T(8,128)(2,1)}, u32[]{:S(2)}, u32[]{:S(2)}) async-start(bf16[8,160,1920]{2,1,0:T(8,128)(2,1)} %bitcast.78), calls=%async_computation | async-start | bytes 9830400 | tf_op jit(solution)/shard_map/all_to_all | solution.py:1200
  202.0 43.6 %attn_bwd.1 = (bf16[2048,1024]{1,0:T(8,128)(2,1)}, f32[8,128]{1,0:T(8,128)}) custom-call(s32[16]{0:T(128)S(1)} %copy-done.7, s32[1]{0:T(128)} %bitcast.mine.shard, bf16[2048,512]{1,0:T(8,128)(2,1)} %get-tuple-element.105.qa, bf16[2048,1024]{1,0:T(8,128)(2,1)} %get-tuple-element.84.kv.kk.vv, bf16[2048,1024]{1,0:T(8,128)(2,1)} %get-tuple-element.84.kv.kk.vv, ...), custom_call_target="tpu_custom_call" | custom-call | flops 299999985664 | bytes 1000 | tf_op jit(solution)/shard_map/attn_bwd/pallas_call | solution.py:314
  245.6 6.8 %back.2 = bf16[2,512,1280]{2,1,0:T(8,128)(2,1)} custom-call(s32[2]{0:T(128)S(1)} %pad_add_fusion.1.shards, bf16[2048,1024]{1,0:T(8,128)(2,1)} %get-tuple-element.114.g_ref, bf16[1024,1280]{1,0:T(8,128)(2,1)} %order.1.w_ref), custom_call_target="tpu_custom_call" | custom-call | flops 1000000 | bytes 1000 | tf_op jit(solution)/shard_map/back/pallas_call | solution.py:924
  252.5 11.6 %cross.1 = (bf16[320,1024]{1,0:T(8,128)(2,1)}, bf16[320,1024]{1,0:T(8,128)(2,1)}, bf16[320,1024]{1,0:T(8,128)(2,1)}, bf16[320,1024]{1,0:T(8,128)(2,1)}) custom-call(s32[2]{0:T(128)S(1)} %pad_add_fusion.2.at, bf16[1280,2048]{1,0:T(8,128)(2,1)} %transpose.15.x_ref, bf16[2048,1024]{1,0:T(8,128)(2,1)} %get-tuple-element.114.g_ref), custom_call_target="tpu_custom_call" | custom-call | flops 1000000 | bytes 1000 | tf_op jit(solution)/shard_map/cross/pallas_call | solution.py:842
  265.6 4.7 %back.3 = bf16[1,512,1280]{2,1,0:T(8,128)(2,1)} custom-call(s32[1]{0:T(128)} %bitcast.26.shards, bf16[2048,1024]{1,0:T(8,128)(2,1)} %get-tuple-element.114.g_ref, bf16[1024,1280]{1,0:T(8,128)(2,1)} %order.1.w_ref, bf16[2,512,1280]{2,1,0:T(8,128)(2,1)S(1)} %collective-permute-done.20.refs_0_.core), custom_call_target="tpu_custom_call" | custom-call | flops 1000000 | bytes 1000 | tf_op jit(solution)/shard_map/back/pallas_call | solution.py:924
  274.2 3.5 total.2.a_ref
  282.6 20.2 %collective-permute-done.23 = bf16[320,1024]{1,0:T(8,128)(2,1)} collective-permute-done((bf16[320,1024]{1,0:T(8,128)(2,1)}, bf16[320,1024]{1,0:T(8,128)(2,1)}, u32[]{:S(2)}, u32[]{:S(2)}) %collective-permute-start.23) | collective-permute-done | bytes 655392 | tf_op jit(solution)/shard_map/ppermute | solution.py:1031
  306.2 8.2 %collective-permute-done.25.b_ref = bf16[160,1920]{1,0:T(8,128)(2,1)} collective-permute-done((bf16[160,1920]{1,0:T(8,128)(2,1)}, bf16[160,1920]{1,0:T(8,128)(2,1)}, u32[]{:S(2)}, u32[]{:S(2)}) %collective-permute-start.25) | collective-permute-done | bytes 614432 | tf_op jit(solution)/shard_map/ppermute | solution.py:1031
  318.8 6.6 %finish.1 = (bf16[512,1280]{1,0:T(8,128)(2,1)}, f32[1,1280]{1,0:T(1,128)S(1)}) custom-call(s32[1]{0:T(128)} %bitcast.mine.shard, bf16[2048,1024]{1,0:T(8,128)(2,1)} %get-tuple-element.114.g_ref, bf16[1024,1280]{1,0:T(8,128)(2,1)} %order.1.w_ref, bf16[2,512,1280]{2,1,0:T(8,128)(2,1)S(1)} %collective-permute-done.20.refs_0_.core, ...), custom_call_target="tpu_custom_call" | custom-call | flops 1000000 | bytes 1000 | tf_op jit(solution)/shard_map/finish/pallas_call | solution.py:962
  325.4 17.9 %collective-permute-done.26.b_ref = bf16[320,1024]{1,0:T(8,128)(2,1)S(1)} collective-permute-done((bf16[320,1024]{1,0:T(8,128)(2,1)}, bf16[320,1024]{1,0:T(8,128)(2,1)S(1)}, u32[]{:S(2)}, u32[]{:S(2)}) %collective-permute-start.26) | collective-permute-done | bytes 655392 | tf_op jit(solution)/shard_map/ppermute | solution.py:1031
  349.9 15.8 %collective-permute-done.29.b_ref = bf16[320,1024]{1,0:T(8,128)(2,1)S(1)} collective-permute-done((bf16[320,1024]{1,0:T(8,128)(2,1)S(1)}, bf16[320,1024]{1,0:T(8,128)(2,1)S(1)}, u32[]{:S(2)}, u32[]{:S(2)}) %collective-permute-start.29) | collective-permute-done | bytes 655392 | tf_op jit(solution)/shard_map/ppermute | solution.py:1031
  370.8 8.3 %collective-permute-done.31.own_x = bf16[2,160,1920]{2,1,0:T(8,128)(2,1)} collective-permute-done((bf16[2,160,1920]{2,1,0:T(8,128)(2,1)}, bf16[2,160,1920]{2,1,0:T(8,128)(2,1)}, u32[]{:S(2)}, u32[]{:S(2)}) %collective-permute-start.31) | collective-permute-done | bytes 1228832 | tf_op jit(solution)/shard_map/ppermute | solution.py:1031
  382.4 6.6 %place_tail.1 = (f32[4,160,1280]{2,1,0:T(8,128)}, f32[4,160,1280]{2,1,0:T(8,128)}, f32[4,160,1280]{2,1,0:T(8,128)}) custom-call(s32[3]{0:T(128)S(1)} %pad_add_fusion.3.at, bf16[2,160,1920]{2,1,0:T(8,128)(2,1)S(1)} %copy-done.1, bf16[2,160,1920]{2,1,0:T(8,128)(2,1)} %collective-permute-done.31.own_x, bf16[2,160,1920]{2,1,0:T(8,128)(2,1)} %collective-permute-done.32.mate, ...), custom_call_target="tpu_custom_call" | custom-call | flops 1000000 | bytes 1000 | tf_op jit(solution)/shard_map/place_tail/pallas_call | solution.py:805
  393.9 3.8 collective-permute-done.36
  402.6 3.7 collective-permute-done.38
  408.9 4.4 %spread.2.refs_0_ = f32[2,320,3840]{2,1,0:T(8,128)} custom-call(s32[3]{0:T(128)S(1)} %pad_add_fusion.5.at, bf16[2,320,1024]{2,1,0:T(8,128)(2,1)S(1)} %copy-done, bf16[2,320,1024]{2,1,0:T(8,128)(2,1)} %collective-permute-done.30.mate), custom_call_target="tpu_custom_call" | custom-call | flops 1000000 | bytes 1000 | tf_op jit(solution)/shard_map/spread/pallas_call | solution.py:888
  (190 shorter events, 91.3 us)
Async XLA Ops:
  0.6 22.2 %collective-permute-start.1 = (bf16[512,1280]{1,0:T(8,128)(2,1)}, bf16[512,1280]{1,0:T(8,128)(2,1)}, u32[]{:S(2)}, u32[]{:S(2)}) collective-permute-start(bf16[512,1280]{1,0:T(8,128)(2,1)} %bitcast.67), channel_id=1, source_target_pairs={{2,0},{3,1},{4,2},{5,3},{6,4},{7,5},{8,10},{9,11},{10,12},{11,13},... | collective-permute-start | bytes 3932168 | tf_op jit(solution)/shard_map/ppermute | solution.py:1031
  1.9 52.1 %collective-permute-start.5 = (bf16[512,1280]{1,0:T(8,128)(2,1)}, bf16[512,1280]{1,0:T(8,128)(2,1)}, u32[]{:S(2)}, u32[]{:S(2)}) collective-permute-start(bf16[512,1280]{1,0:T(8,128)(2,1)} %bitcast.68), channel_id=1, source_target_pairs={{0,8},{1,9},{2,10},{3,11},{12,4},{13,5},{14,6},{15,7},{16,24},{17,... | collective-permute-start | bytes 3932168 | tf_op jit(solution)/shard_map/ppermute | solution.py:1031
  9.2 63.8 %collective-permute-start = (s32[1,2048]{1,0:T(1,128)}, s32[1,2048]{1,0:T(1,128)S(1)}, u32[]{:S(2)}, u32[]{:S(2)}) collective-permute-start(s32[1,2048]{1,0:T(1,128)} %param.11), channel_id=1, source_target_pairs={{0,8},{1,9},{2,10},{3,11},{4,12},{5,13},{6,14},{7,15},{8,0},{9,1},... | collective-permute-start | bytes 24584 | tf_op jit(solution)/shard_map/ppermute | solution.py:1031
  13.6 31.5 %collective-permute-start.7 = (bf16[640,1024]{1,0:T(8,128)(2,1)}, bf16[640,1024]{1,0:T(8,128)(2,1)}, u32[]{:S(2)}, u32[]{:S(2)}) collective-permute-start(bf16[640,1024]{1,0:T(8,128)(2,1)} %pick.1.x_ref.a_ref), channel_id=1, source_target_pairs={{0,1},{1,0},{2,3},{3,2},{4,5},{5,4},{6,7},{7,6},{8,9},{9,8},{10,11... | collective-permute-start | bytes 3932168 | tf_op jit(solution)/shard_map/ppermute | solution.py:1031
  22.9 26.3 %collective-permute-start.2 = (bf16[512,1280]{1,0:T(8,128)(2,1)}, bf16[512,1280]{1,0:T(8,128)(2,1)S(1)}, u32[]{:S(2)}, u32[]{:S(2)}) collective-permute-start(bf16[512,1280]{1,0:T(8,128)(2,1)} %collective-permute-done.1.refs_2_), channel_id=1, source_target_pairs={{2,0},{3,1},{4,2},{5,3},{10,12},{11,13},{12,14},{13,15},{18,16},{1... | collective-permute-start | bytes 3932168 | tf_op jit(solution)/shard_map/ppermute | solution.py:1031
  27.7 26.4 %collective-permute-start.6 = (bf16[512,1280]{1,0:T(8,128)(2,1)}, bf16[512,1280]{1,0:T(8,128)(2,1)}, u32[]{:S(2)}, u32[]{:S(2)}) collective-permute-start(bf16[512,1280]{1,0:T(8,128)(2,1)} %collective-permute-done.1.refs_2_), channel_id=1, source_target_pairs={{0,8},{1,9},{2,10},{3,11},{12,4},{13,5},{14,6},{15,7},{16,24},{17,... | collective-permute-start | bytes 3932168 | tf_op jit(solution)/shard_map/ppermute | solution.py:1031
  49.3 19.6 %collective-permute-start.4 = (bf16[512,1280]{1,0:T(8,128)(2,1)S(1)}, bf16[512,1280]{1,0:T(8,128)(2,1)}, u32[]{:S(2)}, u32[]{:S(2)}) collective-permute-start(bf16[512,1280]{1,0:T(8,128)(2,1)S(1)} %broadcast_select_fusion), channel_id=1, source_target_pairs={{0,2},{1,3},{2,0},{3,1},{12,14},{13,15},{14,12},{15,13},{16,18},{1... | collective-permute-start | bytes 3932168 | tf_op jit(solution)/shard_map/ppermute | solution.py:1031
  51.7 23.9 %collective-permute-start.3 = (bf16[512,1280]{1,0:T(8,128)(2,1)S(1)}, bf16[512,1280]{1,0:T(8,128)(2,1)}, u32[]{:S(2)}, u32[]{:S(2)}) collective-permute-start(bf16[512,1280]{1,0:T(8,128)(2,1)S(1)} %collective-permute-done.2.refs_0_), channel_id=1, source_target_pairs={{0,8},{1,9},{2,10},{3,11},{12,4},{13,5},{14,6},{15,7},{16,24},{17,... | collective-permute-start | bytes 3932168 | tf_op jit(solution)/shard_map/ppermute | solution.py:1031
  71.5 48.9 %collective-permute-start.9 = (bf16[3,320,1280]{2,1,0:T(8,128)(2,1)}, bf16[3,320,1280]{2,1,0:T(8,128)(2,1)}, u32[]{:S(2)}, u32[]{:S(2)}) collective-permute-start(bf16[3,320,1280]{2,1,0:T(8,128)(2,1)} %pad_maximum_fusion), channel_id=1, source_target_pairs={{0,1},{1,0},{2,3},{3,2},{4,5},{5,4},{6,7},{7,6},{8,9},{9,8},{10,11... | collective-permute-start | bytes 7372808 | tf_op jit(solution)/shard_map/ppermute | solution.py:1031
  75.1 45.3 %collective-permute-start.10 = (bf16[512,1280]{1,0:T(8,128)(2,1)}, bf16[512,1280]{1,0:T(8,128)(2,1)S(1)}, u32[]{:S(2)}, u32[]{:S(2)}) collective-permute-start(bf16[512,1280]{1,0:T(8,128)(2,1)} %bitcast.89), channel_id=1, source_target_pairs={{0,8},{1,9},{2,0},{3,1},{4,10},{5,11},{6,2},{7,3},{8,12},{9,13},{1... | collective-permute-start | bytes 3932168 | tf_op jit(solution)/shard_map/ppermute | solution.py:1031
  123.9 16.5 %collective-permute-start.11 = (bf16[512,320]{1,0:T(8,128)(2,1)}, bf16[512,320]{1,0:T(8,128)(2,1)}, u32[]{:S(2)}, u32[]{:S(2)}) collective-permute-start(bf16[512,320]{1,0:T(8,128)(2,1)} %get-tuple-element.151), channel_id=1, source_target_pairs={{0,8},{1,9},{2,10},{3,11},{4,12},{5,13},{6,14},{7,15},{8,0},{9,1},... | collective-permute-start | bytes 983048 | tf_op jit(solution)/shard_map/ppermute | solution.py:1031
  123.9 16.5 %collective-permute-start.12 = (bf16[512,320]{1,0:T(8,128)(2,1)}, bf16[512,320]{1,0:T(8,128)(2,1)}, u32[]{:S(2)}, u32[]{:S(2)}) collective-permute-start(bf16[512,320]{1,0:T(8,128)(2,1)} %get-tuple-element.150), channel_id=1, source_target_pairs={{0,2},{1,3},{2,0},{3,1},{4,6},{5,7},{6,4},{7,5},{8,10},{9,11},{10,... | collective-permute-start | bytes 983048 | tf_op jit(solution)/shard_map/ppermute | solution.py:1031
  124.3 19.4 %collective-permute-start.13 = (bf16[512,320]{1,0:T(8,128)(2,1)}, bf16[512,320]{1,0:T(8,128)(2,1)}, u32[]{:S(2)}, u32[]{:S(2)}) collective-permute-start(bf16[512,320]{1,0:T(8,128)(2,1)} %get-tuple-element.149), channel_id=1, source_target_pairs={{0,10},{1,11},{2,8},{3,9},{4,14},{5,15},{6,12},{7,13},{8,2},{9,3},... | collective-permute-start | bytes 983048 | tf_op jit(solution)/shard_map/ppermute | solution.py:1031
  125.7 18.0 %collective-permute-start.14 = (bf16[3,320,1280]{2,1,0:T(8,128)(2,1)}, bf16[3,320,1280]{2,1,0:T(8,128)(2,1)}, u32[]{:S(2)}, u32[]{:S(2)}) collective-permute-start(bf16[3,320,1280]{2,1,0:T(8,128)(2,1)} %collective-permute-done.9.half), channel_id=1, source_target_pairs={{0,8},{1,9},{2,10},{3,11},{4,12},{5,13},{6,14},{7,15},{8,0},{9,1},... | collective-permute-start | bytes 7372808 | tf_op jit(solution)/shard_map/ppermute | solution.py:1031
  165.6 12.2 %collective-permute-start.16 = (bf16[512,320]{1,0:T(8,128)(2,1)}, bf16[512,320]{1,0:T(8,128)(2,1)S(1)}, u32[]{:S(2)}, u32[]{:S(2)}) collective-permute-start(bf16[512,320]{1,0:T(8,128)(2,1)} %get-tuple-element.97), channel_id=1, source_target_pairs={{0,2},{1,3},{2,0},{3,1},{4,6},{5,7},{6,4},{7,5},{8,10},{9,11},{10,... | collective-permute-start | bytes 983048 | tf_op jit(solution)/shard_map/ppermute | solution.py:1031
  166.0 18.9 %collective-permute-start.17 = (bf16[512,320]{1,0:T(8,128)(2,1)}, bf16[512,320]{1,0:T(8,128)(2,1)S(1)}, u32[]{:S(2)}, u32[]{:S(2)}) collective-permute-start(bf16[512,320]{1,0:T(8,128)(2,1)} %get-tuple-element.102), channel_id=1, source_target_pairs={{0,10},{1,11},{2,8},{3,9},{4,14},{5,15},{6,12},{7,13},{8,2},{9,3},... | collective-permute-start | bytes 983048 | tf_op jit(solution)/shard_map/ppermute | solution.py:1031
  174.7 11.9 %collective-permute-start.19 = (bf16[1280,1920]{1,0:T(8,128)(2,1)}, bf16[1280,1920]{1,0:T(8,128)(2,1)}, u32[]{:S(2)}, u32[]{:S(2)}) collective-permute-start(bf16[1280,1920]{1,0:T(8,128)(2,1)} %share.2), channel_id=1, source_target_pairs={{0,8},{1,9},{2,10},{3,11},{4,12},{5,13},{6,14},{7,15},{8,0},{9,1},... | collective-permute-start | bytes 14745608 | tf_op jit(solution)/shard_map/ppermute | solution.py:1031
  184.8 60.8 %collective-permute-start.18 = (bf16[512,1280]{1,0:T(8,128)(2,1)}, bf16[512,1280]{1,0:T(8,128)(2,1)}, u32[]{:S(2)}, u32[]{:S(2)}) collective-permute-start(bf16[512,1280]{1,0:T(8,128)(2,1)} %get-tuple-element.104), channel_id=1, source_target_pairs={{0,2},{1,3},{2,6},{3,7},{4,10},{5,11},{6,14},{7,15},{8,0},{9,1},{1... | collective-permute-start | bytes 3932168 | tf_op jit(solution)/shard_map/ppermute | solution.py:1031
  195.5 78.6 %all-to-all-start = ((bf16[8,160,1920]{2,1,0:T(8,128)(2,1)}), bf16[8,160,1920]{2,1,0:T(8,128)(2,1)}, u32[]{:S(2)}, u32[]{:S(2)}) async-start(bf16[8,160,1920]{2,1,0:T(8,128)(2,1)} %bitcast.78), calls=%async_computation | async-start | bytes 9830400 | tf_op jit(solution)/shard_map/all_to_all | solution.py:1200
  252.4 13.2 %collective-permute-start.20 = (bf16[2,512,1280]{2,1,0:T(8,128)(2,1)}, bf16[2,512,1280]{2,1,0:T(8,128)(2,1)S(1)}, u32[]{:S(2)}, u32[]{:S(2)}) collective-permute-start(bf16[2,512,1280]{2,1,0:T(8,128)(2,1)} %back.2), channel_id=1, source_target_pairs={{0,8},{1,9},{2,10},{3,11},{4,12},{5,13},{6,14},{7,15},{8,0},{9,1},... | collective-permute-start | bytes 7864328 | tf_op jit(solution)/shard_map/ppermute | solution.py:1031
  264.0 18.6 %collective-permute-start.22 = (bf16[320,1024]{1,0:T(8,128)(2,1)}, bf16[320,1024]{1,0:T(8,128)(2,1)}, u32[]{:S(2)}, u32[]{:S(2)}) collective-permute-start(bf16[320,1024]{1,0:T(8,128)(2,1)} %get-tuple-element.120), channel_id=1, source_target_pairs={{0,16},{1,17},{2,18},{3,19},{4,20},{5,21},{6,22},{7,23},{8,24},{9,... | collective-permute-start | bytes 1966088 | tf_op jit(solution)/shard_map/ppermute | solution.py:1031
  270.3 48.5 %collective-permute-start.21 = (bf16[1,512,1280]{2,1,0:T(8,128)(2,1)}, bf16[1,512,1280]{2,1,0:T(8,128)(2,1)}, u32[]{:S(2)}, u32[]{:S(2)}) collective-permute-start(bf16[1,512,1280]{2,1,0:T(8,128)(2,1)} %back.3), channel_id=1, source_target_pairs={{0,2},{1,3},{2,0},{3,1},{4,6},{5,7},{6,4},{7,5},{8,10},{9,11},{10,... | collective-permute-start | bytes 3932168 | tf_op jit(solution)/shard_map/ppermute | solution.py:1031
  271.8 31.1 %collective-permute-start.23 = (bf16[320,1024]{1,0:T(8,128)(2,1)}, bf16[320,1024]{1,0:T(8,128)(2,1)}, u32[]{:S(2)}, u32[]{:S(2)}) collective-permute-start(bf16[320,1024]{1,0:T(8,128)(2,1)} %get-tuple-element.121), channel_id=1, source_target_pairs={{0,1},{1,0},{2,3},{3,2},{4,5},{5,4},{6,7},{7,6},{8,9},{9,8},{10,11... | collective-permute-start | bytes 1966088 | tf_op jit(solution)/shard_map/ppermute | solution.py:1031
  273.6 29.2 %collective-permute-start.24 = (bf16[320,1024]{1,0:T(8,128)(2,1)}, bf16[320,1024]{1,0:T(8,128)(2,1)}, u32[]{:S(2)}, u32[]{:S(2)}) collective-permute-start(bf16[320,1024]{1,0:T(8,128)(2,1)} %get-tuple-element.122), channel_id=1, source_target_pairs={{0,17},{1,16},{2,19},{3,18},{4,21},{5,20},{6,23},{7,22},{8,25},{9,... | collective-permute-start | bytes 1966088 | tf_op jit(solution)/shard_map/ppermute | solution.py:1031
  277.7 36.8 %collective-permute-start.25 = (bf16[160,1920]{1,0:T(8,128)(2,1)}, bf16[160,1920]{1,0:T(8,128)(2,1)}, u32[]{:S(2)}, u32[]{:S(2)}) collective-permute-start(bf16[160,1920]{1,0:T(8,128)(2,1)} %total.2.a_ref), channel_id=1, source_target_pairs={{0,4},{1,5},{2,6},{3,7},{4,0},{5,1},{6,2},{7,3},{8,12},{9,13},{10,... | collective-permute-start | bytes 1843208 | tf_op jit(solution)/shard_map/ppermute | solution.py:1031
  305.2 38.1 %collective-permute-start.26 = (bf16[320,1024]{1,0:T(8,128)(2,1)}, bf16[320,1024]{1,0:T(8,128)(2,1)S(1)}, u32[]{:S(2)}, u32[]{:S(2)}) collective-permute-start(bf16[320,1024]{1,0:T(8,128)(2,1)} %total.3.a_ref), channel_id=1, source_target_pairs={{0,4},{1,5},{2,6},{3,7},{4,0},{5,1},{6,2},{7,3},{8,12},{9,13},{10,... | collective-permute-start | bytes 1966088 | tf_op jit(solution)/shard_map/ppermute | solution.py:1031
  316.6 29.8 %collective-permute-start.27 = (bf16[160,1920]{1,0:T(8,128)(2,1)}, bf16[160,1920]{1,0:T(8,128)(2,1)}, u32[]{:S(2)}, u32[]{:S(2)}) collective-permute-start(bf16[160,1920]{1,0:T(8,128)(2,1)} %add.135.a_ref), channel_id=1, source_target_pairs={{0,2},{1,3},{2,0},{3,1},{4,6},{5,7},{6,4},{7,5},{8,10},{9,11},{10,... | collective-permute-start | bytes 1843208 | tf_op jit(solution)/shard_map/ppermute | solution.py:1031
  348.9 30.3 %collective-permute-start.31 = (bf16[2,160,1920]{2,1,0:T(8,128)(2,1)}, bf16[2,160,1920]{2,1,0:T(8,128)(2,1)}, u32[]{:S(2)}, u32[]{:S(2)}) collective-permute-start(bf16[2,160,1920]{2,1,0:T(8,128)(2,1)} %pair_up.2.own), channel_id=1, source_target_pairs={{0,16},{1,17},{2,18},{3,19},{4,20},{5,21},{6,22},{7,23},{8,24},{9,... | collective-permute-start | bytes 3686408 | tf_op jit(solution)/shard_map/ppermute | solution.py:1031
  349.2 16.4 %collective-permute-start.29 = (bf16[320,1024]{1,0:T(8,128)(2,1)S(1)}, bf16[320,1024]{1,0:T(8,128)(2,1)S(1)}, u32[]{:S(2)}, u32[]{:S(2)}) collective-permute-start(bf16[320,1024]{1,0:T(8,128)(2,1)S(1)} %copy-done.18), channel_id=1, source_target_pairs={{0,2},{1,3},{2,0},{3,1},{4,6},{5,7},{6,4},{7,5},{8,10},{9,11},{10,... | collective-permute-start | bytes 1966088 | tf_op jit(solution)/shard_map/ppermute | solution.py:1031
  368.9 20.1 %collective-permute-start.30 = (bf16[2,320,1024]{2,1,0:T(8,128)(2,1)}, bf16[2,320,1024]{2,1,0:T(8,128)(2,1)}, u32[]{:S(2)}, u32[]{:S(2)}) collective-permute-start(bf16[2,320,1024]{2,1,0:T(8,128)(2,1)} %pair_up.3.own), channel_id=1, source_target_pairs={{0,8},{1,9},{2,10},{3,11},{4,12},{5,13},{6,14},{7,15},{8,0},{9,1},... | collective-permute-start | bytes 3932168 | tf_op jit(solution)/shard_map/ppermute | solution.py:1031
  368.9 37.5 %collective-permute-start.28 = (bf16[512,1280]{1,0:T(8,128)(2,1)}, bf16[512,1280]{1,0:T(8,128)(2,1)}, u32[]{:S(2)}, u32[]{:S(2)}) collective-permute-start(bf16[512,1280]{1,0:T(8,128)(2,1)} %get-tuple-element.129), channel_id=1, source_target_pairs={{0,2},{1,3},{2,6},{3,7},{4,10},{5,11},{6,14},{7,15},{8,0},{9,1},{1... | collective-permute-start | bytes 3932168 | tf_op jit(solution)/shard_map/ppermute | solution.py:1031
  369.5 39.3 %collective-permute-start.39 = (bf16[2,320,1024]{2,1,0:T(8,128)(2,1)}, bf16[2,320,1024]{2,1,0:T(8,128)(2,1)S(1)}, u32[]{:S(2)}, u32[]{:S(2)}) collective-permute-start(bf16[2,320,1024]{2,1,0:T(8,128)(2,1)} %pair_up.3.own), channel_id=1, source_target_pairs={{0,16},{1,17},{2,18},{3,19},{4,20},{5,21},{6,22},{7,23},{8,24},{9,... | collective-permute-start | bytes 3932168 | tf_op jit(solution)/shard_map/ppermute | solution.py:1031
  (42 other events, 409.0 us)

commit v13 on v12

--- a/solution.py
+++ b/solution.py
@@ -674,14 +674,12 @@
 tn_dims = (((0,), (0,)), ((), ()))
 
 
-def share_kernel(col, left, right, *refs):
+def share_kernel(col, left, right, out):
     value = lax.dot_general(left[0], right[0], tn_dims, preferred_element_type=f32)
-    if len(refs) == 2:
-        value = value + refs[0][...].astype(f32)
-    refs[-1][...] = value.astype(bf16)
-
-
-def share(left, right, col, got=None):
+    out[...] = value.astype(bf16)
+
+
+def share(left, right, col):
     n, rows, d = left.shape
     w = d // 2
     block = pl.BlockSpec((d, w), lambda i, c: (0, i))
@@ -694,14 +692,13 @@
             in_specs=[
                 pl.BlockSpec((1, rows, d), lambda i, c: (i, 0, 0)),
                 pl.BlockSpec((1, rows, w), lambda i, c: (i, 0, c[0])),
-            ]
-            + [block] * (got is not None),
+            ],
             out_specs=block,
         ),
         compiler_params=pltpu.CompilerParams(vmem_limit_bytes=40 << 20),
         cost_estimate=CHEAP,
         name="share",
-    )(col.reshape(1), hbm(left), hbm(right), *(() if got is None else (hbm(got),)))
+    )(col.reshape(1), hbm(left), hbm(right))
 
 
 def copy(x):
@@ -761,6 +758,21 @@
     return pl.pallas_call(
         add_kernel, out_shape=pltpu.HBM(a.shape, bf16), cost_estimate=CHEAP, name="add"
     )(a, b)
+
+
+def add_rows(a, b):
+    rows, cols = a.shape
+    block = pl.BlockSpec((rows // 5, cols), lambda i: (i, 0))
+    return pl.pallas_call(
+        add_kernel,
+        out_shape=pltpu.HBM(a.shape, bf16),
+        grid=(5,),
+        in_specs=[block] * 2,
+        out_specs=block,
+        compiler_params=pltpu.CompilerParams(vmem_limit_bytes=24 << 20),
+        cost_estimate=CHEAP,
+        name="add_rows",
+    )(hbm(a), hbm(b))
 
 
 def pair_kernel(a_ref, b_ref, out):
@@ -1162,8 +1174,8 @@
 
         trades = (core_mate, near_mate, cross_mate)
         att_pieces = [rows_at(att, (mine ^ j) * rows, rows) for j in range(parts)]
+        half_mate = send(after(half_w, *att_pieces), core_mate)
         att_pieces = [att_pieces[0]] + [send(att_pieces[j + 1], trades[j]) for j in range(3)]
-        half_mate = send(half_w, core_mate)
         if pair:
             w_trans = order(after(picked, att), other_w, wt)
         else:
@@ -1193,10 +1205,11 @@
 
         shared = share(after(left, pieces[1]), right, 1 - gc)
         from_core = send(shared, core_mate)
-        pieces[2:] = [after(piece, shared) for piece in pieces[2:]]
+        own_half = share(left, right, after(gc, shared))
+        pieces[2:] = [after(piece, own_half) for piece in pieces[2:]]
         home_out = send(after(layer_out, *pieces[1:]), to_home)
         late_gain = tick(after(gain_attn.reshape(-1, LN), *pieces[1:]))
-        summed = share(left, right, gc, after(from_core, late_gain))
+        summed = add_rows(own_half, after(from_core, late_gain))
         kept = lax.all_to_all(summed, ("wt", "gx", "near"), 0, 0, tiled=True)
 
         scale_row = jnp.tile(dim_scale, nh // groups)[None]

time: 425 us -> 422 us (level)
  waiting for transfers between devices: 127 us -> 114 us
  Pallas kernels: 222 us -> 228 us
    ppermute x41, waiting for transfers between devices: 127 us -> 114 us  [send(): return lax.ppermute(value, AXES, pairs(target))]
    pallas_call x0 -> x1, Pallas kernels: none -> 7.76 us  [add_rows(): pl.pallas_call(add_kernel, out_shape=pltpu.HBM(a.shape, bf16), grid=(5,),...]
  transfers between devices with their start and end apart: 42 -> 42, of which waited for: 18 -> 17; matrix products, arithmetic and copies ran while one was open for 3% -> 3% of each run, Pallas kernels for 47% -> 48%
where the time goes in v13:
time: 422 us; the launch traced here: 415 us
  Pallas kernels  228 us (54%)
  waiting for transfers between devices  114 us (27%)
  starting transfers between devices  54.3 us (13%)
  local copies, waits for them, and re-layouts  10.9 us (3%)
  other arithmetic  5.93 us (1%)
    ppermute x41, waiting for transfers between devices, send(): return lax.ppermute(value, AXES, pairs(target))  114 us
    ppermute x41, starting transfers between devices, send(): return lax.ppermute(value, AXES, pairs(target))  45.2 us
    pallas_call x1, Pallas kernels, attn_bwd(): pl.pallas_call(functools.partial(bwd_kernel, first=group * nh, nh=nh, bq=...  43.5 us
    pallas_call x1, Pallas kernels, attn_fwd(): pl.pallas_call(functools.partial(fwd_kernel, nh=nh, bq=bq, bk=bk, nk=n //...  26 us
    pallas_call x2, Pallas kernels, project(): pl.pallas_call(functools.partial(project_kernel, count=count, halves=len(...  22.8 us
    pallas_call x1, Pallas kernels, tail(): pl.pallas_call(body, out_shape=[pltpu.HBM((rows, d), bf16)] + [pltpu.HBM(...  21.5 us
    pallas_call x2, Pallas kernels, share(): pl.pallas_call(share_kernel, out_shape=pltpu.HBM((d, n * w), bf16), grid_...  14.6 us
    pallas_call x1, Pallas kernels, cross(): pl.pallas_call(cross_kernel, out_shape=[pltpu.HBM((w // 2, cols), bf16)]...  11.6 us
  transfers between devices with their start and end apart: 42, of which 17 were waited for; matrix products, arithmetic and copies ran while one was open for 3% of the time, Pallas kernels for 48%

profile of v13, /device:TPU:0, one launch (start us, length us, event | category | flops | bytes accessed | tf_op | source)
XLA Modules:
  0.0 415.0 jit_solution(3280665199269827397)
XLA Ops:
  1.9 7.3 %collective-permute-start.5 = (bf16[512,1280]{1,0:T(8,128)(2,1)}, bf16[512,1280]{1,0:T(8,128)(2,1)}, u32[]{:S(2)}, u32[]{:S(2)}) collective-permute-start(bf16[512,1280]{1,0:T(8,128)(2,1)} %bitcast.69), channel_id=1, source_target_pairs={{0,8},{1,9},{2,10},{3,11},{12,4},{13,5},{14,6},{15,7},{16,24},{17,... | collective-permute-start | bytes 3932168 | tf_op jit(solution)/shard_map/ppermute | solution.py:1043
  9.2 4.4 %pick.1.x_ref.a_ref = bf16[640,1024]{1,0:T(8,128)(2,1)} custom-call(s32[1]{0:T(128)} %bitcast.mine.shard, bf16[640,3840]{1,0:T(8,128)(2,1)} %w_ref.1), custom_call_target="tpu_custom_call" | custom-call | flops 5000000000 | bytes 1000 | tf_op jit(solution)/shard_map/pick/pallas_call | solution.py:352
  15.7 4.2 %stretch.2.refs_5_ = bf16[640,1536]{1,0:T(8,128)(2,1)} custom-call(bf16[640,1024]{1,0:T(8,128)(2,1)} %pick.1.x_ref.a_ref), custom_call_target="tpu_custom_call" | custom-call | flops 2000000000 | bytes 1000 | tf_op jit(solution)/shard_map/stretch/pallas_call | solution.py:382
  30.7 12.2 %collective-permute-done.7.x_ref.b_ref = bf16[640,1024]{1,0:T(8,128)(2,1)} collective-permute-done((bf16[640,1024]{1,0:T(8,128)(2,1)}, bf16[640,1024]{1,0:T(8,128)(2,1)}, u32[]{:S(2)}, u32[]{:S(2)}) %collective-permute-start.7) | collective-permute-done | bytes 1310752 | tf_op jit(solution)/shard_map/ppermute | solution.py:1043
  42.9 4.0 stretch.3.refs_6_
  51.9 11.2 %project.2 = (bf16[2048,1280]{1,0:T(8,128)(2,1)}, bf16[2048,512]{1,0:T(8,128)(2,1)}, bf16[2048,1024]{1,0:T(8,128)(2,1)}, bf16[512,1280]{1,0:T(8,128)(2,1)}) custom-call(s32[5]{0:T(128)S(1)} %stack.103.info, bf16[512,1280]{1,0:T(8,128)(2,1)S(1)} %bitcast.70, bf16[512,1280]{1,0:T(8,128)(2,1)} %collective-permute-done.5.refs_1_, ...), custom_call_target="tpu_custom_call" | custom-call | flops 15000000512 | bytes 1000 | tf_op jit(solution)/shard_map/project/pallas_call | solution.py:518
  63.1 3.6 collective-permute-done.4.refs_2_
  73.4 11.6 %project.3 = (bf16[2048,1280]{1,0:T(8,128)(2,1)}, bf16[2048,512]{1,0:T(8,128)(2,1)}, bf16[2048,1024]{1,0:T(8,128)(2,1)}, bf16[512,1280]{1,0:T(8,128)(2,1)}) custom-call(s32[5]{0:T(128)S(1)} %stack.100.info, bf16[512,1280]{1,0:T(8,128)(2,1)S(1)} %collective-permute-done.2.refs_0_, ...), custom_call_target="tpu_custom_call", output_to_operand_aliasing={{0}: (11, {}), {1}: (12, {}), {2}: (13, {})} | custom-call | flops 15000000512 | bytes 1000 | tf_op jit(solution)/shard_map/project/pallas_call | solution.py:518
  85.0 26.0 %attn_fwd.1 = (bf16[2048,320]{1,0:T(8,128)(2,1)}, bf16[2048,512]{1,0:T(8,128)(2,1)}, bf16[2048,512]{1,0:T(8,128)(2,1)}) custom-call(s32[16]{0:T(128)S(1)} %reshape.183.flags, bf16[2048,512]{1,0:T(8,128)(2,1)} %get-tuple-element.85.q_ref, bf16[2048,1024]{1,0:T(8,128)(2,1)} %get-tuple-element.86.kv.kk.vv, s32[2048,1]{1,0:T(8,128)S(1)} %copy.29.segc, ...), custom_call_target="tpu_custom_call" | custom-call | flops 10000000 | bytes 1000 | tf_op jit(solution)/shard_map/attn_fwd/pallas_call | solution.py:172
  111.0 4.9 %collective-permute-done.9.half = bf16[3,320,1280]{2,1,0:T(8,128)(2,1)} collective-permute-done((bf16[3,320,1280]{2,1,0:T(8,128)(2,1)}, bf16[3,320,1280]{2,1,0:T(8,128)(2,1)}, u32[]{:S(2)}, u32[]{:S(2)}) %collective-permute-start.9) | collective-permute-done | bytes 2457632 | tf_op jit(solution)/shard_map/ppermute | solution.py:1043
  121.5 6.4 %order.1.w_ref = bf16[1024,1280]{1,0:T(8,128)(2,1)} custom-call(s32[1]{0:T(128)} %bitcast.10.own_first, bf16[640,1024]{1,0:T(8,128)(2,1)} %pick.1.x_ref.a_ref, bf16[640,1024]{1,0:T(8,128)(2,1)} %collective-permute-done.7.x_ref.b_ref), custom_call_target="tpu_custom_call" | custom-call | flops 199999995904 | bytes 1000 | tf_op jit(solution)/shard_map/order/pallas_call | solution.py:408
  127.9 7.9 %transpose.15.x_ref = bf16[1280,2048]{1,0:T(8,128)(2,1)} custom-call(bf16[2048,1280]{1,0:T(8,128)(2,1)} %get-tuple-element.94.x_ref), custom_call_target="tpu_custom_call" | custom-call | flops 1000000 | bytes 1000 | tf_op jit(solution)/shard_map/transpose/pallas_call | solution.py:432
  135.9 3.4 collective-permute-done.13.p3
  139.3 21.5 %tail.1 = (bf16[512,1280]{1,0:T(8,128)(2,1)}, bf16[3,512,1280]{2,1,0:T(8,128)(2,1)}, bf16[3,512,1280]{2,1,0:T(8,128)(2,1)}, f32[512,1280]{1,0:T(8,128)}, bf16[51...) custom-call(s32[4]{0:T(128)S(1)} %pad_add_fusion.at, ...), custom_call_target="tpu_custom_call" | custom-call | flops 10000000 | bytes 1000 | tf_op jit(solution)/shard_map/tail/pallas_call | solution.py:650
  163.2 7.4 %share.2 = bf16[1280,1920]{1,0:T(8,128)(2,1)} custom-call(s32[1]{0:T(128)} %bitcast.21.col, bf16[3,512,1280]{2,1,0:T(8,128)(2,1)} %get-tuple-element.102.left, bf16[3,512,1280]{2,1,0:T(8,128)(2,1)} %get-tuple-element.103.right), custom_call_target="tpu_custom_call" | custom-call | flops 1000000 | bytes 1000 | tf_op jit(solution)/shard_map/share/pallas_call | solution.py:686
  170.6 7.2 %share.3.a_ref = bf16[1280,1920]{1,0:T(8,128)(2,1)} custom-call(s32[1]{0:T(128)} %bitcast.22.col, bf16[3,512,1280]{2,1,0:T(8,128)(2,1)} %get-tuple-element.102.left, bf16[3,512,1280]{2,1,0:T(8,128)(2,1)} %get-tuple-element.103.right), custom_call_target="tpu_custom_call" | custom-call | flops 1000000 | bytes 1000 | tf_op jit(solution)/shard_map/share/pallas_call | solution.py:686
  177.8 3.3 collective-permute-done.16.do2
  182.8 7.8 %add_rows.1 = bf16[1280,1920]{1,0:T(8,128)(2,1)} custom-call(bf16[1280,1920]{1,0:T(8,128)(2,1)} %share.3.a_ref, bf16[1280,1920]{1,0:T(8,128)(2,1)} %collective-permute-done.19.b_ref), custom_call_target="tpu_custom_call" | custom-call | flops 1000000 | bytes 1000 | tf_op jit(solution)/shard_map/add_rows/pallas_call | solution.py:766
  190.6 9.1 %all-to-all-start = ((bf16[8,160,1920]{2,1,0:T(8,128)(2,1)}), bf16[8,160,1920]{2,1,0:T(8,128)(2,1)}, u32[]{:S(2)}, u32[]{:S(2)}) async-start(bf16[8,160,1920]{2,1,0:T(8,128)(2,1)} %bitcast.79), calls=%async_computation | async-start | bytes 9830400 | tf_op jit(solution)/shard_map/all_to_all | solution.py:1213
  199.7 43.5 %attn_bwd.1 = (bf16[2048,1024]{1,0:T(8,128)(2,1)}, f32[8,128]{1,0:T(8,128)}) custom-call(s32[16]{0:T(128)S(1)} %copy-done.7, s32[1]{0:T(128)} %bitcast.mine.shard, bf16[2048,512]{1,0:T(8,128)(2,1)} %get-tuple-element.109.qa, bf16[2048,1024]{1,0:T(8,128)(2,1)} %get-tuple-element.86.kv.kk.vv, bf16[2048,1024]{1,0:T(8,128)(2,1)} %get-tuple-element.86.kv.kk.vv, ...), custom_call_target="tpu_custom_call" | custom-call | flops 299999985664 | bytes 1000 | tf_op jit(solution)/shard_map/attn_bwd/pallas_call | solution.py:314
  243.3 6.8 %back.2 = bf16[2,512,1280]{2,1,0:T(8,128)(2,1)} custom-call(s32[2]{0:T(128)S(1)} %pad_add_fusion.1.shards, bf16[2048,1024]{1,0:T(8,128)(2,1)} %get-tuple-element.118.g_ref, bf16[1024,1280]{1,0:T(8,128)(2,1)} %order.1.w_ref), custom_call_target="tpu_custom_call" | custom-call | flops 1000000 | bytes 1000 | tf_op jit(solution)/shard_map/back/pallas_call | solution.py:936
  250.1 11.6 %cross.1 = (bf16[320,1024]{1,0:T(8,128)(2,1)}, bf16[320,1024]{1,0:T(8,128)(2,1)}, bf16[320,1024]{1,0:T(8,128)(2,1)}, bf16[320,1024]{1,0:T(8,128)(2,1)}) custom-call(s32[2]{0:T(128)S(1)} %pad_add_fusion.2.at, bf16[1280,2048]{1,0:T(8,128)(2,1)} %transpose.15.x_ref, bf16[2048,1024]{1,0:T(8,128)(2,1)} %get-tuple-element.118.g_ref), custom_call_target="tpu_custom_call" | custom-call | flops 1000000 | bytes 1000 | tf_op jit(solution)/shard_map/cross/pallas_call | solution.py:854
  263.7 4.7 %back.3 = bf16[1,512,1280]{2,1,0:T(8,128)(2,1)} custom-call(s32[1]{0:T(128)} %bitcast.26.shards, bf16[2048,1024]{1,0:T(8,128)(2,1)} %get-tuple-element.118.g_ref, bf16[1024,1280]{1,0:T(8,128)(2,1)} %order.1.w_ref, bf16[2,512,1280]{2,1,0:T(8,128)(2,1)S(1)} %collective-permute-done.20.refs_0_.core), custom_call_target="tpu_custom_call" | custom-call | flops 1000000 | bytes 1000 | tf_op jit(solution)/shard_map/back/pallas_call | solution.py:936
  271.9 3.5 total.2.a_ref
  280.1 20.7 %collective-permute-done.23 = bf16[320,1024]{1,0:T(8,128)(2,1)} collective-permute-done((bf16[320,1024]{1,0:T(8,128)(2,1)}, bf16[320,1024]{1,0:T(8,128)(2,1)}, u32[]{:S(2)}, u32[]{:S(2)}) %collective-permute-start.23) | collective-permute-done | bytes 655392 | tf_op jit(solution)/shard_map/ppermute | solution.py:1043
  303.2 9.3 %collective-permute-done.25.b_ref = bf16[160,1920]{1,0:T(8,128)(2,1)} collective-permute-done((bf16[160,1920]{1,0:T(8,128)(2,1)}, bf16[160,1920]{1,0:T(8,128)(2,1)}, u32[]{:S(2)}, u32[]{:S(2)}) %collective-permute-start.25) | collective-permute-done | bytes 614432 | tf_op jit(solution)/shard_map/ppermute | solution.py:1043
  315.9 6.6 %finish.1 = (bf16[512,1280]{1,0:T(8,128)(2,1)}, f32[1,1280]{1,0:T(1,128)S(1)}) custom-call(s32[1]{0:T(128)} %bitcast.mine.shard, bf16[2048,1024]{1,0:T(8,128)(2,1)} %get-tuple-element.118.g_ref, bf16[1024,1280]{1,0:T(8,128)(2,1)} %order.1.w_ref, bf16[2,512,1280]{2,1,0:T(8,128)(2,1)S(1)} %collective-permute-done.20.refs_0_.core, ...), custom_call_target="tpu_custom_call" | custom-call | flops 1000000 | bytes 1000 | tf_op jit(solution)/shard_map/finish/pallas_call | solution.py:974
  322.4 17.9 %collective-permute-done.26.b_ref = bf16[320,1024]{1,0:T(8,128)(2,1)S(1)} collective-permute-done((bf16[320,1024]{1,0:T(8,128)(2,1)}, bf16[320,1024]{1,0:T(8,128)(2,1)S(1)}, u32[]{:S(2)}, u32[]{:S(2)}) %collective-permute-start.26) | collective-permute-done | bytes 655392 | tf_op jit(solution)/shard_map/ppermute | solution.py:1043
  347.5 15.1 %collective-permute-done.29.b_ref = bf16[320,1024]{1,0:T(8,128)(2,1)S(1)} collective-permute-done((bf16[320,1024]{1,0:T(8,128)(2,1)S(1)}, bf16[320,1024]{1,0:T(8,128)(2,1)S(1)}, u32[]{:S(2)}, u32[]{:S(2)}) %collective-permute-start.29) | collective-permute-done | bytes 655392 | tf_op jit(solution)/shard_map/ppermute | solution.py:1043
  368.6 7.5 %collective-permute-done.31.own_x = bf16[2,160,1920]{2,1,0:T(8,128)(2,1)} collective-permute-done((bf16[2,160,1920]{2,1,0:T(8,128)(2,1)}, bf16[2,160,1920]{2,1,0:T(8,128)(2,1)}, u32[]{:S(2)}, u32[]{:S(2)}) %collective-permute-start.31) | collective-permute-done | bytes 1228832 | tf_op jit(solution)/shard_map/ppermute | solution.py:1043
  379.4 6.6 %place_tail.1 = (f32[4,160,1280]{2,1,0:T(8,128)}, f32[4,160,1280]{2,1,0:T(8,128)}, f32[4,160,1280]{2,1,0:T(8,128)}) custom-call(s32[3]{0:T(128)S(1)} %pad_add_fusion.3.at, bf16[2,160,1920]{2,1,0:T(8,128)(2,1)S(1)} %copy-done.1, bf16[2,160,1920]{2,1,0:T(8,128)(2,1)} %collective-permute-done.31.own_x, bf16[2,160,1920]{2,1,0:T(8,128)(2,1)} %collective-permute-done.32.mate, ...), custom_call_target="tpu_custom_call" | custom-call | flops 1000000 | bytes 1000 | tf_op jit(solution)/shard_map/place_tail/pallas_call | solution.py:817
  405.9 4.4 %spread.2.refs_0_ = f32[2,320,3840]{2,1,0:T(8,128)} custom-call(s32[3]{0:T(128)S(1)} %pad_add_fusion.5.at, bf16[2,320,1024]{2,1,0:T(8,128)(2,1)S(1)} %copy-done, bf16[2,320,1024]{2,1,0:T(8,128)(2,1)} %collective-permute-done.30.mate), custom_call_target="tpu_custom_call" | custom-call | flops 1000000 | bytes 1000 | tf_op jit(solution)/shard_map/spread/pallas_call | solution.py:900
  (191 shorter events, 92.1 us)
Async XLA Ops:
  0.6 22.2 %collective-permute-start.1 = (bf16[512,1280]{1,0:T(8,128)(2,1)}, bf16[512,1280]{1,0:T(8,128)(2,1)}, u32[]{:S(2)}, u32[]{:S(2)}) collective-permute-start(bf16[512,1280]{1,0:T(8,128)(2,1)} %bitcast.68), channel_id=1, source_target_pairs={{2,0},{3,1},{4,2},{5,3},{6,4},{7,5},{8,10},{9,11},{10,12},{11,13},... | collective-permute-start | bytes 3932168 | tf_op jit(solution)/shard_map/ppermute | solution.py:1043
  1.9 50.0 %collective-permute-start.5 = (bf16[512,1280]{1,0:T(8,128)(2,1)}, bf16[512,1280]{1,0:T(8,128)(2,1)}, u32[]{:S(2)}, u32[]{:S(2)}) collective-permute-start(bf16[512,1280]{1,0:T(8,128)(2,1)} %bitcast.69), channel_id=1, source_target_pairs={{0,8},{1,9},{2,10},{3,11},{12,4},{13,5},{14,6},{15,7},{16,24},{17,... | collective-permute-start | bytes 3932168 | tf_op jit(solution)/shard_map/ppermute | solution.py:1043
  13.7 29.3 %collective-permute-start.7 = (bf16[640,1024]{1,0:T(8,128)(2,1)}, bf16[640,1024]{1,0:T(8,128)(2,1)}, u32[]{:S(2)}, u32[]{:S(2)}) collective-permute-start(bf16[640,1024]{1,0:T(8,128)(2,1)} %pick.1.x_ref.a_ref), channel_id=1, source_target_pairs={{0,1},{1,0},{2,3},{3,2},{4,5},{5,4},{6,7},{7,6},{8,9},{9,8},{10,11... | collective-permute-start | bytes 3932168 | tf_op jit(solution)/shard_map/ppermute | solution.py:1043
  15.2 55.6 %collective-permute-start = (s32[1,2048]{1,0:T(1,128)S(1)}, s32[1,2048]{1,0:T(1,128)S(1)}, u32[]{:S(2)}, u32[]{:S(2)}) collective-permute-start(s32[1,2048]{1,0:T(1,128)S(1)} %copy-done.25), channel_id=1, source_target_pairs={{0,8},{1,9},{2,10},{3,11},{4,12},{5,13},{6,14},{7,15},{8,0},{9,1},... | collective-permute-start | bytes 24584 | tf_op jit(solution)/shard_map/ppermute | solution.py:1043
  22.9 24.1 %collective-permute-start.2 = (bf16[512,1280]{1,0:T(8,128)(2,1)}, bf16[512,1280]{1,0:T(8,128)(2,1)S(1)}, u32[]{:S(2)}, u32[]{:S(2)}) collective-permute-start(bf16[512,1280]{1,0:T(8,128)(2,1)} %collective-permute-done.1.refs_2_), channel_id=1, source_target_pairs={{2,0},{3,1},{4,2},{5,3},{10,12},{11,13},{12,14},{13,15},{18,16},{1... | collective-permute-start | bytes 3932168 | tf_op jit(solution)/shard_map/ppermute | solution.py:1043
  27.7 24.2 %collective-permute-start.6 = (bf16[512,1280]{1,0:T(8,128)(2,1)}, bf16[512,1280]{1,0:T(8,128)(2,1)}, u32[]{:S(2)}, u32[]{:S(2)}) collective-permute-start(bf16[512,1280]{1,0:T(8,128)(2,1)} %collective-permute-done.1.refs_2_), channel_id=1, source_target_pairs={{0,8},{1,9},{2,10},{3,11},{12,4},{13,5},{14,6},{15,7},{16,24},{17,... | collective-permute-start | bytes 3932168 | tf_op jit(solution)/shard_map/ppermute | solution.py:1043
  47.1 19.6 %collective-permute-start.4 = (bf16[512,1280]{1,0:T(8,128)(2,1)S(1)}, bf16[512,1280]{1,0:T(8,128)(2,1)}, u32[]{:S(2)}, u32[]{:S(2)}) collective-permute-start(bf16[512,1280]{1,0:T(8,128)(2,1)S(1)} %broadcast_select_fusion), channel_id=1, source_target_pairs={{0,2},{1,3},{2,0},{3,1},{12,14},{13,15},{14,12},{15,13},{16,18},{1... | collective-permute-start | bytes 3932168 | tf_op jit(solution)/shard_map/ppermute | solution.py:1043
  49.5 23.9 %collective-permute-start.3 = (bf16[512,1280]{1,0:T(8,128)(2,1)S(1)}, bf16[512,1280]{1,0:T(8,128)(2,1)}, u32[]{:S(2)}, u32[]{:S(2)}) collective-permute-start(bf16[512,1280]{1,0:T(8,128)(2,1)S(1)} %collective-permute-done.2.refs_0_), channel_id=1, source_target_pairs={{0,8},{1,9},{2,10},{3,11},{12,4},{13,5},{14,6},{15,7},{16,24},{17,... | collective-permute-start | bytes 3932168 | tf_op jit(solution)/shard_map/ppermute | solution.py:1043
  69.2 46.6 %collective-permute-start.9 = (bf16[3,320,1280]{2,1,0:T(8,128)(2,1)}, bf16[3,320,1280]{2,1,0:T(8,128)(2,1)}, u32[]{:S(2)}, u32[]{:S(2)}) collective-permute-start(bf16[3,320,1280]{2,1,0:T(8,128)(2,1)} %pad_maximum_fusion), channel_id=1, source_target_pairs={{0,1},{1,0},{2,3},{3,2},{4,5},{5,4},{6,7},{7,6},{8,9},{9,8},{10,11... | collective-permute-start | bytes 7372808 | tf_op jit(solution)/shard_map/ppermute | solution.py:1043
  72.8 43.0 %collective-permute-start.10 = (bf16[512,1280]{1,0:T(8,128)(2,1)}, bf16[512,1280]{1,0:T(8,128)(2,1)S(1)}, u32[]{:S(2)}, u32[]{:S(2)}) collective-permute-start(bf16[512,1280]{1,0:T(8,128)(2,1)} %bitcast.90), channel_id=1, source_target_pairs={{0,8},{1,9},{2,0},{3,1},{4,10},{5,11},{6,2},{7,3},{8,12},{9,13},{1... | collective-permute-start | bytes 3932168 | tf_op jit(solution)/shard_map/ppermute | solution.py:1043
  119.4 16.5 %collective-permute-start.11 = (bf16[512,320]{1,0:T(8,128)(2,1)}, bf16[512,320]{1,0:T(8,128)(2,1)}, u32[]{:S(2)}, u32[]{:S(2)}) collective-permute-start(bf16[512,320]{1,0:T(8,128)(2,1)} %get-tuple-element.155), channel_id=1, source_target_pairs={{0,8},{1,9},{2,10},{3,11},{4,12},{5,13},{6,14},{7,15},{8,0},{9,1},... | collective-permute-start | bytes 983048 | tf_op jit(solution)/shard_map/ppermute | solution.py:1043
  119.4 16.5 %collective-permute-start.12 = (bf16[512,320]{1,0:T(8,128)(2,1)}, bf16[512,320]{1,0:T(8,128)(2,1)}, u32[]{:S(2)}, u32[]{:S(2)}) collective-permute-start(bf16[512,320]{1,0:T(8,128)(2,1)} %get-tuple-element.154), channel_id=1, source_target_pairs={{0,2},{1,3},{2,0},{3,1},{4,6},{5,7},{6,4},{7,5},{8,10},{9,11},{10,... | collective-permute-start | bytes 983048 | tf_op jit(solution)/shard_map/ppermute | solution.py:1043
  119.8 19.5 %collective-permute-start.13 = (bf16[512,320]{1,0:T(8,128)(2,1)}, bf16[512,320]{1,0:T(8,128)(2,1)}, u32[]{:S(2)}, u32[]{:S(2)}) collective-permute-start(bf16[512,320]{1,0:T(8,128)(2,1)} %get-tuple-element.153), channel_id=1, source_target_pairs={{0,10},{1,11},{2,8},{3,9},{4,14},{5,15},{6,12},{7,13},{8,2},{9,3},... | collective-permute-start | bytes 983048 | tf_op jit(solution)/shard_map/ppermute | solution.py:1043
  121.3 18.0 %collective-permute-start.14 = (bf16[3,320,1280]{2,1,0:T(8,128)(2,1)}, bf16[3,320,1280]{2,1,0:T(8,128)(2,1)}, u32[]{:S(2)}, u32[]{:S(2)}) collective-permute-start(bf16[3,320,1280]{2,1,0:T(8,128)(2,1)} %collective-permute-done.9.half), channel_id=1, source_target_pairs={{0,8},{1,9},{2,10},{3,11},{4,12},{5,13},{6,14},{7,15},{8,0},{9,1},... | collective-permute-start | bytes 7372808 | tf_op jit(solution)/shard_map/ppermute | solution.py:1043
  161.1 16.7 %collective-permute-start.17 = (bf16[512,320]{1,0:T(8,128)(2,1)}, bf16[512,320]{1,0:T(8,128)(2,1)S(1)}, u32[]{:S(2)}, u32[]{:S(2)}) collective-permute-start(bf16[512,320]{1,0:T(8,128)(2,1)} %get-tuple-element.106), channel_id=1, source_target_pairs={{0,10},{1,11},{2,8},{3,9},{4,14},{5,15},{6,12},{7,13},{8,2},{9,3},... | collective-permute-start | bytes 983048 | tf_op jit(solution)/shard_map/ppermute | solution.py:1043
  161.4 19.8 %collective-permute-start.16 = (bf16[512,320]{1,0:T(8,128)(2,1)}, bf16[512,320]{1,0:T(8,128)(2,1)S(1)}, u32[]{:S(2)}, u32[]{:S(2)}) collective-permute-start(bf16[512,320]{1,0:T(8,128)(2,1)} %get-tuple-element.100), channel_id=1, source_target_pairs={{0,2},{1,3},{2,0},{3,1},{4,6},{5,7},{6,4},{7,5},{8,10},{9,11},{10,... | collective-permute-start | bytes 983048 | tf_op jit(solution)/shard_map/ppermute | solution.py:1043
  170.6 12.2 %collective-permute-start.19 = (bf16[1280,1920]{1,0:T(8,128)(2,1)}, bf16[1280,1920]{1,0:T(8,128)(2,1)}, u32[]{:S(2)}, u32[]{:S(2)}) collective-permute-start(bf16[1280,1920]{1,0:T(8,128)(2,1)} %share.2), channel_id=1, source_target_pairs={{0,8},{1,9},{2,10},{3,11},{4,12},{5,13},{6,14},{7,15},{8,0},{9,1},... | collective-permute-start | bytes 14745608 | tf_op jit(solution)/shard_map/ppermute | solution.py:1043
  182.4 60.8 %collective-permute-start.18 = (bf16[512,1280]{1,0:T(8,128)(2,1)}, bf16[512,1280]{1,0:T(8,128)(2,1)}, u32[]{:S(2)}, u32[]{:S(2)}) collective-permute-start(bf16[512,1280]{1,0:T(8,128)(2,1)} %get-tuple-element.108), channel_id=1, source_target_pairs={{0,2},{1,3},{2,6},{3,7},{4,10},{5,11},{6,14},{7,15},{8,0},{9,1},{1... | collective-permute-start | bytes 3932168 | tf_op jit(solution)/shard_map/ppermute | solution.py:1043
  190.6 81.2 %all-to-all-start = ((bf16[8,160,1920]{2,1,0:T(8,128)(2,1)}), bf16[8,160,1920]{2,1,0:T(8,128)(2,1)}, u32[]{:S(2)}, u32[]{:S(2)}) async-start(bf16[8,160,1920]{2,1,0:T(8,128)(2,1)} %bitcast.79), calls=%async_computation | async-start | bytes 9830400 | tf_op jit(solution)/shard_map/all_to_all | solution.py:1213
  250.1 13.7 %collective-permute-start.20 = (bf16[2,512,1280]{2,1,0:T(8,128)(2,1)}, bf16[2,512,1280]{2,1,0:T(8,128)(2,1)S(1)}, u32[]{:S(2)}, u32[]{:S(2)}) collective-permute-start(bf16[2,512,1280]{2,1,0:T(8,128)(2,1)} %back.2), channel_id=1, source_target_pairs={{0,8},{1,9},{2,10},{3,11},{4,12},{5,13},{6,14},{7,15},{8,0},{9,1},... | collective-permute-start | bytes 7864328 | tf_op jit(solution)/shard_map/ppermute | solution.py:1043
  261.7 18.4 %collective-permute-start.22 = (bf16[320,1024]{1,0:T(8,128)(2,1)}, bf16[320,1024]{1,0:T(8,128)(2,1)}, u32[]{:S(2)}, u32[]{:S(2)}) collective-permute-start(bf16[320,1024]{1,0:T(8,128)(2,1)} %get-tuple-element.124), channel_id=1, source_target_pairs={{0,16},{1,17},{2,18},{3,19},{4,20},{5,21},{6,22},{7,23},{8,24},{9,... | collective-permute-start | bytes 1966088 | tf_op jit(solution)/shard_map/ppermute | solution.py:1043
  268.4 47.5 %collective-permute-start.21 = (bf16[1,512,1280]{2,1,0:T(8,128)(2,1)}, bf16[1,512,1280]{2,1,0:T(8,128)(2,1)}, u32[]{:S(2)}, u32[]{:S(2)}) collective-permute-start(bf16[1,512,1280]{2,1,0:T(8,128)(2,1)} %back.3), channel_id=1, source_target_pairs={{0,2},{1,3},{2,0},{3,1},{4,6},{5,7},{6,4},{7,5},{8,10},{9,11},{10,... | collective-permute-start | bytes 3932168 | tf_op jit(solution)/shard_map/ppermute | solution.py:1043
  269.8 30.9 %collective-permute-start.23 = (bf16[320,1024]{1,0:T(8,128)(2,1)}, bf16[320,1024]{1,0:T(8,128)(2,1)}, u32[]{:S(2)}, u32[]{:S(2)}) collective-permute-start(bf16[320,1024]{1,0:T(8,128)(2,1)} %get-tuple-element.125), channel_id=1, source_target_pairs={{0,1},{1,0},{2,3},{3,2},{4,5},{5,4},{6,7},{7,6},{8,9},{9,8},{10,11... | collective-permute-start | bytes 1966088 | tf_op jit(solution)/shard_map/ppermute | solution.py:1043
  271.3 29.5 %collective-permute-start.24 = (bf16[320,1024]{1,0:T(8,128)(2,1)}, bf16[320,1024]{1,0:T(8,128)(2,1)}, u32[]{:S(2)}, u32[]{:S(2)}) collective-permute-start(bf16[320,1024]{1,0:T(8,128)(2,1)} %get-tuple-element.126), channel_id=1, source_target_pairs={{0,17},{1,16},{2,19},{3,18},{4,21},{5,20},{6,23},{7,22},{8,25},{9,... | collective-permute-start | bytes 1966088 | tf_op jit(solution)/shard_map/ppermute | solution.py:1043
  275.3 37.2 %collective-permute-start.25 = (bf16[160,1920]{1,0:T(8,128)(2,1)}, bf16[160,1920]{1,0:T(8,128)(2,1)}, u32[]{:S(2)}, u32[]{:S(2)}) collective-permute-start(bf16[160,1920]{1,0:T(8,128)(2,1)} %total.2.a_ref), channel_id=1, source_target_pairs={{0,4},{1,5},{2,6},{3,7},{4,0},{5,1},{6,2},{7,3},{8,12},{9,13},{10,... | collective-permute-start | bytes 1843208 | tf_op jit(solution)/shard_map/ppermute | solution.py:1043
  303.1 37.2 %collective-permute-start.26 = (bf16[320,1024]{1,0:T(8,128)(2,1)}, bf16[320,1024]{1,0:T(8,128)(2,1)S(1)}, u32[]{:S(2)}, u32[]{:S(2)}) collective-permute-start(bf16[320,1024]{1,0:T(8,128)(2,1)} %total.3.a_ref), channel_id=1, source_target_pairs={{0,4},{1,5},{2,6},{3,7},{4,0},{5,1},{6,2},{7,3},{8,12},{9,13},{10,... | collective-permute-start | bytes 1966088 | tf_op jit(solution)/shard_map/ppermute | solution.py:1043
  314.7 28.7 %collective-permute-start.27 = (bf16[160,1920]{1,0:T(8,128)(2,1)}, bf16[160,1920]{1,0:T(8,128)(2,1)}, u32[]{:S(2)}, u32[]{:S(2)}) collective-permute-start(bf16[160,1920]{1,0:T(8,128)(2,1)} %add.135.a_ref), channel_id=1, source_target_pairs={{0,2},{1,3},{2,0},{3,1},{4,6},{5,7},{6,4},{7,5},{8,10},{9,11},{10,... | collective-permute-start | bytes 1843208 | tf_op jit(solution)/shard_map/ppermute | solution.py:1043
  345.9 30.3 %collective-permute-start.31 = (bf16[2,160,1920]{2,1,0:T(8,128)(2,1)}, bf16[2,160,1920]{2,1,0:T(8,128)(2,1)}, u32[]{:S(2)}, u32[]{:S(2)}) collective-permute-start(bf16[2,160,1920]{2,1,0:T(8,128)(2,1)} %pair_up.2.own), channel_id=1, source_target_pairs={{0,16},{1,17},{2,18},{3,19},{4,20},{5,21},{6,22},{7,23},{8,24},{9,... | collective-permute-start | bytes 3686408 | tf_op jit(solution)/shard_map/ppermute | solution.py:1043
  346.5 16.1 %collective-permute-start.29 = (bf16[320,1024]{1,0:T(8,128)(2,1)S(1)}, bf16[320,1024]{1,0:T(8,128)(2,1)S(1)}, u32[]{:S(2)}, u32[]{:S(2)}) collective-permute-start(bf16[320,1024]{1,0:T(8,128)(2,1)S(1)} %copy-done.18), channel_id=1, source_target_pairs={{0,2},{1,3},{2,0},{3,1},{4,6},{5,7},{6,4},{7,5},{8,10},{9,11},{10,... | collective-permute-start | bytes 1966088 | tf_op jit(solution)/shard_map/ppermute | solution.py:1043
  365.9 20.1 %collective-permute-start.30 = (bf16[2,320,1024]{2,1,0:T(8,128)(2,1)}, bf16[2,320,1024]{2,1,0:T(8,128)(2,1)}, u32[]{:S(2)}, u32[]{:S(2)}) collective-permute-start(bf16[2,320,1024]{2,1,0:T(8,128)(2,1)} %pair_up.3.own), channel_id=1, source_target_pairs={{0,8},{1,9},{2,10},{3,11},{4,12},{5,13},{6,14},{7,15},{8,0},{9,1},... | collective-permute-start | bytes 3932168 | tf_op jit(solution)/shard_map/ppermute | solution.py:1043
  365.9 37.5 %collective-permute-start.28 = (bf16[512,1280]{1,0:T(8,128)(2,1)}, bf16[512,1280]{1,0:T(8,128)(2,1)}, u32[]{:S(2)}, u32[]{:S(2)}) collective-permute-start(bf16[512,1280]{1,0:T(8,128)(2,1)} %get-tuple-element.133), channel_id=1, source_target_pairs={{0,2},{1,3},{2,6},{3,7},{4,10},{5,11},{6,14},{7,15},{8,0},{9,1},{1... | collective-permute-start | bytes 3932168 | tf_op jit(solution)/shard_map/ppermute | solution.py:1043
  367.2 38.7 %collective-permute-start.39 = (bf16[2,320,1024]{2,1,0:T(8,128)(2,1)}, bf16[2,320,1024]{2,1,0:T(8,128)(2,1)S(1)}, u32[]{:S(2)}, u32[]{:S(2)}) collective-permute-start(bf16[2,320,1024]{2,1,0:T(8,128)(2,1)} %pair_up.3.own), channel_id=1, source_target_pairs={{0,16},{1,17},{2,18},{3,19},{4,20},{5,21},{6,22},{7,23},{8,24},{9,... | collective-permute-start | bytes 3932168 | tf_op jit(solution)/shard_map/ppermute | solution.py:1043
  (42 other events, 407.9 us)

commit v14 on v13

--- a/solution.py
+++ b/solution.py
@@ -775,17 +775,6 @@
     )(hbm(a), hbm(b))
 
 
-def pair_kernel(a_ref, b_ref, out):
-    out[0] = a_ref[...]
-    out[1] = b_ref[...]
-
-
-def pair_up(a, b, us=0.001):
-    return pl.pallas_call(
-        pair_kernel, out_shape=pltpu.HBM((2,) + a.shape, bf16), cost_estimate=cost(us), name="pair_up"
-    )(a, b)
-
-
 def by_bits(first, second, put):
     for i in range(2):
         for j in range(2):
@@ -795,36 +784,39 @@
                 put(i, j)
 
 
-def place_kernel(at, own, own_x, mate, mate_x, o0, o1, o2):
+def place_kernel(at, *refs):
+    o0, o1, o2 = refs[-3:]
     block = pl.program_id(0)
-    slot = (block % 2) ^ at[1]
     w = o0.shape[2] // 2
 
-    def put(other_x, core):
-        refs = (own_x, mate_x) if other_x else (own, mate)
-        for side in range(2):
-            part = refs[side ^ core][slot].astype(f32)
-            for i, out in enumerate((o0, o1, o2)):
-                out[0, :, side * w : (side + 1) * w] = part[:, i * w : (i + 1) * w]
-
-    by_bits((block // 2) ^ at[0], at[2], put)
+    def put(other_x, other_near):
+        for core in range(2):
+
+            @pl.when(at[2] == core)
+            def _(core=core):
+                for side in range(2):
+                    part = refs[4 * (side ^ core) + 2 * other_x + other_near][...].astype(f32)
+                    for i, out in enumerate((o0, o1, o2)):
+                        out[0, :, side * w : (side + 1) * w] = part[:, i * w : (i + 1) * w]
+
+    by_bits((block // 2) ^ at[0], (block % 2) ^ at[1], put)
 
 
 def place_tail(arrays, at):
-    _, h, width = arrays[0].shape
+    h, width = arrays[0].shape
     d = width // 3 * 2
-    whole = pl.BlockSpec((2, h, width), lambda i, m: (0, 0, 0), pipeline_mode=pl.Buffered(1))
+    whole = pl.BlockSpec((h, width), lambda i, m: (0, 0), pipeline_mode=pl.Buffered(1))
     outs = pl.pallas_call(
         place_kernel,
         out_shape=[pltpu.HBM((4, h, d), f32)] * 3,
         grid_spec=pltpu.PrefetchScalarGridSpec(
             num_scalar_prefetch=1,
             grid=(4,),
-            in_specs=[whole] * 4,
+            in_specs=[whole] * 8,
             out_specs=[pl.BlockSpec((1, h, d), lambda i, m: (i, 0, 0))] * 3,
         ),
         compiler_params=pltpu.CompilerParams(vmem_limit_bytes=40 << 20),
-        cost_estimate=cost(0.001),
+        cost_estimate=CHEAP,
         name="place_tail",
     )(at, *arrays)
     return [out.reshape(4 * h, d) for out in outs]
@@ -870,47 +862,43 @@
     )(at, hbm(x), hbm(g))
 
 
-def spread_kernel(at, own, mate, *refs, width, other_x):
+def spread_kernel(at, *refs, width):
     out = refs[-1]
     step = out.shape[1]
     rows = pl.ds(pl.multiple_of(pl.program_id(0) * step, step), step)
 
-    def put(core):
+    def put(core, near):
         cut = []
         for t in range(3):
             for n in range(2):
                 for c in range(2):
-                    part = (own, mate)[c ^ core][n ^ at[1], rows, :]
+                    part = refs[2 * (c ^ core) + (n ^ near)][rows, :]
                     cut.append(part[:, t * width : (t + 1) * width])
         out[0] = jnp.concatenate(cut, axis=1).astype(f32)
 
-    for core in range(2):
-
-        @pl.when(at[2] == core)
-        def _(core=core):
-            put(core)
-
-
-def spread(own, mate, at, used, other_x, carried=None):
-    _, rows, cols = own.shape
+    by_bits(at[2], at[1], put)
+
+
+def spread(arrays, at, used, other_x, carried=None):
+    rows, cols = arrays[0].shape
     width = 4 * used
     cuts = 2 if rows % 32 == 0 else 1
-    whole = pl.BlockSpec((2, rows, cols), lambda j, m: (0, 0, 0), pipeline_mode=pl.Buffered(1))
+    whole = pl.BlockSpec((rows, cols), lambda j, m: (0, 0), pipeline_mode=pl.Buffered(1))
     more = () if carried is None else (carried,)
     return pl.pallas_call(
-        functools.partial(spread_kernel, width=used // 3, other_x=other_x),
+        functools.partial(spread_kernel, width=used // 3),
         out_shape=pltpu.HBM((2, rows, width), f32),
         grid_spec=pltpu.PrefetchScalarGridSpec(
             num_scalar_prefetch=1,
             grid=(cuts,),
-            in_specs=[whole] * 2 + [pl.BlockSpec(memory_space=pl.ANY)] * len(more),
+            in_specs=[whole] * 4 + [pl.BlockSpec(memory_space=pl.ANY)] * len(more),
             out_specs=pl.BlockSpec((1, rows // cuts, width), lambda j, m: (m[0] ^ other_x, j, 0)),
         ),
-        input_output_aliases={3: 0} if more else {},
+        input_output_aliases={5: 0} if more else {},
         compiler_params=pltpu.CompilerParams(vmem_limit_bytes=40 << 20),
         cost_estimate=CHEAP,
         name="spread",
-    )(at, own, mate, *more)
+    )(at, *arrays, *more)
 
 
 def back_kernel(shards, g_ref, w_ref, *refs):
@@ -1266,6 +1254,7 @@
         q1_far = send(q1, far_mate)
         t2 = done(add(turn(t1), t1_far))
         t2_near = send(t2, near_mate)
+        t2_x = send(t2, x_mate)
         grad_tokens, grad_gain_attn = finish(
             grad_project,
             w_trans,
@@ -1286,28 +1275,37 @@
         small = jnp.concatenate(
             [grad_gain_attn[0], grad_gain_mlp[0], jnp.pad(grad_query_scale, (0, LN - HD))]
         ).reshape(-1, LN)
+        t2_x = done(turn(t2_x))
+        t2_near = done(turn(t2_near))
+        t2_near_x = send(t2_near, x_mate)
+        tails = [t2, t2_near, t2_x]
+        tails_mate = [send(turn(x), core_mate) for x in tails]
         q2 = done(add(turn(q1), q1_far))
         q2_near = send(q2, near_mate)
-        t4 = done(pair_up(turn(t2), t2_near))
-        t4_x = send(t4, x_mate)
-        t4_core = send(t4, core_mate)
+        q2_x = send(q2, x_mate)
         home_grad = send(turn(grad_tokens), to_home)
-        q4 = done(pair_up(turn(q2), q2_near))
-        q4_x = send(q4, x_mate)
-        q4_core = send(q4, core_mate)
-        t4_x = done(turn(t4_x))
-        t4_cross = send(t4_x, core_mate)
+        q2_near = done(turn(q2_near))
+        q2_near_x = send(q2_near, x_mate)
+        t2_near_x = done(turn(t2_near_x))
+        tails += [t2_near_x]
+        tails_mate += [send(t2_near_x, core_mate)]
+        q2_x = done(turn(q2_x))
+        quads_mate = [send(turn(x), core_mate) for x in (q2, q2_near, q2_x)]
+        tails_mate[3] = turn(tails_mate[3])
+        totals = place_tail(tails + tails_mate, jnp.stack([gx, near, gc]))
+        done(totals[0])
         used = 3 * nh * HD
         spread_at = jnp.stack([gx, near, 1 - gc])
-        totals = place_tail((turn(t4), t4_x, t4_core, t4_cross), jnp.stack([gx, near, gc]))
-        done(totals[0])
-        q4_core = done(turn(q4_core))
+        total_qkv = done(
+            spread((turn(q2), q2_near, quads_mate[0], quads_mate[1]), spread_at, used, 0)
+        )
         small = done(sum_all(turn(small))).reshape(-1)
         grad_tokens = done(copy(turn(home_grad)))
-        q4_x = done(turn(q4_x))
-        q4_cross = send(q4_x, core_mate)
-        total_qkv = done(spread(turn(q4), q4_core, spread_at, used, 0))
-        total_qkv = spread(turn(q4_x), q4_cross, spread_at, used, 1, total_qkv).reshape(wrows, 3 * D)
+        q2_near_x = done(turn(q2_near_x))
+        last_mate = send(q2_near_x, core_mate)
+        total_qkv = spread(
+            (q2_x, turn(q2_near_x), quads_mate[2], last_mate), spread_at, used, 1, total_qkv
+        ).reshape(wrows, 3 * D)
         return (
             layer_out[None],
             grad_tokens[None],

time: 422 us -> 427 us (1.012)
  local copies, waits for them, and re-layouts: 10.9 us -> 17.9 us
  Pallas kernels: 228 us -> 222 us
  starting transfers between devices: 54.3 us -> 60.3 us
    unnamed x67 -> x73, local copies, waits for them, and re-layouts: 3.78 us -> 10.8 us
    ppermute x41 -> x47, starting transfers between devices: 45.2 us -> 51.2 us  [send(): return lax.ppermute(value, AXES, pairs(target))]
    pallas_call x4 -> x2, Pallas kernels: 12.3 us -> 7.28 us  [spread(): pl.pallas_call(functools.partial(spread_kernel, width=used // 3), out_sha...]
    ppermute x41 -> x47, waiting for transfers between devices: 114 us -> 112 us  [send(): return lax.ppermute(value, AXES, pairs(target))]
  transfers between devices with their start and end apart: 42 -> 48, of which waited for: 17 -> 19; matrix products, arithmetic and copies ran while one was open for 3% -> 3% of each run, Pallas kernels for 48% -> 46%
where the time goes in v14:
time: 427 us; the launch traced here: 420 us
  Pallas kernels  222 us (52%)
  waiting for transfers between devices  112 us (26%)
  starting transfers between devices  60.3 us (14%)
  local copies, waits for them, and re-layouts  17.9 us (4%)
  other arithmetic  5.96 us (1%)
    ppermute x47, waiting for transfers between devices, send(): return lax.ppermute(value, AXES, pairs(target))  112 us
    ppermute x47, starting transfers between devices, send(): return lax.ppermute(value, AXES, pairs(target))  51.2 us
    pallas_call x1, Pallas kernels, attn_bwd(): pl.pallas_call(functools.partial(bwd_kernel, first=group * nh, nh=nh, bq=...  43.1 us
    pallas_call x1, Pallas kernels, attn_fwd(): pl.pallas_call(functools.partial(fwd_kernel, nh=nh, bq=bq, bk=bk, nk=n //...  25.7 us
    pallas_call x2, Pallas kernels, project(): pl.pallas_call(functools.partial(project_kernel, count=count, halves=len(...  22.7 us
    pallas_call x1, Pallas kernels, tail(): pl.pallas_call(body, out_shape=[pltpu.HBM((rows, d), bf16)] + [pltpu.HBM(...  21.5 us
    pallas_call x2, Pallas kernels, share(): pl.pallas_call(share_kernel, out_shape=pltpu.HBM((d, n * w), bf16), grid_...  14.6 us
    pallas_call x1, Pallas kernels, cross(): pl.pallas_call(cross_kernel, out_shape=[pltpu.HBM((w // 2, cols), bf16)]...  11.6 us
  transfers between devices with their start and end apart: 48, of which 19 were waited for; matrix products, arithmetic and copies ran while one was open for 3% of the time, Pallas kernels for 46%

profile of v14, /device:TPU:0, one launch (start us, length us, event | category | flops | bytes accessed | tf_op | source)
XLA Modules:
  0.0 420.0 jit_solution(8735256082143920192)
XLA Ops:
  1.9 7.3 %collective-permute-start.5 = (bf16[512,1280]{1,0:T(8,128)(2,1)}, bf16[512,1280]{1,0:T(8,128)(2,1)}, u32[]{:S(2)}, u32[]{:S(2)}) collective-permute-start(bf16[512,1280]{1,0:T(8,128)(2,1)} %bitcast.69), channel_id=1, source_target_pairs={{0,8},{1,9},{2,10},{3,11},{12,4},{13,5},{14,6},{15,7},{16,24},{17,... | collective-permute-start | bytes 3932168 | tf_op jit(solution)/shard_map/ppermute | solution.py:1031
  9.3 4.4 %pick.1.x_ref.a_ref = bf16[640,1024]{1,0:T(8,128)(2,1)} custom-call(s32[1]{0:T(128)} %bitcast.mine.shard, bf16[640,3840]{1,0:T(8,128)(2,1)} %w_ref.1), custom_call_target="tpu_custom_call" | custom-call | flops 5000000000 | bytes 1000 | tf_op jit(solution)/shard_map/pick/pallas_call | solution.py:352
  15.8 4.2 stretch.2.refs_5_
  30.9 12.1 %collective-permute-done.7.x_ref.b_ref = bf16[640,1024]{1,0:T(8,128)(2,1)} collective-permute-done((bf16[640,1024]{1,0:T(8,128)(2,1)}, bf16[640,1024]{1,0:T(8,128)(2,1)}, u32[]{:S(2)}, u32[]{:S(2)}) %collective-permute-start.7) | collective-permute-done | bytes 1310752 | tf_op jit(solution)/shard_map/ppermute | solution.py:1031
  43.0 4.0 stretch.3.refs_6_
  51.9 11.2 %project.2 = (bf16[2048,1280]{1,0:T(8,128)(2,1)}, bf16[2048,512]{1,0:T(8,128)(2,1)}, bf16[2048,1024]{1,0:T(8,128)(2,1)}, bf16[512,1280]{1,0:T(8,128)(2,1)}) custom-call(s32[5]{0:T(128)S(1)} %stack.103.info, bf16[512,1280]{1,0:T(8,128)(2,1)S(1)} %bitcast.70, bf16[512,1280]{1,0:T(8,128)(2,1)} %collective-permute-done.5.refs_1_, ...), custom_call_target="tpu_custom_call" | custom-call | flops 15000000512 | bytes 1000 | tf_op jit(solution)/shard_map/project/pallas_call | solution.py:518
  63.1 3.7 collective-permute-done.4.refs_2_
  73.5 11.6 %project.3 = (bf16[2048,1280]{1,0:T(8,128)(2,1)}, bf16[2048,512]{1,0:T(8,128)(2,1)}, bf16[2048,1024]{1,0:T(8,128)(2,1)}, bf16[512,1280]{1,0:T(8,128)(2,1)}) custom-call(s32[5]{0:T(128)S(1)} %stack.100.info, bf16[512,1280]{1,0:T(8,128)(2,1)S(1)} %collective-permute-done.2.refs_0_, ...), custom_call_target="tpu_custom_call", output_to_operand_aliasing={{0}: (11, {}), {1}: (12, {}), {2}: (13, {})} | custom-call | flops 15000000512 | bytes 1000 | tf_op jit(solution)/shard_map/project/pallas_call | solution.py:518
  85.1 25.7 %attn_fwd.1 = (bf16[2048,320]{1,0:T(8,128)(2,1)}, bf16[2048,512]{1,0:T(8,128)(2,1)}, bf16[2048,512]{1,0:T(8,128)(2,1)}) custom-call(s32[16]{0:T(128)S(1)} %reshape.183.flags, bf16[2048,512]{1,0:T(8,128)(2,1)} %get-tuple-element.92.q_ref, bf16[2048,1024]{1,0:T(8,128)(2,1)} %get-tuple-element.93.kv.kk.vv, s32[2048,1]{1,0:T(8,128)S(1)} %copy.29.segc, ...), custom_call_target="tpu_custom_call" | custom-call | flops 10000000 | bytes 1000 | tf_op jit(solution)/shard_map/attn_fwd/pallas_call | solution.py:172
  110.8 5.1 %collective-permute-done.9.half = bf16[3,320,1280]{2,1,0:T(8,128)(2,1)} collective-permute-done((bf16[3,320,1280]{2,1,0:T(8,128)(2,1)}, bf16[3,320,1280]{2,1,0:T(8,128)(2,1)}, u32[]{:S(2)}, u32[]{:S(2)}) %collective-permute-start.9) | collective-permute-done | bytes 2457632 | tf_op jit(solution)/shard_map/ppermute | solution.py:1031
  121.5 6.4 %order.1.w_ref = bf16[1024,1280]{1,0:T(8,128)(2,1)} custom-call(s32[1]{0:T(128)} %bitcast.10.own_first, bf16[640,1024]{1,0:T(8,128)(2,1)} %pick.1.x_ref.a_ref, bf16[640,1024]{1,0:T(8,128)(2,1)} %collective-permute-done.7.x_ref.b_ref), custom_call_target="tpu_custom_call" | custom-call | flops 199999995904 | bytes 1000 | tf_op jit(solution)/shard_map/order/pallas_call | solution.py:408
  127.9 7.8 %transpose.15.x_ref = bf16[1280,2048]{1,0:T(8,128)(2,1)} custom-call(bf16[2048,1280]{1,0:T(8,128)(2,1)} %get-tuple-element.101.x_ref), custom_call_target="tpu_custom_call" | custom-call | flops 1000000 | bytes 1000 | tf_op jit(solution)/shard_map/transpose/pallas_call | solution.py:432
  139.3 21.5 %tail.1 = (bf16[512,1280]{1,0:T(8,128)(2,1)}, bf16[3,512,1280]{2,1,0:T(8,128)(2,1)}, bf16[3,512,1280]{2,1,0:T(8,128)(2,1)}, f32[512,1280]{1,0:T(8,128)}, bf16[51...) custom-call(s32[4]{0:T(128)S(1)} %pad_add_fusion.at, ...), custom_call_target="tpu_custom_call" | custom-call | flops 10000000 | bytes 1000 | tf_op jit(solution)/shard_map/tail/pallas_call | solution.py:650
  163.2 7.4 %share.2 = bf16[1280,1920]{1,0:T(8,128)(2,1)} custom-call(s32[1]{0:T(128)} %bitcast.21.col, bf16[3,512,1280]{2,1,0:T(8,128)(2,1)} %get-tuple-element.109.left, bf16[3,512,1280]{2,1,0:T(8,128)(2,1)} %get-tuple-element.110.right), custom_call_target="tpu_custom_call" | custom-call | flops 1000000 | bytes 1000 | tf_op jit(solution)/shard_map/share/pallas_call | solution.py:686
  170.6 7.2 %share.3.a_ref = bf16[1280,1920]{1,0:T(8,128)(2,1)} custom-call(s32[1]{0:T(128)} %bitcast.22.col, bf16[3,512,1280]{2,1,0:T(8,128)(2,1)} %get-tuple-element.109.left, bf16[3,512,1280]{2,1,0:T(8,128)(2,1)} %get-tuple-element.110.right), custom_call_target="tpu_custom_call" | custom-call | flops 1000000 | bytes 1000 | tf_op jit(solution)/shard_map/share/pallas_call | solution.py:686
  182.8 7.8 %add_rows.1 = bf16[1280,1920]{1,0:T(8,128)(2,1)} custom-call(bf16[1280,1920]{1,0:T(8,128)(2,1)} %share.3.a_ref, bf16[1280,1920]{1,0:T(8,128)(2,1)} %collective-permute-done.19.b_ref), custom_call_target="tpu_custom_call" | custom-call | flops 1000000 | bytes 1000 | tf_op jit(solution)/shard_map/add_rows/pallas_call | solution.py:766
  190.6 9.1 %all-to-all-start = ((bf16[8,160,1920]{2,1,0:T(8,128)(2,1)}), bf16[8,160,1920]{2,1,0:T(8,128)(2,1)}, u32[]{:S(2)}, u32[]{:S(2)}) async-start(bf16[8,160,1920]{2,1,0:T(8,128)(2,1)} %bitcast.79), calls=%async_computation | async-start | bytes 9830400 | tf_op jit(solution)/shard_map/all_to_all | solution.py:1201
  199.7 43.1 %attn_bwd.1 = (bf16[2048,1024]{1,0:T(8,128)(2,1)}, f32[8,128]{1,0:T(8,128)}) custom-call(s32[16]{0:T(128)S(1)} %reshape.183.flags, s32[1]{0:T(128)} %bitcast.mine.shard, bf16[2048,512]{1,0:T(8,128)(2,1)} %get-tuple-element.116.qa, bf16[2048,1024]{1,0:T(8,128)(2,1)} %get-tuple-element.93.kv.kk.vv, bf16[2048,1024]{1,0:T(8,128)(2,1)} %get-tuple-element.93.kv.kk.vv, ...), custom_call_target="tpu_custom_call" | custom-call | flops 299999985664 | bytes 1000 | tf_op jit(solution)/shard_map/attn_bwd/pallas_call | solution.py:314
  242.8 6.8 %back.2 = bf16[2,512,1280]{2,1,0:T(8,128)(2,1)} custom-call(s32[2]{0:T(128)S(1)} %pad_add_fusion.1.shards, bf16[2048,1024]{1,0:T(8,128)(2,1)} %get-tuple-element.125.g_ref, bf16[1024,1280]{1,0:T(8,128)(2,1)} %order.1.w_ref), custom_call_target="tpu_custom_call" | custom-call | flops 1000000 | bytes 1000 | tf_op jit(solution)/shard_map/back/pallas_call | solution.py:924
  249.6 11.6 %cross.1 = (bf16[320,1024]{1,0:T(8,128)(2,1)}, bf16[320,1024]{1,0:T(8,128)(2,1)}, bf16[320,1024]{1,0:T(8,128)(2,1)}, bf16[320,1024]{1,0:T(8,128)(2,1)}) custom-call(s32[2]{0:T(128)S(1)} %pad_add_fusion.2.at, bf16[1280,2048]{1,0:T(8,128)(2,1)} %transpose.15.x_ref, bf16[2048,1024]{1,0:T(8,128)(2,1)} %get-tuple-element.125.g_ref), custom_call_target="tpu_custom_call" | custom-call | flops 1000000 | bytes 1000 | tf_op jit(solution)/shard_map/cross/pallas_call | solution.py:846
  261.2 4.7 %back.3 = bf16[1,512,1280]{2,1,0:T(8,128)(2,1)} custom-call(s32[1]{0:T(128)} %bitcast.26.shards, bf16[2048,1024]{1,0:T(8,128)(2,1)} %get-tuple-element.125.g_ref, bf16[1024,1280]{1,0:T(8,128)(2,1)} %order.1.w_ref, bf16[2,512,1280]{2,1,0:T(8,128)(2,1)S(1)} %collective-permute-done.20.refs_0_.core), custom_call_target="tpu_custom_call" | custom-call | flops 1000000 | bytes 1000 | tf_op jit(solution)/shard_map/back/pallas_call | solution.py:924
  278.0 7.7 %collective-permute-done.22 = bf16[320,1024]{1,0:T(8,128)(2,1)} collective-permute-done((bf16[320,1024]{1,0:T(8,128)(2,1)}, bf16[320,1024]{1,0:T(8,128)(2,1)}, u32[]{:S(2)}, u32[]{:S(2)}) %collective-permute-start.22) | collective-permute-done | bytes 655392 | tf_op jit(solution)/shard_map/ppermute | solution.py:1031
  285.8 14.9 %collective-permute-done.23 = bf16[320,1024]{1,0:T(8,128)(2,1)} collective-permute-done((bf16[320,1024]{1,0:T(8,128)(2,1)}, bf16[320,1024]{1,0:T(8,128)(2,1)}, u32[]{:S(2)}, u32[]{:S(2)}) %collective-permute-start.23) | collective-permute-done | bytes 655392 | tf_op jit(solution)/shard_map/ppermute | solution.py:1031
  303.1 7.4 %collective-permute-done.25.b_ref = bf16[160,1920]{1,0:T(8,128)(2,1)} collective-permute-done((bf16[160,1920]{1,0:T(8,128)(2,1)}, bf16[160,1920]{1,0:T(8,128)(2,1)}, u32[]{:S(2)}, u32[]{:S(2)}) %collective-permute-start.25) | collective-permute-done | bytes 614432 | tf_op jit(solution)/shard_map/ppermute | solution.py:1031
  315.3 6.6 %finish.1 = (bf16[512,1280]{1,0:T(8,128)(2,1)}, f32[1,1280]{1,0:T(1,128)S(1)}) custom-call(s32[1]{0:T(128)} %bitcast.mine.shard, bf16[2048,1024]{1,0:T(8,128)(2,1)} %get-tuple-element.125.g_ref, bf16[1024,1280]{1,0:T(8,128)(2,1)} %order.1.w_ref, bf16[2,512,1280]{2,1,0:T(8,128)(2,1)S(1)} %collective-permute-done.20.refs_0_.core, ...), custom_call_target="tpu_custom_call" | custom-call | flops 1000000 | bytes 1000 | tf_op jit(solution)/shard_map/finish/pallas_call | solution.py:962
  322.0 6.3 %collective-permute-done.27.refs_2_ = bf16[160,1920]{1,0:T(8,128)(2,1)} collective-permute-done((bf16[160,1920]{1,0:T(8,128)(2,1)}, bf16[160,1920]{1,0:T(8,128)(2,1)}, u32[]{:S(2)}, u32[]{:S(2)}) %collective-permute-start.27) | collective-permute-done | bytes 614432 | tf_op jit(solution)/shard_map/ppermute | solution.py:1031
  328.3 15.3 %collective-permute-done.26.refs_1_ = bf16[160,1920]{1,0:T(8,128)(2,1)S(1)} collective-permute-done((bf16[160,1920]{1,0:T(8,128)(2,1)}, bf16[160,1920]{1,0:T(8,128)(2,1)S(1)}, u32[]{:S(2)}, u32[]{:S(2)}) %collective-permute-start.26) | collective-permute-done | bytes 614432 | tf_op jit(solution)/shard_map/ppermute | solution.py:1031
  350.1 18.8 %collective-permute-done.31.refs_1_ = bf16[320,1024]{1,0:T(8,128)(2,1)S(1)} collective-permute-done((bf16[320,1024]{1,0:T(8,128)(2,1)}, bf16[320,1024]{1,0:T(8,128)(2,1)S(1)}, u32[]{:S(2)}, u32[]{:S(2)}) %collective-permute-start.31) | collective-permute-done | bytes 655392 | tf_op jit(solution)/shard_map/ppermute | solution.py:1031
  370.3 3.7 collective-permute-done.36.refs_0_
  384.0 6.1 %place_tail.1 = (f32[4,160,1280]{2,1,0:T(8,128)}, f32[4,160,1280]{2,1,0:T(8,128)}, f32[4,160,1280]{2,1,0:T(8,128)}) custom-call(s32[3]{0:T(128)S(1)} %pad_add_fusion.5.at, bf16[160,1920]{1,0:T(8,128)(2,1)S(1)} %copy-done.1, bf16[160,1920]{1,0:T(8,128)(2,1)S(1)} %copy-done.5, bf16[160,1920]{1,0:T(8,128)(2,1)} %collective-permute-done.27.refs_2_, ...), custom_call_target="tpu_custom_call" | custom-call | flops 1000000 | bytes 1000 | tf_op jit(solution)/shard_map/place_tail/pallas_call | solution.py:809
  390.1 4.2 spread.2.refs_4_
  402.9 3.6 collective-permute-start.42
  (207 shorter events, 101.1 us)
Async XLA Ops:
  0.6 22.3 %collective-permute-start.1 = (bf16[512,1280]{1,0:T(8,128)(2,1)}, bf16[512,1280]{1,0:T(8,128)(2,1)}, u32[]{:S(2)}, u32[]{:S(2)}) collective-permute-start(bf16[512,1280]{1,0:T(8,128)(2,1)} %bitcast.68), channel_id=1, source_target_pairs={{2,0},{3,1},{4,2},{5,3},{6,4},{7,5},{8,10},{9,11},{10,12},{11,13},... | collective-permute-start | bytes 3932168 | tf_op jit(solution)/shard_map/ppermute | solution.py:1031
  1.9 49.9 %collective-permute-start.5 = (bf16[512,1280]{1,0:T(8,128)(2,1)}, bf16[512,1280]{1,0:T(8,128)(2,1)}, u32[]{:S(2)}, u32[]{:S(2)}) collective-permute-start(bf16[512,1280]{1,0:T(8,128)(2,1)} %bitcast.69), channel_id=1, source_target_pairs={{0,8},{1,9},{2,10},{3,11},{12,4},{13,5},{14,6},{15,7},{16,24},{17,... | collective-permute-start | bytes 3932168 | tf_op jit(solution)/shard_map/ppermute | solution.py:1031
  13.7 29.3 %collective-permute-start.7 = (bf16[640,1024]{1,0:T(8,128)(2,1)}, bf16[640,1024]{1,0:T(8,128)(2,1)}, u32[]{:S(2)}, u32[]{:S(2)}) collective-permute-start(bf16[640,1024]{1,0:T(8,128)(2,1)} %pick.1.x_ref.a_ref), channel_id=1, source_target_pairs={{0,1},{1,0},{2,3},{3,2},{4,5},{5,4},{6,7},{7,6},{8,9},{9,8},{10,11... | collective-permute-start | bytes 3932168 | tf_op jit(solution)/shard_map/ppermute | solution.py:1031
  15.2 55.7 %collective-permute-start = (s32[1,2048]{1,0:T(1,128)S(1)}, s32[1,2048]{1,0:T(1,128)S(1)}, u32[]{:S(2)}, u32[]{:S(2)}) collective-permute-start(s32[1,2048]{1,0:T(1,128)S(1)} %copy-done.28), channel_id=1, source_target_pairs={{0,8},{1,9},{2,10},{3,11},{4,12},{5,13},{6,14},{7,15},{8,0},{9,1},... | collective-permute-start | bytes 24584 | tf_op jit(solution)/shard_map/ppermute | solution.py:1031
  22.9 24.0 %collective-permute-start.2 = (bf16[512,1280]{1,0:T(8,128)(2,1)}, bf16[512,1280]{1,0:T(8,128)(2,1)S(1)}, u32[]{:S(2)}, u32[]{:S(2)}) collective-permute-start(bf16[512,1280]{1,0:T(8,128)(2,1)} %collective-permute-done.1.refs_2_), channel_id=1, source_target_pairs={{2,0},{3,1},{4,2},{5,3},{10,12},{11,13},{12,14},{13,15},{18,16},{1... | collective-permute-start | bytes 3932168 | tf_op jit(solution)/shard_map/ppermute | solution.py:1031
  27.7 24.1 %collective-permute-start.6 = (bf16[512,1280]{1,0:T(8,128)(2,1)}, bf16[512,1280]{1,0:T(8,128)(2,1)}, u32[]{:S(2)}, u32[]{:S(2)}) collective-permute-start(bf16[512,1280]{1,0:T(8,128)(2,1)} %collective-permute-done.1.refs_2_), channel_id=1, source_target_pairs={{0,8},{1,9},{2,10},{3,11},{12,4},{13,5},{14,6},{15,7},{16,24},{17,... | collective-permute-start | bytes 3932168 | tf_op jit(solution)/shard_map/ppermute | solution.py:1031
  47.2 19.6 %collective-permute-start.4 = (bf16[512,1280]{1,0:T(8,128)(2,1)S(1)}, bf16[512,1280]{1,0:T(8,128)(2,1)}, u32[]{:S(2)}, u32[]{:S(2)}) collective-permute-start(bf16[512,1280]{1,0:T(8,128)(2,1)S(1)} %broadcast_select_fusion), channel_id=1, source_target_pairs={{0,2},{1,3},{2,0},{3,1},{12,14},{13,15},{14,12},{15,13},{16,18},{1... | collective-permute-start | bytes 3932168 | tf_op jit(solution)/shard_map/ppermute | solution.py:1031
  49.5 24.0 %collective-permute-start.3 = (bf16[512,1280]{1,0:T(8,128)(2,1)S(1)}, bf16[512,1280]{1,0:T(8,128)(2,1)}, u32[]{:S(2)}, u32[]{:S(2)}) collective-permute-start(bf16[512,1280]{1,0:T(8,128)(2,1)S(1)} %collective-permute-done.2.refs_0_), channel_id=1, source_target_pairs={{0,8},{1,9},{2,10},{3,11},{12,4},{13,5},{14,6},{15,7},{16,24},{17,... | collective-permute-start | bytes 3932168 | tf_op jit(solution)/shard_map/ppermute | solution.py:1031
  69.4 46.5 %collective-permute-start.9 = (bf16[3,320,1280]{2,1,0:T(8,128)(2,1)}, bf16[3,320,1280]{2,1,0:T(8,128)(2,1)}, u32[]{:S(2)}, u32[]{:S(2)}) collective-permute-start(bf16[3,320,1280]{2,1,0:T(8,128)(2,1)} %pad_maximum_fusion), channel_id=1, source_target_pairs={{0,1},{1,0},{2,3},{3,2},{4,5},{5,4},{6,7},{7,6},{8,9},{9,8},{10,11... | collective-permute-start | bytes 7372808 | tf_op jit(solution)/shard_map/ppermute | solution.py:1031
  72.9 43.0 %collective-permute-start.10 = (bf16[512,1280]{1,0:T(8,128)(2,1)}, bf16[512,1280]{1,0:T(8,128)(2,1)S(1)}, u32[]{:S(2)}, u32[]{:S(2)}) collective-permute-start(bf16[512,1280]{1,0:T(8,128)(2,1)} %bitcast.90), channel_id=1, source_target_pairs={{0,8},{1,9},{2,0},{3,1},{4,10},{5,11},{6,2},{7,3},{8,12},{9,13},{1... | collective-permute-start | bytes 3932168 | tf_op jit(solution)/shard_map/ppermute | solution.py:1031
  119.4 16.4 %collective-permute-start.11 = (bf16[512,320]{1,0:T(8,128)(2,1)}, bf16[512,320]{1,0:T(8,128)(2,1)}, u32[]{:S(2)}, u32[]{:S(2)}) collective-permute-start(bf16[512,320]{1,0:T(8,128)(2,1)} %get-tuple-element.169), channel_id=1, source_target_pairs={{0,8},{1,9},{2,10},{3,11},{4,12},{5,13},{6,14},{7,15},{8,0},{9,1},... | collective-permute-start | bytes 983048 | tf_op jit(solution)/shard_map/ppermute | solution.py:1031
  119.4 16.4 %collective-permute-start.12 = (bf16[512,320]{1,0:T(8,128)(2,1)}, bf16[512,320]{1,0:T(8,128)(2,1)}, u32[]{:S(2)}, u32[]{:S(2)}) collective-permute-start(bf16[512,320]{1,0:T(8,128)(2,1)} %get-tuple-element.168), channel_id=1, source_target_pairs={{0,2},{1,3},{2,0},{3,1},{4,6},{5,7},{6,4},{7,5},{8,10},{9,11},{10,... | collective-permute-start | bytes 983048 | tf_op jit(solution)/shard_map/ppermute | solution.py:1031
  119.8 19.5 %collective-permute-start.13 = (bf16[512,320]{1,0:T(8,128)(2,1)}, bf16[512,320]{1,0:T(8,128)(2,1)}, u32[]{:S(2)}, u32[]{:S(2)}) collective-permute-start(bf16[512,320]{1,0:T(8,128)(2,1)} %get-tuple-element.167), channel_id=1, source_target_pairs={{0,10},{1,11},{2,8},{3,9},{4,14},{5,15},{6,12},{7,13},{8,2},{9,3},... | collective-permute-start | bytes 983048 | tf_op jit(solution)/shard_map/ppermute | solution.py:1031
  121.2 18.0 %collective-permute-start.14 = (bf16[3,320,1280]{2,1,0:T(8,128)(2,1)}, bf16[3,320,1280]{2,1,0:T(8,128)(2,1)}, u32[]{:S(2)}, u32[]{:S(2)}) collective-permute-start(bf16[3,320,1280]{2,1,0:T(8,128)(2,1)} %collective-permute-done.9.half), channel_id=1, source_target_pairs={{0,8},{1,9},{2,10},{3,11},{4,12},{5,13},{6,14},{7,15},{8,0},{9,1},... | collective-permute-start | bytes 7372808 | tf_op jit(solution)/shard_map/ppermute | solution.py:1031
  161.1 16.7 %collective-permute-start.17 = (bf16[512,320]{1,0:T(8,128)(2,1)}, bf16[512,320]{1,0:T(8,128)(2,1)S(1)}, u32[]{:S(2)}, u32[]{:S(2)}) collective-permute-start(bf16[512,320]{1,0:T(8,128)(2,1)} %get-tuple-element.113), channel_id=1, source_target_pairs={{0,10},{1,11},{2,8},{3,9},{4,14},{5,15},{6,12},{7,13},{8,2},{9,3},... | collective-permute-start | bytes 983048 | tf_op jit(solution)/shard_map/ppermute | solution.py:1031
  161.3 19.8 %collective-permute-start.16 = (bf16[512,320]{1,0:T(8,128)(2,1)}, bf16[512,320]{1,0:T(8,128)(2,1)S(1)}, u32[]{:S(2)}, u32[]{:S(2)}) collective-permute-start(bf16[512,320]{1,0:T(8,128)(2,1)} %get-tuple-element.107), channel_id=1, source_target_pairs={{0,2},{1,3},{2,0},{3,1},{4,6},{5,7},{6,4},{7,5},{8,10},{9,11},{10,... | collective-permute-start | bytes 983048 | tf_op jit(solution)/shard_map/ppermute | solution.py:1031
  182.4 60.4 %collective-permute-start.18 = (bf16[512,1280]{1,0:T(8,128)(2,1)}, bf16[512,1280]{1,0:T(8,128)(2,1)}, u32[]{:S(2)}, u32[]{:S(2)}) collective-permute-start(bf16[512,1280]{1,0:T(8,128)(2,1)} %get-tuple-element.115), channel_id=1, source_target_pairs={{0,2},{1,3},{2,6},{3,7},{4,10},{5,11},{6,14},{7,15},{8,0},{9,1},{1... | collective-permute-start | bytes 3932168 | tf_op jit(solution)/shard_map/ppermute | solution.py:1031
  190.6 80.8 %all-to-all-start = ((bf16[8,160,1920]{2,1,0:T(8,128)(2,1)}), bf16[8,160,1920]{2,1,0:T(8,128)(2,1)}, u32[]{:S(2)}, u32[]{:S(2)}) async-start(bf16[8,160,1920]{2,1,0:T(8,128)(2,1)} %bitcast.79), calls=%async_computation | async-start | bytes 9830400 | tf_op jit(solution)/shard_map/all_to_all | solution.py:1201
  265.9 49.5 %collective-permute-start.21 = (bf16[1,512,1280]{2,1,0:T(8,128)(2,1)}, bf16[1,512,1280]{2,1,0:T(8,128)(2,1)}, u32[]{:S(2)}, u32[]{:S(2)}) collective-permute-start(bf16[1,512,1280]{2,1,0:T(8,128)(2,1)} %back.3), channel_id=1, source_target_pairs={{0,2},{1,3},{2,0},{3,1},{4,6},{5,7},{6,4},{7,5},{8,10},{9,11},{10,... | collective-permute-start | bytes 3932168 | tf_op jit(solution)/shard_map/ppermute | solution.py:1031
  267.9 17.9 %collective-permute-start.22 = (bf16[320,1024]{1,0:T(8,128)(2,1)}, bf16[320,1024]{1,0:T(8,128)(2,1)}, u32[]{:S(2)}, u32[]{:S(2)}) collective-permute-start(bf16[320,1024]{1,0:T(8,128)(2,1)} %get-tuple-element.131), channel_id=1, source_target_pairs={{0,16},{1,17},{2,18},{3,19},{4,20},{5,21},{6,22},{7,23},{8,24},{9,... | collective-permute-start | bytes 1966088 | tf_op jit(solution)/shard_map/ppermute | solution.py:1031
  269.8 30.9 %collective-permute-start.23 = (bf16[320,1024]{1,0:T(8,128)(2,1)}, bf16[320,1024]{1,0:T(8,128)(2,1)}, u32[]{:S(2)}, u32[]{:S(2)}) collective-permute-start(bf16[320,1024]{1,0:T(8,128)(2,1)} %get-tuple-element.132), channel_id=1, source_target_pairs={{0,1},{1,0},{2,3},{3,2},{4,5},{5,4},{6,7},{7,6},{8,9},{9,8},{10,11... | collective-permute-start | bytes 1966088 | tf_op jit(solution)/shard_map/ppermute | solution.py:1031
  271.2 29.5 %collective-permute-start.24 = (bf16[320,1024]{1,0:T(8,128)(2,1)}, bf16[320,1024]{1,0:T(8,128)(2,1)}, u32[]{:S(2)}, u32[]{:S(2)}) collective-permute-start(bf16[320,1024]{1,0:T(8,128)(2,1)} %get-tuple-element.133), channel_id=1, source_target_pairs={{0,17},{1,16},{2,19},{3,18},{4,21},{5,20},{6,23},{7,22},{8,25},{9,... | collective-permute-start | bytes 1966088 | tf_op jit(solution)/shard_map/ppermute | solution.py:1031
  274.9 35.7 %collective-permute-start.25 = (bf16[160,1920]{1,0:T(8,128)(2,1)}, bf16[160,1920]{1,0:T(8,128)(2,1)}, u32[]{:S(2)}, u32[]{:S(2)}) collective-permute-start(bf16[160,1920]{1,0:T(8,128)(2,1)} %total.2.a_ref), channel_id=1, source_target_pairs={{0,4},{1,5},{2,6},{3,7},{4,0},{5,1},{6,2},{7,3},{8,12},{9,13},{10,... | collective-permute-start | bytes 1843208 | tf_op jit(solution)/shard_map/ppermute | solution.py:1031
  303.1 40.5 %collective-permute-start.28 = (bf16[320,1024]{1,0:T(8,128)(2,1)}, bf16[320,1024]{1,0:T(8,128)(2,1)}, u32[]{:S(2)}, u32[]{:S(2)}) collective-permute-start(bf16[320,1024]{1,0:T(8,128)(2,1)} %total.3.a_ref), channel_id=1, source_target_pairs={{0,4},{1,5},{2,6},{3,7},{4,0},{5,1},{6,2},{7,3},{8,12},{9,13},{10,... | collective-permute-start | bytes 1966088 | tf_op jit(solution)/shard_map/ppermute | solution.py:1031
  314.6 29.0 %collective-permute-start.26 = (bf16[160,1920]{1,0:T(8,128)(2,1)}, bf16[160,1920]{1,0:T(8,128)(2,1)S(1)}, u32[]{:S(2)}, u32[]{:S(2)}) collective-permute-start(bf16[160,1920]{1,0:T(8,128)(2,1)} %add.135.refs_0_), channel_id=1, source_target_pairs={{0,2},{1,3},{2,0},{3,1},{4,6},{5,7},{6,4},{7,5},{8,10},{9,11},{10,... | collective-permute-start | bytes 1843208 | tf_op jit(solution)/shard_map/ppermute | solution.py:1031
  346.1 22.9 %collective-permute-start.31 = (bf16[320,1024]{1,0:T(8,128)(2,1)}, bf16[320,1024]{1,0:T(8,128)(2,1)S(1)}, u32[]{:S(2)}, u32[]{:S(2)}) collective-permute-start(bf16[320,1024]{1,0:T(8,128)(2,1)} %add.136.refs_0_), channel_id=1, source_target_pairs={{0,2},{1,3},{2,0},{3,1},{4,6},{5,7},{6,4},{7,5},{8,10},{9,11},{10,... | collective-permute-start | bytes 1966088 | tf_op jit(solution)/shard_map/ppermute | solution.py:1031
  346.1 22.9 %collective-permute-start.30 = (bf16[160,1920]{1,0:T(8,128)(2,1)S(1)}, bf16[160,1920]{1,0:T(8,128)(2,1)S(1)}, u32[]{:S(2)}, u32[]{:S(2)}) collective-permute-start(bf16[160,1920]{1,0:T(8,128)(2,1)S(1)} %collective-permute-done.26.refs_1_), channel_id=1, source_target_pairs={{0,16},{1,17},{2,18},{3,19},{4,20},{5,21},{6,22},{7,23},{8,24},{9,... | collective-permute-start | bytes 1843208 | tf_op jit(solution)/shard_map/ppermute | solution.py:1031
  346.4 27.7 %collective-permute-start.36 = (bf16[320,1024]{1,0:T(8,128)(2,1)}, bf16[320,1024]{1,0:T(8,128)(2,1)S(1)}, u32[]{:S(2)}, u32[]{:S(2)}) collective-permute-start(bf16[320,1024]{1,0:T(8,128)(2,1)} %add.136.refs_0_), channel_id=1, source_target_pairs={{0,16},{1,17},{2,18},{3,19},{4,20},{5,21},{6,22},{7,23},{8,24},{9,... | collective-permute-start | bytes 1966088 | tf_op jit(solution)/shard_map/ppermute | solution.py:1031
  348.1 25.9 %collective-permute-start.34 = (bf16[160,1920]{1,0:T(8,128)(2,1)}, bf16[160,1920]{1,0:T(8,128)(2,1)S(1)}, u32[]{:S(2)}, u32[]{:S(2)}) collective-permute-start(bf16[160,1920]{1,0:T(8,128)(2,1)} %collective-permute-done.27.refs_2_), channel_id=1, source_target_pairs={{0,8},{1,9},{2,10},{3,11},{4,12},{5,13},{6,14},{7,15},{8,0},{9,1},... | collective-permute-start | bytes 1843208 | tf_op jit(solution)/shard_map/ppermute | solution.py:1031
  348.1 63.7 %collective-permute-start.29 = (bf16[512,1280]{1,0:T(8,128)(2,1)}, bf16[512,1280]{1,0:T(8,128)(2,1)}, u32[]{:S(2)}, u32[]{:S(2)}) collective-permute-start(bf16[512,1280]{1,0:T(8,128)(2,1)} %get-tuple-element.141), channel_id=1, source_target_pairs={{0,2},{1,3},{2,6},{3,7},{4,10},{5,11},{6,14},{7,15},{8,0},{9,1},{1... | collective-permute-start | bytes 3932168 | tf_op jit(solution)/shard_map/ppermute | solution.py:1031
  374.0 16.0 %collective-permute-start.38 = (bf16[320,1024]{1,0:T(8,128)(2,1)S(1)}, bf16[320,1024]{1,0:T(8,128)(2,1)S(1)}, u32[]{:S(2)}, u32[]{:S(2)}) collective-permute-start(bf16[320,1024]{1,0:T(8,128)(2,1)S(1)} %collective-permute-done.31.refs_1_), channel_id=1, source_target_pairs={{0,8},{1,9},{2,10},{3,11},{4,12},{5,13},{6,14},{7,15},{8,0},{9,1},... | collective-permute-start | bytes 1966088 | tf_op jit(solution)/shard_map/ppermute | solution.py:1031
  377.1 37.3 %collective-permute-start.44 = (bf16[320,1024]{1,0:T(8,128)(2,1)S(1)}, bf16[320,1024]{1,0:T(8,128)(2,1)S(1)}, u32[]{:S(2)}, u32[]{:S(2)}) collective-permute-start(bf16[320,1024]{1,0:T(8,128)(2,1)S(1)} %collective-permute-done.31.refs_1_), channel_id=1, source_target_pairs={{0,16},{1,17},{2,18},{3,19},{4,20},{5,21},{6,22},{7,23},{8,24},{9,... | collective-permute-start | bytes 1966088 | tf_op jit(solution)/shard_map/ppermute | solution.py:1031
  (51 other events, 550.1 us)

commit v15 on v14

--- a/solution.py
+++ b/solution.py
@@ -177,7 +177,7 @@
             pltpu.HBM((n, w), bf16),
         ],
         grid_spec=spec,
-        compiler_params=pltpu.CompilerParams(vmem_limit_bytes=40 << 20),
+        compiler_params=pltpu.CompilerParams(vmem_limit_bytes=28 << 20),
         cost_estimate=cost(0.01),
         name="attn_fwd",
     )(block_flags(seg_row, bq, bk), hbm(q), hbm(kv), seg_row[:, None], seg_row[None])
@@ -538,7 +538,7 @@
             scratch_shapes=[pltpu.VMEM((d, 3 * width), bf16)],
         ),
         input_output_aliases=aliases,
-        compiler_params=pltpu.CompilerParams(vmem_limit_bytes=48 << 20),
+        compiler_params=pltpu.CompilerParams(vmem_limit_bytes=32 << 20),
         cost_estimate=cost(15),
         name="project",
     )(info, *args)
@@ -695,7 +695,7 @@
             ],
             out_specs=block,
         ),
-        compiler_params=pltpu.CompilerParams(vmem_limit_bytes=40 << 20),
+        compiler_params=pltpu.CompilerParams(vmem_limit_bytes=20 << 20),
         cost_estimate=CHEAP,
         name="share",
     )(col.reshape(1), hbm(left), hbm(right))
@@ -744,7 +744,7 @@
             pl.BlockSpec((x.shape[0], rows // cuts, x.shape[2]), lambda i: (0, i, 0)) for x in flat
         ],
         out_specs=pl.BlockSpec((rows // cuts, width), lambda i: (i, 0)),
-        compiler_params=pltpu.CompilerParams(vmem_limit_bytes=40 << 20),
+        compiler_params=pltpu.CompilerParams(vmem_limit_bytes=16 << 20),
         cost_estimate=cost(0.001),
         name="total",
     )(*flat)
@@ -769,7 +769,7 @@
         grid=(5,),
         in_specs=[block] * 2,
         out_specs=block,
-        compiler_params=pltpu.CompilerParams(vmem_limit_bytes=24 << 20),
+        compiler_params=pltpu.CompilerParams(vmem_limit_bytes=14 << 20),
         cost_estimate=CHEAP,
         name="add_rows",
     )(hbm(a), hbm(b))
@@ -815,7 +815,7 @@
             in_specs=[whole] * 8,
             out_specs=[pl.BlockSpec((1, h, d), lambda i, m: (i, 0, 0))] * 3,
         ),
-        compiler_params=pltpu.CompilerParams(vmem_limit_bytes=40 << 20),
+        compiler_params=pltpu.CompilerParams(vmem_limit_bytes=16 << 20),
         cost_estimate=CHEAP,
         name="place_tail",
     )(at, *arrays)
@@ -856,7 +856,7 @@
             out_specs=[first, first, second, second],
             scratch_shapes=[pltpu.VMEM((w, step), f32)],
         ),
-        compiler_params=pltpu.CompilerParams(vmem_limit_bytes=40 << 20),
+        compiler_params=pltpu.CompilerParams(vmem_limit_bytes=26 << 20),
         cost_estimate=CHEAP,
         name="cross",
     )(at, hbm(x), hbm(g))
@@ -895,7 +895,7 @@
             out_specs=pl.BlockSpec((1, rows // cuts, width), lambda j, m: (m[0] ^ other_x, j, 0)),
         ),
         input_output_aliases={5: 0} if more else {},
-        compiler_params=pltpu.CompilerParams(vmem_limit_bytes=40 << 20),
+        compiler_params=pltpu.CompilerParams(vmem_limit_bytes=20 << 20),
         cost_estimate=CHEAP,
         name="spread",
     )(at, *arrays, *more)
@@ -927,7 +927,7 @@
         grid_spec=pltpu.PrefetchScalarGridSpec(
             num_scalar_prefetch=1, grid=(d // step, n), in_specs=in_specs, out_specs=out
         ),
-        compiler_params=pltpu.CompilerParams(vmem_limit_bytes=40 << 20),
+        compiler_params=pltpu.CompilerParams(vmem_limit_bytes=22 << 20),
         cost_estimate=CHEAP,
         name="back",
     )(shards, *args)
@@ -976,7 +976,7 @@
             ],
             out_specs=[pl.BlockSpec((tile, d), row), pl.BlockSpec((1, d), lambda i, f: (0, 0))],
         ),
-        compiler_params=pltpu.CompilerParams(vmem_limit_bytes=40 << 20),
+        compiler_params=pltpu.CompilerParams(vmem_limit_bytes=24 << 20),
         cost_estimate=CHEAP,
         name="finish",
     )(shard.reshape(1), hbm(grad), hbm(w), core, near, hbm(x), hbm(resid), gain)
@@ -1296,13 +1296,14 @@
         done(totals[0])
         used = 3 * nh * HD
         spread_at = jnp.stack([gx, near, 1 - gc])
-        total_qkv = done(
-            spread((turn(q2), q2_near, quads_mate[0], quads_mate[1]), spread_at, used, 0)
-        )
+        quads_mate[0] = done(after(turn(quads_mate[0]), quads_mate[1]))
         small = done(sum_all(turn(small))).reshape(-1)
         grad_tokens = done(copy(turn(home_grad)))
         q2_near_x = done(turn(q2_near_x))
         last_mate = send(q2_near_x, core_mate)
+        total_qkv = done(
+            spread((turn(q2), q2_near, quads_mate[0], quads_mate[1]), spread_at, used, 0)
+        )
         total_qkv = spread(
             (q2_x, turn(q2_near_x), quads_mate[2], last_mate), spread_at, used, 1, total_qkv
         ).reshape(wrows, 3 * D)

time: 427 us -> 427 us (level)
    unnamed x73 -> x83, local copies, waits for them, and re-layouts: 10.8 us -> 10.8 us
  transfers between devices with their start and end apart: 48 -> 48, of which waited for: 19 -> 18; matrix products, arithmetic and copies ran while one was open for 3% -> 3% of each run, Pallas kernels for 46% -> 46%
where the time goes in v15:
time: 427 us; the launch traced here: 419 us
  Pallas kernels  223 us (52%)
  waiting for transfers between devices  112 us (26%)
  starting transfers between devices  59.9 us (14%)
  local copies, waits for them, and re-layouts  17.9 us (4%)
  other arithmetic  5.75 us (1%)
    ppermute x47, waiting for transfers between devices, send(): return lax.ppermute(value, AXES, pairs(target))  112 us
    ppermute x47, starting transfers between devices, send(): return lax.ppermute(value, AXES, pairs(target))  50.9 us
    pallas_call x1, Pallas kernels, attn_bwd(): pl.pallas_call(functools.partial(bwd_kernel, first=group * nh, nh=nh, bq=...  43.5 us
    pallas_call x1, Pallas kernels, attn_fwd(): pl.pallas_call(functools.partial(fwd_kernel, nh=nh, bq=bq, bk=bk, nk=n //...  26 us
    pallas_call x2, Pallas kernels, project(): pl.pallas_call(functools.partial(project_kernel, count=count, halves=len(...  22.7 us
    pallas_call x1, Pallas kernels, tail(): pl.pallas_call(body, out_shape=[pltpu.HBM((rows, d), bf16)] + [pltpu.HBM(...  21.5 us
    pallas_call x2, Pallas kernels, share(): pl.pallas_call(share_kernel, out_shape=pltpu.HBM((d, n * w), bf16), grid_...  14.6 us
    pallas_call x1, Pallas kernels, cross(): pl.pallas_call(cross_kernel, out_shape=[pltpu.HBM((w // 2, cols), bf16)]...  11.6 us
  transfers between devices with their start and end apart: 48, of which 18 were waited for; matrix products, arithmetic and copies ran while one was open for 3% of the time, Pallas kernels for 46%

profile of v15, /device:TPU:0, one launch (start us, length us, event | category | flops | bytes accessed | tf_op | source)
XLA Modules:
  0.0 419.5 jit_solution(11215343048395044755)
XLA Ops:
  1.9 7.3 %collective-permute-start.5 = (bf16[512,1280]{1,0:T(8,128)(2,1)}, bf16[512,1280]{1,0:T(8,128)(2,1)}, u32[]{:S(2)}, u32[]{:S(2)}) collective-permute-start(bf16[512,1280]{1,0:T(8,128)(2,1)} %bitcast.69), channel_id=1, source_target_pairs={{0,8},{1,9},{2,10},{3,11},{12,4},{13,5},{14,6},{15,7},{16,24},{17,... | collective-permute-start | bytes 3932168 | tf_op jit(solution)/shard_map/ppermute | solution.py:1031
  9.3 4.4 %pick.1.x_ref.a_ref = bf16[640,1024]{1,0:T(8,128)(2,1)} custom-call(s32[1]{0:T(128)} %bitcast.mine.shard, bf16[640,3840]{1,0:T(8,128)(2,1)} %w_ref.1), custom_call_target="tpu_custom_call" | custom-call | flops 5000000000 | bytes 1000 | tf_op jit(solution)/shard_map/pick/pallas_call | solution.py:352
  15.8 4.2 stretch.2.refs_5_
  30.6 12.3 %collective-permute-done.7.x_ref.b_ref = bf16[640,1024]{1,0:T(8,128)(2,1)} collective-permute-done((bf16[640,1024]{1,0:T(8,128)(2,1)}, bf16[640,1024]{1,0:T(8,128)(2,1)}, u32[]{:S(2)}, u32[]{:S(2)}) %collective-permute-start.7) | collective-permute-done | bytes 1310752 | tf_op jit(solution)/shard_map/ppermute | solution.py:1031
  42.9 4.0 stretch.3.refs_6_
  51.9 11.2 %project.2 = (bf16[2048,1280]{1,0:T(8,128)(2,1)}, bf16[2048,512]{1,0:T(8,128)(2,1)}, bf16[2048,1024]{1,0:T(8,128)(2,1)}, bf16[512,1280]{1,0:T(8,128)(2,1)}) custom-call(s32[5]{0:T(128)S(1)} %stack.103.info, bf16[512,1280]{1,0:T(8,128)(2,1)S(1)} %bitcast.70, bf16[512,1280]{1,0:T(8,128)(2,1)} %collective-permute-done.5.refs_1_, ...), custom_call_target="tpu_custom_call" | custom-call | flops 15000000512 | bytes 1000 | tf_op jit(solution)/shard_map/project/pallas_call | solution.py:518
  63.1 3.6 collective-permute-done.4.refs_2_
  73.4 11.6 %project.3 = (bf16[2048,1280]{1,0:T(8,128)(2,1)}, bf16[2048,512]{1,0:T(8,128)(2,1)}, bf16[2048,1024]{1,0:T(8,128)(2,1)}, bf16[512,1280]{1,0:T(8,128)(2,1)}) custom-call(s32[5]{0:T(128)S(1)} %stack.100.info, bf16[512,1280]{1,0:T(8,128)(2,1)S(1)} %collective-permute-done.2.refs_0_, ...), custom_call_target="tpu_custom_call", output_to_operand_aliasing={{0}: (11, {}), {1}: (12, {}), {2}: (13, {})} | custom-call | flops 15000000512 | bytes 1000 | tf_op jit(solution)/shard_map/project/pallas_call | solution.py:518
  85.0 26.0 %attn_fwd.1 = (bf16[2048,320]{1,0:T(8,128)(2,1)}, bf16[2048,512]{1,0:T(8,128)(2,1)}, bf16[2048,512]{1,0:T(8,128)(2,1)}) custom-call(s32[16]{0:T(128)S(1)} %reshape.183.flags, bf16[2048,512]{1,0:T(8,128)(2,1)} %get-tuple-element.94.q_ref, bf16[2048,1024]{1,0:T(8,128)(2,1)} %get-tuple-element.95.kv.kk.vv, s32[2048,1]{1,0:T(8,128)S(1)} %copy.29.segc, ...), custom_call_target="tpu_custom_call" | custom-call | flops 10000000 | bytes 1000 | tf_op jit(solution)/shard_map/attn_fwd/pallas_call | solution.py:172
  111.0 4.8 %collective-permute-done.9.half = bf16[3,320,1280]{2,1,0:T(8,128)(2,1)} collective-permute-done((bf16[3,320,1280]{2,1,0:T(8,128)(2,1)}, bf16[3,320,1280]{2,1,0:T(8,128)(2,1)}, u32[]{:S(2)}, u32[]{:S(2)}) %collective-permute-start.9) | collective-permute-done | bytes 2457632 | tf_op jit(solution)/shard_map/ppermute | solution.py:1031
  121.4 6.4 %order.1.w_ref = bf16[1024,1280]{1,0:T(8,128)(2,1)} custom-call(s32[1]{0:T(128)} %bitcast.10.own_first, bf16[640,1024]{1,0:T(8,128)(2,1)} %pick.1.x_ref.a_ref, bf16[640,1024]{1,0:T(8,128)(2,1)} %collective-permute-done.7.x_ref.b_ref), custom_call_target="tpu_custom_call" | custom-call | flops 199999995904 | bytes 1000 | tf_op jit(solution)/shard_map/order/pallas_call | solution.py:408
  127.8 7.9 %transpose.15.x_ref = bf16[1280,2048]{1,0:T(8,128)(2,1)} custom-call(bf16[2048,1280]{1,0:T(8,128)(2,1)} %get-tuple-element.103.x_ref), custom_call_target="tpu_custom_call" | custom-call | flops 1000000 | bytes 1000 | tf_op jit(solution)/shard_map/transpose/pallas_call | solution.py:432
  139.1 21.5 %tail.1 = (bf16[512,1280]{1,0:T(8,128)(2,1)}, bf16[3,512,1280]{2,1,0:T(8,128)(2,1)}, bf16[3,512,1280]{2,1,0:T(8,128)(2,1)}, f32[512,1280]{1,0:T(8,128)}, bf16[51...) custom-call(s32[4]{0:T(128)S(1)} %pad_add_fusion.at, ...), custom_call_target="tpu_custom_call" | custom-call | flops 10000000 | bytes 1000 | tf_op jit(solution)/shard_map/tail/pallas_call | solution.py:650
  163.0 7.4 %share.2 = bf16[1280,1920]{1,0:T(8,128)(2,1)} custom-call(s32[1]{0:T(128)} %bitcast.21.col, bf16[3,512,1280]{2,1,0:T(8,128)(2,1)} %get-tuple-element.111.left, bf16[3,512,1280]{2,1,0:T(8,128)(2,1)} %get-tuple-element.112.right), custom_call_target="tpu_custom_call" | custom-call | flops 1000000 | bytes 1000 | tf_op jit(solution)/shard_map/share/pallas_call | solution.py:686
  170.4 7.2 %share.3.a_ref = bf16[1280,1920]{1,0:T(8,128)(2,1)} custom-call(s32[1]{0:T(128)} %bitcast.22.col, bf16[3,512,1280]{2,1,0:T(8,128)(2,1)} %get-tuple-element.111.left, bf16[3,512,1280]{2,1,0:T(8,128)(2,1)} %get-tuple-element.112.right), custom_call_target="tpu_custom_call" | custom-call | flops 1000000 | bytes 1000 | tf_op jit(solution)/shard_map/share/pallas_call | solution.py:686
  182.7 7.7 %add_rows.1 = bf16[1280,1920]{1,0:T(8,128)(2,1)} custom-call(bf16[1280,1920]{1,0:T(8,128)(2,1)} %share.3.a_ref, bf16[1280,1920]{1,0:T(8,128)(2,1)} %collective-permute-done.19.b_ref), custom_call_target="tpu_custom_call" | custom-call | flops 1000000 | bytes 1000 | tf_op jit(solution)/shard_map/add_rows/pallas_call | solution.py:766
  190.4 9.1 %all-to-all-start = ((bf16[8,160,1920]{2,1,0:T(8,128)(2,1)}), bf16[8,160,1920]{2,1,0:T(8,128)(2,1)}, u32[]{:S(2)}, u32[]{:S(2)}) async-start(bf16[8,160,1920]{2,1,0:T(8,128)(2,1)} %bitcast.79), calls=%async_computation | async-start | bytes 9830400 | tf_op jit(solution)/shard_map/all_to_all | solution.py:1201
  199.6 43.5 %attn_bwd.1 = (bf16[2048,1024]{1,0:T(8,128)(2,1)}, f32[8,128]{1,0:T(8,128)}) custom-call(s32[16]{0:T(128)S(1)} %copy-done.17, s32[1]{0:T(128)} %bitcast.mine.shard, bf16[2048,512]{1,0:T(8,128)(2,1)} %get-tuple-element.118.qa, bf16[2048,1024]{1,0:T(8,128)(2,1)} %get-tuple-element.95.kv.kk.vv, bf16[2048,1024]{1,0:T(8,128)(2,1)} %get-tuple-element.95.kv.kk.vv, ...), custom_call_target="tpu_custom_call" | custom-call | flops 299999985664 | bytes 1000 | tf_op jit(solution)/shard_map/attn_bwd/pallas_call | solution.py:314
  243.1 6.8 %back.2 = bf16[2,512,1280]{2,1,0:T(8,128)(2,1)} custom-call(s32[2]{0:T(128)S(1)} %pad_add_fusion.1.shards, bf16[2048,1024]{1,0:T(8,128)(2,1)} %get-tuple-element.127.g_ref, bf16[1024,1280]{1,0:T(8,128)(2,1)} %order.1.w_ref), custom_call_target="tpu_custom_call" | custom-call | flops 1000000 | bytes 1000 | tf_op jit(solution)/shard_map/back/pallas_call | solution.py:924
  249.9 11.6 %cross.1 = (bf16[320,1024]{1,0:T(8,128)(2,1)}, bf16[320,1024]{1,0:T(8,128)(2,1)}, bf16[320,1024]{1,0:T(8,128)(2,1)}, bf16[320,1024]{1,0:T(8,128)(2,1)}) custom-call(s32[2]{0:T(128)S(1)} %pad_add_fusion.2.at, bf16[1280,2048]{1,0:T(8,128)(2,1)} %transpose.15.x_ref, bf16[2048,1024]{1,0:T(8,128)(2,1)} %get-tuple-element.127.g_ref), custom_call_target="tpu_custom_call" | custom-call | flops 1000000 | bytes 1000 | tf_op jit(solution)/shard_map/cross/pallas_call | solution.py:846
  261.5 4.7 %back.3 = bf16[1,512,1280]{2,1,0:T(8,128)(2,1)} custom-call(s32[1]{0:T(128)} %bitcast.26.shards, bf16[2048,1024]{1,0:T(8,128)(2,1)} %get-tuple-element.127.g_ref, bf16[1024,1280]{1,0:T(8,128)(2,1)} %order.1.w_ref, bf16[2,512,1280]{2,1,0:T(8,128)(2,1)S(1)} %collective-permute-done.20.refs_0_.core), custom_call_target="tpu_custom_call" | custom-call | flops 1000000 | bytes 1000 | tf_op jit(solution)/shard_map/back/pallas_call | solution.py:924
  277.9 8.2 %collective-permute-done.22 = bf16[320,1024]{1,0:T(8,128)(2,1)} collective-permute-done((bf16[320,1024]{1,0:T(8,128)(2,1)}, bf16[320,1024]{1,0:T(8,128)(2,1)}, u32[]{:S(2)}, u32[]{:S(2)}) %collective-permute-start.22) | collective-permute-done | bytes 655392 | tf_op jit(solution)/shard_map/ppermute | solution.py:1031
  286.0 14.5 %collective-permute-done.23 = bf16[320,1024]{1,0:T(8,128)(2,1)} collective-permute-done((bf16[320,1024]{1,0:T(8,128)(2,1)}, bf16[320,1024]{1,0:T(8,128)(2,1)}, u32[]{:S(2)}, u32[]{:S(2)}) %collective-permute-start.23) | collective-permute-done | bytes 655392 | tf_op jit(solution)/shard_map/ppermute | solution.py:1031
  303.0 7.8 %collective-permute-done.25.b_ref = bf16[160,1920]{1,0:T(8,128)(2,1)} collective-permute-done((bf16[160,1920]{1,0:T(8,128)(2,1)}, bf16[160,1920]{1,0:T(8,128)(2,1)}, u32[]{:S(2)}, u32[]{:S(2)}) %collective-permute-start.25) | collective-permute-done | bytes 614432 | tf_op jit(solution)/shard_map/ppermute | solution.py:1031
  315.6 6.6 %finish.1 = (bf16[512,1280]{1,0:T(8,128)(2,1)}, f32[1,1280]{1,0:T(1,128)S(1)}) custom-call(s32[1]{0:T(128)} %bitcast.mine.shard, bf16[2048,1024]{1,0:T(8,128)(2,1)} %get-tuple-element.127.g_ref, bf16[1024,1280]{1,0:T(8,128)(2,1)} %order.1.w_ref, bf16[2,512,1280]{2,1,0:T(8,128)(2,1)S(1)} %collective-permute-done.20.refs_0_.core, ...), custom_call_target="tpu_custom_call" | custom-call | flops 1000000 | bytes 1000 | tf_op jit(solution)/shard_map/finish/pallas_call | solution.py:962
  322.2 6.1 %collective-permute-done.27.refs_2_ = bf16[160,1920]{1,0:T(8,128)(2,1)S(1)} collective-permute-done((bf16[160,1920]{1,0:T(8,128)(2,1)}, bf16[160,1920]{1,0:T(8,128)(2,1)S(1)}, u32[]{:S(2)}, u32[]{:S(2)}) %collective-permute-start.27) | collective-permute-done | bytes 614432 | tf_op jit(solution)/shard_map/ppermute | solution.py:1031
  328.3 15.2 %collective-permute-done.26.refs_1_ = bf16[160,1920]{1,0:T(8,128)(2,1)} collective-permute-done((bf16[160,1920]{1,0:T(8,128)(2,1)}, bf16[160,1920]{1,0:T(8,128)(2,1)}, u32[]{:S(2)}, u32[]{:S(2)}) %collective-permute-start.26) | collective-permute-done | bytes 614432 | tf_op jit(solution)/shard_map/ppermute | solution.py:1031
  349.9 18.8 %collective-permute-done.32.refs_1_ = bf16[320,1024]{1,0:T(8,128)(2,1)S(1)} collective-permute-done((bf16[320,1024]{1,0:T(8,128)(2,1)}, bf16[320,1024]{1,0:T(8,128)(2,1)S(1)}, u32[]{:S(2)}, u32[]{:S(2)}) %collective-permute-start.32) | collective-permute-done | bytes 655392 | tf_op jit(solution)/shard_map/ppermute | solution.py:1031
  370.0 4.0 collective-permute-done.30.refs_0_
  383.9 6.1 %place_tail.1 = (f32[4,160,1280]{2,1,0:T(8,128)}, f32[4,160,1280]{2,1,0:T(8,128)}, f32[4,160,1280]{2,1,0:T(8,128)}) custom-call(s32[3]{0:T(128)S(1)} %pad_add_fusion.3.at, bf16[160,1920]{1,0:T(8,128)(2,1)S(1)} %copy-done.1, bf16[160,1920]{1,0:T(8,128)(2,1)} %collective-permute-done.26.refs_1_, bf16[160,1920]{1,0:T(8,128)(2,1)S(1)} %copy-done.5, ...), custom_call_target="tpu_custom_call" | custom-call | flops 1000000 | bytes 1000 | tf_op jit(solution)/shard_map/place_tail/pallas_call | solution.py:809
  398.7 3.8 collective-permute-start.42
  414.6 4.4 %spread.3 = f32[2,320,3840]{2,1,0:T(8,128)} custom-call(s32[3]{0:T(128)S(1)} %pad_add_fusion.5.at, bf16[320,1024]{1,0:T(8,128)(2,1)S(1)} %collective-permute-done.30.refs_0_, bf16[320,1024]{1,0:T(8,128)(2,1)} %collective-permute-done.44.refs_1_, bf16[320,1024]{1,0:T(8,128)(2,1)} %collective-permute-done.45.refs_2_, ...), custom_call_target="tpu_custom_call", output_to_operand_aliasing={{}: (5, {})} | custom-call | flops 1000000 | bytes 1000 | tf_op jit(solution)/shard_map/spread/pallas_call | solution.py:888
  (217 shorter events, 99.4 us)
Async XLA Ops:
  0.6 22.3 %collective-permute-start.1 = (bf16[512,1280]{1,0:T(8,128)(2,1)}, bf16[512,1280]{1,0:T(8,128)(2,1)}, u32[]{:S(2)}, u32[]{:S(2)}) collective-permute-start(bf16[512,1280]{1,0:T(8,128)(2,1)} %bitcast.68), channel_id=1, source_target_pairs={{2,0},{3,1},{4,2},{5,3},{6,4},{7,5},{8,10},{9,11},{10,12},{11,13},... | collective-permute-start | bytes 3932168 | tf_op jit(solution)/shard_map/ppermute | solution.py:1031
  1.9 50.0 %collective-permute-start.5 = (bf16[512,1280]{1,0:T(8,128)(2,1)}, bf16[512,1280]{1,0:T(8,128)(2,1)}, u32[]{:S(2)}, u32[]{:S(2)}) collective-permute-start(bf16[512,1280]{1,0:T(8,128)(2,1)} %bitcast.69), channel_id=1, source_target_pairs={{0,8},{1,9},{2,10},{3,11},{12,4},{13,5},{14,6},{15,7},{16,24},{17,... | collective-permute-start | bytes 3932168 | tf_op jit(solution)/shard_map/ppermute | solution.py:1031
  13.7 29.2 %collective-permute-start.7 = (bf16[640,1024]{1,0:T(8,128)(2,1)}, bf16[640,1024]{1,0:T(8,128)(2,1)}, u32[]{:S(2)}, u32[]{:S(2)}) collective-permute-start(bf16[640,1024]{1,0:T(8,128)(2,1)} %pick.1.x_ref.a_ref), channel_id=1, source_target_pairs={{0,1},{1,0},{2,3},{3,2},{4,5},{5,4},{6,7},{7,6},{8,9},{9,8},{10,11... | collective-permute-start | bytes 3932168 | tf_op jit(solution)/shard_map/ppermute | solution.py:1031
  15.2 55.6 %collective-permute-start = (s32[1,2048]{1,0:T(1,128)S(1)}, s32[1,2048]{1,0:T(1,128)S(1)}, u32[]{:S(2)}, u32[]{:S(2)}) collective-permute-start(s32[1,2048]{1,0:T(1,128)S(1)} %copy-done.33), channel_id=1, source_target_pairs={{0,8},{1,9},{2,10},{3,11},{4,12},{5,13},{6,14},{7,15},{8,0},{9,1},... | collective-permute-start | bytes 24584 | tf_op jit(solution)/shard_map/ppermute | solution.py:1031
  23.0 24.0 %collective-permute-start.2 = (bf16[512,1280]{1,0:T(8,128)(2,1)}, bf16[512,1280]{1,0:T(8,128)(2,1)S(1)}, u32[]{:S(2)}, u32[]{:S(2)}) collective-permute-start(bf16[512,1280]{1,0:T(8,128)(2,1)} %collective-permute-done.1.refs_2_), channel_id=1, source_target_pairs={{2,0},{3,1},{4,2},{5,3},{10,12},{11,13},{12,14},{13,15},{18,16},{1... | collective-permute-start | bytes 3932168 | tf_op jit(solution)/shard_map/ppermute | solution.py:1031
  27.5 24.4 %collective-permute-start.6 = (bf16[512,1280]{1,0:T(8,128)(2,1)}, bf16[512,1280]{1,0:T(8,128)(2,1)}, u32[]{:S(2)}, u32[]{:S(2)}) collective-permute-start(bf16[512,1280]{1,0:T(8,128)(2,1)} %collective-permute-done.1.refs_2_), channel_id=1, source_target_pairs={{0,8},{1,9},{2,10},{3,11},{12,4},{13,5},{14,6},{15,7},{16,24},{17,... | collective-permute-start | bytes 3932168 | tf_op jit(solution)/shard_map/ppermute | solution.py:1031
  47.1 19.6 %collective-permute-start.4 = (bf16[512,1280]{1,0:T(8,128)(2,1)S(1)}, bf16[512,1280]{1,0:T(8,128)(2,1)}, u32[]{:S(2)}, u32[]{:S(2)}) collective-permute-start(bf16[512,1280]{1,0:T(8,128)(2,1)S(1)} %broadcast_select_fusion), channel_id=1, source_target_pairs={{0,2},{1,3},{2,0},{3,1},{12,14},{13,15},{14,12},{15,13},{16,18},{1... | collective-permute-start | bytes 3932168 | tf_op jit(solution)/shard_map/ppermute | solution.py:1031
  49.5 23.9 %collective-permute-start.3 = (bf16[512,1280]{1,0:T(8,128)(2,1)S(1)}, bf16[512,1280]{1,0:T(8,128)(2,1)}, u32[]{:S(2)}, u32[]{:S(2)}) collective-permute-start(bf16[512,1280]{1,0:T(8,128)(2,1)S(1)} %collective-permute-done.2.refs_0_), channel_id=1, source_target_pairs={{0,8},{1,9},{2,10},{3,11},{12,4},{13,5},{14,6},{15,7},{16,24},{17,... | collective-permute-start | bytes 3932168 | tf_op jit(solution)/shard_map/ppermute | solution.py:1031
  69.2 46.5 %collective-permute-start.9 = (bf16[3,320,1280]{2,1,0:T(8,128)(2,1)}, bf16[3,320,1280]{2,1,0:T(8,128)(2,1)}, u32[]{:S(2)}, u32[]{:S(2)}) collective-permute-start(bf16[3,320,1280]{2,1,0:T(8,128)(2,1)} %pad_maximum_fusion), channel_id=1, source_target_pairs={{0,1},{1,0},{2,3},{3,2},{4,5},{5,4},{6,7},{7,6},{8,9},{9,8},{10,11... | collective-permute-start | bytes 7372808 | tf_op jit(solution)/shard_map/ppermute | solution.py:1031
  72.8 42.9 %collective-permute-start.10 = (bf16[512,1280]{1,0:T(8,128)(2,1)}, bf16[512,1280]{1,0:T(8,128)(2,1)S(1)}, u32[]{:S(2)}, u32[]{:S(2)}) collective-permute-start(bf16[512,1280]{1,0:T(8,128)(2,1)} %bitcast.90), channel_id=1, source_target_pairs={{0,8},{1,9},{2,0},{3,1},{4,10},{5,11},{6,2},{7,3},{8,12},{9,13},{1... | collective-permute-start | bytes 3932168 | tf_op jit(solution)/shard_map/ppermute | solution.py:1031
  119.2 16.5 %collective-permute-start.11 = (bf16[512,320]{1,0:T(8,128)(2,1)}, bf16[512,320]{1,0:T(8,128)(2,1)}, u32[]{:S(2)}, u32[]{:S(2)}) collective-permute-start(bf16[512,320]{1,0:T(8,128)(2,1)} %get-tuple-element.173), channel_id=1, source_target_pairs={{0,8},{1,9},{2,10},{3,11},{4,12},{5,13},{6,14},{7,15},{8,0},{9,1},... | collective-permute-start | bytes 983048 | tf_op jit(solution)/shard_map/ppermute | solution.py:1031
  119.2 16.5 %collective-permute-start.12 = (bf16[512,320]{1,0:T(8,128)(2,1)}, bf16[512,320]{1,0:T(8,128)(2,1)}, u32[]{:S(2)}, u32[]{:S(2)}) collective-permute-start(bf16[512,320]{1,0:T(8,128)(2,1)} %get-tuple-element.172), channel_id=1, source_target_pairs={{0,2},{1,3},{2,0},{3,1},{4,6},{5,7},{6,4},{7,5},{8,10},{9,11},{10,... | collective-permute-start | bytes 983048 | tf_op jit(solution)/shard_map/ppermute | solution.py:1031
  119.7 19.4 %collective-permute-start.13 = (bf16[512,320]{1,0:T(8,128)(2,1)}, bf16[512,320]{1,0:T(8,128)(2,1)}, u32[]{:S(2)}, u32[]{:S(2)}) collective-permute-start(bf16[512,320]{1,0:T(8,128)(2,1)} %get-tuple-element.171), channel_id=1, source_target_pairs={{0,10},{1,11},{2,8},{3,9},{4,14},{5,15},{6,12},{7,13},{8,2},{9,3},... | collective-permute-start | bytes 983048 | tf_op jit(solution)/shard_map/ppermute | solution.py:1031
  121.1 18.0 %collective-permute-start.14 = (bf16[3,320,1280]{2,1,0:T(8,128)(2,1)}, bf16[3,320,1280]{2,1,0:T(8,128)(2,1)}, u32[]{:S(2)}, u32[]{:S(2)}) collective-permute-start(bf16[3,320,1280]{2,1,0:T(8,128)(2,1)} %collective-permute-done.9.half), channel_id=1, source_target_pairs={{0,8},{1,9},{2,10},{3,11},{4,12},{5,13},{6,14},{7,15},{8,0},{9,1},... | collective-permute-start | bytes 7372808 | tf_op jit(solution)/shard_map/ppermute | solution.py:1031
  160.9 16.7 %collective-permute-start.17 = (bf16[512,320]{1,0:T(8,128)(2,1)}, bf16[512,320]{1,0:T(8,128)(2,1)S(1)}, u32[]{:S(2)}, u32[]{:S(2)}) collective-permute-start(bf16[512,320]{1,0:T(8,128)(2,1)} %get-tuple-element.115), channel_id=1, source_target_pairs={{0,10},{1,11},{2,8},{3,9},{4,14},{5,15},{6,12},{7,13},{8,2},{9,3},... | collective-permute-start | bytes 983048 | tf_op jit(solution)/shard_map/ppermute | solution.py:1031
  161.2 19.7 %collective-permute-start.16 = (bf16[512,320]{1,0:T(8,128)(2,1)}, bf16[512,320]{1,0:T(8,128)(2,1)S(1)}, u32[]{:S(2)}, u32[]{:S(2)}) collective-permute-start(bf16[512,320]{1,0:T(8,128)(2,1)} %get-tuple-element.109), channel_id=1, source_target_pairs={{0,2},{1,3},{2,0},{3,1},{4,6},{5,7},{6,4},{7,5},{8,10},{9,11},{10,... | collective-permute-start | bytes 983048 | tf_op jit(solution)/shard_map/ppermute | solution.py:1031
  182.2 60.8 %collective-permute-start.18 = (bf16[512,1280]{1,0:T(8,128)(2,1)}, bf16[512,1280]{1,0:T(8,128)(2,1)}, u32[]{:S(2)}, u32[]{:S(2)}) collective-permute-start(bf16[512,1280]{1,0:T(8,128)(2,1)} %get-tuple-element.117), channel_id=1, source_target_pairs={{0,2},{1,3},{2,6},{3,7},{4,10},{5,11},{6,14},{7,15},{8,0},{9,1},{1... | collective-permute-start | bytes 3932168 | tf_op jit(solution)/shard_map/ppermute | solution.py:1031
  190.4 81.2 %all-to-all-start = ((bf16[8,160,1920]{2,1,0:T(8,128)(2,1)}), bf16[8,160,1920]{2,1,0:T(8,128)(2,1)}, u32[]{:S(2)}, u32[]{:S(2)}) async-start(bf16[8,160,1920]{2,1,0:T(8,128)(2,1)} %bitcast.79), calls=%async_computation | async-start | bytes 9830400 | tf_op jit(solution)/shard_map/all_to_all | solution.py:1201
  266.2 49.4 %collective-permute-start.21 = (bf16[1,512,1280]{2,1,0:T(8,128)(2,1)}, bf16[1,512,1280]{2,1,0:T(8,128)(2,1)}, u32[]{:S(2)}, u32[]{:S(2)}) collective-permute-start(bf16[1,512,1280]{2,1,0:T(8,128)(2,1)} %back.3), channel_id=1, source_target_pairs={{0,2},{1,3},{2,0},{3,1},{4,6},{5,7},{6,4},{7,5},{8,10},{9,11},{10,... | collective-permute-start | bytes 3932168 | tf_op jit(solution)/shard_map/ppermute | solution.py:1031
  268.2 17.9 %collective-permute-start.22 = (bf16[320,1024]{1,0:T(8,128)(2,1)}, bf16[320,1024]{1,0:T(8,128)(2,1)}, u32[]{:S(2)}, u32[]{:S(2)}) collective-permute-start(bf16[320,1024]{1,0:T(8,128)(2,1)} %get-tuple-element.133), channel_id=1, source_target_pairs={{0,16},{1,17},{2,18},{3,19},{4,20},{5,21},{6,22},{7,23},{8,24},{9,... | collective-permute-start | bytes 1966088 | tf_op jit(solution)/shard_map/ppermute | solution.py:1031
  269.6 30.9 %collective-permute-start.23 = (bf16[320,1024]{1,0:T(8,128)(2,1)}, bf16[320,1024]{1,0:T(8,128)(2,1)}, u32[]{:S(2)}, u32[]{:S(2)}) collective-permute-start(bf16[320,1024]{1,0:T(8,128)(2,1)} %get-tuple-element.134), channel_id=1, source_target_pairs={{0,1},{1,0},{2,3},{3,2},{4,5},{5,4},{6,7},{7,6},{8,9},{9,8},{10,11... | collective-permute-start | bytes 1966088 | tf_op jit(solution)/shard_map/ppermute | solution.py:1031
  271.1 29.5 %collective-permute-start.24 = (bf16[320,1024]{1,0:T(8,128)(2,1)}, bf16[320,1024]{1,0:T(8,128)(2,1)}, u32[]{:S(2)}, u32[]{:S(2)}) collective-permute-start(bf16[320,1024]{1,0:T(8,128)(2,1)} %get-tuple-element.135), channel_id=1, source_target_pairs={{0,17},{1,16},{2,19},{3,18},{4,21},{5,20},{6,23},{7,22},{8,25},{9,... | collective-permute-start | bytes 1966088 | tf_op jit(solution)/shard_map/ppermute | solution.py:1031
  275.1 35.6 %collective-permute-start.25 = (bf16[160,1920]{1,0:T(8,128)(2,1)}, bf16[160,1920]{1,0:T(8,128)(2,1)}, u32[]{:S(2)}, u32[]{:S(2)}) collective-permute-start(bf16[160,1920]{1,0:T(8,128)(2,1)} %total.2.a_ref), channel_id=1, source_target_pairs={{0,4},{1,5},{2,6},{3,7},{4,0},{5,1},{6,2},{7,3},{8,12},{9,13},{10,... | collective-permute-start | bytes 1843208 | tf_op jit(solution)/shard_map/ppermute | solution.py:1031
  303.0 40.6 %collective-permute-start.28 = (bf16[320,1024]{1,0:T(8,128)(2,1)}, bf16[320,1024]{1,0:T(8,128)(2,1)}, u32[]{:S(2)}, u32[]{:S(2)}) collective-permute-start(bf16[320,1024]{1,0:T(8,128)(2,1)} %total.3.a_ref), channel_id=1, source_target_pairs={{0,4},{1,5},{2,6},{3,7},{4,0},{5,1},{6,2},{7,3},{8,12},{9,13},{10,... | collective-permute-start | bytes 1966088 | tf_op jit(solution)/shard_map/ppermute | solution.py:1031
  314.5 29.1 %collective-permute-start.26 = (bf16[160,1920]{1,0:T(8,128)(2,1)}, bf16[160,1920]{1,0:T(8,128)(2,1)}, u32[]{:S(2)}, u32[]{:S(2)}) collective-permute-start(bf16[160,1920]{1,0:T(8,128)(2,1)} %add.135.refs_0_), channel_id=1, source_target_pairs={{0,2},{1,3},{2,0},{3,1},{4,6},{5,7},{6,4},{7,5},{8,10},{9,11},{10,... | collective-permute-start | bytes 1843208 | tf_op jit(solution)/shard_map/ppermute | solution.py:1031
  345.8 22.9 %collective-permute-start.32 = (bf16[320,1024]{1,0:T(8,128)(2,1)}, bf16[320,1024]{1,0:T(8,128)(2,1)S(1)}, u32[]{:S(2)}, u32[]{:S(2)}) collective-permute-start(bf16[320,1024]{1,0:T(8,128)(2,1)} %add.136.refs_0_), channel_id=1, source_target_pairs={{0,2},{1,3},{2,0},{3,1},{4,6},{5,7},{6,4},{7,5},{8,10},{9,11},{10,... | collective-permute-start | bytes 1966088 | tf_op jit(solution)/shard_map/ppermute | solution.py:1031
  345.8 22.9 %collective-permute-start.31 = (bf16[160,1920]{1,0:T(8,128)(2,1)}, bf16[160,1920]{1,0:T(8,128)(2,1)S(1)}, u32[]{:S(2)}, u32[]{:S(2)}) collective-permute-start(bf16[160,1920]{1,0:T(8,128)(2,1)} %collective-permute-done.26.refs_1_), channel_id=1, source_target_pairs={{0,16},{1,17},{2,18},{3,19},{4,20},{5,21},{6,22},{7,23},{8,24},{9,... | collective-permute-start | bytes 1843208 | tf_op jit(solution)/shard_map/ppermute | solution.py:1031
  346.4 27.6 %collective-permute-start.30 = (bf16[320,1024]{1,0:T(8,128)(2,1)}, bf16[320,1024]{1,0:T(8,128)(2,1)S(1)}, u32[]{:S(2)}, u32[]{:S(2)}) collective-permute-start(bf16[320,1024]{1,0:T(8,128)(2,1)} %add.136.refs_0_), channel_id=1, source_target_pairs={{0,16},{1,17},{2,18},{3,19},{4,20},{5,21},{6,22},{7,23},{8,24},{9,... | collective-permute-start | bytes 1966088 | tf_op jit(solution)/shard_map/ppermute | solution.py:1031
  347.9 26.1 %collective-permute-start.36 = (bf16[160,1920]{1,0:T(8,128)(2,1)S(1)}, bf16[160,1920]{1,0:T(8,128)(2,1)S(1)}, u32[]{:S(2)}, u32[]{:S(2)}) collective-permute-start(bf16[160,1920]{1,0:T(8,128)(2,1)S(1)} %collective-permute-done.27.refs_2_), channel_id=1, source_target_pairs={{0,8},{1,9},{2,10},{3,11},{4,12},{5,13},{6,14},{7,15},{8,0},{9,1},... | collective-permute-start | bytes 1843208 | tf_op jit(solution)/shard_map/ppermute | solution.py:1031
  347.9 60.0 %collective-permute-start.29 = (bf16[512,1280]{1,0:T(8,128)(2,1)}, bf16[512,1280]{1,0:T(8,128)(2,1)}, u32[]{:S(2)}, u32[]{:S(2)}) collective-permute-start(bf16[512,1280]{1,0:T(8,128)(2,1)} %get-tuple-element.143), channel_id=1, source_target_pairs={{0,2},{1,3},{2,6},{3,7},{4,10},{5,11},{6,14},{7,15},{8,0},{9,1},{1... | collective-permute-start | bytes 3932168 | tf_op jit(solution)/shard_map/ppermute | solution.py:1031
  374.0 16.0 %collective-permute-start.33 = (bf16[320,1024]{1,0:T(8,128)(2,1)}, bf16[320,1024]{1,0:T(8,128)(2,1)S(1)}, u32[]{:S(2)}, u32[]{:S(2)}) collective-permute-start(bf16[320,1024]{1,0:T(8,128)(2,1)} %add.136.refs_0_), channel_id=1, source_target_pairs={{0,8},{1,9},{2,10},{3,11},{4,12},{5,13},{6,14},{7,15},{8,0},{9,1},... | collective-permute-start | bytes 1966088 | tf_op jit(solution)/shard_map/ppermute | solution.py:1031
  377.0 33.3 %collective-permute-start.44 = (bf16[320,1024]{1,0:T(8,128)(2,1)S(1)}, bf16[320,1024]{1,0:T(8,128)(2,1)}, u32[]{:S(2)}, u32[]{:S(2)}) collective-permute-start(bf16[320,1024]{1,0:T(8,128)(2,1)S(1)} %collective-permute-done.32.refs_1_), channel_id=1, source_target_pairs={{0,16},{1,17},{2,18},{3,19},{4,20},{5,21},{6,22},{7,23},{8,24},{9,... | collective-permute-start | bytes 1966088 | tf_op jit(solution)/shard_map/ppermute | solution.py:1031
  (56 other events, 629.9 us)

commit v16 on v15

--- a/solution.py
+++ b/solution.py
@@ -818,7 +818,7 @@
         compiler_params=pltpu.CompilerParams(vmem_limit_bytes=16 << 20),
         cost_estimate=CHEAP,
         name="place_tail",
-    )(at, *arrays)
+    )(at, *map(hbm, arrays))
     return [out.reshape(4 * h, d) for out in outs]
 
 

time: 427 us -> 423 us (level)
  local copies, waits for them, and re-layouts: 17.9 us -> 10.2 us
    unnamed x83 -> x71, local copies, waits for them, and re-layouts: 10.8 us -> 3.39 us
  transfers between devices with their start and end apart: 48 -> 48, of which waited for: 18 -> 18; matrix products, arithmetic and copies ran while one was open for 3% -> 2% of each run, Pallas kernels for 46% -> 47%
where the time goes in v16:
time: 423 us; the launch traced here: 416 us
  Pallas kernels  224 us (53%)
  waiting for transfers between devices  115 us (27%)
  starting transfers between devices  59.3 us (14%)
  local copies, waits for them, and re-layouts  10.2 us (2%)
  other arithmetic  5.43 us (1%)
    ppermute x47, waiting for transfers between devices, send(): return lax.ppermute(value, AXES, pairs(target))  115 us
    ppermute x47, starting transfers between devices, send(): return lax.ppermute(value, AXES, pairs(target))  50.2 us
    pallas_call x1, Pallas kernels, attn_bwd(): pl.pallas_call(functools.partial(bwd_kernel, first=group * nh, nh=nh, bq=...  43.5 us
    pallas_call x1, Pallas kernels, attn_fwd(): pl.pallas_call(functools.partial(fwd_kernel, nh=nh, bq=bq, bk=bk, nk=n //...  26 us
    pallas_call x2, Pallas kernels, project(): pl.pallas_call(functools.partial(project_kernel, count=count, halves=len(...  22.8 us
    pallas_call x1, Pallas kernels, tail(): pl.pallas_call(body, out_shape=[pltpu.HBM((rows, d), bf16)] + [pltpu.HBM(...  21.5 us
    pallas_call x2, Pallas kernels, share(): pl.pallas_call(share_kernel, out_shape=pltpu.HBM((d, n * w), bf16), grid_...  14.7 us
    pallas_call x1, Pallas kernels, cross(): pl.pallas_call(cross_kernel, out_shape=[pltpu.HBM((w // 2, cols), bf16)]...  11.6 us
  transfers between devices with their start and end apart: 48, of which 18 were waited for; matrix products, arithmetic and copies ran while one was open for 2% of the time, Pallas kernels for 47%

profile of v16, /device:TPU:0, one launch (start us, length us, event | category | flops | bytes accessed | tf_op | source)
XLA Modules:
  0.0 415.8 jit_solution(9408617676653128657)
XLA Ops:
  1.9 7.3 %collective-permute-start.5 = (bf16[512,1280]{1,0:T(8,128)(2,1)}, bf16[512,1280]{1,0:T(8,128)(2,1)}, u32[]{:S(2)}, u32[]{:S(2)}) collective-permute-start(bf16[512,1280]{1,0:T(8,128)(2,1)} %bitcast.69), channel_id=1, source_target_pairs={{0,8},{1,9},{2,10},{3,11},{12,4},{13,5},{14,6},{15,7},{16,24},{17,... | collective-permute-start | bytes 3932168 | tf_op jit(solution)/shard_map/ppermute | solution.py:1031
  9.3 4.4 %pick.1.x_ref.a_ref = bf16[640,1024]{1,0:T(8,128)(2,1)} custom-call(s32[1]{0:T(128)} %bitcast.mine.shard, bf16[640,3840]{1,0:T(8,128)(2,1)} %w_ref.1), custom_call_target="tpu_custom_call" | custom-call | flops 5000000000 | bytes 1000 | tf_op jit(solution)/shard_map/pick/pallas_call | solution.py:352
  15.8 4.2 stretch.2.refs_5_
  30.0 12.9 %collective-permute-done.7.x_ref.b_ref = bf16[640,1024]{1,0:T(8,128)(2,1)} collective-permute-done((bf16[640,1024]{1,0:T(8,128)(2,1)}, bf16[640,1024]{1,0:T(8,128)(2,1)}, u32[]{:S(2)}, u32[]{:S(2)}) %collective-permute-start.7) | collective-permute-done | bytes 1310752 | tf_op jit(solution)/shard_map/ppermute | solution.py:1031
  42.9 4.0 stretch.3.refs_6_
  51.9 11.2 %project.2 = (bf16[2048,1280]{1,0:T(8,128)(2,1)}, bf16[2048,512]{1,0:T(8,128)(2,1)}, bf16[2048,1024]{1,0:T(8,128)(2,1)}, bf16[512,1280]{1,0:T(8,128)(2,1)}) custom-call(s32[5]{0:T(128)S(1)} %stack.103.info, bf16[512,1280]{1,0:T(8,128)(2,1)S(1)} %bitcast.70, bf16[512,1280]{1,0:T(8,128)(2,1)} %collective-permute-done.5.refs_1_, ...), custom_call_target="tpu_custom_call" | custom-call | flops 15000000512 | bytes 1000 | tf_op jit(solution)/shard_map/project/pallas_call | solution.py:518
  63.1 3.6 collective-permute-done.4.refs_2_
  73.4 11.6 %project.3 = (bf16[2048,1280]{1,0:T(8,128)(2,1)}, bf16[2048,512]{1,0:T(8,128)(2,1)}, bf16[2048,1024]{1,0:T(8,128)(2,1)}, bf16[512,1280]{1,0:T(8,128)(2,1)}) custom-call(s32[5]{0:T(128)S(1)} %stack.100.info, bf16[512,1280]{1,0:T(8,128)(2,1)S(1)} %collective-permute-done.2.refs_0_, ...), custom_call_target="tpu_custom_call", output_to_operand_aliasing={{0}: (11, {}), {1}: (12, {}), {2}: (13, {})} | custom-call | flops 15000000512 | bytes 1000 | tf_op jit(solution)/shard_map/project/pallas_call | solution.py:518
  85.0 26.0 %attn_fwd.1 = (bf16[2048,320]{1,0:T(8,128)(2,1)}, bf16[2048,512]{1,0:T(8,128)(2,1)}, bf16[2048,512]{1,0:T(8,128)(2,1)}) custom-call(s32[16]{0:T(128)S(1)} %reshape.183.flags, bf16[2048,512]{1,0:T(8,128)(2,1)} %get-tuple-element.94.q_ref, bf16[2048,1024]{1,0:T(8,128)(2,1)} %get-tuple-element.95.kv.kk.vv, s32[2048,1]{1,0:T(8,128)S(1)} %copy.29.segc, ...), custom_call_target="tpu_custom_call" | custom-call | flops 10000000 | bytes 1000 | tf_op jit(solution)/shard_map/attn_fwd/pallas_call | solution.py:172
  111.0 4.8 %collective-permute-done.9.half = bf16[3,320,1280]{2,1,0:T(8,128)(2,1)} collective-permute-done((bf16[3,320,1280]{2,1,0:T(8,128)(2,1)}, bf16[3,320,1280]{2,1,0:T(8,128)(2,1)}, u32[]{:S(2)}, u32[]{:S(2)}) %collective-permute-start.9) | collective-permute-done | bytes 2457632 | tf_op jit(solution)/shard_map/ppermute | solution.py:1031
  121.4 6.4 %order.1.w_ref = bf16[1024,1280]{1,0:T(8,128)(2,1)} custom-call(s32[1]{0:T(128)} %bitcast.10.own_first, bf16[640,1024]{1,0:T(8,128)(2,1)} %pick.1.x_ref.a_ref, bf16[640,1024]{1,0:T(8,128)(2,1)} %collective-permute-done.7.x_ref.b_ref), custom_call_target="tpu_custom_call" | custom-call | flops 199999995904 | bytes 1000 | tf_op jit(solution)/shard_map/order/pallas_call | solution.py:408
  127.8 7.9 %transpose.15.x_ref = bf16[1280,2048]{1,0:T(8,128)(2,1)} custom-call(bf16[2048,1280]{1,0:T(8,128)(2,1)} %get-tuple-element.103.x_ref), custom_call_target="tpu_custom_call" | custom-call | flops 1000000 | bytes 1000 | tf_op jit(solution)/shard_map/transpose/pallas_call | solution.py:432
  139.2 21.5 %tail.1 = (bf16[512,1280]{1,0:T(8,128)(2,1)}, bf16[3,512,1280]{2,1,0:T(8,128)(2,1)}, bf16[3,512,1280]{2,1,0:T(8,128)(2,1)}, f32[512,1280]{1,0:T(8,128)}, bf16[51...) custom-call(s32[4]{0:T(128)S(1)} %pad_add_fusion.at, ...), custom_call_target="tpu_custom_call" | custom-call | flops 10000000 | bytes 1000 | tf_op jit(solution)/shard_map/tail/pallas_call | solution.py:650
  163.0 7.5 %share.2 = bf16[1280,1920]{1,0:T(8,128)(2,1)} custom-call(s32[1]{0:T(128)} %bitcast.21.col, bf16[3,512,1280]{2,1,0:T(8,128)(2,1)} %get-tuple-element.111.left, bf16[3,512,1280]{2,1,0:T(8,128)(2,1)} %get-tuple-element.112.right), custom_call_target="tpu_custom_call" | custom-call | flops 1000000 | bytes 1000 | tf_op jit(solution)/shard_map/share/pallas_call | solution.py:686
  170.5 7.2 %share.3.a_ref = bf16[1280,1920]{1,0:T(8,128)(2,1)} custom-call(s32[1]{0:T(128)} %bitcast.22.col, bf16[3,512,1280]{2,1,0:T(8,128)(2,1)} %get-tuple-element.111.left, bf16[3,512,1280]{2,1,0:T(8,128)(2,1)} %get-tuple-element.112.right), custom_call_target="tpu_custom_call" | custom-call | flops 1000000 | bytes 1000 | tf_op jit(solution)/shard_map/share/pallas_call | solution.py:686
  182.7 7.8 %add_rows.1 = bf16[1280,1920]{1,0:T(8,128)(2,1)} custom-call(bf16[1280,1920]{1,0:T(8,128)(2,1)} %share.3.a_ref, bf16[1280,1920]{1,0:T(8,128)(2,1)} %collective-permute-done.19.b_ref), custom_call_target="tpu_custom_call" | custom-call | flops 1000000 | bytes 1000 | tf_op jit(solution)/shard_map/add_rows/pallas_call | solution.py:766
  190.5 9.1 %all-to-all-start = ((bf16[8,160,1920]{2,1,0:T(8,128)(2,1)}), bf16[8,160,1920]{2,1,0:T(8,128)(2,1)}, u32[]{:S(2)}, u32[]{:S(2)}) async-start(bf16[8,160,1920]{2,1,0:T(8,128)(2,1)} %bitcast.79), calls=%async_computation | async-start | bytes 9830400 | tf_op jit(solution)/shard_map/all_to_all | solution.py:1201
  199.6 43.5 %attn_bwd.1 = (bf16[2048,1024]{1,0:T(8,128)(2,1)}, f32[8,128]{1,0:T(8,128)}) custom-call(s32[16]{0:T(128)S(1)} %copy-done.6, s32[1]{0:T(128)} %bitcast.mine.shard, bf16[2048,512]{1,0:T(8,128)(2,1)} %get-tuple-element.118.qa, bf16[2048,1024]{1,0:T(8,128)(2,1)} %get-tuple-element.95.kv.kk.vv, bf16[2048,1024]{1,0:T(8,128)(2,1)} %get-tuple-element.95.kv.kk.vv, ...), custom_call_target="tpu_custom_call" | custom-call | flops 299999985664 | bytes 1000 | tf_op jit(solution)/shard_map/attn_bwd/pallas_call | solution.py:314
  243.2 6.8 %back.2 = bf16[2,512,1280]{2,1,0:T(8,128)(2,1)} custom-call(s32[2]{0:T(128)S(1)} %pad_add_fusion.1.shards, bf16[2048,1024]{1,0:T(8,128)(2,1)} %get-tuple-element.127.g_ref, bf16[1024,1280]{1,0:T(8,128)(2,1)} %order.1.w_ref), custom_call_target="tpu_custom_call" | custom-call | flops 1000000 | bytes 1000 | tf_op jit(solution)/shard_map/back/pallas_call | solution.py:924
  250.0 11.6 %cross.1 = (bf16[320,1024]{1,0:T(8,128)(2,1)}, bf16[320,1024]{1,0:T(8,128)(2,1)}, bf16[320,1024]{1,0:T(8,128)(2,1)}, bf16[320,1024]{1,0:T(8,128)(2,1)}) custom-call(s32[2]{0:T(128)S(1)} %pad_add_fusion.2.at, bf16[1280,2048]{1,0:T(8,128)(2,1)} %transpose.15.x_ref, bf16[2048,1024]{1,0:T(8,128)(2,1)} %get-tuple-element.127.g_ref), custom_call_target="tpu_custom_call" | custom-call | flops 1000000 | bytes 1000 | tf_op jit(solution)/shard_map/cross/pallas_call | solution.py:846
  261.6 4.7 %back.3 = bf16[1,512,1280]{2,1,0:T(8,128)(2,1)} custom-call(s32[1]{0:T(128)} %bitcast.26.shards, bf16[2048,1024]{1,0:T(8,128)(2,1)} %get-tuple-element.127.g_ref, bf16[1024,1280]{1,0:T(8,128)(2,1)} %order.1.w_ref, bf16[2,512,1280]{2,1,0:T(8,128)(2,1)S(1)} %collective-permute-done.20.refs_0_.core), custom_call_target="tpu_custom_call" | custom-call | flops 1000000 | bytes 1000 | tf_op jit(solution)/shard_map/back/pallas_call | solution.py:924
  277.9 8.3 %collective-permute-done.22 = bf16[320,1024]{1,0:T(8,128)(2,1)} collective-permute-done((bf16[320,1024]{1,0:T(8,128)(2,1)}, bf16[320,1024]{1,0:T(8,128)(2,1)}, u32[]{:S(2)}, u32[]{:S(2)}) %collective-permute-start.22) | collective-permute-done | bytes 655392 | tf_op jit(solution)/shard_map/ppermute | solution.py:1031
  286.2 14.5 %collective-permute-done.23 = bf16[320,1024]{1,0:T(8,128)(2,1)} collective-permute-done((bf16[320,1024]{1,0:T(8,128)(2,1)}, bf16[320,1024]{1,0:T(8,128)(2,1)}, u32[]{:S(2)}, u32[]{:S(2)}) %collective-permute-start.23) | collective-permute-done | bytes 655392 | tf_op jit(solution)/shard_map/ppermute | solution.py:1031
  303.1 7.8 %collective-permute-done.25.b_ref = bf16[160,1920]{1,0:T(8,128)(2,1)} collective-permute-done((bf16[160,1920]{1,0:T(8,128)(2,1)}, bf16[160,1920]{1,0:T(8,128)(2,1)}, u32[]{:S(2)}, u32[]{:S(2)}) %collective-permute-start.25) | collective-permute-done | bytes 614432 | tf_op jit(solution)/shard_map/ppermute | solution.py:1031
  315.7 6.6 %finish.1 = (bf16[512,1280]{1,0:T(8,128)(2,1)}, f32[1,1280]{1,0:T(1,128)S(1)}) custom-call(s32[1]{0:T(128)} %bitcast.mine.shard, bf16[2048,1024]{1,0:T(8,128)(2,1)} %get-tuple-element.127.g_ref, bf16[1024,1280]{1,0:T(8,128)(2,1)} %order.1.w_ref, bf16[2,512,1280]{2,1,0:T(8,128)(2,1)S(1)} %collective-permute-done.20.refs_0_.core, ...), custom_call_target="tpu_custom_call" | custom-call | flops 1000000 | bytes 1000 | tf_op jit(solution)/shard_map/finish/pallas_call | solution.py:962
  322.3 6.2 %collective-permute-done.27.refs_2_ = bf16[160,1920]{1,0:T(8,128)(2,1)} collective-permute-done((bf16[160,1920]{1,0:T(8,128)(2,1)}, bf16[160,1920]{1,0:T(8,128)(2,1)}, u32[]{:S(2)}, u32[]{:S(2)}) %collective-permute-start.27) | collective-permute-done | bytes 614432 | tf_op jit(solution)/shard_map/ppermute | solution.py:1031
  328.6 15.1 %collective-permute-done.26.refs_1_ = bf16[160,1920]{1,0:T(8,128)(2,1)} collective-permute-done((bf16[160,1920]{1,0:T(8,128)(2,1)}, bf16[160,1920]{1,0:T(8,128)(2,1)}, u32[]{:S(2)}, u32[]{:S(2)}) %collective-permute-start.26) | collective-permute-done | bytes 614432 | tf_op jit(solution)/shard_map/ppermute | solution.py:1031
  350.0 18.8 %collective-permute-done.32.refs_1_ = bf16[320,1024]{1,0:T(8,128)(2,1)S(1)} collective-permute-done((bf16[320,1024]{1,0:T(8,128)(2,1)}, bf16[320,1024]{1,0:T(8,128)(2,1)S(1)}, u32[]{:S(2)}, u32[]{:S(2)}) %collective-permute-start.32) | collective-permute-done | bytes 655392 | tf_op jit(solution)/shard_map/ppermute | solution.py:1031
  369.3 4.8 %collective-permute-done.30.refs_0_ = bf16[320,1024]{1,0:T(8,128)(2,1)S(1)} collective-permute-done((bf16[320,1024]{1,0:T(8,128)(2,1)}, bf16[320,1024]{1,0:T(8,128)(2,1)S(1)}, u32[]{:S(2)}, u32[]{:S(2)}) %collective-permute-start.30) | collective-permute-done | bytes 655392 | tf_op jit(solution)/shard_map/ppermute | solution.py:1031
  379.1 7.2 %place_tail.1 = (f32[4,160,1280]{2,1,0:T(8,128)}, f32[4,160,1280]{2,1,0:T(8,128)}, f32[4,160,1280]{2,1,0:T(8,128)}) custom-call(s32[3]{0:T(128)S(1)} %pad_add_fusion.3.at, bf16[160,1920]{1,0:T(8,128)(2,1)} %add.135.refs_0_, bf16[160,1920]{1,0:T(8,128)(2,1)} %collective-permute-done.26.refs_1_, bf16[160,1920]{1,0:T(8,128)(2,1)} %collective-permute-done.27.refs_2_, ...), custom_call_target="tpu_custom_call" | custom-call | flops 1000000 | bytes 1000 | tf_op jit(solution)/shard_map/place_tail/pallas_call | solution.py:809
  395.0 3.8 collective-permute-start.42
  410.9 4.4 %spread.3 = f32[2,320,3840]{2,1,0:T(8,128)} custom-call(s32[3]{0:T(128)S(1)} %pad_add_fusion.5.at, bf16[320,1024]{1,0:T(8,128)(2,1)S(1)} %collective-permute-done.30.refs_0_, bf16[320,1024]{1,0:T(8,128)(2,1)} %collective-permute-done.44.refs_1_, bf16[320,1024]{1,0:T(8,128)(2,1)} %collective-permute-done.45.refs_2_, ...), custom_call_target="tpu_custom_call", output_to_operand_aliasing={{}: (5, {})} | custom-call | flops 1000000 | bytes 1000 | tf_op jit(solution)/shard_map/spread/pallas_call | solution.py:888
  (205 shorter events, 92.9 us)
Async XLA Ops:
  0.6 22.0 %collective-permute-start.1 = (bf16[512,1280]{1,0:T(8,128)(2,1)}, bf16[512,1280]{1,0:T(8,128)(2,1)}, u32[]{:S(2)}, u32[]{:S(2)}) collective-permute-start(bf16[512,1280]{1,0:T(8,128)(2,1)} %bitcast.68), channel_id=1, source_target_pairs={{2,0},{3,1},{4,2},{5,3},{6,4},{7,5},{8,10},{9,11},{10,12},{11,13},... | collective-permute-start | bytes 3932168 | tf_op jit(solution)/shard_map/ppermute | solution.py:1031
  1.9 49.9 %collective-permute-start.5 = (bf16[512,1280]{1,0:T(8,128)(2,1)}, bf16[512,1280]{1,0:T(8,128)(2,1)}, u32[]{:S(2)}, u32[]{:S(2)}) collective-permute-start(bf16[512,1280]{1,0:T(8,128)(2,1)} %bitcast.69), channel_id=1, source_target_pairs={{0,8},{1,9},{2,10},{3,11},{12,4},{13,5},{14,6},{15,7},{16,24},{17,... | collective-permute-start | bytes 3932168 | tf_op jit(solution)/shard_map/ppermute | solution.py:1031
  13.7 29.2 %collective-permute-start.7 = (bf16[640,1024]{1,0:T(8,128)(2,1)}, bf16[640,1024]{1,0:T(8,128)(2,1)}, u32[]{:S(2)}, u32[]{:S(2)}) collective-permute-start(bf16[640,1024]{1,0:T(8,128)(2,1)} %pick.1.x_ref.a_ref), channel_id=1, source_target_pairs={{0,1},{1,0},{2,3},{3,2},{4,5},{5,4},{6,7},{7,6},{8,9},{9,8},{10,11... | collective-permute-start | bytes 3932168 | tf_op jit(solution)/shard_map/ppermute | solution.py:1031
  15.2 55.6 %collective-permute-start = (s32[1,2048]{1,0:T(1,128)S(1)}, s32[1,2048]{1,0:T(1,128)S(1)}, u32[]{:S(2)}, u32[]{:S(2)}) collective-permute-start(s32[1,2048]{1,0:T(1,128)S(1)} %copy-done.27), channel_id=1, source_target_pairs={{0,8},{1,9},{2,10},{3,11},{4,12},{5,13},{6,14},{7,15},{8,0},{9,1},... | collective-permute-start | bytes 24584 | tf_op jit(solution)/shard_map/ppermute | solution.py:1031
  22.7 24.3 %collective-permute-start.2 = (bf16[512,1280]{1,0:T(8,128)(2,1)}, bf16[512,1280]{1,0:T(8,128)(2,1)S(1)}, u32[]{:S(2)}, u32[]{:S(2)}) collective-permute-start(bf16[512,1280]{1,0:T(8,128)(2,1)} %collective-permute-done.1.refs_2_), channel_id=1, source_target_pairs={{2,0},{3,1},{4,2},{5,3},{10,12},{11,13},{12,14},{13,15},{18,16},{1... | collective-permute-start | bytes 3932168 | tf_op jit(solution)/shard_map/ppermute | solution.py:1031
  27.0 24.9 %collective-permute-start.6 = (bf16[512,1280]{1,0:T(8,128)(2,1)}, bf16[512,1280]{1,0:T(8,128)(2,1)}, u32[]{:S(2)}, u32[]{:S(2)}) collective-permute-start(bf16[512,1280]{1,0:T(8,128)(2,1)} %collective-permute-done.1.refs_2_), channel_id=1, source_target_pairs={{0,8},{1,9},{2,10},{3,11},{12,4},{13,5},{14,6},{15,7},{16,24},{17,... | collective-permute-start | bytes 3932168 | tf_op jit(solution)/shard_map/ppermute | solution.py:1031
  47.1 19.6 %collective-permute-start.4 = (bf16[512,1280]{1,0:T(8,128)(2,1)S(1)}, bf16[512,1280]{1,0:T(8,128)(2,1)}, u32[]{:S(2)}, u32[]{:S(2)}) collective-permute-start(bf16[512,1280]{1,0:T(8,128)(2,1)S(1)} %broadcast_select_fusion), channel_id=1, source_target_pairs={{0,2},{1,3},{2,0},{3,1},{12,14},{13,15},{14,12},{15,13},{16,18},{1... | collective-permute-start | bytes 3932168 | tf_op jit(solution)/shard_map/ppermute | solution.py:1031
  49.5 24.0 %collective-permute-start.3 = (bf16[512,1280]{1,0:T(8,128)(2,1)S(1)}, bf16[512,1280]{1,0:T(8,128)(2,1)}, u32[]{:S(2)}, u32[]{:S(2)}) collective-permute-start(bf16[512,1280]{1,0:T(8,128)(2,1)S(1)} %collective-permute-done.2.refs_0_), channel_id=1, source_target_pairs={{0,8},{1,9},{2,10},{3,11},{12,4},{13,5},{14,6},{15,7},{16,24},{17,... | collective-permute-start | bytes 3932168 | tf_op jit(solution)/shard_map/ppermute | solution.py:1031
  69.2 46.5 %collective-permute-start.9 = (bf16[3,320,1280]{2,1,0:T(8,128)(2,1)}, bf16[3,320,1280]{2,1,0:T(8,128)(2,1)}, u32[]{:S(2)}, u32[]{:S(2)}) collective-permute-start(bf16[3,320,1280]{2,1,0:T(8,128)(2,1)} %pad_maximum_fusion), channel_id=1, source_target_pairs={{0,1},{1,0},{2,3},{3,2},{4,5},{5,4},{6,7},{7,6},{8,9},{9,8},{10,11... | collective-permute-start | bytes 7372808 | tf_op jit(solution)/shard_map/ppermute | solution.py:1031
  72.8 43.0 %collective-permute-start.10 = (bf16[512,1280]{1,0:T(8,128)(2,1)}, bf16[512,1280]{1,0:T(8,128)(2,1)S(1)}, u32[]{:S(2)}, u32[]{:S(2)}) collective-permute-start(bf16[512,1280]{1,0:T(8,128)(2,1)} %bitcast.90), channel_id=1, source_target_pairs={{0,8},{1,9},{2,0},{3,1},{4,10},{5,11},{6,2},{7,3},{8,12},{9,13},{1... | collective-permute-start | bytes 3932168 | tf_op jit(solution)/shard_map/ppermute | solution.py:1031
  119.3 16.5 %collective-permute-start.11 = (bf16[512,320]{1,0:T(8,128)(2,1)}, bf16[512,320]{1,0:T(8,128)(2,1)}, u32[]{:S(2)}, u32[]{:S(2)}) collective-permute-start(bf16[512,320]{1,0:T(8,128)(2,1)} %get-tuple-element.173), channel_id=1, source_target_pairs={{0,8},{1,9},{2,10},{3,11},{4,12},{5,13},{6,14},{7,15},{8,0},{9,1},... | collective-permute-start | bytes 983048 | tf_op jit(solution)/shard_map/ppermute | solution.py:1031
  119.3 16.5 %collective-permute-start.12 = (bf16[512,320]{1,0:T(8,128)(2,1)}, bf16[512,320]{1,0:T(8,128)(2,1)}, u32[]{:S(2)}, u32[]{:S(2)}) collective-permute-start(bf16[512,320]{1,0:T(8,128)(2,1)} %get-tuple-element.172), channel_id=1, source_target_pairs={{0,2},{1,3},{2,0},{3,1},{4,6},{5,7},{6,4},{7,5},{8,10},{9,11},{10,... | collective-permute-start | bytes 983048 | tf_op jit(solution)/shard_map/ppermute | solution.py:1031
  119.7 19.5 %collective-permute-start.13 = (bf16[512,320]{1,0:T(8,128)(2,1)}, bf16[512,320]{1,0:T(8,128)(2,1)}, u32[]{:S(2)}, u32[]{:S(2)}) collective-permute-start(bf16[512,320]{1,0:T(8,128)(2,1)} %get-tuple-element.171), channel_id=1, source_target_pairs={{0,10},{1,11},{2,8},{3,9},{4,14},{5,15},{6,12},{7,13},{8,2},{9,3},... | collective-permute-start | bytes 983048 | tf_op jit(solution)/shard_map/ppermute | solution.py:1031
  121.1 18.0 %collective-permute-start.14 = (bf16[3,320,1280]{2,1,0:T(8,128)(2,1)}, bf16[3,320,1280]{2,1,0:T(8,128)(2,1)}, u32[]{:S(2)}, u32[]{:S(2)}) collective-permute-start(bf16[3,320,1280]{2,1,0:T(8,128)(2,1)} %collective-permute-done.9.half), channel_id=1, source_target_pairs={{0,8},{1,9},{2,10},{3,11},{4,12},{5,13},{6,14},{7,15},{8,0},{9,1},... | collective-permute-start | bytes 7372808 | tf_op jit(solution)/shard_map/ppermute | solution.py:1031
  161.0 16.8 %collective-permute-start.17 = (bf16[512,320]{1,0:T(8,128)(2,1)}, bf16[512,320]{1,0:T(8,128)(2,1)S(1)}, u32[]{:S(2)}, u32[]{:S(2)}) collective-permute-start(bf16[512,320]{1,0:T(8,128)(2,1)} %get-tuple-element.115), channel_id=1, source_target_pairs={{0,10},{1,11},{2,8},{3,9},{4,14},{5,15},{6,12},{7,13},{8,2},{9,3},... | collective-permute-start | bytes 983048 | tf_op jit(solution)/shard_map/ppermute | solution.py:1031
  161.3 19.8 %collective-permute-start.16 = (bf16[512,320]{1,0:T(8,128)(2,1)}, bf16[512,320]{1,0:T(8,128)(2,1)S(1)}, u32[]{:S(2)}, u32[]{:S(2)}) collective-permute-start(bf16[512,320]{1,0:T(8,128)(2,1)} %get-tuple-element.109), channel_id=1, source_target_pairs={{0,2},{1,3},{2,0},{3,1},{4,6},{5,7},{6,4},{7,5},{8,10},{9,11},{10,... | collective-permute-start | bytes 983048 | tf_op jit(solution)/shard_map/ppermute | solution.py:1031
  182.3 60.9 %collective-permute-start.18 = (bf16[512,1280]{1,0:T(8,128)(2,1)}, bf16[512,1280]{1,0:T(8,128)(2,1)}, u32[]{:S(2)}, u32[]{:S(2)}) collective-permute-start(bf16[512,1280]{1,0:T(8,128)(2,1)} %get-tuple-element.117), channel_id=1, source_target_pairs={{0,2},{1,3},{2,6},{3,7},{4,10},{5,11},{6,14},{7,15},{8,0},{9,1},{1... | collective-permute-start | bytes 3932168 | tf_op jit(solution)/shard_map/ppermute | solution.py:1031
  190.5 81.3 %all-to-all-start = ((bf16[8,160,1920]{2,1,0:T(8,128)(2,1)}), bf16[8,160,1920]{2,1,0:T(8,128)(2,1)}, u32[]{:S(2)}, u32[]{:S(2)}) async-start(bf16[8,160,1920]{2,1,0:T(8,128)(2,1)} %bitcast.79), calls=%async_computation | async-start | bytes 9830400 | tf_op jit(solution)/shard_map/all_to_all | solution.py:1201
  266.3 49.4 %collective-permute-start.21 = (bf16[1,512,1280]{2,1,0:T(8,128)(2,1)}, bf16[1,512,1280]{2,1,0:T(8,128)(2,1)}, u32[]{:S(2)}, u32[]{:S(2)}) collective-permute-start(bf16[1,512,1280]{2,1,0:T(8,128)(2,1)} %back.3), channel_id=1, source_target_pairs={{0,2},{1,3},{2,0},{3,1},{4,6},{5,7},{6,4},{7,5},{8,10},{9,11},{10,... | collective-permute-start | bytes 3932168 | tf_op jit(solution)/shard_map/ppermute | solution.py:1031
  268.3 17.9 %collective-permute-start.22 = (bf16[320,1024]{1,0:T(8,128)(2,1)}, bf16[320,1024]{1,0:T(8,128)(2,1)}, u32[]{:S(2)}, u32[]{:S(2)}) collective-permute-start(bf16[320,1024]{1,0:T(8,128)(2,1)} %get-tuple-element.133), channel_id=1, source_target_pairs={{0,16},{1,17},{2,18},{3,19},{4,20},{5,21},{6,22},{7,23},{8,24},{9,... | collective-permute-start | bytes 1966088 | tf_op jit(solution)/shard_map/ppermute | solution.py:1031
  269.8 30.9 %collective-permute-start.23 = (bf16[320,1024]{1,0:T(8,128)(2,1)}, bf16[320,1024]{1,0:T(8,128)(2,1)}, u32[]{:S(2)}, u32[]{:S(2)}) collective-permute-start(bf16[320,1024]{1,0:T(8,128)(2,1)} %get-tuple-element.134), channel_id=1, source_target_pairs={{0,1},{1,0},{2,3},{3,2},{4,5},{5,4},{6,7},{7,6},{8,9},{9,8},{10,11... | collective-permute-start | bytes 1966088 | tf_op jit(solution)/shard_map/ppermute | solution.py:1031
  271.2 29.5 %collective-permute-start.24 = (bf16[320,1024]{1,0:T(8,128)(2,1)}, bf16[320,1024]{1,0:T(8,128)(2,1)}, u32[]{:S(2)}, u32[]{:S(2)}) collective-permute-start(bf16[320,1024]{1,0:T(8,128)(2,1)} %get-tuple-element.135), channel_id=1, source_target_pairs={{0,17},{1,16},{2,19},{3,18},{4,21},{5,20},{6,23},{7,22},{8,25},{9,... | collective-permute-start | bytes 1966088 | tf_op jit(solution)/shard_map/ppermute | solution.py:1031
  275.2 35.7 %collective-permute-start.25 = (bf16[160,1920]{1,0:T(8,128)(2,1)}, bf16[160,1920]{1,0:T(8,128)(2,1)}, u32[]{:S(2)}, u32[]{:S(2)}) collective-permute-start(bf16[160,1920]{1,0:T(8,128)(2,1)} %total.2.a_ref), channel_id=1, source_target_pairs={{0,4},{1,5},{2,6},{3,7},{4,0},{5,1},{6,2},{7,3},{8,12},{9,13},{10,... | collective-permute-start | bytes 1843208 | tf_op jit(solution)/shard_map/ppermute | solution.py:1031
  303.1 40.6 %collective-permute-start.28 = (bf16[320,1024]{1,0:T(8,128)(2,1)}, bf16[320,1024]{1,0:T(8,128)(2,1)}, u32[]{:S(2)}, u32[]{:S(2)}) collective-permute-start(bf16[320,1024]{1,0:T(8,128)(2,1)} %total.3.a_ref), channel_id=1, source_target_pairs={{0,4},{1,5},{2,6},{3,7},{4,0},{5,1},{6,2},{7,3},{8,12},{9,13},{10,... | collective-permute-start | bytes 1966088 | tf_op jit(solution)/shard_map/ppermute | solution.py:1031
  313.1 15.4 %collective-permute-start.27 = (bf16[160,1920]{1,0:T(8,128)(2,1)}, bf16[160,1920]{1,0:T(8,128)(2,1)}, u32[]{:S(2)}, u32[]{:S(2)}) collective-permute-start(bf16[160,1920]{1,0:T(8,128)(2,1)} %add.135.refs_0_), channel_id=1, source_target_pairs={{0,16},{1,17},{2,18},{3,19},{4,20},{5,21},{6,22},{7,23},{8,24},{9,... | collective-permute-start | bytes 1843208 | tf_op jit(solution)/shard_map/ppermute | solution.py:1031
  314.6 29.1 %collective-permute-start.26 = (bf16[160,1920]{1,0:T(8,128)(2,1)}, bf16[160,1920]{1,0:T(8,128)(2,1)}, u32[]{:S(2)}, u32[]{:S(2)}) collective-permute-start(bf16[160,1920]{1,0:T(8,128)(2,1)} %add.135.refs_0_), channel_id=1, source_target_pairs={{0,2},{1,3},{2,0},{3,1},{4,6},{5,7},{6,4},{7,5},{8,10},{9,11},{10,... | collective-permute-start | bytes 1843208 | tf_op jit(solution)/shard_map/ppermute | solution.py:1031
  346.0 22.9 %collective-permute-start.32 = (bf16[320,1024]{1,0:T(8,128)(2,1)}, bf16[320,1024]{1,0:T(8,128)(2,1)S(1)}, u32[]{:S(2)}, u32[]{:S(2)}) collective-permute-start(bf16[320,1024]{1,0:T(8,128)(2,1)} %add.136.refs_0_), channel_id=1, source_target_pairs={{0,2},{1,3},{2,0},{3,1},{4,6},{5,7},{6,4},{7,5},{8,10},{9,11},{10,... | collective-permute-start | bytes 1966088 | tf_op jit(solution)/shard_map/ppermute | solution.py:1031
  346.0 22.9 %collective-permute-start.31 = (bf16[160,1920]{1,0:T(8,128)(2,1)}, bf16[160,1920]{1,0:T(8,128)(2,1)S(1)}, u32[]{:S(2)}, u32[]{:S(2)}) collective-permute-start(bf16[160,1920]{1,0:T(8,128)(2,1)} %collective-permute-done.26.refs_1_), channel_id=1, source_target_pairs={{0,16},{1,17},{2,18},{3,19},{4,20},{5,21},{6,22},{7,23},{8,24},{9,... | collective-permute-start | bytes 1843208 | tf_op jit(solution)/shard_map/ppermute | solution.py:1031
  346.5 27.6 %collective-permute-start.30 = (bf16[320,1024]{1,0:T(8,128)(2,1)}, bf16[320,1024]{1,0:T(8,128)(2,1)S(1)}, u32[]{:S(2)}, u32[]{:S(2)}) collective-permute-start(bf16[320,1024]{1,0:T(8,128)(2,1)} %add.136.refs_0_), channel_id=1, source_target_pairs={{0,16},{1,17},{2,18},{3,19},{4,20},{5,21},{6,22},{7,23},{8,24},{9,... | collective-permute-start | bytes 1966088 | tf_op jit(solution)/shard_map/ppermute | solution.py:1031
  348.0 26.1 %collective-permute-start.36 = (bf16[160,1920]{1,0:T(8,128)(2,1)}, bf16[160,1920]{1,0:T(8,128)(2,1)}, u32[]{:S(2)}, u32[]{:S(2)}) collective-permute-start(bf16[160,1920]{1,0:T(8,128)(2,1)} %collective-permute-done.27.refs_2_), channel_id=1, source_target_pairs={{0,8},{1,9},{2,10},{3,11},{4,12},{5,13},{6,14},{7,15},{8,0},{9,1},... | collective-permute-start | bytes 1843208 | tf_op jit(solution)/shard_map/ppermute | solution.py:1031
  348.0 56.1 %collective-permute-start.29 = (bf16[512,1280]{1,0:T(8,128)(2,1)}, bf16[512,1280]{1,0:T(8,128)(2,1)}, u32[]{:S(2)}, u32[]{:S(2)}) collective-permute-start(bf16[512,1280]{1,0:T(8,128)(2,1)} %get-tuple-element.143), channel_id=1, source_target_pairs={{0,2},{1,3},{2,6},{3,7},{4,10},{5,11},{6,14},{7,15},{8,0},{9,1},{1... | collective-permute-start | bytes 3932168 | tf_op jit(solution)/shard_map/ppermute | solution.py:1031
  374.7 31.9 %collective-permute-start.44 = (bf16[320,1024]{1,0:T(8,128)(2,1)S(1)}, bf16[320,1024]{1,0:T(8,128)(2,1)}, u32[]{:S(2)}, u32[]{:S(2)}) collective-permute-start(bf16[320,1024]{1,0:T(8,128)(2,1)S(1)} %collective-permute-done.32.refs_1_), channel_id=1, source_target_pairs={{0,16},{1,17},{2,18},{3,19},{4,20},{5,21},{6,22},{7,23},{8,24},{9,... | collective-permute-start | bytes 1966088 | tf_op jit(solution)/shard_map/ppermute | solution.py:1031
  (50 other events, 572.1 us)

commit v17 on v16

--- a/solution.py
+++ b/solution.py
@@ -1298,12 +1298,13 @@
         spread_at = jnp.stack([gx, near, 1 - gc])
         quads_mate[0] = done(after(turn(quads_mate[0]), quads_mate[1]))
         small = done(sum_all(turn(small))).reshape(-1)
-        grad_tokens = done(copy(turn(home_grad)))
+        home_grad = done(turn(home_grad))
         q2_near_x = done(turn(q2_near_x))
         last_mate = send(q2_near_x, core_mate)
         total_qkv = done(
             spread((turn(q2), q2_near, quads_mate[0], quads_mate[1]), spread_at, used, 0)
         )
+        grad_tokens = done(copy(turn(home_grad)))
         total_qkv = spread(
             (q2_x, turn(q2_near_x), quads_mate[2], last_mate), spread_at, used, 1, total_qkv
         ).reshape(wrows, 3 * D)

time: 423 us -> 422 us (level)
  no operation moved by 1% of the time
where the time goes in v17:
time: 422 us; the launch traced here: 415 us
  Pallas kernels  224 us (53%)
  waiting for transfers between devices  115 us (27%)
  starting transfers between devices  59.3 us (14%)
  local copies, waits for them, and re-layouts  9.3 us (2%)
  other arithmetic  5.44 us (1%)
    ppermute x47, waiting for transfers between devices, send(): return lax.ppermute(value, AXES, pairs(target))  115 us
    ppermute x47, starting transfers between devices, send(): return lax.ppermute(value, AXES, pairs(target))  50.2 us
    pallas_call x1, Pallas kernels, attn_bwd(): pl.pallas_call(functools.partial(bwd_kernel, first=group * nh, nh=nh, bq=...  43.5 us
    pallas_call x1, Pallas kernels, attn_fwd(): pl.pallas_call(functools.partial(fwd_kernel, nh=nh, bq=bq, bk=bk, nk=n //...  26 us
    pallas_call x2, Pallas kernels, project(): pl.pallas_call(functools.partial(project_kernel, count=count, halves=len(...  22.7 us
    pallas_call x1, Pallas kernels, tail(): pl.pallas_call(body, out_shape=[pltpu.HBM((rows, d), bf16)] + [pltpu.HBM(...  21.5 us
    pallas_call x2, Pallas kernels, share(): pl.pallas_call(share_kernel, out_shape=pltpu.HBM((d, n * w), bf16), grid_...  14.6 us
    pallas_call x1, Pallas kernels, cross(): pl.pallas_call(cross_kernel, out_shape=[pltpu.HBM((w // 2, cols), bf16)]...  11.6 us
  transfers between devices with their start and end apart: 48, of which 18 were waited for; matrix products, arithmetic and copies ran while one was open for 2% of the time, Pallas kernels for 47%

profile of v17, /device:TPU:0, one launch (start us, length us, event | category | flops | bytes accessed | tf_op | source)
XLA Modules:
  0.0 415.0 jit_solution(11820531403591185853)
XLA Ops:
  1.9 7.3 %collective-permute-start.5 = (bf16[512,1280]{1,0:T(8,128)(2,1)}, bf16[512,1280]{1,0:T(8,128)(2,1)}, u32[]{:S(2)}, u32[]{:S(2)}) collective-permute-start(bf16[512,1280]{1,0:T(8,128)(2,1)} %bitcast.69), channel_id=1, source_target_pairs={{0,8},{1,9},{2,10},{3,11},{12,4},{13,5},{14,6},{15,7},{16,24},{17,... | collective-permute-start | bytes 3932168 | tf_op jit(solution)/shard_map/ppermute | solution.py:1031
  9.3 4.4 %pick.1.x_ref.a_ref = bf16[640,1024]{1,0:T(8,128)(2,1)} custom-call(s32[1]{0:T(128)} %bitcast.mine.shard, bf16[640,3840]{1,0:T(8,128)(2,1)} %w_ref.1), custom_call_target="tpu_custom_call" | custom-call | flops 5000000000 | bytes 1000 | tf_op jit(solution)/shard_map/pick/pallas_call | solution.py:352
  15.8 4.2 %stretch.2.refs_5_ = bf16[640,1536]{1,0:T(8,128)(2,1)} custom-call(bf16[640,1024]{1,0:T(8,128)(2,1)} %pick.1.x_ref.a_ref), custom_call_target="tpu_custom_call" | custom-call | flops 2000000000 | bytes 1000 | tf_op jit(solution)/shard_map/stretch/pallas_call | solution.py:382
  30.1 12.9 %collective-permute-done.7.x_ref.b_ref = bf16[640,1024]{1,0:T(8,128)(2,1)} collective-permute-done((bf16[640,1024]{1,0:T(8,128)(2,1)}, bf16[640,1024]{1,0:T(8,128)(2,1)}, u32[]{:S(2)}, u32[]{:S(2)}) %collective-permute-start.7) | collective-permute-done | bytes 1310752 | tf_op jit(solution)/shard_map/ppermute | solution.py:1031
  42.9 4.0 stretch.3.refs_6_
  51.9 11.2 %project.2 = (bf16[2048,1280]{1,0:T(8,128)(2,1)}, bf16[2048,512]{1,0:T(8,128)(2,1)}, bf16[2048,1024]{1,0:T(8,128)(2,1)}, bf16[512,1280]{1,0:T(8,128)(2,1)}) custom-call(s32[5]{0:T(128)S(1)} %stack.103.info, bf16[512,1280]{1,0:T(8,128)(2,1)S(1)} %bitcast.70, bf16[512,1280]{1,0:T(8,128)(2,1)} %collective-permute-done.5.refs_1_, ...), custom_call_target="tpu_custom_call" | custom-call | flops 15000000512 | bytes 1000 | tf_op jit(solution)/shard_map/project/pallas_call | solution.py:518
  63.1 3.6 collective-permute-done.4.refs_2_
  73.4 11.6 %project.3 = (bf16[2048,1280]{1,0:T(8,128)(2,1)}, bf16[2048,512]{1,0:T(8,128)(2,1)}, bf16[2048,1024]{1,0:T(8,128)(2,1)}, bf16[512,1280]{1,0:T(8,128)(2,1)}) custom-call(s32[5]{0:T(128)S(1)} %stack.100.info, bf16[512,1280]{1,0:T(8,128)(2,1)S(1)} %collective-permute-done.2.refs_0_, ...), custom_call_target="tpu_custom_call", output_to_operand_aliasing={{0}: (11, {}), {1}: (12, {}), {2}: (13, {})} | custom-call | flops 15000000512 | bytes 1000 | tf_op jit(solution)/shard_map/project/pallas_call | solution.py:518
  85.0 26.0 %attn_fwd.1 = (bf16[2048,320]{1,0:T(8,128)(2,1)}, bf16[2048,512]{1,0:T(8,128)(2,1)}, bf16[2048,512]{1,0:T(8,128)(2,1)}) custom-call(s32[16]{0:T(128)S(1)} %reshape.183.flags, bf16[2048,512]{1,0:T(8,128)(2,1)} %get-tuple-element.95.q_ref, bf16[2048,1024]{1,0:T(8,128)(2,1)} %get-tuple-element.96.kv.kk.vv, s32[2048,1]{1,0:T(8,128)S(1)} %copy.29.segc, ...), custom_call_target="tpu_custom_call" | custom-call | flops 10000000 | bytes 1000 | tf_op jit(solution)/shard_map/attn_fwd/pallas_call | solution.py:172
  111.0 4.7 %collective-permute-done.9.half = bf16[3,320,1280]{2,1,0:T(8,128)(2,1)} collective-permute-done((bf16[3,320,1280]{2,1,0:T(8,128)(2,1)}, bf16[3,320,1280]{2,1,0:T(8,128)(2,1)}, u32[]{:S(2)}, u32[]{:S(2)}) %collective-permute-start.9) | collective-permute-done | bytes 2457632 | tf_op jit(solution)/shard_map/ppermute | solution.py:1031
  121.4 6.4 %order.1.w_ref = bf16[1024,1280]{1,0:T(8,128)(2,1)} custom-call(s32[1]{0:T(128)} %bitcast.10.own_first, bf16[640,1024]{1,0:T(8,128)(2,1)} %pick.1.x_ref.a_ref, bf16[640,1024]{1,0:T(8,128)(2,1)} %collective-permute-done.7.x_ref.b_ref), custom_call_target="tpu_custom_call" | custom-call | flops 199999995904 | bytes 1000 | tf_op jit(solution)/shard_map/order/pallas_call | solution.py:408
  127.8 7.8 %transpose.15.x_ref = bf16[1280,2048]{1,0:T(8,128)(2,1)} custom-call(bf16[2048,1280]{1,0:T(8,128)(2,1)} %get-tuple-element.104.x_ref), custom_call_target="tpu_custom_call" | custom-call | flops 1000000 | bytes 1000 | tf_op jit(solution)/shard_map/transpose/pallas_call | solution.py:432
  139.1 21.5 %tail.1 = (bf16[512,1280]{1,0:T(8,128)(2,1)}, bf16[3,512,1280]{2,1,0:T(8,128)(2,1)}, bf16[3,512,1280]{2,1,0:T(8,128)(2,1)}, f32[512,1280]{1,0:T(8,128)}, bf16[51...) custom-call(s32[4]{0:T(128)S(1)} %pad_add_fusion.at, ...), custom_call_target="tpu_custom_call" | custom-call | flops 10000000 | bytes 1000 | tf_op jit(solution)/shard_map/tail/pallas_call | solution.py:650
  163.0 7.4 %share.2 = bf16[1280,1920]{1,0:T(8,128)(2,1)} custom-call(s32[1]{0:T(128)} %bitcast.21.col, bf16[3,512,1280]{2,1,0:T(8,128)(2,1)} %get-tuple-element.112.left, bf16[3,512,1280]{2,1,0:T(8,128)(2,1)} %get-tuple-element.113.right), custom_call_target="tpu_custom_call" | custom-call | flops 1000000 | bytes 1000 | tf_op jit(solution)/shard_map/share/pallas_call | solution.py:686
  170.5 7.2 %share.3.a_ref = bf16[1280,1920]{1,0:T(8,128)(2,1)} custom-call(s32[1]{0:T(128)} %bitcast.22.col, bf16[3,512,1280]{2,1,0:T(8,128)(2,1)} %get-tuple-element.112.left, bf16[3,512,1280]{2,1,0:T(8,128)(2,1)} %get-tuple-element.113.right), custom_call_target="tpu_custom_call" | custom-call | flops 1000000 | bytes 1000 | tf_op jit(solution)/shard_map/share/pallas_call | solution.py:686
  182.7 7.8 %add_rows.1 = bf16[1280,1920]{1,0:T(8,128)(2,1)} custom-call(bf16[1280,1920]{1,0:T(8,128)(2,1)} %share.3.a_ref, bf16[1280,1920]{1,0:T(8,128)(2,1)} %collective-permute-done.19.b_ref), custom_call_target="tpu_custom_call" | custom-call | flops 1000000 | bytes 1000 | tf_op jit(solution)/shard_map/add_rows/pallas_call | solution.py:766
  190.5 9.1 %all-to-all-start = ((bf16[8,160,1920]{2,1,0:T(8,128)(2,1)}), bf16[8,160,1920]{2,1,0:T(8,128)(2,1)}, u32[]{:S(2)}, u32[]{:S(2)}) async-start(bf16[8,160,1920]{2,1,0:T(8,128)(2,1)} %bitcast.79), calls=%async_computation | async-start | bytes 9830400 | tf_op jit(solution)/shard_map/all_to_all | solution.py:1201
  199.6 43.5 %attn_bwd.1 = (bf16[2048,1024]{1,0:T(8,128)(2,1)}, f32[8,128]{1,0:T(8,128)}) custom-call(s32[16]{0:T(128)S(1)} %copy-done.6, s32[1]{0:T(128)} %bitcast.mine.shard, bf16[2048,512]{1,0:T(8,128)(2,1)} %get-tuple-element.119.qa, bf16[2048,1024]{1,0:T(8,128)(2,1)} %get-tuple-element.96.kv.kk.vv, bf16[2048,1024]{1,0:T(8,128)(2,1)} %get-tuple-element.96.kv.kk.vv, ...), custom_call_target="tpu_custom_call" | custom-call | flops 299999985664 | bytes 1000 | tf_op jit(solution)/shard_map/attn_bwd/pallas_call | solution.py:314
  243.2 6.8 %back.2 = bf16[2,512,1280]{2,1,0:T(8,128)(2,1)} custom-call(s32[2]{0:T(128)S(1)} %pad_add_fusion.1.shards, bf16[2048,1024]{1,0:T(8,128)(2,1)} %get-tuple-element.128.g_ref, bf16[1024,1280]{1,0:T(8,128)(2,1)} %order.1.w_ref), custom_call_target="tpu_custom_call" | custom-call | flops 1000000 | bytes 1000 | tf_op jit(solution)/shard_map/back/pallas_call | solution.py:924
  250.0 11.6 %cross.1 = (bf16[320,1024]{1,0:T(8,128)(2,1)}, bf16[320,1024]{1,0:T(8,128)(2,1)}, bf16[320,1024]{1,0:T(8,128)(2,1)}, bf16[320,1024]{1,0:T(8,128)(2,1)}) custom-call(s32[2]{0:T(128)S(1)} %pad_add_fusion.2.at, bf16[1280,2048]{1,0:T(8,128)(2,1)} %transpose.15.x_ref, bf16[2048,1024]{1,0:T(8,128)(2,1)} %get-tuple-element.128.g_ref), custom_call_target="tpu_custom_call" | custom-call | flops 1000000 | bytes 1000 | tf_op jit(solution)/shard_map/cross/pallas_call | solution.py:846
  261.6 4.7 %back.3 = bf16[1,512,1280]{2,1,0:T(8,128)(2,1)} custom-call(s32[1]{0:T(128)} %bitcast.26.shards, bf16[2048,1024]{1,0:T(8,128)(2,1)} %get-tuple-element.128.g_ref, bf16[1024,1280]{1,0:T(8,128)(2,1)} %order.1.w_ref, bf16[2,512,1280]{2,1,0:T(8,128)(2,1)S(1)} %collective-permute-done.20.refs_0_.core), custom_call_target="tpu_custom_call" | custom-call | flops 1000000 | bytes 1000 | tf_op jit(solution)/shard_map/back/pallas_call | solution.py:924
  277.9 8.3 %collective-permute-done.22 = bf16[320,1024]{1,0:T(8,128)(2,1)} collective-permute-done((bf16[320,1024]{1,0:T(8,128)(2,1)}, bf16[320,1024]{1,0:T(8,128)(2,1)}, u32[]{:S(2)}, u32[]{:S(2)}) %collective-permute-start.22) | collective-permute-done | bytes 655392 | tf_op jit(solution)/shard_map/ppermute | solution.py:1031
  286.2 14.5 %collective-permute-done.23 = bf16[320,1024]{1,0:T(8,128)(2,1)} collective-permute-done((bf16[320,1024]{1,0:T(8,128)(2,1)}, bf16[320,1024]{1,0:T(8,128)(2,1)}, u32[]{:S(2)}, u32[]{:S(2)}) %collective-permute-start.23) | collective-permute-done | bytes 655392 | tf_op jit(solution)/shard_map/ppermute | solution.py:1031
  303.1 7.8 %collective-permute-done.25.b_ref = bf16[160,1920]{1,0:T(8,128)(2,1)} collective-permute-done((bf16[160,1920]{1,0:T(8,128)(2,1)}, bf16[160,1920]{1,0:T(8,128)(2,1)}, u32[]{:S(2)}, u32[]{:S(2)}) %collective-permute-start.25) | collective-permute-done | bytes 614432 | tf_op jit(solution)/shard_map/ppermute | solution.py:1031
  315.7 6.6 %finish.1 = (bf16[512,1280]{1,0:T(8,128)(2,1)}, f32[1,1280]{1,0:T(1,128)S(1)}) custom-call(s32[1]{0:T(128)} %bitcast.mine.shard, bf16[2048,1024]{1,0:T(8,128)(2,1)} %get-tuple-element.128.g_ref, bf16[1024,1280]{1,0:T(8,128)(2,1)} %order.1.w_ref, bf16[2,512,1280]{2,1,0:T(8,128)(2,1)S(1)} %collective-permute-done.20.refs_0_.core, ...), custom_call_target="tpu_custom_call" | custom-call | flops 1000000 | bytes 1000 | tf_op jit(solution)/shard_map/finish/pallas_call | solution.py:962
  322.3 6.1 %collective-permute-done.27.refs_2_ = bf16[160,1920]{1,0:T(8,128)(2,1)S(1)} collective-permute-done((bf16[160,1920]{1,0:T(8,128)(2,1)}, bf16[160,1920]{1,0:T(8,128)(2,1)S(1)}, u32[]{:S(2)}, u32[]{:S(2)}) %collective-permute-start.27) | collective-permute-done | bytes 614432 | tf_op jit(solution)/shard_map/ppermute | solution.py:1031
  328.4 15.2 %collective-permute-done.26.refs_1_ = bf16[160,1920]{1,0:T(8,128)(2,1)} collective-permute-done((bf16[160,1920]{1,0:T(8,128)(2,1)}, bf16[160,1920]{1,0:T(8,128)(2,1)}, u32[]{:S(2)}, u32[]{:S(2)}) %collective-permute-start.26) | collective-permute-done | bytes 614432 | tf_op jit(solution)/shard_map/ppermute | solution.py:1031
  350.0 18.8 %collective-permute-done.32.refs_1_ = bf16[320,1024]{1,0:T(8,128)(2,1)S(1)} collective-permute-done((bf16[320,1024]{1,0:T(8,128)(2,1)}, bf16[320,1024]{1,0:T(8,128)(2,1)S(1)}, u32[]{:S(2)}, u32[]{:S(2)}) %collective-permute-start.32) | collective-permute-done | bytes 655392 | tf_op jit(solution)/shard_map/ppermute | solution.py:1031
  369.3 4.8 %collective-permute-done.30.refs_0_ = bf16[320,1024]{1,0:T(8,128)(2,1)S(1)} collective-permute-done((bf16[320,1024]{1,0:T(8,128)(2,1)}, bf16[320,1024]{1,0:T(8,128)(2,1)S(1)}, u32[]{:S(2)}, u32[]{:S(2)}) %collective-permute-start.30) | collective-permute-done | bytes 655392 | tf_op jit(solution)/shard_map/ppermute | solution.py:1031
  378.4 7.2 %place_tail.1 = (f32[4,160,1280]{2,1,0:T(8,128)}, f32[4,160,1280]{2,1,0:T(8,128)}, f32[4,160,1280]{2,1,0:T(8,128)}) custom-call(s32[3]{0:T(128)S(1)} %pad_add_fusion.3.at, bf16[160,1920]{1,0:T(8,128)(2,1)} %add.135.refs_0_, bf16[160,1920]{1,0:T(8,128)(2,1)} %collective-permute-done.26.refs_1_, bf16[160,1920]{1,0:T(8,128)(2,1)} %copy-done.20, ...), custom_call_target="tpu_custom_call" | custom-call | flops 1000000 | bytes 1000 | tf_op jit(solution)/shard_map/place_tail/pallas_call | solution.py:809
  394.2 3.7 collective-permute-start.42
  410.1 4.4 %spread.3 = f32[2,320,3840]{2,1,0:T(8,128)} custom-call(s32[3]{0:T(128)S(1)} %pad_add_fusion.5.at, bf16[320,1024]{1,0:T(8,128)(2,1)S(1)} %collective-permute-done.30.refs_0_, bf16[320,1024]{1,0:T(8,128)(2,1)S(1)} %collective-permute-done.44.refs_1_, bf16[320,1024]{1,0:T(8,128)(2,1)} %collective-permute-done.45.refs_2_, ...), custom_call_target="tpu_custom_call", output_to_operand_aliasing={{}: (5, {})} | custom-call | flops 1000000 | bytes 1000 | tf_op jit(solution)/shard_map/spread/pallas_call | solution.py:888
  (207 shorter events, 92.4 us)
Async XLA Ops:
  0.6 22.0 %collective-permute-start.1 = (bf16[512,1280]{1,0:T(8,128)(2,1)}, bf16[512,1280]{1,0:T(8,128)(2,1)}, u32[]{:S(2)}, u32[]{:S(2)}) collective-permute-start(bf16[512,1280]{1,0:T(8,128)(2,1)} %bitcast.68), channel_id=1, source_target_pairs={{2,0},{3,1},{4,2},{5,3},{6,4},{7,5},{8,10},{9,11},{10,12},{11,13},... | collective-permute-start | bytes 3932168 | tf_op jit(solution)/shard_map/ppermute | solution.py:1031
  1.9 50.0 %collective-permute-start.5 = (bf16[512,1280]{1,0:T(8,128)(2,1)}, bf16[512,1280]{1,0:T(8,128)(2,1)}, u32[]{:S(2)}, u32[]{:S(2)}) collective-permute-start(bf16[512,1280]{1,0:T(8,128)(2,1)} %bitcast.69), channel_id=1, source_target_pairs={{0,8},{1,9},{2,10},{3,11},{12,4},{13,5},{14,6},{15,7},{16,24},{17,... | collective-permute-start | bytes 3932168 | tf_op jit(solution)/shard_map/ppermute | solution.py:1031
  13.7 29.2 %collective-permute-start.7 = (bf16[640,1024]{1,0:T(8,128)(2,1)}, bf16[640,1024]{1,0:T(8,128)(2,1)}, u32[]{:S(2)}, u32[]{:S(2)}) collective-permute-start(bf16[640,1024]{1,0:T(8,128)(2,1)} %pick.1.x_ref.a_ref), channel_id=1, source_target_pairs={{0,1},{1,0},{2,3},{3,2},{4,5},{5,4},{6,7},{7,6},{8,9},{9,8},{10,11... | collective-permute-start | bytes 3932168 | tf_op jit(solution)/shard_map/ppermute | solution.py:1031
  15.2 55.6 %collective-permute-start = (s32[1,2048]{1,0:T(1,128)S(1)}, s32[1,2048]{1,0:T(1,128)S(1)}, u32[]{:S(2)}, u32[]{:S(2)}) collective-permute-start(s32[1,2048]{1,0:T(1,128)S(1)} %copy-done.28), channel_id=1, source_target_pairs={{0,8},{1,9},{2,10},{3,11},{4,12},{5,13},{6,14},{7,15},{8,0},{9,1},... | collective-permute-start | bytes 24584 | tf_op jit(solution)/shard_map/ppermute | solution.py:1031
  22.7 24.3 %collective-permute-start.2 = (bf16[512,1280]{1,0:T(8,128)(2,1)}, bf16[512,1280]{1,0:T(8,128)(2,1)S(1)}, u32[]{:S(2)}, u32[]{:S(2)}) collective-permute-start(bf16[512,1280]{1,0:T(8,128)(2,1)} %collective-permute-done.1.refs_2_), channel_id=1, source_target_pairs={{2,0},{3,1},{4,2},{5,3},{10,12},{11,13},{12,14},{13,15},{18,16},{1... | collective-permute-start | bytes 3932168 | tf_op jit(solution)/shard_map/ppermute | solution.py:1031
  27.0 24.9 %collective-permute-start.6 = (bf16[512,1280]{1,0:T(8,128)(2,1)}, bf16[512,1280]{1,0:T(8,128)(2,1)}, u32[]{:S(2)}, u32[]{:S(2)}) collective-permute-start(bf16[512,1280]{1,0:T(8,128)(2,1)} %collective-permute-done.1.refs_2_), channel_id=1, source_target_pairs={{0,8},{1,9},{2,10},{3,11},{12,4},{13,5},{14,6},{15,7},{16,24},{17,... | collective-permute-start | bytes 3932168 | tf_op jit(solution)/shard_map/ppermute | solution.py:1031
  47.1 19.6 %collective-permute-start.4 = (bf16[512,1280]{1,0:T(8,128)(2,1)S(1)}, bf16[512,1280]{1,0:T(8,128)(2,1)}, u32[]{:S(2)}, u32[]{:S(2)}) collective-permute-start(bf16[512,1280]{1,0:T(8,128)(2,1)S(1)} %broadcast_select_fusion), channel_id=1, source_target_pairs={{0,2},{1,3},{2,0},{3,1},{12,14},{13,15},{14,12},{15,13},{16,18},{1... | collective-permute-start | bytes 3932168 | tf_op jit(solution)/shard_map/ppermute | solution.py:1031
  49.5 24.0 %collective-permute-start.3 = (bf16[512,1280]{1,0:T(8,128)(2,1)S(1)}, bf16[512,1280]{1,0:T(8,128)(2,1)}, u32[]{:S(2)}, u32[]{:S(2)}) collective-permute-start(bf16[512,1280]{1,0:T(8,128)(2,1)S(1)} %collective-permute-done.2.refs_0_), channel_id=1, source_target_pairs={{0,8},{1,9},{2,10},{3,11},{12,4},{13,5},{14,6},{15,7},{16,24},{17,... | collective-permute-start | bytes 3932168 | tf_op jit(solution)/shard_map/ppermute | solution.py:1031
  69.2 46.5 %collective-permute-start.9 = (bf16[3,320,1280]{2,1,0:T(8,128)(2,1)}, bf16[3,320,1280]{2,1,0:T(8,128)(2,1)}, u32[]{:S(2)}, u32[]{:S(2)}) collective-permute-start(bf16[3,320,1280]{2,1,0:T(8,128)(2,1)} %pad_maximum_fusion), channel_id=1, source_target_pairs={{0,1},{1,0},{2,3},{3,2},{4,5},{5,4},{6,7},{7,6},{8,9},{9,8},{10,11... | collective-permute-start | bytes 7372808 | tf_op jit(solution)/shard_map/ppermute | solution.py:1031
  72.8 42.9 %collective-permute-start.10 = (bf16[512,1280]{1,0:T(8,128)(2,1)}, bf16[512,1280]{1,0:T(8,128)(2,1)S(1)}, u32[]{:S(2)}, u32[]{:S(2)}) collective-permute-start(bf16[512,1280]{1,0:T(8,128)(2,1)} %bitcast.90), channel_id=1, source_target_pairs={{0,8},{1,9},{2,0},{3,1},{4,10},{5,11},{6,2},{7,3},{8,12},{9,13},{1... | collective-permute-start | bytes 3932168 | tf_op jit(solution)/shard_map/ppermute | solution.py:1031
  119.2 16.4 %collective-permute-start.11 = (bf16[512,320]{1,0:T(8,128)(2,1)}, bf16[512,320]{1,0:T(8,128)(2,1)}, u32[]{:S(2)}, u32[]{:S(2)}) collective-permute-start(bf16[512,320]{1,0:T(8,128)(2,1)} %get-tuple-element.175), channel_id=1, source_target_pairs={{0,8},{1,9},{2,10},{3,11},{4,12},{5,13},{6,14},{7,15},{8,0},{9,1},... | collective-permute-start | bytes 983048 | tf_op jit(solution)/shard_map/ppermute | solution.py:1031
  119.3 16.4 %collective-permute-start.12 = (bf16[512,320]{1,0:T(8,128)(2,1)}, bf16[512,320]{1,0:T(8,128)(2,1)}, u32[]{:S(2)}, u32[]{:S(2)}) collective-permute-start(bf16[512,320]{1,0:T(8,128)(2,1)} %get-tuple-element.174), channel_id=1, source_target_pairs={{0,2},{1,3},{2,0},{3,1},{4,6},{5,7},{6,4},{7,5},{8,10},{9,11},{10,... | collective-permute-start | bytes 983048 | tf_op jit(solution)/shard_map/ppermute | solution.py:1031
  119.7 19.5 %collective-permute-start.13 = (bf16[512,320]{1,0:T(8,128)(2,1)}, bf16[512,320]{1,0:T(8,128)(2,1)}, u32[]{:S(2)}, u32[]{:S(2)}) collective-permute-start(bf16[512,320]{1,0:T(8,128)(2,1)} %get-tuple-element.173), channel_id=1, source_target_pairs={{0,10},{1,11},{2,8},{3,9},{4,14},{5,15},{6,12},{7,13},{8,2},{9,3},... | collective-permute-start | bytes 983048 | tf_op jit(solution)/shard_map/ppermute | solution.py:1031
  121.1 18.0 %collective-permute-start.14 = (bf16[3,320,1280]{2,1,0:T(8,128)(2,1)}, bf16[3,320,1280]{2,1,0:T(8,128)(2,1)}, u32[]{:S(2)}, u32[]{:S(2)}) collective-permute-start(bf16[3,320,1280]{2,1,0:T(8,128)(2,1)} %collective-permute-done.9.half), channel_id=1, source_target_pairs={{0,8},{1,9},{2,10},{3,11},{4,12},{5,13},{6,14},{7,15},{8,0},{9,1},... | collective-permute-start | bytes 7372808 | tf_op jit(solution)/shard_map/ppermute | solution.py:1031
  160.9 16.7 %collective-permute-start.17 = (bf16[512,320]{1,0:T(8,128)(2,1)}, bf16[512,320]{1,0:T(8,128)(2,1)S(1)}, u32[]{:S(2)}, u32[]{:S(2)}) collective-permute-start(bf16[512,320]{1,0:T(8,128)(2,1)} %get-tuple-element.116), channel_id=1, source_target_pairs={{0,10},{1,11},{2,8},{3,9},{4,14},{5,15},{6,12},{7,13},{8,2},{9,3},... | collective-permute-start | bytes 983048 | tf_op jit(solution)/shard_map/ppermute | solution.py:1031
  161.2 19.7 %collective-permute-start.16 = (bf16[512,320]{1,0:T(8,128)(2,1)}, bf16[512,320]{1,0:T(8,128)(2,1)S(1)}, u32[]{:S(2)}, u32[]{:S(2)}) collective-permute-start(bf16[512,320]{1,0:T(8,128)(2,1)} %get-tuple-element.110), channel_id=1, source_target_pairs={{0,2},{1,3},{2,0},{3,1},{4,6},{5,7},{6,4},{7,5},{8,10},{9,11},{10,... | collective-permute-start | bytes 983048 | tf_op jit(solution)/shard_map/ppermute | solution.py:1031
  182.3 60.9 %collective-permute-start.18 = (bf16[512,1280]{1,0:T(8,128)(2,1)}, bf16[512,1280]{1,0:T(8,128)(2,1)}, u32[]{:S(2)}, u32[]{:S(2)}) collective-permute-start(bf16[512,1280]{1,0:T(8,128)(2,1)} %get-tuple-element.118), channel_id=1, source_target_pairs={{0,2},{1,3},{2,6},{3,7},{4,10},{5,11},{6,14},{7,15},{8,0},{9,1},{1... | collective-permute-start | bytes 3932168 | tf_op jit(solution)/shard_map/ppermute | solution.py:1031
  190.5 81.3 %all-to-all-start = ((bf16[8,160,1920]{2,1,0:T(8,128)(2,1)}), bf16[8,160,1920]{2,1,0:T(8,128)(2,1)}, u32[]{:S(2)}, u32[]{:S(2)}) async-start(bf16[8,160,1920]{2,1,0:T(8,128)(2,1)} %bitcast.79), calls=%async_computation | async-start | bytes 9830400 | tf_op jit(solution)/shard_map/all_to_all | solution.py:1201
  266.3 49.4 %collective-permute-start.21 = (bf16[1,512,1280]{2,1,0:T(8,128)(2,1)}, bf16[1,512,1280]{2,1,0:T(8,128)(2,1)}, u32[]{:S(2)}, u32[]{:S(2)}) collective-permute-start(bf16[1,512,1280]{2,1,0:T(8,128)(2,1)} %back.3), channel_id=1, source_target_pairs={{0,2},{1,3},{2,0},{3,1},{4,6},{5,7},{6,4},{7,5},{8,10},{9,11},{10,... | collective-permute-start | bytes 3932168 | tf_op jit(solution)/shard_map/ppermute | solution.py:1031
  268.3 17.9 %collective-permute-start.22 = (bf16[320,1024]{1,0:T(8,128)(2,1)}, bf16[320,1024]{1,0:T(8,128)(2,1)}, u32[]{:S(2)}, u32[]{:S(2)}) collective-permute-start(bf16[320,1024]{1,0:T(8,128)(2,1)} %get-tuple-element.134), channel_id=1, source_target_pairs={{0,16},{1,17},{2,18},{3,19},{4,20},{5,21},{6,22},{7,23},{8,24},{9,... | collective-permute-start | bytes 1966088 | tf_op jit(solution)/shard_map/ppermute | solution.py:1031
  269.7 30.9 %collective-permute-start.23 = (bf16[320,1024]{1,0:T(8,128)(2,1)}, bf16[320,1024]{1,0:T(8,128)(2,1)}, u32[]{:S(2)}, u32[]{:S(2)}) collective-permute-start(bf16[320,1024]{1,0:T(8,128)(2,1)} %get-tuple-element.135), channel_id=1, source_target_pairs={{0,1},{1,0},{2,3},{3,2},{4,5},{5,4},{6,7},{7,6},{8,9},{9,8},{10,11... | collective-permute-start | bytes 1966088 | tf_op jit(solution)/shard_map/ppermute | solution.py:1031
  271.2 29.5 %collective-permute-start.24 = (bf16[320,1024]{1,0:T(8,128)(2,1)}, bf16[320,1024]{1,0:T(8,128)(2,1)}, u32[]{:S(2)}, u32[]{:S(2)}) collective-permute-start(bf16[320,1024]{1,0:T(8,128)(2,1)} %get-tuple-element.136), channel_id=1, source_target_pairs={{0,17},{1,16},{2,19},{3,18},{4,21},{5,20},{6,23},{7,22},{8,25},{9,... | collective-permute-start | bytes 1966088 | tf_op jit(solution)/shard_map/ppermute | solution.py:1031
  275.2 35.7 %collective-permute-start.25 = (bf16[160,1920]{1,0:T(8,128)(2,1)}, bf16[160,1920]{1,0:T(8,128)(2,1)}, u32[]{:S(2)}, u32[]{:S(2)}) collective-permute-start(bf16[160,1920]{1,0:T(8,128)(2,1)} %total.2.a_ref), channel_id=1, source_target_pairs={{0,4},{1,5},{2,6},{3,7},{4,0},{5,1},{6,2},{7,3},{8,12},{9,13},{10,... | collective-permute-start | bytes 1843208 | tf_op jit(solution)/shard_map/ppermute | solution.py:1031
  303.1 40.6 %collective-permute-start.28 = (bf16[320,1024]{1,0:T(8,128)(2,1)}, bf16[320,1024]{1,0:T(8,128)(2,1)}, u32[]{:S(2)}, u32[]{:S(2)}) collective-permute-start(bf16[320,1024]{1,0:T(8,128)(2,1)} %total.3.a_ref), channel_id=1, source_target_pairs={{0,4},{1,5},{2,6},{3,7},{4,0},{5,1},{6,2},{7,3},{8,12},{9,13},{10,... | collective-permute-start | bytes 1966088 | tf_op jit(solution)/shard_map/ppermute | solution.py:1031
  313.1 15.3 %collective-permute-start.27 = (bf16[160,1920]{1,0:T(8,128)(2,1)}, bf16[160,1920]{1,0:T(8,128)(2,1)S(1)}, u32[]{:S(2)}, u32[]{:S(2)}) collective-permute-start(bf16[160,1920]{1,0:T(8,128)(2,1)} %add.135.refs_0_), channel_id=1, source_target_pairs={{0,16},{1,17},{2,18},{3,19},{4,20},{5,21},{6,22},{7,23},{8,24},{9,... | collective-permute-start | bytes 1843208 | tf_op jit(solution)/shard_map/ppermute | solution.py:1031
  314.6 29.1 %collective-permute-start.26 = (bf16[160,1920]{1,0:T(8,128)(2,1)}, bf16[160,1920]{1,0:T(8,128)(2,1)}, u32[]{:S(2)}, u32[]{:S(2)}) collective-permute-start(bf16[160,1920]{1,0:T(8,128)(2,1)} %add.135.refs_0_), channel_id=1, source_target_pairs={{0,2},{1,3},{2,0},{3,1},{4,6},{5,7},{6,4},{7,5},{8,10},{9,11},{10,... | collective-permute-start | bytes 1843208 | tf_op jit(solution)/shard_map/ppermute | solution.py:1031
  345.9 22.9 %collective-permute-start.32 = (bf16[320,1024]{1,0:T(8,128)(2,1)}, bf16[320,1024]{1,0:T(8,128)(2,1)S(1)}, u32[]{:S(2)}, u32[]{:S(2)}) collective-permute-start(bf16[320,1024]{1,0:T(8,128)(2,1)} %add.136.refs_0_), channel_id=1, source_target_pairs={{0,2},{1,3},{2,0},{3,1},{4,6},{5,7},{6,4},{7,5},{8,10},{9,11},{10,... | collective-permute-start | bytes 1966088 | tf_op jit(solution)/shard_map/ppermute | solution.py:1031
  346.0 22.9 %collective-permute-start.31 = (bf16[160,1920]{1,0:T(8,128)(2,1)}, bf16[160,1920]{1,0:T(8,128)(2,1)S(1)}, u32[]{:S(2)}, u32[]{:S(2)}) collective-permute-start(bf16[160,1920]{1,0:T(8,128)(2,1)} %collective-permute-done.26.refs_1_), channel_id=1, source_target_pairs={{0,16},{1,17},{2,18},{3,19},{4,20},{5,21},{6,22},{7,23},{8,24},{9,... | collective-permute-start | bytes 1843208 | tf_op jit(solution)/shard_map/ppermute | solution.py:1031
  346.5 27.6 %collective-permute-start.30 = (bf16[320,1024]{1,0:T(8,128)(2,1)}, bf16[320,1024]{1,0:T(8,128)(2,1)S(1)}, u32[]{:S(2)}, u32[]{:S(2)}) collective-permute-start(bf16[320,1024]{1,0:T(8,128)(2,1)} %add.136.refs_0_), channel_id=1, source_target_pairs={{0,16},{1,17},{2,18},{3,19},{4,20},{5,21},{6,22},{7,23},{8,24},{9,... | collective-permute-start | bytes 1966088 | tf_op jit(solution)/shard_map/ppermute | solution.py:1031
  348.0 26.1 %collective-permute-start.36 = (bf16[160,1920]{1,0:T(8,128)(2,1)S(1)}, bf16[160,1920]{1,0:T(8,128)(2,1)S(1)}, u32[]{:S(2)}, u32[]{:S(2)}) collective-permute-start(bf16[160,1920]{1,0:T(8,128)(2,1)S(1)} %collective-permute-done.27.refs_2_), channel_id=1, source_target_pairs={{0,8},{1,9},{2,10},{3,11},{4,12},{5,13},{6,14},{7,15},{8,0},{9,1},... | collective-permute-start | bytes 1843208 | tf_op jit(solution)/shard_map/ppermute | solution.py:1031
  348.0 55.3 %collective-permute-start.29 = (bf16[512,1280]{1,0:T(8,128)(2,1)}, bf16[512,1280]{1,0:T(8,128)(2,1)}, u32[]{:S(2)}, u32[]{:S(2)}) collective-permute-start(bf16[512,1280]{1,0:T(8,128)(2,1)} %get-tuple-element.144), channel_id=1, source_target_pairs={{0,2},{1,3},{2,6},{3,7},{4,10},{5,11},{6,14},{7,15},{8,0},{9,1},{1... | collective-permute-start | bytes 3932168 | tf_op jit(solution)/shard_map/ppermute | solution.py:1031
  374.8 28.5 %collective-permute-start.44 = (bf16[320,1024]{1,0:T(8,128)(2,1)S(1)}, bf16[320,1024]{1,0:T(8,128)(2,1)S(1)}, u32[]{:S(2)}, u32[]{:S(2)}) collective-permute-start(bf16[320,1024]{1,0:T(8,128)(2,1)S(1)} %collective-permute-done.32.refs_1_), channel_id=1, source_target_pairs={{0,16},{1,17},{2,18},{3,19},{4,20},{5,21},{6,22},{7,23},{8,24},{9,... | collective-permute-start | bytes 1966088 | tf_op jit(solution)/shard_map/ppermute | solution.py:1031
  (51 other events, 626.1 us)

commit v18 on v17

--- a/solution.py
+++ b/solution.py
@@ -1110,8 +1110,8 @@
         picked = pick(w_qkv, mine, parts, groups, nh)
         own = tokens[0]
         got1 = send(own, hop1)
-        own_share = send(own, lane_share)
-        seg_mate = send(segments, core_mate)
+        own_share = send(after(own, picked), lane_share)
+        seg_mate = send(after(segments, picked), core_mate)
         got2 = send(got1, hop2)
         got1_share = send(got1, lane_share)
         end = jnp.where(gc == 0, z == 0, z == 3)

time: 422 us -> 420 us (level)
  waiting for transfers between devices: 115 us -> 109 us
    ppermute x47, waiting for transfers between devices: 115 us -> 109 us  [send(): return lax.ppermute(value, AXES, pairs(target))]
    ppermute x47, starting transfers between devices: 50.2 us -> 56 us  [send(): return lax.ppermute(value, AXES, pairs(target))]
  transfers between devices with their start and end apart: 48 -> 48, of which waited for: 18 -> 19; matrix products, arithmetic and copies ran while one was open for 2% -> 3% of each run, Pallas kernels for 47% -> 47%
where the time goes in v18:
time: 420 us; the launch traced here: 412 us
  Pallas kernels  224 us (53%)
  waiting for transfers between devices  109 us (26%)
  starting transfers between devices  61 us (15%)
  local copies, waits for them, and re-layouts  11 us (3%)
  other arithmetic  5.71 us (1%)
    ppermute x47, waiting for transfers between devices, send(): return lax.ppermute(value, AXES, pairs(target))  109 us
    ppermute x47, starting transfers between devices, send(): return lax.ppermute(value, AXES, pairs(target))  56 us
    pallas_call x1, Pallas kernels, attn_bwd(): pl.pallas_call(functools.partial(bwd_kernel, first=group * nh, nh=nh, bq=...  43.5 us
    pallas_call x1, Pallas kernels, attn_fwd(): pl.pallas_call(functools.partial(fwd_kernel, nh=nh, bq=bq, bk=bk, nk=n //...  26 us
    pallas_call x2, Pallas kernels, project(): pl.pallas_call(functools.partial(project_kernel, count=count, halves=len(...  22.8 us
    pallas_call x1, Pallas kernels, tail(): pl.pallas_call(body, out_shape=[pltpu.HBM((rows, d), bf16)] + [pltpu.HBM(...  21.5 us
    pallas_call x2, Pallas kernels, share(): pl.pallas_call(share_kernel, out_shape=pltpu.HBM((d, n * w), bf16), grid_...  14.6 us
    pallas_call x1, Pallas kernels, cross(): pl.pallas_call(cross_kernel, out_shape=[pltpu.HBM((w // 2, cols), bf16)]...  11.6 us
  transfers between devices with their start and end apart: 48, of which 19 were waited for; matrix products, arithmetic and copies ran while one was open for 3% of the time, Pallas kernels for 47%

profile of v18, /device:TPU:0, one launch (start us, length us, event | category | flops | bytes accessed | tf_op | source)
XLA Modules:
  0.0 412.4 jit_solution(2697110241402556630)
XLA Ops:
  2.0 4.5 %pick.1.x_ref.a_ref = bf16[640,1024]{1,0:T(8,128)(2,1)} custom-call(s32[1]{0:T(128)} %bitcast.mine.shard, bf16[640,3840]{1,0:T(8,128)(2,1)} %w_ref.1), custom_call_target="tpu_custom_call" | custom-call | flops 5000000000 | bytes 1000 | tf_op jit(solution)/shard_map/pick/pallas_call | solution.py:352
  9.5 5.5 %collective-permute-start.5 = (bf16[512,1280]{1,0:T(8,128)(2,1)S(1)}, bf16[512,1280]{1,0:T(8,128)(2,1)}, u32[]{:S(2)}, u32[]{:S(2)}) collective-permute-start(bf16[512,1280]{1,0:T(8,128)(2,1)S(1)} %bitcast.69), channel_id=1, source_target_pairs={{0,8},{1,9},{2,10},{3,11},{12,4},{13,5},{14,6},{15,7},{16,24},{17,... | collective-permute-start | bytes 3932168 | tf_op jit(solution)/shard_map/ppermute | solution.py:1031
  15.6 4.0 stretch.2.refs_5_
  31.2 5.9 %collective-permute-done.7.x_ref.b_ref = bf16[640,1024]{1,0:T(8,128)(2,1)} collective-permute-done((bf16[640,1024]{1,0:T(8,128)(2,1)}, bf16[640,1024]{1,0:T(8,128)(2,1)}, u32[]{:S(2)}, u32[]{:S(2)}) %collective-permute-start.7) | collective-permute-done | bytes 1310752 | tf_op jit(solution)/shard_map/ppermute | solution.py:1031
  37.1 4.0 stretch.3.refs_6_
  43.5 4.6 %collective-permute-start.4 = (bf16[512,1280]{1,0:T(8,128)(2,1)S(1)}, bf16[512,1280]{1,0:T(8,128)(2,1)}, u32[]{:S(2)}, u32[]{:S(2)}) collective-permute-start(bf16[512,1280]{1,0:T(8,128)(2,1)S(1)} %broadcast_select_fusion), channel_id=1, source_target_pairs={{0,2},{1,3},{2,0},{3,1},{12,14},{13,15},{14,12},{15,13},{16,18},{1... | collective-permute-start | bytes 3932168 | tf_op jit(solution)/shard_map/ppermute | solution.py:1031
  50.5 11.2 %project.2 = (bf16[2048,1280]{1,0:T(8,128)(2,1)}, bf16[2048,512]{1,0:T(8,128)(2,1)}, bf16[2048,1024]{1,0:T(8,128)(2,1)}, bf16[512,1280]{1,0:T(8,128)(2,1)}) custom-call(s32[5]{0:T(128)S(1)} %stack.103.info, bf16[512,1280]{1,0:T(8,128)(2,1)S(1)} %bitcast.70, bf16[512,1280]{1,0:T(8,128)(2,1)} %collective-permute-done.5.refs_1_, ...), custom_call_target="tpu_custom_call" | custom-call | flops 15000000512 | bytes 1000 | tf_op jit(solution)/shard_map/project/pallas_call | solution.py:518
  70.7 11.6 %project.3 = (bf16[2048,1280]{1,0:T(8,128)(2,1)}, bf16[2048,512]{1,0:T(8,128)(2,1)}, bf16[2048,1024]{1,0:T(8,128)(2,1)}, bf16[512,1280]{1,0:T(8,128)(2,1)}) custom-call(s32[5]{0:T(128)S(1)} %stack.100.info, bf16[512,1280]{1,0:T(8,128)(2,1)S(1)} %collective-permute-done.2.refs_0_, ...), custom_call_target="tpu_custom_call", output_to_operand_aliasing={{0}: (11, {}), {1}: (12, {}), {2}: (13, {})} | custom-call | flops 15000000512 | bytes 1000 | tf_op jit(solution)/shard_map/project/pallas_call | solution.py:518
  82.3 26.0 %attn_fwd.1 = (bf16[2048,320]{1,0:T(8,128)(2,1)}, bf16[2048,512]{1,0:T(8,128)(2,1)}, bf16[2048,512]{1,0:T(8,128)(2,1)}) custom-call(s32[16]{0:T(128)S(1)} %reshape.183.flags, bf16[2048,512]{1,0:T(8,128)(2,1)} %get-tuple-element.99.q_ref, bf16[2048,1024]{1,0:T(8,128)(2,1)} %get-tuple-element.100.kv.kk.vv, s32[2048,1]{1,0:T(8,128)S(1)} %copy.29.segc, ...), custom_call_target="tpu_custom_call" | custom-call | flops 10000000 | bytes 1000 | tf_op jit(solution)/shard_map/attn_fwd/pallas_call | solution.py:172
  108.3 7.0 %collective-permute-done.9.half = bf16[3,320,1280]{2,1,0:T(8,128)(2,1)} collective-permute-done((bf16[3,320,1280]{2,1,0:T(8,128)(2,1)}, bf16[3,320,1280]{2,1,0:T(8,128)(2,1)}, u32[]{:S(2)}, u32[]{:S(2)}) %collective-permute-start.9) | collective-permute-done | bytes 2457632 | tf_op jit(solution)/shard_map/ppermute | solution.py:1031
  121.4 6.4 %order.1.w_ref = bf16[1024,1280]{1,0:T(8,128)(2,1)} custom-call(s32[1]{0:T(128)} %bitcast.10.own_first, bf16[640,1024]{1,0:T(8,128)(2,1)} %pick.1.x_ref.a_ref, bf16[640,1024]{1,0:T(8,128)(2,1)} %collective-permute-done.7.x_ref.b_ref), custom_call_target="tpu_custom_call" | custom-call | flops 199999995904 | bytes 1000 | tf_op jit(solution)/shard_map/order/pallas_call | solution.py:408
  127.8 7.9 %transpose.15.x_ref = bf16[1280,2048]{1,0:T(8,128)(2,1)} custom-call(bf16[2048,1280]{1,0:T(8,128)(2,1)} %get-tuple-element.108.x_ref), custom_call_target="tpu_custom_call" | custom-call | flops 1000000 | bytes 1000 | tf_op jit(solution)/shard_map/transpose/pallas_call | solution.py:432
  135.7 3.8 collective-permute-done.13.p3
  139.5 21.5 %tail.1 = (bf16[512,1280]{1,0:T(8,128)(2,1)}, bf16[3,512,1280]{2,1,0:T(8,128)(2,1)}, bf16[3,512,1280]{2,1,0:T(8,128)(2,1)}, f32[512,1280]{1,0:T(8,128)}, bf16[51...) custom-call(s32[4]{0:T(128)S(1)} %pad_add_fusion.at, ...), custom_call_target="tpu_custom_call" | custom-call | flops 10000000 | bytes 1000 | tf_op jit(solution)/shard_map/tail/pallas_call | solution.py:650
  163.4 7.4 %share.2 = bf16[1280,1920]{1,0:T(8,128)(2,1)} custom-call(s32[1]{0:T(128)} %bitcast.21.col, bf16[3,512,1280]{2,1,0:T(8,128)(2,1)} %get-tuple-element.116.left, bf16[3,512,1280]{2,1,0:T(8,128)(2,1)} %get-tuple-element.117.right), custom_call_target="tpu_custom_call" | custom-call | flops 1000000 | bytes 1000 | tf_op jit(solution)/shard_map/share/pallas_call | solution.py:686
  170.8 7.2 %share.3.a_ref = bf16[1280,1920]{1,0:T(8,128)(2,1)} custom-call(s32[1]{0:T(128)} %bitcast.22.col, bf16[3,512,1280]{2,1,0:T(8,128)(2,1)} %get-tuple-element.116.left, bf16[3,512,1280]{2,1,0:T(8,128)(2,1)} %get-tuple-element.117.right), custom_call_target="tpu_custom_call" | custom-call | flops 1000000 | bytes 1000 | tf_op jit(solution)/shard_map/share/pallas_call | solution.py:686
  184.2 7.8 %add_rows.1 = bf16[1280,1920]{1,0:T(8,128)(2,1)} custom-call(bf16[1280,1920]{1,0:T(8,128)(2,1)} %share.3.a_ref, bf16[1280,1920]{1,0:T(8,128)(2,1)} %collective-permute-done.19.b_ref), custom_call_target="tpu_custom_call" | custom-call | flops 1000000 | bytes 1000 | tf_op jit(solution)/shard_map/add_rows/pallas_call | solution.py:766
  192.0 5.0 %all-to-all-start = ((bf16[8,160,1920]{2,1,0:T(8,128)(2,1)}), bf16[8,160,1920]{2,1,0:T(8,128)(2,1)}, u32[]{:S(2)}, u32[]{:S(2)}) async-start(bf16[8,160,1920]{2,1,0:T(8,128)(2,1)} %bitcast.79), calls=%async_computation | async-start | bytes 9830400 | tf_op jit(solution)/shard_map/all_to_all | solution.py:1201
  197.0 43.5 %attn_bwd.1 = (bf16[2048,1024]{1,0:T(8,128)(2,1)}, f32[8,128]{1,0:T(8,128)}) custom-call(s32[16]{0:T(128)S(1)} %copy-done.6, s32[1]{0:T(128)} %bitcast.mine.shard, bf16[2048,512]{1,0:T(8,128)(2,1)} %get-tuple-element.123.qa, bf16[2048,1024]{1,0:T(8,128)(2,1)} %get-tuple-element.100.kv.kk.vv, bf16[2048,1024]{1,0:T(8,128)(2,1)} %get-tuple-element.100.kv.kk.vv, ...), custom_call_target="tpu_custom_call" | custom-call | flops 299999985664 | bytes 1000 | tf_op jit(solution)/shard_map/attn_bwd/pallas_call | solution.py:314
  240.6 6.8 %back.2 = bf16[2,512,1280]{2,1,0:T(8,128)(2,1)} custom-call(s32[2]{0:T(128)S(1)} %pad_add_fusion.1.shards, bf16[2048,1024]{1,0:T(8,128)(2,1)} %get-tuple-element.132.g_ref, bf16[1024,1280]{1,0:T(8,128)(2,1)} %order.1.w_ref), custom_call_target="tpu_custom_call" | custom-call | flops 1000000 | bytes 1000 | tf_op jit(solution)/shard_map/back/pallas_call | solution.py:924
  247.6 11.6 %cross.1 = (bf16[320,1024]{1,0:T(8,128)(2,1)}, bf16[320,1024]{1,0:T(8,128)(2,1)}, bf16[320,1024]{1,0:T(8,128)(2,1)}, bf16[320,1024]{1,0:T(8,128)(2,1)}) custom-call(s32[2]{0:T(128)S(1)} %pad_add_fusion.2.at, bf16[1280,2048]{1,0:T(8,128)(2,1)} %transpose.15.x_ref, bf16[2048,1024]{1,0:T(8,128)(2,1)} %get-tuple-element.132.g_ref), custom_call_target="tpu_custom_call" | custom-call | flops 1000000 | bytes 1000 | tf_op jit(solution)/shard_map/cross/pallas_call | solution.py:846
  259.2 4.7 %back.3 = bf16[1,512,1280]{2,1,0:T(8,128)(2,1)} custom-call(s32[1]{0:T(128)} %bitcast.26.shards, bf16[2048,1024]{1,0:T(8,128)(2,1)} %get-tuple-element.132.g_ref, bf16[1024,1280]{1,0:T(8,128)(2,1)} %order.1.w_ref, bf16[2,512,1280]{2,1,0:T(8,128)(2,1)S(1)} %collective-permute-done.20.refs_0_.core), custom_call_target="tpu_custom_call" | custom-call | flops 1000000 | bytes 1000 | tf_op jit(solution)/shard_map/back/pallas_call | solution.py:924
  276.2 7.4 %collective-permute-done.22 = bf16[320,1024]{1,0:T(8,128)(2,1)} collective-permute-done((bf16[320,1024]{1,0:T(8,128)(2,1)}, bf16[320,1024]{1,0:T(8,128)(2,1)}, u32[]{:S(2)}, u32[]{:S(2)}) %collective-permute-start.22) | collective-permute-done | bytes 655392 | tf_op jit(solution)/shard_map/ppermute | solution.py:1031
  283.6 14.5 %collective-permute-done.23 = bf16[320,1024]{1,0:T(8,128)(2,1)} collective-permute-done((bf16[320,1024]{1,0:T(8,128)(2,1)}, bf16[320,1024]{1,0:T(8,128)(2,1)}, u32[]{:S(2)}, u32[]{:S(2)}) %collective-permute-start.23) | collective-permute-done | bytes 655392 | tf_op jit(solution)/shard_map/ppermute | solution.py:1031
  301.6 6.7 %collective-permute-done.25.b_ref = bf16[160,1920]{1,0:T(8,128)(2,1)} collective-permute-done((bf16[160,1920]{1,0:T(8,128)(2,1)}, bf16[160,1920]{1,0:T(8,128)(2,1)}, u32[]{:S(2)}, u32[]{:S(2)}) %collective-permute-start.25) | collective-permute-done | bytes 614432 | tf_op jit(solution)/shard_map/ppermute | solution.py:1031
  314.2 6.6 %finish.1 = (bf16[512,1280]{1,0:T(8,128)(2,1)}, f32[1,1280]{1,0:T(1,128)S(1)}) custom-call(s32[1]{0:T(128)} %bitcast.mine.shard, bf16[2048,1024]{1,0:T(8,128)(2,1)} %get-tuple-element.132.g_ref, bf16[1024,1280]{1,0:T(8,128)(2,1)} %order.1.w_ref, bf16[2,512,1280]{2,1,0:T(8,128)(2,1)S(1)} %collective-permute-done.20.refs_0_.core, ...), custom_call_target="tpu_custom_call" | custom-call | flops 1000000 | bytes 1000 | tf_op jit(solution)/shard_map/finish/pallas_call | solution.py:962
  320.8 5.0 %collective-permute-done.27.refs_2_ = bf16[160,1920]{1,0:T(8,128)(2,1)S(1)} collective-permute-done((bf16[160,1920]{1,0:T(8,128)(2,1)}, bf16[160,1920]{1,0:T(8,128)(2,1)S(1)}, u32[]{:S(2)}, u32[]{:S(2)}) %collective-permute-start.27) | collective-permute-done | bytes 614432 | tf_op jit(solution)/shard_map/ppermute | solution.py:1031
  325.9 15.7 %collective-permute-done.26.refs_1_ = bf16[160,1920]{1,0:T(8,128)(2,1)} collective-permute-done((bf16[160,1920]{1,0:T(8,128)(2,1)}, bf16[160,1920]{1,0:T(8,128)(2,1)}, u32[]{:S(2)}, u32[]{:S(2)}) %collective-permute-start.26) | collective-permute-done | bytes 614432 | tf_op jit(solution)/shard_map/ppermute | solution.py:1031
  347.8 19.9 %collective-permute-done.32.refs_1_ = bf16[320,1024]{1,0:T(8,128)(2,1)S(1)} collective-permute-done((bf16[320,1024]{1,0:T(8,128)(2,1)}, bf16[320,1024]{1,0:T(8,128)(2,1)S(1)}, u32[]{:S(2)}, u32[]{:S(2)}) %collective-permute-start.32) | collective-permute-done | bytes 655392 | tf_op jit(solution)/shard_map/ppermute | solution.py:1031
  368.3 3.9 collective-permute-done.30.refs_0_
  376.4 7.2 %place_tail.1 = (f32[4,160,1280]{2,1,0:T(8,128)}, f32[4,160,1280]{2,1,0:T(8,128)}, f32[4,160,1280]{2,1,0:T(8,128)}) custom-call(s32[3]{0:T(128)S(1)} %pad_add_fusion.3.at, bf16[160,1920]{1,0:T(8,128)(2,1)} %add.135.refs_0_, bf16[160,1920]{1,0:T(8,128)(2,1)} %collective-permute-done.26.refs_1_, bf16[160,1920]{1,0:T(8,128)(2,1)} %copy-done.17, ...), custom_call_target="tpu_custom_call" | custom-call | flops 1000000 | bytes 1000 | tf_op jit(solution)/shard_map/place_tail/pallas_call | solution.py:809
  407.5 4.4 %spread.3 = f32[2,320,3840]{2,1,0:T(8,128)} custom-call(s32[3]{0:T(128)S(1)} %pad_add_fusion.5.at, bf16[320,1024]{1,0:T(8,128)(2,1)S(1)} %collective-permute-done.30.refs_0_, bf16[320,1024]{1,0:T(8,128)(2,1)S(1)} %collective-permute-done.44.refs_1_, bf16[320,1024]{1,0:T(8,128)(2,1)} %collective-permute-done.45.refs_2_, ...), custom_call_target="tpu_custom_call", output_to_operand_aliasing={{}: (5, {})} | custom-call | flops 1000000 | bytes 1000 | tf_op jit(solution)/shard_map/spread/pallas_call | solution.py:888
  (201 shorter events, 101.6 us)
Async XLA Ops:
  0.6 23.0 %collective-permute-start.1 = (bf16[512,1280]{1,0:T(8,128)(2,1)}, bf16[512,1280]{1,0:T(8,128)(2,1)}, u32[]{:S(2)}, u32[]{:S(2)}) collective-permute-start(bf16[512,1280]{1,0:T(8,128)(2,1)} %bitcast.68), channel_id=1, source_target_pairs={{2,0},{3,1},{4,2},{5,3},{6,4},{7,5},{8,10},{9,11},{10,12},{11,13},... | collective-permute-start | bytes 3932168 | tf_op jit(solution)/shard_map/ppermute | solution.py:1031
  6.5 30.6 %collective-permute-start.7 = (bf16[640,1024]{1,0:T(8,128)(2,1)}, bf16[640,1024]{1,0:T(8,128)(2,1)}, u32[]{:S(2)}, u32[]{:S(2)}) collective-permute-start(bf16[640,1024]{1,0:T(8,128)(2,1)} %pick.1.x_ref.a_ref), channel_id=1, source_target_pairs={{0,1},{1,0},{2,3},{3,2},{4,5},{5,4},{6,7},{7,6},{8,9},{9,8},{10,11... | collective-permute-start | bytes 3932168 | tf_op jit(solution)/shard_map/ppermute | solution.py:1031
  9.5 41.0 %collective-permute-start.5 = (bf16[512,1280]{1,0:T(8,128)(2,1)S(1)}, bf16[512,1280]{1,0:T(8,128)(2,1)}, u32[]{:S(2)}, u32[]{:S(2)}) collective-permute-start(bf16[512,1280]{1,0:T(8,128)(2,1)S(1)} %bitcast.69), channel_id=1, source_target_pairs={{0,8},{1,9},{2,10},{3,11},{12,4},{13,5},{14,6},{15,7},{16,24},{17,... | collective-permute-start | bytes 3932168 | tf_op jit(solution)/shard_map/ppermute | solution.py:1031
  15.0 53.0 %collective-permute-start = (s32[1,2048]{1,0:T(1,128)S(1)}, s32[1,2048]{1,0:T(1,128)S(1)}, u32[]{:S(2)}, u32[]{:S(2)}) collective-permute-start(s32[1,2048]{1,0:T(1,128)S(1)} %copy-done.25), channel_id=1, source_target_pairs={{0,8},{1,9},{2,10},{3,11},{4,12},{5,13},{6,14},{7,15},{8,0},{9,1},... | collective-permute-start | bytes 24584 | tf_op jit(solution)/shard_map/ppermute | solution.py:1031
  23.7 19.7 %collective-permute-start.2 = (bf16[512,1280]{1,0:T(8,128)(2,1)}, bf16[512,1280]{1,0:T(8,128)(2,1)S(1)}, u32[]{:S(2)}, u32[]{:S(2)}) collective-permute-start(bf16[512,1280]{1,0:T(8,128)(2,1)} %collective-permute-done.1.refs_2_), channel_id=1, source_target_pairs={{2,0},{3,1},{4,2},{5,3},{10,12},{11,13},{12,14},{13,15},{18,16},{1... | collective-permute-start | bytes 3932168 | tf_op jit(solution)/shard_map/ppermute | solution.py:1031
  28.2 22.3 %collective-permute-start.6 = (bf16[512,1280]{1,0:T(8,128)(2,1)}, bf16[512,1280]{1,0:T(8,128)(2,1)}, u32[]{:S(2)}, u32[]{:S(2)}) collective-permute-start(bf16[512,1280]{1,0:T(8,128)(2,1)} %collective-permute-done.1.refs_2_), channel_id=1, source_target_pairs={{0,8},{1,9},{2,10},{3,11},{12,4},{13,5},{14,6},{15,7},{16,24},{17,... | collective-permute-start | bytes 3932168 | tf_op jit(solution)/shard_map/ppermute | solution.py:1031
  43.5 20.2 %collective-permute-start.4 = (bf16[512,1280]{1,0:T(8,128)(2,1)S(1)}, bf16[512,1280]{1,0:T(8,128)(2,1)}, u32[]{:S(2)}, u32[]{:S(2)}) collective-permute-start(bf16[512,1280]{1,0:T(8,128)(2,1)S(1)} %broadcast_select_fusion), channel_id=1, source_target_pairs={{0,2},{1,3},{2,0},{3,1},{12,14},{13,15},{14,12},{15,13},{16,18},{1... | collective-permute-start | bytes 3932168 | tf_op jit(solution)/shard_map/ppermute | solution.py:1031
  48.1 22.6 %collective-permute-start.3 = (bf16[512,1280]{1,0:T(8,128)(2,1)S(1)}, bf16[512,1280]{1,0:T(8,128)(2,1)}, u32[]{:S(2)}, u32[]{:S(2)}) collective-permute-start(bf16[512,1280]{1,0:T(8,128)(2,1)S(1)} %collective-permute-done.2.refs_0_), channel_id=1, source_target_pairs={{0,8},{1,9},{2,10},{3,11},{12,4},{13,5},{14,6},{15,7},{16,24},{17,... | collective-permute-start | bytes 3932168 | tf_op jit(solution)/shard_map/ppermute | solution.py:1031
  66.3 49.0 %collective-permute-start.9 = (bf16[3,320,1280]{2,1,0:T(8,128)(2,1)}, bf16[3,320,1280]{2,1,0:T(8,128)(2,1)}, u32[]{:S(2)}, u32[]{:S(2)}) collective-permute-start(bf16[3,320,1280]{2,1,0:T(8,128)(2,1)} %pad_maximum_fusion), channel_id=1, source_target_pairs={{0,1},{1,0},{2,3},{3,2},{4,5},{5,4},{6,7},{7,6},{8,9},{9,8},{10,11... | collective-permute-start | bytes 7372808 | tf_op jit(solution)/shard_map/ppermute | solution.py:1031
  70.1 45.2 %collective-permute-start.10 = (bf16[512,1280]{1,0:T(8,128)(2,1)}, bf16[512,1280]{1,0:T(8,128)(2,1)S(1)}, u32[]{:S(2)}, u32[]{:S(2)}) collective-permute-start(bf16[512,1280]{1,0:T(8,128)(2,1)} %bitcast.90), channel_id=1, source_target_pairs={{0,8},{1,9},{2,0},{3,1},{4,10},{5,11},{6,2},{7,3},{8,12},{9,13},{1... | collective-permute-start | bytes 3932168 | tf_op jit(solution)/shard_map/ppermute | solution.py:1031
  118.8 16.9 %collective-permute-start.11 = (bf16[512,320]{1,0:T(8,128)(2,1)}, bf16[512,320]{1,0:T(8,128)(2,1)}, u32[]{:S(2)}, u32[]{:S(2)}) collective-permute-start(bf16[512,320]{1,0:T(8,128)(2,1)} %get-tuple-element.179), channel_id=1, source_target_pairs={{0,8},{1,9},{2,10},{3,11},{4,12},{5,13},{6,14},{7,15},{8,0},{9,1},... | collective-permute-start | bytes 983048 | tf_op jit(solution)/shard_map/ppermute | solution.py:1031
  118.8 16.9 %collective-permute-start.12 = (bf16[512,320]{1,0:T(8,128)(2,1)}, bf16[512,320]{1,0:T(8,128)(2,1)}, u32[]{:S(2)}, u32[]{:S(2)}) collective-permute-start(bf16[512,320]{1,0:T(8,128)(2,1)} %get-tuple-element.178), channel_id=1, source_target_pairs={{0,2},{1,3},{2,0},{3,1},{4,6},{5,7},{6,4},{7,5},{8,10},{9,11},{10,... | collective-permute-start | bytes 983048 | tf_op jit(solution)/shard_map/ppermute | solution.py:1031
  121.1 18.3 %collective-permute-start.13 = (bf16[512,320]{1,0:T(8,128)(2,1)}, bf16[512,320]{1,0:T(8,128)(2,1)}, u32[]{:S(2)}, u32[]{:S(2)}) collective-permute-start(bf16[512,320]{1,0:T(8,128)(2,1)} %get-tuple-element.177), channel_id=1, source_target_pairs={{0,10},{1,11},{2,8},{3,9},{4,14},{5,15},{6,12},{7,13},{8,2},{9,3},... | collective-permute-start | bytes 983048 | tf_op jit(solution)/shard_map/ppermute | solution.py:1031
  121.3 18.2 %collective-permute-start.14 = (bf16[3,320,1280]{2,1,0:T(8,128)(2,1)}, bf16[3,320,1280]{2,1,0:T(8,128)(2,1)}, u32[]{:S(2)}, u32[]{:S(2)}) collective-permute-start(bf16[3,320,1280]{2,1,0:T(8,128)(2,1)} %collective-permute-done.9.half), channel_id=1, source_target_pairs={{0,8},{1,9},{2,10},{3,11},{4,12},{5,13},{6,14},{7,15},{8,0},{9,1},... | collective-permute-start | bytes 7372808 | tf_op jit(solution)/shard_map/ppermute | solution.py:1031
  161.2 16.8 %collective-permute-start.17 = (bf16[512,320]{1,0:T(8,128)(2,1)}, bf16[512,320]{1,0:T(8,128)(2,1)S(1)}, u32[]{:S(2)}, u32[]{:S(2)}) collective-permute-start(bf16[512,320]{1,0:T(8,128)(2,1)} %get-tuple-element.120), channel_id=1, source_target_pairs={{0,10},{1,11},{2,8},{3,9},{4,14},{5,15},{6,12},{7,13},{8,2},{9,3},... | collective-permute-start | bytes 983048 | tf_op jit(solution)/shard_map/ppermute | solution.py:1031
  162.7 18.5 %collective-permute-start.16 = (bf16[512,320]{1,0:T(8,128)(2,1)}, bf16[512,320]{1,0:T(8,128)(2,1)S(1)}, u32[]{:S(2)}, u32[]{:S(2)}) collective-permute-start(bf16[512,320]{1,0:T(8,128)(2,1)} %get-tuple-element.114), channel_id=1, source_target_pairs={{0,2},{1,3},{2,0},{3,1},{4,6},{5,7},{6,4},{7,5},{8,10},{9,11},{10,... | collective-permute-start | bytes 983048 | tf_op jit(solution)/shard_map/ppermute | solution.py:1031
  182.6 58.0 %collective-permute-start.18 = (bf16[512,1280]{1,0:T(8,128)(2,1)}, bf16[512,1280]{1,0:T(8,128)(2,1)}, u32[]{:S(2)}, u32[]{:S(2)}) collective-permute-start(bf16[512,1280]{1,0:T(8,128)(2,1)} %get-tuple-element.122), channel_id=1, source_target_pairs={{0,2},{1,3},{2,6},{3,7},{4,10},{5,11},{6,14},{7,15},{8,0},{9,1},{1... | collective-permute-start | bytes 3932168 | tf_op jit(solution)/shard_map/ppermute | solution.py:1031
  192.0 77.2 %all-to-all-start = ((bf16[8,160,1920]{2,1,0:T(8,128)(2,1)}), bf16[8,160,1920]{2,1,0:T(8,128)(2,1)}, u32[]{:S(2)}, u32[]{:S(2)}) async-start(bf16[8,160,1920]{2,1,0:T(8,128)(2,1)} %bitcast.79), calls=%async_computation | async-start | bytes 9830400 | tf_op jit(solution)/shard_map/all_to_all | solution.py:1201
  263.8 50.4 %collective-permute-start.21 = (bf16[1,512,1280]{2,1,0:T(8,128)(2,1)}, bf16[1,512,1280]{2,1,0:T(8,128)(2,1)}, u32[]{:S(2)}, u32[]{:S(2)}) collective-permute-start(bf16[1,512,1280]{2,1,0:T(8,128)(2,1)} %back.3), channel_id=1, source_target_pairs={{0,2},{1,3},{2,0},{3,1},{4,6},{5,7},{6,4},{7,5},{8,10},{9,11},{10,... | collective-permute-start | bytes 3932168 | tf_op jit(solution)/shard_map/ppermute | solution.py:1031
  265.7 17.9 %collective-permute-start.22 = (bf16[320,1024]{1,0:T(8,128)(2,1)}, bf16[320,1024]{1,0:T(8,128)(2,1)}, u32[]{:S(2)}, u32[]{:S(2)}) collective-permute-start(bf16[320,1024]{1,0:T(8,128)(2,1)} %get-tuple-element.138), channel_id=1, source_target_pairs={{0,16},{1,17},{2,18},{3,19},{4,20},{5,21},{6,22},{7,23},{8,24},{9,... | collective-permute-start | bytes 1966088 | tf_op jit(solution)/shard_map/ppermute | solution.py:1031
  267.2 30.9 %collective-permute-start.23 = (bf16[320,1024]{1,0:T(8,128)(2,1)}, bf16[320,1024]{1,0:T(8,128)(2,1)}, u32[]{:S(2)}, u32[]{:S(2)}) collective-permute-start(bf16[320,1024]{1,0:T(8,128)(2,1)} %get-tuple-element.139), channel_id=1, source_target_pairs={{0,1},{1,0},{2,3},{3,2},{4,5},{5,4},{6,7},{7,6},{8,9},{9,8},{10,11... | collective-permute-start | bytes 1966088 | tf_op jit(solution)/shard_map/ppermute | solution.py:1031
  268.6 29.5 %collective-permute-start.24 = (bf16[320,1024]{1,0:T(8,128)(2,1)}, bf16[320,1024]{1,0:T(8,128)(2,1)}, u32[]{:S(2)}, u32[]{:S(2)}) collective-permute-start(bf16[320,1024]{1,0:T(8,128)(2,1)} %get-tuple-element.140), channel_id=1, source_target_pairs={{0,17},{1,16},{2,19},{3,18},{4,21},{5,20},{6,23},{7,22},{8,25},{9,... | collective-permute-start | bytes 1966088 | tf_op jit(solution)/shard_map/ppermute | solution.py:1031
  272.6 35.7 %collective-permute-start.25 = (bf16[160,1920]{1,0:T(8,128)(2,1)}, bf16[160,1920]{1,0:T(8,128)(2,1)}, u32[]{:S(2)}, u32[]{:S(2)}) collective-permute-start(bf16[160,1920]{1,0:T(8,128)(2,1)} %total.2.a_ref), channel_id=1, source_target_pairs={{0,4},{1,5},{2,6},{3,7},{4,0},{5,1},{6,2},{7,3},{8,12},{9,13},{10,... | collective-permute-start | bytes 1843208 | tf_op jit(solution)/shard_map/ppermute | solution.py:1031
  300.5 41.0 %collective-permute-start.28 = (bf16[320,1024]{1,0:T(8,128)(2,1)}, bf16[320,1024]{1,0:T(8,128)(2,1)}, u32[]{:S(2)}, u32[]{:S(2)}) collective-permute-start(bf16[320,1024]{1,0:T(8,128)(2,1)} %total.3.a_ref), channel_id=1, source_target_pairs={{0,4},{1,5},{2,6},{3,7},{4,0},{5,1},{6,2},{7,3},{8,12},{9,13},{10,... | collective-permute-start | bytes 1966088 | tf_op jit(solution)/shard_map/ppermute | solution.py:1031
  310.5 15.3 %collective-permute-start.27 = (bf16[160,1920]{1,0:T(8,128)(2,1)}, bf16[160,1920]{1,0:T(8,128)(2,1)S(1)}, u32[]{:S(2)}, u32[]{:S(2)}) collective-permute-start(bf16[160,1920]{1,0:T(8,128)(2,1)} %add.135.refs_0_), channel_id=1, source_target_pairs={{0,16},{1,17},{2,18},{3,19},{4,20},{5,21},{6,22},{7,23},{8,24},{9,... | collective-permute-start | bytes 1843208 | tf_op jit(solution)/shard_map/ppermute | solution.py:1031
  312.0 29.5 %collective-permute-start.26 = (bf16[160,1920]{1,0:T(8,128)(2,1)}, bf16[160,1920]{1,0:T(8,128)(2,1)}, u32[]{:S(2)}, u32[]{:S(2)}) collective-permute-start(bf16[160,1920]{1,0:T(8,128)(2,1)} %add.135.refs_0_), channel_id=1, source_target_pairs={{0,2},{1,3},{2,0},{3,1},{4,6},{5,7},{6,4},{7,5},{8,10},{9,11},{10,... | collective-permute-start | bytes 1843208 | tf_op jit(solution)/shard_map/ppermute | solution.py:1031
  343.8 24.0 %collective-permute-start.32 = (bf16[320,1024]{1,0:T(8,128)(2,1)}, bf16[320,1024]{1,0:T(8,128)(2,1)S(1)}, u32[]{:S(2)}, u32[]{:S(2)}) collective-permute-start(bf16[320,1024]{1,0:T(8,128)(2,1)} %add.136.refs_0_), channel_id=1, source_target_pairs={{0,2},{1,3},{2,0},{3,1},{4,6},{5,7},{6,4},{7,5},{8,10},{9,11},{10,... | collective-permute-start | bytes 1966088 | tf_op jit(solution)/shard_map/ppermute | solution.py:1031
  343.8 24.0 %collective-permute-start.31 = (bf16[160,1920]{1,0:T(8,128)(2,1)}, bf16[160,1920]{1,0:T(8,128)(2,1)S(1)}, u32[]{:S(2)}, u32[]{:S(2)}) collective-permute-start(bf16[160,1920]{1,0:T(8,128)(2,1)} %collective-permute-done.26.refs_1_), channel_id=1, source_target_pairs={{0,16},{1,17},{2,18},{3,19},{4,20},{5,21},{6,22},{7,23},{8,24},{9,... | collective-permute-start | bytes 1843208 | tf_op jit(solution)/shard_map/ppermute | solution.py:1031
  344.1 28.0 %collective-permute-start.30 = (bf16[320,1024]{1,0:T(8,128)(2,1)}, bf16[320,1024]{1,0:T(8,128)(2,1)S(1)}, u32[]{:S(2)}, u32[]{:S(2)}) collective-permute-start(bf16[320,1024]{1,0:T(8,128)(2,1)} %add.136.refs_0_), channel_id=1, source_target_pairs={{0,16},{1,17},{2,18},{3,19},{4,20},{5,21},{6,22},{7,23},{8,24},{9,... | collective-permute-start | bytes 1966088 | tf_op jit(solution)/shard_map/ppermute | solution.py:1031
  345.8 26.4 %collective-permute-start.36 = (bf16[160,1920]{1,0:T(8,128)(2,1)S(1)}, bf16[160,1920]{1,0:T(8,128)(2,1)S(1)}, u32[]{:S(2)}, u32[]{:S(2)}) collective-permute-start(bf16[160,1920]{1,0:T(8,128)(2,1)S(1)} %collective-permute-done.27.refs_2_), channel_id=1, source_target_pairs={{0,8},{1,9},{2,10},{3,11},{4,12},{5,13},{6,14},{7,15},{8,0},{9,1},... | collective-permute-start | bytes 1843208 | tf_op jit(solution)/shard_map/ppermute | solution.py:1031
  345.8 54.8 %collective-permute-start.29 = (bf16[512,1280]{1,0:T(8,128)(2,1)}, bf16[512,1280]{1,0:T(8,128)(2,1)}, u32[]{:S(2)}, u32[]{:S(2)}) collective-permute-start(bf16[512,1280]{1,0:T(8,128)(2,1)} %get-tuple-element.148), channel_id=1, source_target_pairs={{0,2},{1,3},{2,6},{3,7},{4,10},{5,11},{6,14},{7,15},{8,0},{9,1},{1... | collective-permute-start | bytes 3932168 | tf_op jit(solution)/shard_map/ppermute | solution.py:1031
  372.9 27.8 %collective-permute-start.44 = (bf16[320,1024]{1,0:T(8,128)(2,1)S(1)}, bf16[320,1024]{1,0:T(8,128)(2,1)S(1)}, u32[]{:S(2)}, u32[]{:S(2)}) collective-permute-start(bf16[320,1024]{1,0:T(8,128)(2,1)S(1)} %collective-permute-done.32.refs_1_), channel_id=1, source_target_pairs={{0,16},{1,17},{2,18},{3,19},{4,20},{5,21},{6,22},{7,23},{8,24},{9,... | collective-permute-start | bytes 1966088 | tf_op jit(solution)/shard_map/ppermute | solution.py:1031
  (48 other events, 589.3 us)

commit v19 on v18

--- a/solution.py
+++ b/solution.py
@@ -594,12 +594,16 @@
                 out[...] = grad_att[:, (i ^ j) * cols : ((i ^ j) + 1) * cols]
 
 
-def tail_kernel(at, p0, p1, p2, p3, x_ref, g_ref, own0, own1, own2, half, other, gain, *refs, rows, hrows):
+def tail_kernel(at, p0, p1, p2, p3, x_ref, g_ref, own0, own1, own2, half0, half, other0, other, gain, *refs, rows, hrows):
     w_s, sems = refs[-2:]
     outs = refs[:-2]
 
     def copies(i):
-        parts = (((own0, own1, own2)[i], at[1], rows), (half.at[i], at[2], hrows), (other.at[i], at[3], hrows))
+        parts = (
+            ((own0, own1, own2)[i], at[1], rows),
+            (half.at[i - 1] if i else half0, at[2], hrows),
+            (other.at[i - 1] if i else other0, at[3], hrows),
+        )
         return [
             pltpu.make_async_copy(
                 part, w_s.at[i, pl.ds(pl.multiple_of(start, 16), n), :], sems.at[3 * i + k]
@@ -639,10 +643,10 @@
     whole = lambda *shape: pl.BlockSpec(shape, lambda i, m: (0,) * len(shape), pipeline_mode=once)
     wide = pl.BlockSpec((tile, d), row)
     slim = pl.BlockSpec((tile, cols), row)
-    if len(weights) == 5:
-        body = functools.partial(tail_kernel, rows=weights[0].shape[0], hrows=weights[3].shape[1])
+    if len(weights) == 7:
+        body = functools.partial(tail_kernel, rows=weights[0].shape[0], hrows=weights[3].shape[0])
         scratch = [pltpu.VMEM((3, d, d), bf16), pltpu.SemaphoreType.DMA((9,))]
-        weight_specs = [pl.BlockSpec(memory_space=pl.ANY)] * 5
+        weight_specs = [pl.BlockSpec(memory_space=pl.ANY)] * 7
     else:
         body = whole_tail_kernel
         scratch = []
@@ -1137,10 +1141,12 @@
         places = (z, z + way, z + 2 * way, last)
 
         half_rows = wrows // 2
-        half_w = jnp.stack([rows_at(w, gc * half_rows, half_rows) for w in (w_proj, w_in, w_out)])
         if pair:
-            half_w = send(after(half_w, other_w), wt_mate)
+            half_a = send(after(rows_at(w_proj, gc * half_rows, half_rows), other_w), wt_mate)
+            half_w = jnp.stack([rows_at(w, gc * half_rows, half_rows) for w in (w_in, w_out)])
+            half_w = send(after(half_w, half_a), wt_mate)
         else:
+            half_w = jnp.stack([rows_at(w, gc * half_rows, half_rows) for w in (w_proj, w_in, w_out)])
             half_w = lax.all_gather(half_w, "wt", axis=0, tiled=False)
 
         dim_scale = scale_base / math.sqrt(HD) * jax.nn.softplus(query_scale)
@@ -1152,8 +1158,9 @@
         fixed = (lane, mine, wt, gain_attn[None], wide_w, lane_scale, ones, group_len)
         carried = project(((own, own_share), (got1, got1_share)), places[:2], *fixed)
         got3_share = send(after(got3, carried[0]), lane_share)
+        first_done = (lambda x: after(x, half_a)) if pair else (lambda x: x)
         all_normed, queries, keyval, inputs = project(
-            ((got2, got2_share), (got3, got3_share)), places[2:], *fixed, carried=carried
+            ((got2, got2_share), (got3, first_done(got3_share))), places[2:], *fixed, carried=carried
         )
         grad_mlp = send(after(cotangent[0], got3_share), to_host)
 
@@ -1170,7 +1177,8 @@
             w_trans = flat_all.T
         normed_trans = transpose(after(all_normed, w_trans))
         if pair:
-            weights = (w_proj, w_in, w_out, half_w, half_mate)
+            mate_a = send(after(half_a, *att_pieces[1:2]), core_mate)
+            weights = (w_proj, w_in, w_out, half_a, half_w, mate_a, half_mate)
             starts = (wt * wrows, (1 - wt) * wrows + gc * half_rows, (1 - wt) * wrows + (1 - gc) * half_rows)
         else:
             one = gc == 0

time: 420 us -> 418 us (level)
    ppermute x47 -> x49, waiting for transfers between devices: 109 us -> 106 us  [send(): return lax.ppermute(value, AXES, pairs(target))]
    ppermute x47 -> x49, starting transfers between devices: 56 us -> 57.9 us  [send(): return lax.ppermute(value, AXES, pairs(target))]
  transfers between devices with their start and end apart: 48 -> 50, of which waited for: 19 -> 17; matrix products, arithmetic and copies ran while one was open for 3% -> 3% of each run, Pallas kernels for 47% -> 48%
where the time goes in v19:
time: 418 us; the launch traced here: 411 us
  Pallas kernels  224 us (54%)
  waiting for transfers between devices  106 us (25%)
  starting transfers between devices  63.9 us (15%)
  local copies, waits for them, and re-layouts  11.3 us (3%)
    ppermute x49, waiting for transfers between devices, send(): return lax.ppermute(value, AXES, pairs(target))  106 us
    ppermute x49, starting transfers between devices, send(): return lax.ppermute(value, AXES, pairs(target))  57.9 us
    pallas_call x1, Pallas kernels, attn_bwd(): pl.pallas_call(functools.partial(bwd_kernel, first=group * nh, nh=nh, bq=...  43.5 us
    pallas_call x1, Pallas kernels, attn_fwd(): pl.pallas_call(functools.partial(fwd_kernel, nh=nh, bq=bq, bk=bk, nk=n //...  25.9 us
    pallas_call x2, Pallas kernels, project(): pl.pallas_call(functools.partial(project_kernel, count=count, halves=len(...  22.7 us
    pallas_call x1, Pallas kernels, tail(): pl.pallas_call(body, out_shape=[pltpu.HBM((rows, d), bf16)] + [pltpu.HBM(...  21.5 us
    pallas_call x2, Pallas kernels, share(): pl.pallas_call(share_kernel, out_shape=pltpu.HBM((d, n * w), bf16), grid_...  14.7 us
    pallas_call x1, Pallas kernels, cross(): pl.pallas_call(cross_kernel, out_shape=[pltpu.HBM((w // 2, cols), bf16)]...  11.6 us
  transfers between devices with their start and end apart: 50, of which 17 were waited for; matrix products, arithmetic and copies ran while one was open for 3% of the time, Pallas kernels for 48%

profile of v19, /device:TPU:0, one launch (start us, length us, event | category | flops | bytes accessed | tf_op | source)
XLA Modules:
  0.0 410.7 jit_solution(13439397942126141190)
XLA Ops:
  2.0 4.5 %pick.1.x_ref.a_ref = bf16[640,1024]{1,0:T(8,128)(2,1)} custom-call(s32[1]{0:T(128)} %bitcast.mine.shard, bf16[640,3840]{1,0:T(8,128)(2,1)} %w_ref.1), custom_call_target="tpu_custom_call" | custom-call | flops 5000000000 | bytes 1000 | tf_op jit(solution)/shard_map/pick/pallas_call | solution.py:352
  9.5 5.4 %collective-permute-start.5 = (bf16[512,1280]{1,0:T(8,128)(2,1)S(1)}, bf16[512,1280]{1,0:T(8,128)(2,1)}, u32[]{:S(2)}, u32[]{:S(2)}) collective-permute-start(bf16[512,1280]{1,0:T(8,128)(2,1)S(1)} %bitcast.67), channel_id=1, source_target_pairs={{0,8},{1,9},{2,10},{3,11},{12,4},{13,5},{14,6},{15,7},{16,24},{17,... | collective-permute-start | bytes 3932168 | tf_op jit(solution)/shard_map/ppermute | solution.py:1035
  15.6 4.0 stretch.2.refs_5_
  25.4 11.8 %collective-permute-done.7.x_ref.b_ref = bf16[640,1024]{1,0:T(8,128)(2,1)} collective-permute-done((bf16[640,1024]{1,0:T(8,128)(2,1)}, bf16[640,1024]{1,0:T(8,128)(2,1)}, u32[]{:S(2)}, u32[]{:S(2)}) %collective-permute-start.7) | collective-permute-done | bytes 1310752 | tf_op jit(solution)/shard_map/ppermute | solution.py:1035
  39.6 4.5 %collective-permute-start.6 = (bf16[512,1280]{1,0:T(8,128)(2,1)}, bf16[512,1280]{1,0:T(8,128)(2,1)}, u32[]{:S(2)}, u32[]{:S(2)}) collective-permute-start(bf16[512,1280]{1,0:T(8,128)(2,1)} %collective-permute-done.1.refs_2_), channel_id=1, source_target_pairs={{0,8},{1,9},{2,10},{3,11},{12,4},{13,5},{14,6},{15,7},{16,24},{17,... | collective-permute-start | bytes 3932168 | tf_op jit(solution)/shard_map/ppermute | solution.py:1035
  44.1 4.0 stretch.3.refs_6_
  48.3 4.0 collective-permute-start.4
  54.7 11.2 %project.2 = (bf16[2048,1280]{1,0:T(8,128)(2,1)}, bf16[2048,512]{1,0:T(8,128)(2,1)}, bf16[2048,1024]{1,0:T(8,128)(2,1)}, bf16[512,1280]{1,0:T(8,128)(2,1)}) custom-call(s32[5]{0:T(128)S(1)} %stack.100.info, bf16[512,1280]{1,0:T(8,128)(2,1)S(1)} %bitcast.68, bf16[512,1280]{1,0:T(8,128)(2,1)} %collective-permute-done.5.refs_1_, ...), custom_call_target="tpu_custom_call" | custom-call | flops 15000000512 | bytes 1000 | tf_op jit(solution)/shard_map/project/pallas_call | solution.py:518
  75.1 11.6 %project.3 = (bf16[2048,1280]{1,0:T(8,128)(2,1)}, bf16[2048,512]{1,0:T(8,128)(2,1)}, bf16[2048,1024]{1,0:T(8,128)(2,1)}, bf16[512,1280]{1,0:T(8,128)(2,1)}) custom-call(s32[5]{0:T(128)S(1)} %stack.97.info, bf16[512,1280]{1,0:T(8,128)(2,1)S(1)} %collective-permute-done.2.refs_0_, ...), custom_call_target="tpu_custom_call", output_to_operand_aliasing={{0}: (11, {}), {1}: (12, {}), {2}: (13, {})} | custom-call | flops 15000000512 | bytes 1000 | tf_op jit(solution)/shard_map/project/pallas_call | solution.py:518
  86.6 25.9 %attn_fwd.1 = (bf16[2048,320]{1,0:T(8,128)(2,1)}, bf16[2048,512]{1,0:T(8,128)(2,1)}, bf16[2048,512]{1,0:T(8,128)(2,1)}) custom-call(s32[16]{0:T(128)S(1)} %reshape.183.flags, bf16[2048,512]{1,0:T(8,128)(2,1)} %get-tuple-element.104.q_ref, bf16[2048,1024]{1,0:T(8,128)(2,1)} %get-tuple-element.105.kv.kk.vv, s32[2048,1]{1,0:T(8,128)S(1)} %copy.29.segc, ...), custom_call_target="tpu_custom_call" | custom-call | flops 10000000 | bytes 1000 | tf_op jit(solution)/shard_map/attn_fwd/pallas_call | solution.py:172
  119.9 6.4 %order.1.w_ref = bf16[1024,1280]{1,0:T(8,128)(2,1)} custom-call(s32[1]{0:T(128)} %bitcast.10.own_first, bf16[640,1024]{1,0:T(8,128)(2,1)} %pick.1.x_ref.a_ref, bf16[640,1024]{1,0:T(8,128)(2,1)} %collective-permute-done.7.x_ref.b_ref), custom_call_target="tpu_custom_call" | custom-call | flops 199999995904 | bytes 1000 | tf_op jit(solution)/shard_map/order/pallas_call | solution.py:408
  126.4 7.9 %transpose.15.x_ref = bf16[1280,2048]{1,0:T(8,128)(2,1)} custom-call(bf16[2048,1280]{1,0:T(8,128)(2,1)} %get-tuple-element.113.x_ref), custom_call_target="tpu_custom_call" | custom-call | flops 1000000 | bytes 1000 | tf_op jit(solution)/shard_map/transpose/pallas_call | solution.py:432
  136.6 21.5 %tail.1 = (bf16[512,1280]{1,0:T(8,128)(2,1)}, bf16[3,512,1280]{2,1,0:T(8,128)(2,1)}, bf16[3,512,1280]{2,1,0:T(8,128)(2,1)}, f32[512,1280]{1,0:T(8,128)}, bf16[51...) custom-call(s32[4]{0:T(128)S(1)} %pad_add_fusion.at, ...), custom_call_target="tpu_custom_call" | custom-call | flops 10000000 | bytes 1000 | tf_op jit(solution)/shard_map/tail/pallas_call | solution.py:654
  160.8 7.5 %share.2 = bf16[1280,1920]{1,0:T(8,128)(2,1)} custom-call(s32[1]{0:T(128)} %bitcast.20.col, bf16[3,512,1280]{2,1,0:T(8,128)(2,1)} %get-tuple-element.122.left, bf16[3,512,1280]{2,1,0:T(8,128)(2,1)} %get-tuple-element.123.right), custom_call_target="tpu_custom_call" | custom-call | flops 1000000 | bytes 1000 | tf_op jit(solution)/shard_map/share/pallas_call | solution.py:690
  168.5 7.2 %share.3.a_ref = bf16[1280,1920]{1,0:T(8,128)(2,1)} custom-call(s32[1]{0:T(128)} %bitcast.21.col, bf16[3,512,1280]{2,1,0:T(8,128)(2,1)} %get-tuple-element.122.left, bf16[3,512,1280]{2,1,0:T(8,128)(2,1)} %get-tuple-element.123.right), custom_call_target="tpu_custom_call" | custom-call | flops 1000000 | bytes 1000 | tf_op jit(solution)/shard_map/share/pallas_call | solution.py:690
  180.7 7.8 %add_rows.1 = bf16[1280,1920]{1,0:T(8,128)(2,1)} custom-call(bf16[1280,1920]{1,0:T(8,128)(2,1)} %share.3.a_ref, bf16[1280,1920]{1,0:T(8,128)(2,1)} %collective-permute-done.21.b_ref), custom_call_target="tpu_custom_call" | custom-call | flops 1000000 | bytes 1000 | tf_op jit(solution)/shard_map/add_rows/pallas_call | solution.py:770
  188.5 6.0 %all-to-all-start = ((bf16[8,160,1920]{2,1,0:T(8,128)(2,1)}), bf16[8,160,1920]{2,1,0:T(8,128)(2,1)}, u32[]{:S(2)}, u32[]{:S(2)}) async-start(bf16[8,160,1920]{2,1,0:T(8,128)(2,1)} %bitcast.77), calls=%async_computation | async-start | bytes 9830400 | tf_op jit(solution)/shard_map/all_to_all | solution.py:1209
  194.5 43.5 %attn_bwd.1 = (bf16[2048,1024]{1,0:T(8,128)(2,1)}, f32[8,128]{1,0:T(8,128)}) custom-call(s32[16]{0:T(128)S(1)} %copy-done.6, s32[1]{0:T(128)} %bitcast.mine.shard, bf16[2048,512]{1,0:T(8,128)(2,1)} %get-tuple-element.129.qa, bf16[2048,1024]{1,0:T(8,128)(2,1)} %get-tuple-element.105.kv.kk.vv, bf16[2048,1024]{1,0:T(8,128)(2,1)} %get-tuple-element.105.kv.kk.vv, ...), custom_call_target="tpu_custom_call" | custom-call | flops 299999985664 | bytes 1000 | tf_op jit(solution)/shard_map/attn_bwd/pallas_call | solution.py:314
  238.0 6.8 %back.2 = bf16[2,512,1280]{2,1,0:T(8,128)(2,1)} custom-call(s32[2]{0:T(128)S(1)} %pad_add_fusion.1.shards, bf16[2048,1024]{1,0:T(8,128)(2,1)} %get-tuple-element.138.g_ref, bf16[1024,1280]{1,0:T(8,128)(2,1)} %order.1.w_ref), custom_call_target="tpu_custom_call" | custom-call | flops 1000000 | bytes 1000 | tf_op jit(solution)/shard_map/back/pallas_call | solution.py:928
  244.9 11.6 %cross.1 = (bf16[320,1024]{1,0:T(8,128)(2,1)}, bf16[320,1024]{1,0:T(8,128)(2,1)}, bf16[320,1024]{1,0:T(8,128)(2,1)}, bf16[320,1024]{1,0:T(8,128)(2,1)}) custom-call(s32[2]{0:T(128)S(1)} %pad_add_fusion.2.at, bf16[1280,2048]{1,0:T(8,128)(2,1)} %transpose.15.x_ref, bf16[2048,1024]{1,0:T(8,128)(2,1)} %get-tuple-element.138.g_ref), custom_call_target="tpu_custom_call" | custom-call | flops 1000000 | bytes 1000 | tf_op jit(solution)/shard_map/cross/pallas_call | solution.py:850
  256.5 4.7 %back.3 = bf16[1,512,1280]{2,1,0:T(8,128)(2,1)} custom-call(s32[1]{0:T(128)} %bitcast.25.shards, bf16[2048,1024]{1,0:T(8,128)(2,1)} %get-tuple-element.138.g_ref, bf16[1024,1280]{1,0:T(8,128)(2,1)} %order.1.w_ref, bf16[2,512,1280]{2,1,0:T(8,128)(2,1)S(1)} %collective-permute-done.22.refs_0_.core), custom_call_target="tpu_custom_call" | custom-call | flops 1000000 | bytes 1000 | tf_op jit(solution)/shard_map/back/pallas_call | solution.py:928
  273.0 8.0 %collective-permute-done.24 = bf16[320,1024]{1,0:T(8,128)(2,1)} collective-permute-done((bf16[320,1024]{1,0:T(8,128)(2,1)}, bf16[320,1024]{1,0:T(8,128)(2,1)}, u32[]{:S(2)}, u32[]{:S(2)}) %collective-permute-start.24) | collective-permute-done | bytes 655392 | tf_op jit(solution)/shard_map/ppermute | solution.py:1035
  281.0 14.5 %collective-permute-done.25 = bf16[320,1024]{1,0:T(8,128)(2,1)} collective-permute-done((bf16[320,1024]{1,0:T(8,128)(2,1)}, bf16[320,1024]{1,0:T(8,128)(2,1)}, u32[]{:S(2)}, u32[]{:S(2)}) %collective-permute-start.25) | collective-permute-done | bytes 655392 | tf_op jit(solution)/shard_map/ppermute | solution.py:1035
  298.0 7.8 %collective-permute-done.27.b_ref = bf16[160,1920]{1,0:T(8,128)(2,1)} collective-permute-done((bf16[160,1920]{1,0:T(8,128)(2,1)}, bf16[160,1920]{1,0:T(8,128)(2,1)}, u32[]{:S(2)}, u32[]{:S(2)}) %collective-permute-start.27) | collective-permute-done | bytes 614432 | tf_op jit(solution)/shard_map/ppermute | solution.py:1035
  311.1 6.6 %finish.1 = (bf16[512,1280]{1,0:T(8,128)(2,1)}, f32[1,1280]{1,0:T(1,128)S(1)}) custom-call(s32[1]{0:T(128)} %bitcast.mine.shard, bf16[2048,1024]{1,0:T(8,128)(2,1)} %get-tuple-element.138.g_ref, bf16[1024,1280]{1,0:T(8,128)(2,1)} %order.1.w_ref, bf16[2,512,1280]{2,1,0:T(8,128)(2,1)S(1)} %collective-permute-done.22.refs_0_.core, ...), custom_call_target="tpu_custom_call" | custom-call | flops 1000000 | bytes 1000 | tf_op jit(solution)/shard_map/finish/pallas_call | solution.py:966
  317.7 5.7 %collective-permute-done.29.refs_2_ = bf16[160,1920]{1,0:T(8,128)(2,1)} collective-permute-done((bf16[160,1920]{1,0:T(8,128)(2,1)}, bf16[160,1920]{1,0:T(8,128)(2,1)}, u32[]{:S(2)}, u32[]{:S(2)}) %collective-permute-start.29) | collective-permute-done | bytes 614432 | tf_op jit(solution)/shard_map/ppermute | solution.py:1035
  323.4 15.1 %collective-permute-done.28.refs_1_ = bf16[160,1920]{1,0:T(8,128)(2,1)} collective-permute-done((bf16[160,1920]{1,0:T(8,128)(2,1)}, bf16[160,1920]{1,0:T(8,128)(2,1)}, u32[]{:S(2)}, u32[]{:S(2)}) %collective-permute-start.28) | collective-permute-done | bytes 614432 | tf_op jit(solution)/shard_map/ppermute | solution.py:1035
  345.7 18.8 %collective-permute-done.34.refs_1_ = bf16[320,1024]{1,0:T(8,128)(2,1)S(1)} collective-permute-done((bf16[320,1024]{1,0:T(8,128)(2,1)}, bf16[320,1024]{1,0:T(8,128)(2,1)S(1)}, u32[]{:S(2)}, u32[]{:S(2)}) %collective-permute-start.34) | collective-permute-done | bytes 655392 | tf_op jit(solution)/shard_map/ppermute | solution.py:1035
  365.0 4.8 %collective-permute-done.32.refs_0_ = bf16[320,1024]{1,0:T(8,128)(2,1)S(1)} collective-permute-done((bf16[320,1024]{1,0:T(8,128)(2,1)}, bf16[320,1024]{1,0:T(8,128)(2,1)S(1)}, u32[]{:S(2)}, u32[]{:S(2)}) %collective-permute-start.32) | collective-permute-done | bytes 655392 | tf_op jit(solution)/shard_map/ppermute | solution.py:1035
  374.1 7.2 %place_tail.1 = (f32[4,160,1280]{2,1,0:T(8,128)}, f32[4,160,1280]{2,1,0:T(8,128)}, f32[4,160,1280]{2,1,0:T(8,128)}) custom-call(s32[3]{0:T(128)S(1)} %pad_add_fusion.3.at, bf16[160,1920]{1,0:T(8,128)(2,1)} %add.135.refs_0_, bf16[160,1920]{1,0:T(8,128)(2,1)} %collective-permute-done.28.refs_1_, bf16[160,1920]{1,0:T(8,128)(2,1)} %collective-permute-done.29.refs_2_, ...), custom_call_target="tpu_custom_call" | custom-call | flops 1000000 | bytes 1000 | tf_op jit(solution)/shard_map/place_tail/pallas_call | solution.py:813
  390.0 3.7 collective-permute-start.44
  405.9 4.4 %spread.3 = f32[2,320,3840]{2,1,0:T(8,128)} custom-call(s32[3]{0:T(128)S(1)} %pad_add_fusion.5.at, bf16[320,1024]{1,0:T(8,128)(2,1)S(1)} %collective-permute-done.32.refs_0_, bf16[320,1024]{1,0:T(8,128)(2,1)S(1)} %collective-permute-done.46.refs_1_, bf16[320,1024]{1,0:T(8,128)(2,1)} %collective-permute-done.47.refs_2_, ...), custom_call_target="tpu_custom_call", output_to_operand_aliasing={{}: (5, {})} | custom-call | flops 1000000 | bytes 1000 | tf_op jit(solution)/shard_map/spread/pallas_call | solution.py:892
  (205 shorter events, 94.9 us)
Async XLA Ops:
  0.6 21.2 %collective-permute-start.1 = (bf16[512,1280]{1,0:T(8,128)(2,1)}, bf16[512,1280]{1,0:T(8,128)(2,1)}, u32[]{:S(2)}, u32[]{:S(2)}) collective-permute-start(bf16[512,1280]{1,0:T(8,128)(2,1)} %bitcast.66), channel_id=1, source_target_pairs={{2,0},{3,1},{4,2},{5,3},{6,4},{7,5},{8,10},{9,11},{10,12},{11,13},... | collective-permute-start | bytes 3932168 | tf_op jit(solution)/shard_map/ppermute | solution.py:1035
  6.5 30.6 %collective-permute-start.7 = (bf16[640,1024]{1,0:T(8,128)(2,1)}, bf16[640,1024]{1,0:T(8,128)(2,1)}, u32[]{:S(2)}, u32[]{:S(2)}) collective-permute-start(bf16[640,1024]{1,0:T(8,128)(2,1)} %pick.1.x_ref.a_ref), channel_id=1, source_target_pairs={{0,1},{1,0},{2,3},{3,2},{4,5},{5,4},{6,7},{7,6},{8,9},{9,8},{10,11... | collective-permute-start | bytes 3932168 | tf_op jit(solution)/shard_map/ppermute | solution.py:1035
  9.5 42.8 %collective-permute-start.5 = (bf16[512,1280]{1,0:T(8,128)(2,1)S(1)}, bf16[512,1280]{1,0:T(8,128)(2,1)}, u32[]{:S(2)}, u32[]{:S(2)}) collective-permute-start(bf16[512,1280]{1,0:T(8,128)(2,1)S(1)} %bitcast.67), channel_id=1, source_target_pairs={{0,8},{1,9},{2,10},{3,11},{12,4},{13,5},{14,6},{15,7},{16,24},{17,... | collective-permute-start | bytes 3932168 | tf_op jit(solution)/shard_map/ppermute | solution.py:1035
  14.9 56.8 %collective-permute-start = (s32[1,2048]{1,0:T(1,128)S(1)}, s32[1,2048]{1,0:T(1,128)S(1)}, u32[]{:S(2)}, u32[]{:S(2)}) collective-permute-start(s32[1,2048]{1,0:T(1,128)S(1)} %copy-done.25), channel_id=1, source_target_pairs={{0,8},{1,9},{2,10},{3,11},{4,12},{5,13},{6,14},{7,15},{8,0},{9,1},... | collective-permute-start | bytes 24584 | tf_op jit(solution)/shard_map/ppermute | solution.py:1035
  21.9 26.3 %collective-permute-start.2 = (bf16[512,1280]{1,0:T(8,128)(2,1)}, bf16[512,1280]{1,0:T(8,128)(2,1)S(1)}, u32[]{:S(2)}, u32[]{:S(2)}) collective-permute-start(bf16[512,1280]{1,0:T(8,128)(2,1)} %collective-permute-done.1.refs_2_), channel_id=1, source_target_pairs={{2,0},{3,1},{4,2},{5,3},{10,12},{11,13},{12,14},{13,15},{18,16},{1... | collective-permute-start | bytes 3932168 | tf_op jit(solution)/shard_map/ppermute | solution.py:1035
  37.1 36.1 %collective-permute-start.9 = (bf16[320,1280]{1,0:T(8,128)(2,1)}, bf16[320,1280]{1,0:T(8,128)(2,1)}, u32[]{:S(2)}, u32[]{:S(2)}) collective-permute-start(bf16[320,1280]{1,0:T(8,128)(2,1)} %constant_dynamic-slice_fusion.4), channel_id=1, source_target_pairs={{0,1},{1,0},{2,3},{3,2},{4,5},{5,4},{6,7},{7,6},{8,9},{9,8},{10,11... | collective-permute-start | bytes 2457608 | tf_op jit(solution)/shard_map/ppermute | solution.py:1035
  48.3 19.6 %collective-permute-start.4 = (bf16[512,1280]{1,0:T(8,128)(2,1)S(1)}, bf16[512,1280]{1,0:T(8,128)(2,1)}, u32[]{:S(2)}, u32[]{:S(2)}) collective-permute-start(bf16[512,1280]{1,0:T(8,128)(2,1)S(1)} %broadcast_select_fusion), channel_id=1, source_target_pairs={{0,2},{1,3},{2,0},{3,1},{12,14},{13,15},{14,12},{15,13},{16,18},{1... | collective-permute-start | bytes 3932168 | tf_op jit(solution)/shard_map/ppermute | solution.py:1035
  52.3 22.8 %collective-permute-start.3 = (bf16[512,1280]{1,0:T(8,128)(2,1)S(1)}, bf16[512,1280]{1,0:T(8,128)(2,1)}, u32[]{:S(2)}, u32[]{:S(2)}) collective-permute-start(bf16[512,1280]{1,0:T(8,128)(2,1)S(1)} %collective-permute-done.2.refs_0_), channel_id=1, source_target_pairs={{0,8},{1,9},{2,10},{3,11},{12,4},{13,5},{14,6},{15,7},{16,24},{17,... | collective-permute-start | bytes 3932168 | tf_op jit(solution)/shard_map/ppermute | solution.py:1035
  73.2 39.4 %collective-permute-start.10 = (bf16[2,320,1280]{2,1,0:T(8,128)(2,1)}, bf16[2,320,1280]{2,1,0:T(8,128)(2,1)}, u32[]{:S(2)}, u32[]{:S(2)}) collective-permute-start(bf16[2,320,1280]{2,1,0:T(8,128)(2,1)} %pad_maximum_fusion), channel_id=1, source_target_pairs={{0,1},{1,0},{2,3},{3,2},{4,5},{5,4},{6,7},{7,6},{8,9},{9,8},{10,11... | collective-permute-start | bytes 4915208 | tf_op jit(solution)/shard_map/ppermute | solution.py:1035
  74.5 38.1 %collective-permute-start.11 = (bf16[512,1280]{1,0:T(8,128)(2,1)}, bf16[512,1280]{1,0:T(8,128)(2,1)S(1)}, u32[]{:S(2)}, u32[]{:S(2)}) collective-permute-start(bf16[512,1280]{1,0:T(8,128)(2,1)} %bitcast.88), channel_id=1, source_target_pairs={{0,8},{1,9},{2,0},{3,1},{4,10},{5,11},{6,2},{7,3},{8,12},{9,13},{1... | collective-permute-start | bytes 3932168 | tf_op jit(solution)/shard_map/ppermute | solution.py:1035
  117.8 16.5 %collective-permute-start.13 = (bf16[512,320]{1,0:T(8,128)(2,1)}, bf16[512,320]{1,0:T(8,128)(2,1)}, u32[]{:S(2)}, u32[]{:S(2)}) collective-permute-start(bf16[512,320]{1,0:T(8,128)(2,1)} %get-tuple-element.184), channel_id=1, source_target_pairs={{0,2},{1,3},{2,0},{3,1},{4,6},{5,7},{6,4},{7,5},{8,10},{9,11},{10,... | collective-permute-start | bytes 983048 | tf_op jit(solution)/shard_map/ppermute | solution.py:1035
  117.8 18.8 %collective-permute-start.14 = (bf16[512,320]{1,0:T(8,128)(2,1)}, bf16[512,320]{1,0:T(8,128)(2,1)}, u32[]{:S(2)}, u32[]{:S(2)}) collective-permute-start(bf16[512,320]{1,0:T(8,128)(2,1)} %get-tuple-element.183), channel_id=1, source_target_pairs={{0,10},{1,11},{2,8},{3,9},{4,14},{5,15},{6,12},{7,13},{8,2},{9,3},... | collective-permute-start | bytes 983048 | tf_op jit(solution)/shard_map/ppermute | solution.py:1035
  119.2 17.5 %collective-permute-start.16 = (bf16[2,320,1280]{2,1,0:T(8,128)(2,1)}, bf16[2,320,1280]{2,1,0:T(8,128)(2,1)}, u32[]{:S(2)}, u32[]{:S(2)}) collective-permute-start(bf16[2,320,1280]{2,1,0:T(8,128)(2,1)} %collective-permute-done.10.half), channel_id=1, source_target_pairs={{0,8},{1,9},{2,10},{3,11},{4,12},{5,13},{6,14},{7,15},{8,0},{9,1},... | collective-permute-start | bytes 4915208 | tf_op jit(solution)/shard_map/ppermute | solution.py:1035
  119.9 16.7 %collective-permute-start.15 = (bf16[320,1280]{1,0:T(8,128)(2,1)}, bf16[320,1280]{1,0:T(8,128)(2,1)}, u32[]{:S(2)}, u32[]{:S(2)}) collective-permute-start(bf16[320,1280]{1,0:T(8,128)(2,1)} %collective-permute-done.9.half0), channel_id=1, source_target_pairs={{0,8},{1,9},{2,10},{3,11},{4,12},{5,13},{6,14},{7,15},{8,0},{9,1},... | collective-permute-start | bytes 2457608 | tf_op jit(solution)/shard_map/ppermute | solution.py:1035
  158.9 16.7 %collective-permute-start.19 = (bf16[512,320]{1,0:T(8,128)(2,1)}, bf16[512,320]{1,0:T(8,128)(2,1)S(1)}, u32[]{:S(2)}, u32[]{:S(2)}) collective-permute-start(bf16[512,320]{1,0:T(8,128)(2,1)} %get-tuple-element.126), channel_id=1, source_target_pairs={{0,10},{1,11},{2,8},{3,9},{4,14},{5,15},{6,12},{7,13},{8,2},{9,3},... | collective-permute-start | bytes 983048 | tf_op jit(solution)/shard_map/ppermute | solution.py:1035
  159.1 19.9 %collective-permute-start.18 = (bf16[512,320]{1,0:T(8,128)(2,1)}, bf16[512,320]{1,0:T(8,128)(2,1)S(1)}, u32[]{:S(2)}, u32[]{:S(2)}) collective-permute-start(bf16[512,320]{1,0:T(8,128)(2,1)} %get-tuple-element.120), channel_id=1, source_target_pairs={{0,2},{1,3},{2,0},{3,1},{4,6},{5,7},{6,4},{7,5},{8,10},{9,11},{10,... | collective-permute-start | bytes 983048 | tf_op jit(solution)/shard_map/ppermute | solution.py:1035
  180.3 57.7 %collective-permute-start.20 = (bf16[512,1280]{1,0:T(8,128)(2,1)}, bf16[512,1280]{1,0:T(8,128)(2,1)}, u32[]{:S(2)}, u32[]{:S(2)}) collective-permute-start(bf16[512,1280]{1,0:T(8,128)(2,1)} %get-tuple-element.128), channel_id=1, source_target_pairs={{0,2},{1,3},{2,6},{3,7},{4,10},{5,11},{6,14},{7,15},{8,0},{9,1},{1... | collective-permute-start | bytes 3932168 | tf_op jit(solution)/shard_map/ppermute | solution.py:1035
  188.5 78.2 %all-to-all-start = ((bf16[8,160,1920]{2,1,0:T(8,128)(2,1)}), bf16[8,160,1920]{2,1,0:T(8,128)(2,1)}, u32[]{:S(2)}, u32[]{:S(2)}) async-start(bf16[8,160,1920]{2,1,0:T(8,128)(2,1)} %bitcast.77), calls=%async_computation | async-start | bytes 9830400 | tf_op jit(solution)/shard_map/all_to_all | solution.py:1209
  261.1 50.0 %collective-permute-start.23 = (bf16[1,512,1280]{2,1,0:T(8,128)(2,1)}, bf16[1,512,1280]{2,1,0:T(8,128)(2,1)}, u32[]{:S(2)}, u32[]{:S(2)}) collective-permute-start(bf16[1,512,1280]{2,1,0:T(8,128)(2,1)} %back.3), channel_id=1, source_target_pairs={{0,2},{1,3},{2,0},{3,1},{4,6},{5,7},{6,4},{7,5},{8,10},{9,11},{10,... | collective-permute-start | bytes 3932168 | tf_op jit(solution)/shard_map/ppermute | solution.py:1035
  263.2 17.9 %collective-permute-start.24 = (bf16[320,1024]{1,0:T(8,128)(2,1)}, bf16[320,1024]{1,0:T(8,128)(2,1)}, u32[]{:S(2)}, u32[]{:S(2)}) collective-permute-start(bf16[320,1024]{1,0:T(8,128)(2,1)} %get-tuple-element.144), channel_id=1, source_target_pairs={{0,16},{1,17},{2,18},{3,19},{4,20},{5,21},{6,22},{7,23},{8,24},{9,... | collective-permute-start | bytes 1966088 | tf_op jit(solution)/shard_map/ppermute | solution.py:1035
  264.6 30.9 %collective-permute-start.25 = (bf16[320,1024]{1,0:T(8,128)(2,1)}, bf16[320,1024]{1,0:T(8,128)(2,1)}, u32[]{:S(2)}, u32[]{:S(2)}) collective-permute-start(bf16[320,1024]{1,0:T(8,128)(2,1)} %get-tuple-element.145), channel_id=1, source_target_pairs={{0,1},{1,0},{2,3},{3,2},{4,5},{5,4},{6,7},{7,6},{8,9},{9,8},{10,11... | collective-permute-start | bytes 1966088 | tf_op jit(solution)/shard_map/ppermute | solution.py:1035
  266.1 29.5 %collective-permute-start.26 = (bf16[320,1024]{1,0:T(8,128)(2,1)}, bf16[320,1024]{1,0:T(8,128)(2,1)}, u32[]{:S(2)}, u32[]{:S(2)}) collective-permute-start(bf16[320,1024]{1,0:T(8,128)(2,1)} %get-tuple-element.146), channel_id=1, source_target_pairs={{0,17},{1,16},{2,19},{3,18},{4,21},{5,20},{6,23},{7,22},{8,25},{9,... | collective-permute-start | bytes 1966088 | tf_op jit(solution)/shard_map/ppermute | solution.py:1035
  270.1 35.7 %collective-permute-start.27 = (bf16[160,1920]{1,0:T(8,128)(2,1)}, bf16[160,1920]{1,0:T(8,128)(2,1)}, u32[]{:S(2)}, u32[]{:S(2)}) collective-permute-start(bf16[160,1920]{1,0:T(8,128)(2,1)} %total.2.a_ref), channel_id=1, source_target_pairs={{0,4},{1,5},{2,6},{3,7},{4,0},{5,1},{6,2},{7,3},{8,12},{9,13},{10,... | collective-permute-start | bytes 1843208 | tf_op jit(solution)/shard_map/ppermute | solution.py:1035
  297.9 40.6 %collective-permute-start.30 = (bf16[320,1024]{1,0:T(8,128)(2,1)}, bf16[320,1024]{1,0:T(8,128)(2,1)S(1)}, u32[]{:S(2)}, u32[]{:S(2)}) collective-permute-start(bf16[320,1024]{1,0:T(8,128)(2,1)} %total.3.a_ref), channel_id=1, source_target_pairs={{0,4},{1,5},{2,6},{3,7},{4,0},{5,1},{6,2},{7,3},{8,12},{9,13},{10,... | collective-permute-start | bytes 1966088 | tf_op jit(solution)/shard_map/ppermute | solution.py:1035
  308.0 15.4 %collective-permute-start.29 = (bf16[160,1920]{1,0:T(8,128)(2,1)}, bf16[160,1920]{1,0:T(8,128)(2,1)}, u32[]{:S(2)}, u32[]{:S(2)}) collective-permute-start(bf16[160,1920]{1,0:T(8,128)(2,1)} %add.135.refs_0_), channel_id=1, source_target_pairs={{0,16},{1,17},{2,18},{3,19},{4,20},{5,21},{6,22},{7,23},{8,24},{9,... | collective-permute-start | bytes 1843208 | tf_op jit(solution)/shard_map/ppermute | solution.py:1035
  309.5 29.1 %collective-permute-start.28 = (bf16[160,1920]{1,0:T(8,128)(2,1)}, bf16[160,1920]{1,0:T(8,128)(2,1)}, u32[]{:S(2)}, u32[]{:S(2)}) collective-permute-start(bf16[160,1920]{1,0:T(8,128)(2,1)} %add.135.refs_0_), channel_id=1, source_target_pairs={{0,2},{1,3},{2,0},{3,1},{4,6},{5,7},{6,4},{7,5},{8,10},{9,11},{10,... | collective-permute-start | bytes 1843208 | tf_op jit(solution)/shard_map/ppermute | solution.py:1035
  341.7 22.9 %collective-permute-start.34 = (bf16[320,1024]{1,0:T(8,128)(2,1)}, bf16[320,1024]{1,0:T(8,128)(2,1)S(1)}, u32[]{:S(2)}, u32[]{:S(2)}) collective-permute-start(bf16[320,1024]{1,0:T(8,128)(2,1)} %add.136.refs_0_), channel_id=1, source_target_pairs={{0,2},{1,3},{2,0},{3,1},{4,6},{5,7},{6,4},{7,5},{8,10},{9,11},{10,... | collective-permute-start | bytes 1966088 | tf_op jit(solution)/shard_map/ppermute | solution.py:1035
  341.7 22.9 %collective-permute-start.33 = (bf16[160,1920]{1,0:T(8,128)(2,1)}, bf16[160,1920]{1,0:T(8,128)(2,1)S(1)}, u32[]{:S(2)}, u32[]{:S(2)}) collective-permute-start(bf16[160,1920]{1,0:T(8,128)(2,1)} %collective-permute-done.28.refs_1_), channel_id=1, source_target_pairs={{0,16},{1,17},{2,18},{3,19},{4,20},{5,21},{6,22},{7,23},{8,24},{9,... | collective-permute-start | bytes 1843208 | tf_op jit(solution)/shard_map/ppermute | solution.py:1035
  342.2 27.6 %collective-permute-start.32 = (bf16[320,1024]{1,0:T(8,128)(2,1)}, bf16[320,1024]{1,0:T(8,128)(2,1)S(1)}, u32[]{:S(2)}, u32[]{:S(2)}) collective-permute-start(bf16[320,1024]{1,0:T(8,128)(2,1)} %add.136.refs_0_), channel_id=1, source_target_pairs={{0,16},{1,17},{2,18},{3,19},{4,20},{5,21},{6,22},{7,23},{8,24},{9,... | collective-permute-start | bytes 1966088 | tf_op jit(solution)/shard_map/ppermute | solution.py:1035
  343.7 26.1 %collective-permute-start.38 = (bf16[160,1920]{1,0:T(8,128)(2,1)}, bf16[160,1920]{1,0:T(8,128)(2,1)}, u32[]{:S(2)}, u32[]{:S(2)}) collective-permute-start(bf16[160,1920]{1,0:T(8,128)(2,1)} %collective-permute-done.29.refs_2_), channel_id=1, source_target_pairs={{0,8},{1,9},{2,10},{3,11},{4,12},{5,13},{6,14},{7,15},{8,0},{9,1},... | collective-permute-start | bytes 1843208 | tf_op jit(solution)/shard_map/ppermute | solution.py:1035
  343.7 55.3 %collective-permute-start.31 = (bf16[512,1280]{1,0:T(8,128)(2,1)}, bf16[512,1280]{1,0:T(8,128)(2,1)}, u32[]{:S(2)}, u32[]{:S(2)}) collective-permute-start(bf16[512,1280]{1,0:T(8,128)(2,1)} %get-tuple-element.154), channel_id=1, source_target_pairs={{0,2},{1,3},{2,6},{3,7},{4,10},{5,11},{6,14},{7,15},{8,0},{9,1},{1... | collective-permute-start | bytes 3932168 | tf_op jit(solution)/shard_map/ppermute | solution.py:1035
  370.4 28.6 %collective-permute-start.46 = (bf16[320,1024]{1,0:T(8,128)(2,1)S(1)}, bf16[320,1024]{1,0:T(8,128)(2,1)S(1)}, u32[]{:S(2)}, u32[]{:S(2)}) collective-permute-start(bf16[320,1024]{1,0:T(8,128)(2,1)S(1)} %collective-permute-done.34.refs_1_), channel_id=1, source_target_pairs={{0,16},{1,17},{2,18},{3,19},{4,20},{5,21},{6,22},{7,23},{8,24},{9,... | collective-permute-start | bytes 1966088 | tf_op jit(solution)/shard_map/ppermute | solution.py:1035
  (50 other events, 588.5 us)

commit v20 on v19

--- a/solution.py
+++ b/solution.py
@@ -348,7 +348,7 @@
 
 def pick(w, mine, parts, groups, nh):
     rows = w.shape[0]
-    step = 160 if rows % 160 == 0 else rows
+    step = 320 if rows % 320 == 0 else rows
     return pl.pallas_call(
         functools.partial(pick_kernel, parts=parts, groups=groups, nh=nh),
         out_shape=pltpu.HBM((rows, lanes_up(3 * nh * HD)), w.dtype),
@@ -378,7 +378,7 @@
 
 def stretch(x, groups, nh, us):
     rows, width = x.shape
-    step = 160
+    step = 320
     return pl.pallas_call(
         functools.partial(stretch_kernel, groups=groups, nh=nh),
         out_shape=pltpu.HBM((rows, 3 * nh * LN), x.dtype),

time: 418 us -> 416 us (level)
  transfers between devices with their start and end apart: 50 -> 50, of which waited for: 17 -> 18; matrix products, arithmetic and copies ran while one was open for 3% -> 3% of each run, Pallas kernels for 48% -> 47%
where the time goes in v20:
time: 416 us; the launch traced here: 409 us
  Pallas kernels  221 us (53%)
  waiting for transfers between devices  107 us (26%)
  starting transfers between devices  63.9 us (15%)
  local copies, waits for them, and re-layouts  11.3 us (3%)
    ppermute x49, waiting for transfers between devices, send(): return lax.ppermute(value, AXES, pairs(target))  107 us
    ppermute x49, starting transfers between devices, send(): return lax.ppermute(value, AXES, pairs(target))  57.9 us
    pallas_call x1, Pallas kernels, attn_bwd(): pl.pallas_call(functools.partial(bwd_kernel, first=group * nh, nh=nh, bq=...  43.5 us
    pallas_call x1, Pallas kernels, attn_fwd(): pl.pallas_call(functools.partial(fwd_kernel, nh=nh, bq=bq, bk=bk, nk=n //...  25.9 us
    pallas_call x2, Pallas kernels, project(): pl.pallas_call(functools.partial(project_kernel, count=count, halves=len(...  22.7 us
    pallas_call x1, Pallas kernels, tail(): pl.pallas_call(body, out_shape=[pltpu.HBM((rows, d), bf16)] + [pltpu.HBM(...  21.4 us
    pallas_call x2, Pallas kernels, share(): pl.pallas_call(share_kernel, out_shape=pltpu.HBM((d, n * w), bf16), grid_...  14.7 us
    pallas_call x1, Pallas kernels, cross(): pl.pallas_call(cross_kernel, out_shape=[pltpu.HBM((w // 2, cols), bf16)]...  11.6 us
  transfers between devices with their start and end apart: 50, of which 18 were waited for; matrix products, arithmetic and copies ran while one was open for 3% of the time, Pallas kernels for 47%

profile of v20, /device:TPU:0, one launch (start us, length us, event | category | flops | bytes accessed | tf_op | source)
XLA Modules:
  0.0 408.7 jit_solution(5144905192550183251)
XLA Ops:
  2.0 3.6 pick.1.x_ref.a_ref
  8.6 5.4 %collective-permute-start.5 = (bf16[512,1280]{1,0:T(8,128)(2,1)S(1)}, bf16[512,1280]{1,0:T(8,128)(2,1)}, u32[]{:S(2)}, u32[]{:S(2)}) collective-permute-start(bf16[512,1280]{1,0:T(8,128)(2,1)S(1)} %bitcast.67), channel_id=1, source_target_pairs={{0,8},{1,9},{2,10},{3,11},{12,4},{13,5},{14,6},{15,7},{16,24},{17,... | collective-permute-start | bytes 3932168 | tf_op jit(solution)/shard_map/ppermute | solution.py:1035
  25.0 11.2 %collective-permute-done.7.x_ref.b_ref = bf16[640,1024]{1,0:T(8,128)(2,1)} collective-permute-done((bf16[640,1024]{1,0:T(8,128)(2,1)}, bf16[640,1024]{1,0:T(8,128)(2,1)}, u32[]{:S(2)}, u32[]{:S(2)}) %collective-permute-start.7) | collective-permute-done | bytes 1310752 | tf_op jit(solution)/shard_map/ppermute | solution.py:1035
  38.7 4.5 %collective-permute-start.6 = (bf16[512,1280]{1,0:T(8,128)(2,1)}, bf16[512,1280]{1,0:T(8,128)(2,1)}, u32[]{:S(2)}, u32[]{:S(2)}) collective-permute-start(bf16[512,1280]{1,0:T(8,128)(2,1)} %collective-permute-done.1.refs_2_), channel_id=1, source_target_pairs={{0,8},{1,9},{2,10},{3,11},{12,4},{13,5},{14,6},{15,7},{16,24},{17,... | collective-permute-start | bytes 3932168 | tf_op jit(solution)/shard_map/ppermute | solution.py:1035
  46.2 4.0 collective-permute-start.4
  52.6 11.2 %project.2 = (bf16[2048,1280]{1,0:T(8,128)(2,1)}, bf16[2048,512]{1,0:T(8,128)(2,1)}, bf16[2048,1024]{1,0:T(8,128)(2,1)}, bf16[512,1280]{1,0:T(8,128)(2,1)}) custom-call(s32[5]{0:T(128)S(1)} %stack.100.info, bf16[512,1280]{1,0:T(8,128)(2,1)S(1)} %bitcast.68, bf16[512,1280]{1,0:T(8,128)(2,1)} %collective-permute-done.5.refs_1_, ...), custom_call_target="tpu_custom_call" | custom-call | flops 15000000512 | bytes 1000 | tf_op jit(solution)/shard_map/project/pallas_call | solution.py:518
  73.0 11.6 %project.3 = (bf16[2048,1280]{1,0:T(8,128)(2,1)}, bf16[2048,512]{1,0:T(8,128)(2,1)}, bf16[2048,1024]{1,0:T(8,128)(2,1)}, bf16[512,1280]{1,0:T(8,128)(2,1)}) custom-call(s32[5]{0:T(128)S(1)} %stack.97.info, bf16[512,1280]{1,0:T(8,128)(2,1)S(1)} %collective-permute-done.2.refs_0_, ...), custom_call_target="tpu_custom_call", output_to_operand_aliasing={{0}: (11, {}), {1}: (12, {}), {2}: (13, {})} | custom-call | flops 15000000512 | bytes 1000 | tf_op jit(solution)/shard_map/project/pallas_call | solution.py:518
  84.6 25.9 %attn_fwd.1 = (bf16[2048,320]{1,0:T(8,128)(2,1)}, bf16[2048,512]{1,0:T(8,128)(2,1)}, bf16[2048,512]{1,0:T(8,128)(2,1)}) custom-call(s32[16]{0:T(128)S(1)} %reshape.183.flags, bf16[2048,512]{1,0:T(8,128)(2,1)} %get-tuple-element.104.q_ref, bf16[2048,1024]{1,0:T(8,128)(2,1)} %get-tuple-element.105.kv.kk.vv, s32[2048,1]{1,0:T(8,128)S(1)} %copy.29.segc, ...), custom_call_target="tpu_custom_call" | custom-call | flops 10000000 | bytes 1000 | tf_op jit(solution)/shard_map/attn_fwd/pallas_call | solution.py:172
  117.9 6.4 %order.1.w_ref = bf16[1024,1280]{1,0:T(8,128)(2,1)} custom-call(s32[1]{0:T(128)} %bitcast.10.own_first, bf16[640,1024]{1,0:T(8,128)(2,1)} %pick.1.x_ref.a_ref, bf16[640,1024]{1,0:T(8,128)(2,1)} %collective-permute-done.7.x_ref.b_ref), custom_call_target="tpu_custom_call" | custom-call | flops 199999995904 | bytes 1000 | tf_op jit(solution)/shard_map/order/pallas_call | solution.py:408
  124.3 7.9 %transpose.15.x_ref = bf16[1280,2048]{1,0:T(8,128)(2,1)} custom-call(bf16[2048,1280]{1,0:T(8,128)(2,1)} %get-tuple-element.113.x_ref), custom_call_target="tpu_custom_call" | custom-call | flops 1000000 | bytes 1000 | tf_op jit(solution)/shard_map/transpose/pallas_call | solution.py:432
  134.6 21.4 %tail.1 = (bf16[512,1280]{1,0:T(8,128)(2,1)}, bf16[3,512,1280]{2,1,0:T(8,128)(2,1)}, bf16[3,512,1280]{2,1,0:T(8,128)(2,1)}, f32[512,1280]{1,0:T(8,128)}, bf16[51...) custom-call(s32[4]{0:T(128)S(1)} %pad_add_fusion.at, ...), custom_call_target="tpu_custom_call" | custom-call | flops 10000000 | bytes 1000 | tf_op jit(solution)/shard_map/tail/pallas_call | solution.py:654
  158.8 7.5 %share.2 = bf16[1280,1920]{1,0:T(8,128)(2,1)} custom-call(s32[1]{0:T(128)} %bitcast.20.col, bf16[3,512,1280]{2,1,0:T(8,128)(2,1)} %get-tuple-element.122.left, bf16[3,512,1280]{2,1,0:T(8,128)(2,1)} %get-tuple-element.123.right), custom_call_target="tpu_custom_call" | custom-call | flops 1000000 | bytes 1000 | tf_op jit(solution)/shard_map/share/pallas_call | solution.py:690
  166.4 7.2 %share.3.a_ref = bf16[1280,1920]{1,0:T(8,128)(2,1)} custom-call(s32[1]{0:T(128)} %bitcast.21.col, bf16[3,512,1280]{2,1,0:T(8,128)(2,1)} %get-tuple-element.122.left, bf16[3,512,1280]{2,1,0:T(8,128)(2,1)} %get-tuple-element.123.right), custom_call_target="tpu_custom_call" | custom-call | flops 1000000 | bytes 1000 | tf_op jit(solution)/shard_map/share/pallas_call | solution.py:690
  173.6 3.3 collective-permute-done.18.do2
  178.6 7.8 %add_rows.1 = bf16[1280,1920]{1,0:T(8,128)(2,1)} custom-call(bf16[1280,1920]{1,0:T(8,128)(2,1)} %share.3.a_ref, bf16[1280,1920]{1,0:T(8,128)(2,1)} %collective-permute-done.21.b_ref), custom_call_target="tpu_custom_call" | custom-call | flops 1000000 | bytes 1000 | tf_op jit(solution)/shard_map/add_rows/pallas_call | solution.py:770
  186.4 6.0 %all-to-all-start = ((bf16[8,160,1920]{2,1,0:T(8,128)(2,1)}), bf16[8,160,1920]{2,1,0:T(8,128)(2,1)}, u32[]{:S(2)}, u32[]{:S(2)}) async-start(bf16[8,160,1920]{2,1,0:T(8,128)(2,1)} %bitcast.77), calls=%async_computation | async-start | bytes 9830400 | tf_op jit(solution)/shard_map/all_to_all | solution.py:1209
  192.5 43.5 %attn_bwd.1 = (bf16[2048,1024]{1,0:T(8,128)(2,1)}, f32[8,128]{1,0:T(8,128)}) custom-call(s32[16]{0:T(128)S(1)} %copy-done.6, s32[1]{0:T(128)} %bitcast.mine.shard, bf16[2048,512]{1,0:T(8,128)(2,1)} %get-tuple-element.129.qa, bf16[2048,1024]{1,0:T(8,128)(2,1)} %get-tuple-element.105.kv.kk.vv, bf16[2048,1024]{1,0:T(8,128)(2,1)} %get-tuple-element.105.kv.kk.vv, ...), custom_call_target="tpu_custom_call" | custom-call | flops 299999985664 | bytes 1000 | tf_op jit(solution)/shard_map/attn_bwd/pallas_call | solution.py:314
  236.0 6.8 %back.2 = bf16[2,512,1280]{2,1,0:T(8,128)(2,1)} custom-call(s32[2]{0:T(128)S(1)} %pad_add_fusion.1.shards, bf16[2048,1024]{1,0:T(8,128)(2,1)} %get-tuple-element.138.g_ref, bf16[1024,1280]{1,0:T(8,128)(2,1)} %order.1.w_ref), custom_call_target="tpu_custom_call" | custom-call | flops 1000000 | bytes 1000 | tf_op jit(solution)/shard_map/back/pallas_call | solution.py:928
  242.8 11.6 %cross.1 = (bf16[320,1024]{1,0:T(8,128)(2,1)}, bf16[320,1024]{1,0:T(8,128)(2,1)}, bf16[320,1024]{1,0:T(8,128)(2,1)}, bf16[320,1024]{1,0:T(8,128)(2,1)}) custom-call(s32[2]{0:T(128)S(1)} %pad_add_fusion.2.at, bf16[1280,2048]{1,0:T(8,128)(2,1)} %transpose.15.x_ref, bf16[2048,1024]{1,0:T(8,128)(2,1)} %get-tuple-element.138.g_ref), custom_call_target="tpu_custom_call" | custom-call | flops 1000000 | bytes 1000 | tf_op jit(solution)/shard_map/cross/pallas_call | solution.py:850
  254.4 4.7 %back.3 = bf16[1,512,1280]{2,1,0:T(8,128)(2,1)} custom-call(s32[1]{0:T(128)} %bitcast.25.shards, bf16[2048,1024]{1,0:T(8,128)(2,1)} %get-tuple-element.138.g_ref, bf16[1024,1280]{1,0:T(8,128)(2,1)} %order.1.w_ref, bf16[2,512,1280]{2,1,0:T(8,128)(2,1)S(1)} %collective-permute-done.22.refs_0_.core), custom_call_target="tpu_custom_call" | custom-call | flops 1000000 | bytes 1000 | tf_op jit(solution)/shard_map/back/pallas_call | solution.py:928
  264.6 3.5 total.2.a_ref
  271.0 8.0 %collective-permute-done.24 = bf16[320,1024]{1,0:T(8,128)(2,1)} collective-permute-done((bf16[320,1024]{1,0:T(8,128)(2,1)}, bf16[320,1024]{1,0:T(8,128)(2,1)}, u32[]{:S(2)}, u32[]{:S(2)}) %collective-permute-start.24) | collective-permute-done | bytes 655392 | tf_op jit(solution)/shard_map/ppermute | solution.py:1035
  279.0 14.5 %collective-permute-done.25 = bf16[320,1024]{1,0:T(8,128)(2,1)} collective-permute-done((bf16[320,1024]{1,0:T(8,128)(2,1)}, bf16[320,1024]{1,0:T(8,128)(2,1)}, u32[]{:S(2)}, u32[]{:S(2)}) %collective-permute-start.25) | collective-permute-done | bytes 655392 | tf_op jit(solution)/shard_map/ppermute | solution.py:1035
  295.9 7.8 %collective-permute-done.27.b_ref = bf16[160,1920]{1,0:T(8,128)(2,1)} collective-permute-done((bf16[160,1920]{1,0:T(8,128)(2,1)}, bf16[160,1920]{1,0:T(8,128)(2,1)}, u32[]{:S(2)}, u32[]{:S(2)}) %collective-permute-start.27) | collective-permute-done | bytes 614432 | tf_op jit(solution)/shard_map/ppermute | solution.py:1035
  309.1 6.6 %finish.1 = (bf16[512,1280]{1,0:T(8,128)(2,1)}, f32[1,1280]{1,0:T(1,128)S(1)}) custom-call(s32[1]{0:T(128)} %bitcast.mine.shard, bf16[2048,1024]{1,0:T(8,128)(2,1)} %get-tuple-element.138.g_ref, bf16[1024,1280]{1,0:T(8,128)(2,1)} %order.1.w_ref, bf16[2,512,1280]{2,1,0:T(8,128)(2,1)S(1)} %collective-permute-done.22.refs_0_.core, ...), custom_call_target="tpu_custom_call" | custom-call | flops 1000000 | bytes 1000 | tf_op jit(solution)/shard_map/finish/pallas_call | solution.py:966
  315.7 5.7 %collective-permute-done.29.refs_2_ = bf16[160,1920]{1,0:T(8,128)(2,1)} collective-permute-done((bf16[160,1920]{1,0:T(8,128)(2,1)}, bf16[160,1920]{1,0:T(8,128)(2,1)}, u32[]{:S(2)}, u32[]{:S(2)}) %collective-permute-start.29) | collective-permute-done | bytes 614432 | tf_op jit(solution)/shard_map/ppermute | solution.py:1035
  321.4 15.1 %collective-permute-done.28.refs_1_ = bf16[160,1920]{1,0:T(8,128)(2,1)} collective-permute-done((bf16[160,1920]{1,0:T(8,128)(2,1)}, bf16[160,1920]{1,0:T(8,128)(2,1)}, u32[]{:S(2)}, u32[]{:S(2)}) %collective-permute-start.28) | collective-permute-done | bytes 614432 | tf_op jit(solution)/shard_map/ppermute | solution.py:1035
  343.7 18.8 %collective-permute-done.34.refs_1_ = bf16[320,1024]{1,0:T(8,128)(2,1)S(1)} collective-permute-done((bf16[320,1024]{1,0:T(8,128)(2,1)}, bf16[320,1024]{1,0:T(8,128)(2,1)S(1)}, u32[]{:S(2)}, u32[]{:S(2)}) %collective-permute-start.34) | collective-permute-done | bytes 655392 | tf_op jit(solution)/shard_map/ppermute | solution.py:1035
  363.0 4.8 %collective-permute-done.32.refs_0_ = bf16[320,1024]{1,0:T(8,128)(2,1)S(1)} collective-permute-done((bf16[320,1024]{1,0:T(8,128)(2,1)}, bf16[320,1024]{1,0:T(8,128)(2,1)S(1)}, u32[]{:S(2)}, u32[]{:S(2)}) %collective-permute-start.32) | collective-permute-done | bytes 655392 | tf_op jit(solution)/shard_map/ppermute | solution.py:1035
  372.0 7.2 %place_tail.1 = (f32[4,160,1280]{2,1,0:T(8,128)}, f32[4,160,1280]{2,1,0:T(8,128)}, f32[4,160,1280]{2,1,0:T(8,128)}) custom-call(s32[3]{0:T(128)S(1)} %pad_add_fusion.3.at, bf16[160,1920]{1,0:T(8,128)(2,1)} %add.135.refs_0_, bf16[160,1920]{1,0:T(8,128)(2,1)} %collective-permute-done.28.refs_1_, bf16[160,1920]{1,0:T(8,128)(2,1)} %collective-permute-done.29.refs_2_, ...), custom_call_target="tpu_custom_call" | custom-call | flops 1000000 | bytes 1000 | tf_op jit(solution)/shard_map/place_tail/pallas_call | solution.py:813
  387.9 3.7 collective-permute-start.44
  403.8 4.4 %spread.3 = f32[2,320,3840]{2,1,0:T(8,128)} custom-call(s32[3]{0:T(128)S(1)} %pad_add_fusion.5.at, bf16[320,1024]{1,0:T(8,128)(2,1)S(1)} %collective-permute-done.32.refs_0_, bf16[320,1024]{1,0:T(8,128)(2,1)S(1)} %collective-permute-done.46.refs_1_, bf16[320,1024]{1,0:T(8,128)(2,1)} %collective-permute-done.47.refs_2_, ...), custom_call_target="tpu_custom_call", output_to_operand_aliasing={{}: (5, {})} | custom-call | flops 1000000 | bytes 1000 | tf_op jit(solution)/shard_map/spread/pallas_call | solution.py:892
  (205 shorter events, 95.6 us)
Async XLA Ops:
  0.6 20.8 %collective-permute-start.1 = (bf16[512,1280]{1,0:T(8,128)(2,1)}, bf16[512,1280]{1,0:T(8,128)(2,1)}, u32[]{:S(2)}, u32[]{:S(2)}) collective-permute-start(bf16[512,1280]{1,0:T(8,128)(2,1)} %bitcast.66), channel_id=1, source_target_pairs={{2,0},{3,1},{4,2},{5,3},{6,4},{7,5},{8,10},{9,11},{10,12},{11,13},... | collective-permute-start | bytes 3932168 | tf_op jit(solution)/shard_map/ppermute | solution.py:1035
  5.6 30.6 %collective-permute-start.7 = (bf16[640,1024]{1,0:T(8,128)(2,1)}, bf16[640,1024]{1,0:T(8,128)(2,1)}, u32[]{:S(2)}, u32[]{:S(2)}) collective-permute-start(bf16[640,1024]{1,0:T(8,128)(2,1)} %pick.1.x_ref.a_ref), channel_id=1, source_target_pairs={{0,1},{1,0},{2,3},{3,2},{4,5},{5,4},{6,7},{7,6},{8,9},{9,8},{10,11... | collective-permute-start | bytes 3932168 | tf_op jit(solution)/shard_map/ppermute | solution.py:1035
  8.6 41.6 %collective-permute-start.5 = (bf16[512,1280]{1,0:T(8,128)(2,1)S(1)}, bf16[512,1280]{1,0:T(8,128)(2,1)}, u32[]{:S(2)}, u32[]{:S(2)}) collective-permute-start(bf16[512,1280]{1,0:T(8,128)(2,1)S(1)} %bitcast.67), channel_id=1, source_target_pairs={{0,8},{1,9},{2,10},{3,11},{12,4},{13,5},{14,6},{15,7},{16,24},{17,... | collective-permute-start | bytes 3932168 | tf_op jit(solution)/shard_map/ppermute | solution.py:1035
  14.0 55.7 %collective-permute-start = (s32[1,2048]{1,0:T(1,128)S(1)}, s32[1,2048]{1,0:T(1,128)S(1)}, u32[]{:S(2)}, u32[]{:S(2)}) collective-permute-start(s32[1,2048]{1,0:T(1,128)S(1)} %copy-done.25), channel_id=1, source_target_pairs={{0,8},{1,9},{2,10},{3,11},{4,12},{5,13},{6,14},{7,15},{8,0},{9,1},... | collective-permute-start | bytes 24584 | tf_op jit(solution)/shard_map/ppermute | solution.py:1035
  21.5 24.6 %collective-permute-start.2 = (bf16[512,1280]{1,0:T(8,128)(2,1)}, bf16[512,1280]{1,0:T(8,128)(2,1)S(1)}, u32[]{:S(2)}, u32[]{:S(2)}) collective-permute-start(bf16[512,1280]{1,0:T(8,128)(2,1)} %collective-permute-done.1.refs_2_), channel_id=1, source_target_pairs={{2,0},{3,1},{4,2},{5,3},{10,12},{11,13},{12,14},{13,15},{18,16},{1... | collective-permute-start | bytes 3932168 | tf_op jit(solution)/shard_map/ppermute | solution.py:1035
  36.2 34.9 %collective-permute-start.9 = (bf16[320,1280]{1,0:T(8,128)(2,1)}, bf16[320,1280]{1,0:T(8,128)(2,1)}, u32[]{:S(2)}, u32[]{:S(2)}) collective-permute-start(bf16[320,1280]{1,0:T(8,128)(2,1)} %constant_dynamic-slice_fusion.4), channel_id=1, source_target_pairs={{0,1},{1,0},{2,3},{3,2},{4,5},{5,4},{6,7},{7,6},{8,9},{9,8},{10,11... | collective-permute-start | bytes 2457608 | tf_op jit(solution)/shard_map/ppermute | solution.py:1035
  46.2 19.6 %collective-permute-start.4 = (bf16[512,1280]{1,0:T(8,128)(2,1)S(1)}, bf16[512,1280]{1,0:T(8,128)(2,1)}, u32[]{:S(2)}, u32[]{:S(2)}) collective-permute-start(bf16[512,1280]{1,0:T(8,128)(2,1)S(1)} %broadcast_select_fusion), channel_id=1, source_target_pairs={{0,2},{1,3},{2,0},{3,1},{12,14},{13,15},{14,12},{15,13},{16,18},{1... | collective-permute-start | bytes 3932168 | tf_op jit(solution)/shard_map/ppermute | solution.py:1035
  50.2 22.8 %collective-permute-start.3 = (bf16[512,1280]{1,0:T(8,128)(2,1)S(1)}, bf16[512,1280]{1,0:T(8,128)(2,1)}, u32[]{:S(2)}, u32[]{:S(2)}) collective-permute-start(bf16[512,1280]{1,0:T(8,128)(2,1)S(1)} %collective-permute-done.2.refs_0_), channel_id=1, source_target_pairs={{0,8},{1,9},{2,10},{3,11},{12,4},{13,5},{14,6},{15,7},{16,24},{17,... | collective-permute-start | bytes 3932168 | tf_op jit(solution)/shard_map/ppermute | solution.py:1035
  71.1 39.4 %collective-permute-start.10 = (bf16[2,320,1280]{2,1,0:T(8,128)(2,1)}, bf16[2,320,1280]{2,1,0:T(8,128)(2,1)}, u32[]{:S(2)}, u32[]{:S(2)}) collective-permute-start(bf16[2,320,1280]{2,1,0:T(8,128)(2,1)} %pad_maximum_fusion), channel_id=1, source_target_pairs={{0,1},{1,0},{2,3},{3,2},{4,5},{5,4},{6,7},{7,6},{8,9},{9,8},{10,11... | collective-permute-start | bytes 4915208 | tf_op jit(solution)/shard_map/ppermute | solution.py:1035
  72.4 38.1 %collective-permute-start.11 = (bf16[512,1280]{1,0:T(8,128)(2,1)}, bf16[512,1280]{1,0:T(8,128)(2,1)S(1)}, u32[]{:S(2)}, u32[]{:S(2)}) collective-permute-start(bf16[512,1280]{1,0:T(8,128)(2,1)} %bitcast.88), channel_id=1, source_target_pairs={{0,8},{1,9},{2,0},{3,1},{4,10},{5,11},{6,2},{7,3},{8,12},{9,13},{1... | collective-permute-start | bytes 3932168 | tf_op jit(solution)/shard_map/ppermute | solution.py:1035
  115.7 16.5 %collective-permute-start.13 = (bf16[512,320]{1,0:T(8,128)(2,1)}, bf16[512,320]{1,0:T(8,128)(2,1)}, u32[]{:S(2)}, u32[]{:S(2)}) collective-permute-start(bf16[512,320]{1,0:T(8,128)(2,1)} %get-tuple-element.184), channel_id=1, source_target_pairs={{0,2},{1,3},{2,0},{3,1},{4,6},{5,7},{6,4},{7,5},{8,10},{9,11},{10,... | collective-permute-start | bytes 983048 | tf_op jit(solution)/shard_map/ppermute | solution.py:1035
  115.8 18.8 %collective-permute-start.14 = (bf16[512,320]{1,0:T(8,128)(2,1)}, bf16[512,320]{1,0:T(8,128)(2,1)}, u32[]{:S(2)}, u32[]{:S(2)}) collective-permute-start(bf16[512,320]{1,0:T(8,128)(2,1)} %get-tuple-element.183), channel_id=1, source_target_pairs={{0,10},{1,11},{2,8},{3,9},{4,14},{5,15},{6,12},{7,13},{8,2},{9,3},... | collective-permute-start | bytes 983048 | tf_op jit(solution)/shard_map/ppermute | solution.py:1035
  117.1 17.5 %collective-permute-start.16 = (bf16[2,320,1280]{2,1,0:T(8,128)(2,1)}, bf16[2,320,1280]{2,1,0:T(8,128)(2,1)}, u32[]{:S(2)}, u32[]{:S(2)}) collective-permute-start(bf16[2,320,1280]{2,1,0:T(8,128)(2,1)} %collective-permute-done.10.half), channel_id=1, source_target_pairs={{0,8},{1,9},{2,10},{3,11},{4,12},{5,13},{6,14},{7,15},{8,0},{9,1},... | collective-permute-start | bytes 4915208 | tf_op jit(solution)/shard_map/ppermute | solution.py:1035
  117.9 16.7 %collective-permute-start.15 = (bf16[320,1280]{1,0:T(8,128)(2,1)}, bf16[320,1280]{1,0:T(8,128)(2,1)}, u32[]{:S(2)}, u32[]{:S(2)}) collective-permute-start(bf16[320,1280]{1,0:T(8,128)(2,1)} %collective-permute-done.9.half0), channel_id=1, source_target_pairs={{0,8},{1,9},{2,10},{3,11},{4,12},{5,13},{6,14},{7,15},{8,0},{9,1},... | collective-permute-start | bytes 2457608 | tf_op jit(solution)/shard_map/ppermute | solution.py:1035
  156.9 16.7 %collective-permute-start.19 = (bf16[512,320]{1,0:T(8,128)(2,1)}, bf16[512,320]{1,0:T(8,128)(2,1)S(1)}, u32[]{:S(2)}, u32[]{:S(2)}) collective-permute-start(bf16[512,320]{1,0:T(8,128)(2,1)} %get-tuple-element.126), channel_id=1, source_target_pairs={{0,10},{1,11},{2,8},{3,9},{4,14},{5,15},{6,12},{7,13},{8,2},{9,3},... | collective-permute-start | bytes 983048 | tf_op jit(solution)/shard_map/ppermute | solution.py:1035
  157.1 19.9 %collective-permute-start.18 = (bf16[512,320]{1,0:T(8,128)(2,1)}, bf16[512,320]{1,0:T(8,128)(2,1)S(1)}, u32[]{:S(2)}, u32[]{:S(2)}) collective-permute-start(bf16[512,320]{1,0:T(8,128)(2,1)} %get-tuple-element.120), channel_id=1, source_target_pairs={{0,2},{1,3},{2,0},{3,1},{4,6},{5,7},{6,4},{7,5},{8,10},{9,11},{10,... | collective-permute-start | bytes 983048 | tf_op jit(solution)/shard_map/ppermute | solution.py:1035
  178.2 57.7 %collective-permute-start.20 = (bf16[512,1280]{1,0:T(8,128)(2,1)}, bf16[512,1280]{1,0:T(8,128)(2,1)}, u32[]{:S(2)}, u32[]{:S(2)}) collective-permute-start(bf16[512,1280]{1,0:T(8,128)(2,1)} %get-tuple-element.128), channel_id=1, source_target_pairs={{0,2},{1,3},{2,6},{3,7},{4,10},{5,11},{6,14},{7,15},{8,0},{9,1},{1... | collective-permute-start | bytes 3932168 | tf_op jit(solution)/shard_map/ppermute | solution.py:1035
  186.4 78.2 %all-to-all-start = ((bf16[8,160,1920]{2,1,0:T(8,128)(2,1)}), bf16[8,160,1920]{2,1,0:T(8,128)(2,1)}, u32[]{:S(2)}, u32[]{:S(2)}) async-start(bf16[8,160,1920]{2,1,0:T(8,128)(2,1)} %bitcast.77), calls=%async_computation | async-start | bytes 9830400 | tf_op jit(solution)/shard_map/all_to_all | solution.py:1209
  259.1 50.0 %collective-permute-start.23 = (bf16[1,512,1280]{2,1,0:T(8,128)(2,1)}, bf16[1,512,1280]{2,1,0:T(8,128)(2,1)}, u32[]{:S(2)}, u32[]{:S(2)}) collective-permute-start(bf16[1,512,1280]{2,1,0:T(8,128)(2,1)} %back.3), channel_id=1, source_target_pairs={{0,2},{1,3},{2,0},{3,1},{4,6},{5,7},{6,4},{7,5},{8,10},{9,11},{10,... | collective-permute-start | bytes 3932168 | tf_op jit(solution)/shard_map/ppermute | solution.py:1035
  261.1 17.9 %collective-permute-start.24 = (bf16[320,1024]{1,0:T(8,128)(2,1)}, bf16[320,1024]{1,0:T(8,128)(2,1)}, u32[]{:S(2)}, u32[]{:S(2)}) collective-permute-start(bf16[320,1024]{1,0:T(8,128)(2,1)} %get-tuple-element.144), channel_id=1, source_target_pairs={{0,16},{1,17},{2,18},{3,19},{4,20},{5,21},{6,22},{7,23},{8,24},{9,... | collective-permute-start | bytes 1966088 | tf_op jit(solution)/shard_map/ppermute | solution.py:1035
  262.6 30.9 %collective-permute-start.25 = (bf16[320,1024]{1,0:T(8,128)(2,1)}, bf16[320,1024]{1,0:T(8,128)(2,1)}, u32[]{:S(2)}, u32[]{:S(2)}) collective-permute-start(bf16[320,1024]{1,0:T(8,128)(2,1)} %get-tuple-element.145), channel_id=1, source_target_pairs={{0,1},{1,0},{2,3},{3,2},{4,5},{5,4},{6,7},{7,6},{8,9},{9,8},{10,11... | collective-permute-start | bytes 1966088 | tf_op jit(solution)/shard_map/ppermute | solution.py:1035
  264.0 29.5 %collective-permute-start.26 = (bf16[320,1024]{1,0:T(8,128)(2,1)}, bf16[320,1024]{1,0:T(8,128)(2,1)}, u32[]{:S(2)}, u32[]{:S(2)}) collective-permute-start(bf16[320,1024]{1,0:T(8,128)(2,1)} %get-tuple-element.146), channel_id=1, source_target_pairs={{0,17},{1,16},{2,19},{3,18},{4,21},{5,20},{6,23},{7,22},{8,25},{9,... | collective-permute-start | bytes 1966088 | tf_op jit(solution)/shard_map/ppermute | solution.py:1035
  268.0 35.7 %collective-permute-start.27 = (bf16[160,1920]{1,0:T(8,128)(2,1)}, bf16[160,1920]{1,0:T(8,128)(2,1)}, u32[]{:S(2)}, u32[]{:S(2)}) collective-permute-start(bf16[160,1920]{1,0:T(8,128)(2,1)} %total.2.a_ref), channel_id=1, source_target_pairs={{0,4},{1,5},{2,6},{3,7},{4,0},{5,1},{6,2},{7,3},{8,12},{9,13},{10,... | collective-permute-start | bytes 1843208 | tf_op jit(solution)/shard_map/ppermute | solution.py:1035
  295.9 40.6 %collective-permute-start.30 = (bf16[320,1024]{1,0:T(8,128)(2,1)}, bf16[320,1024]{1,0:T(8,128)(2,1)S(1)}, u32[]{:S(2)}, u32[]{:S(2)}) collective-permute-start(bf16[320,1024]{1,0:T(8,128)(2,1)} %total.3.a_ref), channel_id=1, source_target_pairs={{0,4},{1,5},{2,6},{3,7},{4,0},{5,1},{6,2},{7,3},{8,12},{9,13},{10,... | collective-permute-start | bytes 1966088 | tf_op jit(solution)/shard_map/ppermute | solution.py:1035
  306.0 15.4 %collective-permute-start.29 = (bf16[160,1920]{1,0:T(8,128)(2,1)}, bf16[160,1920]{1,0:T(8,128)(2,1)}, u32[]{:S(2)}, u32[]{:S(2)}) collective-permute-start(bf16[160,1920]{1,0:T(8,128)(2,1)} %add.135.refs_0_), channel_id=1, source_target_pairs={{0,16},{1,17},{2,18},{3,19},{4,20},{5,21},{6,22},{7,23},{8,24},{9,... | collective-permute-start | bytes 1843208 | tf_op jit(solution)/shard_map/ppermute | solution.py:1035
  307.4 29.1 %collective-permute-start.28 = (bf16[160,1920]{1,0:T(8,128)(2,1)}, bf16[160,1920]{1,0:T(8,128)(2,1)}, u32[]{:S(2)}, u32[]{:S(2)}) collective-permute-start(bf16[160,1920]{1,0:T(8,128)(2,1)} %add.135.refs_0_), channel_id=1, source_target_pairs={{0,2},{1,3},{2,0},{3,1},{4,6},{5,7},{6,4},{7,5},{8,10},{9,11},{10,... | collective-permute-start | bytes 1843208 | tf_op jit(solution)/shard_map/ppermute | solution.py:1035
  339.6 22.9 %collective-permute-start.34 = (bf16[320,1024]{1,0:T(8,128)(2,1)}, bf16[320,1024]{1,0:T(8,128)(2,1)S(1)}, u32[]{:S(2)}, u32[]{:S(2)}) collective-permute-start(bf16[320,1024]{1,0:T(8,128)(2,1)} %add.136.refs_0_), channel_id=1, source_target_pairs={{0,2},{1,3},{2,0},{3,1},{4,6},{5,7},{6,4},{7,5},{8,10},{9,11},{10,... | collective-permute-start | bytes 1966088 | tf_op jit(solution)/shard_map/ppermute | solution.py:1035
  339.6 22.9 %collective-permute-start.33 = (bf16[160,1920]{1,0:T(8,128)(2,1)}, bf16[160,1920]{1,0:T(8,128)(2,1)S(1)}, u32[]{:S(2)}, u32[]{:S(2)}) collective-permute-start(bf16[160,1920]{1,0:T(8,128)(2,1)} %collective-permute-done.28.refs_1_), channel_id=1, source_target_pairs={{0,16},{1,17},{2,18},{3,19},{4,20},{5,21},{6,22},{7,23},{8,24},{9,... | collective-permute-start | bytes 1843208 | tf_op jit(solution)/shard_map/ppermute | solution.py:1035
  340.2 27.6 %collective-permute-start.32 = (bf16[320,1024]{1,0:T(8,128)(2,1)}, bf16[320,1024]{1,0:T(8,128)(2,1)S(1)}, u32[]{:S(2)}, u32[]{:S(2)}) collective-permute-start(bf16[320,1024]{1,0:T(8,128)(2,1)} %add.136.refs_0_), channel_id=1, source_target_pairs={{0,16},{1,17},{2,18},{3,19},{4,20},{5,21},{6,22},{7,23},{8,24},{9,... | collective-permute-start | bytes 1966088 | tf_op jit(solution)/shard_map/ppermute | solution.py:1035
  341.6 26.1 %collective-permute-start.38 = (bf16[160,1920]{1,0:T(8,128)(2,1)}, bf16[160,1920]{1,0:T(8,128)(2,1)}, u32[]{:S(2)}, u32[]{:S(2)}) collective-permute-start(bf16[160,1920]{1,0:T(8,128)(2,1)} %collective-permute-done.29.refs_2_), channel_id=1, source_target_pairs={{0,8},{1,9},{2,10},{3,11},{4,12},{5,13},{6,14},{7,15},{8,0},{9,1},... | collective-permute-start | bytes 1843208 | tf_op jit(solution)/shard_map/ppermute | solution.py:1035
  341.6 55.3 %collective-permute-start.31 = (bf16[512,1280]{1,0:T(8,128)(2,1)}, bf16[512,1280]{1,0:T(8,128)(2,1)}, u32[]{:S(2)}, u32[]{:S(2)}) collective-permute-start(bf16[512,1280]{1,0:T(8,128)(2,1)} %get-tuple-element.154), channel_id=1, source_target_pairs={{0,2},{1,3},{2,6},{3,7},{4,10},{5,11},{6,14},{7,15},{8,0},{9,1},{1... | collective-permute-start | bytes 3932168 | tf_op jit(solution)/shard_map/ppermute | solution.py:1035
  368.4 28.6 %collective-permute-start.46 = (bf16[320,1024]{1,0:T(8,128)(2,1)S(1)}, bf16[320,1024]{1,0:T(8,128)(2,1)S(1)}, u32[]{:S(2)}, u32[]{:S(2)}) collective-permute-start(bf16[320,1024]{1,0:T(8,128)(2,1)S(1)} %collective-permute-done.34.refs_1_), channel_id=1, source_target_pairs={{0,16},{1,17},{2,18},{3,19},{4,20},{5,21},{6,22},{7,23},{8,24},{9,... | collective-permute-start | bytes 1966088 | tf_op jit(solution)/shard_map/ppermute | solution.py:1035
  (50 other events, 584.0 us)

commit v21 on v20

--- a/solution.py
+++ b/solution.py
@@ -766,14 +766,14 @@
 
 def add_rows(a, b):
     rows, cols = a.shape
-    block = pl.BlockSpec((rows // 5, cols), lambda i: (i, 0))
+    block = pl.BlockSpec((rows // 2, cols), lambda i: (i, 0))
     return pl.pallas_call(
         add_kernel,
         out_shape=pltpu.HBM(a.shape, bf16),
-        grid=(5,),
+        grid=(2,),
         in_specs=[block] * 2,
         out_specs=block,
-        compiler_params=pltpu.CompilerParams(vmem_limit_bytes=14 << 20),
+        compiler_params=pltpu.CompilerParams(vmem_limit_bytes=24 << 20),
         cost_estimate=CHEAP,
         name="add_rows",
     )(hbm(a), hbm(b))

time: 416 us -> 414 us (level)
  no operation moved by 1% of the time
where the time goes in v21:
time: 414 us; the launch traced here: 406 us
  Pallas kernels  219 us (53%)
  waiting for transfers between devices  106 us (26%)
  starting transfers between devices  65.5 us (16%)
  local copies, waits for them, and re-layouts  11.3 us (3%)
    ppermute x49, waiting for transfers between devices, send(): return lax.ppermute(value, AXES, pairs(target))  106 us
    ppermute x49, starting transfers between devices, send(): return lax.ppermute(value, AXES, pairs(target))  59.7 us
    pallas_call x1, Pallas kernels, attn_bwd(): pl.pallas_call(functools.partial(bwd_kernel, first=group * nh, nh=nh, bq=...  43.5 us
    pallas_call x1, Pallas kernels, attn_fwd(): pl.pallas_call(functools.partial(fwd_kernel, nh=nh, bq=bq, bk=bk, nk=n //...  25.9 us
    pallas_call x2, Pallas kernels, project(): pl.pallas_call(functools.partial(project_kernel, count=count, halves=len(...  22.7 us
    pallas_call x1, Pallas kernels, tail(): pl.pallas_call(body, out_shape=[pltpu.HBM((rows, d), bf16)] + [pltpu.HBM(...  21.4 us
    pallas_call x2, Pallas kernels, share(): pl.pallas_call(share_kernel, out_shape=pltpu.HBM((d, n * w), bf16), grid_...  14.7 us
    pallas_call x1, Pallas kernels, cross(): pl.pallas_call(cross_kernel, out_shape=[pltpu.HBM((w // 2, cols), bf16)]...  11.6 us
  transfers between devices with their start and end apart: 50, of which 18 were waited for; matrix products, arithmetic and copies ran while one was open for 3% of the time, Pallas kernels for 47%

profile of v21, /device:TPU:0, one launch (start us, length us, event | category | flops | bytes accessed | tf_op | source)
XLA Modules:
  0.0 406.4 jit_solution(15432162968314142293)
XLA Ops:
  2.0 3.6 pick.1.x_ref.a_ref
  8.6 5.4 %collective-permute-start.5 = (bf16[512,1280]{1,0:T(8,128)(2,1)S(1)}, bf16[512,1280]{1,0:T(8,128)(2,1)}, u32[]{:S(2)}, u32[]{:S(2)}) collective-permute-start(bf16[512,1280]{1,0:T(8,128)(2,1)S(1)} %bitcast.67), channel_id=1, source_target_pairs={{0,8},{1,9},{2,10},{3,11},{12,4},{13,5},{14,6},{15,7},{16,24},{17,... | collective-permute-start | bytes 3932168 | tf_op jit(solution)/shard_map/ppermute | solution.py:1035
  25.0 11.2 %collective-permute-done.7.x_ref.b_ref = bf16[640,1024]{1,0:T(8,128)(2,1)} collective-permute-done((bf16[640,1024]{1,0:T(8,128)(2,1)}, bf16[640,1024]{1,0:T(8,128)(2,1)}, u32[]{:S(2)}, u32[]{:S(2)}) %collective-permute-start.7) | collective-permute-done | bytes 1310752 | tf_op jit(solution)/shard_map/ppermute | solution.py:1035
  38.7 4.5 %collective-permute-start.6 = (bf16[512,1280]{1,0:T(8,128)(2,1)}, bf16[512,1280]{1,0:T(8,128)(2,1)}, u32[]{:S(2)}, u32[]{:S(2)}) collective-permute-start(bf16[512,1280]{1,0:T(8,128)(2,1)} %collective-permute-done.1.refs_2_), channel_id=1, source_target_pairs={{0,8},{1,9},{2,10},{3,11},{12,4},{13,5},{14,6},{15,7},{16,24},{17,... | collective-permute-start | bytes 3932168 | tf_op jit(solution)/shard_map/ppermute | solution.py:1035
  46.2 4.0 collective-permute-start.4
  52.6 11.2 %project.2 = (bf16[2048,1280]{1,0:T(8,128)(2,1)}, bf16[2048,512]{1,0:T(8,128)(2,1)}, bf16[2048,1024]{1,0:T(8,128)(2,1)}, bf16[512,1280]{1,0:T(8,128)(2,1)}) custom-call(s32[5]{0:T(128)S(1)} %stack.100.info, bf16[512,1280]{1,0:T(8,128)(2,1)S(1)} %bitcast.68, bf16[512,1280]{1,0:T(8,128)(2,1)} %collective-permute-done.5.refs_1_, ...), custom_call_target="tpu_custom_call" | custom-call | flops 15000000512 | bytes 1000 | tf_op jit(solution)/shard_map/project/pallas_call | solution.py:518
  73.0 11.6 %project.3 = (bf16[2048,1280]{1,0:T(8,128)(2,1)}, bf16[2048,512]{1,0:T(8,128)(2,1)}, bf16[2048,1024]{1,0:T(8,128)(2,1)}, bf16[512,1280]{1,0:T(8,128)(2,1)}) custom-call(s32[5]{0:T(128)S(1)} %stack.97.info, bf16[512,1280]{1,0:T(8,128)(2,1)S(1)} %collective-permute-done.2.refs_0_, ...), custom_call_target="tpu_custom_call", output_to_operand_aliasing={{0}: (11, {}), {1}: (12, {}), {2}: (13, {})} | custom-call | flops 15000000512 | bytes 1000 | tf_op jit(solution)/shard_map/project/pallas_call | solution.py:518
  84.6 25.9 %attn_fwd.1 = (bf16[2048,320]{1,0:T(8,128)(2,1)}, bf16[2048,512]{1,0:T(8,128)(2,1)}, bf16[2048,512]{1,0:T(8,128)(2,1)}) custom-call(s32[16]{0:T(128)S(1)} %reshape.183.flags, bf16[2048,512]{1,0:T(8,128)(2,1)} %get-tuple-element.104.q_ref, bf16[2048,1024]{1,0:T(8,128)(2,1)} %get-tuple-element.105.kv.kk.vv, s32[2048,1]{1,0:T(8,128)S(1)} %copy.29.segc, ...), custom_call_target="tpu_custom_call" | custom-call | flops 10000000 | bytes 1000 | tf_op jit(solution)/shard_map/attn_fwd/pallas_call | solution.py:172
  117.9 6.4 %order.1.w_ref = bf16[1024,1280]{1,0:T(8,128)(2,1)} custom-call(s32[1]{0:T(128)} %bitcast.10.own_first, bf16[640,1024]{1,0:T(8,128)(2,1)} %pick.1.x_ref.a_ref, bf16[640,1024]{1,0:T(8,128)(2,1)} %collective-permute-done.7.x_ref.b_ref), custom_call_target="tpu_custom_call" | custom-call | flops 199999995904 | bytes 1000 | tf_op jit(solution)/shard_map/order/pallas_call | solution.py:408
  124.3 7.9 %transpose.15.x_ref = bf16[1280,2048]{1,0:T(8,128)(2,1)} custom-call(bf16[2048,1280]{1,0:T(8,128)(2,1)} %get-tuple-element.113.x_ref), custom_call_target="tpu_custom_call" | custom-call | flops 1000000 | bytes 1000 | tf_op jit(solution)/shard_map/transpose/pallas_call | solution.py:432
  134.6 21.4 %tail.1 = (bf16[512,1280]{1,0:T(8,128)(2,1)}, bf16[3,512,1280]{2,1,0:T(8,128)(2,1)}, bf16[3,512,1280]{2,1,0:T(8,128)(2,1)}, f32[512,1280]{1,0:T(8,128)}, bf16[51...) custom-call(s32[4]{0:T(128)S(1)} %pad_add_fusion.at, ...), custom_call_target="tpu_custom_call" | custom-call | flops 10000000 | bytes 1000 | tf_op jit(solution)/shard_map/tail/pallas_call | solution.py:654
  158.8 7.5 %share.2 = bf16[1280,1920]{1,0:T(8,128)(2,1)} custom-call(s32[1]{0:T(128)} %bitcast.20.col, bf16[3,512,1280]{2,1,0:T(8,128)(2,1)} %get-tuple-element.122.left, bf16[3,512,1280]{2,1,0:T(8,128)(2,1)} %get-tuple-element.123.right), custom_call_target="tpu_custom_call" | custom-call | flops 1000000 | bytes 1000 | tf_op jit(solution)/shard_map/share/pallas_call | solution.py:690
  166.4 7.2 %share.3.a_ref = bf16[1280,1920]{1,0:T(8,128)(2,1)} custom-call(s32[1]{0:T(128)} %bitcast.21.col, bf16[3,512,1280]{2,1,0:T(8,128)(2,1)} %get-tuple-element.122.left, bf16[3,512,1280]{2,1,0:T(8,128)(2,1)} %get-tuple-element.123.right), custom_call_target="tpu_custom_call" | custom-call | flops 1000000 | bytes 1000 | tf_op jit(solution)/shard_map/share/pallas_call | solution.py:690
  173.6 3.3 collective-permute-done.18.do2
  178.6 5.9 %add_rows.1 = bf16[1280,1920]{1,0:T(8,128)(2,1)} custom-call(bf16[1280,1920]{1,0:T(8,128)(2,1)} %share.3.a_ref, bf16[1280,1920]{1,0:T(8,128)(2,1)} %collective-permute-done.21.b_ref), custom_call_target="tpu_custom_call" | custom-call | flops 1000000 | bytes 1000 | tf_op jit(solution)/shard_map/add_rows/pallas_call | solution.py:770
  184.5 5.8 %all-to-all-start = ((bf16[8,160,1920]{2,1,0:T(8,128)(2,1)}), bf16[8,160,1920]{2,1,0:T(8,128)(2,1)}, u32[]{:S(2)}, u32[]{:S(2)}) async-start(bf16[8,160,1920]{2,1,0:T(8,128)(2,1)} %bitcast.77), calls=%async_computation | async-start | bytes 9830400 | tf_op jit(solution)/shard_map/all_to_all | solution.py:1209
  190.4 43.5 %attn_bwd.1 = (bf16[2048,1024]{1,0:T(8,128)(2,1)}, f32[8,128]{1,0:T(8,128)}) custom-call(s32[16]{0:T(128)S(1)} %copy-done.6, s32[1]{0:T(128)} %bitcast.mine.shard, bf16[2048,512]{1,0:T(8,128)(2,1)} %get-tuple-element.129.qa, bf16[2048,1024]{1,0:T(8,128)(2,1)} %get-tuple-element.105.kv.kk.vv, bf16[2048,1024]{1,0:T(8,128)(2,1)} %get-tuple-element.105.kv.kk.vv, ...), custom_call_target="tpu_custom_call" | custom-call | flops 299999985664 | bytes 1000 | tf_op jit(solution)/shard_map/attn_bwd/pallas_call | solution.py:314
  233.9 6.8 %back.2 = bf16[2,512,1280]{2,1,0:T(8,128)(2,1)} custom-call(s32[2]{0:T(128)S(1)} %pad_add_fusion.1.shards, bf16[2048,1024]{1,0:T(8,128)(2,1)} %get-tuple-element.138.g_ref, bf16[1024,1280]{1,0:T(8,128)(2,1)} %order.1.w_ref), custom_call_target="tpu_custom_call" | custom-call | flops 1000000 | bytes 1000 | tf_op jit(solution)/shard_map/back/pallas_call | solution.py:928
  240.7 11.6 %cross.1 = (bf16[320,1024]{1,0:T(8,128)(2,1)}, bf16[320,1024]{1,0:T(8,128)(2,1)}, bf16[320,1024]{1,0:T(8,128)(2,1)}, bf16[320,1024]{1,0:T(8,128)(2,1)}) custom-call(s32[2]{0:T(128)S(1)} %pad_add_fusion.2.at, bf16[1280,2048]{1,0:T(8,128)(2,1)} %transpose.15.x_ref, bf16[2048,1024]{1,0:T(8,128)(2,1)} %get-tuple-element.138.g_ref), custom_call_target="tpu_custom_call" | custom-call | flops 1000000 | bytes 1000 | tf_op jit(solution)/shard_map/cross/pallas_call | solution.py:850
  252.3 4.7 %back.3 = bf16[1,512,1280]{2,1,0:T(8,128)(2,1)} custom-call(s32[1]{0:T(128)} %bitcast.25.shards, bf16[2048,1024]{1,0:T(8,128)(2,1)} %get-tuple-element.138.g_ref, bf16[1024,1280]{1,0:T(8,128)(2,1)} %order.1.w_ref, bf16[2,512,1280]{2,1,0:T(8,128)(2,1)S(1)} %collective-permute-done.22.refs_0_.core), custom_call_target="tpu_custom_call" | custom-call | flops 1000000 | bytes 1000 | tf_op jit(solution)/shard_map/back/pallas_call | solution.py:928
  262.5 3.5 total.2.a_ref
  270.2 6.7 %collective-permute-done.24 = bf16[320,1024]{1,0:T(8,128)(2,1)} collective-permute-done((bf16[320,1024]{1,0:T(8,128)(2,1)}, bf16[320,1024]{1,0:T(8,128)(2,1)}, u32[]{:S(2)}, u32[]{:S(2)}) %collective-permute-start.24) | collective-permute-done | bytes 655392 | tf_op jit(solution)/shard_map/ppermute | solution.py:1035
  276.9 14.5 %collective-permute-done.25 = bf16[320,1024]{1,0:T(8,128)(2,1)} collective-permute-done((bf16[320,1024]{1,0:T(8,128)(2,1)}, bf16[320,1024]{1,0:T(8,128)(2,1)}, u32[]{:S(2)}, u32[]{:S(2)}) %collective-permute-start.25) | collective-permute-done | bytes 655392 | tf_op jit(solution)/shard_map/ppermute | solution.py:1035
  294.0 7.6 %collective-permute-done.27.b_ref = bf16[160,1920]{1,0:T(8,128)(2,1)} collective-permute-done((bf16[160,1920]{1,0:T(8,128)(2,1)}, bf16[160,1920]{1,0:T(8,128)(2,1)}, u32[]{:S(2)}, u32[]{:S(2)}) %collective-permute-start.27) | collective-permute-done | bytes 614432 | tf_op jit(solution)/shard_map/ppermute | solution.py:1035
  307.2 6.6 %finish.1 = (bf16[512,1280]{1,0:T(8,128)(2,1)}, f32[1,1280]{1,0:T(1,128)S(1)}) custom-call(s32[1]{0:T(128)} %bitcast.mine.shard, bf16[2048,1024]{1,0:T(8,128)(2,1)} %get-tuple-element.138.g_ref, bf16[1024,1280]{1,0:T(8,128)(2,1)} %order.1.w_ref, bf16[2,512,1280]{2,1,0:T(8,128)(2,1)S(1)} %collective-permute-done.22.refs_0_.core, ...), custom_call_target="tpu_custom_call" | custom-call | flops 1000000 | bytes 1000 | tf_op jit(solution)/shard_map/finish/pallas_call | solution.py:966
  313.8 5.4 %collective-permute-done.29.refs_2_ = bf16[160,1920]{1,0:T(8,128)(2,1)} collective-permute-done((bf16[160,1920]{1,0:T(8,128)(2,1)}, bf16[160,1920]{1,0:T(8,128)(2,1)}, u32[]{:S(2)}, u32[]{:S(2)}) %collective-permute-start.29) | collective-permute-done | bytes 614432 | tf_op jit(solution)/shard_map/ppermute | solution.py:1035
  319.3 15.1 %collective-permute-done.28.refs_1_ = bf16[160,1920]{1,0:T(8,128)(2,1)} collective-permute-done((bf16[160,1920]{1,0:T(8,128)(2,1)}, bf16[160,1920]{1,0:T(8,128)(2,1)}, u32[]{:S(2)}, u32[]{:S(2)}) %collective-permute-start.28) | collective-permute-done | bytes 614432 | tf_op jit(solution)/shard_map/ppermute | solution.py:1035
  341.6 18.8 %collective-permute-done.34.refs_1_ = bf16[320,1024]{1,0:T(8,128)(2,1)S(1)} collective-permute-done((bf16[320,1024]{1,0:T(8,128)(2,1)}, bf16[320,1024]{1,0:T(8,128)(2,1)S(1)}, u32[]{:S(2)}, u32[]{:S(2)}) %collective-permute-start.34) | collective-permute-done | bytes 655392 | tf_op jit(solution)/shard_map/ppermute | solution.py:1035
  360.9 4.8 %collective-permute-done.32.refs_0_ = bf16[320,1024]{1,0:T(8,128)(2,1)S(1)} collective-permute-done((bf16[320,1024]{1,0:T(8,128)(2,1)}, bf16[320,1024]{1,0:T(8,128)(2,1)S(1)}, u32[]{:S(2)}, u32[]{:S(2)}) %collective-permute-start.32) | collective-permute-done | bytes 655392 | tf_op jit(solution)/shard_map/ppermute | solution.py:1035
  369.9 7.4 %place_tail.1 = (f32[4,160,1280]{2,1,0:T(8,128)}, f32[4,160,1280]{2,1,0:T(8,128)}, f32[4,160,1280]{2,1,0:T(8,128)}) custom-call(s32[3]{0:T(128)S(1)} %pad_add_fusion.3.at, bf16[160,1920]{1,0:T(8,128)(2,1)} %add.135.refs_0_, bf16[160,1920]{1,0:T(8,128)(2,1)} %collective-permute-done.28.refs_1_, bf16[160,1920]{1,0:T(8,128)(2,1)} %collective-permute-done.29.refs_2_, ...), custom_call_target="tpu_custom_call" | custom-call | flops 1000000 | bytes 1000 | tf_op jit(solution)/shard_map/place_tail/pallas_call | solution.py:813
  386.0 3.7 collective-permute-start.44
  401.9 4.4 %spread.3 = f32[2,320,3840]{2,1,0:T(8,128)} custom-call(s32[3]{0:T(128)S(1)} %pad_add_fusion.5.at, bf16[320,1024]{1,0:T(8,128)(2,1)S(1)} %collective-permute-done.32.refs_0_, bf16[320,1024]{1,0:T(8,128)(2,1)S(1)} %collective-permute-done.46.refs_1_, bf16[320,1024]{1,0:T(8,128)(2,1)} %collective-permute-done.47.refs_2_, ...), custom_call_target="tpu_custom_call", output_to_operand_aliasing={{}: (5, {})} | custom-call | flops 1000000 | bytes 1000 | tf_op jit(solution)/shard_map/spread/pallas_call | solution.py:892
  (205 shorter events, 97.4 us)
Async XLA Ops:
  0.6 20.8 %collective-permute-start.1 = (bf16[512,1280]{1,0:T(8,128)(2,1)}, bf16[512,1280]{1,0:T(8,128)(2,1)}, u32[]{:S(2)}, u32[]{:S(2)}) collective-permute-start(bf16[512,1280]{1,0:T(8,128)(2,1)} %bitcast.66), channel_id=1, source_target_pairs={{2,0},{3,1},{4,2},{5,3},{6,4},{7,5},{8,10},{9,11},{10,12},{11,13},... | collective-permute-start | bytes 3932168 | tf_op jit(solution)/shard_map/ppermute | solution.py:1035
  5.6 30.6 %collective-permute-start.7 = (bf16[640,1024]{1,0:T(8,128)(2,1)}, bf16[640,1024]{1,0:T(8,128)(2,1)}, u32[]{:S(2)}, u32[]{:S(2)}) collective-permute-start(bf16[640,1024]{1,0:T(8,128)(2,1)} %pick.1.x_ref.a_ref), channel_id=1, source_target_pairs={{0,1},{1,0},{2,3},{3,2},{4,5},{5,4},{6,7},{7,6},{8,9},{9,8},{10,11... | collective-permute-start | bytes 3932168 | tf_op jit(solution)/shard_map/ppermute | solution.py:1035
  8.6 41.6 %collective-permute-start.5 = (bf16[512,1280]{1,0:T(8,128)(2,1)S(1)}, bf16[512,1280]{1,0:T(8,128)(2,1)}, u32[]{:S(2)}, u32[]{:S(2)}) collective-permute-start(bf16[512,1280]{1,0:T(8,128)(2,1)S(1)} %bitcast.67), channel_id=1, source_target_pairs={{0,8},{1,9},{2,10},{3,11},{12,4},{13,5},{14,6},{15,7},{16,24},{17,... | collective-permute-start | bytes 3932168 | tf_op jit(solution)/shard_map/ppermute | solution.py:1035
  14.0 55.7 %collective-permute-start = (s32[1,2048]{1,0:T(1,128)S(1)}, s32[1,2048]{1,0:T(1,128)S(1)}, u32[]{:S(2)}, u32[]{:S(2)}) collective-permute-start(s32[1,2048]{1,0:T(1,128)S(1)} %copy-done.25), channel_id=1, source_target_pairs={{0,8},{1,9},{2,10},{3,11},{4,12},{5,13},{6,14},{7,15},{8,0},{9,1},... | collective-permute-start | bytes 24584 | tf_op jit(solution)/shard_map/ppermute | solution.py:1035
  21.5 24.6 %collective-permute-start.2 = (bf16[512,1280]{1,0:T(8,128)(2,1)}, bf16[512,1280]{1,0:T(8,128)(2,1)S(1)}, u32[]{:S(2)}, u32[]{:S(2)}) collective-permute-start(bf16[512,1280]{1,0:T(8,128)(2,1)} %collective-permute-done.1.refs_2_), channel_id=1, source_target_pairs={{2,0},{3,1},{4,2},{5,3},{10,12},{11,13},{12,14},{13,15},{18,16},{1... | collective-permute-start | bytes 3932168 | tf_op jit(solution)/shard_map/ppermute | solution.py:1035
  36.2 34.9 %collective-permute-start.9 = (bf16[320,1280]{1,0:T(8,128)(2,1)}, bf16[320,1280]{1,0:T(8,128)(2,1)}, u32[]{:S(2)}, u32[]{:S(2)}) collective-permute-start(bf16[320,1280]{1,0:T(8,128)(2,1)} %constant_dynamic-slice_fusion.4), channel_id=1, source_target_pairs={{0,1},{1,0},{2,3},{3,2},{4,5},{5,4},{6,7},{7,6},{8,9},{9,8},{10,11... | collective-permute-start | bytes 2457608 | tf_op jit(solution)/shard_map/ppermute | solution.py:1035
  46.2 19.6 %collective-permute-start.4 = (bf16[512,1280]{1,0:T(8,128)(2,1)S(1)}, bf16[512,1280]{1,0:T(8,128)(2,1)}, u32[]{:S(2)}, u32[]{:S(2)}) collective-permute-start(bf16[512,1280]{1,0:T(8,128)(2,1)S(1)} %broadcast_select_fusion), channel_id=1, source_target_pairs={{0,2},{1,3},{2,0},{3,1},{12,14},{13,15},{14,12},{15,13},{16,18},{1... | collective-permute-start | bytes 3932168 | tf_op jit(solution)/shard_map/ppermute | solution.py:1035
  50.2 22.8 %collective-permute-start.3 = (bf16[512,1280]{1,0:T(8,128)(2,1)S(1)}, bf16[512,1280]{1,0:T(8,128)(2,1)}, u32[]{:S(2)}, u32[]{:S(2)}) collective-permute-start(bf16[512,1280]{1,0:T(8,128)(2,1)S(1)} %collective-permute-done.2.refs_0_), channel_id=1, source_target_pairs={{0,8},{1,9},{2,10},{3,11},{12,4},{13,5},{14,6},{15,7},{16,24},{17,... | collective-permute-start | bytes 3932168 | tf_op jit(solution)/shard_map/ppermute | solution.py:1035
  71.1 39.4 %collective-permute-start.10 = (bf16[2,320,1280]{2,1,0:T(8,128)(2,1)}, bf16[2,320,1280]{2,1,0:T(8,128)(2,1)}, u32[]{:S(2)}, u32[]{:S(2)}) collective-permute-start(bf16[2,320,1280]{2,1,0:T(8,128)(2,1)} %pad_maximum_fusion), channel_id=1, source_target_pairs={{0,1},{1,0},{2,3},{3,2},{4,5},{5,4},{6,7},{7,6},{8,9},{9,8},{10,11... | collective-permute-start | bytes 4915208 | tf_op jit(solution)/shard_map/ppermute | solution.py:1035
  72.4 38.1 %collective-permute-start.11 = (bf16[512,1280]{1,0:T(8,128)(2,1)}, bf16[512,1280]{1,0:T(8,128)(2,1)S(1)}, u32[]{:S(2)}, u32[]{:S(2)}) collective-permute-start(bf16[512,1280]{1,0:T(8,128)(2,1)} %bitcast.88), channel_id=1, source_target_pairs={{0,8},{1,9},{2,0},{3,1},{4,10},{5,11},{6,2},{7,3},{8,12},{9,13},{1... | collective-permute-start | bytes 3932168 | tf_op jit(solution)/shard_map/ppermute | solution.py:1035
  115.7 16.5 %collective-permute-start.13 = (bf16[512,320]{1,0:T(8,128)(2,1)}, bf16[512,320]{1,0:T(8,128)(2,1)}, u32[]{:S(2)}, u32[]{:S(2)}) collective-permute-start(bf16[512,320]{1,0:T(8,128)(2,1)} %get-tuple-element.184), channel_id=1, source_target_pairs={{0,2},{1,3},{2,0},{3,1},{4,6},{5,7},{6,4},{7,5},{8,10},{9,11},{10,... | collective-permute-start | bytes 983048 | tf_op jit(solution)/shard_map/ppermute | solution.py:1035
  115.8 18.8 %collective-permute-start.14 = (bf16[512,320]{1,0:T(8,128)(2,1)}, bf16[512,320]{1,0:T(8,128)(2,1)}, u32[]{:S(2)}, u32[]{:S(2)}) collective-permute-start(bf16[512,320]{1,0:T(8,128)(2,1)} %get-tuple-element.183), channel_id=1, source_target_pairs={{0,10},{1,11},{2,8},{3,9},{4,14},{5,15},{6,12},{7,13},{8,2},{9,3},... | collective-permute-start | bytes 983048 | tf_op jit(solution)/shard_map/ppermute | solution.py:1035
  117.1 17.5 %collective-permute-start.16 = (bf16[2,320,1280]{2,1,0:T(8,128)(2,1)}, bf16[2,320,1280]{2,1,0:T(8,128)(2,1)}, u32[]{:S(2)}, u32[]{:S(2)}) collective-permute-start(bf16[2,320,1280]{2,1,0:T(8,128)(2,1)} %collective-permute-done.10.half), channel_id=1, source_target_pairs={{0,8},{1,9},{2,10},{3,11},{4,12},{5,13},{6,14},{7,15},{8,0},{9,1},... | collective-permute-start | bytes 4915208 | tf_op jit(solution)/shard_map/ppermute | solution.py:1035
  117.9 16.7 %collective-permute-start.15 = (bf16[320,1280]{1,0:T(8,128)(2,1)}, bf16[320,1280]{1,0:T(8,128)(2,1)}, u32[]{:S(2)}, u32[]{:S(2)}) collective-permute-start(bf16[320,1280]{1,0:T(8,128)(2,1)} %collective-permute-done.9.half0), channel_id=1, source_target_pairs={{0,8},{1,9},{2,10},{3,11},{4,12},{5,13},{6,14},{7,15},{8,0},{9,1},... | collective-permute-start | bytes 2457608 | tf_op jit(solution)/shard_map/ppermute | solution.py:1035
  156.9 16.7 %collective-permute-start.19 = (bf16[512,320]{1,0:T(8,128)(2,1)}, bf16[512,320]{1,0:T(8,128)(2,1)S(1)}, u32[]{:S(2)}, u32[]{:S(2)}) collective-permute-start(bf16[512,320]{1,0:T(8,128)(2,1)} %get-tuple-element.126), channel_id=1, source_target_pairs={{0,10},{1,11},{2,8},{3,9},{4,14},{5,15},{6,12},{7,13},{8,2},{9,3},... | collective-permute-start | bytes 983048 | tf_op jit(solution)/shard_map/ppermute | solution.py:1035
  157.1 19.9 %collective-permute-start.18 = (bf16[512,320]{1,0:T(8,128)(2,1)}, bf16[512,320]{1,0:T(8,128)(2,1)S(1)}, u32[]{:S(2)}, u32[]{:S(2)}) collective-permute-start(bf16[512,320]{1,0:T(8,128)(2,1)} %get-tuple-element.120), channel_id=1, source_target_pairs={{0,2},{1,3},{2,0},{3,1},{4,6},{5,7},{6,4},{7,5},{8,10},{9,11},{10,... | collective-permute-start | bytes 983048 | tf_op jit(solution)/shard_map/ppermute | solution.py:1035
  178.2 55.6 %collective-permute-start.20 = (bf16[512,1280]{1,0:T(8,128)(2,1)}, bf16[512,1280]{1,0:T(8,128)(2,1)}, u32[]{:S(2)}, u32[]{:S(2)}) collective-permute-start(bf16[512,1280]{1,0:T(8,128)(2,1)} %get-tuple-element.128), channel_id=1, source_target_pairs={{0,2},{1,3},{2,6},{3,7},{4,10},{5,11},{6,14},{7,15},{8,0},{9,1},{1... | collective-permute-start | bytes 3932168 | tf_op jit(solution)/shard_map/ppermute | solution.py:1035
  184.5 77.9 %all-to-all-start = ((bf16[8,160,1920]{2,1,0:T(8,128)(2,1)}), bf16[8,160,1920]{2,1,0:T(8,128)(2,1)}, u32[]{:S(2)}, u32[]{:S(2)}) async-start(bf16[8,160,1920]{2,1,0:T(8,128)(2,1)} %bitcast.77), calls=%async_computation | async-start | bytes 9830400 | tf_op jit(solution)/shard_map/all_to_all | solution.py:1209
  257.0 50.2 %collective-permute-start.23 = (bf16[1,512,1280]{2,1,0:T(8,128)(2,1)}, bf16[1,512,1280]{2,1,0:T(8,128)(2,1)}, u32[]{:S(2)}, u32[]{:S(2)}) collective-permute-start(bf16[1,512,1280]{2,1,0:T(8,128)(2,1)} %back.3), channel_id=1, source_target_pairs={{0,2},{1,3},{2,0},{3,1},{4,6},{5,7},{6,4},{7,5},{8,10},{9,11},{10,... | collective-permute-start | bytes 3932168 | tf_op jit(solution)/shard_map/ppermute | solution.py:1035
  259.0 17.9 %collective-permute-start.24 = (bf16[320,1024]{1,0:T(8,128)(2,1)}, bf16[320,1024]{1,0:T(8,128)(2,1)}, u32[]{:S(2)}, u32[]{:S(2)}) collective-permute-start(bf16[320,1024]{1,0:T(8,128)(2,1)} %get-tuple-element.144), channel_id=1, source_target_pairs={{0,16},{1,17},{2,18},{3,19},{4,20},{5,21},{6,22},{7,23},{8,24},{9,... | collective-permute-start | bytes 1966088 | tf_op jit(solution)/shard_map/ppermute | solution.py:1035
  260.5 30.9 %collective-permute-start.25 = (bf16[320,1024]{1,0:T(8,128)(2,1)}, bf16[320,1024]{1,0:T(8,128)(2,1)}, u32[]{:S(2)}, u32[]{:S(2)}) collective-permute-start(bf16[320,1024]{1,0:T(8,128)(2,1)} %get-tuple-element.145), channel_id=1, source_target_pairs={{0,1},{1,0},{2,3},{3,2},{4,5},{5,4},{6,7},{7,6},{8,9},{9,8},{10,11... | collective-permute-start | bytes 1966088 | tf_op jit(solution)/shard_map/ppermute | solution.py:1035
  261.9 29.5 %collective-permute-start.26 = (bf16[320,1024]{1,0:T(8,128)(2,1)}, bf16[320,1024]{1,0:T(8,128)(2,1)}, u32[]{:S(2)}, u32[]{:S(2)}) collective-permute-start(bf16[320,1024]{1,0:T(8,128)(2,1)} %get-tuple-element.146), channel_id=1, source_target_pairs={{0,17},{1,16},{2,19},{3,18},{4,21},{5,20},{6,23},{7,22},{8,25},{9,... | collective-permute-start | bytes 1966088 | tf_op jit(solution)/shard_map/ppermute | solution.py:1035
  265.9 35.7 %collective-permute-start.27 = (bf16[160,1920]{1,0:T(8,128)(2,1)}, bf16[160,1920]{1,0:T(8,128)(2,1)}, u32[]{:S(2)}, u32[]{:S(2)}) collective-permute-start(bf16[160,1920]{1,0:T(8,128)(2,1)} %total.2.a_ref), channel_id=1, source_target_pairs={{0,4},{1,5},{2,6},{3,7},{4,0},{5,1},{6,2},{7,3},{8,12},{9,13},{10,... | collective-permute-start | bytes 1843208 | tf_op jit(solution)/shard_map/ppermute | solution.py:1035
  293.8 40.6 %collective-permute-start.30 = (bf16[320,1024]{1,0:T(8,128)(2,1)}, bf16[320,1024]{1,0:T(8,128)(2,1)S(1)}, u32[]{:S(2)}, u32[]{:S(2)}) collective-permute-start(bf16[320,1024]{1,0:T(8,128)(2,1)} %total.3.a_ref), channel_id=1, source_target_pairs={{0,4},{1,5},{2,6},{3,7},{4,0},{5,1},{6,2},{7,3},{8,12},{9,13},{10,... | collective-permute-start | bytes 1966088 | tf_op jit(solution)/shard_map/ppermute | solution.py:1035
  303.8 15.4 %collective-permute-start.29 = (bf16[160,1920]{1,0:T(8,128)(2,1)}, bf16[160,1920]{1,0:T(8,128)(2,1)}, u32[]{:S(2)}, u32[]{:S(2)}) collective-permute-start(bf16[160,1920]{1,0:T(8,128)(2,1)} %add.135.refs_0_), channel_id=1, source_target_pairs={{0,16},{1,17},{2,18},{3,19},{4,20},{5,21},{6,22},{7,23},{8,24},{9,... | collective-permute-start | bytes 1843208 | tf_op jit(solution)/shard_map/ppermute | solution.py:1035
  305.3 29.1 %collective-permute-start.28 = (bf16[160,1920]{1,0:T(8,128)(2,1)}, bf16[160,1920]{1,0:T(8,128)(2,1)}, u32[]{:S(2)}, u32[]{:S(2)}) collective-permute-start(bf16[160,1920]{1,0:T(8,128)(2,1)} %add.135.refs_0_), channel_id=1, source_target_pairs={{0,2},{1,3},{2,0},{3,1},{4,6},{5,7},{6,4},{7,5},{8,10},{9,11},{10,... | collective-permute-start | bytes 1843208 | tf_op jit(solution)/shard_map/ppermute | solution.py:1035
  337.5 22.9 %collective-permute-start.34 = (bf16[320,1024]{1,0:T(8,128)(2,1)}, bf16[320,1024]{1,0:T(8,128)(2,1)S(1)}, u32[]{:S(2)}, u32[]{:S(2)}) collective-permute-start(bf16[320,1024]{1,0:T(8,128)(2,1)} %add.136.refs_0_), channel_id=1, source_target_pairs={{0,2},{1,3},{2,0},{3,1},{4,6},{5,7},{6,4},{7,5},{8,10},{9,11},{10,... | collective-permute-start | bytes 1966088 | tf_op jit(solution)/shard_map/ppermute | solution.py:1035
  337.5 22.9 %collective-permute-start.33 = (bf16[160,1920]{1,0:T(8,128)(2,1)}, bf16[160,1920]{1,0:T(8,128)(2,1)S(1)}, u32[]{:S(2)}, u32[]{:S(2)}) collective-permute-start(bf16[160,1920]{1,0:T(8,128)(2,1)} %collective-permute-done.28.refs_1_), channel_id=1, source_target_pairs={{0,16},{1,17},{2,18},{3,19},{4,20},{5,21},{6,22},{7,23},{8,24},{9,... | collective-permute-start | bytes 1843208 | tf_op jit(solution)/shard_map/ppermute | solution.py:1035
  338.1 27.6 %collective-permute-start.32 = (bf16[320,1024]{1,0:T(8,128)(2,1)}, bf16[320,1024]{1,0:T(8,128)(2,1)S(1)}, u32[]{:S(2)}, u32[]{:S(2)}) collective-permute-start(bf16[320,1024]{1,0:T(8,128)(2,1)} %add.136.refs_0_), channel_id=1, source_target_pairs={{0,16},{1,17},{2,18},{3,19},{4,20},{5,21},{6,22},{7,23},{8,24},{9,... | collective-permute-start | bytes 1966088 | tf_op jit(solution)/shard_map/ppermute | solution.py:1035
  339.5 26.1 %collective-permute-start.38 = (bf16[160,1920]{1,0:T(8,128)(2,1)}, bf16[160,1920]{1,0:T(8,128)(2,1)}, u32[]{:S(2)}, u32[]{:S(2)}) collective-permute-start(bf16[160,1920]{1,0:T(8,128)(2,1)} %collective-permute-done.29.refs_2_), channel_id=1, source_target_pairs={{0,8},{1,9},{2,10},{3,11},{4,12},{5,13},{6,14},{7,15},{8,0},{9,1},... | collective-permute-start | bytes 1843208 | tf_op jit(solution)/shard_map/ppermute | solution.py:1035
  339.5 55.5 %collective-permute-start.31 = (bf16[512,1280]{1,0:T(8,128)(2,1)}, bf16[512,1280]{1,0:T(8,128)(2,1)}, u32[]{:S(2)}, u32[]{:S(2)}) collective-permute-start(bf16[512,1280]{1,0:T(8,128)(2,1)} %get-tuple-element.154), channel_id=1, source_target_pairs={{0,2},{1,3},{2,6},{3,7},{4,10},{5,11},{6,14},{7,15},{8,0},{9,1},{1... | collective-permute-start | bytes 3932168 | tf_op jit(solution)/shard_map/ppermute | solution.py:1035
  366.3 28.8 %collective-permute-start.46 = (bf16[320,1024]{1,0:T(8,128)(2,1)S(1)}, bf16[320,1024]{1,0:T(8,128)(2,1)S(1)}, u32[]{:S(2)}, u32[]{:S(2)}) collective-permute-start(bf16[320,1024]{1,0:T(8,128)(2,1)S(1)} %collective-permute-done.34.refs_1_), channel_id=1, source_target_pairs={{0,16},{1,17},{2,18},{3,19},{4,20},{5,21},{6,22},{7,23},{8,24},{9,... | collective-permute-start | bytes 1966088 | tf_op jit(solution)/shard_map/ppermute | solution.py:1035
  (50 other events, 582.6 us)
